TPU v7x, 32 devices: a whole 2x2x4 slice. The times are simulated.
32 devices in a mesh: rep: 2 (over y), shard: 8 (over z, x), mp: 2 (over core).
Axes of the slice: x: 2, y: 2, z: 4, core: 2. Of those that a mesh axis runs over, the one named last changes fastest.
Arguments:
- inputs: bfloat16 [32, 512, 1024], P(('rep', 'shard'), None, 'mp'), may hold values from -6 to 6
- encoded: bfloat16 [32, 128, 1024], P(('rep', 'shard'), None, 'mp'), may hold values from -6 to 6
- cotangent: bfloat16 [32, 512, 1024], P(('rep', 'shard'), None, 'mp'), may hold values from -6 to 6
- lengths: int32 [32], replicated, may hold values from 64 to 512, as said below
- seq_slots: int32 [32], replicated, may hold values from 0 to 31, each once
- block_slots: int32 [128], replicated, may hold values from 0 to 127, as said below
- weights: float32 [2, 128, 256, 256], P('mp', 'shard')
- left_stat: float32 [2, 128, 256, 256], P('mp', 'shard')
- right_stat: float32 [2, 128, 256, 256], P('mp', 'shard')
- left_root: float32 [2, 128, 256, 256], P('mp', 'shard')
- right_root: float32 [2, 128, 256, 256], P('mp', 'shard')
- vectors: float32 [2, 8704], P('mp', 'shard')
- vec_stat: float32 [2, 8704], P('mp', 'shard'), may hold values from 819 to 16384
Outputs:
- outputs: bfloat16 [32, 512, 1024], P(('rep', 'shard'), None, 'mp')
- input_grad: bfloat16 [32, 512, 1024], P(('rep', 'shard'), None, 'mp')
- encoded_grad: bfloat16 [32, 128, 1024], P(('rep', 'shard'), None, 'mp')
- block_grad: float32 [2, 128, 256, 256], P('mp', 'shard')
- left_new: float32 [2, 128, 256, 256], P('mp', 'shard')
- right_new: float32 [2, 128, 256, 256], P('mp', 'shard')
- weights_new: float32 [2, 128, 256, 256], P('mp', 'shard')
- vector_grad: float32 [2, 8704], P('mp', 'shard')
- vec_stat_new: float32 [2, 8704], P('mp', 'shard')
- vectors_new: float32 [2, 8704], P('mp', 'shard')
Inputs may be any that keep to these rules, and one draw needn't show every extreme that they name: Rows from lengths[i] on are padding; some sequence has exactly 512 valid tokens. `seq_slots`: slot s lies on the data device s // 2 of the joined rep and shard axes; each slot holds one sequence. `block_slots`: A permutation of the 128 natural blocks.
All inputs are finite; a program needn't handle non-finite values.
Results may differ from a plain program's by a relative error of at most 0.029.
Values may be sent and summed in bfloat16 or wider, within the bound.
No kernel may reach another device: no remote copies, remote signals or barrier semaphores. Data moves between devices by JAX's collectives and lax.ppermute only.
A program may use at most 168 MiB of HBM per device.

v0:
```python
import jax
import jax.numpy as jnp
from jax import lax
from jax.sharding import PartitionSpec as P

D = 1024
FF = 4096
HEAD_DIM = 64
BS = 256


eps_norm = 1e-05
masked_score = -1e30


def layouts(model_width, half_d, half_f):
    return (
        (model_width, half_d),
        (model_width, half_d),
        (model_width, half_d),
        (half_d, model_width),
        (model_width, half_d),
        (model_width, half_d),
        (model_width, half_d),
        (half_d, model_width),
        (model_width, half_f),
        (half_f, model_width),
    )


def to_blocks(matrix):
    row_count, col_count = matrix.shape
    tiles = matrix.reshape(row_count // BS, BS, col_count // BS, BS)
    return jnp.transpose(tiles, (0, 2, 1, 3)).reshape(-1, BS, BS)


def from_blocks(blocks, row_count, col_count):
    tiles = blocks.reshape(row_count // BS, col_count // BS, BS, BS)
    return jnp.transpose(tiles, (0, 2, 1, 3)).reshape(row_count, col_count)


def split_blocks(natural, shapes):
    matrices = []
    offset = 0
    for row_count, col_count in shapes:
        amount = row_count // BS * (col_count // BS)
        matrices.append(from_blocks(natural[offset : offset + amount], row_count, col_count))
        offset = offset + amount
    return matrices


def split_vector(vector, half_d, half_f):
    pieces = [vector[which * half_d : (which + 1) * half_d] for which in range(13)]
    pieces.append(vector[13 * half_d : 13 * half_d + half_f])
    return pieces


def dot_plain(former, latter):
    return jnp.dot(former, latter, preferred_element_type=jnp.float32)


def dot_rows(former, latter):
    return lax.dot_general(
        former, latter, (((1,), (1,)), ((), ())), preferred_element_type=jnp.float32
    )


def dot_cols(former, latter):
    return lax.dot_general(
        former, latter, (((0,), (0,)), ((), ())), preferred_element_type=jnp.float32
    )


def exact_gelu(operand):
    return jax.nn.gelu(operand, approximate=False)


def feature_gather(operand):
    return lax.all_gather(operand, "mp", axis=1, tiled=True)


def head_sum(operand):
    return lax.psum_scatter(
        operand.astype(jnp.bfloat16), "mp", scatter_dimension=1, tiled=True
    ).astype(jnp.float32)


def row_sums(former, latter):
    return lax.psum((jnp.sum(former, axis=1), jnp.sum(latter, axis=1)), "mp")


def route_rows(former, latter, ordering):
    device_count = lax.axis_size(("rep", "shard"))
    former_cut = former.reshape(
        former.shape[0], device_count, former.shape[1] // device_count, former.shape[2]
    )
    latter_cut = latter.reshape(
        latter.shape[0], device_count, latter.shape[1] // device_count, latter.shape[2]
    )
    former_all, latter_all = (
        lax.all_to_all(former_cut, ("rep", "shard"), split_axis=1, concat_axis=0, tiled=True),
        lax.all_to_all(latter_cut, ("rep", "shard"), split_axis=1, concat_axis=0, tiled=True),
    )
    former_moved = jnp.take(former_all, ordering, axis=0)
    latter_moved = jnp.take(latter_all, ordering, axis=0)
    former_back, latter_back = (
        lax.all_to_all(former_moved, ("rep", "shard"), split_axis=0, concat_axis=1, tiled=True),
        lax.all_to_all(latter_moved, ("rep", "shard"), split_axis=0, concat_axis=1, tiled=True),
    )
    return (
        former_back.reshape(former_back.shape[0], -1, former_back.shape[3]),
        latter_back.reshape(latter_back.shape[0], -1, latter_back.shape[3]),
    )


def norm_forward(operand, gain, shift, model_width):
    sum_plain, sum_square = row_sums(operand, operand * operand)
    center = sum_plain / model_width
    inv_std = lax.rsqrt(sum_square / model_width - center * center + eps_norm)
    normed = (operand - center[:, None]) * inv_std[:, None]
    return (normed * gain + shift, normed, inv_std)


def norm_backward(grad_out, normed, inv_std, gain, model_width):
    scaled = grad_out * gain
    sum_plain, sum_cross = row_sums(scaled, scaled * normed)
    grad_in = inv_std[:, None] * (
        scaled - sum_plain[:, None] / model_width - normed * (sum_cross[:, None] / model_width)
    )
    return (grad_in, jnp.sum(grad_out * normed, axis=0), jnp.sum(grad_out, axis=0))


def allowed_keys(block_rows, key_count, limit, causal):
    key_pos = jnp.arange(key_count)
    allowed = key_pos[None, :] < limit
    if causal:
        allowed = allowed & (key_pos[None, :] <= jnp.arange(block_rows)[:, None])
    return allowed


def attend_forward(q_low, k_low, v_low, limit, causal):
    seq_len = q_low.shape[0]
    key_count = k_low.shape[0]
    head_count = q_low.shape[1] // HEAD_DIM
    block_rows = min(512, seq_len)
    scale = HEAD_DIM ** (-0.5)
    q_heads = q_low.reshape(seq_len, head_count, HEAD_DIM)
    k_heads = k_low.reshape(key_count, head_count, HEAD_DIM)
    v_heads = v_low.reshape(key_count, head_count, HEAD_DIM)
    allowed = allowed_keys(block_rows, key_count, limit, causal)
    scores = (
        jnp.einsum("qhd,khd->hqk", q_heads, k_heads, preferred_element_type=jnp.float32) * scale
    )
    scores = jnp.where(allowed[None], scores, masked_score)
    top_score = jnp.max(scores, axis=-1, keepdims=True)
    expo = jnp.exp(scores - top_score)
    row_total = jnp.sum(expo, axis=-1, keepdims=True)
    probs = (expo / row_total).astype(jnp.bfloat16)
    results = jnp.einsum("hqk,khd->qhd", probs, v_heads, preferred_element_type=jnp.float32)
    totals = top_score + jnp.log(row_total)
    return (results.reshape(seq_len, -1), totals)


def attend_backward(q_low, k_low, v_low, log_total, d_out, limit, causal):
    seq_len = q_low.shape[0]
    key_count = k_low.shape[0]
    head_count = q_low.shape[1] // HEAD_DIM
    block_rows = min(512, seq_len)
    scale = HEAD_DIM ** (-0.5)
    q_heads = q_low.reshape(seq_len, head_count, HEAD_DIM)
    k_heads = k_low.reshape(key_count, head_count, HEAD_DIM)
    v_heads = v_low.reshape(key_count, head_count, HEAD_DIM)
    d_heads = d_out.reshape(seq_len, head_count, HEAD_DIM)
    allowed = allowed_keys(block_rows, key_count, limit, causal)
    scores = (
        jnp.einsum("qhd,khd->hqk", q_heads, k_heads, preferred_element_type=jnp.float32) * scale
    )
    scores = jnp.where(allowed[None], scores, masked_score)
    probs = jnp.exp(scores - log_total)
    d_value = jnp.einsum(
        "hqk,qhd->khd", probs.astype(jnp.bfloat16), d_heads, preferred_element_type=jnp.float32
    )
    d_probs = jnp.einsum("qhd,khd->hqk", d_heads, v_heads, preferred_element_type=jnp.float32)
    d_scores = (probs * (d_probs - jnp.sum(probs * d_probs, axis=-1, keepdims=True))).astype(
        jnp.bfloat16
    )
    d_query = (
        jnp.einsum("hqk,khd->qhd", d_scores, k_heads, preferred_element_type=jnp.float32) * scale
    )
    d_key = (
        jnp.einsum("hqk,qhd->khd", d_scores, q_heads, preferred_element_type=jnp.float32) * scale
    )
    return (
        d_query.reshape(seq_len, -1),
        d_key.reshape(key_count, -1),
        d_value.reshape(key_count, -1),
    )


def unpack(stored, inverse, shapes, half_d, half_f):
    blocks, vector = stored
    natural = jnp.take(blocks[0], inverse, axis=0)
    matrices = split_blocks(natural, shapes)
    vector_parts = [piece.astype(jnp.float32) for piece in split_vector(vector[0], half_d, half_f)]
    return (matrices, vector_parts)


def per_device(
    inputs,
    encoded,
    cotangent,
    lengths,
    seq_slots,
    block_slots,
    weights,
    left_stat,
    right_stat,
    left_root,
    right_root,
    vectors,
    vec_stat,
):
    micro_count = inputs.shape[0]
    half_d = inputs.shape[2]
    model_width = D
    half_f = FF * half_d // D
    shapes = layouts(model_width, half_d, half_f)
    seq_total = seq_slots.shape[0]
    block_total = block_slots.shape[0]
    source = (
        jnp.zeros((seq_total,), jnp.int32).at[seq_slots].set(jnp.arange(seq_total, dtype=jnp.int32))
    )
    inverse = (
        jnp.zeros((block_total,), jnp.int32)
        .at[block_slots]
        .set(jnp.arange(block_total, dtype=jnp.int32))
    )
    my_slots = lax.axis_index(("rep", "shard")) * micro_count + jnp.arange(
        micro_count, dtype=jnp.int32
    )
    my_lengths = jnp.take(lengths, jnp.take(source, my_slots))
    token_rows, state_rows = route_rows(inputs, encoded, source)
    weights_low = weights.astype(jnp.bfloat16)
    vectors_low = vectors.astype(jnp.bfloat16)
    gradients = [jnp.zeros(shape_pair, jnp.float32) for shape_pair in shapes]
    vec_grads = [jnp.zeros((half_d,), jnp.float32) for which in range(13)] + [
        jnp.zeros((half_f,), jnp.float32)
    ]
    results = []
    input_grads = []
    state_grads = []
    for micro_index in range(micro_count):
        stored = (
            lax.all_gather(weights_low, "shard", axis=1, tiled=True),
            lax.all_gather(vectors_low, "shard", axis=1, tiled=True),
        )
        matrices, vector_parts = unpack(stored, inverse, shapes, half_d, half_f)
        w_sq, w_sk, w_sv, w_so, w_cq, w_ck, w_cv, w_co, w_fi, w_fo = matrices
        (
            b_sq,
            b_sv,
            b_so,
            g_one,
            b_one,
            b_cq,
            b_cv,
            b_co,
            g_two,
            b_two,
            b_fo,
            g_three,
            b_three,
            b_fi,
        ) = vector_parts
        seq_len = my_lengths[micro_index]
        x_half = token_rows[micro_index]
        x_full = feature_gather(x_half)
        q_self = (dot_plain(x_full, w_sq) + b_sq).astype(jnp.bfloat16)
        k_self = dot_plain(x_full, w_sk).astype(jnp.bfloat16)
        v_self = (dot_plain(x_full, w_sv) + b_sv).astype(jnp.bfloat16)
        o_self, lse_self = attend_forward(q_self, k_self, v_self, seq_len, True)
        o_self = o_self.astype(jnp.bfloat16)
        z_one = x_half.astype(jnp.float32) + head_sum(dot_plain(o_self, w_so)) + b_so
        h_one, n_one, r_one = norm_forward(z_one, g_one, b_one, model_width)
        h_one_full = feature_gather(h_one.astype(jnp.bfloat16))
        e_full = feature_gather(state_rows[micro_index])
        key_count = e_full.shape[0]
        q_cross = (dot_plain(h_one_full, w_cq) + b_cq).astype(jnp.bfloat16)
        k_cross = dot_plain(e_full, w_ck).astype(jnp.bfloat16)
        v_cross = (dot_plain(e_full, w_cv) + b_cv).astype(jnp.bfloat16)
        o_cross, lse_cross = attend_forward(q_cross, k_cross, v_cross, key_count, False)
        o_cross = o_cross.astype(jnp.bfloat16)
        z_two = h_one + head_sum(dot_plain(o_cross, w_co)) + b_co
        h_two, n_two, r_two = norm_forward(z_two, g_two, b_two, model_width)
        h_two_full = feature_gather(h_two.astype(jnp.bfloat16))
        hidden = dot_plain(h_two_full, w_fi) + b_fi
        active, gelu_back = jax.vjp(exact_gelu, hidden)
        active_low = active.astype(jnp.bfloat16)
        z_three = h_two + head_sum(dot_plain(active_low, w_fo)) + b_fo
        h_three, n_three, r_three = norm_forward(z_three, g_three, b_three, model_width)
        live_rows = (jnp.arange(x_half.shape[0]) < seq_len).astype(jnp.float32)[:, None]
        results.append((h_three * live_rows).astype(jnp.bfloat16))
        stored = (
            lax.all_gather(weights_low, "shard", axis=1, tiled=True),
            lax.all_gather(vectors_low, "shard", axis=1, tiled=True),
        )
        matrices, vector_parts = unpack(stored, inverse, shapes, half_d, half_f)
        w_sq, w_sk, w_sv, w_so, w_cq, w_ck, w_cv, w_co, w_fi, w_fo = matrices
        (
            b_sq,
            b_sv,
            b_so,
            g_one,
            b_one,
            b_cq,
            b_cv,
            b_co,
            g_two,
            b_two,
            b_fo,
            g_three,
            b_three,
            b_fi,
        ) = vector_parts
        grad_y = cotangent[micro_index].astype(jnp.float32) * live_rows
        d_three, dg_three, db_three = norm_backward(grad_y, n_three, r_three, g_three, model_width)
        a_three = feature_gather(d_three.astype(jnp.bfloat16))
        gradients[9] = gradients[9] + dot_cols(active_low, a_three)
        d_hidden = gelu_back(dot_rows(a_three, w_fo))[0].astype(jnp.bfloat16)
        gradients[8] = gradients[8] + dot_cols(h_two_full, d_hidden)
        d_h_two = d_three + head_sum(dot_rows(d_hidden, w_fi))
        d_two, dg_two, db_two = norm_backward(d_h_two, n_two, r_two, g_two, model_width)
        a_two = feature_gather(d_two.astype(jnp.bfloat16))
        gradients[7] = gradients[7] + dot_cols(o_cross, a_two)
        d_oc = dot_rows(a_two, w_co).astype(jnp.bfloat16)
        dq_c, dk_c, dv_c = attend_backward(
            q_cross, k_cross, v_cross, lse_cross, d_oc, key_count, False
        )
        dq_c = dq_c.astype(jnp.bfloat16)
        dk_c = dk_c.astype(jnp.bfloat16)
        dv_c = dv_c.astype(jnp.bfloat16)
        gradients[4] = gradients[4] + dot_cols(h_one_full, dq_c)
        gradients[5] = gradients[5] + dot_cols(e_full, dk_c)
        gradients[6] = gradients[6] + dot_cols(e_full, dv_c)
        d_h_one = d_two + head_sum(dot_rows(dq_c, w_cq))
        state_grads.append(
            head_sum(dot_rows(dk_c, w_ck) + dot_rows(dv_c, w_cv)).astype(jnp.bfloat16)
        )
        d_one, dg_one, db_one = norm_backward(d_h_one, n_one, r_one, g_one, model_width)
        a_one = feature_gather(d_one.astype(jnp.bfloat16))
        gradients[3] = gradients[3] + dot_cols(o_self, a_one)
        d_os = dot_rows(a_one, w_so).astype(jnp.bfloat16)
        dq_s, dk_s, dv_s = attend_backward(q_self, k_self, v_self, lse_self, d_os, seq_len, True)
        dq_s = dq_s.astype(jnp.bfloat16)
        dk_s = dk_s.astype(jnp.bfloat16)
        dv_s = dv_s.astype(jnp.bfloat16)
        gradients[0] = gradients[0] + dot_cols(x_full, dq_s)
        gradients[1] = gradients[1] + dot_cols(x_full, dk_s)
        gradients[2] = gradients[2] + dot_cols(x_full, dv_s)
        back_sum = head_sum(dot_rows(dq_s, w_sq) + dot_rows(dk_s, w_sk) + dot_rows(dv_s, w_sv))
        input_grads.append((d_one + back_sum).astype(jnp.bfloat16))
        increments = (
            jnp.sum(dq_s.astype(jnp.float32), axis=0),
            jnp.sum(dv_s.astype(jnp.float32), axis=0),
            jnp.sum(d_one, axis=0),
            dg_one,
            db_one,
            jnp.sum(dq_c.astype(jnp.float32), axis=0),
            jnp.sum(dv_c.astype(jnp.float32), axis=0),
            jnp.sum(d_two, axis=0),
            dg_two,
            db_two,
            jnp.sum(d_three, axis=0),
            dg_three,
            db_three,
            jnp.sum(d_hidden.astype(jnp.float32), axis=0),
        )
        vec_grads = [vec_grads[which] + increments[which] for which in range(14)]
    natural = jnp.concatenate([to_blocks(gradient) for gradient in gradients])
    dealt = jnp.take(natural, block_slots, axis=0)
    vec_total = jnp.concatenate(vec_grads)
    owned, vec_owned = (
        lax.psum_scatter(dealt, "shard", scatter_dimension=0, tiled=True),
        lax.psum_scatter(vec_total, "shard", scatter_dimension=0, tiled=True),
    )
    owned, vec_owned = (
        lax.psum(owned.astype(jnp.bfloat16), "rep").astype(jnp.float32),
        lax.psum(vec_owned.astype(jnp.bfloat16), "rep").astype(jnp.float32),
    )
    highest = lax.Precision.HIGHEST
    left_new = 0.5 * left_stat[0] + 0.5 * jnp.einsum(
        "nij,nkj->nik", owned, owned, precision=highest
    )
    right_new = 0.5 * right_stat[0] + 0.5 * jnp.einsum(
        "nji,njk->nik", owned, owned, precision=highest
    )
    inner = jnp.einsum("nij,njk->nik", owned, right_root[0], precision=highest)
    direction = jnp.einsum("nij,njk->nik", left_root[0], inner, precision=highest)
    spread = jnp.sqrt(jnp.mean(direction * direction, axis=(1, 2), keepdims=True) + 1e-06)
    weights_new = weights[0] - D ** (-0.5) * direction / spread
    vec_stat_new = 0.5 * vec_stat[0] + 0.5 * vec_owned * vec_owned
    vectors_new = vectors[0] - 0.1 * vec_owned * lax.rsqrt(vec_stat_new)
    input_back, state_back = route_rows(jnp.stack(input_grads), jnp.stack(state_grads), seq_slots)
    return (
        jnp.stack(results),
        input_back,
        state_back,
        owned[None],
        left_new[None],
        right_new[None],
        weights_new[None],
        vec_owned[None],
        vec_stat_new[None],
        vectors_new[None],
    )


def solution(mesh):
    in_specs = (
        P(("rep", "shard"), None, "mp"),
        P(("rep", "shard"), None, "mp"),
        P(("rep", "shard"), None, "mp"),
        P(),
        P(),
        P(),
        P("mp", "shard", None, None),
        P("mp", "shard", None, None),
        P("mp", "shard", None, None),
        P("mp", "shard", None, None),
        P("mp", "shard", None, None),
        P("mp", "shard"),
        P("mp", "shard"),
    )
    out_specs = (
        P(("rep", "shard"), None, "mp"),
        P(("rep", "shard"), None, "mp"),
        P(("rep", "shard"), None, "mp"),
        P("mp", "shard", None, None),
        P("mp", "shard", None, None),
        P("mp", "shard", None, None),
        P("mp", "shard", None, None),
        P("mp", "shard"),
        P("mp", "shard"),
        P("mp", "shard"),
    )
    return jax.shard_map(
        per_device, mesh=mesh, in_specs=in_specs, out_specs=out_specs, check_vma=False
    )
```

profile of v0, /device:TPU:0, one launch (start us, length us, event | category | flops | bytes accessed | tf_op | source)
XLA Modules:
  0.0 1590.3 jit_solution(4674921074078943311)
XLA Ops:
  7.2 3.8 bitcast_convert_fusion
  12.2 8.5 all-to-all-start
  21.4 48.5 %all-to-all-done = bf16[2,16,32,512]{3,2,0,1:T(8,128)(2,1)S(1)} async-done(((bf16[2,16,32,512]{3,2,0,1:T(8,128)(2,1)}), bf16[2,16,32,512]{3,2,0,1:T(8,128)(2,1)S(1)}, u32[]{:S(2)}, u32[]{:S(2)}) %all-to-all-start) | async-done | bytes 1048608 | tf_op jit(solution)/shard_map/all_to_all | solution.py:101
  71.7 7.8 all-to-all-start.1
  83.6 43.5 %all-to-all-done.1 = bf16[32,1,32,512]{3,2,1,0:T(8,128)(2,1)S(1)} async-done(((bf16[32,1,32,512]{3,2,1,0:T(8,128)(2,1)}), bf16[32,1,32,512]{3,2,1,0:T(8,128)(2,1)S(1)}, u32[]{:S(2)}, u32[]{:S(2)}) %all-to-all-start.1) | async-done | bytes 1048608 | tf_op jit(solution)/shard_map/all_to_all | solution.py:107
  130.6 36.2 %all-reduce = bf16[8704]{0:T(1024)(128)(2,1)S(1)} all-reduce(bf16[8704]{0:T(1024)(128)(2,1)S(1)} %dynamic-update-slice), channel_id=1, replica_groups=mesh['rep'=2,'shard'=8,'mp'=2] {'shard'}, use_global_device_ids=true, to_apply=%add | all-reduce | flops 8704 | bytes 34816
  169.1 113.5 %all-gather.16.cloned.1.call-done = bf16[1,128,256,256]{3,2,0,1:T(8,128)(2,1)} async-done(((bf16[1,16,256,256]{3,2,0,1:T(8,128)(2,1)}), bf16[1,128,256,256]{3,2,0,1:T(8,128)(2,1)}) %all-gather.16.cloned.1.call-update) | async-done | bytes 16777232 | tf_op jit(solution)/shard_map/all_gather | solution.py:254
  282.6 14.2 gather_fusion.2
  296.9 8.8 broadcast_select_fusion.1
  308.4 4.4 copy-done.5
  345.7 13.7 all_to_all.132
  408.9 12.4 reduce-scatter.24.cloned.1.call-done
  421.4 3.8 fusion.113
  431.1 5.1 fusion.126
  442.2 7.8 copy.167
  450.0 6.0 copy.233
  456.1 6.9 fusion.135
  462.9 24.2 %multiply_convert_fusion.3 = (bf16[512,2048]{1,0:T(8,128)(2,1)S(1)}, f32[512,2048]{1,0:T(8,128)}, bf16[512,2048]{1,0:T(8,128)(2,1)}, f32[512,2048]{1,0:T(8,128)}, f32[512,2048]{1,0:T(8,128)}) fusion(f32[2048]{0:T(1024)S(1)} %bitcast.704, f32[512,2048]{1,0:T(8,128)} %fusion.135, bf16[512,1024]{1,0:T(8,128)(2,1)} %all-gather.20.cloned.1.call-done, ...), kind=kOutput, calls=%fused_computation.67 | convolution fusion | flops 2285895680 | bytes 26222592 | tf_op jit(solution)/shard_map/dot_general | solution.py:59
  491.9 6.2 convolution_convert_fusion.8
  501.6 11.8 reduce-scatter.26.cloned.1.call-done
  513.4 3.7 fusion.112
  525.3 3.9 fusion.122
  530.3 9.3 all-gather.28.cloned.1.call-done
  539.6 6.9 fusion.136
  546.5 4.7 all-gather.34.cloned.1.call-done
  551.2 14.3 convert_reduce_fusion
  570.3 6.2 convolution_convert_fusion.7
  579.9 12.2 reduce-scatter.28.cloned.1.call-done
  598.1 3.7 fusion.118
  602.8 7.7 fusion.151
  619.2 10.7 convolution_add_fusion.1
  630.0 5.7 fusion.152
  644.4 10.1 convolution_add_fusion
  654.5 7.5 copy.234
  662.0 5.9 copy.200
  667.9 11.0 reshape.640
  678.9 8.3 copy.201
  703.6 3.9 fusion.117
  709.5 3.6 convolution_add_fusion.9
  724.2 3.7 reshape.632
  751.3 5.5 multiply_reduce_fusion
  766.8 5.5 multiply_reduce_fusion.1
  804.1 5.6 convert_reduce_fusion.5
  814.9 3.7 reshape.626
  849.6 4.3 constant_dynamic-update-slice_fusion.1
  854.2 3.8 constant_dynamic-update-slice_fusion
  858.0 23.6 %gather_fusion = f32[128,256,256]{2,1,0:T(8,128)} fusion(f32[128,256,256]{2,1,0:T(8,128)} %constant_dynamic-update-slice_fusion, s32[1024]{0:T(1024)} %get-tuple-element.260), kind=kCustom, calls=%fused_computation.7 | custom fusion | bytes 67109376 | tf_op jit(solution)/shard_map/jit(_take)/gather | solution.py:380
  881.6 23.0 %broadcast_select_fusion = f32[128,256,256]{2,1,0:T(8,128)} fusion(f32[128,256,256]{2,1,0:T(8,128)} %gather_fusion, pred[128]{0:T(512)(128)(4,1)S(1)} %copy-done.203), kind=kLoop, calls=%fused_computation.10 | loop fusion | flops 8388608 | bytes 67108992 | tf_op jit(solution)/shard_map/jit(_take)/select_n | solution.py:380
  906.5 6.8 all-to-all-start.6
  913.4 16.5 %all-to-all-done.6 = bf16[2,16,8,512]{3,2,0,1:T(8,128)(2,1)S(1)} async-done(((bf16[2,16,8,512]{3,2,0,1:T(8,128)(2,1)}), bf16[2,16,8,512]{3,2,0,1:T(8,128)(2,1)S(1)}, u32[]{:S(2)}, u32[]{:S(2)}) %all-to-all-start.6) | async-done | bytes 262176 | tf_op jit(solution)/shard_map/all_to_all | solution.py:102
  931.3 3.9 all-to-all-start.7
  938.8 12.3 all-to-all-done.7
  951.2 4.6 all-to-all-start.4
  956.0 5.7 copy.203
  964.7 37.5 %all-to-all-done.4 = bf16[2,16,32,512]{3,2,0,1:T(8,128)(2,1)S(1)} async-done(((bf16[2,16,32,512]{3,2,0,1:T(8,128)(2,1)}), bf16[2,16,32,512]{3,2,0,1:T(8,128)(2,1)S(1)}, u32[]{:S(2)}, u32[]{:S(2)}) %all-to-all-start.4) | async-done | bytes 1048608 | tf_op jit(solution)/shard_map/all_to_all | solution.py:101
  1002.8 473.1 %reduce-scatter.44.cloned.1.call-done = f32[16,256,256]{2,1,0:T(8,128)} async-done(((f32[128,256,256]{2,1,0:T(8,128)}), f32[16,256,256]{2,1,0:T(8,128)}) %reduce-scatter.44.cloned.1.call-update) | async-done | bytes 4194320 | tf_op jit(solution)/shard_map/reduce_scatter | solution.py:383
  1475.9 3.8 convert_element_type.668
  1480.9 4.7 all-to-all-start.5
  1485.9 49.3 %all-reduce.1 = bf16[8704]{0:T(1024)(128)(2,1)S(1)} all-reduce(f32[8704]{0:T(1024)S(1)} %add_dynamic-update-slice_fusion), channel_id=17, replica_groups=mesh['rep'=2,'shard'=8,'mp'=2] {'shard'}, use_global_device_ids=true, to_apply=%region_107.112.clone | all-reduce | flops 8704 | bytes 52224
  1535.2 5.1 psum.207
  1543.2 10.1 all-reduce.10.cloned.1.call-done
  1553.3 6.6 fusion.13
  1560.0 5.4 multiply_reduce_fusion.2
  1568.2 5.5 copy.205
  (779 shorter events, 315.4 us)
Async XLA Ops:
  7.2 74.6 %copy-start = (s32[32]{0:T(128)S(1)}, s32[32]{0:T(128)}, u32[]{:S(2)}) copy-start(s32[32]{0:T(128)} %param.24) | copy-start | bytes 388
  7.2 275.4 %all-gather.16.cloned.1.call-start = ((), (), s32[]{:S(2)}) async-start(), calls=%async_computation.24 | async-start | bytes 18874368 | tf_op jit(solution)/shard_map/all_gather | solution.py:254
  12.2 68.0 %copy-start.207 = (s32[128]{0:T(128)S(1)}, s32[128]{0:T(128)}, u32[]{:S(2)}) copy-start(s32[128]{0:T(128)} %param.26) | copy-start | bytes 1540
  12.2 57.7 %all-to-all-start = ((bf16[2,16,32,512]{3,2,0,1:T(8,128)(2,1)}), bf16[2,16,32,512]{3,2,0,1:T(8,128)(2,1)S(1)}, u32[]{:S(2)}, u32[]{:S(2)}) async-start(bf16[2,16,32,512]{3,2,0,1:T(8,128)(2,1)} %copy.149), calls=%async_computation | async-start | bytes 2097152 | tf_op jit(solution)/shard_map/all_to_all | solution.py:101
  20.7 62.9 %copy-start.170 = (f32[1,1088]{1,0:T(1,128)S(1)}, f32[1,1088]{1,0:T(1,128)}, u32[]{:S(2)}) copy-start(f32[1,1088]{1,0:T(1,128)} %param.32) | copy-start | bytes 13060
  20.7 49.2 %copy-start.204 = (s32[32]{0:T(128)}, s32[32]{0:T(128)S(1)}, u32[]{:S(2)}) copy-start(s32[32]{0:T(128)S(1)} %compare_select_fusion.5) | copy-start | bytes 388
  70.5 58.5 %copy-start.201 = (u32[32]{0:T(128)S(1)}, u32[32]{0:T(128)}, u32[]{:S(2)}) copy-start(u32[32]{0:T(128)} %constant.200) | copy-start | bytes 388
  71.7 55.5 %all-to-all-start.1 = ((bf16[32,1,32,512]{3,2,1,0:T(8,128)(2,1)}), bf16[32,1,32,512]{3,2,1,0:T(8,128)(2,1)S(1)}, u32[]{:S(2)}, u32[]{:S(2)}) async-start(bf16[32,1,32,512]{3,2,1,0:T(8,128)(2,1)} %fusion.86), calls=%async_computation.1 | async-start | bytes 2097152 | tf_op jit(solution)/shard_map/all_to_all | solution.py:107
  79.4 239.4 %all-gather.14.cloned.1.call-start = ((), (), s32[]{:S(2)}) async-start(), calls=%async_computation.23 | async-start | bytes 1572864 | tf_op jit(solution)/shard_map/all_gather | solution.py:79
  128.3 204.1 %all-gather.22.cloned.1.call-start = ((), (), s32[]{:S(2)}) async-start(), calls=%async_computation.30 | async-start | bytes 1572864 | tf_op jit(solution)/shard_map/all_gather | solution.py:79
  168.1 200.7 %copy-start.164 = (f32[1,512]{1,0:T(1,128)}, f32[1,512]{1,0:T(1,128)S(1)}, u32[]{:S(2)}) copy-start(f32[1,512]{1,0:T(1,128)S(1)} %get-tuple-element.180) | copy-start | bytes 6148
  168.1 200.7 %copy-start.167 = (f32[1,512]{1,0:T(1,128)}, f32[1,512]{1,0:T(1,128)S(1)}, u32[]{:S(2)}) copy-start(f32[1,512]{1,0:T(1,128)S(1)} %get-tuple-element.179) | copy-start | bytes 6148
  168.1 209.8 %copy-start.169 = (f32[1,512]{1,0:T(1,128)}, f32[1,512]{1,0:T(1,128)S(1)}, u32[]{:S(2)}) copy-start(f32[1,512]{1,0:T(1,128)S(1)} %get-tuple-element.178) | copy-start | bytes 6148
  168.1 253.3 %copy-start.146 = (f32[1,512]{1,0:T(1,128)}, f32[1,512]{1,0:T(1,128)S(1)}, u32[]{:S(2)}) copy-start(f32[1,512]{1,0:T(1,128)S(1)} %get-tuple-element.181) | copy-start | bytes 6148
  169.1 195.3 %reduce-scatter.16.cloned.1.call-start = ((), (), s32[]{:S(2)}) async-start(), calls=%async_computation.25 | async-start | bytes 1572864 | tf_op jit(solution)/shard_map/reduce_scatter | solution.py:83
  314.1 24.0 %copy-start.33 = (bf16[128,8,2,256]{3,1,2,0:T(8,128)(2,1)}, bf16[128,8,2,256]{3,1,2,0:T(8,128)(2,1)S(1)}, u32[]{:S(2)}) copy-start(bf16[128,8,2,256]{3,1,2,0:T(8,128)(2,1)S(1)} %copy.224) | copy-start | bytes 3145732
  316.8 17.6 %copy-start.24 = (bf16[128,8,2,256]{3,1,2,0:T(8,128)(2,1)}, bf16[128,8,2,256]{3,1,2,0:T(8,128)(2,1)S(1)}, u32[]{:S(2)}) copy-start(bf16[128,8,2,256]{3,1,2,0:T(8,128)(2,1)S(1)} %copy.226) | copy-start | bytes 3145732
  332.1 32.3 %reduce-scatter.22.cloned.1.call-start = ((), (), s32[]{:S(2)}) async-start(), calls=%async_computation.31 | async-start | bytes 1572864 | tf_op jit(solution)/shard_map/reduce_scatter | solution.py:83
  343.2 21.2 %copy-start.13 = (bf16[1,16,1,32,512]{4,3,0,1,2:T(8,128)(2,1)S(1)}, bf16[1,16,1,32,512]{4,3,0,1,2:T(8,128)(2,1)}, u32[]{:S(2)}) copy-start(bf16[1,16,1,32,512]{4,3,0,1,2:T(8,128)(2,1)} %get-tuple-element.167) | copy-start | bytes 1572868
  343.2 21.2 %copy-start.15 = (bf16[1,16,1,32,512]{4,3,0,1,2:T(8,128)(2,1)S(1)}, bf16[1,16,1,32,512]{4,3,0,1,2:T(8,128)(2,1)}, u32[]{:S(2)}) copy-start(bf16[1,16,1,32,512]{4,3,0,1,2:T(8,128)(2,1)} %get-tuple-element.168) | copy-start | bytes 1572868
  359.4 17.2 %copy-start.67 = (bf16[8,256,256]{2,1,0:T(8,128)(2,1)S(1)}, bf16[8,256,256]{2,1,0:T(8,128)(2,1)}, u32[]{:S(2)}) copy-start(bf16[8,256,256]{2,1,0:T(8,128)(2,1)} %get-tuple-element.157) | copy-start | bytes 3145732
  360.8 12.7 all-to-all-start.3
  364.3 22.7 %all-gather.18.cloned.1.call-start = ((), (), s32[]{:S(2)}) async-start(), calls=%async_computation.26 | async-start | bytes 1572864 | tf_op jit(solution)/shard_map/all_gather | solution.py:79
  368.7 52.6 %copy-start.156 = (f32[512]{0:T(512)}, f32[512]{0:T(512)S(1)}, u32[]{:S(2)}) copy-start(f32[512]{0:T(512)S(1)} %get-tuple-element.217) | copy-start | bytes 6148
  368.8 52.6 %copy-start.158 = (f32[512]{0:T(512)}, f32[512]{0:T(512)S(1)}, u32[]{:S(2)}) copy-start(f32[512]{0:T(512)S(1)} %get-tuple-element.218) | copy-start | bytes 6148
  368.8 52.6 %copy-start.160 = (f32[512]{0:T(512)}, f32[512]{0:T(512)S(1)}, u32[]{:S(2)}) copy-start(f32[512]{0:T(512)S(1)} %get-tuple-element.219) | copy-start | bytes 6148
  372.1 28.0 %all-gather.24.cloned.1.call-start = ((), (), s32[]{:S(2)}) async-start(), calls=%async_computation.32 | async-start | bytes 1572864 | tf_op jit(solution)/shard_map/all_gather | solution.py:79
  377.9 17.9 %copy-start.9 = (bf16[128,8,2,256]{3,1,2,0:T(8,128)(2,1)}, bf16[128,8,2,256]{3,1,2,0:T(8,128)(2,1)S(1)}, u32[]{:S(2)}) copy-start(bf16[128,8,2,256]{3,1,2,0:T(8,128)(2,1)S(1)} %copy.228) | copy-start | bytes 3145732
  386.9 22.0 %reduce-scatter.18.cloned.1.call-start = ((), (), s32[]{:S(2)}) async-start(), calls=%async_computation.27 | async-start | bytes 1572864 | tf_op jit(solution)/shard_map/reduce_scatter | solution.py:83
  393.4 28.0 %reduce-scatter.24.cloned.1.call-start = ((), (), s32[]{:S(2)}) async-start(), calls=%async_computation.33 | async-start | bytes 1572864 | tf_op jit(solution)/shard_map/reduce_scatter | solution.py:83
  407.4 48.7 %all-gather.26.cloned.1.call-start = ((), (), s32[]{:S(2)}) async-start(), calls=%async_computation.34 | async-start | bytes 1572864 | tf_op jit(solution)/shard_map/all_gather | solution.py:79
  430.3 32.6 %all-gather.20.cloned.1.call-start = ((), (), s32[]{:S(2)}) async-start(), calls=%async_computation.28 | async-start | bytes 1572864 | tf_op jit(solution)/shard_map/all_gather | solution.py:79
  431.1 70.5 %reduce-scatter.20.cloned.1.call-start = ((), (), s32[]{:S(2)}) async-start(), calls=%async_computation.29 | async-start | bytes 1572864 | tf_op jit(solution)/shard_map/reduce_scatter | solution.py:83
  462.9 25.5 %copy-start.70 = (bf16[128,8,8,256]{3,1,2,0:T(8,128)(2,1)S(1)}, bf16[128,8,8,256]{3,1,2,0:T(8,128)(2,1)}, u32[]{:S(2)}) copy-start(bf16[128,8,8,256]{3,1,2,0:T(8,128)(2,1)} %copy.233) | copy-start | bytes 12582916
  491.9 21.5 %reduce-scatter.26.cloned.1.call-start = ((), (), s32[]{:S(2)}) async-start(), calls=%async_computation.35 | async-start | bytes 1572864 | tf_op jit(solution)/shard_map/reduce_scatter | solution.py:83
  491.9 21.5 %copy-start.166 = (f32[1,512]{1,0:T(1,128)S(1)}, f32[1,512]{1,0:T(1,128)}, u32[]{:S(2)}) copy-start(f32[1,512]{1,0:T(1,128)} %get-tuple-element.175) | copy-start | bytes 6148
  491.9 21.5 %copy-start.168 = (f32[1,512]{1,0:T(1,128)S(1)}, f32[1,512]{1,0:T(1,128)}, u32[]{:S(2)}) copy-start(f32[1,512]{1,0:T(1,128)} %get-tuple-element.174) | copy-start | bytes 6148
  491.9 21.5 %copy-start.192 = (f32[1,512]{1,0:T(1,128)S(1)}, f32[1,512]{1,0:T(1,128)}, u32[]{:S(2)}) copy-start(f32[1,512]{1,0:T(1,128)} %get-tuple-element.173) | copy-start | bytes 6148
  498.1 21.5 %copy-start.172 = (f32[1,512]{1,0:T(1,128)S(1)}, f32[1,512]{1,0:T(1,128)}, u32[]{:S(2)}) copy-start(f32[1,512]{1,0:T(1,128)} %get-tuple-element.171) | copy-start | bytes 6148
  498.1 41.4 %all-gather.28.cloned.1.call-start = ((), (), s32[]{:S(2)}) async-start(), calls=%async_computation.36 | async-start | bytes 1572864 | tf_op jit(solution)/shard_map/all_gather | solution.py:79
  529.2 22.0 %all-gather.34.cloned.1.call-start = ((), (), s32[]{:S(2)}) async-start(), calls=%async_computation.42 | async-start | bytes 1572864 | tf_op jit(solution)/shard_map/all_gather | solution.py:79
  529.8 50.1 %reduce-scatter.34.cloned.1.call-start = ((), (), s32[]{:S(2)}) async-start(), calls=%async_computation.43 | async-start | bytes 1572864 | tf_op jit(solution)/shard_map/reduce_scatter | solution.py:83
  570.2 22.0 %reduce-scatter.28.cloned.1.call-start = ((), (), s32[]{:S(2)}) async-start(), calls=%async_computation.37 | async-start | bytes 1572864 | tf_op jit(solution)/shard_map/reduce_scatter | solution.py:83
  576.5 35.7 %all-gather.30.cloned.1.call-start = ((), (), s32[]{:S(2)}) async-start(), calls=%async_computation.38 | async-start | bytes 1572864 | tf_op jit(solution)/shard_map/all_gather | solution.py:79
  601.9 33.9 %all-gather.36.cloned.1.call-start = ((), (), s32[]{:S(2)}) async-start(), calls=%async_computation.44 | async-start | bytes 1572864 | tf_op jit(solution)/shard_map/all_gather | solution.py:79
  610.5 87.0 %reduce-scatter.30.cloned.1.call-start = ((), (), s32[]{:S(2)}) async-start(), calls=%async_computation.39 | async-start | bytes 1572864 | tf_op jit(solution)/shard_map/reduce_scatter | solution.py:83
  619.2 78.4 %reduce-scatter.36.cloned.1.call-start = ((), (), s32[]{:S(2)}) async-start(), calls=%async_computation.45 | async-start | bytes 1572864 | tf_op jit(solution)/shard_map/reduce_scatter | solution.py:83
  644.2 104.8 %all-gather.38.cloned.1.call-start = ((), (), s32[]{:S(2)}) async-start(), calls=%async_computation.46 | async-start | bytes 1572864 | tf_op jit(solution)/shard_map/all_gather | solution.py:79
  709.4 55.3 %all-gather.32.cloned.1.call-start = ((), (), s32[]{:S(2)}) async-start(), calls=%async_computation.40 | async-start | bytes 1572864 | tf_op jit(solution)/shard_map/all_gather | solution.py:79
  717.9 186.7 %reduce-scatter.42.cloned.1.call-start = ((), (), s32[]{:S(2)}) async-start(), calls=%async_computation.49 | async-start | bytes 393216 | tf_op jit(solution)/shard_map/reduce_scatter | solution.py:83
  747.1 157.5 %reduce-scatter.40.cloned.1.call-start = ((), (), s32[]{:S(2)}) async-start(), calls=%async_computation.48 | async-start | bytes 393216 | tf_op jit(solution)/shard_map/reduce_scatter | solution.py:83
  748.9 186.3 %reduce-scatter.38.cloned.1.call-start = ((), (), s32[]{:S(2)}) async-start(), calls=%async_computation.47 | async-start | bytes 1572864 | tf_op jit(solution)/shard_map/reduce_scatter | solution.py:83
  761.0 18.4 %copy-start.59 = (bf16[8,64,512]{2,1,0:T(8,128)(2,1)}, bf16[8,64,512]{2,1,0:T(8,128)(2,1)S(1)}, u32[]{:S(2)}) copy-start(bf16[8,64,512]{2,1,0:T(8,128)(2,1)S(1)} %get-tuple-element.247) | copy-start | bytes 1572868
  762.4 17.8 %copy-start.60 = (bf16[8,64,512]{2,1,0:T(8,128)(2,1)}, bf16[8,64,512]{2,1,0:T(8,128)(2,1)S(1)}, u32[]{:S(2)}) copy-start(bf16[8,64,512]{2,1,0:T(8,128)(2,1)S(1)} %fusion.56) | copy-start | bytes 1572868
  809.8 126.7 %reduce-scatter.32.cloned.1.call-start = ((), (), s32[]{:S(2)}) async-start(), calls=%async_computation.41 | async-start | bytes 1572864 | tf_op jit(solution)/shard_map/reduce_scatter | solution.py:83
  836.3 639.6 %reduce-scatter.44.cloned.1.call-start = ((), (), s32[]{:S(2)}) async-start(), calls=%async_computation.50 | async-start | bytes 37748736 | tf_op jit(solution)/shard_map/reduce_scatter | solution.py:383
  858.0 23.6 %copy-start.203 = (pred[128]{0:T(512)(128)(4,1)S(1)}, pred[128]{0:T(512)(128)(4,1)}, u32[]{:S(2)}) copy-start(pred[128]{0:T(512)(128)(4,1)} %compare_and_fusion.3) | copy-start | bytes 388
  904.6 30.6 %copy-start.32 = (f32[512,512]{1,0:T(8,128)S(1)}, f32[512,512]{1,0:T(8,128)}, u32[]{:S(2)}) copy-start(f32[512,512]{1,0:T(8,128)} %copy-done.31) | copy-start | bytes 3145732
  904.6 31.9 %copy-start.30 = (f32[512,512]{1,0:T(8,128)S(1)}, f32[512,512]{1,0:T(8,128)}, u32[]{:S(2)}) copy-start(f32[512,512]{1,0:T(8,128)} %get-tuple-element.135) | copy-start | bytes 3145732
  906.5 23.4 %all-to-all-start.6 = ((bf16[2,16,8,512]{3,2,0,1:T(8,128)(2,1)}), bf16[2,16,8,512]{3,2,0,1:T(8,128)(2,1)S(1)}, u32[]{:S(2)}, u32[]{:S(2)}) async-start(bf16[2,16,8,512]{3,2,0,1:T(8,128)(2,1)} %pad_maximum_fusion.2), calls=%async_computation.20 | async-start | bytes 524288 | tf_op jit(solution)/shard_map/all_to_all | solution.py:102
  931.3 19.9 %all-to-all-start.7 = ((bf16[32,1,8,512]{3,2,1,0:T(8,128)(2,1)}), bf16[32,1,8,512]{3,2,1,0:T(8,128)(2,1)S(1)}, u32[]{:S(2)}, u32[]{:S(2)}) async-start(bf16[32,1,8,512]{3,2,1,0:T(8,128)(2,1)} %fusion.99), calls=%async_computation.21 | async-start | bytes 524288 | tf_op jit(solution)/shard_map/all_to_all | solution.py:108
  951.2 51.0 %all-to-all-start.4 = ((bf16[2,16,32,512]{3,2,0,1:T(8,128)(2,1)}), bf16[2,16,32,512]{3,2,0,1:T(8,128)(2,1)S(1)}, u32[]{:S(2)}, u32[]{:S(2)}) async-start(bf16[2,16,32,512]{3,2,0,1:T(8,128)(2,1)} %pad_maximum_fusion.1), calls=%async_computation.16 | async-start | bytes 2097152 | tf_op jit(solution)/shard_map/all_to_all | solution.py:101
  956.0 597.4 %all-reduce.10.cloned.1.call-start = ((), (), s32[]{:S(2)}) async-start(), calls=%async_computation.51 | async-start | bytes 4194304 | tf_op jit(solution)/shard_map/psum | solution.py:387
  1480.9 61.3 %all-to-all-start.5 = ((bf16[32,1,32,512]{3,2,1,0:T(8,128)(2,1)}), bf16[32,1,32,512]{3,2,1,0:T(8,128)(2,1)S(1)}, u32[]{:S(2)}, u32[]{:S(2)}) async-start(bf16[32,1,32,512]{3,2,1,0:T(8,128)(2,1)} %fusion.85), calls=%async_computation.17 | async-start | bytes 2097152 | tf_op jit(solution)/shard_map/all_to_all | solution.py:107
  (193 other events, 942.4 us)
Sparse Core Ops, SparseCore 0:
  11.2 271.3 all-gather.15
  284.2 7.2 all-gather.13
  293.0 10.1 all-gather.21
  332.2 6.5 reduce-scatter.15
  345.8 6.6 reduce-scatter.21
  372.2 10.2 all-gather.17
  387.1 9.4 all-gather.23
  399.4 9.5 reduce-scatter.17
  411.8 9.5 reduce-scatter.23
  430.4 10.1 all-gather.25
  442.8 10.1 all-gather.19
  492.0 9.5 reduce-scatter.19
  503.8 9.5 reduce-scatter.25
  529.4 10.1 all-gather.27
  541.0 10.1 all-gather.33
  570.3 9.5 reduce-scatter.33
  582.6 9.5 reduce-scatter.27
  602.0 10.1 all-gather.29
  614.3 10.1 all-gather.35
  626.6 9.5 reduce-scatter.29
  644.3 9.5 reduce-scatter.35
  709.5 10.1 all-gather.37
  721.3 10.1 all-gather.31
  747.2 8.9 reduce-scatter.41
  758.4 8.8 reduce-scatter.39
  809.9 9.5 reduce-scatter.37
  836.4 9.5 reduce-scatter.31
  904.7 571.1 reduce-scatter.43
  1479.9 73.3 all-reduce.9
where the time goes:
time: 1600 us; the launch traced here: 1590 us
  waiting for transfers between devices  815 us (51%)
  matrix products  245 us (15%)
  local copies, waits for them, and re-layouts  235 us (15%)
  blocking collectives  124 us (8%)
  other arithmetic  111 us (7%)
  starting transfers between devices  42.2 us (3%)
  between operations  18.8 us (1%)
    reduce_scatter x1, waiting for transfers between devices, per_device(): lax.psum_scatter(dealt, 'shard', scatter_dimension=0, tiled=True)  473 us
    all_gather x1, waiting for transfers between devices, per_device(): lax.all_gather(weights_low, 'shard', axis=1, tiled=True)  113 us
    all_to_all x2, waiting for transfers between devices, route_rows(): lax.all_to_all(former_cut, ('rep', 'shard'), split_axis=1, concat_axis=0,...  85.9 us
    unnamed x2, blocking collectives  85.4 us
    unnamed x473, local copies, waits for them, and re-layouts  76 us
    reshape x19, local copies, waits for them, and re-layouts, to_blocks(): tiles = matrix.reshape(row_count // BS, BS, col_count // BS, BS)  75.5 us
    dot_general x20, matrix products, dot_cols(): lax.dot_general(former, latter, (((0,), (0,)), ((), ())), preferred_eleme...  67.3 us
    dot_general x20, matrix products, dot_plain(): return jnp.dot(former, latter, preferred_element_type=jnp.float32)  65.8 us
  transfers between devices with their start and end apart: 36, of which 18 were waited for; matrix products, arithmetic and copies ran while one was open for 28% of the time, Pallas kernels for 0%

commit v1 on v0

v1 whole, which is shorter than its diff:
```python
import functools

import jax
import jax.numpy as jnp
from jax import lax
from jax.experimental import pallas as pl
from jax.experimental.pallas import tpu as pltpu
from jax.sharding import PartitionSpec as P

D = 1024
FF = 4096
HEAD_DIM = 64
BS = 256
LANES = 128

eps_norm = 1e-05
masked_score = -1e30
scale = HEAD_DIM**-0.5
bf16 = jnp.bfloat16
f32 = jnp.float32

NT = (((1,), (1,)), ((), ()))
TN = (((0,), (0,)), ((), ()))

VMEM_LIMIT = 60 * 1024 * 1024

ERFC_SLOPE = 0.3
ERFC_POLY = (
    0.1691880090604902,
    0.17071516163759975,
    0.14833963774537734,
    0.21492421686136995,
    -0.09464635292673967,
    0.5477136065073498,
    -0.5122723795383668,
    0.4855603950654946,
    -0.1295223139805042,
)


def dot_nn(a, b):
    return jnp.dot(a, b, preferred_element_type=f32)


def dot_nt(a, b):
    return lax.dot_general(a, b, NT, preferred_element_type=f32)


def dot_tn(a, b):
    return lax.dot_general(a, b, TN, preferred_element_type=f32)


def params(**kw):
    return pltpu.CompilerParams(vmem_limit_bytes=VMEM_LIMIT, **kw)


class Net:
    def __init__(self, n_rep, n_shard, n_mp):
        self.n_rep, self.n_shard, self.n_mp = n_rep, n_shard, n_mp
        bits = []
        b = 1
        while b < n_shard:
            bits.append(b)
            b *= 2
        down = tuple(reversed(bits))
        if len(bits) == 3:
            x, z1, z2 = bits
            self.near_order = ((z2, x, z1), (z2, z1, x))
            self.mid_order = ((z1, z2, x), (z2, x, z1))
        else:
            self.near_order = (down, down)
            self.mid_order = (down[1:] + down[:1], down)
        self.depth = len(bits)

    def swap_core(self, value):
        return lax.ppermute(value, "mp", [(i, i ^ 1) for i in range(self.n_mp)])

    def swap_rep(self, value):
        return lax.ppermute(value, "rep", [(i, i ^ 1) for i in range(self.n_rep)])

    def swap_shard(self, value, order, step):
        pairs = []
        for r in range(self.n_rep):
            for s in range(self.n_shard):
                for m in range(self.n_mp):
                    here = (r * self.n_shard + s) * self.n_mp + m
                    there = (r * self.n_shard + (s ^ order[m][step])) * self.n_mp + m
                    pairs.append((here, there))
        return lax.ppermute(value, ("rep", "shard", "mp"), pairs)


def together(*values):
    return lax.optimization_barrier(values)


def start_of(part, plane, counts):
    nblk, na, _ = counts
    return {
        "own": 0,
        "mid": na,
        "near": plane * (nblk - na),
        "far": (1 - plane) * (nblk - na),
    }[part]


def relative(q, which, order):
    rel = 0
    for s in range(len(order[0])):
        bit = jnp.where(which == 0, order[0][s], order[1][s])
        rel = rel + ((q >> s) & 1) * bit
    return rel


def place_body(scal, tab, *refs, pieces, first, counts):
    nblk, na, total = counts
    many = len(pieces)
    srcs = refs[: 2 * many]
    refs = refs[2 * many :]
    if not first:
        refs = refs[3:]
    sq, fi, fo, buf, s_in, s_out = refs
    me, plane, core = scal[0], scal[1], scal[2]

    base = 0
    for k, (order, position, part) in enumerate(pieces):
        n = srcs[2 * k].shape[0]
        for h in range(2):

            def incoming(i, src=srcs[2 * k + h], at=base + h * n):
                pltpu.make_async_copy(src.at[i], buf.at[at + i], s_in.at[at + i]).start()

            pl.loop(0, n)(incoming)
        base += 2 * n

    base = 0
    for k, (order, position, part) in enumerate(pieces):
        n = srcs[2 * k].shape[0]
        per = n // position[1]
        for h in range(2):

            def outgoing(
                i, src=srcs[2 * k + h], at=base + h * n, which=core if h == 0 else 1 - core
            ):
                pltpu.make_async_copy(src.at[i], buf.at[at + i], s_in.at[at + i]).wait()
                shard = me ^ relative(position[0] + i // per, which, order)
                slot = shard * nblk + start_of(part, plane, counts) + i % per
                row_of = (which * total + slot) * 3
                kind = tab[row_of]
                row = pl.multiple_of(tab[row_of + 1], BS)
                col = pl.multiple_of(tab[row_of + 2], BS)
                for c, dst in enumerate((sq, fi, fo)):

                    @pl.when(kind == c)
                    def _():
                        pltpu.make_async_copy(
                            buf.at[at + i],
                            dst.at[pl.ds(row, BS), pl.ds(col, BS)],
                            s_out.at[at + i],
                        ).start()

            pl.loop(0, n)(outgoing)
        base += 2 * n

    def finish(i):
        pltpu.make_async_copy(
            buf.at[i], sq.at[pl.ds(0, BS), pl.ds(0, BS)], s_out.at[i]
        ).wait()

    pl.loop(0, base)(finish)


def place(scal, tab, todo, held, counts):
    first = held is None
    shapes = (
        jax.ShapeDtypeStruct((8 * D, D), bf16),
        jax.ShapeDtypeStruct((D, FF), bf16),
        jax.ShapeDtypeStruct((FF, D), bf16),
    )
    anyspec = pl.BlockSpec(memory_space=pl.ANY)
    smem = pl.BlockSpec(memory_space=pltpu.SMEM)
    values = [v for item in todo for v in item[:2]]
    pieces = [item[2:] for item in todo]
    n = sum(v.shape[0] for v in values)
    ins = [scal, tab] + values + ([] if first else list(held))
    at = 2 + len(values)
    return pl.pallas_call(
        functools.partial(place_body, pieces=pieces, first=first, counts=counts),
        out_shape=shapes,
        in_specs=[smem, smem] + [anyspec] * (len(ins) - 2),
        out_specs=(anyspec,) * 3,
        scratch_shapes=[
            pltpu.VMEM((n, BS, BS), bf16),
            pltpu.SemaphoreType.DMA((n,)),
            pltpu.SemaphoreType.DMA((n,)),
        ],
        input_output_aliases={} if first else {at: 0, at + 1: 1, at + 2: 2},
        compiler_params=pltpu.CompilerParams(vmem_limit_bytes=n * BS * BS * 2 + (2 << 20)),
        cost_estimate=pl.CostEstimate(
            flops=0, bytes_accessed=4 * n * BS * BS, transcendentals=0
        ),
        name="place",
    )(*ins)


def place_table(block_slots, half_d, half_f):
    j = block_slots
    rows_d = D // BS
    cols_h = half_d // BS
    per = rows_d * cols_h
    mid = jnp.minimum(j // per, 7)
    t = j - mid * per
    tall = (mid == 3) | (mid == 7)
    f0 = 8 * per
    cols_f = half_f // BS
    per_f = rows_d * cols_f
    tf = j - f0
    to = tf - per_f
    is_sq, is_fi = j < f0, (j >= f0) & (j < f0 + per_f)
    out = []
    for p in range(D // half_d):
        row_sq = mid * D + jnp.where(tall, p * half_d + (t // rows_d) * BS, (t // cols_h) * BS)
        col_sq = jnp.where(tall, (t % rows_d) * BS, p * half_d + (t % cols_h) * BS)
        row_fi, col_fi = (tf // cols_f) * BS, p * half_f + (tf % cols_f) * BS
        row_fo, col_fo = p * half_f + (to // rows_d) * BS, (to % rows_d) * BS
        kind = jnp.where(is_sq, 0, jnp.where(is_fi, 1, 2))
        row = jnp.where(is_sq, row_sq, jnp.where(is_fi, row_fi, row_fo))
        col = jnp.where(is_sq, col_sq, jnp.where(is_fi, col_fi, col_fo))
        out.append(jnp.stack([kind, row, col], axis=1))
    return jnp.stack(out).astype(jnp.int32).reshape(-1)


def gather_weights(net, scal, tab, low, plane, counts):
    nblk, na, _ = counts
    depth = net.depth
    lag = 1 if na else 0
    cur = {}
    if na:
        cur["near"] = lax.dynamic_slice_in_dim(low, plane * (nblk - na), na, axis=0)
    cur["mid"] = low[na : nblk - na]
    kept = []
    fresh = [(low, net.near_order, (0, 1), "own")]
    waiting = []
    held = None
    last = depth + lag
    for r in range(last):
        todo = []
        moved = []
        if na and r < depth:
            got = net.swap_shard(cur["near"], net.near_order, r)
            moved.append((got, net.near_order, (1 << r, 1 << r), "near"))
        if 0 <= r - lag < depth:
            s = r - lag
            got = net.swap_shard(cur["mid"], net.mid_order, s)
            moved.append((got, net.mid_order, (1 << s, 1 << s), "mid"))
        if na and r == depth - 1:
            across = net.swap_rep(jnp.concatenate(kept) if len(kept) > 1 else kept[0])
            moved.append((across, net.near_order, (1, (1 << (depth - 1)) - 1), "far"))
        if na and r == depth:
            across = net.swap_rep(kept[-1])
            moved.append((across, net.near_order, (1 << (depth - 1), 1 << (depth - 1)), "far"))
        others = [net.swap_core(item[0]) for item in fresh]
        if waiting:
            held = place(scal, tab, waiting, held, counts)
        values = together(*[m[0] for m in moved], *others, *(held or ()))
        moved = [(v,) + m[1:] for v, m in zip(values, moved)]
        others = values[len(moved) : len(moved) + len(fresh)]
        held = values[len(moved) + len(fresh) :] or None
        waiting = [(f[0], o) + f[1:] for f, o in zip(fresh, others)]
        for v, _, position, part in moved:
            if part == "near":
                kept.append(v)
                cur[part] = jnp.concatenate([cur[part], v])
            elif part == "mid":
                cur[part] = jnp.concatenate([cur[part], v])
        fresh = moved
    others = [net.swap_core(item[0]) for item in fresh]
    held = place(scal, tab, waiting, held, counts)
    waiting = [(f[0], o) + f[1:] for f, o in zip(fresh, others)]
    return place(scal, tab, waiting, held, counts)


def deal_body(scal, slots, grads, *refs, pieces, counts):
    nblk, na, _ = counts
    outs = refs[: len(pieces)]
    buf, s_in, s_out = refs[len(pieces) :]
    me, plane, core = scal[0], scal[1], scal[2]
    base = 0
    for out, (order, first, part) in zip(outs, pieces):
        n = out.shape[0]
        per = na if part != "mid" else nblk - 2 * na

        def incoming(i, at=base, order=order, first=first, part=part, per=per):
            shard = me ^ relative(first + i // per, core, order)
            slot = shard * nblk + start_of(part, plane, counts) + i % per
            pltpu.make_async_copy(
                grads.at[slots[slot]], buf.at[at + i], s_in.at[at + i]
            ).start()

        pl.loop(0, n)(incoming)
        base += n
    base = 0
    for out in outs:

        def outgoing(i, at=base, out=out):
            pltpu.make_async_copy(grads.at[0], buf.at[at + i], s_in.at[at + i]).wait()
            pltpu.make_async_copy(buf.at[at + i], out.at[i], s_out.at[at + i]).start()

        pl.loop(0, out.shape[0])(outgoing)
        base += out.shape[0]

    def finish(i):
        pltpu.make_async_copy(buf.at[i], outs[0].at[0], s_out.at[i]).wait()

    pl.loop(0, base)(finish)


def deal(scal, block_slots, grads, pieces, sizes, counts):
    anyspec = pl.BlockSpec(memory_space=pl.ANY)
    smem = pl.BlockSpec(memory_space=pltpu.SMEM)
    n = sum(sizes)
    return pl.pallas_call(
        functools.partial(deal_body, pieces=pieces, counts=counts),
        out_shape=tuple(jax.ShapeDtypeStruct((k, BS, BS), bf16) for k in sizes),
        in_specs=[smem, smem, anyspec],
        out_specs=(anyspec,) * len(sizes),
        scratch_shapes=[
            pltpu.VMEM((n, BS, BS), bf16),
            pltpu.SemaphoreType.DMA((n,)),
            pltpu.SemaphoreType.DMA((n,)),
        ],
        compiler_params=pltpu.CompilerParams(vmem_limit_bytes=n * BS * BS * 2 + (2 << 20)),
        cost_estimate=pl.CostEstimate(
            flops=0, bytes_accessed=4 * n * BS * BS, transcendentals=0
        ),
        name="deal",
    )(scal, block_slots, grads)


def total_of(*terms):
    acc = terms[0].astype(f32)
    for t in terms[1:]:
        acc = acc + t.astype(f32)
    return acc.astype(bf16)


def reduce_gradients(net, scal, grads, plane, block_slots, counts):
    nblk, na, _ = counts
    n = net.n_shard
    depth = net.depth
    cm = nblk - 2 * na
    half = n // 2
    near, mid = net.near_order, net.mid_order
    if na:
        far_send, mid_send = deal(
            scal, block_slots, grads, [(near, half, "far"), (mid, half, "mid")],
            [half * na, half * cm], counts,
        )
        got_far = net.swap_rep(far_send)
        got_mid = net.swap_shard(mid_send, mid, depth - 1)
        far_keep, near_send, near_keep, mid_keep = deal(
            scal, block_slots, grads,
            [(near, 0, "far"), (near, half, "near"), (near, 0, "near"), (mid, 0, "mid")],
            [half * na] * 3 + [half * cm], counts,
        )
        got_far, got_mid, far_keep, near_send, near_keep, mid_keep = together(
            got_far, got_mid, far_keep, near_send, near_keep, mid_keep
        )
        next_near = total_of(near_send, got_far)
        parts_n = [near_keep]
    else:
        mid_send, mid_keep = deal(
            scal, block_slots, grads, [(mid, half, "mid"), (mid, 0, "mid")],
            [half * cm] * 2, counts,
        )
        got_mid = net.swap_shard(mid_send, mid, depth - 1)
    parts_m = [mid_keep, got_mid]
    step_n = depth - 1
    for s in range(depth - 2, -1, -1):
        width = 1 << s
        send_m = total_of(*[p[width * cm :] for p in parts_m])
        keep_m = total_of(*[p[: width * cm] for p in parts_m])
        got = [net.swap_shard(send_m, mid, s)]
        if na:
            got.append(net.swap_shard(next_near, near, step_n))
            if step_n == depth - 1:
                got.append(net.swap_rep(far_keep))
            got = together(*got)
            parts_n = parts_n + list(got[1:])
            low_n = 1 << (step_n - 1)
            next_near = total_of(*[p[low_n * na :] for p in parts_n])
            parts_n = [total_of(*[p[: low_n * na] for p in parts_n])]
            step_n -= 1
        parts_m = [keep_m, got[0]]
    mine = total_of(*parts_m)
    got_m = net.swap_rep(mine)
    if not na:
        return total_of(mine, got_m)
    got_n = net.swap_shard(next_near, near, 0)
    got_m, got_n = together(got_m, got_n)
    summed = total_of(*parts_n, got_n)
    far = net.swap_rep(summed)
    mine = total_of(mine, got_m)
    low_part = jnp.where(plane == 0, summed, far)
    high_part = jnp.where(plane == 0, far, summed)
    return jnp.concatenate([low_part, mine, high_part])


def attend_forward_body(lim, q_ref, k_ref, v_ref, o_ref, lse_ref, *, causal, rows):
    pair = pl.program_id(0)
    seq, keys = q_ref.shape[0], k_ref.shape[0]
    lane = lax.broadcasted_iota(jnp.int32, (1, LANES), 1)
    top = lim[0] - 1

    @pl.when(pair == 0)
    def _():
        lse_ref[...] = jnp.zeros_like(lse_ref)

    for blk in range(seq // rows):
        here = pl.ds(blk * rows, rows)
        width = (blk + 1) * rows if causal else keys
        q = q_ref[here, :] * bf16(scale)
        k = k_ref[pl.ds(0, width), :]
        v = v_ref[pl.ds(0, width), :]
        outs = []
        kept = lse_ref[here, :]
        if causal:
            row = lax.broadcasted_iota(jnp.int32, (rows, 1), 0) + blk * rows
            col = lax.broadcasted_iota(jnp.int32, (1, width), 1)
            allowed = col <= jnp.minimum(row, top)
        for h in range(2):
            mine = (lane // HEAD_DIM) == h
            s = dot_nt(jnp.where(mine, q, bf16(0)), k)
            if causal:
                s = jnp.where(allowed, s, masked_score)
            peak = jnp.max(s, axis=1, keepdims=True)
            e = jnp.exp(s - peak)
            mass = jnp.sum(e, axis=1, keepdims=True)
            outs.append(dot_nn(e.astype(bf16), v) * (1.0 / mass))
            kept = jnp.where(lane == 2 * pair + h, peak + jnp.log(mass), kept)
        o_ref[here, :] = jnp.where(lane < HEAD_DIM, outs[0], outs[1]).astype(bf16)
        lse_ref[here, :] = kept


def attend_forward(limit, q, k, v, causal):
    seq, width = q.shape
    keys = k.shape[0]
    pairs = width // LANES
    rows = min(128 if causal else 256, seq)
    o, lse = pl.pallas_call(
        functools.partial(attend_forward_body, causal=causal, rows=rows),
        grid=(pairs,),
        out_shape=(
            jax.ShapeDtypeStruct((seq, width), bf16),
            jax.ShapeDtypeStruct((seq, LANES), f32),
        ),
        in_specs=[
            pl.BlockSpec(memory_space=pltpu.SMEM),
            pl.BlockSpec((seq, LANES), lambda i: (0, i)),
            pl.BlockSpec((keys, LANES), lambda i: (0, i)),
            pl.BlockSpec((keys, LANES), lambda i: (0, i)),
        ],
        out_specs=(
            pl.BlockSpec((seq, LANES), lambda i: (0, i)),
            pl.BlockSpec((seq, LANES), lambda i: (0, 0)),
        ),
        compiler_params=params(),
        cost_estimate=pl.CostEstimate(
            flops=4 * seq * keys * width, bytes_accessed=8 * seq * width, transcendentals=0
        ),
        name="attend_forward",
    )(limit, q, k, v)
    return o, lse[:, : 2 * pairs].T.reshape(pairs, 2, seq)


def attend_backward_body(
    lim, q_ref, k_ref, v_ref, o_ref, do_ref, lse_ref, dq_ref, dk_ref, dv_ref, dk_acc, dv_acc, *, causal, rows
):
    seq, keys = q_ref.shape[0], k_ref.shape[0]
    lane = lax.broadcasted_iota(jnp.int32, (1, LANES), 1)
    top = lim[0] - 1
    dk_acc[...] = jnp.zeros_like(dk_acc)
    dv_acc[...] = jnp.zeros_like(dv_acc)
    head_row = lax.broadcasted_iota(jnp.int32, (8, LANES), 0)
    head_lane = lax.broadcasted_iota(jnp.int32, (8, LANES), 1) // HEAD_DIM
    pick = (head_row == head_lane).astype(bf16)
    for blk in range(seq // rows):
        here = pl.ds(blk * rows, rows)
        width = (blk + 1) * rows if causal else keys
        span = pl.ds(0, width)
        q = q_ref[here, :] * bf16(scale)
        do = do_ref[here, :]
        k = k_ref[span, :]
        v = v_ref[span, :]
        prod = do.astype(f32) * o_ref[here, :].astype(f32)
        hi = prod.astype(bf16)
        lo = (prod - hi.astype(f32)).astype(bf16)
        delta = dot_nt(pick, hi) + dot_nt(pick, lo)
        lse = lse_ref[0][:, blk * rows : (blk + 1) * rows]
        if causal:
            key = lax.broadcasted_iota(jnp.int32, (width, 1), 0)
            row = lax.broadcasted_iota(jnp.int32, (1, rows), 1) + blk * rows
            allowed = key <= jnp.minimum(row, top)
        dq = jnp.zeros((rows, LANES), f32)
        dk = jnp.zeros((width, LANES), f32)
        dv = jnp.zeros((width, LANES), f32)
        for h in range(2):
            mine = (lane // HEAD_DIM) == h
            qm = jnp.where(mine, q, bf16(0))
            dom = jnp.where(mine, do, bf16(0))
            km = jnp.where(mine, k, bf16(0))
            s = dot_nt(k, qm)
            if causal:
                s = jnp.where(allowed, s, masked_score)
            p = jnp.exp(s - lse[h : h + 1, :])
            dp = dot_nt(v, dom)
            ds = (p * (dp - delta[h : h + 1, :])).astype(bf16)
            dv = dv + dot_nn(p.astype(bf16), dom)
            dk = dk + dot_nn(ds, qm)
            dq = dq + dot_tn(ds, km)
        dq_ref[here, :] = (dq * scale).astype(bf16)
        dk_acc[span, :] += dk
        dv_acc[span, :] += dv
    dk_ref[...] = dk_acc[...].astype(bf16)
    dv_ref[...] = dv_acc[...].astype(bf16)


def attend_backward(limit, q, k, v, o, do, lse, causal):
    seq, width = q.shape
    keys = k.shape[0]
    pairs = width // LANES
    rows = min(128 if causal else 256, seq)
    q_spec = pl.BlockSpec((seq, LANES), lambda i: (0, i))
    k_spec = pl.BlockSpec((keys, LANES), lambda i: (0, i))
    return pl.pallas_call(
        functools.partial(attend_backward_body, causal=causal, rows=rows),
        grid=(pairs,),
        out_shape=(
            jax.ShapeDtypeStruct((seq, width), bf16),
            jax.ShapeDtypeStruct((keys, width), bf16),
            jax.ShapeDtypeStruct((keys, width), bf16),
        ),
        in_specs=[
            pl.BlockSpec(memory_space=pltpu.SMEM),
            q_spec,
            k_spec,
            k_spec,
            q_spec,
            q_spec,
            pl.BlockSpec((1, 2, seq), lambda i: (i, 0, 0)),
        ],
        out_specs=(q_spec, k_spec, k_spec),
        scratch_shapes=[pltpu.VMEM((keys, LANES), f32), pltpu.VMEM((keys, LANES), f32)],
        compiler_params=params(),
        cost_estimate=pl.CostEstimate(
            flops=10 * seq * keys * width, bytes_accessed=16 * seq * width, transcendentals=0
        ),
        name="attend_backward",
    )(limit, q, k, v, o, do, lse)


def gelu_body(h_ref, w_ref, b_ref, act_ref, slope_ref, u_ref, *, chunk):
    u_ref[...] = dot_nn(h_ref[...], w_ref[...]) + b_ref[...]

    def part(i):
        here = pl.ds(pl.multiple_of(i * chunk, chunk), chunk)
        u = u_ref[here, :]
        x = jnp.abs(u) * (0.5**0.5)
        t = 1.0 / (1.0 + ERFC_SLOPE * x)
        poly = jnp.full_like(t, ERFC_POLY[-1])
        for c in ERFC_POLY[-2::-1]:
            poly = poly * t + c
        bell = jnp.exp(-0.5 * (u * u))
        tail = 0.5 * (bell * (t * poly))
        cdf = jnp.where(u < 0, tail, 1.0 - tail)
        act_ref[here, :] = (u * cdf).astype(bf16)
        slope_ref[here, :] = (cdf + u * (bell * 0.3989422804014327)).astype(bf16)

    pl.loop(0, u_ref.shape[0] // chunk)(part)


def gelu_forward(h, w, b):
    seq, width = h.shape
    hidden = w.shape[1]
    tile = 512
    spec = pl.BlockSpec((seq, tile), lambda i: (0, i))
    return pl.pallas_call(
        functools.partial(gelu_body, chunk=32),
        grid=(hidden // tile,),
        out_shape=(jax.ShapeDtypeStruct((seq, hidden), bf16),) * 2,
        in_specs=[
            pl.BlockSpec((seq, width), lambda i: (0, 0)),
            pl.BlockSpec((width, tile), lambda i: (0, i)),
            pl.BlockSpec((1, tile), lambda i: (0, i)),
        ],
        out_specs=(spec, spec),
        scratch_shapes=[pltpu.VMEM((seq, tile), f32)],
        compiler_params=params(),
        cost_estimate=pl.CostEstimate(
            flops=2 * seq * width * hidden + 60 * seq * hidden,
            bytes_accessed=4 * seq * hidden + 2 * width * hidden,
            transcendentals=0,
        ),
        name="gelu_forward",
    )(h, w, b)


def weight_grad_body(scal, x_own, x_sib, y_own, y_sib, *refs):
    out = refs[-1]
    acc = dot_tn(x_own[...], y_own[...]) + dot_tn(x_sib[...], y_sib[...])
    for c in range(out.shape[0]):
        out[c] = acc[:, c * BS : (c + 1) * BS].astype(bf16)


def weight_grad(scal, x_own, x_sib, y_own, y_sib, held, first_block, total, tall, halves):
    seq = x_own.shape[0]
    if tall:
        steps = x_own.shape[1] // halves // BS
        y_width = y_own.shape[1]
        x_spec = pl.BlockSpec((seq, BS), lambda i, s: (0, s[2] * steps + i))
        y_spec = pl.BlockSpec((seq, y_width), lambda i, s: (0, 0))
    else:
        steps = x_own.shape[1] // BS
        y_width = y_own.shape[1] // halves
        x_spec = pl.BlockSpec((seq, BS), lambda i, s: (0, i))
        y_spec = pl.BlockSpec((seq, y_width), lambda i, s: (0, s[2]))
    nb = y_width // BS
    at = first_block // nb
    anyspec = pl.BlockSpec(memory_space=pl.ANY)
    first = held is None
    return pl.pallas_call(
        weight_grad_body,
        grid_spec=pltpu.PrefetchScalarGridSpec(
            num_scalar_prefetch=1,
            grid=(steps,),
            in_specs=[x_spec, x_spec, y_spec, y_spec] + ([] if first else [anyspec]),
            out_specs=pl.BlockSpec((nb, BS, BS), lambda i, s: (at + i, 0, 0)),
        ),
        out_shape=jax.ShapeDtypeStruct((total, BS, BS), bf16),
        input_output_aliases={} if first else {5: 0},
        compiler_params=params(),
        cost_estimate=pl.CostEstimate(
            flops=4 * seq * steps * BS * y_width,
            bytes_accessed=4 * seq * (steps * BS + y_width) + 2 * steps * BS * y_width,
            transcendentals=0,
        ),
        name="weight_grad",
    )(scal, x_own, x_sib, y_own, y_sib, *([] if first else [held]))


def split_low(a):
    hi = a.astype(bf16)
    return hi, (a - hi.astype(f32)).astype(bf16)


def shampoo_body(g_ref, w_ref, ls_ref, rs_ref, lr_ref, rr_ref, og, ol, orr, ow):
    g = g_ref[0]
    og[0, 0] = g.astype(f32)
    ol[0, 0] = 0.5 * ls_ref[0, 0] + 0.5 * dot_nt(g, g)
    orr[0, 0] = 0.5 * rs_ref[0, 0] + 0.5 * dot_tn(g, g)
    r_hi, r_lo = split_low(rr_ref[0, 0])
    i_hi, i_lo = split_low(dot_nn(g, r_hi) + dot_nn(g, r_lo))
    l_hi, l_lo = split_low(lr_ref[0, 0])
    d = dot_nn(l_hi, i_hi) + (dot_nn(l_hi, i_lo) + dot_nn(l_lo, i_hi))
    mean = jnp.mean(jnp.mean(d * d, axis=1, keepdims=True), axis=0, keepdims=True)
    ow[0, 0] = w_ref[0, 0] - (D**-0.5) * d / jnp.sqrt(mean + 1e-06)


def shampoo(owned, weights, left_stat, right_stat, left_root, right_root):
    n = owned.shape[0]
    spec = pl.BlockSpec((1, 1, BS, BS), lambda i: (0, i, 0, 0))
    return pl.pallas_call(
        shampoo_body,
        grid=(n,),
        out_shape=(jax.ShapeDtypeStruct((1, n, BS, BS), f32),) * 4,
        in_specs=[pl.BlockSpec((1, BS, BS), lambda i: (i, 0, 0))] + [spec] * 5,
        out_specs=(spec,) * 4,
        compiler_params=params(),
        cost_estimate=pl.CostEstimate(
            flops=14 * n * BS**3, bytes_accessed=38 * n * BS * BS, transcendentals=0
        ),
        name="shampoo",
    )(owned, weights, left_stat, right_stat, left_root, right_root)


def norm_forward(z, gain, shift):
    center = z - jnp.mean(z, axis=1, keepdims=True)
    inv = lax.rsqrt(jnp.mean(center * center, axis=1, keepdims=True) + eps_norm)
    normed = center * inv
    return normed * gain + shift, normed, inv


def norm_backward(grad, normed, inv, gain):
    scaled = grad * gain
    mean_plain = jnp.mean(scaled, axis=1, keepdims=True)
    mean_cross = jnp.mean(scaled * normed, axis=1, keepdims=True)
    back = inv * (scaled - mean_plain - normed * mean_cross)
    return back, jnp.sum(grad * normed, axis=0), jnp.sum(grad, axis=0)


def route_out(value):
    axes = ("rep", "shard")
    count = lax.axis_size(axes)
    cut = value.reshape(value.shape[0], count, value.shape[1] // count, value.shape[2])
    return lax.all_to_all(cut, axes, split_axis=1, concat_axis=0, tiled=True)


def route_home(pieces, ordering):
    moved = pieces.at[ordering].get(mode="promise_in_bounds")
    back = lax.all_to_all(moved, ("rep", "shard"), split_axis=0, concat_axis=1, tiled=True)
    return back.reshape(back.shape[0], -1, back.shape[3])


def per_device(
    net,
    inputs,
    encoded,
    cotangent,
    lengths,
    seq_slots,
    block_slots,
    weights,
    left_stat,
    right_stat,
    left_root,
    right_root,
    vectors,
    vec_stat,
):
    half_d = inputs.shape[2]
    halves = D // half_d
    half_f = FF // halves
    nblk = weights.shape[1]
    total = block_slots.shape[0]
    counts = (nblk, nblk // 4, total)
    core = lax.axis_index("mp")
    me = lax.axis_index("shard")
    plane = lax.axis_index("rep")
    seq_index = lax.axis_index(("rep", "shard")) * inputs.shape[0] + core
    limit = lax.dynamic_slice_in_dim(lengths, seq_index, 1)
    scal = jnp.stack([me, plane, core]).astype(jnp.int32)
    tab = place_table(block_slots, half_d, half_f)
    is_first = core == 0

    def pick(pair, which):
        return lax.dynamic_index_in_dim(pair, which, axis=0, keepdims=False)

    def joined(low_half, high_half):
        return jnp.concatenate(
            [
                jnp.where(is_first, low_half, high_half),
                jnp.where(is_first, high_half, low_half),
            ],
            axis=1,
        )

    def whole(value):
        other = net.swap_core(value)
        own = joined(pick(value, core), pick(other, core))
        sib = joined(pick(value, 1 - core), pick(other, 1 - core))
        return own, sib

    def halved(full):
        mine = lax.dynamic_slice_in_dim(full, core * half_d, half_d, axis=1)
        away = lax.dynamic_slice_in_dim(full, (1 - core) * half_d, half_d, axis=1)
        got = net.swap_core(away)
        return jnp.stack([jnp.where(is_first, mine, got), jnp.where(is_first, got, mine)])

    x, x_sib = whole(inputs)
    e, e_sib = whole(encoded)

    low = weights[0].astype(bf16)
    sq, w_fi, w_fo = gather_weights(net, scal, tab, low, plane, counts)
    w_sq, w_sk, w_sv, w_so, w_cq, w_ck, w_cv, w_co = [
        lax.slice_in_dim(sq, i * D, (i + 1) * D, axis=0) for i in range(8)
    ]

    vec_low = vectors.astype(bf16)
    vec_mine = lax.all_to_all(
        jnp.broadcast_to(vec_low, (net.n_shard, vec_low.shape[1])),
        "shard",
        split_axis=0,
        concat_axis=0,
        tiled=True,
    ).reshape(1, -1)
    vec_other = net.swap_core(vec_mine)
    vec_both = jnp.concatenate(
        [jnp.where(is_first, vec_mine, vec_other), jnp.where(is_first, vec_other, vec_mine)]
    ).astype(f32)
    vecs = [vec_both[:, i * half_d : (i + 1) * half_d].reshape(1, D) for i in range(13)]
    vecs.append(vec_both[:, 13 * half_d :].reshape(1, FF))
    b_sq, b_sv, b_so, g_one, b_one, b_cq, b_cv, b_co, g_two, b_two, b_fo, g_three, b_three, b_fi = vecs

    q_s = (dot_nn(x, w_sq) + b_sq).astype(bf16)
    k_s = dot_nn(x, w_sk).astype(bf16)
    v_s = (dot_nn(x, w_sv) + b_sv).astype(bf16)
    cot_in, q_s = lax.optimization_barrier((cotangent, q_s))
    o_s, lse_s = attend_forward(limit, q_s, k_s, v_s, True)
    cot_pieces, o_s = together(route_out(cot_in), o_s)
    cot_home = route_home(cot_pieces, seq_slots)
    z_one = x.astype(f32) + dot_nn(o_s, w_so) + b_so
    h_one, n_one, r_one = norm_forward(z_one, g_one, b_one)
    h_one_low = h_one.astype(bf16)
    q_c = (dot_nn(h_one_low, w_cq) + b_cq).astype(bf16)
    k_c = dot_nn(e, w_ck).astype(bf16)
    v_c = (dot_nn(e, w_cv) + b_cv).astype(bf16)
    o_c, lse_c = attend_forward(limit, q_c, k_c, v_c, False)
    z_two = h_one + dot_nn(o_c, w_co) + b_co
    h_two, n_two, r_two = norm_forward(z_two, g_two, b_two)
    h_two_low = h_two.astype(bf16)
    act, slope = gelu_forward(h_two_low, w_fi, b_fi)
    z_three = h_two + dot_nn(act, w_fo) + b_fo
    h_three, n_three, r_three = norm_forward(z_three, g_three, b_three)
    live = (jnp.arange(x.shape[0]) < limit).astype(f32)[:, None]
    source = jnp.sum(
        jnp.where(
            seq_slots[:, None] == jnp.arange(seq_slots.shape[0], dtype=jnp.int32)[None, :],
            jnp.arange(seq_slots.shape[0], dtype=jnp.int32)[:, None],
            0,
        ),
        axis=0,
    )
    finished = halved((h_three * live).astype(bf16))

    cot, _ = whole(cot_home)
    grad_y = cot.astype(f32) * live
    d_three, dg_three, db_three = norm_backward(grad_y, n_three, r_three, g_three)
    a_three = d_three.astype(bf16)
    d_hidden = (dot_nt(a_three, w_fo) * slope.astype(f32)).astype(bf16)
    pieces, d_hidden = together(route_out(finished), d_hidden)
    d_h_two = d_three + dot_nt(d_hidden, w_fi)
    d_two, dg_two, db_two = norm_backward(d_h_two, n_two, r_two, g_two)
    a_two = d_two.astype(bf16)
    d_oc = dot_nt(a_two, w_co).astype(bf16)
    outputs = route_home(pieces, source)
    dq_c, dk_c, dv_c = attend_backward(limit, q_c, k_c, v_c, o_c, d_oc, lse_c, False)
    d_h_one = d_two + dot_nt(dq_c, w_cq)
    d_one, dg_one, db_one = norm_backward(d_h_one, n_one, r_one, g_one)
    a_one = d_one.astype(bf16)
    d_os = dot_nt(a_one, w_so).astype(bf16)
    outputs, d_os = together(outputs, d_os)
    dq_s, dk_s, dv_s = attend_backward(limit, q_s, k_s, v_s, o_s, d_os, lse_s, True)

    per = (D // BS) * (half_d // BS)
    per_f = (D // BS) * (half_f // BS)
    grads = None
    for xo, yo, at, tall, xs in (
        (act, a_three, 8 * per + per_f, True, None),
        (h_two_low, d_hidden, 8 * per, False, None),
        (o_c, a_two, 7 * per, True, None),
        (h_one_low, dq_c, 4 * per, False, None),
        (e, dk_c, 5 * per, False, e_sib),
        (e, dv_c, 6 * per, False, e_sib),
        (o_s, a_one, 3 * per, True, None),
        (x, dq_s, 0, False, x_sib),
        (x, dk_s, per, False, x_sib),
        (x, dv_s, 2 * per, False, x_sib),
    ):
        if xs is None:
            xs = net.swap_core(xo)
        ys = net.swap_core(yo)
        grads = weight_grad(scal, xo, xs, yo, ys, grads, at, total, tall, halves)
    owned = reduce_gradients(net, scal, grads, plane, block_slots, counts)

    back = d_one + dot_nt(dq_s, w_sq) + dot_nt(dk_s, w_sk) + dot_nt(dv_s, w_sv)
    input_grad = halved(back.astype(bf16))
    encoded_grad = halved((dot_nt(dk_c, w_ck) + dot_nt(dv_c, w_cv)).astype(bf16))

    sums = (
        jnp.sum(dq_s.astype(f32), axis=0),
        jnp.sum(dv_s.astype(f32), axis=0),
        jnp.sum(d_one, axis=0),
        dg_one,
        db_one,
        jnp.sum(dq_c.astype(f32), axis=0),
        jnp.sum(dv_c.astype(f32), axis=0),
        jnp.sum(d_two, axis=0),
        dg_two,
        db_two,
        jnp.sum(d_three, axis=0),
        dg_three,
        db_three,
        jnp.sum(d_hidden.astype(f32), axis=0),
    )
    vec_pair = jnp.concatenate([s.reshape(halves, -1) for s in sums], axis=1)
    vec_sum = pick(vec_pair, core) + net.swap_core(pick(vec_pair, 1 - core))
    vec_parts = lax.all_to_all(
        vec_sum.reshape(net.n_shard, -1), "shard", split_axis=0, concat_axis=0, tiled=True
    )
    vec_owned = jnp.sum(vec_parts, axis=0, keepdims=True)
    vec_owned = vec_owned + net.swap_rep(vec_owned)

    block_grad, left_new, right_new, weights_new = shampoo(
        owned, weights, left_stat, right_stat, left_root, right_root
    )
    vec_stat_new = 0.5 * vec_stat + 0.5 * vec_owned * vec_owned
    vectors_new = vectors - 0.1 * vec_owned * lax.rsqrt(vec_stat_new)
    return (
        outputs,
        input_grad,
        encoded_grad,
        block_grad,
        left_new,
        right_new,
        weights_new,
        vec_owned,
        vec_stat_new,
        vectors_new,
    )


def solution(mesh):
    net = Net(mesh.shape["rep"], mesh.shape["shard"], mesh.shape["mp"])
    rows = P(("rep", "shard"), None, "mp")
    blocks = P("mp", "shard", None, None)
    vector = P("mp", "shard")
    in_specs = (rows, rows, rows, P(), P(), P()) + (blocks,) * 5 + (vector, vector)
    out_specs = (rows, rows, rows) + (blocks,) * 4 + (vector,) * 3
    return jax.shard_map(
        functools.partial(per_device, net),
        mesh=mesh,
        in_specs=in_specs,
        out_specs=out_specs,
        check_vma=False,
    )
```

time: 1600 us -> 791 us (0.49)
  waiting for transfers between devices: 815 us -> 195 us
  Pallas kernels: 0 us -> 248 us
  matrix products: 245 us -> 90 us
  local copies, waits for them, and re-layouts: 235 us -> 97.7 us
  blocking collectives: 124 us -> 0 us
  other arithmetic: 111 us -> 69.2 us
  starting transfers between devices: 42.2 us -> 82.8 us
  between operations: 18.8 us -> 2.14 us
    reduce_scatter x15 -> x0, waiting for transfers between devices: 515 us -> none  [the longest x1 473 us: per_device(): lax.psum_scatter(dealt, 'shard', scatter_dimension=0, tiled=True)]
    pallas_call x0 -> x23, Pallas kernels: none -> 248 us  [the longest x10 61 us: weight_grad(): pl.pallas_call(weight_grad_body, grid_spec=pltpu.PrefetchScalarGridSpec(n...]
    ppermute x0 -> x51, waiting for transfers between devices: none -> 179 us  [the longest x12 109 us: swap_shard(): return lax.ppermute(value, ('rep', 'shard', 'mp'), pairs)]
    dot_general x88 -> x19, matrix products: 245 us -> 90 us  [the longest x10 51.8 us: dot_nt(): return lax.dot_general(a, b, NT, preferred_element_type=f32)]
    all_to_all x7 -> x6, waiting for transfers between devices: 159 us -> 15.8 us  [the longest x2 9.94 us: route_out(): return lax.all_to_all(cut, axes, split_axis=1, concat_axis=0, tiled=True)]
    all_gather x13 -> x0, waiting for transfers between devices: 129 us -> none  [the longest x1 113 us: per_device(): lax.all_gather(weights_low, 'shard', axis=1, tiled=True)]
    reshape x31 -> x19, local copies, waits for them, and re-layouts: 96.3 us -> 9.64 us  [the longest x14 6.97 us: per_device(): vec_pair = jnp.concatenate([s.reshape(halves, -1) for s in sums], axis=1)]
    unnamed x2 -> x0, blocking collectives: 85.4 us -> none
  transfers between devices with their start and end apart: 36 -> 57, of which waited for: 18 -> 15; matrix products, arithmetic and copies ran while one was open for 28% -> 21% of each run, Pallas kernels for 0% -> 27%
where the time goes in v1:
time: 791 us; the launch traced here: 785 us
  Pallas kernels  248 us (31%)
  waiting for transfers between devices  195 us (25%)
  local copies, waits for them, and re-layouts  97.7 us (12%)
  matrix products  90 us (11%)
  starting transfers between devices  82.8 us (10%)
  other arithmetic  69.2 us (9%)
    ppermute x12, waiting for transfers between devices, swap_shard(): return lax.ppermute(value, ('rep', 'shard', 'mp'), pairs)  109 us
    unnamed x223, local copies, waits for them, and re-layouts  76.7 us
    ppermute x7, waiting for transfers between devices, swap_rep(): return lax.ppermute(value, 'rep', [(i, i ^ 1) for i in range(self.n_rep)])  69.4 us
    pallas_call x10, Pallas kernels, weight_grad(): pl.pallas_call(weight_grad_body, grid_spec=pltpu.PrefetchScalarGridSpec(n...  61 us
    dot_general x10, matrix products, dot_nt(): return lax.dot_general(a, b, NT, preferred_element_type=f32)  51.8 us
    pallas_call x5, Pallas kernels, place(): pl.pallas_call(functools.partial(place_body, pieces=pieces, first=first,...  49.9 us
    pallas_call x2, Pallas kernels, deal(): pl.pallas_call(functools.partial(deal_body, pieces=pieces, counts=counts)...  42.4 us
    dot_general x9, matrix products, dot_nn(): return jnp.dot(a, b, preferred_element_type=f32)  38.3 us
  transfers between devices with their start and end apart: 57, of which 15 were waited for; matrix products, arithmetic and copies ran while one was open for 21% of the time, Pallas kernels for 27%

profile of v1, /device:TPU:0, one launch (start us, length us, event | category | flops | bytes accessed | tf_op | source)
XLA Modules:
  0.0 784.6 jit_solution(12689344801998450542)
XLA Ops:
  0.7 3.9 convert_bitcast_fusion.14.refs_0_
  5.4 3.6 collective-permute-start.1
  11.7 32.2 %collective-permute-done.1.refs_0_ = bf16[4,256,256]{2,1,0:T(8,128)(2,1)S(1)} collective-permute-done((bf16[4,256,256]{2,1,0:T(8,128)(2,1)S(1)}, bf16[4,256,256]{2,1,0:T(8,128)(2,1)S(1)}, u32[]{:S(2)}, u32[]{:S(2)}) %collective-permute-start.1) | collective-permute-done | bytes 524320 | tf_op jit(solution)/shard_map/ppermute | solution.py:89
  47.7 3.9 place.5
  51.6 8.5 %collective-permute-done.3.refs_0_ = bf16[8,256,256]{2,1,0:T(8,128)(2,1)S(1)} collective-permute-done((bf16[8,256,256]{2,1,0:T(8,128)(2,1)}, bf16[8,256,256]{2,1,0:T(8,128)(2,1)S(1)}, u32[]{:S(2)}, u32[]{:S(2)}) %collective-permute-start.3) | collective-permute-done | bytes 1048608 | tf_op jit(solution)/shard_map/ppermute | solution.py:89
  64.4 4.3 collective-permute-start.6
  78.5 25.1 %collective-permute-done.8.refs_4_ = bf16[12,256,256]{2,1,0:T(8,128)(2,1)S(1)} collective-permute-done((bf16[12,256,256]{2,1,0:T(8,128)(2,1)S(1)}, bf16[12,256,256]{2,1,0:T(8,128)(2,1)S(1)}, u32[]{:S(2)}, u32[]{:S(2)}) %collective-permute-start.8) | collective-permute-done | bytes 1572896 | tf_op jit(solution)/shard_map/ppermute | solution.py:79
  103.6 9.0 %collective-permute-done.7.refs_2_ = bf16[16,256,256]{2,1,0:T(8,128)(2,1)S(1)} collective-permute-done((bf16[16,256,256]{2,1,0:T(8,128)(2,1)}, bf16[16,256,256]{2,1,0:T(8,128)(2,1)S(1)}, u32[]{:S(2)}, u32[]{:S(2)}) %collective-permute-start.7) | collective-permute-done | bytes 2097184 | tf_op jit(solution)/shard_map/ppermute | solution.py:89
  114.5 3.9 pad_maximum_fusion
  123.7 8.6 %place.7 = (bf16[8192,1024]{1,0:T(8,128)(2,1)S(1)}, bf16[1024,4096]{1,0:T(8,128)(2,1)S(1)}, bf16[4096,1024]{1,0:T(8,128)(2,1)S(1)}) custom-call(s32[3]{0:T(128)S(1)} %pad_add_fusion.3.scal, s32[768]{0:T(1024)S(1)} %reshape.232.tab, ...), custom_call_target="tpu_custom_call", output_to_operand_aliasing={{0}: (6, {}), {1}: (7, {}), {2}: (8, {})} | custom-call | bytes 8388608 | tf_op jit(solution)/shard_map/place/pallas_call | solution.py:186
  132.3 5.8 copy-done.2
  145.9 22.3 %collective-permute-done.12.refs_2_ = bf16[16,256,256]{2,1,0:T(8,128)(2,1)S(1)} collective-permute-done((bf16[16,256,256]{2,1,0:T(8,128)(2,1)S(1)}, bf16[16,256,256]{2,1,0:T(8,128)(2,1)S(1)}, u32[]{:S(2)}, u32[]{:S(2)}) %collective-permute-start.12) | collective-permute-done | bytes 2097184 | tf_op jit(solution)/shard_map/ppermute | solution.py:79
  178.2 5.8 all-to-all-done
  201.5 21.9 %place.8 = (bf16[8192,1024]{1,0:T(8,128)(2,1)}, bf16[1024,4096]{1,0:T(8,128)(2,1)S(1)}, bf16[4096,1024]{1,0:T(8,128)(2,1)S(1)}) custom-call(s32[3]{0:T(128)S(1)} %pad_add_fusion.3.scal, s32[768]{0:T(1024)S(1)} %reshape.232.tab, bf16[16,256,256]{2,1,0:T(8,128)(2,1)S(1)} %copy-done.16, ...), custom_call_target="tpu_custom_call", output_to_operand_aliasing={{0}: (8, {}), {1}: (9, {}), {2}: (10, {})} | custom-call | bytes 23068672 | tf_op jit(solution)/shard_map/place/pallas_call | solution.py:186
  236.8 13.0 %place.9 = (bf16[8192,1024]{1,0:T(8,128)(2,1)}, bf16[1024,4096]{1,0:T(8,128)(2,1)S(1)}, bf16[4096,1024]{1,0:T(8,128)(2,1)S(1)}) custom-call(s32[3]{0:T(128)S(1)} %pad_add_fusion.3.scal, s32[768]{0:T(1024)S(1)} %reshape.232.tab, bf16[32,256,256]{2,1,0:T(8,128)(2,1)} %collective-permute-done.11.refs_0_, ...), custom_call_target="tpu_custom_call", output_to_operand_aliasing={{0}: (6, {}), {1}: (7, {}), {2}: (8, {})} | custom-call | bytes 25165824 | tf_op jit(solution)/shard_map/place/pallas_call | solution.py:186
  253.0 5.5 add_convert_fusion.12.q_ref
  259.6 14.2 %all-to-all-start.1 = ((bf16[2,16,32,512]{3,2,0,1:T(8,128)(2,1)}), bf16[2,16,32,512]{3,2,0,1:T(8,128)(2,1)S(1)}, u32[]{:S(2)}, u32[]{:S(2)}) async-start(bf16[2,16,32,512]{3,2,0,1:T(8,128)(2,1)} %copy.91), calls=%async_computation.1 | async-start | bytes 2097152 | tf_op jit(solution)/shard_map/all_to_all | solution.py:704
  278.8 3.9 fusion.40.k_ref
  282.7 3.8 add_convert_fusion.11.v_ref
  286.5 19.9 %attend_forward.2 = (bf16[512,1024]{1,0:T(8,128)(2,1)}, f32[512,128]{1,0:T(8,128)}) custom-call(s32[1]{0:T(128)} %dynamic_slice.69.lim, bf16[512,1024]{1,0:T(8,128)(2,1)} %add_convert_fusion.12.q_ref, bf16[512,1024]{1,0:T(8,128)(2,1)} %fusion.40.k_ref, bf16[512,1024]{1,0:T(8,128)(2,1)} %add_convert_fusion.11.v_ref), custom_call_target="tpu_custom_call" | custom-call | flops 1073741824 | bytes 4194304 | tf_op jit(solution)/shard_map/attend_forward/pallas_call | solution.py:449
  313.5 6.7 all-to-all-start.3
  325.8 4.2 add_convert_fusion.10.q_ref
  329.9 8.9 %attend_forward.3 = (bf16[512,1024]{1,0:T(8,128)(2,1)}, f32[512,128]{1,0:T(8,128)}) custom-call(s32[1]{0:T(128)} %dynamic_slice.69.lim, bf16[512,1024]{1,0:T(8,128)(2,1)} %add_convert_fusion.10.q_ref, bf16[128,1024]{1,0:T(8,128)(2,1)} %fusion.65.k_ref, bf16[128,1024]{1,0:T(8,128)(2,1)} %fusion.68.v_ref), custom_call_target="tpu_custom_call" | custom-call | flops 268435456 | bytes 4194304 | tf_op jit(solution)/shard_map/attend_forward/pallas_call | solution.py:449
  344.3 19.1 %gelu_forward.1 = (bf16[512,4096]{1,0:T(8,128)(2,1)}, bf16[512,4096]{1,0:T(8,128)(2,1)}) custom-call(bf16[512,1024]{1,0:T(8,128)(2,1)} %fusion.4.h_ref.x_own, bf16[1024,4096]{1,0:T(8,128)(2,1)} %copy-done.7, f32[1,4096]{1,0:T(1,128)} %bitcast.177), custom_call_target="tpu_custom_call" | custom-call | flops 4420796416 | bytes 16777216 | tf_op jit(solution)/shard_map/gelu_forward/pallas_call | solution.py:586
  365.0 8.5 %fusion.101 = (f32[512]{0:T(512)S(1)}, f32[512,1024]{1,0:T(8,128)S(1)}) fusion(f32[1024]{0:T(1024)} %bitcast.178, bf16[512,4096]{1,0:T(8,128)(2,1)} %get-tuple-element.135.x_own, bf16[4096,1024]{1,0:T(8,128)(2,1)} %copy-done.12, f32[1024]{0:T(1024)S(1)} %bitcast.174, f32[1024]{0:T(1024)S(1)} %bitcast.167, f32[512]{0:T(512)S(1)} %copy-done.79, ...), kind=kOutput, calls=%fused_computation.249 | convolution fusion | flops 4298636800 | bytes 16795648 | tf_op jit(solution)/shard_map/dot_general | solution.py:42
  382.7 7.3 all-to-all-start.2
  396.4 10.5 %multiply_convert_fusion.y_own = bf16[512,4096]{1,0:T(8,128)(2,1)} fusion(bf16[512,4096]{1,0:T(8,128)(2,1)} %get-tuple-element.138, bf16[512,1024]{1,0:T(8,128)(2,1)S(1)} %convert_element_type.226.y_own, bf16[4096,1024]{1,0:T(8,128)(2,1)} %copy-done.12), kind=kOutput, calls=%fused_computation.3 | convolution fusion | flops 4301258752 | bytes 17825792 | tf_op jit(solution)/shard_map/dot_general | solution.py:46
  406.9 9.9 %all-to-all-done.2 = bf16[2,16,32,512]{3,2,0,1:T(8,128)(2,1)} async-done(((bf16[2,16,32,512]{3,2,0,1:T(8,128)(2,1)}), bf16[2,16,32,512]{3,2,0,1:T(8,128)(2,1)}, u32[]{:S(2)}, u32[]{:S(2)}) %all-to-all-start.2) | async-done | bytes 1048608 | tf_op jit(solution)/shard_map/all_to_all | solution.py:704
  416.8 11.6 %multiply_reduce_fusion.1 = (f32[1024]{0:T(1024)}, f32[512]{0:T(512)S(1)}, f32[512]{0:T(512)S(1)}, f32[1024]{0:T(1024)}, f32[512,1024]{1,0:T(8,128)S(1)}) fusion(f32[512,1024]{1,0:T(8,128)} %copy-done.38, f32[512]{0:T(512)S(1)} %copy-done.80, f32[512]{0:T(512)S(1)} %copy-done.74, f32[1024]{0:T(1024)S(1)} %bitcast.168, f32[512,1024]{1,0:T(8,128)} %get-tuple-element.192, ...), kind=kOutput, calls=%fused_computation.12 | convolution fusion | flops 4300207104 | bytes 18894848 | tf_op jit(solution)/shard_map/dot_general | solution.py:46
  435.1 4.8 all-to-all-start.4
  439.9 4.2 fusion.46.do_ref
  444.1 10.2 %attend_backward.2 = (bf16[512,1024]{1,0:T(8,128)(2,1)}, bf16[128,1024]{1,0:T(8,128)(2,1)}, bf16[128,1024]{1,0:T(8,128)(2,1)}) custom-call(s32[1]{0:T(128)} %dynamic_slice.69.lim, bf16[512,1024]{1,0:T(8,128)(2,1)} %add_convert_fusion.10.q_ref, bf16[128,1024]{1,0:T(8,128)(2,1)} %fusion.65.k_ref, bf16[128,1024]{1,0:T(8,128)(2,1)} %fusion.68.v_ref, ...), custom_call_target="tpu_custom_call" | custom-call | flops 671088640 | bytes 8388608 | tf_op jit(solution)/shard_map/attend_backward/pallas_call | solution.py:534
  454.9 4.4 multiply_reduce_fusion.2
  463.1 3.9 fusion.43.do_ref
  469.2 16.2 %attend_backward.3 = (bf16[512,1024]{1,0:T(8,128)(2,1)}, bf16[512,1024]{1,0:T(8,128)(2,1)}, bf16[512,1024]{1,0:T(8,128)(2,1)}) custom-call(s32[1]{0:T(128)} %dynamic_slice.69.lim, bf16[512,1024]{1,0:T(8,128)(2,1)} %add_convert_fusion.12.q_ref, bf16[512,1024]{1,0:T(8,128)(2,1)} %fusion.40.k_ref, bf16[512,1024]{1,0:T(8,128)(2,1)} %add_convert_fusion.11.v_ref, ...), custom_call_target="tpu_custom_call" | custom-call | flops 2684354560 | bytes 8388608 | tf_op jit(solution)/shard_map/attend_backward/pallas_call | solution.py:534
  486.7 10.8 %weight_grad.10.refs_0_ = bf16[128,256,256]{2,1,0:T(8,128)(2,1)} custom-call(s32[3]{0:T(128)} %copy-done.31, bf16[512,4096]{1,0:T(8,128)(2,1)} %get-tuple-element.135.x_own, bf16[512,4096]{1,0:T(8,128)(2,1)} %collective-permute-done.37.x_sib, bf16[512,1024]{1,0:T(8,128)(2,1)} %copy-done.48, bf16[512,1024]{1,0:T(8,128)(2,1)} %copy-done.63), custom_call_target="tpu_custom_call" | custom-call | flops 4294967296 | bytes 10485760 | tf_op jit(solution)/shard_map/weight_grad/pallas_call | solution.py:630
  497.4 9.4 %weight_grad.11.refs_0_ = bf16[128,256,256]{2,1,0:T(8,128)(2,1)} custom-call(s32[3]{0:T(128)} %copy-done.31, bf16[512,1024]{1,0:T(8,128)(2,1)} %fusion.4.h_ref.x_own, bf16[512,1024]{1,0:T(8,128)(2,1)} %collective-permute-done.35.x_sib, bf16[512,4096]{1,0:T(8,128)(2,1)} %multiply_convert_fusion.y_own, ...), custom_call_target="tpu_custom_call", output_to_operand_aliasing={{}: (5, {})} | custom-call | flops 4294967296 | bytes 10485760 | tf_op jit(solution)/shard_map/weight_grad/pallas_call | solution.py:630
  506.8 4.7 weight_grad.12.refs_0_
  511.5 5.5 weight_grad.13.refs_0_
  517.0 4.6 weight_grad.14.refs_0_
  521.6 4.7 weight_grad.15.refs_0_
  527.2 4.7 weight_grad.16.refs_0_
  531.9 5.5 weight_grad.17.refs_0_
  537.4 5.5 weight_grad.18.refs_0_
  542.9 5.8 weight_grad.19.grads
  548.7 5.8 copy-done
  554.4 13.2 %deal.2 = (bf16[16,256,256]{2,1,0:T(8,128)(2,1)}, bf16[32,256,256]{2,1,0:T(8,128)(2,1)}) custom-call(s32[3]{0:T(128)S(1)} %copy-done.32, s32[128]{0:T(128)S(1)} %copy-done.34, bf16[128,256,256]{2,1,0:T(8,128)(2,1)S(1)} %copy-done), custom_call_target="tpu_custom_call" | custom-call | bytes 12582912 | tf_op jit(solution)/shard_map/deal/pallas_call | solution.py:321
  582.9 5.8 copy-done.1
  588.6 29.3 %deal.3 = (bf16[16,256,256]{2,1,0:T(8,128)(2,1)}, bf16[16,256,256]{2,1,0:T(8,128)(2,1)S(1)}, bf16[16,256,256]{2,1,0:T(8,128)(2,1)S(1)}, bf16[32,256,256]{2,1,0:T(8,128)(2,1)S(1)}) custom-call(s32[3]{0:T(128)S(1)} %copy-done.32, s32[128]{0:T(128)S(1)} %copy-done.34, bf16[128,256,256]{2,1,0:T(8,128)(2,1)S(1)} %copy-done.1), custom_call_target="tpu_custom_call" | custom-call | bytes 20971520 | tf_op jit(solution)/shard_map/deal/pallas_call | solution.py:321
  617.9 3.5 add_convert_fusion.1
  622.9 4.2 add_convert_fusion.2
  641.0 24.6 %collective-permute-done.42 = bf16[16,256,256]{2,1,0:T(8,128)(2,1)} collective-permute-done((bf16[16,256,256]{2,1,0:T(8,128)(2,1)}, bf16[16,256,256]{2,1,0:T(8,128)(2,1)}, u32[]{:S(2)}, u32[]{:S(2)}) %collective-permute-start.42) | collective-permute-done | bytes 2097184 | tf_op jit(solution)/shard_map/ppermute | solution.py:89
  665.6 11.3 %collective-permute-done.41 = bf16[16,256,256]{2,1,0:T(8,128)(2,1)} collective-permute-done((bf16[16,256,256]{2,1,0:T(8,128)(2,1)}, bf16[16,256,256]{2,1,0:T(8,128)(2,1)}, u32[]{:S(2)}, u32[]{:S(2)}) %collective-permute-start.41) | collective-permute-done | bytes 2097184 | tf_op jit(solution)/shard_map/ppermute | solution.py:89
  676.9 4.4 add_convert_fusion.8
  686.1 4.2 fusion.33
  690.3 4.3 fusion.29
  695.3 4.1 all-to-all-start.5
  699.5 15.3 %collective-permute-done.44 = bf16[8,256,256]{2,1,0:T(8,128)(2,1)} collective-permute-done((bf16[8,256,256]{2,1,0:T(8,128)(2,1)}, bf16[8,256,256]{2,1,0:T(8,128)(2,1)}, u32[]{:S(2)}, u32[]{:S(2)}) %collective-permute-start.44) | collective-permute-done | bytes 1048608 | tf_op jit(solution)/shard_map/ppermute | solution.py:89
  717.8 3.6 add_convert_fusion.9
  724.6 3.7 collective-permute-start.47
  728.4 14.0 %collective-permute-done.50 = f32[1,1088]{1,0:T(1,128)S(1)} collective-permute-done((f32[1,1088]{1,0:T(1,128)S(1)}, f32[1,1088]{1,0:T(1,128)S(1)}, u32[]{:S(2)}, u32[]{:S(2)}) %collective-permute-start.50) | collective-permute-done | bytes 4384 | tf_op jit(solution)/shard_map/ppermute | solution.py:79
  743.0 6.8 collective-permute-done.47
  754.6 8.0 %collective-permute-done.48 = bf16[4,256,256]{2,1,0:T(8,128)(2,1)S(1)} collective-permute-done((bf16[4,256,256]{2,1,0:T(8,128)(2,1)S(1)}, bf16[4,256,256]{2,1,0:T(8,128)(2,1)S(1)}, u32[]{:S(2)}, u32[]{:S(2)}) %collective-permute-start.48) | collective-permute-done | bytes 524320 | tf_op jit(solution)/shard_map/ppermute | solution.py:79
  764.2 20.2 %shampoo.1 = (f32[1,16,256,256]{3,2,1,0:T(8,128)}, f32[1,16,256,256]{3,2,1,0:T(8,128)}, f32[1,16,256,256]{3,2,1,0:T(8,128)}, f32[1,16,256,256]{3,2,1,0:T(8,128)}) custom-call(bf16[16,256,256]{2,1,0:T(8,128)(2,1)} %pad_maximum_fusion.3.g_ref, f32[1,16,256,256]{3,2,1,0:T(8,128)} %w_ref.1, f32[1,16,256,256]{3,2,1,0:T(8,128)} %ls_ref.1, ...), custom_call_target="tpu_custom_call" | custom-call | flops 3758096384 | bytes 39845888 | tf_op jit(solution)/shard_map/shampoo/pallas_call | solution.py:671
  (433 shorter events, 186.0 us)
Async XLA Ops:
  4.6 39.3 %collective-permute-start.2 = (bf16[16,256,256]{2,1,0:T(8,128)(2,1)}, bf16[16,256,256]{2,1,0:T(8,128)(2,1)}, u32[]{:S(2)}, u32[]{:S(2)}) collective-permute-start(bf16[16,256,256]{2,1,0:T(8,128)(2,1)} %convert_bitcast_fusion.14.refs_0_), channel_id=1, source_target_pairs={{0,1},{1,0},{2,3},{3,2},{4,5},{5,4},{6,7},{7,6},{8,9},{9,8},{10,11... | collective-permute-start | bytes 6291464 | tf_op jit(solution)/shard_map/ppermute | solution.py:76
  5.4 38.4 %collective-permute-start.1 = (bf16[4,256,256]{2,1,0:T(8,128)(2,1)S(1)}, bf16[4,256,256]{2,1,0:T(8,128)(2,1)S(1)}, u32[]{:S(2)}, u32[]{:S(2)}) collective-permute-start(bf16[4,256,256]{2,1,0:T(8,128)(2,1)S(1)} %dynamic-slice_bitcast_fusion), channel_id=1, source_target_pairs={{0,8},{1,9},{2,10},{3,11},{4,12},{5,13},{6,14},{7,15},{8,0},{9,1},... | collective-permute-start | bytes 1572872 | tf_op jit(solution)/shard_map/ppermute | solution.py:89
  10.1 41.4 %collective-permute-start.4 = (bf16[8,256,256]{2,1,0:T(8,128)(2,1)}, bf16[8,256,256]{2,1,0:T(8,128)(2,1)S(1)}, u32[]{:S(2)}, u32[]{:S(2)}) collective-permute-start(bf16[8,256,256]{2,1,0:T(8,128)(2,1)} %slice_bitcast_fusion), channel_id=1, source_target_pairs={{0,4},{1,9},{2,6},{3,11},{4,0},{5,13},{6,2},{7,15},{8,12},{9,1},{1... | collective-permute-start | bytes 3145736 | tf_op jit(solution)/shard_map/ppermute | solution.py:89
  44.9 15.1 %collective-permute-start.3 = (bf16[8,256,256]{2,1,0:T(8,128)(2,1)}, bf16[8,256,256]{2,1,0:T(8,128)(2,1)S(1)}, u32[]{:S(2)}, u32[]{:S(2)}) collective-permute-start(bf16[8,256,256]{2,1,0:T(8,128)(2,1)} %pad_maximum_fusion.6), channel_id=1, source_target_pairs={{0,2},{1,5},{2,0},{3,7},{4,6},{5,1},{6,4},{7,3},{8,10},{9,13},{10,... | collective-permute-start | bytes 3145736 | tf_op jit(solution)/shard_map/ppermute | solution.py:89
  47.1 4.5 collective-permute-start.5
  47.7 182.4 %copy-start.31 = (s32[3]{0:T(128)}, s32[3]{0:T(128)S(1)}, u32[]{:S(2)}) copy-start(s32[3]{0:T(128)S(1)} %pad_add_fusion.3.scal) | copy-start | bytes 40
  62.8 49.7 %collective-permute-start.7 = (bf16[16,256,256]{2,1,0:T(8,128)(2,1)}, bf16[16,256,256]{2,1,0:T(8,128)(2,1)S(1)}, u32[]{:S(2)}, u32[]{:S(2)}) collective-permute-start(bf16[16,256,256]{2,1,0:T(8,128)(2,1)} %pad_maximum_fusion.2), channel_id=1, source_target_pairs={{0,8},{1,3},{2,10},{3,1},{4,12},{5,7},{6,14},{7,5},{8,0},{9,11},{1... | collective-permute-start | bytes 6291464 | tf_op jit(solution)/shard_map/ppermute | solution.py:89
  64.4 50.1 %collective-permute-start.6 = (bf16[16,256,256]{2,1,0:T(8,128)(2,1)}, bf16[16,256,256]{2,1,0:T(8,128)(2,1)S(1)}, u32[]{:S(2)}, u32[]{:S(2)}) collective-permute-start(bf16[16,256,256]{2,1,0:T(8,128)(2,1)} %pad_maximum_fusion.1), channel_id=1, source_target_pairs={{0,4},{1,3},{2,6},{3,1},{4,0},{5,7},{6,2},{7,5},{8,12},{9,11},{10,... | collective-permute-start | bytes 6291464 | tf_op jit(solution)/shard_map/ppermute | solution.py:89
  68.8 34.8 %collective-permute-start.8 = (bf16[12,256,256]{2,1,0:T(8,128)(2,1)S(1)}, bf16[12,256,256]{2,1,0:T(8,128)(2,1)S(1)}, u32[]{:S(2)}, u32[]{:S(2)}) collective-permute-start(bf16[12,256,256]{2,1,0:T(8,128)(2,1)S(1)} %pad_maximum_fusion.4), channel_id=1, source_target_pairs={{0,16},{16,0},{1,17},{17,1},{2,18},{18,2},{3,19},{19,3},{4,20},{20... | collective-permute-start | bytes 4718600 | tf_op jit(solution)/shard_map/ppermute | solution.py:79
  70.4 5.9 collective-permute-start.10
  73.7 3.8 collective-permute-start.9
  114.5 63.0 %copy-start.68 = (bf16[2,128,512]{2,1,0:T(8,128)(2,1)S(1)}, bf16[2,128,512]{2,1,0:T(8,128)(2,1)}, u32[]{:S(2)}) copy-start(bf16[2,128,512]{2,1,0:T(8,128)(2,1)} %param.14) | copy-start | bytes 786436
  114.5 63.1 %copy-start.95 = (s32[32]{0:T(128)S(1)}, s32[32]{0:T(128)}, u32[]{:S(2)}) copy-start(s32[32]{0:T(128)} %param.17) | copy-start | bytes 388
  114.5 63.2 %copy-start.94 = (s32[32]{0:T(128)S(1)}, s32[32]{0:T(128)}, u32[]{:S(2)}) copy-start(s32[32]{0:T(128)} %param.16) | copy-start | bytes 388
  118.4 53.3 %collective-permute-start.11 = (bf16[32,256,256]{2,1,0:T(8,128)(2,1)}, bf16[32,256,256]{2,1,0:T(8,128)(2,1)}, u32[]{:S(2)}, u32[]{:S(2)}) collective-permute-start(bf16[32,256,256]{2,1,0:T(8,128)(2,1)} %pad_maximum_fusion), channel_id=1, source_target_pairs={{0,2},{1,5},{2,0},{3,7},{4,6},{5,1},{6,4},{7,3},{8,10},{9,13},{10,... | collective-permute-start | bytes 12582920 | tf_op jit(solution)/shard_map/ppermute | solution.py:89
  120.4 47.8 %collective-permute-start.12 = (bf16[16,256,256]{2,1,0:T(8,128)(2,1)S(1)}, bf16[16,256,256]{2,1,0:T(8,128)(2,1)S(1)}, u32[]{:S(2)}, u32[]{:S(2)}) collective-permute-start(bf16[16,256,256]{2,1,0:T(8,128)(2,1)S(1)} %collective-permute-done.6.refs_0_), channel_id=1, source_target_pairs={{0,16},{16,0},{1,17},{17,1},{2,18},{18,2},{3,19},{19,3},{4,20},{20... | collective-permute-start | bytes 6291464 | tf_op jit(solution)/shard_map/ppermute | solution.py:79
  121.9 46.3 %collective-permute-start.13 = (bf16[16,256,256]{2,1,0:T(8,128)(2,1)S(1)}, bf16[16,256,256]{2,1,0:T(8,128)(2,1)S(1)}, u32[]{:S(2)}, u32[]{:S(2)}) collective-permute-start(bf16[16,256,256]{2,1,0:T(8,128)(2,1)S(1)} %collective-permute-done.6.refs_0_), channel_id=1, source_target_pairs={{0,1},{1,0},{2,3},{3,2},{4,5},{5,4},{6,7},{7,6},{8,9},{9,8},{10,11... | collective-permute-start | bytes 6291464 | tf_op jit(solution)/shard_map/ppermute | solution.py:76
  122.0 47.6 %collective-permute-start.14 = (bf16[16,256,256]{2,1,0:T(8,128)(2,1)S(1)}, bf16[16,256,256]{2,1,0:T(8,128)(2,1)S(1)}, u32[]{:S(2)}, u32[]{:S(2)}) collective-permute-start(bf16[16,256,256]{2,1,0:T(8,128)(2,1)S(1)} %collective-permute-done.7.refs_2_), channel_id=1, source_target_pairs={{0,1},{1,0},{2,3},{3,2},{4,5},{5,4},{6,7},{7,6},{8,9},{9,8},{10,11... | collective-permute-start | bytes 6291464 | tf_op jit(solution)/shard_map/ppermute | solution.py:76
  122.4 22.3 %collective-permute-start.15 = (bf16[12,256,256]{2,1,0:T(8,128)(2,1)}, bf16[12,256,256]{2,1,0:T(8,128)(2,1)S(1)}, u32[]{:S(2)}, u32[]{:S(2)}) collective-permute-start(bf16[12,256,256]{2,1,0:T(8,128)(2,1)} %copy-done.23), channel_id=1, source_target_pairs={{0,1},{1,0},{2,3},{3,2},{4,5},{5,4},{6,7},{7,6},{8,9},{9,8},{10,11... | collective-permute-start | bytes 4718600 | tf_op jit(solution)/shard_map/ppermute | solution.py:76
  171.6 58.4 %collective-permute-start.16 = (bf16[32,256,256]{2,1,0:T(8,128)(2,1)}, bf16[32,256,256]{2,1,0:T(8,128)(2,1)}, u32[]{:S(2)}, u32[]{:S(2)}) collective-permute-start(bf16[32,256,256]{2,1,0:T(8,128)(2,1)} %collective-permute-done.11.refs_0_), channel_id=1, source_target_pairs={{0,1},{1,0},{2,3},{3,2},{4,5},{5,4},{6,7},{7,6},{8,9},{9,8},{10,11... | collective-permute-start | bytes 12582920 | tf_op jit(solution)/shard_map/ppermute | solution.py:76
  171.6 14.6 %collective-permute-start = (bf16[2,512,512]{2,1,0:T(8,128)(2,1)}, bf16[2,512,512]{2,1,0:T(8,128)(2,1)S(1)}, u32[]{:S(2)}, u32[]{:S(2)}) collective-permute-start(bf16[2,512,512]{2,1,0:T(8,128)(2,1)} %param.13), channel_id=1, source_target_pairs={{0,1},{1,0},{2,3},{3,2},{4,5},{5,4},{6,7},{7,6},{8,9},{9,8},{10,11... | collective-permute-start | bytes 3145736 | tf_op jit(solution)/shard_map/ppermute | solution.py:76
  174.1 9.9 %all-to-all-start = ((bf16[8,2,544]{2,1,0:T(2,128)(2,1)}), bf16[8,2,544]{2,1,0:T(2,128)(2,1)S(1)}, u32[]{:S(2)}, u32[]{:S(2)}) async-start(bf16[8,2,544]{2,1,0:T(2,128)(2,1)} %reshape.279), calls=%async_computation | async-start | bytes 40960 | tf_op jit(solution)/shard_map/all_to_all | solution.py:778
  177.5 101.2 %collective-permute-start.19 = (bf16[2,128,512]{2,1,0:T(8,128)(2,1)S(1)}, bf16[2,128,512]{2,1,0:T(8,128)(2,1)S(1)}, u32[]{:S(2)}, u32[]{:S(2)}) collective-permute-start(bf16[2,128,512]{2,1,0:T(8,128)(2,1)S(1)} %copy-done.68), channel_id=1, source_target_pairs={{0,1},{1,0},{2,3},{3,2},{4,5},{5,4},{6,7},{7,6},{8,9},{9,8},{10,11... | collective-permute-start | bytes 786440 | tf_op jit(solution)/shard_map/ppermute | solution.py:76
  184.3 1.7 collective-permute-start.18
  185.5 44.5 %collective-permute-start.17 = (bf16[16,256,256]{2,1,0:T(8,128)(2,1)}, bf16[16,256,256]{2,1,0:T(8,128)(2,1)S(1)}, u32[]{:S(2)}, u32[]{:S(2)}) collective-permute-start(bf16[16,256,256]{2,1,0:T(8,128)(2,1)} %copy-done.17), channel_id=1, source_target_pairs={{0,1},{1,0},{2,3},{3,2},{4,5},{5,4},{6,7},{7,6},{8,9},{9,8},{10,11... | collective-permute-start | bytes 6291464 | tf_op jit(solution)/shard_map/ppermute | solution.py:76
  201.5 81.2 %copy-start.55 = (bf16[512,512]{1,0:T(8,128)(2,1)}, bf16[512,512]{1,0:T(8,128)(2,1)S(1)}, u32[]{:S(2)}) copy-start(bf16[512,512]{1,0:T(8,128)(2,1)S(1)} %get-tuple-element.207) | copy-start | bytes 1572868
  201.5 81.2 %copy-start.57 = (bf16[512,512]{1,0:T(8,128)(2,1)}, bf16[512,512]{1,0:T(8,128)(2,1)S(1)}, u32[]{:S(2)}) copy-start(bf16[512,512]{1,0:T(8,128)(2,1)S(1)} %get-tuple-element.209) | copy-start | bytes 1572868
  259.6 52.3 %all-to-all-start.1 = ((bf16[2,16,32,512]{3,2,0,1:T(8,128)(2,1)}), bf16[2,16,32,512]{3,2,0,1:T(8,128)(2,1)S(1)}, u32[]{:S(2)}, u32[]{:S(2)}) async-start(bf16[2,16,32,512]{3,2,0,1:T(8,128)(2,1)} %copy.91), calls=%async_computation.1 | async-start | bytes 2097152 | tf_op jit(solution)/shard_map/all_to_all | solution.py:704
  313.5 49.9 %all-to-all-start.3 = ((bf16[32,1,32,512]{3,2,1,0:T(8,128)(2,1)}), bf16[32,1,32,512]{3,2,1,0:T(8,128)(2,1)S(1)}, u32[]{:S(2)}, u32[]{:S(2)}) async-start(bf16[32,1,32,512]{3,2,1,0:T(8,128)(2,1)} %bitcast.31), calls=%async_computation.3 | async-start | bytes 2097152 | tf_op jit(solution)/shard_map/all_to_all | solution.py:709
  363.5 10.4 %collective-permute-start.21 = (bf16[2,512,512]{2,1,0:T(8,128)(2,1)S(1)}, bf16[2,512,512]{2,1,0:T(8,128)(2,1)S(1)}, u32[]{:S(2)}, u32[]{:S(2)}) collective-permute-start(bf16[2,512,512]{2,1,0:T(8,128)(2,1)S(1)} %bitcast.156), channel_id=1, source_target_pairs={{0,1},{1,0},{2,3},{3,2},{4,5},{5,4},{6,7},{7,6},{8,9},{9,8},{10,11... | collective-permute-start | bytes 3145736 | tf_op jit(solution)/shard_map/ppermute | solution.py:76
  378.6 2.7 collective-permute-start.20
  382.7 34.2 %all-to-all-start.2 = ((bf16[2,16,32,512]{3,2,0,1:T(8,128)(2,1)}), bf16[2,16,32,512]{3,2,0,1:T(8,128)(2,1)}, u32[]{:S(2)}, u32[]{:S(2)}) async-start(bf16[2,16,32,512]{3,2,0,1:T(8,128)(2,1)} %pad_maximum_fusion.7), calls=%async_computation.2 | async-start | bytes 2097152 | tf_op jit(solution)/shard_map/all_to_all | solution.py:704
  391.9 70.3 %collective-permute-start.37 = (bf16[512,4096]{1,0:T(8,128)(2,1)}, bf16[512,4096]{1,0:T(8,128)(2,1)}, u32[]{:S(2)}, u32[]{:S(2)}) collective-permute-start(bf16[512,4096]{1,0:T(8,128)(2,1)} %get-tuple-element.135.x_own), channel_id=1, source_target_pairs={{0,1},{1,0},{2,3},{3,2},{4,5},{5,4},{6,7},{7,6},{8,9},{9,8},{10,11... | collective-permute-start | bytes 12582920 | tf_op jit(solution)/shard_map/ppermute | solution.py:76
  392.1 62.2 %collective-permute-start.35 = (bf16[512,1024]{1,0:T(8,128)(2,1)}, bf16[512,1024]{1,0:T(8,128)(2,1)}, u32[]{:S(2)}, u32[]{:S(2)}) collective-permute-start(bf16[512,1024]{1,0:T(8,128)(2,1)} %fusion.4.h_ref.x_own), channel_id=1, source_target_pairs={{0,1},{1,0},{2,3},{3,2},{4,5},{5,4},{6,7},{7,6},{8,9},{9,8},{10,11... | collective-permute-start | bytes 3145736 | tf_op jit(solution)/shard_map/ppermute | solution.py:76
  392.4 66.8 %collective-permute-start.33 = (bf16[512,1024]{1,0:T(8,128)(2,1)}, bf16[512,1024]{1,0:T(8,128)(2,1)}, u32[]{:S(2)}, u32[]{:S(2)}) collective-permute-start(bf16[512,1024]{1,0:T(8,128)(2,1)} %get-tuple-element.133.o_ref.x_own), channel_id=1, source_target_pairs={{0,1},{1,0},{2,3},{3,2},{4,5},{5,4},{6,7},{7,6},{8,9},{9,8},{10,11... | collective-permute-start | bytes 3145736 | tf_op jit(solution)/shard_map/ppermute | solution.py:76
  392.6 66.8 %collective-permute-start.31 = (bf16[512,1024]{1,0:T(8,128)(2,1)}, bf16[512,1024]{1,0:T(8,128)(2,1)}, u32[]{:S(2)}, u32[]{:S(2)}) collective-permute-start(bf16[512,1024]{1,0:T(8,128)(2,1)} %fusion.3.x_own), channel_id=1, source_target_pairs={{0,1},{1,0},{2,3},{3,2},{4,5},{5,4},{6,7},{7,6},{8,9},{9,8},{10,11... | collective-permute-start | bytes 3145736 | tf_op jit(solution)/shard_map/ppermute | solution.py:76
  396.4 57.9 %copy-start.48 = (bf16[512,1024]{1,0:T(8,128)(2,1)}, bf16[512,1024]{1,0:T(8,128)(2,1)S(1)}, u32[]{:S(2)}) copy-start(bf16[512,1024]{1,0:T(8,128)(2,1)S(1)} %convert_element_type.226.y_own) | copy-start | bytes 3145732
  416.8 69.7 %collective-permute-start.36 = (bf16[512,4096]{1,0:T(8,128)(2,1)}, bf16[512,4096]{1,0:T(8,128)(2,1)}, u32[]{:S(2)}, u32[]{:S(2)}) collective-permute-start(bf16[512,4096]{1,0:T(8,128)(2,1)} %multiply_convert_fusion.y_own), channel_id=1, source_target_pairs={{0,1},{1,0},{2,3},{3,2},{4,5},{5,4},{6,7},{7,6},{8,9},{9,8},{10,11... | collective-permute-start | bytes 12582920 | tf_op jit(solution)/shard_map/ppermute | solution.py:76
  435.1 31.8 %all-to-all-start.4 = ((bf16[32,1,32,512]{3,2,1,0:T(8,128)(2,1)}), bf16[32,1,32,512]{3,2,1,0:T(8,128)(2,1)}, u32[]{:S(2)}, u32[]{:S(2)}) async-start(bf16[32,1,32,512]{3,2,1,0:T(8,128)(2,1)} %bitcast.153), calls=%async_computation.4 | async-start | bytes 2097152 | tf_op jit(solution)/shard_map/all_to_all | solution.py:709
  454.3 7.7 collective-permute-start.38
  459.3 26.8 %collective-permute-start.34 = (bf16[512,1024]{1,0:T(8,128)(2,1)}, bf16[512,1024]{1,0:T(8,128)(2,1)}, u32[]{:S(2)}, u32[]{:S(2)}) collective-permute-start(bf16[512,1024]{1,0:T(8,128)(2,1)} %convert_element_type.229.y_own), channel_id=1, source_target_pairs={{0,1},{1,0},{2,3},{3,2},{4,5},{5,4},{6,7},{7,6},{8,9},{9,8},{10,11... | collective-permute-start | bytes 3145736 | tf_op jit(solution)/shard_map/ppermute | solution.py:76
  459.4 26.8 %collective-permute-start.32 = (bf16[512,1024]{1,0:T(8,128)(2,1)}, bf16[512,1024]{1,0:T(8,128)(2,1)}, u32[]{:S(2)}, u32[]{:S(2)}) collective-permute-start(bf16[512,1024]{1,0:T(8,128)(2,1)} %get-tuple-element.142.y_own), channel_id=1, source_target_pairs={{0,1},{1,0},{2,3},{3,2},{4,5},{5,4},{6,7},{7,6},{8,9},{9,8},{10,11... | collective-permute-start | bytes 3145736 | tf_op jit(solution)/shard_map/ppermute | solution.py:76
  462.1 23.4 %collective-permute-start.30 = (bf16[128,1024]{1,0:T(8,128)(2,1)}, bf16[128,1024]{1,0:T(8,128)(2,1)}, u32[]{:S(2)}, u32[]{:S(2)}) collective-permute-start(bf16[128,1024]{1,0:T(8,128)(2,1)} %get-tuple-element.149.y_own), channel_id=1, source_target_pairs={{0,1},{1,0},{2,3},{3,2},{4,5},{5,4},{6,7},{7,6},{8,9},{9,8},{10,11... | collective-permute-start | bytes 786440 | tf_op jit(solution)/shard_map/ppermute | solution.py:76
  462.2 23.4 %collective-permute-start.29 = (bf16[128,1024]{1,0:T(8,128)(2,1)S(1)}, bf16[128,1024]{1,0:T(8,128)(2,1)}, u32[]{:S(2)}, u32[]{:S(2)}) collective-permute-start(bf16[128,1024]{1,0:T(8,128)(2,1)S(1)} %copy-done.59), channel_id=1, source_target_pairs={{0,1},{1,0},{2,3},{3,2},{4,5},{5,4},{6,7},{7,6},{8,9},{9,8},{10,11... | collective-permute-start | bytes 786440 | tf_op jit(solution)/shard_map/ppermute | solution.py:76
  485.5 40.8 %collective-permute-start.27 = (bf16[512,1024]{1,0:T(8,128)(2,1)S(1)}, bf16[512,1024]{1,0:T(8,128)(2,1)S(1)}, u32[]{:S(2)}, u32[]{:S(2)}) collective-permute-start(bf16[512,1024]{1,0:T(8,128)(2,1)S(1)} %copy-done.61), channel_id=1, source_target_pairs={{0,1},{1,0},{2,3},{3,2},{4,5},{5,4},{6,7},{7,6},{8,9},{9,8},{10,11... | collective-permute-start | bytes 3145736 | tf_op jit(solution)/shard_map/ppermute | solution.py:76
  485.6 40.7 %collective-permute-start.28 = (bf16[512,1024]{1,0:T(8,128)(2,1)S(1)}, bf16[512,1024]{1,0:T(8,128)(2,1)}, u32[]{:S(2)}, u32[]{:S(2)}) collective-permute-start(bf16[512,1024]{1,0:T(8,128)(2,1)S(1)} %convert_element_type.231.y_own), channel_id=1, source_target_pairs={{0,1},{1,0},{2,3},{3,2},{4,5},{5,4},{6,7},{7,6},{8,9},{9,8},{10,11... | collective-permute-start | bytes 3145736 | tf_op jit(solution)/shard_map/ppermute | solution.py:76
  486.0 45.9 %collective-permute-start.26 = (bf16[512,1024]{1,0:T(8,128)(2,1)}, bf16[512,1024]{1,0:T(8,128)(2,1)}, u32[]{:S(2)}, u32[]{:S(2)}) collective-permute-start(bf16[512,1024]{1,0:T(8,128)(2,1)} %get-tuple-element.146.y_own), channel_id=1, source_target_pairs={{0,1},{1,0},{2,3},{3,2},{4,5},{5,4},{6,7},{7,6},{8,9},{9,8},{10,11... | collective-permute-start | bytes 3145736 | tf_op jit(solution)/shard_map/ppermute | solution.py:76
  486.1 51.3 %collective-permute-start.25 = (bf16[512,1024]{1,0:T(8,128)(2,1)}, bf16[512,1024]{1,0:T(8,128)(2,1)}, u32[]{:S(2)}, u32[]{:S(2)}) collective-permute-start(bf16[512,1024]{1,0:T(8,128)(2,1)} %get-tuple-element.147.y_own), channel_id=1, source_target_pairs={{0,1},{1,0},{2,3},{3,2},{4,5},{5,4},{6,7},{7,6},{8,9},{9,8},{10,11... | collective-permute-start | bytes 3145736 | tf_op jit(solution)/shard_map/ppermute | solution.py:76
  486.6 56.3 %collective-permute-start.24 = (bf16[512,1024]{1,0:T(8,128)(2,1)}, bf16[512,1024]{1,0:T(8,128)(2,1)}, u32[]{:S(2)}, u32[]{:S(2)}) collective-permute-start(bf16[512,1024]{1,0:T(8,128)(2,1)} %get-tuple-element.148.y_own), channel_id=1, source_target_pairs={{0,1},{1,0},{2,3},{3,2},{4,5},{5,4},{6,7},{7,6},{8,9},{9,8},{10,11... | collective-permute-start | bytes 3145736 | tf_op jit(solution)/shard_map/ppermute | solution.py:76
  567.6 50.3 %collective-permute-start.40 = (bf16[32,256,256]{2,1,0:T(8,128)(2,1)}, bf16[32,256,256]{2,1,0:T(8,128)(2,1)}, u32[]{:S(2)}, u32[]{:S(2)}) collective-permute-start(bf16[32,256,256]{2,1,0:T(8,128)(2,1)} %get-tuple-element.152), channel_id=1, source_target_pairs={{0,2},{1,5},{2,0},{3,7},{4,6},{5,1},{6,4},{7,3},{8,10},{9,13},{10,... | collective-permute-start | bytes 12582920 | tf_op jit(solution)/shard_map/ppermute | solution.py:89
  569.5 48.4 %collective-permute-start.39 = (bf16[16,256,256]{2,1,0:T(8,128)(2,1)}, bf16[16,256,256]{2,1,0:T(8,128)(2,1)}, u32[]{:S(2)}, u32[]{:S(2)}) collective-permute-start(bf16[16,256,256]{2,1,0:T(8,128)(2,1)} %get-tuple-element.151), channel_id=1, source_target_pairs={{0,16},{16,0},{1,17},{17,1},{2,18},{18,2},{3,19},{19,3},{4,20},{20... | collective-permute-start | bytes 6291464 | tf_op jit(solution)/shard_map/ppermute | solution.py:79
  581.8 51.7 %collective-permute-start.23 = (bf16[128,512]{1,0:T(8,128)(2,1)S(1)}, bf16[128,512]{1,0:T(8,128)(2,1)}, u32[]{:S(2)}, u32[]{:S(2)}) collective-permute-start(bf16[128,512]{1,0:T(8,128)(2,1)S(1)} %constant_dynamic-slice_fusion), channel_id=1, source_target_pairs={{0,1},{1,0},{2,3},{3,2},{4,5},{5,4},{6,7},{7,6},{8,9},{9,8},{10,11... | collective-permute-start | bytes 393224 | tf_op jit(solution)/shard_map/ppermute | solution.py:76
  621.5 44.1 %collective-permute-start.42 = (bf16[16,256,256]{2,1,0:T(8,128)(2,1)}, bf16[16,256,256]{2,1,0:T(8,128)(2,1)}, u32[]{:S(2)}, u32[]{:S(2)}) collective-permute-start(bf16[16,256,256]{2,1,0:T(8,128)(2,1)} %add_convert_fusion.1), channel_id=1, source_target_pairs={{0,4},{1,3},{2,6},{3,1},{4,0},{5,7},{6,2},{7,5},{8,12},{9,11},{10,... | collective-permute-start | bytes 6291464 | tf_op jit(solution)/shard_map/ppermute | solution.py:89
  627.1 49.8 %collective-permute-start.41 = (bf16[16,256,256]{2,1,0:T(8,128)(2,1)}, bf16[16,256,256]{2,1,0:T(8,128)(2,1)}, u32[]{:S(2)}, u32[]{:S(2)}) collective-permute-start(bf16[16,256,256]{2,1,0:T(8,128)(2,1)} %get-tuple-element.201), channel_id=1, source_target_pairs={{0,8},{1,3},{2,10},{3,1},{4,12},{5,7},{6,14},{7,5},{8,0},{9,11},{1... | collective-permute-start | bytes 6291464 | tf_op jit(solution)/shard_map/ppermute | solution.py:89
  629.5 47.4 %collective-permute-start.43 = (bf16[16,256,256]{2,1,0:T(8,128)(2,1)}, bf16[16,256,256]{2,1,0:T(8,128)(2,1)}, u32[]{:S(2)}, u32[]{:S(2)}) collective-permute-start(bf16[16,256,256]{2,1,0:T(8,128)(2,1)} %get-tuple-element.162), channel_id=1, source_target_pairs={{0,16},{16,0},{1,17},{17,1},{2,18},{18,2},{3,19},{19,3},{4,20},{20... | collective-permute-start | bytes 6291464 | tf_op jit(solution)/shard_map/ppermute | solution.py:79
  681.3 18.1 %collective-permute-start.45 = (bf16[8,256,256]{2,1,0:T(8,128)(2,1)}, bf16[8,256,256]{2,1,0:T(8,128)(2,1)}, u32[]{:S(2)}, u32[]{:S(2)}) collective-permute-start(bf16[8,256,256]{2,1,0:T(8,128)(2,1)} %get-tuple-element.204), channel_id=1, source_target_pairs={{0,2},{1,5},{2,0},{3,7},{4,6},{5,1},{6,4},{7,3},{8,10},{9,13},{10,... | collective-permute-start | bytes 3145736 | tf_op jit(solution)/shard_map/ppermute | solution.py:89
  684.4 30.4 %collective-permute-start.44 = (bf16[8,256,256]{2,1,0:T(8,128)(2,1)}, bf16[8,256,256]{2,1,0:T(8,128)(2,1)}, u32[]{:S(2)}, u32[]{:S(2)}) collective-permute-start(bf16[8,256,256]{2,1,0:T(8,128)(2,1)} %add_convert_fusion.7), channel_id=1, source_target_pairs={{0,4},{1,9},{2,6},{3,11},{4,0},{5,13},{6,2},{7,15},{8,12},{9,1},{1... | collective-permute-start | bytes 3145736 | tf_op jit(solution)/shard_map/ppermute | solution.py:89
  684.8 9.9 %collective-permute-start.49 = (f32[8704]{0:T(1024)S(1)}, f32[8704]{0:T(1024)S(1)}, u32[]{:S(2)}, u32[]{:S(2)}) collective-permute-start(f32[8704]{0:T(1024)S(1)} %get-tuple-element.186), channel_id=1, source_target_pairs={{0,1},{1,0},{2,3},{3,2},{4,5},{5,4},{6,7},{7,6},{8,9},{9,8},{10,11... | collective-permute-start | bytes 104456 | tf_op jit(solution)/shard_map/ppermute | solution.py:76
  695.3 26.2 %all-to-all-start.5 = ((f32[8,1,1088]{2,1,0:T(1,128)}), f32[8,1,1088]{2,1,0:T(1,128)S(1)}, u32[]{:S(2)}, u32[]{:S(2)}) async-start(f32[8,1,1088]{2,1,0:T(1,128)} %all_to_all.73), calls=%async_computation.5 | async-start | bytes 73728 | tf_op jit(solution)/shard_map/all_to_all | solution.py:886
  717.7 32.1 %collective-permute-start.46 = (bf16[8,256,256]{2,1,0:T(8,128)(2,1)}, bf16[8,256,256]{2,1,0:T(8,128)(2,1)}, u32[]{:S(2)}, u32[]{:S(2)}) collective-permute-start(bf16[8,256,256]{2,1,0:T(8,128)(2,1)} %add_convert_fusion.4), channel_id=1, source_target_pairs={{0,16},{16,0},{1,17},{17,1},{2,18},{18,2},{3,19},{19,3},{4,20},{20... | collective-permute-start | bytes 3145736 | tf_op jit(solution)/shard_map/ppermute | solution.py:79
  721.6 20.9 %collective-permute-start.50 = (f32[1,1088]{1,0:T(1,128)S(1)}, f32[1,1088]{1,0:T(1,128)S(1)}, u32[]{:S(2)}, u32[]{:S(2)}) collective-permute-start(f32[1,1088]{1,0:T(1,128)S(1)} %broadcast_in_dim.62), channel_id=1, source_target_pairs={{0,16},{16,0},{1,17},{17,1},{2,18},{18,2},{3,19},{19,3},{4,20},{20... | collective-permute-start | bytes 13064 | tf_op jit(solution)/shard_map/ppermute | solution.py:79
  724.6 25.2 %collective-permute-start.47 = (bf16[4,256,256]{2,1,0:T(8,128)(2,1)S(1)}, bf16[4,256,256]{2,1,0:T(8,128)(2,1)S(1)}, u32[]{:S(2)}, u32[]{:S(2)}) collective-permute-start(bf16[4,256,256]{2,1,0:T(8,128)(2,1)S(1)} %add_convert_fusion.14), channel_id=1, source_target_pairs={{0,8},{1,9},{2,10},{3,11},{4,12},{5,13},{6,14},{7,15},{8,0},{9,1},... | collective-permute-start | bytes 1572872 | tf_op jit(solution)/shard_map/ppermute | solution.py:89
  728.3 23.2 %collective-permute-start.22 = (bf16[512,512]{1,0:T(8,128)(2,1)S(1)}, bf16[512,512]{1,0:T(8,128)(2,1)S(1)}, u32[]{:S(2)}, u32[]{:S(2)}) collective-permute-start(bf16[512,512]{1,0:T(8,128)(2,1)S(1)} %constant_dynamic-slice_fusion.1), channel_id=1, source_target_pairs={{0,1},{1,0},{2,3},{3,2},{4,5},{5,4},{6,7},{7,6},{8,9},{9,8},{10,11... | collective-permute-start | bytes 1572872 | tf_op jit(solution)/shard_map/ppermute | solution.py:76
  751.0 11.5 %collective-permute-start.48 = (bf16[4,256,256]{2,1,0:T(8,128)(2,1)S(1)}, bf16[4,256,256]{2,1,0:T(8,128)(2,1)S(1)}, u32[]{:S(2)}, u32[]{:S(2)}) collective-permute-start(bf16[4,256,256]{2,1,0:T(8,128)(2,1)S(1)} %add_convert_fusion.13), channel_id=1, source_target_pairs={{0,16},{16,0},{1,17},{17,1},{2,18},{18,2},{3,19},{19,3},{4,20},{20... | collective-permute-start | bytes 1572872 | tf_op jit(solution)/shard_map/ppermute | solution.py:79
  (90 other events, 793.6 us)

commit v2 on v1

v2 whole, which is shorter than its diff:
```python
import functools

import jax
import jax.numpy as jnp
import numpy as np
from jax import lax
from jax.experimental import pallas as pl
from jax.experimental.pallas import tpu as pltpu
from jax.sharding import PartitionSpec as P

D = 1024
FF = 4096
HEAD_DIM = 64
BS = 256
LANES = 128

eps_norm = 1e-05
masked_score = -1e30
scale = HEAD_DIM**-0.5
bf16 = jnp.bfloat16
f32 = jnp.float32

NT = (((1,), (1,)), ((), ()))
TN = (((0,), (0,)), ((), ()))

VMEM_LIMIT = 60 * 1024 * 1024

ERFC_SLOPE = 0.3
ERFC_POLY = (
    0.1691880090604902,
    0.17071516163759975,
    0.14833963774537734,
    0.21492421686136995,
    -0.09464635292673967,
    0.5477136065073498,
    -0.5122723795383668,
    0.4855603950654946,
    -0.1295223139805042,
)


def dot_nn(a, b):
    return jnp.dot(a, b, preferred_element_type=f32)


def dot_nt(a, b):
    return lax.dot_general(a, b, NT, preferred_element_type=f32)


def dot_tn(a, b):
    return lax.dot_general(a, b, TN, preferred_element_type=f32)


def params(**kw):
    return pltpu.CompilerParams(vmem_limit_bytes=VMEM_LIMIT, **kw)


GROUPS = (
    (("sq", True), ("sk", True), ("sv", True)),
    (("so", False), ("cq", True), ("ck", True), ("cv", True), ("co", False)),
    (("fi", True),),
    (("fo", False),),
)
SHAPES = {name: (D, D) for name in ("sq", "sk", "sv", "so", "cq", "ck", "cv", "co")}
SHAPES["fi"], SHAPES["fo"] = (D, FF), (FF, D)


class Net:
    def __init__(self, n_rep, n_shard, n_mp):
        self.n_rep, self.n_shard, self.n_mp = n_rep, n_shard, n_mp
        self.n_data = n_rep * n_shard
        power = self.n_data & (self.n_data - 1) == 0
        self.pieces = self.n_data if power and BS % (16 * self.n_data) == 0 else 1
        self.rows = BS // self.pieces
        self.depth = self.pieces.bit_length() - 1
        if self.pieces == 16:
            x, z1, z2, y = 1, 2, 4, 8
            self.orders = (
                ((z2, y, z1, x), (z2, z1, x, y)),
                ((z2, y, z1, x), (z2, x, z1, y)),
                ((z2, z1, x, y), (z2, x, y, z1)),
                ((z2, y, z1, x), (z2, x, y, z1)),
            )
        else:
            down = tuple(1 << s for s in range(self.depth - 1, -1, -1))
            self.orders = ((down,) * n_mp,) * len(GROUPS)

    def swap_core(self, value):
        return lax.ppermute(value, "mp", [(i, i ^ 1) for i in range(self.n_mp)])

    def swap_rep(self, value):
        return lax.ppermute(value, "rep", [(i, i ^ 1) for i in range(self.n_rep)])

    def swap_data(self, value, group, step):
        pairs = []
        for i in range(self.n_data):
            for m in range(self.n_mp):
                there = i ^ self.orders[group][m][step]
                pairs.append((i * self.n_mp + m, there * self.n_mp + m))
        return lax.ppermute(value, ("rep", "shard", "mp"), pairs)

    def table(self, group, core, data_index):
        many = self.pieces
        half = max(many // 2, 1)
        rel = []
        for order in self.orders[group]:
            rel.append([sum(b for s, b in enumerate(order) if q >> s & 1) for q in range(many)])
        rows = []
        for m in range(self.n_mp):
            place = [rel[self.n_mp - 1 - m].index(r) for r in rel[m]]
            low = [p for p in place if p < half][0]
            high = ([p - half for p in place if p >= half] or [0])[0]
            lows, highs = [], []
            for p in place:
                low, high = (p, high) if p < half else (low, p - half)
                lows.append(low)
                highs.append(high)
            rows.append([rel[m], lows, highs, [int(p >= half) for p in place]])
        mine = jnp.asarray(np.array(rows, np.int32))[core]
        mine = mine.at[0].set(mine[0] ^ data_index)
        return jnp.concatenate([mine.reshape(-1), core.reshape(1)]).astype(jnp.int32)


def together(*values):
    return lax.optimization_barrier(values)


class Flow:
    def __init__(self, rounds):
        self.rounds = rounds
        self.flying = next(rounds)

    def advance(self, values):
        try:
            self.flying = self.rounds.send(values)
        except StopIteration as stop:
            self.flying = None
            self.result = stop.value

    def finish(self):
        while self.flying is not None:
            self.advance(self.flying)
        return self.result


def step(main, *flows):
    flows = [f for f in flows if f.flying is not None]
    values = list(together(*main, *[v for f in flows for v in f.flying]))
    main, values = values[: len(main)], values[len(main) :]
    for f in flows:
        many = len(f.flying)
        f.advance(tuple(values[:many]))
        values = values[many:]
    return main


def blocks_of(name, n_mp):
    rows, cols = SHAPES[name]
    return rows * cols // n_mp // (BS * BS)


def group_blocks(group, n_mp):
    return sum(blocks_of(name, n_mp) for name, _ in GROUPS[group])


def place_body(s, *refs, dests, many, half, two):
    q = pl.program_id(0)
    if two:
        own_lo, own_hi, sib_lo, sib_hi = refs[:4]
        outs = refs[4:]
    else:
        own_lo, sib_lo = refs[:2]
        outs = refs[2:]
    core = s[4 * many]
    for b in range(own_lo.shape[1]):
        own, sib = own_lo[0, b], sib_lo[0, b]
        if two:
            own = jnp.where(q < half, own, own_hi[0, b])
            sib = jnp.where(s[3 * many + q] == 0, sib, sib_hi[0, b])
        for h in range(2):
            which, row, col = dests[h][b]
            outs[which][row, :, col : col + BS] = jnp.where(core == h, own, sib)


def place(net, group, table, own, sib):
    many, rows, n_mp = net.pieces, net.rows, net.n_mp
    two = many > 1
    half = max(many // 2, 1)
    dests = ([], [])
    shapes, specs = [], []
    for which, (name, wide) in enumerate(GROUPS[group]):
        height, width = SHAPES[name]
        tall = height if wide else height // n_mp
        flat = width // n_mp if wide else width
        for h in range(n_mp):
            for r in range(tall // BS):
                for c in range(flat // BS):
                    if wide:
                        dests[h].append((which, r, h * flat + c * BS))
                    else:
                        dests[h].append((which, h * (tall // BS) + r, c * BS))
        shapes.append(jax.ShapeDtypeStruct((height // BS, BS, width), bf16))
        specs.append(pl.BlockSpec((height // BS, rows, width), lambda q, s: (0, s[q], 0)))
    nb = own[0].shape[1]
    block = (1, nb, rows, BS)
    lo = pl.BlockSpec(block, lambda q, s: (jnp.minimum(q, half - 1), 0, 0, 0))
    hi = pl.BlockSpec(block, lambda q, s: (jnp.maximum(q - half, 0), 0, 0, 0))
    sib_lo = pl.BlockSpec(block, lambda q, s: (s[many + q], 0, 0, 0))
    sib_hi = pl.BlockSpec(block, lambda q, s: (s[2 * many + q], 0, 0, 0))
    out = pl.pallas_call(
        functools.partial(place_body, dests=dests, many=many, half=half, two=two),
        grid_spec=pltpu.PrefetchScalarGridSpec(
            num_scalar_prefetch=1,
            grid=(many,),
            in_specs=[lo, hi, sib_lo, sib_hi] if two else [lo, sib_lo],
            out_specs=tuple(specs),
        ),
        out_shape=tuple(shapes),
        compiler_params=params(),
        cost_estimate=pl.CostEstimate(
            flops=0, bytes_accessed=8 * many * nb * rows * BS, transcendentals=0
        ),
        name="place",
    )(table, *own, *sib)
    return [o.reshape(-1, o.shape[2]) for o in out]


def gather_rounds(net, group, piece):
    (piece,) = yield (piece,)
    cur = piece[None]
    if net.pieces == 1:
        (sib,) = yield (net.swap_core(cur),)
        return (cur,), (sib,)
    for k in range(net.depth - 1):
        (got,) = yield (net.swap_data(cur, group, k),)
        cur = jnp.concatenate([cur, got])
    got, sib_lo = yield (net.swap_data(cur, group, net.depth - 1), net.swap_core(cur))
    (sib_hi,) = yield (net.swap_core(got),)
    return (cur, got), (sib_lo, sib_hi)


def first_pieces(net, weights, inverse):
    low = weights[0].astype(bf16)
    if net.pieces == 1:
        every = lax.all_gather(low, "shard", axis=0, tiled=True)
    else:
        plane = lax.axis_index("rep")
        nblk = low.shape[0]
        cut = low.reshape(nblk, net.n_rep, net.n_shard, net.rows, BS)
        cut = lax.dynamic_index_in_dim(cut, plane, axis=1, keepdims=False)
        cut = jnp.swapaxes(cut, 0, 1).reshape(-1, net.rows, BS)
        every = lax.all_to_all(cut, "shard", split_axis=0, concat_axis=0, tiled=True)
    return every.at[inverse].get(mode="promise_in_bounds")


def total_of(*terms):
    acc = terms[0].astype(f32)
    for t in terms[1:]:
        acc = acc + t.astype(f32)
    return acc.astype(bf16)


def reduce_rounds(net, group, parts):
    parts = yield parts
    if net.pieces == 1:
        return parts[0][0]
    lo, hi = parts
    (got,) = yield (net.swap_data(hi, group, net.depth - 1),)
    terms = [lo, got]
    for k in range(net.depth - 2, -1, -1):
        width = 1 << k
        send = total_of(*[t[width:] for t in terms])
        keep = total_of(*[t[:width] for t in terms])
        (got,) = yield (net.swap_data(send, group, k),)
        terms = [keep, got]
    return total_of(*terms)[0]


def last_pieces(net, natural, block_slots):
    dealt = natural.at[block_slots].get(mode="promise_in_bounds")
    if net.pieces == 1:
        owned = lax.psum_scatter(dealt, "shard", scatter_dimension=0, tiled=True)
        owned = total_of(owned, net.swap_rep(owned))
        cut = owned.reshape(-1, 2, BS // 32, 16, BS).transpose(1, 2, 0, 3, 4)
        return cut[0], cut[1], jnp.zeros((1,), jnp.int32)
    mine = lax.all_to_all(dealt, "shard", split_axis=0, concat_axis=0, tiled=True)
    mine = mine.reshape(net.n_shard, -1, net.rows, BS)
    return mine, net.swap_rep(mine), lax.axis_index("rep").astype(jnp.int32).reshape(1)


def attend_forward_body(lim, q_ref, k_ref, v_ref, o_ref, lse_ref, *, causal, rows):
    pair = pl.program_id(0)
    seq, keys = q_ref.shape[0], k_ref.shape[0]
    lane = lax.broadcasted_iota(jnp.int32, (1, LANES), 1)
    top = lim[0] - 1

    @pl.when(pair == 0)
    def _():
        lse_ref[...] = jnp.zeros_like(lse_ref)

    for blk in range(seq // rows):
        here = pl.ds(blk * rows, rows)
        width = (blk + 1) * rows if causal else keys
        q = q_ref[here, :] * bf16(scale)
        k = k_ref[pl.ds(0, width), :]
        v = v_ref[pl.ds(0, width), :]
        outs = []
        kept = lse_ref[here, :]
        if causal:
            row = lax.broadcasted_iota(jnp.int32, (rows, 1), 0) + blk * rows
            col = lax.broadcasted_iota(jnp.int32, (1, width), 1)
            allowed = col <= jnp.minimum(row, top)
        for h in range(2):
            mine = (lane // HEAD_DIM) == h
            s = dot_nt(jnp.where(mine, q, bf16(0)), k)
            if causal:
                s = jnp.where(allowed, s, masked_score)
            peak = jnp.max(s, axis=1, keepdims=True)
            e = jnp.exp(s - peak)
            mass = jnp.sum(e, axis=1, keepdims=True)
            outs.append(dot_nn(e.astype(bf16), v) * (1.0 / mass))
            kept = jnp.where(lane == 2 * pair + h, peak + jnp.log(mass), kept)
        o_ref[here, :] = jnp.where(lane < HEAD_DIM, outs[0], outs[1]).astype(bf16)
        lse_ref[here, :] = kept


def attend_forward(limit, q, k, v, causal):
    seq, width = q.shape
    keys = k.shape[0]
    pairs = width // LANES
    rows = min(128 if causal else 256, seq)
    o, lse = pl.pallas_call(
        functools.partial(attend_forward_body, causal=causal, rows=rows),
        grid=(pairs,),
        out_shape=(
            jax.ShapeDtypeStruct((seq, width), bf16),
            jax.ShapeDtypeStruct((seq, LANES), f32),
        ),
        in_specs=[
            pl.BlockSpec(memory_space=pltpu.SMEM),
            pl.BlockSpec((seq, LANES), lambda i: (0, i)),
            pl.BlockSpec((keys, LANES), lambda i: (0, i)),
            pl.BlockSpec((keys, LANES), lambda i: (0, i)),
        ],
        out_specs=(
            pl.BlockSpec((seq, LANES), lambda i: (0, i)),
            pl.BlockSpec((seq, LANES), lambda i: (0, 0)),
        ),
        compiler_params=params(),
        cost_estimate=pl.CostEstimate(
            flops=4 * seq * keys * width, bytes_accessed=8 * seq * width, transcendentals=0
        ),
        name="attend_forward",
    )(limit, q, k, v)
    return o, lse[:, : 2 * pairs].T.reshape(pairs, 2, seq)


def attend_backward_body(
    lim, q_ref, k_ref, v_ref, o_ref, do_ref, lse_ref, dq_ref, dk_ref, dv_ref, dk_acc, dv_acc, *, causal, rows
):
    seq, keys = q_ref.shape[0], k_ref.shape[0]
    lane = lax.broadcasted_iota(jnp.int32, (1, LANES), 1)
    top = lim[0] - 1
    dk_acc[...] = jnp.zeros_like(dk_acc)
    dv_acc[...] = jnp.zeros_like(dv_acc)
    head_row = lax.broadcasted_iota(jnp.int32, (8, LANES), 0)
    head_lane = lax.broadcasted_iota(jnp.int32, (8, LANES), 1) // HEAD_DIM
    pick = (head_row == head_lane).astype(bf16)
    for blk in range(seq // rows):
        here = pl.ds(blk * rows, rows)
        width = (blk + 1) * rows if causal else keys
        span = pl.ds(0, width)
        q = q_ref[here, :] * bf16(scale)
        do = do_ref[here, :]
        k = k_ref[span, :]
        v = v_ref[span, :]
        prod = do.astype(f32) * o_ref[here, :].astype(f32)
        hi = prod.astype(bf16)
        lo = (prod - hi.astype(f32)).astype(bf16)
        delta = dot_nt(pick, hi) + dot_nt(pick, lo)
        lse = lse_ref[0][:, blk * rows : (blk + 1) * rows]
        if causal:
            key = lax.broadcasted_iota(jnp.int32, (width, 1), 0)
            row = lax.broadcasted_iota(jnp.int32, (1, rows), 1) + blk * rows
            allowed = key <= jnp.minimum(row, top)
        dq = jnp.zeros((rows, LANES), f32)
        dk = jnp.zeros((width, LANES), f32)
        dv = jnp.zeros((width, LANES), f32)
        for h in range(2):
            mine = (lane // HEAD_DIM) == h
            qm = jnp.where(mine, q, bf16(0))
            dom = jnp.where(mine, do, bf16(0))
            km = jnp.where(mine, k, bf16(0))
            s = dot_nt(k, qm)
            if causal:
                s = jnp.where(allowed, s, masked_score)
            p = jnp.exp(s - lse[h : h + 1, :])
            dp = dot_nt(v, dom)
            ds = (p * (dp - delta[h : h + 1, :])).astype(bf16)
            dv = dv + dot_nn(p.astype(bf16), dom)
            dk = dk + dot_nn(ds, qm)
            dq = dq + dot_tn(ds, km)
        dq_ref[here, :] = (dq * scale).astype(bf16)
        dk_acc[span, :] += dk
        dv_acc[span, :] += dv
    dk_ref[...] = dk_acc[...].astype(bf16)
    dv_ref[...] = dv_acc[...].astype(bf16)


def attend_backward(limit, q, k, v, o, do, lse, causal):
    seq, width = q.shape
    keys = k.shape[0]
    pairs = width // LANES
    rows = min(128 if causal else 256, seq)
    q_spec = pl.BlockSpec((seq, LANES), lambda i: (0, i))
    k_spec = pl.BlockSpec((keys, LANES), lambda i: (0, i))
    return pl.pallas_call(
        functools.partial(attend_backward_body, causal=causal, rows=rows),
        grid=(pairs,),
        out_shape=(
            jax.ShapeDtypeStruct((seq, width), bf16),
            jax.ShapeDtypeStruct((keys, width), bf16),
            jax.ShapeDtypeStruct((keys, width), bf16),
        ),
        in_specs=[
            pl.BlockSpec(memory_space=pltpu.SMEM),
            q_spec,
            k_spec,
            k_spec,
            q_spec,
            q_spec,
            pl.BlockSpec((1, 2, seq), lambda i: (i, 0, 0)),
        ],
        out_specs=(q_spec, k_spec, k_spec),
        scratch_shapes=[pltpu.VMEM((keys, LANES), f32), pltpu.VMEM((keys, LANES), f32)],
        compiler_params=params(),
        cost_estimate=pl.CostEstimate(
            flops=10 * seq * keys * width, bytes_accessed=16 * seq * width, transcendentals=0
        ),
        name="attend_backward",
    )(limit, q, k, v, o, do, lse)


def gelu_body(h_ref, w_ref, b_ref, act_ref, slope_ref, u_ref, *, chunk):
    u_ref[...] = dot_nn(h_ref[...], w_ref[...]) + b_ref[...]

    def part(i):
        here = pl.ds(pl.multiple_of(i * chunk, chunk), chunk)
        u = u_ref[here, :]
        x = jnp.abs(u) * (0.5**0.5)
        t = 1.0 / (1.0 + ERFC_SLOPE * x)
        poly = jnp.full_like(t, ERFC_POLY[-1])
        for c in ERFC_POLY[-2::-1]:
            poly = poly * t + c
        bell = jnp.exp(-0.5 * (u * u))
        tail = 0.5 * (bell * (t * poly))
        cdf = jnp.where(u < 0, tail, 1.0 - tail)
        act_ref[here, :] = (u * cdf).astype(bf16)
        slope_ref[here, :] = (cdf + u * (bell * 0.3989422804014327)).astype(bf16)

    pl.loop(0, u_ref.shape[0] // chunk)(part)


def gelu_forward(h, w, b):
    seq, width = h.shape
    hidden = w.shape[1]
    tile = 512
    spec = pl.BlockSpec((seq, tile), lambda i: (0, i))
    return pl.pallas_call(
        functools.partial(gelu_body, chunk=32),
        grid=(hidden // tile,),
        out_shape=(jax.ShapeDtypeStruct((seq, hidden), bf16),) * 2,
        in_specs=[
            pl.BlockSpec((seq, width), lambda i: (0, 0)),
            pl.BlockSpec((width, tile), lambda i: (0, i)),
            pl.BlockSpec((1, tile), lambda i: (0, i)),
        ],
        out_specs=(spec, spec),
        scratch_shapes=[pltpu.VMEM((seq, tile), f32)],
        compiler_params=params(),
        cost_estimate=pl.CostEstimate(
            flops=2 * seq * width * hidden + 60 * seq * hidden,
            bytes_accessed=4 * seq * hidden + 2 * width * hidden,
            transcendentals=0,
        ),
        name="gelu_forward",
    )(h, w, b)


def weight_grad_body(s, x_own, x_sib, y_own, y_sib, *refs, outs, many, rows):
    targets, buf = refs[-1 - outs : -1], refs[-1]
    acc = dot_tn(x_own[...], y_own[...]) + dot_tn(x_sib[...], y_sib[...])
    buf[...] = acc.astype(bf16)
    per = many // outs
    for q in range(many):
        here = pl.ds(pl.multiple_of(s[q] * rows, rows), rows)
        for c in range(targets[0].shape[1]):
            targets[q // per][q % per, c] = buf[here, c * BS : (c + 1) * BS]


def weight_grad(net, group, table, x_own, x_sib, y_own, y_sib, held, first_block, wide):
    seq = x_own.shape[0]
    many, rows, halves = net.pieces, net.rows, net.n_mp
    at_core = 4 * many
    if wide:
        steps = x_own.shape[1] // BS
        y_width = y_own.shape[1] // halves
        x_spec = pl.BlockSpec((seq, BS), lambda i, s: (0, i))
        y_spec = pl.BlockSpec((seq, y_width), lambda i, s: (0, s[at_core]))
    else:
        steps = x_own.shape[1] // halves // BS
        y_width = y_own.shape[1]
        x_spec = pl.BlockSpec((seq, BS), lambda i, s: (0, s[at_core] * steps + i))
        y_spec = pl.BlockSpec((seq, y_width), lambda i, s: (0, 0))
    nb = y_width // BS
    at = first_block // nb
    total = group_blocks(group, halves)
    outs = 2 if many > 1 else 1
    anyspec = pl.BlockSpec(memory_space=pl.ANY)
    held = held or ()
    return pl.pallas_call(
        functools.partial(weight_grad_body, outs=outs, many=many, rows=rows),
        grid_spec=pltpu.PrefetchScalarGridSpec(
            num_scalar_prefetch=1,
            grid=(steps,),
            in_specs=[x_spec, x_spec, y_spec, y_spec] + [anyspec] * len(held),
            out_specs=(pl.BlockSpec((many // outs, nb, rows, BS), lambda i, s: (0, at + i, 0, 0)),)
            * outs,
            scratch_shapes=[pltpu.VMEM((BS, y_width), bf16)],
        ),
        out_shape=(jax.ShapeDtypeStruct((many // outs, total, rows, BS), bf16),) * outs,
        input_output_aliases={5 + k: k for k in range(len(held))},
        compiler_params=params(),
        cost_estimate=pl.CostEstimate(
            flops=4 * seq * steps * BS * y_width,
            bytes_accessed=4 * seq * (steps * BS + y_width) + 2 * steps * BS * y_width,
            transcendentals=0,
        ),
        name="weight_grad",
    )(table, x_own, x_sib, y_own, y_sib, *held)


def split_low(a):
    hi = a.astype(bf16)
    return hi, (a - hi.astype(f32)).astype(bf16)


def shampoo_body(flag, mine_ref, other_ref, w_ref, ls_ref, rs_ref, lr_ref, rr_ref, og, ol, orr, ow, g_ref):
    size = mine_ref.shape[0] * mine_ref.shape[2]
    g_ref[pl.ds(pl.multiple_of(flag[0] * size, size), size), :] = mine_ref[:, 0].reshape(size, BS)
    g_ref[pl.ds(pl.multiple_of((1 - flag[0]) * size, size), size), :] = other_ref[:, 0].reshape(size, BS)
    g = g_ref[...]
    og[0, 0] = g.astype(f32)
    ol[0, 0] = 0.5 * ls_ref[0, 0] + 0.5 * dot_nt(g, g)
    orr[0, 0] = 0.5 * rs_ref[0, 0] + 0.5 * dot_tn(g, g)
    r_hi, r_lo = split_low(rr_ref[0, 0])
    i_hi, i_lo = split_low(dot_nn(g, r_hi) + dot_nn(g, r_lo))
    l_hi, l_lo = split_low(lr_ref[0, 0])
    d = dot_nn(l_hi, i_hi) + (dot_nn(l_hi, i_lo) + dot_nn(l_lo, i_hi))
    mean = jnp.mean(jnp.mean(d * d, axis=1, keepdims=True), axis=0, keepdims=True)
    ow[0, 0] = w_ref[0, 0] - (D**-0.5) * d / jnp.sqrt(mean + 1e-06)


def shampoo(flag, mine, other, weights, left_stat, right_stat, left_root, right_root):
    n = mine.shape[1]
    spec = pl.BlockSpec((1, 1, BS, BS), lambda i: (0, i, 0, 0))
    g_spec = pl.BlockSpec((mine.shape[0], 1, mine.shape[2], BS), lambda i: (0, i, 0, 0))
    return pl.pallas_call(
        shampoo_body,
        grid=(n,),
        out_shape=(jax.ShapeDtypeStruct((1, n, BS, BS), f32),) * 4,
        in_specs=[pl.BlockSpec(memory_space=pltpu.SMEM), g_spec, g_spec] + [spec] * 5,
        out_specs=(spec,) * 4,
        scratch_shapes=[pltpu.VMEM((BS, BS), bf16)],
        compiler_params=params(),
        cost_estimate=pl.CostEstimate(
            flops=14 * n * BS**3, bytes_accessed=38 * n * BS * BS, transcendentals=0
        ),
        name="shampoo",
    )(flag, mine, other, weights, left_stat, right_stat, left_root, right_root)


def norm_forward(z, gain, shift):
    center = z - jnp.mean(z, axis=1, keepdims=True)
    inv = lax.rsqrt(jnp.mean(center * center, axis=1, keepdims=True) + eps_norm)
    normed = center * inv
    return normed * gain + shift, normed, inv


def norm_backward(grad, normed, inv, gain):
    scaled = grad * gain
    mean_plain = jnp.mean(scaled, axis=1, keepdims=True)
    mean_cross = jnp.mean(scaled * normed, axis=1, keepdims=True)
    back = inv * (scaled - mean_plain - normed * mean_cross)
    return back, jnp.sum(grad * normed, axis=0), jnp.sum(grad, axis=0)


def inverse_of(order):
    many = jnp.arange(order.shape[0], dtype=jnp.int32)
    return jnp.sum(jnp.where(order[:, None] == many[None, :], many[:, None], 0), axis=0)


def route_out(value):
    axes = ("rep", "shard")
    count = lax.axis_size(axes)
    cut = value.reshape(value.shape[0], count, value.shape[1] // count, value.shape[2])
    return lax.all_to_all(cut, axes, split_axis=1, concat_axis=0, tiled=True)


def route_home(pieces, ordering):
    moved = pieces.at[ordering].get(mode="promise_in_bounds")
    back = lax.all_to_all(moved, ("rep", "shard"), split_axis=0, concat_axis=1, tiled=True)
    return back.reshape(back.shape[0], -1, back.shape[3])


def per_device(
    net,
    inputs,
    encoded,
    cotangent,
    lengths,
    seq_slots,
    block_slots,
    weights,
    left_stat,
    right_stat,
    left_root,
    right_root,
    vectors,
    vec_stat,
):
    half_d = inputs.shape[2]
    halves = D // half_d
    core = lax.axis_index("mp")
    data_index = lax.axis_index(("rep", "shard"))
    seq_index = data_index * inputs.shape[0] + core
    limit = lax.dynamic_slice_in_dim(lengths, seq_index, 1)
    tables = [net.table(k, core, data_index) for k in range(len(GROUPS))]
    is_first = core == 0

    def pick(pair, which):
        return lax.dynamic_index_in_dim(pair, which, axis=0, keepdims=False)

    def joined(low_half, high_half):
        return jnp.concatenate(
            [
                jnp.where(is_first, low_half, high_half),
                jnp.where(is_first, high_half, low_half),
            ],
            axis=1,
        )

    def whole(value):
        other = net.swap_core(value)
        own = joined(pick(value, core), pick(other, core))
        sib = joined(pick(value, 1 - core), pick(other, 1 - core))
        return own, sib

    def halved(full):
        mine = lax.dynamic_slice_in_dim(full, core * half_d, half_d, axis=1)
        away = lax.dynamic_slice_in_dim(full, (1 - core) * half_d, half_d, axis=1)
        got = net.swap_core(away)
        return jnp.stack([jnp.where(is_first, mine, got), jnp.where(is_first, got, mine)])

    x, x_sib = whole(inputs)
    e, e_sib = whole(encoded)

    pieces = first_pieces(net, weights, inverse_of(block_slots))
    flows, base = [], 0
    for k in range(len(GROUPS)):
        size = group_blocks(k, halves)
        flows.append(Flow(gather_rounds(net, k, pieces[base : base + size])))
        base += size
    attn, cross, up, down = flows

    def placed(k):
        return place(net, k, tables[k], *flows[k].finish())

    step((), attn)
    step((), attn, cross)
    step((), attn, cross)
    step((), attn, cross)
    step((), attn, up)
    w_sq, w_sk, w_sv = step(placed(0), cross, up)

    vec_low = vectors.astype(bf16)
    vec_mine = lax.all_to_all(
        jnp.broadcast_to(vec_low, (net.n_shard, vec_low.shape[1])),
        "shard",
        split_axis=0,
        concat_axis=0,
        tiled=True,
    ).reshape(1, -1)
    vec_other = net.swap_core(vec_mine)
    vec_both = jnp.concatenate(
        [jnp.where(is_first, vec_mine, vec_other), jnp.where(is_first, vec_other, vec_mine)]
    ).astype(f32)
    vecs = [vec_both[:, i * half_d : (i + 1) * half_d].reshape(1, D) for i in range(13)]
    vecs.append(vec_both[:, 13 * half_d :].reshape(1, FF))
    b_sq, b_sv, b_so, g_one, b_one, b_cq, b_cv, b_co, g_two, b_two, b_fo, g_three, b_three, b_fi = vecs

    q_s = (dot_nn(x, w_sq) + b_sq).astype(bf16)
    k_s = dot_nn(x, w_sk).astype(bf16)
    v_s = (dot_nn(x, w_sv) + b_sv).astype(bf16)
    cot_in, q_s, k_s, v_s = step((cotangent, q_s, k_s, v_s), up, down)
    cot_pieces = route_out(cot_in)
    o_s, lse_s = attend_forward(limit, q_s, k_s, v_s, True)
    o_s, lse_s = step((o_s, lse_s), cross, up, down)
    w_so, w_cq, w_ck, w_cv, w_co = placed(1)
    z_one = x.astype(f32) + dot_nn(o_s, w_so) + b_so
    h_one, n_one, r_one = norm_forward(z_one, g_one, b_one)
    h_one_low = h_one.astype(bf16)
    q_c = (dot_nn(h_one_low, w_cq) + b_cq).astype(bf16)
    k_c = dot_nn(e, w_ck).astype(bf16)
    v_c = (dot_nn(e, w_cv) + b_cv).astype(bf16)
    cot_pieces, q_c, k_c, v_c = step((cot_pieces, q_c, k_c, v_c), down)
    cot_home = route_home(cot_pieces, seq_slots)
    o_c, lse_c = attend_forward(limit, q_c, k_c, v_c, False)
    z_two = h_one + dot_nn(o_c, w_co) + b_co
    h_two, n_two, r_two = norm_forward(z_two, g_two, b_two)
    h_two, h_two_low = step((h_two, h_two.astype(bf16)), up, down)
    (w_fi,) = placed(2)
    act, slope = gelu_forward(h_two_low, w_fi, b_fi)
    act_sib = net.swap_core(act)
    act, slope = step((act, slope), down)
    (w_fo,) = placed(3)
    z_three = h_two + dot_nn(act, w_fo) + b_fo
    h_three, n_three, r_three = norm_forward(z_three, g_three, b_three)
    live = (jnp.arange(x.shape[0]) < limit).astype(f32)[:, None]
    source = inverse_of(seq_slots)
    finished = halved((h_three * live).astype(bf16))

    def gradient(k, *operands):
        held, base = None, 0
        for (name, wide), ops in zip(GROUPS[k], operands):
            held = weight_grad(net, k, tables[k], *ops, held, base, wide)
            base += blocks_of(name, halves)
        return Flow(reduce_rounds(net, k, held))

    cot, _ = whole(cot_home)
    grad_y = cot.astype(f32) * live
    d_three, dg_three, db_three = norm_backward(grad_y, n_three, r_three, g_three)
    a_three = d_three.astype(bf16)
    d_hidden = (dot_nt(a_three, w_fo) * slope.astype(f32)).astype(bf16)
    d_hidden_sib = net.swap_core(d_hidden)
    down = gradient(3, (act, act_sib, a_three, net.swap_core(a_three)))
    finished, d_hidden, d_hidden_sib = step((finished, d_hidden, d_hidden_sib), down)
    out_pieces = route_out(finished)
    up = gradient(2, (h_two_low, net.swap_core(h_two_low), d_hidden, d_hidden_sib))
    (d_hidden,) = step((d_hidden,), up)
    d_h_two = d_three + dot_nt(d_hidden, w_fi)
    d_two, dg_two, db_two = norm_backward(d_h_two, n_two, r_two, g_two)
    a_two = d_two.astype(bf16)
    d_oc = dot_nt(a_two, w_co).astype(bf16)
    out_pieces, d_oc = step((out_pieces, d_oc), down)
    outputs = route_home(out_pieces, source)
    dq_c, dk_c, dv_c = attend_backward(limit, q_c, k_c, v_c, o_c, d_oc, lse_c, False)
    dq_c_sib, dk_c_sib, dv_c_sib = [net.swap_core(v) for v in (dq_c, dk_c, dv_c)]
    dq_c, dk_c, dv_c = step((dq_c, dk_c, dv_c), up)
    d_h_one = d_two + dot_nt(dq_c, w_cq)
    d_one, dg_one, db_one = norm_backward(d_h_one, n_one, r_one, g_one)
    a_one = d_one.astype(bf16)
    a_one_sib = net.swap_core(a_one)
    d_os = dot_nt(a_one, w_so).astype(bf16)
    a_one, a_one_sib, d_os = step((a_one, a_one_sib, d_os), down)
    cross = gradient(
        1,
        (o_s, net.swap_core(o_s), a_one, a_one_sib),
        (h_one_low, net.swap_core(h_one_low), dq_c, dq_c_sib),
        (e, e_sib, dk_c, dk_c_sib),
        (e, e_sib, dv_c, dv_c_sib),
        (o_c, net.swap_core(o_c), a_two, net.swap_core(a_two)),
    )
    (d_os,) = step((d_os,), cross, up, down)
    dq_s, dk_s, dv_s = attend_backward(limit, q_s, k_s, v_s, o_s, d_os, lse_s, True)
    sibs = [net.swap_core(v) for v in (dq_s, dk_s, dv_s)]
    outputs, dq_s, dk_s, dv_s = step((outputs, dq_s, dk_s, dv_s), up, down)
    state_back = dot_nt(dk_c, w_ck) + dot_nt(dv_c, w_cv)
    attn = gradient(0, *[(x, x_sib, v, w) for v, w in zip((dq_s, dk_s, dv_s), sibs)])
    dq_s, dk_s, dv_s = step((dq_s, dk_s, dv_s), attn, cross, up)
    back = d_one + dot_nt(dq_s, w_sq) + dot_nt(dk_s, w_sk) + dot_nt(dv_s, w_sv)
    (back,) = step((back,), attn, cross)
    input_grad = halved(back.astype(bf16))
    encoded_grad = halved(state_back.astype(bf16))
    step((), attn, cross)
    step((), attn, cross)
    natural = [f.finish() for f in (attn, cross, up, down)]
    mine, other, flag = last_pieces(net, jnp.concatenate(natural), block_slots)

    sums = (
        jnp.sum(dq_s.astype(f32), axis=0),
        jnp.sum(dv_s.astype(f32), axis=0),
        jnp.sum(d_one, axis=0),
        dg_one,
        db_one,
        jnp.sum(dq_c.astype(f32), axis=0),
        jnp.sum(dv_c.astype(f32), axis=0),
        jnp.sum(d_two, axis=0),
        dg_two,
        db_two,
        jnp.sum(d_three, axis=0),
        dg_three,
        db_three,
        jnp.sum(d_hidden.astype(f32), axis=0),
    )
    vec_pair = jnp.concatenate([s.reshape(halves, -1) for s in sums], axis=1)
    vec_sum = pick(vec_pair, core) + net.swap_core(pick(vec_pair, 1 - core))
    vec_parts = lax.all_to_all(
        vec_sum.reshape(net.n_shard, -1), "shard", split_axis=0, concat_axis=0, tiled=True
    )
    vec_owned = jnp.sum(vec_parts, axis=0, keepdims=True)
    vec_owned = vec_owned + net.swap_rep(vec_owned)

    block_grad, left_new, right_new, weights_new = shampoo(
        flag, mine, other, weights, left_stat, right_stat, left_root, right_root
    )
    vec_stat_new = 0.5 * vec_stat + 0.5 * vec_owned * vec_owned
    vectors_new = vectors - 0.1 * vec_owned * lax.rsqrt(vec_stat_new)
    return (
        outputs,
        input_grad,
        encoded_grad,
        block_grad,
        left_new,
        right_new,
        weights_new,
        vec_owned,
        vec_stat_new,
        vectors_new,
    )


def solution(mesh):
    net = Net(mesh.shape["rep"], mesh.shape["shard"], mesh.shape["mp"])
    rows = P(("rep", "shard"), None, "mp")
    blocks = P("mp", "shard", None, None)
    vector = P("mp", "shard")
    in_specs = (rows, rows, rows, P(), P(), P()) + (blocks,) * 5 + (vector, vector)
    out_specs = (rows, rows, rows) + (blocks,) * 4 + (vector,) * 3
    return jax.shard_map(
        functools.partial(per_device, net),
        mesh=mesh,
        in_specs=in_specs,
        out_specs=out_specs,
        check_vma=False,
    )
```

time: 791 us -> 749 us (0.947)
  local copies, waits for them, and re-layouts: 97.7 us -> 39.6 us
  Pallas kernels: 248 us -> 208 us
  waiting for transfers between devices: 195 us -> 230 us
  starting transfers between devices: 82.8 us -> 116 us
  matrix products: 90 us -> 65.3 us
    unnamed x223 -> x270, local copies, waits for them, and re-layouts: 76.7 us -> 17.5 us
    ppermute x7 -> x2, waiting for transfers between devices: 69.4 us -> 18.7 us  [swap_rep(): return lax.ppermute(value, 'rep', [(i, i ^ 1) for i in range(self.n_rep)])]
    all_to_all x0 -> x2, waiting for transfers between devices: none -> 45.6 us  [the longest x1 25.6 us: first_pieces(): lax.all_to_all(cut, 'shard', split_axis=0, concat_axis=0, tiled=True)]
    pallas_call x17 -> x14, Pallas kernels: 153 us -> 113 us  [the longest x10 62 us: weight_grad(): pl.pallas_call(functools.partial(weight_grad_body, outs=outs, many=many,...]
    ppermute x12 -> x32, waiting for transfers between devices: 109 us -> 148 us  [swap_data(): return lax.ppermute(value, ('rep', 'shard', 'mp'), pairs)]
    ppermute x32 -> x31, starting transfers between devices: 11.1 us -> 35.5 us  [swap_core(): return lax.ppermute(value, 'mp', [(i, i ^ 1) for i in range(self.n_mp)])]
    ppermute x12 -> x32, starting transfers between devices: 23.8 us -> 36.8 us  [swap_data(): return lax.ppermute(value, ('rep', 'shard', 'mp'), pairs)]
    dot_general x10, matrix products: 51.8 us -> 39 us  [dot_nt(): return lax.dot_general(a, b, NT, preferred_element_type=f32)]
  transfers between devices with their start and end apart: 57 -> 73, of which waited for: 15 -> 25; matrix products, arithmetic and copies ran while one was open for 21% -> 22% of each run, Pallas kernels for 27% -> 25%
where the time goes in v2:
time: 749 us; the launch traced here: 738 us
  waiting for transfers between devices  230 us (31%)
  Pallas kernels  208 us (28%)
  starting transfers between devices  116 us (15%)
  other arithmetic  75.5 us (10%)
  matrix products  65.3 us (9%)
  local copies, waits for them, and re-layouts  39.6 us (5%)
    ppermute x32, waiting for transfers between devices, swap_data(): return lax.ppermute(value, ('rep', 'shard', 'mp'), pairs)  148 us
    pallas_call x10, Pallas kernels, weight_grad(): pl.pallas_call(functools.partial(weight_grad_body, outs=outs, many=many,...  62 us
    pallas_call x4, Pallas kernels, place(): pl.pallas_call(functools.partial(place_body, dests=dests, many=many, half...  51.2 us
    dot_general x10, matrix products, dot_nt(): return lax.dot_general(a, b, NT, preferred_element_type=f32)  39 us
    ppermute x32, starting transfers between devices, swap_data(): return lax.ppermute(value, ('rep', 'shard', 'mp'), pairs)  36.8 us
    ppermute x31, starting transfers between devices, swap_core(): return lax.ppermute(value, 'mp', [(i, i ^ 1) for i in range(self.n_mp)])  35.5 us
    pallas_call x2, Pallas kernels, attend_forward(): pl.pallas_call(functools.partial(attend_forward_body, causal=causal, rows...  28.8 us
    pallas_call x2, Pallas kernels, attend_backward(): pl.pallas_call(functools.partial(attend_backward_body, causal=causal, row...  26.8 us
  transfers between devices with their start and end apart: 73, of which 25 were waited for; matrix products, arithmetic and copies ran while one was open for 22% of the time, Pallas kernels for 25%

profile of v2, /device:TPU:0, one launch (start us, length us, event | category | flops | bytes accessed | tf_op | source)
XLA Modules:
  0.0 738.0 jit_solution(3732675817998710530)
XLA Ops:
  4.3 7.3 all-to-all-start
  11.7 25.6 %all-to-all-done = bf16[128,16,256]{2,1,0:T(8,128)(2,1)S(1)} async-done(((bf16[128,16,256]{2,1,0:T(8,128)(2,1)}), bf16[128,16,256]{2,1,0:T(8,128)(2,1)S(1)}, u32[]{:S(2)}, u32[]{:S(2)}) %all-to-all-start) | async-done | bytes 1048608 | tf_op jit(solution)/shard_map/all_to_all | solution.py:252
  38.1 10.4 %collective-permute-done.1 = bf16[1,24,16,256]{3,2,1,0:T(8,128)(2,1)S(1)} collective-permute-done((bf16[1,24,16,256]{3,2,1,0:T(8,128)(2,1)S(1)}, bf16[1,24,16,256]{3,2,1,0:T(8,128)(2,1)S(1)}, u32[]{:S(2)}, u32[]{:S(2)}) %collective-permute-start.1) | collective-permute-done | bytes 196640 | tf_op jit(solution)/shard_map/ppermute | solution.py:100
  50.2 16.1 %collective-permute-done.3 = bf16[1,40,16,256]{3,2,1,0:T(8,128)(2,1)S(1)} collective-permute-done((bf16[1,40,16,256]{3,2,1,0:T(8,128)(2,1)S(1)}, bf16[1,40,16,256]{3,2,1,0:T(8,128)(2,1)S(1)}, u32[]{:S(2)}, u32[]{:S(2)}) %collective-permute-start.3) | collective-permute-done | bytes 327712 | tf_op jit(solution)/shard_map/ppermute | solution.py:100
  68.1 9.1 %collective-permute-done.5 = bf16[2,40,16,256]{3,2,1,0:T(8,128)(2,1)S(1)} collective-permute-done((bf16[2,40,16,256]{3,2,1,0:T(8,128)(2,1)S(1)}, bf16[2,40,16,256]{3,2,1,0:T(8,128)(2,1)S(1)}, u32[]{:S(2)}, u32[]{:S(2)}) %collective-permute-start.5) | collective-permute-done | bytes 655392 | tf_op jit(solution)/shard_map/ppermute | solution.py:100
  80.4 7.7 %collective-permute-start.7 = (bf16[8,24,16,256]{3,2,1,0:T(8,128)(2,1)S(1)}, bf16[8,24,16,256]{3,2,1,0:T(8,128)(2,1)}, u32[]{:S(2)}, u32[]{:S(2)}) collective-permute-start(bf16[8,24,16,256]{3,2,1,0:T(8,128)(2,1)S(1)} %pad_maximum_fusion.3.refs_0_), channel_id=1, source_target_pairs={{0,1},{1,0},{2,3},{3,2},{4,5},{5,4},{6,7},{7,6},{8,9},{9,8},{10,11... | collective-permute-start | bytes 4718600 | tf_op jit(solution)/shard_map/ppermute | solution.py:89
  90.1 3.3 all-to-all-start.1
  94.3 5.8 all-to-all-done.1
  106.1 3.3 collective-permute-done.8.refs_3_
  109.4 12.2 %place.4 = (bf16[4,256,1024]{2,1,0:T(8,128)(2,1)}, bf16[4,256,1024]{2,1,0:T(8,128)(2,1)}, bf16[4,256,1024]{2,1,0:T(8,128)(2,1)}) custom-call(s32[65]{0:T(128)} %pad_add_fusion.s, bf16[8,24,16,256]{3,2,1,0:T(8,128)(2,1)} %copy-done.14, bf16[8,24,16,256]{3,2,1,0:T(8,128)(2,1)} %collective-permute-done.6.refs_1_, ...), custom_call_target="tpu_custom_call" | custom-call | bytes 12582912 | tf_op jit(solution)/shard_map/place/pallas_call | solution.py:210
  121.5 18.6 %collective-permute-done.9 = bf16[4,40,16,256]{3,2,1,0:T(8,128)(2,1)} collective-permute-done((bf16[4,40,16,256]{3,2,1,0:T(8,128)(2,1)}, bf16[4,40,16,256]{3,2,1,0:T(8,128)(2,1)}, u32[]{:S(2)}, u32[]{:S(2)}) %collective-permute-start.9) | collective-permute-done | bytes 1310752 | tf_op jit(solution)/shard_map/ppermute | solution.py:100
  161.1 19.9 %attend_forward.2 = (bf16[512,1024]{1,0:T(8,128)(2,1)}, f32[512,128]{1,0:T(8,128)}) custom-call(s32[1]{0:T(128)} %dynamic_slice.78.lim, bf16[512,1024]{1,0:T(8,128)(2,1)} %add_convert_fusion.8.q_ref, bf16[512,1024]{1,0:T(8,128)(2,1)} %convolution_convert_fusion.2.k_ref, bf16[512,1024]{1,0:T(8,128)(2,1)} %add_convert_fusion.7.v_ref), custom_call_target="tpu_custom_call" | custom-call | flops 1073741824 | bytes 4194304 | tf_op jit(solution)/shard_map/attend_forward/pallas_call | solution.py:332
  182.7 8.0 %collective-permute-done.15 = bf16[4,32,16,256]{3,2,1,0:T(8,128)(2,1)} collective-permute-done((bf16[4,32,16,256]{3,2,1,0:T(8,128)(2,1)}, bf16[4,32,16,256]{3,2,1,0:T(8,128)(2,1)}, u32[]{:S(2)}, u32[]{:S(2)}) %collective-permute-start.15) | collective-permute-done | bytes 1048608 | tf_op jit(solution)/shard_map/ppermute | solution.py:100
  200.3 5.7 all-to-all-start.2
  206.0 2.8 pad_maximum_fusion.1.refs_0_
  212.5 13.5 %place.5 = (bf16[4,256,1024]{2,1,0:T(8,128)(2,1)}, bf16[4,256,1024]{2,1,0:T(8,128)(2,1)}, bf16[4,256,1024]{2,1,0:T(8,128)(2,1)}, bf16[4,256,1024]{2,1,0:T(8,128)(2,1)}, bf16[4,256,1024]{2,1,0:T(8,128)(2,1)}) custom-call(s32[65]{0:T(128)} %pad_add_fusion.1.s, bf16[8,40,16,256]{3,2,1,0:T(8,128)(2,1)} %copy-done.6, ...), custom_call_target="tpu_custom_call" | custom-call | bytes 20971520 | tf_op jit(solution)/shard_map/place/pallas_call | solution.py:210
  226.0 3.4 fusion.25
  237.6 15.2 %collective-permute-done.19 = bf16[2,32,16,256]{3,2,1,0:T(8,128)(2,1)} collective-permute-done((bf16[2,32,16,256]{3,2,1,0:T(8,128)(2,1)}, bf16[2,32,16,256]{3,2,1,0:T(8,128)(2,1)}, u32[]{:S(2)}, u32[]{:S(2)}) %collective-permute-start.19) | collective-permute-done | bytes 524320 | tf_op jit(solution)/shard_map/ppermute | solution.py:100
  256.5 8.9 %attend_forward.3 = (bf16[512,1024]{1,0:T(8,128)(2,1)}, f32[512,128]{1,0:T(8,128)}) custom-call(s32[1]{0:T(128)} %dynamic_slice.78.lim, bf16[512,1024]{1,0:T(8,128)(2,1)} %add_convert_fusion.6.q_ref, bf16[128,1024]{1,0:T(8,128)(2,1)} %convolution_convert_fusion.3.k_ref, bf16[128,1024]{1,0:T(8,128)(2,1)} %fusion.4.v_ref), custom_call_target="tpu_custom_call" | custom-call | flops 268435456 | bytes 4194304 | tf_op jit(solution)/shard_map/attend_forward/pallas_call | solution.py:332
  265.5 3.4 fusion.26
  271.8 2.9 pad_maximum_fusion.2.refs_0_
  278.4 6.3 all-to-all-start.3
  286.1 12.6 %place.6 = bf16[4,256,4096]{2,1,0:T(8,128)(2,1)} custom-call(s32[65]{0:T(128)} %pad_add_fusion.2.s, bf16[8,32,16,256]{3,2,1,0:T(8,128)(2,1)} %pad_maximum_fusion.1.refs_0_, bf16[8,32,16,256]{3,2,1,0:T(8,128)(2,1)} %collective-permute-done.20.refs_1_, bf16[8,32,16,256]{3,2,1,0:T(8,128)(2,1)} %collective-permute-done.21.refs_2_, ...), custom_call_target="tpu_custom_call" | custom-call | bytes 16777216 | tf_op jit(solution)/shard_map/place/pallas_call | solution.py:210
  298.8 19.1 %gelu_forward.1 = (bf16[512,4096]{1,0:T(8,128)(2,1)}, bf16[512,4096]{1,0:T(8,128)(2,1)}) custom-call(bf16[512,1024]{1,0:T(8,128)(2,1)} %get-tuple-element.227.h_ref.x_own, bf16[1024,4096]{1,0:T(8,128)(2,1)} %bitcast.196, f32[1,4096]{1,0:T(1,128)} %bitcast.248), custom_call_target="tpu_custom_call" | custom-call | flops 4420796416 | bytes 16777216 | tf_op jit(solution)/shard_map/gelu_forward/pallas_call | solution.py:469
  325.5 12.9 %place.7 = bf16[16,256,1024]{2,1,0:T(8,128)(2,1)} custom-call(s32[65]{0:T(128)} %pad_add_fusion.3.s, bf16[8,32,16,256]{3,2,1,0:T(8,128)(2,1)} %pad_maximum_fusion.2.refs_0_, bf16[8,32,16,256]{3,2,1,0:T(8,128)(2,1)} %collective-permute-done.24.refs_1_, bf16[8,32,16,256]{3,2,1,0:T(8,128)(2,1)} %collective-permute-done.25.refs_2_, ...), custom_call_target="tpu_custom_call" | custom-call | bytes 16777216 | tf_op jit(solution)/shard_map/place/pallas_call | solution.py:210
  338.4 8.3 %fusion.27 = f32[512,1024]{1,0:T(8,128)S(1)} fusion(bf16[512,4096]{1,0:T(8,128)(2,1)} %get-tuple-element.233.x_own, bf16[4096,1024]{1,0:T(8,128)(2,1)} %bitcast.198), kind=kOutput, calls=%fused_computation.216 | convolution fusion | flops 4294967296 | bytes 14680064 | tf_op jit(solution)/shard_map/dot_general | solution.py:43
  353.0 8.1 %multiply_convert_fusion.y_own = bf16[512,4096]{1,0:T(8,128)(2,1)} fusion(bf16[512,4096]{1,0:T(8,128)(2,1)} %get-tuple-element.237, bf16[512,1024]{1,0:T(8,128)(2,1)S(1)} %convert_element_type.366.y_own, bf16[4096,1024]{1,0:T(8,128)(2,1)S(1)} %bitcast.201), kind=kOutput, calls=%fused_computation.5 | convolution fusion | flops 4301258752 | bytes 17825792 | tf_op jit(solution)/shard_map/dot_general | solution.py:47
  366.0 4.8 collective-permute-done.27
  372.3 10.9 %weight_grad.10 = (bf16[8,32,16,256]{3,2,1,0:T(8,128)(2,1)}, bf16[8,32,16,256]{3,2,1,0:T(8,128)(2,1)}) custom-call(s32[65]{0:T(128)} %pad_add_fusion.3.s, bf16[512,4096]{1,0:T(8,128)(2,1)} %get-tuple-element.233.x_own, bf16[512,4096]{1,0:T(8,128)(2,1)} %collective-permute-done.30.x_sib, bf16[512,1024]{1,0:T(8,128)(2,1)} %copy-done.59, ...), custom_call_target="tpu_custom_call" | custom-call | flops 4294967296 | bytes 10485760 | tf_op jit(solution)/shard_map/weight_grad/pallas_call | solution.py:521
  384.4 7.3 all-to-all-start.4
  391.7 9.6 %weight_grad.11 = (bf16[8,32,16,256]{3,2,1,0:T(8,128)(2,1)}, bf16[8,32,16,256]{3,2,1,0:T(8,128)(2,1)}) custom-call(s32[65]{0:T(128)} %pad_add_fusion.2.s, bf16[512,1024]{1,0:T(8,128)(2,1)} %get-tuple-element.227.h_ref.x_own, bf16[512,1024]{1,0:T(8,128)(2,1)} %collective-permute-done.32.x_sib, bf16[512,4096]{1,0:T(8,128)(2,1)} %multiply_convert_fusion.y_own, ...), custom_call_target="tpu_custom_call" | custom-call | flops 4294967296 | bytes 10485760 | tf_op jit(solution)/shard_map/weight_grad/pallas_call | solution.py:521
  404.7 11.5 %multiply_reduce_fusion.1 = (f32[1024]{0:T(1024)}, f32[512]{0:T(512)S(1)}, f32[512]{0:T(512)S(1)}, f32[1024]{0:T(1024)}, f32[512,1024]{1,0:T(8,128)S(1)}) fusion(f32[512,1024]{1,0:T(8,128)} %copy-done.3, f32[512]{0:T(512)S(1)} %copy-done.82, f32[512]{0:T(512)S(1)} %broadcast_multiply_fusion.7, f32[1024]{0:T(1024)S(1)} %bitcast.241, ...), kind=kOutput, calls=%fused_computation.12 | convolution fusion | flops 4300207104 | bytes 18894848 | tf_op jit(solution)/shard_map/dot_general | solution.py:47
  422.1 10.5 %collective-permute-done.33 = bf16[8,32,16,256]{3,2,1,0:T(8,128)(2,1)} collective-permute-done((bf16[8,32,16,256]{3,2,1,0:T(8,128)(2,1)}, bf16[8,32,16,256]{3,2,1,0:T(8,128)(2,1)}, u32[]{:S(2)}, u32[]{:S(2)}) %collective-permute-start.33) | collective-permute-done | bytes 2097184 | tf_op jit(solution)/shard_map/ppermute | solution.py:100
  432.6 10.7 %attend_backward.2 = (bf16[512,1024]{1,0:T(8,128)(2,1)}, bf16[128,1024]{1,0:T(8,128)(2,1)}, bf16[128,1024]{1,0:T(8,128)(2,1)}) custom-call(s32[1]{0:T(128)} %dynamic_slice.78.lim, bf16[512,1024]{1,0:T(8,128)(2,1)} %add_convert_fusion.6.q_ref, bf16[128,1024]{1,0:T(8,128)(2,1)} %convolution_convert_fusion.3.k_ref, bf16[128,1024]{1,0:T(8,128)(2,1)} %fusion.4.v_ref, ...), custom_call_target="tpu_custom_call" | custom-call | flops 671088640 | bytes 8388608 | tf_op jit(solution)/shard_map/attend_backward/pallas_call | solution.py:417
  443.3 5.0 multiply_reduce_fusion.2
  450.6 12.9 %collective-permute-start.35 = (bf16[512,1024]{1,0:T(8,128)(2,1)S(1)}, bf16[512,1024]{1,0:T(8,128)(2,1)S(1)}, u32[]{:S(2)}, u32[]{:S(2)}) collective-permute-start(bf16[512,1024]{1,0:T(8,128)(2,1)S(1)} %convert_element_type.371.y_own), channel_id=1, source_target_pairs={{0,1},{1,0},{2,3},{3,2},{4,5},{5,4},{6,7},{7,6},{8,9},{9,8},{10,11... | collective-permute-start | bytes 3145736 | tf_op jit(solution)/shard_map/ppermute | solution.py:89
  465.9 2.6 collective-permute-start.41
  468.7 3.6 add_convert_fusion.2
  472.9 7.7 %collective-permute-done.36 = bf16[4,32,16,256]{3,2,1,0:T(8,128)(2,1)S(1)} collective-permute-done((bf16[4,32,16,256]{3,2,1,0:T(8,128)(2,1)S(1)}, bf16[4,32,16,256]{3,2,1,0:T(8,128)(2,1)S(1)}, u32[]{:S(2)}, u32[]{:S(2)}) %collective-permute-start.36) | collective-permute-done | bytes 1048608 | tf_op jit(solution)/shard_map/ppermute | solution.py:100
  488.5 2.8 gather_fusion.2
  491.3 4.4 all-to-all-start.5
  495.7 4.8 weight_grad.12
  500.5 5.5 weight_grad.13
  506.0 4.7 weight_grad.14
  510.7 4.7 weight_grad.15
  515.4 4.9 weight_grad.16
  522.6 3.0 pad_maximum_fusion.5
  532.9 16.2 %attend_backward.3 = (bf16[512,1024]{1,0:T(8,128)(2,1)}, bf16[512,1024]{1,0:T(8,128)(2,1)}, bf16[512,1024]{1,0:T(8,128)(2,1)}) custom-call(s32[1]{0:T(128)} %dynamic_slice.78.lim, bf16[512,1024]{1,0:T(8,128)(2,1)} %add_convert_fusion.8.q_ref, bf16[512,1024]{1,0:T(8,128)(2,1)} %convolution_convert_fusion.2.k_ref, bf16[512,1024]{1,0:T(8,128)(2,1)} %add_convert_fusion.7.v_ref, ...), custom_call_target="tpu_custom_call" | custom-call | flops 2684354560 | bytes 8388608 | tf_op jit(solution)/shard_map/attend_backward/pallas_call | solution.py:417
  549.8 3.3 convert_reduce_fusion
  557.8 5.5 weight_grad.17
  563.3 5.5 weight_grad.18
  568.8 5.9 weight_grad.19
  576.1 4.0 add_convert_fusion
  581.3 3.0 fusion.28
  588.9 22.7 %collective-permute-done.54 = bf16[4,40,16,256]{3,2,1,0:T(8,128)(2,1)} collective-permute-done((bf16[4,40,16,256]{3,2,1,0:T(8,128)(2,1)}, bf16[4,40,16,256]{3,2,1,0:T(8,128)(2,1)}, u32[]{:S(2)}, u32[]{:S(2)}) %collective-permute-start.54) | collective-permute-done | bytes 1310752 | tf_op jit(solution)/shard_map/ppermute | solution.py:100
  616.5 9.8 %collective-permute-done.58 = bf16[2,40,16,256]{3,2,1,0:T(8,128)(2,1)S(1)} collective-permute-done((bf16[2,40,16,256]{3,2,1,0:T(8,128)(2,1)S(1)}, bf16[2,40,16,256]{3,2,1,0:T(8,128)(2,1)S(1)}, u32[]{:S(2)}, u32[]{:S(2)}) %collective-permute-start.58) | collective-permute-done | bytes 655392 | tf_op jit(solution)/shard_map/ppermute | solution.py:100
  630.1 4.1 collective-permute-start.63
  636.0 3.3 all-to-all-start.7
  639.3 6.1 collective-permute-done.60
  647.6 11.7 %collective-permute-done.61 = bf16[1,24,16,256]{3,2,1,0:T(8,128)(2,1)S(1)} collective-permute-done((bf16[1,24,16,256]{3,2,1,0:T(8,128)(2,1)S(1)}, bf16[1,24,16,256]{3,2,1,0:T(8,128)(2,1)S(1)}, u32[]{:S(2)}, u32[]{:S(2)}) %collective-permute-start.61) | collective-permute-done | bytes 196640 | tf_op jit(solution)/shard_map/ppermute | solution.py:100
  662.1 3.7 all-to-all-start.6
  672.1 19.9 %all-to-all-done.6 = bf16[128,16,256]{2,1,0:T(8,128)(2,1)S(1)} async-done(((bf16[128,16,256]{2,1,0:T(8,128)(2,1)}), bf16[128,16,256]{2,1,0:T(8,128)(2,1)S(1)}, u32[]{:S(2)}, u32[]{:S(2)}) %all-to-all-start.6) | async-done | bytes 1048608 | tf_op jit(solution)/shard_map/all_to_all | solution.py:286
  697.7 18.6 %collective-permute-done.62.other_ref = bf16[8,16,16,256]{3,2,1,0:T(8,128)(2,1)S(1)} collective-permute-done((bf16[8,16,16,256]{3,2,1,0:T(8,128)(2,1)S(1)}, bf16[8,16,16,256]{3,2,1,0:T(8,128)(2,1)S(1)}, u32[]{:S(2)}, u32[]{:S(2)}) %collective-permute-start.62) | collective-permute-done | bytes 1048608 | tf_op jit(solution)/shard_map/ppermute | solution.py:92
  717.3 20.5 %shampoo.1 = (f32[1,16,256,256]{3,2,1,0:T(8,128)}, f32[1,16,256,256]{3,2,1,0:T(8,128)}, f32[1,16,256,256]{3,2,1,0:T(8,128)}, f32[1,16,256,256]{3,2,1,0:T(8,128)}) custom-call(s32[1]{0:T(128)} %bitcast.70.flag, bf16[8,16,16,256]{3,2,1,0:T(8,128)(2,1)} %bitcast.212, bf16[8,16,16,256]{3,2,1,0:T(8,128)(2,1)} %copy-done.60, f32[1,16,256,256]{3,2,1,0:T(8,128)} %w_ref.1, ...), custom_call_target="tpu_custom_call" | custom-call | flops 3758096384 | bytes 39845888 | tf_op jit(solution)/shard_map/shampoo/pallas_call | solution.py:568
  (545 shorter events, 169.1 us)
Async XLA Ops:
  4.3 33.0 %all-to-all-start = ((bf16[128,16,256]{2,1,0:T(8,128)(2,1)}), bf16[128,16,256]{2,1,0:T(8,128)(2,1)S(1)}, u32[]{:S(2)}, u32[]{:S(2)}) async-start(bf16[128,16,256]{2,1,0:T(8,128)(2,1)} %bitcast.8), calls=%async_computation | async-start | bytes 2097152 | tf_op jit(solution)/shard_map/all_to_all | solution.py:252
  38.0 10.5 %collective-permute-start.1 = (bf16[1,24,16,256]{3,2,1,0:T(8,128)(2,1)S(1)}, bf16[1,24,16,256]{3,2,1,0:T(8,128)(2,1)S(1)}, u32[]{:S(2)}, u32[]{:S(2)}) collective-permute-start(bf16[1,24,16,256]{3,2,1,0:T(8,128)(2,1)S(1)} %bitcast.226), channel_id=1, source_target_pairs={{0,8},{1,9},{2,10},{3,11},{4,12},{5,13},{6,14},{7,15},{8,0},{9,1},... | collective-permute-start | bytes 589832 | tf_op jit(solution)/shard_map/ppermute | solution.py:100
  48.6 17.7 %collective-permute-start.2 = (bf16[2,24,16,256]{3,2,1,0:T(8,128)(2,1)S(1)}, bf16[2,24,16,256]{3,2,1,0:T(8,128)(2,1)S(1)}, u32[]{:S(2)}, u32[]{:S(2)}) collective-permute-start(bf16[2,24,16,256]{3,2,1,0:T(8,128)(2,1)S(1)} %pad_maximum_fusion.17), channel_id=1, source_target_pairs={{0,16},{1,5},{2,18},{3,7},{4,20},{5,1},{6,22},{7,3},{8,24},{9,13},... | collective-permute-start | bytes 1179656 | tf_op jit(solution)/shard_map/ppermute | solution.py:100
  50.2 16.1 %collective-permute-start.3 = (bf16[1,40,16,256]{3,2,1,0:T(8,128)(2,1)S(1)}, bf16[1,40,16,256]{3,2,1,0:T(8,128)(2,1)S(1)}, u32[]{:S(2)}, u32[]{:S(2)}) collective-permute-start(bf16[1,40,16,256]{3,2,1,0:T(8,128)(2,1)S(1)} %bitcast.206), channel_id=1, source_target_pairs={{0,8},{1,9},{2,10},{3,11},{4,12},{5,13},{6,14},{7,15},{8,0},{9,1},... | collective-permute-start | bytes 983048 | tf_op jit(solution)/shard_map/ppermute | solution.py:100
  66.4 12.1 %collective-permute-start.4 = (bf16[4,24,16,256]{3,2,1,0:T(8,128)(2,1)S(1)}, bf16[4,24,16,256]{3,2,1,0:T(8,128)(2,1)S(1)}, u32[]{:S(2)}, u32[]{:S(2)}) collective-permute-start(bf16[4,24,16,256]{3,2,1,0:T(8,128)(2,1)S(1)} %pad_maximum_fusion.13), channel_id=1, source_target_pairs={{0,4},{1,3},{2,6},{3,1},{4,0},{5,7},{6,2},{7,5},{8,12},{9,11},{10,... | collective-permute-start | bytes 2359304 | tf_op jit(solution)/shard_map/ppermute | solution.py:100
  66.6 10.7 %collective-permute-start.5 = (bf16[2,40,16,256]{3,2,1,0:T(8,128)(2,1)S(1)}, bf16[2,40,16,256]{3,2,1,0:T(8,128)(2,1)S(1)}, u32[]{:S(2)}, u32[]{:S(2)}) collective-permute-start(bf16[2,40,16,256]{3,2,1,0:T(8,128)(2,1)S(1)} %pad_maximum_fusion.14), channel_id=1, source_target_pairs={{0,16},{1,3},{2,18},{3,1},{4,20},{5,7},{6,22},{7,5},{8,24},{9,11},... | collective-permute-start | bytes 1966088 | tf_op jit(solution)/shard_map/ppermute | solution.py:100
  78.6 25.3 %collective-permute-start.6 = (bf16[8,24,16,256]{3,2,1,0:T(8,128)(2,1)S(1)}, bf16[8,24,16,256]{3,2,1,0:T(8,128)(2,1)}, u32[]{:S(2)}, u32[]{:S(2)}) collective-permute-start(bf16[8,24,16,256]{3,2,1,0:T(8,128)(2,1)S(1)} %pad_maximum_fusion.3.refs_0_), channel_id=1, source_target_pairs={{0,2},{1,17},{2,0},{3,19},{4,6},{5,21},{6,4},{7,23},{8,10},{9,25},... | collective-permute-start | bytes 4718600 | tf_op jit(solution)/shard_map/ppermute | solution.py:100
  80.4 23.5 %collective-permute-start.7 = (bf16[8,24,16,256]{3,2,1,0:T(8,128)(2,1)S(1)}, bf16[8,24,16,256]{3,2,1,0:T(8,128)(2,1)}, u32[]{:S(2)}, u32[]{:S(2)}) collective-permute-start(bf16[8,24,16,256]{3,2,1,0:T(8,128)(2,1)S(1)} %pad_maximum_fusion.3.refs_0_), channel_id=1, source_target_pairs={{0,1},{1,0},{2,3},{3,2},{4,5},{5,4},{6,7},{7,6},{8,9},{9,8},{10,11... | collective-permute-start | bytes 4718600 | tf_op jit(solution)/shard_map/ppermute | solution.py:89
  90.1 10.0 %all-to-all-start.1 = ((bf16[8,2,544]{2,1,0:T(2,128)(2,1)}), bf16[8,2,544]{2,1,0:T(2,128)(2,1)S(1)}, u32[]{:S(2)}, u32[]{:S(2)}) async-start(bf16[8,2,544]{2,1,0:T(2,128)(2,1)} %reshape.519), calls=%async_computation.1 | async-start | bytes 40960 | tf_op jit(solution)/shard_map/all_to_all | solution.py:687
  93.4 51.0 %collective-permute-start = (bf16[2,512,512]{2,1,0:T(8,128)(2,1)}, bf16[2,512,512]{2,1,0:T(8,128)(2,1)}, u32[]{:S(2)}, u32[]{:S(2)}) collective-permute-start(bf16[2,512,512]{2,1,0:T(8,128)(2,1)} %param.25), channel_id=1, source_target_pairs={{0,1},{1,0},{2,3},{3,2},{4,5},{5,4},{6,7},{7,6},{8,9},{9,8},{10,11... | collective-permute-start | bytes 3145736 | tf_op jit(solution)/shard_map/ppermute | solution.py:89
  103.0 37.1 %collective-permute-start.9 = (bf16[4,40,16,256]{3,2,1,0:T(8,128)(2,1)}, bf16[4,40,16,256]{3,2,1,0:T(8,128)(2,1)}, u32[]{:S(2)}, u32[]{:S(2)}) collective-permute-start(bf16[4,40,16,256]{3,2,1,0:T(8,128)(2,1)} %pad_maximum_fusion.4), channel_id=1, source_target_pairs={{0,4},{1,5},{2,6},{3,7},{4,0},{5,1},{6,2},{7,3},{8,12},{9,13},{10,... | collective-permute-start | bytes 3932168 | tf_op jit(solution)/shard_map/ppermute | solution.py:100
  106.0 34.2 %collective-permute-start.10 = (bf16[1,32,16,256]{3,2,1,0:T(8,128)(2,1)S(1)}, bf16[1,32,16,256]{3,2,1,0:T(8,128)(2,1)S(1)}, u32[]{:S(2)}, u32[]{:S(2)}) collective-permute-start(bf16[1,32,16,256]{3,2,1,0:T(8,128)(2,1)S(1)} %bitcast.222), channel_id=1, source_target_pairs={{0,8},{1,9},{2,10},{3,11},{4,12},{5,13},{6,14},{7,15},{8,0},{9,1},... | collective-permute-start | bytes 786440 | tf_op jit(solution)/shard_map/ppermute | solution.py:100
  142.0 48.7 %collective-permute-start.13 = (bf16[8,40,16,256]{3,2,1,0:T(8,128)(2,1)S(1)}, bf16[8,40,16,256]{3,2,1,0:T(8,128)(2,1)}, u32[]{:S(2)}, u32[]{:S(2)}) collective-permute-start(bf16[8,40,16,256]{3,2,1,0:T(8,128)(2,1)S(1)} %pad_maximum_fusion.refs_0_), channel_id=1, source_target_pairs={{0,2},{1,17},{2,0},{3,19},{4,6},{5,21},{6,4},{7,23},{8,10},{9,25},... | collective-permute-start | bytes 7864328 | tf_op jit(solution)/shard_map/ppermute | solution.py:100
  143.8 46.9 %collective-permute-start.14 = (bf16[8,40,16,256]{3,2,1,0:T(8,128)(2,1)S(1)}, bf16[8,40,16,256]{3,2,1,0:T(8,128)(2,1)}, u32[]{:S(2)}, u32[]{:S(2)}) collective-permute-start(bf16[8,40,16,256]{3,2,1,0:T(8,128)(2,1)S(1)} %pad_maximum_fusion.refs_0_), channel_id=1, source_target_pairs={{0,1},{1,0},{2,3},{3,2},{4,5},{5,4},{6,7},{7,6},{8,9},{9,8},{10,11... | collective-permute-start | bytes 7864328 | tf_op jit(solution)/shard_map/ppermute | solution.py:89
  147.0 9.2 %collective-permute-start.12 = (bf16[2,32,16,256]{3,2,1,0:T(8,128)(2,1)S(1)}, bf16[2,32,16,256]{3,2,1,0:T(8,128)(2,1)S(1)}, u32[]{:S(2)}, u32[]{:S(2)}) collective-permute-start(bf16[2,32,16,256]{3,2,1,0:T(8,128)(2,1)S(1)} %pad_maximum_fusion.15), channel_id=1, source_target_pairs={{0,4},{1,3},{2,6},{3,1},{4,0},{5,7},{6,2},{7,5},{8,12},{9,11},{10,... | collective-permute-start | bytes 1572872 | tf_op jit(solution)/shard_map/ppermute | solution.py:100
  157.4 33.3 %collective-permute-start.15 = (bf16[4,32,16,256]{3,2,1,0:T(8,128)(2,1)}, bf16[4,32,16,256]{3,2,1,0:T(8,128)(2,1)}, u32[]{:S(2)}, u32[]{:S(2)}) collective-permute-start(bf16[4,32,16,256]{3,2,1,0:T(8,128)(2,1)} %pad_maximum_fusion.6), channel_id=1, source_target_pairs={{0,2},{1,17},{2,0},{3,19},{4,6},{5,21},{6,4},{7,23},{8,10},{9,25},... | collective-permute-start | bytes 3145736 | tf_op jit(solution)/shard_map/ppermute | solution.py:100
  159.7 23.0 %collective-permute-start.16 = (bf16[1,32,16,256]{3,2,1,0:T(8,128)(2,1)S(1)}, bf16[1,32,16,256]{3,2,1,0:T(8,128)(2,1)S(1)}, u32[]{:S(2)}, u32[]{:S(2)}) collective-permute-start(bf16[1,32,16,256]{3,2,1,0:T(8,128)(2,1)S(1)} %bitcast.218), channel_id=1, source_target_pairs={{0,8},{1,9},{2,10},{3,11},{4,12},{5,13},{6,14},{7,15},{8,0},{9,1},... | collective-permute-start | bytes 786440 | tf_op jit(solution)/shard_map/ppermute | solution.py:100
  190.7 21.8 %collective-permute-start.17 = (bf16[8,40,16,256]{3,2,1,0:T(8,128)(2,1)}, bf16[8,40,16,256]{3,2,1,0:T(8,128)(2,1)}, u32[]{:S(2)}, u32[]{:S(2)}) collective-permute-start(bf16[8,40,16,256]{3,2,1,0:T(8,128)(2,1)} %collective-permute-done.13.refs_1_), channel_id=1, source_target_pairs={{0,1},{1,0},{2,3},{3,2},{4,5},{5,4},{6,7},{7,6},{8,9},{9,8},{10,11... | collective-permute-start | bytes 7864328 | tf_op jit(solution)/shard_map/ppermute | solution.py:89
  200.3 37.2 %all-to-all-start.2 = ((bf16[2,16,32,512]{3,2,0,1:T(8,128)(2,1)}), bf16[2,16,32,512]{3,2,0,1:T(8,128)(2,1)S(1)}, u32[]{:S(2)}, u32[]{:S(2)}) async-start(bf16[2,16,32,512]{3,2,0,1:T(8,128)(2,1)} %copy.82), calls=%async_computation.2 | async-start | bytes 2097152 | tf_op jit(solution)/shard_map/all_to_all | solution.py:607
  208.8 62.8 %collective-permute-start.20 = (bf16[8,32,16,256]{3,2,1,0:T(8,128)(2,1)}, bf16[8,32,16,256]{3,2,1,0:T(8,128)(2,1)}, u32[]{:S(2)}, u32[]{:S(2)}) collective-permute-start(bf16[8,32,16,256]{3,2,1,0:T(8,128)(2,1)} %pad_maximum_fusion.1.refs_0_), channel_id=1, source_target_pairs={{0,16},{1,5},{2,18},{3,7},{4,20},{5,1},{6,22},{7,3},{8,24},{9,13},... | collective-permute-start | bytes 6291464 | tf_op jit(solution)/shard_map/ppermute | solution.py:100
  210.9 60.8 %collective-permute-start.21 = (bf16[8,32,16,256]{3,2,1,0:T(8,128)(2,1)}, bf16[8,32,16,256]{3,2,1,0:T(8,128)(2,1)}, u32[]{:S(2)}, u32[]{:S(2)}) collective-permute-start(bf16[8,32,16,256]{3,2,1,0:T(8,128)(2,1)} %pad_maximum_fusion.1.refs_0_), channel_id=1, source_target_pairs={{0,1},{1,0},{2,3},{3,2},{4,5},{5,4},{6,7},{7,6},{8,9},{9,8},{10,11... | collective-permute-start | bytes 6291464 | tf_op jit(solution)/shard_map/ppermute | solution.py:89
  211.7 41.0 %collective-permute-start.19 = (bf16[2,32,16,256]{3,2,1,0:T(8,128)(2,1)}, bf16[2,32,16,256]{3,2,1,0:T(8,128)(2,1)}, u32[]{:S(2)}, u32[]{:S(2)}) collective-permute-start(bf16[2,32,16,256]{3,2,1,0:T(8,128)(2,1)} %pad_maximum_fusion.16), channel_id=1, source_target_pairs={{0,16},{1,3},{2,18},{3,1},{4,20},{5,7},{6,22},{7,5},{8,24},{9,11},... | collective-permute-start | bytes 1572872 | tf_op jit(solution)/shard_map/ppermute | solution.py:100
  255.0 16.7 %collective-permute-start.22 = (bf16[4,32,16,256]{3,2,1,0:T(8,128)(2,1)}, bf16[4,32,16,256]{3,2,1,0:T(8,128)(2,1)}, u32[]{:S(2)}, u32[]{:S(2)}) collective-permute-start(bf16[4,32,16,256]{3,2,1,0:T(8,128)(2,1)} %pad_maximum_fusion.7), channel_id=1, source_target_pairs={{0,4},{1,17},{2,6},{3,19},{4,0},{5,21},{6,2},{7,23},{8,12},{9,25},... | collective-permute-start | bytes 3145736 | tf_op jit(solution)/shard_map/ppermute | solution.py:100
  271.7 14.4 %collective-permute-start.23 = (bf16[8,32,16,256]{3,2,1,0:T(8,128)(2,1)}, bf16[8,32,16,256]{3,2,1,0:T(8,128)(2,1)}, u32[]{:S(2)}, u32[]{:S(2)}) collective-permute-start(bf16[8,32,16,256]{3,2,1,0:T(8,128)(2,1)} %collective-permute-done.20.refs_1_), channel_id=1, source_target_pairs={{0,1},{1,0},{2,3},{3,2},{4,5},{5,4},{6,7},{7,6},{8,9},{9,8},{10,11... | collective-permute-start | bytes 6291464 | tf_op jit(solution)/shard_map/ppermute | solution.py:89
  274.8 43.1 %collective-permute-start.24 = (bf16[8,32,16,256]{3,2,1,0:T(8,128)(2,1)}, bf16[8,32,16,256]{3,2,1,0:T(8,128)(2,1)}, u32[]{:S(2)}, u32[]{:S(2)}) collective-permute-start(bf16[8,32,16,256]{3,2,1,0:T(8,128)(2,1)} %pad_maximum_fusion.2.refs_0_), channel_id=1, source_target_pairs={{0,2},{1,5},{2,0},{3,7},{4,6},{5,1},{6,4},{7,3},{8,10},{9,13},{10,... | collective-permute-start | bytes 6291464 | tf_op jit(solution)/shard_map/ppermute | solution.py:100
  276.7 41.2 %collective-permute-start.25 = (bf16[8,32,16,256]{3,2,1,0:T(8,128)(2,1)}, bf16[8,32,16,256]{3,2,1,0:T(8,128)(2,1)}, u32[]{:S(2)}, u32[]{:S(2)}) collective-permute-start(bf16[8,32,16,256]{3,2,1,0:T(8,128)(2,1)} %pad_maximum_fusion.2.refs_0_), channel_id=1, source_target_pairs={{0,1},{1,0},{2,3},{3,2},{4,5},{5,4},{6,7},{7,6},{8,9},{9,8},{10,11... | collective-permute-start | bytes 6291464 | tf_op jit(solution)/shard_map/ppermute | solution.py:89
  278.4 39.6 %all-to-all-start.3 = ((bf16[32,1,32,512]{3,2,1,0:T(8,128)(2,1)}), bf16[32,1,32,512]{3,2,1,0:T(8,128)(2,1)S(1)}, u32[]{:S(2)}, u32[]{:S(2)}) async-start(bf16[32,1,32,512]{3,2,1,0:T(8,128)(2,1)} %bitcast.214), calls=%async_computation.3 | async-start | bytes 2097152 | tf_op jit(solution)/shard_map/all_to_all | solution.py:612
  325.3 47.1 %collective-permute-start.30 = (bf16[512,4096]{1,0:T(8,128)(2,1)}, bf16[512,4096]{1,0:T(8,128)(2,1)}, u32[]{:S(2)}, u32[]{:S(2)}) collective-permute-start(bf16[512,4096]{1,0:T(8,128)(2,1)} %get-tuple-element.233.x_own), channel_id=1, source_target_pairs={{0,1},{1,0},{2,3},{3,2},{4,5},{5,4},{6,7},{7,6},{8,9},{9,8},{10,11... | collective-permute-start | bytes 12582920 | tf_op jit(solution)/shard_map/ppermute | solution.py:89
  361.1 22.2 %collective-permute-start.29 = (bf16[512,4096]{1,0:T(8,128)(2,1)}, bf16[512,4096]{1,0:T(8,128)(2,1)}, u32[]{:S(2)}, u32[]{:S(2)}) collective-permute-start(bf16[512,4096]{1,0:T(8,128)(2,1)} %multiply_convert_fusion.y_own), channel_id=1, source_target_pairs={{0,1},{1,0},{2,3},{3,2},{4,5},{5,4},{6,7},{7,6},{8,9},{9,8},{10,11... | collective-permute-start | bytes 12582920 | tf_op jit(solution)/shard_map/ppermute | solution.py:89
  361.2 11.1 %collective-permute-start.31 = (bf16[512,1024]{1,0:T(8,128)(2,1)}, bf16[512,1024]{1,0:T(8,128)(2,1)}, u32[]{:S(2)}, u32[]{:S(2)}) collective-permute-start(bf16[512,1024]{1,0:T(8,128)(2,1)} %copy-done.59), channel_id=1, source_target_pairs={{0,1},{1,0},{2,3},{3,2},{4,5},{5,4},{6,7},{7,6},{8,9},{9,8},{10,11... | collective-permute-start | bytes 3145736 | tf_op jit(solution)/shard_map/ppermute | solution.py:89
  362.4 8.4 %collective-permute-start.27 = (bf16[512,512]{1,0:T(8,128)(2,1)}, bf16[512,512]{1,0:T(8,128)(2,1)}, u32[]{:S(2)}, u32[]{:S(2)}) collective-permute-start(bf16[512,512]{1,0:T(8,128)(2,1)} %constant_dynamic-slice_fusion.2), channel_id=1, source_target_pairs={{0,1},{1,0},{2,3},{3,2},{4,5},{5,4},{6,7},{7,6},{8,9},{9,8},{10,11... | collective-permute-start | bytes 1572872 | tf_op jit(solution)/shard_map/ppermute | solution.py:89
  362.6 29.1 %collective-permute-start.32 = (bf16[512,1024]{1,0:T(8,128)(2,1)}, bf16[512,1024]{1,0:T(8,128)(2,1)}, u32[]{:S(2)}, u32[]{:S(2)}) collective-permute-start(bf16[512,1024]{1,0:T(8,128)(2,1)} %get-tuple-element.227.h_ref.x_own), channel_id=1, source_target_pairs={{0,1},{1,0},{2,3},{3,2},{4,5},{5,4},{6,7},{7,6},{8,9},{9,8},{10,11... | collective-permute-start | bytes 3145736 | tf_op jit(solution)/shard_map/ppermute | solution.py:89
  370.8 101.5 %collective-permute-start.43 = (bf16[512,1024]{1,0:T(8,128)(2,1)}, bf16[512,1024]{1,0:T(8,128)(2,1)}, u32[]{:S(2)}, u32[]{:S(2)}) collective-permute-start(bf16[512,1024]{1,0:T(8,128)(2,1)} %get-tuple-element.210.x_own.o_ref), channel_id=1, source_target_pairs={{0,1},{1,0},{2,3},{3,2},{4,5},{5,4},{6,7},{7,6},{8,9},{9,8},{10,11... | collective-permute-start | bytes 3145736 | tf_op jit(solution)/shard_map/ppermute | solution.py:89
  384.4 37.8 %all-to-all-start.4 = ((bf16[2,16,32,512]{3,2,0,1:T(8,128)(2,1)}), bf16[2,16,32,512]{3,2,0,1:T(8,128)(2,1)}, u32[]{:S(2)}, u32[]{:S(2)}) async-start(bf16[2,16,32,512]{3,2,0,1:T(8,128)(2,1)} %copy.85), calls=%async_computation.4 | async-start | bytes 2097152 | tf_op jit(solution)/shard_map/all_to_all | solution.py:607
  401.2 31.4 %collective-permute-start.33 = (bf16[8,32,16,256]{3,2,1,0:T(8,128)(2,1)}, bf16[8,32,16,256]{3,2,1,0:T(8,128)(2,1)}, u32[]{:S(2)}, u32[]{:S(2)}) collective-permute-start(bf16[8,32,16,256]{3,2,1,0:T(8,128)(2,1)} %get-tuple-element.246), channel_id=1, source_target_pairs={{0,2},{1,5},{2,0},{3,7},{4,6},{5,1},{6,4},{7,3},{8,10},{9,13},{10,... | collective-permute-start | bytes 6291464 | tf_op jit(solution)/shard_map/ppermute | solution.py:100
  403.3 40.0 %collective-permute-start.34 = (bf16[8,32,16,256]{3,2,1,0:T(8,128)(2,1)}, bf16[8,32,16,256]{3,2,1,0:T(8,128)(2,1)}, u32[]{:S(2)}, u32[]{:S(2)}) collective-permute-start(bf16[8,32,16,256]{3,2,1,0:T(8,128)(2,1)} %get-tuple-element.253), channel_id=1, source_target_pairs={{0,16},{1,5},{2,18},{3,7},{4,20},{5,1},{6,22},{7,3},{8,24},{9,13},... | collective-permute-start | bytes 6291464 | tf_op jit(solution)/shard_map/ppermute | solution.py:100
  450.6 22.1 %collective-permute-start.35 = (bf16[512,1024]{1,0:T(8,128)(2,1)S(1)}, bf16[512,1024]{1,0:T(8,128)(2,1)S(1)}, u32[]{:S(2)}, u32[]{:S(2)}) collective-permute-start(bf16[512,1024]{1,0:T(8,128)(2,1)S(1)} %convert_element_type.371.y_own), channel_id=1, source_target_pairs={{0,1},{1,0},{2,3},{3,2},{4,5},{5,4},{6,7},{7,6},{8,9},{9,8},{10,11... | collective-permute-start | bytes 3145736 | tf_op jit(solution)/shard_map/ppermute | solution.py:89
  465.7 14.9 %collective-permute-start.36 = (bf16[4,32,16,256]{3,2,1,0:T(8,128)(2,1)S(1)}, bf16[4,32,16,256]{3,2,1,0:T(8,128)(2,1)S(1)}, u32[]{:S(2)}, u32[]{:S(2)}) collective-permute-start(bf16[4,32,16,256]{3,2,1,0:T(8,128)(2,1)S(1)} %get-tuple-element.346), channel_id=1, source_target_pairs={{0,4},{1,17},{2,6},{3,19},{4,0},{5,21},{6,2},{7,23},{8,12},{9,25},... | collective-permute-start | bytes 3145736 | tf_op jit(solution)/shard_map/ppermute | solution.py:100
  465.9 18.4 %collective-permute-start.41 = (bf16[512,1024]{1,0:T(8,128)(2,1)S(1)}, bf16[512,1024]{1,0:T(8,128)(2,1)S(1)}, u32[]{:S(2)}, u32[]{:S(2)}) collective-permute-start(bf16[512,1024]{1,0:T(8,128)(2,1)S(1)} %copy-done.19), channel_id=1, source_target_pairs={{0,1},{1,0},{2,3},{3,2},{4,5},{5,4},{6,7},{7,6},{8,9},{9,8},{10,11... | collective-permute-start | bytes 3145736 | tf_op jit(solution)/shard_map/ppermute | solution.py:89
  468.6 18.7 %collective-permute-start.42 = (bf16[512,1024]{1,0:T(8,128)(2,1)S(1)}, bf16[512,1024]{1,0:T(8,128)(2,1)S(1)}, u32[]{:S(2)}, u32[]{:S(2)}) collective-permute-start(bf16[512,1024]{1,0:T(8,128)(2,1)S(1)} %copy-done.20), channel_id=1, source_target_pairs={{0,1},{1,0},{2,3},{3,2},{4,5},{5,4},{6,7},{7,6},{8,9},{9,8},{10,11... | collective-permute-start | bytes 3145736 | tf_op jit(solution)/shard_map/ppermute | solution.py:89
  472.3 43.1 %collective-permute-start.37 = (bf16[512,1024]{1,0:T(8,128)(2,1)}, bf16[512,1024]{1,0:T(8,128)(2,1)}, u32[]{:S(2)}, u32[]{:S(2)}) collective-permute-start(bf16[512,1024]{1,0:T(8,128)(2,1)} %get-tuple-element.222.o_ref.x_own), channel_id=1, source_target_pairs={{0,1},{1,0},{2,3},{3,2},{4,5},{5,4},{6,7},{7,6},{8,9},{9,8},{10,11... | collective-permute-start | bytes 3145736 | tf_op jit(solution)/shard_map/ppermute | solution.py:89
  472.7 42.7 %collective-permute-start.38 = (bf16[512,1024]{1,0:T(8,128)(2,1)S(1)}, bf16[512,1024]{1,0:T(8,128)(2,1)}, u32[]{:S(2)}, u32[]{:S(2)}) collective-permute-start(bf16[512,1024]{1,0:T(8,128)(2,1)S(1)} %convert_element_type.369.y_own), channel_id=1, source_target_pairs={{0,1},{1,0},{2,3},{3,2},{4,5},{5,4},{6,7},{7,6},{8,9},{9,8},{10,11... | collective-permute-start | bytes 3145736 | tf_op jit(solution)/shard_map/ppermute | solution.py:89
  480.6 39.8 %collective-permute-start.44 = (bf16[4,32,16,256]{3,2,1,0:T(8,128)(2,1)}, bf16[4,32,16,256]{3,2,1,0:T(8,128)(2,1)}, u32[]{:S(2)}, u32[]{:S(2)}) collective-permute-start(bf16[4,32,16,256]{3,2,1,0:T(8,128)(2,1)} %get-tuple-element.344), channel_id=1, source_target_pairs={{0,2},{1,17},{2,0},{3,19},{4,6},{5,21},{6,4},{7,23},{8,10},{9,25},... | collective-permute-start | bytes 3145736 | tf_op jit(solution)/shard_map/ppermute | solution.py:100
  485.9 34.5 %collective-permute-start.45 = (bf16[2,32,16,256]{3,2,1,0:T(8,128)(2,1)S(1)}, bf16[2,32,16,256]{3,2,1,0:T(8,128)(2,1)S(1)}, u32[]{:S(2)}, u32[]{:S(2)}) collective-permute-start(bf16[2,32,16,256]{3,2,1,0:T(8,128)(2,1)S(1)} %get-tuple-element.359), channel_id=1, source_target_pairs={{0,16},{1,3},{2,18},{3,1},{4,20},{5,7},{6,22},{7,5},{8,24},{9,11},... | collective-permute-start | bytes 1572872 | tf_op jit(solution)/shard_map/ppermute | solution.py:100
  487.3 23.4 %collective-permute-start.39 = (bf16[128,1024]{1,0:T(8,128)(2,1)S(1)}, bf16[128,1024]{1,0:T(8,128)(2,1)}, u32[]{:S(2)}, u32[]{:S(2)}) collective-permute-start(bf16[128,1024]{1,0:T(8,128)(2,1)S(1)} %copy-done.32), channel_id=1, source_target_pairs={{0,1},{1,0},{2,3},{3,2},{4,5},{5,4},{6,7},{7,6},{8,9},{9,8},{10,11... | collective-permute-start | bytes 786440 | tf_op jit(solution)/shard_map/ppermute | solution.py:89
  491.3 62.3 %all-to-all-start.5 = ((bf16[32,1,32,512]{3,2,1,0:T(8,128)(2,1)}), bf16[32,1,32,512]{3,2,1,0:T(8,128)(2,1)S(1)}, u32[]{:S(2)}, u32[]{:S(2)}) async-start(bf16[32,1,32,512]{3,2,1,0:T(8,128)(2,1)} %bitcast.57), calls=%async_computation.5 | async-start | bytes 2097152 | tf_op jit(solution)/shard_map/all_to_all | solution.py:612
  520.4 54.3 %collective-permute-start.51 = (bf16[8,40,16,256]{3,2,1,0:T(8,128)(2,1)}, bf16[8,40,16,256]{3,2,1,0:T(8,128)(2,1)}, u32[]{:S(2)}, u32[]{:S(2)}) collective-permute-start(bf16[8,40,16,256]{3,2,1,0:T(8,128)(2,1)} %get-tuple-element.292), channel_id=1, source_target_pairs={{0,2},{1,17},{2,0},{3,19},{4,6},{5,21},{6,4},{7,23},{8,10},{9,25},... | collective-permute-start | bytes 7864328 | tf_op jit(solution)/shard_map/ppermute | solution.py:100
  526.6 23.0 %collective-permute-start.47 = (bf16[1,32,16,256]{3,2,1,0:T(8,128)(2,1)S(1)}, bf16[1,32,16,256]{3,2,1,0:T(8,128)(2,1)S(1)}, u32[]{:S(2)}, u32[]{:S(2)}) collective-permute-start(bf16[1,32,16,256]{3,2,1,0:T(8,128)(2,1)S(1)} %add_convert_fusion.27), channel_id=1, source_target_pairs={{0,8},{1,9},{2,10},{3,11},{4,12},{5,13},{6,14},{7,15},{8,0},{9,1},... | collective-permute-start | bytes 786440 | tf_op jit(solution)/shard_map/ppermute | solution.py:100
  531.4 23.3 %collective-permute-start.46 = (bf16[2,32,16,256]{3,2,1,0:T(8,128)(2,1)}, bf16[2,32,16,256]{3,2,1,0:T(8,128)(2,1)}, u32[]{:S(2)}, u32[]{:S(2)}) collective-permute-start(bf16[2,32,16,256]{3,2,1,0:T(8,128)(2,1)} %get-tuple-element.353), channel_id=1, source_target_pairs={{0,4},{1,3},{2,6},{3,1},{4,0},{5,7},{6,2},{7,5},{8,12},{9,11},{10,... | collective-permute-start | bytes 1572872 | tf_op jit(solution)/shard_map/ppermute | solution.py:100
  549.1 19.7 %collective-permute-start.48 = (bf16[512,1024]{1,0:T(8,128)(2,1)}, bf16[512,1024]{1,0:T(8,128)(2,1)}, u32[]{:S(2)}, u32[]{:S(2)}) collective-permute-start(bf16[512,1024]{1,0:T(8,128)(2,1)} %get-tuple-element.296.y_own), channel_id=1, source_target_pairs={{0,1},{1,0},{2,3},{3,2},{4,5},{5,4},{6,7},{7,6},{8,9},{9,8},{10,11... | collective-permute-start | bytes 3145736 | tf_op jit(solution)/shard_map/ppermute | solution.py:89
  549.1 14.1 %collective-permute-start.49 = (bf16[512,1024]{1,0:T(8,128)(2,1)}, bf16[512,1024]{1,0:T(8,128)(2,1)}, u32[]{:S(2)}, u32[]{:S(2)}) collective-permute-start(bf16[512,1024]{1,0:T(8,128)(2,1)} %get-tuple-element.295.y_own), channel_id=1, source_target_pairs={{0,1},{1,0},{2,3},{3,2},{4,5},{5,4},{6,7},{7,6},{8,9},{9,8},{10,11... | collective-permute-start | bytes 3145736 | tf_op jit(solution)/shard_map/ppermute | solution.py:89
  549.7 8.1 %collective-permute-start.50 = (bf16[512,1024]{1,0:T(8,128)(2,1)}, bf16[512,1024]{1,0:T(8,128)(2,1)}, u32[]{:S(2)}, u32[]{:S(2)}) collective-permute-start(bf16[512,1024]{1,0:T(8,128)(2,1)} %get-tuple-element.294.y_own), channel_id=1, source_target_pairs={{0,1},{1,0},{2,3},{3,2},{4,5},{5,4},{6,7},{7,6},{8,9},{9,8},{10,11... | collective-permute-start | bytes 3145736 | tf_op jit(solution)/shard_map/ppermute | solution.py:89
  556.4 18.3 %collective-permute-start.52 = (bf16[1,32,16,256]{3,2,1,0:T(8,128)(2,1)}, bf16[1,32,16,256]{3,2,1,0:T(8,128)(2,1)S(1)}, u32[]{:S(2)}, u32[]{:S(2)}) collective-permute-start(bf16[1,32,16,256]{3,2,1,0:T(8,128)(2,1)} %add_convert_fusion.26), channel_id=1, source_target_pairs={{0,8},{1,9},{2,10},{3,11},{4,12},{5,13},{6,14},{7,15},{8,0},{9,1},... | collective-permute-start | bytes 786440 | tf_op jit(solution)/shard_map/ppermute | solution.py:100
  575.4 36.2 %collective-permute-start.53 = (bf16[8,24,16,256]{3,2,1,0:T(8,128)(2,1)}, bf16[8,24,16,256]{3,2,1,0:T(8,128)(2,1)}, u32[]{:S(2)}, u32[]{:S(2)}) collective-permute-start(bf16[8,24,16,256]{3,2,1,0:T(8,128)(2,1)} %get-tuple-element.297), channel_id=1, source_target_pairs={{0,2},{1,17},{2,0},{3,19},{4,6},{5,21},{6,4},{7,23},{8,10},{9,25},... | collective-permute-start | bytes 4718600 | tf_op jit(solution)/shard_map/ppermute | solution.py:100
  580.1 31.5 %collective-permute-start.54 = (bf16[4,40,16,256]{3,2,1,0:T(8,128)(2,1)}, bf16[4,40,16,256]{3,2,1,0:T(8,128)(2,1)}, u32[]{:S(2)}, u32[]{:S(2)}) collective-permute-start(bf16[4,40,16,256]{3,2,1,0:T(8,128)(2,1)} %get-tuple-element.342), channel_id=1, source_target_pairs={{0,4},{1,5},{2,6},{3,7},{4,0},{5,1},{6,2},{7,3},{8,12},{9,13},{10,... | collective-permute-start | bytes 3932168 | tf_op jit(solution)/shard_map/ppermute | solution.py:100
  613.4 13.0 %collective-permute-start.57 = (bf16[4,24,16,256]{3,2,1,0:T(8,128)(2,1)S(1)}, bf16[4,24,16,256]{3,2,1,0:T(8,128)(2,1)S(1)}, u32[]{:S(2)}, u32[]{:S(2)}) collective-permute-start(bf16[4,24,16,256]{3,2,1,0:T(8,128)(2,1)S(1)} %get-tuple-element.347), channel_id=1, source_target_pairs={{0,4},{1,3},{2,6},{3,1},{4,0},{5,7},{6,2},{7,5},{8,12},{9,11},{10,... | collective-permute-start | bytes 2359304 | tf_op jit(solution)/shard_map/ppermute | solution.py:100
  615.7 10.7 %collective-permute-start.58 = (bf16[2,40,16,256]{3,2,1,0:T(8,128)(2,1)S(1)}, bf16[2,40,16,256]{3,2,1,0:T(8,128)(2,1)S(1)}, u32[]{:S(2)}, u32[]{:S(2)}) collective-permute-start(bf16[2,40,16,256]{3,2,1,0:T(8,128)(2,1)S(1)} %get-tuple-element.350), channel_id=1, source_target_pairs={{0,16},{1,3},{2,18},{3,1},{4,20},{5,7},{6,22},{7,5},{8,24},{9,11},... | collective-permute-start | bytes 1966088 | tf_op jit(solution)/shard_map/ppermute | solution.py:100
  626.6 18.9 %collective-permute-start.59 = (bf16[2,24,16,256]{3,2,1,0:T(8,128)(2,1)S(1)}, bf16[2,24,16,256]{3,2,1,0:T(8,128)(2,1)}, u32[]{:S(2)}, u32[]{:S(2)}) collective-permute-start(bf16[2,24,16,256]{3,2,1,0:T(8,128)(2,1)S(1)} %get-tuple-element.363), channel_id=1, source_target_pairs={{0,16},{1,5},{2,18},{3,7},{4,20},{5,1},{6,22},{7,3},{8,24},{9,13},... | collective-permute-start | bytes 1179656 | tf_op jit(solution)/shard_map/ppermute | solution.py:100
  627.4 18.0 %collective-permute-start.60 = (bf16[1,40,16,256]{3,2,1,0:T(8,128)(2,1)S(1)}, bf16[1,40,16,256]{3,2,1,0:T(8,128)(2,1)S(1)}, u32[]{:S(2)}, u32[]{:S(2)}) collective-permute-start(bf16[1,40,16,256]{3,2,1,0:T(8,128)(2,1)S(1)} %add_convert_fusion.21), channel_id=1, source_target_pairs={{0,8},{1,9},{2,10},{3,11},{4,12},{5,13},{6,14},{7,15},{8,0},{9,1},... | collective-permute-start | bytes 983048 | tf_op jit(solution)/shard_map/ppermute | solution.py:100
  636.0 26.1 %all-to-all-start.7 = ((f32[8,1,1088]{2,1,0:T(1,128)}), f32[8,1,1088]{2,1,0:T(1,128)S(1)}, u32[]{:S(2)}, u32[]{:S(2)}) async-start(f32[8,1,1088]{2,1,0:T(1,128)} %all_to_all.81), calls=%async_computation.7 | async-start | bytes 73728 | tf_op jit(solution)/shard_map/all_to_all | solution.py:808
  646.4 12.9 %collective-permute-start.61 = (bf16[1,24,16,256]{3,2,1,0:T(8,128)(2,1)S(1)}, bf16[1,24,16,256]{3,2,1,0:T(8,128)(2,1)S(1)}, u32[]{:S(2)}, u32[]{:S(2)}) collective-permute-start(bf16[1,24,16,256]{3,2,1,0:T(8,128)(2,1)S(1)} %add_convert_fusion.29), channel_id=1, source_target_pairs={{0,8},{1,9},{2,10},{3,11},{4,12},{5,13},{6,14},{7,15},{8,0},{9,1},... | collective-permute-start | bytes 589832 | tf_op jit(solution)/shard_map/ppermute | solution.py:100
  662.1 29.9 %all-to-all-start.6 = ((bf16[128,16,256]{2,1,0:T(8,128)(2,1)}), bf16[128,16,256]{2,1,0:T(8,128)(2,1)S(1)}, u32[]{:S(2)}, u32[]{:S(2)}) async-start(bf16[128,16,256]{2,1,0:T(8,128)(2,1)} %gather_fusion.3), calls=%async_computation.6 | async-start | bytes 2097152 | tf_op jit(solution)/shard_map/all_to_all | solution.py:286
  670.7 24.5 %collective-permute-start.64 = (f32[1,1088]{1,0:T(1,128)S(1)}, f32[1,1088]{1,0:T(1,128)S(1)}, u32[]{:S(2)}, u32[]{:S(2)}) collective-permute-start(f32[1,1088]{1,0:T(1,128)S(1)} %broadcast_in_dim.82), channel_id=1, source_target_pairs={{0,16},{16,0},{1,17},{17,1},{2,18},{18,2},{3,19},{19,3},{4,20},{20... | collective-permute-start | bytes 13064 | tf_op jit(solution)/shard_map/ppermute | solution.py:92
  692.0 24.3 %collective-permute-start.62 = (bf16[8,16,16,256]{3,2,1,0:T(8,128)(2,1)S(1)}, bf16[8,16,16,256]{3,2,1,0:T(8,128)(2,1)S(1)}, u32[]{:S(2)}, u32[]{:S(2)}) collective-permute-start(bf16[8,16,16,256]{3,2,1,0:T(8,128)(2,1)S(1)} %bitcast.211), channel_id=1, source_target_pairs={{0,16},{16,0},{1,17},{17,1},{2,18},{18,2},{3,19},{19,3},{4,20},{20... | collective-permute-start | bytes 3145736 | tf_op jit(solution)/shard_map/ppermute | solution.py:92
  (129 other events, 1339.1 us)

commit v3 on v2

--- a/solution.py
+++ b/solution.py
@@ -51,6 +51,10 @@
     return lax.dot_general(a, b, TN, preferred_element_type=f32)
 
 
+def small():
+    return pl.CostEstimate(flops=1 << 20, bytes_accessed=1 << 20, transcendentals=0)
+
+
 def params(**kw):
     return pltpu.CompilerParams(vmem_limit_bytes=VMEM_LIMIT, **kw)
 
@@ -65,25 +69,24 @@
 SHAPES["fi"], SHAPES["fo"] = (D, FF), (FF, D)
 
 
+def chunk_of(i):
+    return (i & 8) | ((i & 2) << 1) | ((i & 1) << 1) | ((i & 4) >> 2)
+
+
 class Net:
     def __init__(self, n_rep, n_shard, n_mp):
         self.n_rep, self.n_shard, self.n_mp = n_rep, n_shard, n_mp
         self.n_data = n_rep * n_shard
-        power = self.n_data & (self.n_data - 1) == 0
-        self.pieces = self.n_data if power and BS % (16 * self.n_data) == 0 else 1
+        self.pieces = 16 if (n_rep, n_shard, n_mp) == (2, 8, 2) else 1
         self.rows = BS // self.pieces
         self.depth = self.pieces.bit_length() - 1
-        if self.pieces == 16:
-            x, z1, z2, y = 1, 2, 4, 8
-            self.orders = (
-                ((z2, y, z1, x), (z2, z1, x, y)),
-                ((z2, y, z1, x), (z2, x, z1, y)),
-                ((z2, z1, x, y), (z2, x, y, z1)),
-                ((z2, y, z1, x), (z2, x, y, z1)),
-            )
-        else:
-            down = tuple(1 << s for s in range(self.depth - 1, -1, -1))
-            self.orders = ((down,) * n_mp,) * len(GROUPS)
+        x, z1, z2, y = 1, 2, 4, 8
+        self.orders = (
+            ((z2, y, z1, x), (z2, z1, x, y)),
+            ((z2, z1, y, x), (z2, z1, x, y)),
+            ((z2, x, z1, y), (z2, y, z1, x)),
+            ((z2, x, y, z1), (z2, y, z1, x)),
+        )
 
     def swap_core(self, value):
         return lax.ppermute(value, "mp", [(i, i ^ 1) for i in range(self.n_mp)])
@@ -101,24 +104,26 @@
 
     def table(self, group, core, data_index):
         many = self.pieces
-        half = max(many // 2, 1)
+        if many == 1:
+            return jnp.stack([0, 0, 0, 0, core]).astype(jnp.int32)
+        half = many // 4
         rel = []
         for order in self.orders[group]:
             rel.append([sum(b for s, b in enumerate(order) if q >> s & 1) for q in range(many)])
         rows = []
         for m in range(self.n_mp):
-            place = [rel[self.n_mp - 1 - m].index(r) for r in rel[m]]
+            place = [rel[1 - m].index(r) // 2 for r in rel[m][::2]]
             low = [p for p in place if p < half][0]
-            high = ([p - half for p in place if p >= half] or [0])[0]
+            high = [p - half for p in place if p >= half][0]
             lows, highs = [], []
             for p in place:
                 low, high = (p, high) if p < half else (low, p - half)
                 lows.append(low)
                 highs.append(high)
-            rows.append([rel[m], lows, highs, [int(p >= half) for p in place]])
+            rows.append([chunk_of(r) for r in rel[m]] + lows + highs + [int(p >= half) for p in place])
         mine = jnp.asarray(np.array(rows, np.int32))[core]
-        mine = mine.at[0].set(mine[0] ^ data_index)
-        return jnp.concatenate([mine.reshape(-1), core.reshape(1)]).astype(jnp.int32)
+        chunks = mine[:many] ^ chunk_of(data_index)
+        return jnp.concatenate([chunks, mine[many:], core.reshape(1)]).astype(jnp.int32)
 
 
 def together(*values):
@@ -163,29 +168,37 @@
     return sum(blocks_of(name, n_mp) for name, _ in GROUPS[group])
 
 
-def place_body(s, *refs, dests, many, half, two):
+def place_body(s, *refs, dests, many, two):
     q = pl.program_id(0)
+    steps = many // 2 if two else 1
     if two:
         own_lo, own_hi, sib_lo, sib_hi = refs[:4]
         outs = refs[4:]
     else:
         own_lo, sib_lo = refs[:2]
         outs = refs[2:]
-    core = s[4 * many]
-    for b in range(own_lo.shape[1]):
-        own, sib = own_lo[0, b], sib_lo[0, b]
+    core = s[many + 3 * steps]
+    rows = own_lo.shape[2]
+    for t in range(own_lo.shape[0]):
+        here = pl.ds(0, rows)
         if two:
-            own = jnp.where(q < half, own, own_hi[0, b])
-            sib = jnp.where(s[3 * many + q] == 0, sib, sib_hi[0, b])
-        for h in range(2):
-            which, row, col = dests[h][b]
-            outs[which][row, :, col : col + BS] = jnp.where(core == h, own, sib)
+            here = pl.ds(pl.multiple_of((s[2 * q + t] & 1) * rows, rows), rows)
+        for b in range(own_lo.shape[1]):
+            own, sib = own_lo[t, b], sib_lo[t, b]
+            if two:
+                own = jnp.where(q < steps // 2, own, own_hi[t, b])
+                sib = jnp.where(s[many + 2 * steps + q] == 0, sib, sib_hi[t, b])
+            for h in range(2):
+                which, row, col = dests[h][b]
+                outs[which][row, here, col : col + BS] = jnp.where(core == h, own, sib)
 
 
 def place(net, group, table, own, sib):
     many, rows, n_mp = net.pieces, net.rows, net.n_mp
     two = many > 1
-    half = max(many // 2, 1)
+    per = 2 if two else 1
+    steps = many // per
+    half = max(steps // 2, 1)
     dests = ([], [])
     shapes, specs = [], []
     for which, (name, wide) in enumerate(GROUPS[group]):
@@ -200,26 +213,26 @@
                     else:
                         dests[h].append((which, h * (tall // BS) + r, c * BS))
         shapes.append(jax.ShapeDtypeStruct((height // BS, BS, width), bf16))
-        specs.append(pl.BlockSpec((height // BS, rows, width), lambda q, s: (0, s[q], 0)))
+        specs.append(
+            pl.BlockSpec((height // BS, per * rows, width), lambda q, s: (0, s[per * q] // per, 0))
+        )
     nb = own[0].shape[1]
-    block = (1, nb, rows, BS)
+    block = (per, nb, rows, BS)
     lo = pl.BlockSpec(block, lambda q, s: (jnp.minimum(q, half - 1), 0, 0, 0))
     hi = pl.BlockSpec(block, lambda q, s: (jnp.maximum(q - half, 0), 0, 0, 0))
     sib_lo = pl.BlockSpec(block, lambda q, s: (s[many + q], 0, 0, 0))
-    sib_hi = pl.BlockSpec(block, lambda q, s: (s[2 * many + q], 0, 0, 0))
+    sib_hi = pl.BlockSpec(block, lambda q, s: (s[many + steps + q], 0, 0, 0))
     out = pl.pallas_call(
-        functools.partial(place_body, dests=dests, many=many, half=half, two=two),
+        functools.partial(place_body, dests=dests, many=many, two=two),
         grid_spec=pltpu.PrefetchScalarGridSpec(
             num_scalar_prefetch=1,
-            grid=(many,),
+            grid=(steps,),
             in_specs=[lo, hi, sib_lo, sib_hi] if two else [lo, sib_lo],
             out_specs=tuple(specs),
         ),
         out_shape=tuple(shapes),
         compiler_params=params(),
-        cost_estimate=pl.CostEstimate(
-            flops=0, bytes_accessed=8 * many * nb * rows * BS, transcendentals=0
-        ),
+        cost_estimate=small(),
         name="place",
     )(table, *own, *sib)
     return [o.reshape(-1, o.shape[2]) for o in out]
@@ -239,18 +252,26 @@
     return (cur, got), (sib_lo, sib_hi)
 
 
-def first_pieces(net, weights, inverse):
+def first_pieces(net, weights, vectors, inverse):
     low = weights[0].astype(bf16)
+    vec = vectors.astype(bf16)
     if net.pieces == 1:
         every = lax.all_gather(low, "shard", axis=0, tiled=True)
-    else:
-        plane = lax.axis_index("rep")
-        nblk = low.shape[0]
-        cut = low.reshape(nblk, net.n_rep, net.n_shard, net.rows, BS)
-        cut = lax.dynamic_index_in_dim(cut, plane, axis=1, keepdims=False)
-        cut = jnp.swapaxes(cut, 0, 1).reshape(-1, net.rows, BS)
-        every = lax.all_to_all(cut, "shard", split_axis=0, concat_axis=0, tiled=True)
-    return every.at[inverse].get(mode="promise_in_bounds")
+        vec_every = lax.all_gather(vec, "shard", axis=1, tiled=True)
+        return every.at[inverse].get(mode="promise_in_bounds"), vec_every
+    nblk = low.shape[0]
+    cut = low.reshape(nblk, 2, 2, 2, 2, net.rows, BS)
+    cut = lax.dynamic_index_in_dim(cut, lax.axis_index("rep"), axis=1, keepdims=False)
+    cut = cut.transpose(3, 1, 2, 0, 4, 5).reshape(net.n_shard, nblk, net.rows, BS)
+    room = net.rows * BS
+    vec_cut = jnp.pad(vec.reshape(-1), (0, room - vec.shape[1])).reshape(1, 1, net.rows, BS)
+    cut = jnp.concatenate([cut, jnp.broadcast_to(vec_cut, (net.n_shard,) + vec_cut.shape[1:])], axis=1)
+    every = lax.all_to_all(
+        cut.reshape(-1, net.rows, BS), "shard", split_axis=0, concat_axis=0, tiled=True
+    )
+    pieces = every.at[inverse + inverse // nblk].get(mode="promise_in_bounds")
+    vec_every = every.reshape(net.n_shard, nblk + 1, room)[:, nblk, : vec.shape[1]]
+    return pieces, vec_every.reshape(1, -1)
 
 
 def total_of(*terms):
@@ -281,7 +302,8 @@
     if net.pieces == 1:
         owned = lax.psum_scatter(dealt, "shard", scatter_dimension=0, tiled=True)
         owned = total_of(owned, net.swap_rep(owned))
-        cut = owned.reshape(-1, 2, BS // 32, 16, BS).transpose(1, 2, 0, 3, 4)
+        cut = owned.reshape(-1, 2, 8, 16, BS).transpose(1, 2, 0, 3, 4)
+        cut = cut[:, np.array([chunk_of(k) for k in range(8)])]
         return cut[0], cut[1], jnp.zeros((1,), jnp.int32)
     mine = lax.all_to_all(dealt, "shard", split_axis=0, concat_axis=0, tiled=True)
     mine = mine.reshape(net.n_shard, -1, net.rows, BS)
@@ -347,9 +369,7 @@
             pl.BlockSpec((seq, LANES), lambda i: (0, 0)),
         ),
         compiler_params=params(),
-        cost_estimate=pl.CostEstimate(
-            flops=4 * seq * keys * width, bytes_accessed=8 * seq * width, transcendentals=0
-        ),
+        cost_estimate=small(),
         name="attend_forward",
     )(limit, q, k, v)
     return o, lse[:, : 2 * pairs].T.reshape(pairs, 2, seq)
@@ -434,9 +454,7 @@
         out_specs=(q_spec, k_spec, k_spec),
         scratch_shapes=[pltpu.VMEM((keys, LANES), f32), pltpu.VMEM((keys, LANES), f32)],
         compiler_params=params(),
-        cost_estimate=pl.CostEstimate(
-            flops=10 * seq * keys * width, bytes_accessed=16 * seq * width, transcendentals=0
-        ),
+        cost_estimate=small(),
         name="attend_backward",
     )(limit, q, k, v, o, do, lse)
 
@@ -478,66 +496,73 @@
         out_specs=(spec, spec),
         scratch_shapes=[pltpu.VMEM((seq, tile), f32)],
         compiler_params=params(),
-        cost_estimate=pl.CostEstimate(
-            flops=2 * seq * width * hidden + 60 * seq * hidden,
-            bytes_accessed=4 * seq * hidden + 2 * width * hidden,
-            transcendentals=0,
-        ),
+        cost_estimate=small(),
         name="gelu_forward",
     )(h, w, b)
 
 
-def weight_grad_body(s, x_own, x_sib, y_own, y_sib, *refs, outs, many, rows):
-    targets, buf = refs[-1 - outs : -1], refs[-1]
-    acc = dot_tn(x_own[...], y_own[...]) + dot_tn(x_sib[...], y_sib[...])
-    buf[...] = acc.astype(bf16)
+def weight_grad_body(s, x_own, x_sib, *refs, count, outs, many, rows):
+    y_own, y_sib = refs[:count], refs[count : 2 * count]
+    targets = refs[-3 - outs : -3]
+    t_own, t_sib, buf = refs[-3:]
+    t_own[...] = x_own[...].T
+    t_sib[...] = x_sib[...].T
     per = many // outs
+    for k in range(count):
+        acc = dot_nn(t_own[...], y_own[k][...]) + dot_nn(t_sib[...], y_sib[k][...])
+        buf[k] = acc.astype(bf16)
     for q in range(many):
         here = pl.ds(pl.multiple_of(s[q] * rows, rows), rows)
-        for c in range(targets[0].shape[1]):
-            targets[q // per][q % per, c] = buf[here, c * BS : (c + 1) * BS]
-
-
-def weight_grad(net, group, table, x_own, x_sib, y_own, y_sib, held, first_block, wide):
-    seq = x_own.shape[0]
+        for k in range(count):
+            for c in range(targets[0].shape[2]):
+                targets[q // per][q % per, k, c] = buf[k, here, c * BS : (c + 1) * BS]
+
+
+def weight_grad(net, group, table, xs, ys, held, first, wide):
+    seq = xs[0].shape[0]
     many, rows, halves = net.pieces, net.rows, net.n_mp
-    at_core = 4 * many
+    at_core = table.shape[0] - 1
+    count = len(ys)
+    width = ys[0][0].shape[1]
     if wide:
-        steps = x_own.shape[1] // BS
-        y_width = y_own.shape[1] // halves
+        steps = xs[0].shape[1] // BS
+        y_width = width // halves
         x_spec = pl.BlockSpec((seq, BS), lambda i, s: (0, i))
         y_spec = pl.BlockSpec((seq, y_width), lambda i, s: (0, s[at_core]))
     else:
-        steps = x_own.shape[1] // halves // BS
-        y_width = y_own.shape[1]
+        steps = xs[0].shape[1] // halves // BS
+        y_width = width
         x_spec = pl.BlockSpec((seq, BS), lambda i, s: (0, s[at_core] * steps + i))
         y_spec = pl.BlockSpec((seq, y_width), lambda i, s: (0, 0))
     nb = y_width // BS
-    at = first_block // nb
-    total = group_blocks(group, halves)
+    at = first // count
     outs = 2 if many > 1 else 1
+    shape = (many // outs, len(GROUPS[group]), steps * nb, rows, BS)
     anyspec = pl.BlockSpec(memory_space=pl.ANY)
     held = held or ()
+    before = 3 + 2 * count
     return pl.pallas_call(
-        functools.partial(weight_grad_body, outs=outs, many=many, rows=rows),
+        functools.partial(weight_grad_body, count=count, outs=outs, many=many, rows=rows),
         grid_spec=pltpu.PrefetchScalarGridSpec(
             num_scalar_prefetch=1,
             grid=(steps,),
-            in_specs=[x_spec, x_spec, y_spec, y_spec] + [anyspec] * len(held),
-            out_specs=(pl.BlockSpec((many // outs, nb, rows, BS), lambda i, s: (0, at + i, 0, 0)),)
+            in_specs=[x_spec] * 2 + [y_spec] * (2 * count) + [anyspec] * len(held),
+            out_specs=(
+                pl.BlockSpec((many // outs, count, nb, rows, BS), lambda i, s: (0, at, i, 0, 0)),
+            )
             * outs,
-            scratch_shapes=[pltpu.VMEM((BS, y_width), bf16)],
+            scratch_shapes=[
+                pltpu.VMEM((BS, seq), bf16),
+                pltpu.VMEM((BS, seq), bf16),
+                pltpu.VMEM((count, BS, y_width), bf16),
+            ],
         ),
-        out_shape=(jax.ShapeDtypeStruct((many // outs, total, rows, BS), bf16),) * outs,
-        input_output_aliases={5 + k: k for k in range(len(held))},
+        out_shape=(jax.ShapeDtypeStruct(shape, bf16),) * outs,
+        input_output_aliases={before + k: k for k in range(len(held))},
         compiler_params=params(),
-        cost_estimate=pl.CostEstimate(
-            flops=4 * seq * steps * BS * y_width,
-            bytes_accessed=4 * seq * (steps * BS + y_width) + 2 * steps * BS * y_width,
-            transcendentals=0,
-        ),
+        cost_estimate=small(),
         name="weight_grad",
-    )(table, x_own, x_sib, y_own, y_sib, *held)
+    )(table, *xs, *[y[0] for y in ys], *[y[1] for y in ys], *held)
 
 
 def split_low(a):
@@ -546,9 +571,10 @@
 
 
 def shampoo_body(flag, mine_ref, other_ref, w_ref, ls_ref, rs_ref, lr_ref, rr_ref, og, ol, orr, ow, g_ref):
-    size = mine_ref.shape[0] * mine_ref.shape[2]
-    g_ref[pl.ds(pl.multiple_of(flag[0] * size, size), size), :] = mine_ref[:, 0].reshape(size, BS)
-    g_ref[pl.ds(pl.multiple_of((1 - flag[0]) * size, size), size), :] = other_ref[:, 0].reshape(size, BS)
+    for k in range(mine_ref.shape[0]):
+        for plane, src in ((flag[0], mine_ref), (1 - flag[0], other_ref)):
+            row = pl.multiple_of(plane * 128 + chunk_of(k) * 16, 16)
+            g_ref[pl.ds(row, 16), :] = src[k, 0]
     g = g_ref[...]
     og[0, 0] = g.astype(f32)
     ol[0, 0] = 0.5 * ls_ref[0, 0] + 0.5 * dot_nt(g, g)
@@ -573,9 +599,7 @@
         out_specs=(spec,) * 4,
         scratch_shapes=[pltpu.VMEM((BS, BS), bf16)],
         compiler_params=params(),
-        cost_estimate=pl.CostEstimate(
-            flops=14 * n * BS**3, bytes_accessed=38 * n * BS * BS, transcendentals=0
-        ),
+        cost_estimate=small(),
         name="shampoo",
     )(flag, mine, other, weights, left_stat, right_stat, left_root, right_root)
 
@@ -665,7 +689,7 @@
     x, x_sib = whole(inputs)
     e, e_sib = whole(encoded)
 
-    pieces = first_pieces(net, weights, inverse_of(block_slots))
+    pieces, vec_mine = first_pieces(net, weights, vectors, inverse_of(block_slots))
     flows, base = [], 0
     for k in range(len(GROUPS)):
         size = group_blocks(k, halves)
@@ -678,19 +702,11 @@
 
     step((), attn)
     step((), attn, cross)
+    step((), attn)
     step((), attn, cross)
-    step((), attn, cross)
-    step((), attn, up)
-    w_sq, w_sk, w_sv = step(placed(0), cross, up)
-
-    vec_low = vectors.astype(bf16)
-    vec_mine = lax.all_to_all(
-        jnp.broadcast_to(vec_low, (net.n_shard, vec_low.shape[1])),
-        "shard",
-        split_axis=0,
-        concat_axis=0,
-        tiled=True,
-    ).reshape(1, -1)
+    vec_mine, x, x_sib, e, e_sib = step((vec_mine, x, x_sib, e, e_sib), attn, cross, up)
+    w_sq, w_sk, w_sv = step(placed(0), up)
+
     vec_other = net.swap_core(vec_mine)
     vec_both = jnp.concatenate(
         [jnp.where(is_first, vec_mine, vec_other), jnp.where(is_first, vec_other, vec_mine)]
@@ -702,10 +718,10 @@
     q_s = (dot_nn(x, w_sq) + b_sq).astype(bf16)
     k_s = dot_nn(x, w_sk).astype(bf16)
     v_s = (dot_nn(x, w_sv) + b_sv).astype(bf16)
-    cot_in, q_s, k_s, v_s = step((cotangent, q_s, k_s, v_s), up, down)
-    cot_pieces = route_out(cot_in)
+    q_s, k_s, v_s = step((q_s, k_s, v_s), cross, up, down)
     o_s, lse_s = attend_forward(limit, q_s, k_s, v_s, True)
-    o_s, lse_s = step((o_s, lse_s), cross, up, down)
+    cotangent, o_s, lse_s = step((cotangent, o_s, lse_s), cross, up, down)
+    cot_pieces = route_out(cotangent)
     w_so, w_cq, w_ck, w_cv, w_co = placed(1)
     z_one = x.astype(f32) + dot_nn(o_s, w_so) + b_so
     h_one, n_one, r_one = norm_forward(z_one, g_one, b_one)
@@ -713,12 +729,12 @@
     q_c = (dot_nn(h_one_low, w_cq) + b_cq).astype(bf16)
     k_c = dot_nn(e, w_ck).astype(bf16)
     v_c = (dot_nn(e, w_cv) + b_cv).astype(bf16)
-    cot_pieces, q_c, k_c, v_c = step((cot_pieces, q_c, k_c, v_c), down)
-    cot_home = route_home(cot_pieces, seq_slots)
+    q_c, k_c, v_c = step((q_c, k_c, v_c), down)
     o_c, lse_c = attend_forward(limit, q_c, k_c, v_c, False)
     z_two = h_one + dot_nn(o_c, w_co) + b_co
     h_two, n_two, r_two = norm_forward(z_two, g_two, b_two)
-    h_two, h_two_low = step((h_two, h_two.astype(bf16)), up, down)
+    cot_pieces, h_two, h_two_low = step((cot_pieces, h_two, h_two.astype(bf16)), up, down)
+    cot_home = route_home(cot_pieces, seq_slots)
     (w_fi,) = placed(2)
     act, slope = gelu_forward(h_two_low, w_fi, b_fi)
     act_sib = net.swap_core(act)
@@ -730,12 +746,13 @@
     source = inverse_of(seq_slots)
     finished = halved((h_three * live).astype(bf16))
 
-    def gradient(k, *operands):
-        held, base = None, 0
-        for (name, wide), ops in zip(GROUPS[k], operands):
-            held = weight_grad(net, k, tables[k], *ops, held, base, wide)
-            base += blocks_of(name, halves)
-        return Flow(reduce_rounds(net, k, held))
+    def gradient(k, *calls):
+        held, first = None, 0
+        for xs, *ys in calls:
+            held = weight_grad(net, k, tables[k], xs, ys, held, first, GROUPS[k][first][1])
+            first += len(ys)
+        parts = tuple(h.reshape(h.shape[0], -1, net.rows, BS) for h in held)
+        return Flow(reduce_rounds(net, k, parts))
 
     cot, _ = whole(cot_home)
     grad_y = cot.astype(f32) * live
@@ -743,10 +760,10 @@
     a_three = d_three.astype(bf16)
     d_hidden = (dot_nt(a_three, w_fo) * slope.astype(f32)).astype(bf16)
     d_hidden_sib = net.swap_core(d_hidden)
-    down = gradient(3, (act, act_sib, a_three, net.swap_core(a_three)))
+    down = gradient(3, ((act, act_sib), (a_three, net.swap_core(a_three))))
     finished, d_hidden, d_hidden_sib = step((finished, d_hidden, d_hidden_sib), down)
     out_pieces = route_out(finished)
-    up = gradient(2, (h_two_low, net.swap_core(h_two_low), d_hidden, d_hidden_sib))
+    up = gradient(2, ((h_two_low, net.swap_core(h_two_low)), (d_hidden, d_hidden_sib)))
     (d_hidden,) = step((d_hidden,), up)
     d_h_two = d_three + dot_nt(d_hidden, w_fi)
     d_two, dg_two, db_two = norm_backward(d_h_two, n_two, r_two, g_two)
@@ -765,24 +782,24 @@
     a_one, a_one_sib, d_os = step((a_one, a_one_sib, d_os), down)
     cross = gradient(
         1,
-        (o_s, net.swap_core(o_s), a_one, a_one_sib),
-        (h_one_low, net.swap_core(h_one_low), dq_c, dq_c_sib),
-        (e, e_sib, dk_c, dk_c_sib),
-        (e, e_sib, dv_c, dv_c_sib),
-        (o_c, net.swap_core(o_c), a_two, net.swap_core(a_two)),
+        ((o_s, net.swap_core(o_s)), (a_one, a_one_sib)),
+        ((h_one_low, net.swap_core(h_one_low)), (dq_c, dq_c_sib)),
+        ((e, e_sib), (dk_c, dk_c_sib), (dv_c, dv_c_sib)),
+        ((o_c, net.swap_core(o_c)), (a_two, net.swap_core(a_two))),
     )
     (d_os,) = step((d_os,), cross, up, down)
     dq_s, dk_s, dv_s = attend_backward(limit, q_s, k_s, v_s, o_s, d_os, lse_s, True)
     sibs = [net.swap_core(v) for v in (dq_s, dk_s, dv_s)]
-    outputs, dq_s, dk_s, dv_s = step((outputs, dq_s, dk_s, dv_s), up, down)
+    outputs, dq_s, dk_s, dv_s = step((outputs, dq_s, dk_s, dv_s), cross, up, down)
     state_back = dot_nt(dk_c, w_ck) + dot_nt(dv_c, w_cv)
-    attn = gradient(0, *[(x, x_sib, v, w) for v, w in zip((dq_s, dk_s, dv_s), sibs)])
+    attn = gradient(0, ((x, x_sib), *zip((dq_s, dk_s, dv_s), sibs)))
     dq_s, dk_s, dv_s = step((dq_s, dk_s, dv_s), attn, cross, up)
     back = d_one + dot_nt(dq_s, w_sq) + dot_nt(dk_s, w_sk) + dot_nt(dv_s, w_sv)
-    (back,) = step((back,), attn, cross)
+    (back,) = step((back,), attn)
+    step((), cross)
     input_grad = halved(back.astype(bf16))
     encoded_grad = halved(state_back.astype(bf16))
-    step((), attn, cross)
+    step((), attn)
     step((), attn, cross)
     natural = [f.finish() for f in (attn, cross, up, down)]
     mine, other, flag = last_pieces(net, jnp.concatenate(natural), block_slots)

time: 749 us -> 685 us (0.915)
  waiting for transfers between devices: 230 us -> 201 us
  Pallas kernels: 208 us -> 183 us
  starting transfers between devices: 116 us -> 102 us
    ppermute x32, waiting for transfers between devices: 148 us -> 109 us  [swap_data(): return lax.ppermute(value, ('rep', 'shard', 'mp'), pairs)]
    pallas_call x14 -> x11, Pallas kernels: 113 us -> 87.3 us  [the longest x7 49.3 us: weight_grad(): pl.pallas_call(functools.partial(weight_grad_body, count=count, outs=outs...]
    ppermute x31, starting transfers between devices: 35.5 us -> 18.7 us  [swap_core(): return lax.ppermute(value, 'mp', [(i, i ^ 1) for i in range(self.n_mp)])]
    all_to_all x2, waiting for transfers between devices: 0.01 us -> 16.3 us  [route_home(): lax.all_to_all(moved, ('rep', 'shard'), split_axis=0, concat_axis=1, tile...]
    all_to_all x2 -> x1, waiting for transfers between devices: 31.5 us -> 27 us  [first_pieces(): lax.all_to_all(cut.reshape(-1, net.rows, BS), 'shard', split_axis=0, conc...]
    unnamed x270 -> x198, local copies, waits for them, and re-layouts: 17.5 us -> 14.5 us
  transfers between devices with their start and end apart: 73 -> 72, of which waited for: 25 -> 30; matrix products, arithmetic and copies ran while one was open for 22% -> 24% of each run, Pallas kernels for 25% -> 24%
where the time goes in v3:
time: 685 us; the launch traced here: 673 us
  waiting for transfers between devices  201 us (29%)
  Pallas kernels  183 us (27%)
  starting transfers between devices  102 us (15%)
  other arithmetic  75.6 us (11%)
  matrix products  67.7 us (10%)
  local copies, waits for them, and re-layouts  41.5 us (6%)
    ppermute x32, waiting for transfers between devices, swap_data(): return lax.ppermute(value, ('rep', 'shard', 'mp'), pairs)  109 us
    pallas_call x7, Pallas kernels, weight_grad(): pl.pallas_call(functools.partial(weight_grad_body, count=count, outs=outs...  49.3 us
    ppermute x32, starting transfers between devices, swap_data(): return lax.ppermute(value, ('rep', 'shard', 'mp'), pairs)  43.7 us
    dot_general x10, matrix products, dot_nt(): return lax.dot_general(a, b, NT, preferred_element_type=f32)  39.4 us
    pallas_call x4, Pallas kernels, place(): pl.pallas_call(functools.partial(place_body, dests=dests, many=many, two=...  37.9 us
    pallas_call x2, Pallas kernels, attend_forward(): pl.pallas_call(functools.partial(attend_forward_body, causal=causal, rows...  29.1 us
    dot_general x9, matrix products, dot_nn(): return jnp.dot(a, b, preferred_element_type=f32)  28.3 us
    all_to_all x1, waiting for transfers between devices, first_pieces(): lax.all_to_all(cut.reshape(-1, net.rows, BS), 'shard', split_axis=0, conc...  27 us
  transfers between devices with their start and end apart: 72, of which 30 were waited for; matrix products, arithmetic and copies ran while one was open for 24% of the time, Pallas kernels for 24%

profile of v3, /device:TPU:0, one launch (start us, length us, event | category | flops | bytes accessed | tf_op | source)
XLA Modules:
  0.0 673.2 jit_solution(11923976104112896110)
XLA Ops:
  1.4 2.4 convert_element_type.349
  5.2 7.3 %all-to-all-start = ((bf16[136,16,256]{2,1,0:T(8,128)(2,1)}), bf16[136,16,256]{2,1,0:T(8,128)(2,1)S(1)}, u32[]{:S(2)}, u32[]{:S(2)}) async-start(bf16[136,16,256]{2,1,0:T(8,128)(2,1)} %bitcast.4), calls=%async_computation | async-start | bytes 2228224 | tf_op jit(solution)/shard_map/all_to_all | solution.py:269
  12.6 27.0 %all-to-all-done = bf16[136,16,256]{2,1,0:T(8,128)(2,1)S(1)} async-done(((bf16[136,16,256]{2,1,0:T(8,128)(2,1)}), bf16[136,16,256]{2,1,0:T(8,128)(2,1)S(1)}, u32[]{:S(2)}, u32[]{:S(2)}) %all-to-all-start) | async-done | bytes 1114144 | tf_op jit(solution)/shard_map/all_to_all | solution.py:269
  40.4 10.6 %collective-permute-done.2 = bf16[1,24,16,256]{3,2,1,0:T(8,128)(2,1)S(1)} collective-permute-done((bf16[1,24,16,256]{3,2,1,0:T(8,128)(2,1)S(1)}, bf16[1,24,16,256]{3,2,1,0:T(8,128)(2,1)S(1)}, u32[]{:S(2)}, u32[]{:S(2)}) %collective-permute-start.2) | collective-permute-done | bytes 196640 | tf_op jit(solution)/shard_map/ppermute | solution.py:103
  52.7 6.3 collective-permute-done.3
  62.2 14.0 %collective-permute-done.5 = bf16[1,40,16,256]{3,2,1,0:T(8,128)(2,1)S(1)} collective-permute-done((bf16[1,40,16,256]{3,2,1,0:T(8,128)(2,1)S(1)}, bf16[1,40,16,256]{3,2,1,0:T(8,128)(2,1)S(1)}, u32[]{:S(2)}, u32[]{:S(2)}) %collective-permute-start.5) | collective-permute-done | bytes 327712 | tf_op jit(solution)/shard_map/ppermute | solution.py:103
  93.2 9.8 %collective-permute-done.8 = bf16[2,40,16,256]{3,2,1,0:T(8,128)(2,1)} collective-permute-done((bf16[2,40,16,256]{3,2,1,0:T(8,128)(2,1)}, bf16[2,40,16,256]{3,2,1,0:T(8,128)(2,1)}, u32[]{:S(2)}, u32[]{:S(2)}) %collective-permute-start.8) | collective-permute-done | bytes 655392 | tf_op jit(solution)/shard_map/ppermute | solution.py:103
  104.0 2.4 pad_maximum_fusion.4
  109.1 8.5 %place.4 = (bf16[4,256,1024]{2,1,0:T(8,128)(2,1)}, bf16[4,256,1024]{2,1,0:T(8,128)(2,1)}, bf16[4,256,1024]{2,1,0:T(8,128)(2,1)}) custom-call(s32[41]{0:T(128)} %add_add_fusion.4.s, bf16[8,24,16,256]{3,2,1,0:T(8,128)(2,1)} %copy-done.13, bf16[8,24,16,256]{3,2,1,0:T(8,128)(2,1)} %collective-permute-done.6.refs_1_, ...), custom_call_target="tpu_custom_call" | custom-call | flops 1048576 | bytes 1048576 | tf_op jit(solution)/shard_map/place/pallas_call | solution.py:225
  119.3 4.0 add_convert_fusion.8.q_ref
  137.2 20.1 %attend_forward.2 = (bf16[512,1024]{1,0:T(8,128)(2,1)}, f32[512,128]{1,0:T(8,128)}) custom-call(s32[1]{0:T(128)} %dynamic_slice.76.lim, bf16[512,1024]{1,0:T(8,128)(2,1)} %add_convert_fusion.8.q_ref, bf16[512,1024]{1,0:T(8,128)(2,1)} %convolution_convert_fusion.2.k_ref, bf16[512,1024]{1,0:T(8,128)(2,1)} %add_convert_fusion.7.v_ref), custom_call_target="tpu_custom_call" | custom-call | flops 1048576 | bytes 1048576 | tf_op jit(solution)/shard_map/attend_forward/pallas_call | solution.py:354
  160.6 3.8 collective-permute-done.17
  166.1 3.0 pad_maximum_fusion.1.refs_0_
  171.7 5.6 all-to-all-start.1
  181.1 10.3 %place.5 = (bf16[4,256,1024]{2,1,0:T(8,128)(2,1)}, bf16[4,256,1024]{2,1,0:T(8,128)(2,1)}, bf16[4,256,1024]{2,1,0:T(8,128)(2,1)}, bf16[4,256,1024]{2,1,0:T(8,128)(2,1)}, bf16[4,256,1024]{2,1,0:T(8,128)(2,1)}) custom-call(s32[41]{0:T(128)} %add_add_fusion.5.s, bf16[8,40,16,256]{3,2,1,0:T(8,128)(2,1)} %copy-done.5, ...), custom_call_target="tpu_custom_call" | custom-call | flops 1048576 | bytes 1048576 | tf_op jit(solution)/shard_map/place/pallas_call | solution.py:225
  191.3 3.5 fusion.21
  206.8 9.0 %attend_forward.3 = (bf16[512,1024]{1,0:T(8,128)(2,1)}, f32[512,128]{1,0:T(8,128)}) custom-call(s32[1]{0:T(128)} %dynamic_slice.76.lim, bf16[512,1024]{1,0:T(8,128)(2,1)} %add_convert_fusion.6.q_ref, bf16[128,1024]{1,0:T(8,128)(2,1)} %convolution_convert_fusion.3.k_ref, bf16[128,1024]{1,0:T(8,128)(2,1)} %fusion.4.v_ref), custom_call_target="tpu_custom_call" | custom-call | flops 1048576 | bytes 1048576 | tf_op jit(solution)/shard_map/attend_forward/pallas_call | solution.py:354
  215.8 3.4 fusion.23
  223.6 2.9 pad_maximum_fusion.2.refs_0_
  230.4 5.2 all-to-all-start.2
  236.9 9.6 %place.6 = bf16[4,256,4096]{2,1,0:T(8,128)(2,1)} custom-call(s32[41]{0:T(128)} %add_add_fusion.6.s, bf16[8,32,16,256]{3,2,1,0:T(8,128)(2,1)} %pad_maximum_fusion.1.refs_0_, bf16[8,32,16,256]{3,2,1,0:T(8,128)(2,1)} %collective-permute-done.20.refs_1_, bf16[8,32,16,256]{3,2,1,0:T(8,128)(2,1)} %collective-permute-done.21.refs_2_, ...), custom_call_target="tpu_custom_call" | custom-call | flops 1048576 | bytes 1048576 | tf_op jit(solution)/shard_map/place/pallas_call | solution.py:225
  246.5 19.1 %gelu_forward.1 = (bf16[512,4096]{1,0:T(8,128)(2,1)}, bf16[512,4096]{1,0:T(8,128)(2,1)}) custom-call(bf16[512,1024]{1,0:T(8,128)(2,1)} %get-tuple-element.177.h_ref.x_own, bf16[1024,4096]{1,0:T(8,128)(2,1)} %bitcast.219, f32[1,4096]{1,0:T(1,128)} %bitcast.263), custom_call_target="tpu_custom_call" | custom-call | flops 1048576 | bytes 1048576 | tf_op jit(solution)/shard_map/gelu_forward/pallas_call | solution.py:487
  265.9 6.2 all-to-all-done.2
  275.1 9.6 %place.7 = bf16[16,256,1024]{2,1,0:T(8,128)(2,1)} custom-call(s32[41]{0:T(128)} %add_add_fusion.7.s, bf16[8,32,16,256]{3,2,1,0:T(8,128)(2,1)} %pad_maximum_fusion.2.refs_0_, bf16[8,32,16,256]{3,2,1,0:T(8,128)(2,1)} %collective-permute-done.24.refs_1_, bf16[8,32,16,256]{3,2,1,0:T(8,128)(2,1)} %collective-permute-done.25.refs_2_, ...), custom_call_target="tpu_custom_call" | custom-call | flops 1048576 | bytes 1048576 | tf_op jit(solution)/shard_map/place/pallas_call | solution.py:225
  284.7 8.3 %fusion.24 = f32[512,1024]{1,0:T(8,128)S(1)} fusion(bf16[512,4096]{1,0:T(8,128)(2,1)} %get-tuple-element.183.x_own, bf16[4096,1024]{1,0:T(8,128)(2,1)} %bitcast.222), kind=kOutput, calls=%fused_computation.224 | convolution fusion | flops 4294967296 | bytes 14680064 | tf_op jit(solution)/shard_map/dot_general | solution.py:43
  298.2 8.1 %multiply_convert_fusion.refs_0_ = bf16[512,4096]{1,0:T(8,128)(2,1)} fusion(bf16[512,4096]{1,0:T(8,128)(2,1)} %get-tuple-element.187, bf16[512,1024]{1,0:T(8,128)(2,1)S(1)} %convert_element_type.365.refs_0_, bf16[4096,1024]{1,0:T(8,128)(2,1)S(1)} %bitcast.225), kind=kOutput, calls=%fused_computation.5 | convolution fusion | flops 4301258752 | bytes 17825792 | tf_op jit(solution)/shard_map/dot_general | solution.py:47
  310.9 6.6 collective-permute-done.27
  320.2 11.0 %weight_grad.7 = (bf16[8,1,32,16,256]{4,3,2,1,0:T(8,128)(2,1)}, bf16[8,1,32,16,256]{4,3,2,1,0:T(8,128)(2,1)}) custom-call(s32[41]{0:T(128)} %add_add_fusion.7.s, bf16[512,4096]{1,0:T(8,128)(2,1)} %get-tuple-element.183.x_own, bf16[512,4096]{1,0:T(8,128)(2,1)} %collective-permute-done.30.x_sib, bf16[512,1024]{1,0:T(8,128)(2,1)} %copy-done.28, ...), custom_call_target="tpu_custom_call" | custom-call | flops 1048576 | bytes 1048576 | tf_op jit(solution)/shard_map/weight_grad/pallas_call | solution.py:544
  333.5 4.5 all-to-all-start.3
  338.1 9.6 %weight_grad.8 = (bf16[8,1,32,16,256]{4,3,2,1,0:T(8,128)(2,1)}, bf16[8,1,32,16,256]{4,3,2,1,0:T(8,128)(2,1)}) custom-call(s32[41]{0:T(128)} %add_add_fusion.6.s, bf16[512,1024]{1,0:T(8,128)(2,1)} %get-tuple-element.177.h_ref.x_own, bf16[512,1024]{1,0:T(8,128)(2,1)} %collective-permute-done.32.x_sib, bf16[512,4096]{1,0:T(8,128)(2,1)} %multiply_convert_fusion.refs_0_, ...), custom_call_target="tpu_custom_call" | custom-call | flops 1048576 | bytes 1048576 | tf_op jit(solution)/shard_map/weight_grad/pallas_call | solution.py:544
  351.1 11.1 %multiply_reduce_fusion.1 = (f32[1024]{0:T(1024)S(1)}, f32[512]{0:T(512)S(1)}, f32[512]{0:T(512)S(1)}, f32[1024]{0:T(1024)S(1)}, f32[512,1024]{1,0:T(8,128)S(1)}) fusion(f32[512,1024]{1,0:T(8,128)} %copy-done.3, f32[512]{0:T(512)S(1)} %add_rsqrt_fusion.1, f32[512]{0:T(512)S(1)} %broadcast_multiply_fusion.7, f32[1024]{0:T(1024)S(1)} %bitcast.271, ...), kind=kOutput, calls=%fused_computation.12 | convolution fusion | flops 4300207104 | bytes 18894848 | tf_op jit(solution)/shard_map/dot_general | solution.py:47
  367.6 13.5 %collective-permute-done.33 = bf16[8,32,16,256]{3,2,1,0:T(8,128)(2,1)} collective-permute-done((bf16[8,32,16,256]{3,2,1,0:T(8,128)(2,1)}, bf16[8,32,16,256]{3,2,1,0:T(8,128)(2,1)}, u32[]{:S(2)}, u32[]{:S(2)}) %collective-permute-start.33) | collective-permute-done | bytes 2097184 | tf_op jit(solution)/shard_map/ppermute | solution.py:103
  381.1 10.6 %attend_backward.2 = (bf16[512,1024]{1,0:T(8,128)(2,1)}, bf16[128,1024]{1,0:T(8,128)(2,1)}, bf16[128,1024]{1,0:T(8,128)(2,1)}) custom-call(s32[1]{0:T(128)} %dynamic_slice.76.lim, bf16[512,1024]{1,0:T(8,128)(2,1)} %add_convert_fusion.6.q_ref, bf16[128,1024]{1,0:T(8,128)(2,1)} %convolution_convert_fusion.3.k_ref, bf16[128,1024]{1,0:T(8,128)(2,1)} %fusion.4.v_ref, ...), custom_call_target="tpu_custom_call" | custom-call | flops 1048576 | bytes 1048576 | tf_op jit(solution)/shard_map/attend_backward/pallas_call | solution.py:437
  391.7 4.4 multiply_reduce_fusion.2
  398.4 10.1 %collective-permute-start.35 = (bf16[512,1024]{1,0:T(8,128)(2,1)S(1)}, bf16[512,1024]{1,0:T(8,128)(2,1)S(1)}, u32[]{:S(2)}, u32[]{:S(2)}) collective-permute-start(bf16[512,1024]{1,0:T(8,128)(2,1)S(1)} %convert_element_type.370.refs_0_), channel_id=1, source_target_pairs={{0,1},{1,0},{2,3},{3,2},{4,5},{5,4},{6,7},{7,6},{8,9},{9,8},{10,11... | collective-permute-start | bytes 3145736 | tf_op jit(solution)/shard_map/ppermute | solution.py:92
  414.4 3.6 add_convert_fusion.2
  418.6 7.0 %collective-permute-done.36 = bf16[4,32,16,256]{3,2,1,0:T(8,128)(2,1)S(1)} collective-permute-done((bf16[4,32,16,256]{3,2,1,0:T(8,128)(2,1)S(1)}, bf16[4,32,16,256]{3,2,1,0:T(8,128)(2,1)S(1)}, u32[]{:S(2)}, u32[]{:S(2)}) %collective-permute-start.36) | collective-permute-done | bytes 1048608 | tf_op jit(solution)/shard_map/ppermute | solution.py:103
  425.6 2.4 collective-permute-start.44
  434.2 4.8 weight_grad.9
  439.0 5.5 weight_grad.10
  445.2 5.3 weight_grad.11
  450.6 4.8 weight_grad.12
  456.5 2.9 gather_fusion.2
  459.4 5.3 all-to-all-start.4
  469.2 2.4 collective-permute-start.48
  471.6 16.4 %attend_backward.3 = (bf16[512,1024]{1,0:T(8,128)(2,1)}, bf16[512,1024]{1,0:T(8,128)(2,1)}, bf16[512,1024]{1,0:T(8,128)(2,1)}) custom-call(s32[1]{0:T(128)} %dynamic_slice.76.lim, bf16[512,1024]{1,0:T(8,128)(2,1)} %add_convert_fusion.8.q_ref, bf16[512,1024]{1,0:T(8,128)(2,1)} %convolution_convert_fusion.2.k_ref, bf16[512,1024]{1,0:T(8,128)(2,1)} %add_convert_fusion.7.v_ref, ...), custom_call_target="tpu_custom_call" | custom-call | flops 1048576 | bytes 1048576 | tf_op jit(solution)/shard_map/attend_backward/pallas_call | solution.py:437
  488.6 10.1 %all-to-all-done.4 = bf16[32,1,32,512]{3,2,1,0:T(8,128)(2,1)} async-done(((bf16[32,1,32,512]{3,2,1,0:T(8,128)(2,1)}), bf16[32,1,32,512]{3,2,1,0:T(8,128)(2,1)}, u32[]{:S(2)}, u32[]{:S(2)}) %all-to-all-start.4) | async-done | bytes 1048608 | tf_op jit(solution)/shard_map/all_to_all | solution.py:636
  504.3 3.9 add_convert_fusion
  509.4 3.3 convert_reduce_fusion
  515.4 8.3 %weight_grad.13 = (bf16[8,3,8,16,256]{4,3,2,1,0:T(8,128)(2,1)}, bf16[8,3,8,16,256]{4,3,2,1,0:T(8,128)(2,1)}) custom-call(s32[41]{0:T(128)} %add_add_fusion.4.s, bf16[512,1024]{1,0:T(8,128)(2,1)} %get-tuple-element.138.x_own, bf16[512,1024]{1,0:T(8,128)(2,1)} %get-tuple-element.236.x_sib, bf16[512,1024]{1,0:T(8,128)(2,1)} %get-tuple-element.242.refs_0_, ...), custom_call_target="tpu_custom_call" | custom-call | flops 1048576 | bytes 1048576 | tf_op jit(solution)/shard_map/weight_grad/pallas_call | solution.py:544
  528.6 2.5 add_convert_fusion.12
  533.3 3.0 fusion.25
  538.5 3.6 add_add_fusion
  542.2 6.2 collective-permute-done.54
  552.1 3.1 collective-permute-start.60
  555.2 17.5 %collective-permute-done.57 = bf16[4,24,16,256]{3,2,1,0:T(8,128)(2,1)S(1)} collective-permute-done((bf16[4,24,16,256]{3,2,1,0:T(8,128)(2,1)S(1)}, bf16[4,24,16,256]{3,2,1,0:T(8,128)(2,1)S(1)}, u32[]{:S(2)}, u32[]{:S(2)}) %collective-permute-start.57) | collective-permute-done | bytes 786464 | tf_op jit(solution)/shard_map/ppermute | solution.py:103
  577.3 4.5 all-to-all-start.6
  581.9 3.0 collective-permute-start.61
  586.1 8.7 %collective-permute-done.61 = bf16[1,24,16,256]{3,2,1,0:T(8,128)(2,1)S(1)} collective-permute-done((bf16[1,24,16,256]{3,2,1,0:T(8,128)(2,1)S(1)}, bf16[1,24,16,256]{3,2,1,0:T(8,128)(2,1)S(1)}, u32[]{:S(2)}, u32[]{:S(2)}) %collective-permute-start.61) | collective-permute-done | bytes 196640 | tf_op jit(solution)/shard_map/ppermute | solution.py:103
  596.6 5.1 all-to-all-start.5
  601.7 2.5 fusion.27
  607.7 20.0 %all-to-all-done.5 = bf16[128,16,256]{2,1,0:T(8,128)(2,1)S(1)} async-done(((bf16[128,16,256]{2,1,0:T(8,128)(2,1)}), bf16[128,16,256]{2,1,0:T(8,128)(2,1)S(1)}, u32[]{:S(2)}, u32[]{:S(2)}) %all-to-all-start.5) | async-done | bytes 1048608 | tf_op jit(solution)/shard_map/all_to_all | solution.py:308
  633.0 18.6 %collective-permute-done.62.other_ref = bf16[8,16,16,256]{3,2,1,0:T(8,128)(2,1)S(1)} collective-permute-done((bf16[8,16,16,256]{3,2,1,0:T(8,128)(2,1)S(1)}, bf16[8,16,16,256]{3,2,1,0:T(8,128)(2,1)S(1)}, u32[]{:S(2)}, u32[]{:S(2)}) %collective-permute-start.62) | collective-permute-done | bytes 1048608 | tf_op jit(solution)/shard_map/ppermute | solution.py:95
  652.6 20.3 %shampoo.1 = (f32[1,16,256,256]{3,2,1,0:T(8,128)}, f32[1,16,256,256]{3,2,1,0:T(8,128)}, f32[1,16,256,256]{3,2,1,0:T(8,128)}, f32[1,16,256,256]{3,2,1,0:T(8,128)}) custom-call(s32[1]{0:T(128)} %bitcast.79.flag, bf16[8,16,16,256]{3,2,1,0:T(8,128)(2,1)} %bitcast.236, bf16[8,16,16,256]{3,2,1,0:T(8,128)(2,1)} %copy-done.58, f32[1,16,256,256]{3,2,1,0:T(8,128)} %w_ref.1, ...), custom_call_target="tpu_custom_call" | custom-call | flops 1048576 | bytes 1048576 | tf_op jit(solution)/shard_map/shampoo/pallas_call | solution.py:594
  (466 shorter events, 164.9 us)
Async XLA Ops:
  5.2 34.5 %all-to-all-start = ((bf16[136,16,256]{2,1,0:T(8,128)(2,1)}), bf16[136,16,256]{2,1,0:T(8,128)(2,1)S(1)}, u32[]{:S(2)}, u32[]{:S(2)}) async-start(bf16[136,16,256]{2,1,0:T(8,128)(2,1)} %bitcast.4), calls=%async_computation | async-start | bytes 2228224 | tf_op jit(solution)/shard_map/all_to_all | solution.py:269
  40.3 10.7 %collective-permute-start.2 = (bf16[1,24,16,256]{3,2,1,0:T(8,128)(2,1)S(1)}, bf16[1,24,16,256]{3,2,1,0:T(8,128)(2,1)S(1)}, u32[]{:S(2)}, u32[]{:S(2)}) collective-permute-start(bf16[1,24,16,256]{3,2,1,0:T(8,128)(2,1)S(1)} %bitcast.250), channel_id=1, source_target_pairs={{0,8},{1,9},{2,10},{3,11},{4,12},{5,13},{6,14},{7,15},{8,0},{9,1},... | collective-permute-start | bytes 589832 | tf_op jit(solution)/shard_map/ppermute | solution.py:103
  59.9 19.3 %collective-permute-start.4 = (bf16[4,24,16,256]{3,2,1,0:T(8,128)(2,1)}, bf16[4,24,16,256]{3,2,1,0:T(8,128)(2,1)}, u32[]{:S(2)}, u32[]{:S(2)}) collective-permute-start(bf16[4,24,16,256]{3,2,1,0:T(8,128)(2,1)} %pad_maximum_fusion.14), channel_id=1, source_target_pairs={{0,4},{1,3},{2,6},{3,1},{4,0},{5,7},{6,2},{7,5},{8,12},{9,11},{10,... | collective-permute-start | bytes 2359304 | tf_op jit(solution)/shard_map/ppermute | solution.py:103
  59.9 16.3 %collective-permute-start.5 = (bf16[1,40,16,256]{3,2,1,0:T(8,128)(2,1)S(1)}, bf16[1,40,16,256]{3,2,1,0:T(8,128)(2,1)S(1)}, u32[]{:S(2)}, u32[]{:S(2)}) collective-permute-start(bf16[1,40,16,256]{3,2,1,0:T(8,128)(2,1)S(1)} %bitcast.230), channel_id=1, source_target_pairs={{0,8},{1,9},{2,10},{3,11},{4,12},{5,13},{6,14},{7,15},{8,0},{9,1},... | collective-permute-start | bytes 983048 | tf_op jit(solution)/shard_map/ppermute | solution.py:103
  61.7 23.8 %collective-permute-start = (bf16[2,512,512]{2,1,0:T(8,128)(2,1)}, bf16[2,512,512]{2,1,0:T(8,128)(2,1)}, u32[]{:S(2)}, u32[]{:S(2)}) collective-permute-start(bf16[2,512,512]{2,1,0:T(8,128)(2,1)} %param.17), channel_id=1, source_target_pairs={{0,1},{1,0},{2,3},{3,2},{4,5},{5,4},{6,7},{7,6},{8,9},{9,8},{10,11... | collective-permute-start | bytes 3145736 | tf_op jit(solution)/shard_map/ppermute | solution.py:92
  61.7 21.0 %collective-permute-start.1 = (bf16[2,128,512]{2,1,0:T(8,128)(2,1)}, bf16[2,128,512]{2,1,0:T(8,128)(2,1)}, u32[]{:S(2)}, u32[]{:S(2)}) collective-permute-start(bf16[2,128,512]{2,1,0:T(8,128)(2,1)} %param.18), channel_id=1, source_target_pairs={{0,1},{1,0},{2,3},{3,2},{4,5},{5,4},{6,7},{7,6},{8,9},{9,8},{10,11... | collective-permute-start | bytes 786440 | tf_op jit(solution)/shard_map/ppermute | solution.py:92
  80.7 22.3 %collective-permute-start.6 = (bf16[8,24,16,256]{3,2,1,0:T(8,128)(2,1)S(1)}, bf16[8,24,16,256]{3,2,1,0:T(8,128)(2,1)}, u32[]{:S(2)}, u32[]{:S(2)}) collective-permute-start(bf16[8,24,16,256]{3,2,1,0:T(8,128)(2,1)S(1)} %pad_maximum_fusion.3.refs_0_), channel_id=1, source_target_pairs={{0,2},{1,17},{2,0},{3,19},{4,6},{5,21},{6,4},{7,23},{8,10},{9,25},... | collective-permute-start | bytes 4718600 | tf_op jit(solution)/shard_map/ppermute | solution.py:103
  82.0 20.9 %collective-permute-start.7 = (bf16[8,24,16,256]{3,2,1,0:T(8,128)(2,1)S(1)}, bf16[8,24,16,256]{3,2,1,0:T(8,128)(2,1)}, u32[]{:S(2)}, u32[]{:S(2)}) collective-permute-start(bf16[8,24,16,256]{3,2,1,0:T(8,128)(2,1)S(1)} %pad_maximum_fusion.3.refs_0_), channel_id=1, source_target_pairs={{0,1},{1,0},{2,3},{3,2},{4,5},{5,4},{6,7},{7,6},{8,9},{9,8},{10,11... | collective-permute-start | bytes 4718600 | tf_op jit(solution)/shard_map/ppermute | solution.py:92
  85.5 17.5 %collective-permute-start.8 = (bf16[2,40,16,256]{3,2,1,0:T(8,128)(2,1)}, bf16[2,40,16,256]{3,2,1,0:T(8,128)(2,1)}, u32[]{:S(2)}, u32[]{:S(2)}) collective-permute-start(bf16[2,40,16,256]{3,2,1,0:T(8,128)(2,1)} %pad_maximum_fusion.15), channel_id=1, source_target_pairs={{0,4},{1,5},{2,6},{3,7},{4,0},{5,1},{6,2},{7,3},{8,12},{9,13},{10,... | collective-permute-start | bytes 1966088 | tf_op jit(solution)/shard_map/ppermute | solution.py:103
  103.5 14.5 %collective-permute-start.10 = (bf16[1,32,16,256]{3,2,1,0:T(8,128)(2,1)S(1)}, bf16[1,32,16,256]{3,2,1,0:T(8,128)(2,1)S(1)}, u32[]{:S(2)}, u32[]{:S(2)}) collective-permute-start(bf16[1,32,16,256]{3,2,1,0:T(8,128)(2,1)S(1)} %bitcast.246), channel_id=1, source_target_pairs={{0,8},{1,9},{2,10},{3,11},{4,12},{5,13},{6,14},{7,15},{8,0},{9,1},... | collective-permute-start | bytes 786440 | tf_op jit(solution)/shard_map/ppermute | solution.py:103
  106.3 21.5 %collective-permute-start.12 = (bf16[4,40,16,256]{3,2,1,0:T(8,128)(2,1)}, bf16[4,40,16,256]{3,2,1,0:T(8,128)(2,1)}, u32[]{:S(2)}, u32[]{:S(2)}) collective-permute-start(bf16[4,40,16,256]{3,2,1,0:T(8,128)(2,1)} %pad_maximum_fusion.4), channel_id=1, source_target_pairs={{0,16},{1,3},{2,18},{3,1},{4,20},{5,7},{6,22},{7,5},{8,24},{9,11},... | collective-permute-start | bytes 3932168 | tf_op jit(solution)/shard_map/ppermute | solution.py:103
  118.1 10.5 %collective-permute-start.13 = (bf16[2,32,16,256]{3,2,1,0:T(8,128)(2,1)S(1)}, bf16[2,32,16,256]{3,2,1,0:T(8,128)(2,1)S(1)}, u32[]{:S(2)}, u32[]{:S(2)}) collective-permute-start(bf16[2,32,16,256]{3,2,1,0:T(8,128)(2,1)S(1)} %pad_maximum_fusion.16), channel_id=1, source_target_pairs={{0,2},{1,17},{2,0},{3,19},{4,6},{5,21},{6,4},{7,23},{8,10},{9,25},... | collective-permute-start | bytes 1572872 | tf_op jit(solution)/shard_map/ppermute | solution.py:103
  130.4 34.8 %collective-permute-start.14 = (bf16[8,40,16,256]{3,2,1,0:T(8,128)(2,1)S(1)}, bf16[8,40,16,256]{3,2,1,0:T(8,128)(2,1)}, u32[]{:S(2)}, u32[]{:S(2)}) collective-permute-start(bf16[8,40,16,256]{3,2,1,0:T(8,128)(2,1)S(1)} %pad_maximum_fusion.refs_0_), channel_id=1, source_target_pairs={{0,2},{1,17},{2,0},{3,19},{4,6},{5,21},{6,4},{7,23},{8,10},{9,25},... | collective-permute-start | bytes 7864328 | tf_op jit(solution)/shard_map/ppermute | solution.py:103
  131.9 33.3 %collective-permute-start.15 = (bf16[8,40,16,256]{3,2,1,0:T(8,128)(2,1)S(1)}, bf16[8,40,16,256]{3,2,1,0:T(8,128)(2,1)}, u32[]{:S(2)}, u32[]{:S(2)}) collective-permute-start(bf16[8,40,16,256]{3,2,1,0:T(8,128)(2,1)S(1)} %pad_maximum_fusion.refs_0_), channel_id=1, source_target_pairs={{0,1},{1,0},{2,3},{3,2},{4,5},{5,4},{6,7},{7,6},{8,9},{9,8},{10,11... | collective-permute-start | bytes 7864328 | tf_op jit(solution)/shard_map/ppermute | solution.py:92
  133.8 31.4 %collective-permute-start.16 = (bf16[4,32,16,256]{3,2,1,0:T(8,128)(2,1)}, bf16[4,32,16,256]{3,2,1,0:T(8,128)(2,1)}, u32[]{:S(2)}, u32[]{:S(2)}) collective-permute-start(bf16[4,32,16,256]{3,2,1,0:T(8,128)(2,1)} %pad_maximum_fusion.8), channel_id=1, source_target_pairs={{0,4},{1,5},{2,6},{3,7},{4,0},{5,1},{6,2},{7,3},{8,12},{9,13},{10,... | collective-permute-start | bytes 3145736 | tf_op jit(solution)/shard_map/ppermute | solution.py:103
  136.0 28.4 %collective-permute-start.17 = (bf16[1,32,16,256]{3,2,1,0:T(8,128)(2,1)S(1)}, bf16[1,32,16,256]{3,2,1,0:T(8,128)(2,1)}, u32[]{:S(2)}, u32[]{:S(2)}) collective-permute-start(bf16[1,32,16,256]{3,2,1,0:T(8,128)(2,1)S(1)} %bitcast.242), channel_id=1, source_target_pairs={{0,8},{1,9},{2,10},{3,11},{4,12},{5,13},{6,14},{7,15},{8,0},{9,1},... | collective-permute-start | bytes 786440 | tf_op jit(solution)/shard_map/ppermute | solution.py:103
  165.2 15.8 %collective-permute-start.18 = (bf16[8,40,16,256]{3,2,1,0:T(8,128)(2,1)}, bf16[8,40,16,256]{3,2,1,0:T(8,128)(2,1)}, u32[]{:S(2)}, u32[]{:S(2)}) collective-permute-start(bf16[8,40,16,256]{3,2,1,0:T(8,128)(2,1)} %collective-permute-done.14.refs_1_), channel_id=1, source_target_pairs={{0,1},{1,0},{2,3},{3,2},{4,5},{5,4},{6,7},{7,6},{8,9},{9,8},{10,11... | collective-permute-start | bytes 7864328 | tf_op jit(solution)/shard_map/ppermute | solution.py:92
  169.2 53.5 %collective-permute-start.20 = (bf16[8,32,16,256]{3,2,1,0:T(8,128)(2,1)}, bf16[8,32,16,256]{3,2,1,0:T(8,128)(2,1)}, u32[]{:S(2)}, u32[]{:S(2)}) collective-permute-start(bf16[8,32,16,256]{3,2,1,0:T(8,128)(2,1)} %pad_maximum_fusion.1.refs_0_), channel_id=1, source_target_pairs={{0,16},{1,3},{2,18},{3,1},{4,20},{5,7},{6,22},{7,5},{8,24},{9,11},... | collective-permute-start | bytes 6291464 | tf_op jit(solution)/shard_map/ppermute | solution.py:103
  170.1 52.6 %collective-permute-start.21 = (bf16[8,32,16,256]{3,2,1,0:T(8,128)(2,1)}, bf16[8,32,16,256]{3,2,1,0:T(8,128)(2,1)}, u32[]{:S(2)}, u32[]{:S(2)}) collective-permute-start(bf16[8,32,16,256]{3,2,1,0:T(8,128)(2,1)} %pad_maximum_fusion.1.refs_0_), channel_id=1, source_target_pairs={{0,1},{1,0},{2,3},{3,2},{4,5},{5,4},{6,7},{7,6},{8,9},{9,8},{10,11... | collective-permute-start | bytes 6291464 | tf_op jit(solution)/shard_map/ppermute | solution.py:92
  171.7 51.0 %all-to-all-start.1 = ((bf16[2,16,32,512]{3,2,0,1:T(8,128)(2,1)}), bf16[2,16,32,512]{3,2,0,1:T(8,128)(2,1)S(1)}, u32[]{:S(2)}, u32[]{:S(2)}) async-start(bf16[2,16,32,512]{3,2,0,1:T(8,128)(2,1)} %copy.67), calls=%async_computation.1 | async-start | bytes 2097152 | tf_op jit(solution)/shard_map/all_to_all | solution.py:631
  179.1 24.0 %collective-permute-start.19 = (bf16[2,32,16,256]{3,2,1,0:T(8,128)(2,1)}, bf16[2,32,16,256]{3,2,1,0:T(8,128)(2,1)S(1)}, u32[]{:S(2)}, u32[]{:S(2)}) collective-permute-start(bf16[2,32,16,256]{3,2,1,0:T(8,128)(2,1)} %pad_maximum_fusion.17), channel_id=1, source_target_pairs={{0,2},{1,17},{2,0},{3,19},{4,6},{5,21},{6,4},{7,23},{8,10},{9,25},... | collective-permute-start | bytes 1572872 | tf_op jit(solution)/shard_map/ppermute | solution.py:103
  205.3 18.3 %collective-permute-start.22 = (bf16[4,32,16,256]{3,2,1,0:T(8,128)(2,1)}, bf16[4,32,16,256]{3,2,1,0:T(8,128)(2,1)}, u32[]{:S(2)}, u32[]{:S(2)}) collective-permute-start(bf16[4,32,16,256]{3,2,1,0:T(8,128)(2,1)} %pad_maximum_fusion.9), channel_id=1, source_target_pairs={{0,16},{1,5},{2,18},{3,7},{4,20},{5,1},{6,22},{7,3},{8,24},{9,13},... | collective-permute-start | bytes 3145736 | tf_op jit(solution)/shard_map/ppermute | solution.py:103
  223.6 13.3 %collective-permute-start.23 = (bf16[8,32,16,256]{3,2,1,0:T(8,128)(2,1)}, bf16[8,32,16,256]{3,2,1,0:T(8,128)(2,1)}, u32[]{:S(2)}, u32[]{:S(2)}) collective-permute-start(bf16[8,32,16,256]{3,2,1,0:T(8,128)(2,1)} %collective-permute-done.20.refs_1_), channel_id=1, source_target_pairs={{0,1},{1,0},{2,3},{3,2},{4,5},{5,4},{6,7},{7,6},{8,9},{9,8},{10,11... | collective-permute-start | bytes 6291464 | tf_op jit(solution)/shard_map/ppermute | solution.py:92
  226.6 39.1 %collective-permute-start.24 = (bf16[8,32,16,256]{3,2,1,0:T(8,128)(2,1)}, bf16[8,32,16,256]{3,2,1,0:T(8,128)(2,1)}, u32[]{:S(2)}, u32[]{:S(2)}) collective-permute-start(bf16[8,32,16,256]{3,2,1,0:T(8,128)(2,1)} %pad_maximum_fusion.2.refs_0_), channel_id=1, source_target_pairs={{0,4},{1,3},{2,6},{3,1},{4,0},{5,7},{6,2},{7,5},{8,12},{9,11},{10,... | collective-permute-start | bytes 6291464 | tf_op jit(solution)/shard_map/ppermute | solution.py:103
  228.7 36.9 %collective-permute-start.25 = (bf16[8,32,16,256]{3,2,1,0:T(8,128)(2,1)}, bf16[8,32,16,256]{3,2,1,0:T(8,128)(2,1)}, u32[]{:S(2)}, u32[]{:S(2)}) collective-permute-start(bf16[8,32,16,256]{3,2,1,0:T(8,128)(2,1)} %pad_maximum_fusion.2.refs_0_), channel_id=1, source_target_pairs={{0,1},{1,0},{2,3},{3,2},{4,5},{5,4},{6,7},{7,6},{8,9},{9,8},{10,11... | collective-permute-start | bytes 6291464 | tf_op jit(solution)/shard_map/ppermute | solution.py:92
  230.4 41.8 %all-to-all-start.2 = ((bf16[32,1,32,512]{3,2,1,0:T(8,128)(2,1)}), bf16[32,1,32,512]{3,2,1,0:T(8,128)(2,1)S(1)}, u32[]{:S(2)}, u32[]{:S(2)}) async-start(bf16[32,1,32,512]{3,2,1,0:T(8,128)(2,1)} %bitcast.238), calls=%async_computation.2 | async-start | bytes 2097152 | tf_op jit(solution)/shard_map/all_to_all | solution.py:636
  265.6 9.4 %collective-permute-start.26 = (bf16[8,32,16,256]{3,2,1,0:T(8,128)(2,1)}, bf16[8,32,16,256]{3,2,1,0:T(8,128)(2,1)}, u32[]{:S(2)}, u32[]{:S(2)}) collective-permute-start(bf16[8,32,16,256]{3,2,1,0:T(8,128)(2,1)} %collective-permute-done.24.refs_1_), channel_id=1, source_target_pairs={{0,1},{1,0},{2,3},{3,2},{4,5},{5,4},{6,7},{7,6},{8,9},{9,8},{10,11... | collective-permute-start | bytes 6291464 | tf_op jit(solution)/shard_map/ppermute | solution.py:92
  273.8 46.4 %collective-permute-start.30 = (bf16[512,4096]{1,0:T(8,128)(2,1)}, bf16[512,4096]{1,0:T(8,128)(2,1)}, u32[]{:S(2)}, u32[]{:S(2)}) collective-permute-start(bf16[512,4096]{1,0:T(8,128)(2,1)} %get-tuple-element.183.x_own), channel_id=1, source_target_pairs={{0,1},{1,0},{2,3},{3,2},{4,5},{5,4},{6,7},{7,6},{8,9},{9,8},{10,11... | collective-permute-start | bytes 12582920 | tf_op jit(solution)/shard_map/ppermute | solution.py:92
  306.3 24.9 %collective-permute-start.29 = (bf16[512,4096]{1,0:T(8,128)(2,1)}, bf16[512,4096]{1,0:T(8,128)(2,1)}, u32[]{:S(2)}, u32[]{:S(2)}) collective-permute-start(bf16[512,4096]{1,0:T(8,128)(2,1)} %multiply_convert_fusion.refs_0_), channel_id=1, source_target_pairs={{0,1},{1,0},{2,3},{3,2},{4,5},{5,4},{6,7},{7,6},{8,9},{9,8},{10,11... | collective-permute-start | bytes 12582920 | tf_op jit(solution)/shard_map/ppermute | solution.py:92
  306.3 31.7 %collective-permute-start.32 = (bf16[512,1024]{1,0:T(8,128)(2,1)S(1)}, bf16[512,1024]{1,0:T(8,128)(2,1)}, u32[]{:S(2)}, u32[]{:S(2)}) collective-permute-start(bf16[512,1024]{1,0:T(8,128)(2,1)S(1)} %copy-done.6), channel_id=1, source_target_pairs={{0,1},{1,0},{2,3},{3,2},{4,5},{5,4},{6,7},{7,6},{8,9},{9,8},{10,11... | collective-permute-start | bytes 3145736 | tf_op jit(solution)/shard_map/ppermute | solution.py:92
  306.8 13.4 %collective-permute-start.31 = (bf16[512,1024]{1,0:T(8,128)(2,1)}, bf16[512,1024]{1,0:T(8,128)(2,1)}, u32[]{:S(2)}, u32[]{:S(2)}) collective-permute-start(bf16[512,1024]{1,0:T(8,128)(2,1)} %copy-done.28), channel_id=1, source_target_pairs={{0,1},{1,0},{2,3},{3,2},{4,5},{5,4},{6,7},{7,6},{8,9},{9,8},{10,11... | collective-permute-start | bytes 3145736 | tf_op jit(solution)/shard_map/ppermute | solution.py:92
  308.8 8.8 %collective-permute-start.27 = (bf16[512,512]{1,0:T(8,128)(2,1)}, bf16[512,512]{1,0:T(8,128)(2,1)}, u32[]{:S(2)}, u32[]{:S(2)}) collective-permute-start(bf16[512,512]{1,0:T(8,128)(2,1)} %constant_dynamic-slice_fusion.2), channel_id=1, source_target_pairs={{0,1},{1,0},{2,3},{3,2},{4,5},{5,4},{6,7},{7,6},{8,9},{9,8},{10,11... | collective-permute-start | bytes 1572872 | tf_op jit(solution)/shard_map/ppermute | solution.py:92
  317.6 100.5 %collective-permute-start.43 = (bf16[512,1024]{1,0:T(8,128)(2,1)}, bf16[512,1024]{1,0:T(8,128)(2,1)}, u32[]{:S(2)}, u32[]{:S(2)}) collective-permute-start(bf16[512,1024]{1,0:T(8,128)(2,1)} %get-tuple-element.160.x_own.o_ref), channel_id=1, source_target_pairs={{0,1},{1,0},{2,3},{3,2},{4,5},{5,4},{6,7},{7,6},{8,9},{9,8},{10,11... | collective-permute-start | bytes 3145736 | tf_op jit(solution)/shard_map/ppermute | solution.py:92
  333.5 34.1 %all-to-all-start.3 = ((bf16[2,16,32,512]{3,2,0,1:T(8,128)(2,1)}), bf16[2,16,32,512]{3,2,0,1:T(8,128)(2,1)}, u32[]{:S(2)}, u32[]{:S(2)}) async-start(bf16[2,16,32,512]{3,2,0,1:T(8,128)(2,1)} %copy.70), calls=%async_computation.3 | async-start | bytes 2097152 | tf_op jit(solution)/shard_map/all_to_all | solution.py:631
  347.7 33.4 %collective-permute-start.33 = (bf16[8,32,16,256]{3,2,1,0:T(8,128)(2,1)}, bf16[8,32,16,256]{3,2,1,0:T(8,128)(2,1)}, u32[]{:S(2)}, u32[]{:S(2)}) collective-permute-start(bf16[8,32,16,256]{3,2,1,0:T(8,128)(2,1)} %bitcast.294), channel_id=1, source_target_pairs={{0,4},{1,3},{2,6},{3,1},{4,0},{5,7},{6,2},{7,5},{8,12},{9,11},{10,... | collective-permute-start | bytes 6291464 | tf_op jit(solution)/shard_map/ppermute | solution.py:103
  349.6 42.2 %collective-permute-start.34 = (bf16[8,32,16,256]{3,2,1,0:T(8,128)(2,1)}, bf16[8,32,16,256]{3,2,1,0:T(8,128)(2,1)}, u32[]{:S(2)}, u32[]{:S(2)}) collective-permute-start(bf16[8,32,16,256]{3,2,1,0:T(8,128)(2,1)} %bitcast.295), channel_id=1, source_target_pairs={{0,16},{1,3},{2,18},{3,1},{4,20},{5,7},{6,22},{7,5},{8,24},{9,11},... | collective-permute-start | bytes 6291464 | tf_op jit(solution)/shard_map/ppermute | solution.py:103
  398.4 20.1 %collective-permute-start.35 = (bf16[512,1024]{1,0:T(8,128)(2,1)S(1)}, bf16[512,1024]{1,0:T(8,128)(2,1)S(1)}, u32[]{:S(2)}, u32[]{:S(2)}) collective-permute-start(bf16[512,1024]{1,0:T(8,128)(2,1)S(1)} %convert_element_type.370.refs_0_), channel_id=1, source_target_pairs={{0,1},{1,0},{2,3},{3,2},{4,5},{5,4},{6,7},{7,6},{8,9},{9,8},{10,11... | collective-permute-start | bytes 3145736 | tf_op jit(solution)/shard_map/ppermute | solution.py:92
  410.7 14.9 %collective-permute-start.36 = (bf16[4,32,16,256]{3,2,1,0:T(8,128)(2,1)S(1)}, bf16[4,32,16,256]{3,2,1,0:T(8,128)(2,1)S(1)}, u32[]{:S(2)}, u32[]{:S(2)}) collective-permute-start(bf16[4,32,16,256]{3,2,1,0:T(8,128)(2,1)S(1)} %get-tuple-element.292), channel_id=1, source_target_pairs={{0,16},{1,5},{2,18},{3,7},{4,20},{5,1},{6,22},{7,3},{8,24},{9,13},... | collective-permute-start | bytes 3145736 | tf_op jit(solution)/shard_map/ppermute | solution.py:103
  412.2 18.1 %collective-permute-start.41 = (bf16[512,1024]{1,0:T(8,128)(2,1)S(1)}, bf16[512,1024]{1,0:T(8,128)(2,1)S(1)}, u32[]{:S(2)}, u32[]{:S(2)}) collective-permute-start(bf16[512,1024]{1,0:T(8,128)(2,1)S(1)} %copy-done.18), channel_id=1, source_target_pairs={{0,1},{1,0},{2,3},{3,2},{4,5},{5,4},{6,7},{7,6},{8,9},{9,8},{10,11... | collective-permute-start | bytes 3145736 | tf_op jit(solution)/shard_map/ppermute | solution.py:92
  414.4 18.4 %collective-permute-start.42 = (bf16[512,1024]{1,0:T(8,128)(2,1)S(1)}, bf16[512,1024]{1,0:T(8,128)(2,1)S(1)}, u32[]{:S(2)}, u32[]{:S(2)}) collective-permute-start(bf16[512,1024]{1,0:T(8,128)(2,1)S(1)} %copy-done.19), channel_id=1, source_target_pairs={{0,1},{1,0},{2,3},{3,2},{4,5},{5,4},{6,7},{7,6},{8,9},{9,8},{10,11... | collective-permute-start | bytes 3145736 | tf_op jit(solution)/shard_map/ppermute | solution.py:92
  418.0 32.5 %collective-permute-start.37 = (bf16[512,1024]{1,0:T(8,128)(2,1)}, bf16[512,1024]{1,0:T(8,128)(2,1)}, u32[]{:S(2)}, u32[]{:S(2)}) collective-permute-start(bf16[512,1024]{1,0:T(8,128)(2,1)} %get-tuple-element.172.o_ref.x_own), channel_id=1, source_target_pairs={{0,1},{1,0},{2,3},{3,2},{4,5},{5,4},{6,7},{7,6},{8,9},{9,8},{10,11... | collective-permute-start | bytes 3145736 | tf_op jit(solution)/shard_map/ppermute | solution.py:92
  418.5 32.1 %collective-permute-start.38 = (bf16[512,1024]{1,0:T(8,128)(2,1)S(1)}, bf16[512,1024]{1,0:T(8,128)(2,1)}, u32[]{:S(2)}, u32[]{:S(2)}) collective-permute-start(bf16[512,1024]{1,0:T(8,128)(2,1)S(1)} %convert_element_type.368.refs_0_), channel_id=1, source_target_pairs={{0,1},{1,0},{2,3},{3,2},{4,5},{5,4},{6,7},{7,6},{8,9},{9,8},{10,11... | collective-permute-start | bytes 3145736 | tf_op jit(solution)/shard_map/ppermute | solution.py:92
  425.6 29.8 %collective-permute-start.44 = (bf16[4,32,16,256]{3,2,1,0:T(8,128)(2,1)}, bf16[4,32,16,256]{3,2,1,0:T(8,128)(2,1)}, u32[]{:S(2)}, u32[]{:S(2)}) collective-permute-start(bf16[4,32,16,256]{3,2,1,0:T(8,128)(2,1)} %get-tuple-element.290), channel_id=1, source_target_pairs={{0,4},{1,5},{2,6},{3,7},{4,0},{5,1},{6,2},{7,3},{8,12},{9,13},{10,... | collective-permute-start | bytes 3145736 | tf_op jit(solution)/shard_map/ppermute | solution.py:103
  431.9 23.5 %collective-permute-start.45 = (bf16[2,32,16,256]{3,2,1,0:T(8,128)(2,1)S(1)}, bf16[2,32,16,256]{3,2,1,0:T(8,128)(2,1)S(1)}, u32[]{:S(2)}, u32[]{:S(2)}) collective-permute-start(bf16[2,32,16,256]{3,2,1,0:T(8,128)(2,1)S(1)} %get-tuple-element.301), channel_id=1, source_target_pairs={{0,2},{1,17},{2,0},{3,19},{4,6},{5,21},{6,4},{7,23},{8,10},{9,25},... | collective-permute-start | bytes 1572872 | tf_op jit(solution)/shard_map/ppermute | solution.py:103
  433.8 10.7 %collective-permute-start.40 = (bf16[128,1024]{1,0:T(8,128)(2,1)S(1)}, bf16[128,1024]{1,0:T(8,128)(2,1)S(1)}, u32[]{:S(2)}, u32[]{:S(2)}) collective-permute-start(bf16[128,1024]{1,0:T(8,128)(2,1)S(1)} %copy-done.39), channel_id=1, source_target_pairs={{0,1},{1,0},{2,3},{3,2},{4,5},{5,4},{6,7},{7,6},{8,9},{9,8},{10,11... | collective-permute-start | bytes 786440 | tf_op jit(solution)/shard_map/ppermute | solution.py:92
  455.4 48.9 %collective-permute-start.46 = (bf16[8,40,16,256]{3,2,1,0:T(8,128)(2,1)}, bf16[8,40,16,256]{3,2,1,0:T(8,128)(2,1)}, u32[]{:S(2)}, u32[]{:S(2)}) collective-permute-start(bf16[8,40,16,256]{3,2,1,0:T(8,128)(2,1)} %bitcast.221), channel_id=1, source_target_pairs={{0,2},{1,17},{2,0},{3,19},{4,6},{5,21},{6,4},{7,23},{8,10},{9,25},... | collective-permute-start | bytes 7864328 | tf_op jit(solution)/shard_map/ppermute | solution.py:103
  459.4 39.2 %all-to-all-start.4 = ((bf16[32,1,32,512]{3,2,1,0:T(8,128)(2,1)}), bf16[32,1,32,512]{3,2,1,0:T(8,128)(2,1)}, u32[]{:S(2)}, u32[]{:S(2)}) async-start(bf16[32,1,32,512]{3,2,1,0:T(8,128)(2,1)} %bitcast.66), calls=%async_computation.4 | async-start | bytes 2097152 | tf_op jit(solution)/shard_map/all_to_all | solution.py:636
  467.1 37.2 %collective-permute-start.47 = (bf16[2,32,16,256]{3,2,1,0:T(8,128)(2,1)}, bf16[2,32,16,256]{3,2,1,0:T(8,128)(2,1)}, u32[]{:S(2)}, u32[]{:S(2)}) collective-permute-start(bf16[2,32,16,256]{3,2,1,0:T(8,128)(2,1)} %get-tuple-element.299), channel_id=1, source_target_pairs={{0,2},{1,17},{2,0},{3,19},{4,6},{5,21},{6,4},{7,23},{8,10},{9,25},... | collective-permute-start | bytes 1572872 | tf_op jit(solution)/shard_map/ppermute | solution.py:103
  469.2 33.2 %collective-permute-start.48 = (bf16[1,32,16,256]{3,2,1,0:T(8,128)(2,1)S(1)}, bf16[1,32,16,256]{3,2,1,0:T(8,128)(2,1)}, u32[]{:S(2)}, u32[]{:S(2)}) collective-permute-start(bf16[1,32,16,256]{3,2,1,0:T(8,128)(2,1)S(1)} %add_convert_fusion.27), channel_id=1, source_target_pairs={{0,8},{1,9},{2,10},{3,11},{4,12},{5,13},{6,14},{7,15},{8,0},{9,1},... | collective-permute-start | bytes 786440 | tf_op jit(solution)/shard_map/ppermute | solution.py:103
  488.0 27.4 %collective-permute-start.49 = (bf16[512,1024]{1,0:T(8,128)(2,1)}, bf16[512,1024]{1,0:T(8,128)(2,1)}, u32[]{:S(2)}, u32[]{:S(2)}) collective-permute-start(bf16[512,1024]{1,0:T(8,128)(2,1)} %get-tuple-element.242.refs_0_), channel_id=1, source_target_pairs={{0,1},{1,0},{2,3},{3,2},{4,5},{5,4},{6,7},{7,6},{8,9},{9,8},{10,11... | collective-permute-start | bytes 3145736 | tf_op jit(solution)/shard_map/ppermute | solution.py:92
  488.1 27.3 %collective-permute-start.50 = (bf16[512,1024]{1,0:T(8,128)(2,1)}, bf16[512,1024]{1,0:T(8,128)(2,1)}, u32[]{:S(2)}, u32[]{:S(2)}) collective-permute-start(bf16[512,1024]{1,0:T(8,128)(2,1)} %get-tuple-element.243.refs_1_), channel_id=1, source_target_pairs={{0,1},{1,0},{2,3},{3,2},{4,5},{5,4},{6,7},{7,6},{8,9},{9,8},{10,11... | collective-permute-start | bytes 3145736 | tf_op jit(solution)/shard_map/ppermute | solution.py:92
  502.4 13.0 %collective-permute-start.51 = (bf16[512,1024]{1,0:T(8,128)(2,1)}, bf16[512,1024]{1,0:T(8,128)(2,1)}, u32[]{:S(2)}, u32[]{:S(2)}) collective-permute-start(bf16[512,1024]{1,0:T(8,128)(2,1)} %get-tuple-element.244.refs_2_), channel_id=1, source_target_pairs={{0,1},{1,0},{2,3},{3,2},{4,5},{5,4},{6,7},{7,6},{8,9},{9,8},{10,11... | collective-permute-start | bytes 3145736 | tf_op jit(solution)/shard_map/ppermute | solution.py:92
  508.2 19.4 %collective-permute-start.52 = (bf16[4,40,16,256]{3,2,1,0:T(8,128)(2,1)}, bf16[4,40,16,256]{3,2,1,0:T(8,128)(2,1)}, u32[]{:S(2)}, u32[]{:S(2)}) collective-permute-start(bf16[4,40,16,256]{3,2,1,0:T(8,128)(2,1)} %get-tuple-element.288), channel_id=1, source_target_pairs={{0,16},{1,3},{2,18},{3,1},{4,20},{5,7},{6,22},{7,5},{8,24},{9,11},... | collective-permute-start | bytes 3932168 | tf_op jit(solution)/shard_map/ppermute | solution.py:103
  513.9 13.7 %collective-permute-start.53 = (bf16[1,32,16,256]{3,2,1,0:T(8,128)(2,1)S(1)}, bf16[1,32,16,256]{3,2,1,0:T(8,128)(2,1)S(1)}, u32[]{:S(2)}, u32[]{:S(2)}) collective-permute-start(bf16[1,32,16,256]{3,2,1,0:T(8,128)(2,1)S(1)} %add_convert_fusion.26), channel_id=1, source_target_pairs={{0,8},{1,9},{2,10},{3,11},{4,12},{5,13},{6,14},{7,15},{8,0},{9,1},... | collective-permute-start | bytes 786440 | tf_op jit(solution)/shard_map/ppermute | solution.py:103
  527.6 20.7 %collective-permute-start.54 = (bf16[8,24,16,256]{3,2,1,0:T(8,128)(2,1)}, bf16[8,24,16,256]{3,2,1,0:T(8,128)(2,1)}, u32[]{:S(2)}, u32[]{:S(2)}) collective-permute-start(bf16[8,24,16,256]{3,2,1,0:T(8,128)(2,1)} %bitcast.296), channel_id=1, source_target_pairs={{0,2},{1,17},{2,0},{3,19},{4,6},{5,21},{6,4},{7,23},{8,10},{9,25},... | collective-permute-start | bytes 4718600 | tf_op jit(solution)/shard_map/ppermute | solution.py:103
  531.1 19.3 %collective-permute-start.59 = (bf16[2,40,16,256]{3,2,1,0:T(8,128)(2,1)}, bf16[2,40,16,256]{3,2,1,0:T(8,128)(2,1)}, u32[]{:S(2)}, u32[]{:S(2)}) collective-permute-start(bf16[2,40,16,256]{3,2,1,0:T(8,128)(2,1)} %get-tuple-element.296), channel_id=1, source_target_pairs={{0,4},{1,5},{2,6},{3,7},{4,0},{5,1},{6,2},{7,3},{8,12},{9,13},{10,... | collective-permute-start | bytes 1966088 | tf_op jit(solution)/shard_map/ppermute | solution.py:103
  550.2 22.5 %collective-permute-start.57 = (bf16[4,24,16,256]{3,2,1,0:T(8,128)(2,1)S(1)}, bf16[4,24,16,256]{3,2,1,0:T(8,128)(2,1)S(1)}, u32[]{:S(2)}, u32[]{:S(2)}) collective-permute-start(bf16[4,24,16,256]{3,2,1,0:T(8,128)(2,1)S(1)} %get-tuple-element.294), channel_id=1, source_target_pairs={{0,4},{1,3},{2,6},{3,1},{4,0},{5,7},{6,2},{7,5},{8,12},{9,11},{10,... | collective-permute-start | bytes 2359304 | tf_op jit(solution)/shard_map/ppermute | solution.py:103
  552.1 29.7 %collective-permute-start.60 = (bf16[1,40,16,256]{3,2,1,0:T(8,128)(2,1)}, bf16[1,40,16,256]{3,2,1,0:T(8,128)(2,1)}, u32[]{:S(2)}, u32[]{:S(2)}) collective-permute-start(bf16[1,40,16,256]{3,2,1,0:T(8,128)(2,1)} %add_convert_fusion.21), channel_id=1, source_target_pairs={{0,8},{1,9},{2,10},{3,11},{4,12},{5,13},{6,14},{7,15},{8,0},{9,1},... | collective-permute-start | bytes 983048 | tf_op jit(solution)/shard_map/ppermute | solution.py:103
  573.6 8.2 %collective-permute-start.58 = (bf16[2,24,16,256]{3,2,1,0:T(8,128)(2,1)}, bf16[2,24,16,256]{3,2,1,0:T(8,128)(2,1)S(1)}, u32[]{:S(2)}, u32[]{:S(2)}) collective-permute-start(bf16[2,24,16,256]{3,2,1,0:T(8,128)(2,1)} %get-tuple-element.309), channel_id=1, source_target_pairs={{0,16},{1,5},{2,18},{3,7},{4,20},{5,1},{6,22},{7,3},{8,24},{9,13},... | collective-permute-start | bytes 1179656 | tf_op jit(solution)/shard_map/ppermute | solution.py:103
  577.3 19.4 %all-to-all-start.6 = ((f32[8,1,1088]{2,1,0:T(1,128)}), f32[8,1,1088]{2,1,0:T(1,128)S(1)}, u32[]{:S(2)}, u32[]{:S(2)}) async-start(f32[8,1,1088]{2,1,0:T(1,128)} %all_to_all.76), calls=%async_computation.6 | async-start | bytes 73728 | tf_op jit(solution)/shard_map/all_to_all | solution.py:825
  581.9 12.9 %collective-permute-start.61 = (bf16[1,24,16,256]{3,2,1,0:T(8,128)(2,1)S(1)}, bf16[1,24,16,256]{3,2,1,0:T(8,128)(2,1)S(1)}, u32[]{:S(2)}, u32[]{:S(2)}) collective-permute-start(bf16[1,24,16,256]{3,2,1,0:T(8,128)(2,1)S(1)} %add_convert_fusion.29), channel_id=1, source_target_pairs={{0,8},{1,9},{2,10},{3,11},{4,12},{5,13},{6,14},{7,15},{8,0},{9,1},... | collective-permute-start | bytes 589832 | tf_op jit(solution)/shard_map/ppermute | solution.py:103
  596.6 31.0 %all-to-all-start.5 = ((bf16[128,16,256]{2,1,0:T(8,128)(2,1)}), bf16[128,16,256]{2,1,0:T(8,128)(2,1)S(1)}, u32[]{:S(2)}, u32[]{:S(2)}) async-start(bf16[128,16,256]{2,1,0:T(8,128)(2,1)} %gather_fusion.3), calls=%async_computation.5 | async-start | bytes 2097152 | tf_op jit(solution)/shard_map/all_to_all | solution.py:308
  606.6 23.9 %collective-permute-start.64 = (f32[1,1088]{1,0:T(1,128)S(1)}, f32[1,1088]{1,0:T(1,128)S(1)}, u32[]{:S(2)}, u32[]{:S(2)}) collective-permute-start(f32[1,1088]{1,0:T(1,128)S(1)} %broadcast_in_dim.85), channel_id=1, source_target_pairs={{0,16},{16,0},{1,17},{17,1},{2,18},{18,2},{3,19},{19,3},{4,20},{20... | collective-permute-start | bytes 13064 | tf_op jit(solution)/shard_map/ppermute | solution.py:95
  627.7 24.0 %collective-permute-start.62 = (bf16[8,16,16,256]{3,2,1,0:T(8,128)(2,1)S(1)}, bf16[8,16,16,256]{3,2,1,0:T(8,128)(2,1)S(1)}, u32[]{:S(2)}, u32[]{:S(2)}) collective-permute-start(bf16[8,16,16,256]{3,2,1,0:T(8,128)(2,1)S(1)} %bitcast.235), channel_id=1, source_target_pairs={{0,16},{16,0},{1,17},{17,1},{2,18},{18,2},{3,19},{19,3},{4,20},{20... | collective-permute-start | bytes 3145736 | tf_op jit(solution)/shard_map/ppermute | solution.py:95
  (93 other events, 990.6 us)

commit v4 on v3

--- a/solution.py
+++ b/solution.py
@@ -81,12 +81,14 @@
         self.rows = BS // self.pieces
         self.depth = self.pieces.bit_length() - 1
         x, z1, z2, y = 1, 2, 4, 8
-        self.orders = (
+        gathering = (
             ((z2, y, z1, x), (z2, z1, x, y)),
             ((z2, z1, y, x), (z2, z1, x, y)),
             ((z2, x, z1, y), (z2, y, z1, x)),
             ((z2, x, y, z1), (z2, y, z1, x)),
         )
+        reducing = (((z2, y, z1, x), (z2, x, z1, y)),) + gathering[1:]
+        self.orders = gathering + reducing
 
     def swap_core(self, value):
         return lax.ppermute(value, "mp", [(i, i ^ 1) for i in range(self.n_mp)])
@@ -297,17 +299,37 @@
     return total_of(*terms)[0]
 
 
-def last_pieces(net, natural, block_slots):
-    dealt = natural.at[block_slots].get(mode="promise_in_bounds")
+def last_pieces(net, natural, block_slots, vec_sum):
     if net.pieces == 1:
+        dealt = natural.at[block_slots].get(mode="promise_in_bounds")
         owned = lax.psum_scatter(dealt, "shard", scatter_dimension=0, tiled=True)
         owned = total_of(owned, net.swap_rep(owned))
         cut = owned.reshape(-1, 2, 8, 16, BS).transpose(1, 2, 0, 3, 4)
         cut = cut[:, np.array([chunk_of(k) for k in range(8)])]
-        return cut[0], cut[1], jnp.zeros((1,), jnp.int32)
-    mine = lax.all_to_all(dealt, "shard", split_axis=0, concat_axis=0, tiled=True)
-    mine = mine.reshape(net.n_shard, -1, net.rows, BS)
-    return mine, net.swap_rep(mine), lax.axis_index("rep").astype(jnp.int32).reshape(1)
+        vec = lax.psum_scatter(vec_sum, "shard", scatter_dimension=0, tiled=True)[None]
+        parts = [(cut[0], cut[1], owned.shape[0])]
+        return parts, jnp.zeros((1,), jnp.int32), vec + net.swap_rep(vec)
+    n = net.n_shard
+    slots = block_slots.reshape(n, -1)
+    half = slots.shape[1] // 2
+    room = net.rows * BS
+    vec_cut = vec_sum.reshape(n, -1)
+    width = vec_cut.shape[1]
+    vec_cut = jnp.pad(vec_cut.astype(bf16), ((0, 0), (0, room - width)))
+    vec_cut = vec_cut.reshape(n, 1, net.rows, BS)
+    parts = []
+    for k in range(2):
+        index = slots[:, k * half : (k + 1) * half].reshape(-1)
+        cut = natural.at[index].get(mode="promise_in_bounds")
+        if k == 1:
+            cut = jnp.concatenate([cut.reshape(n, half, net.rows, BS), vec_cut], axis=1)
+            cut = cut.reshape(-1, net.rows, BS)
+        mine = lax.all_to_all(cut, "shard", split_axis=0, concat_axis=0, tiled=True)
+        mine = mine.reshape(n, -1, net.rows, BS)
+        parts.append((mine, net.swap_rep(mine), half))
+    terms = [v[:, half].reshape(n, room)[:, :width].astype(f32) for v in parts[1][:2]]
+    flag = lax.axis_index("rep").astype(jnp.int32).reshape(1)
+    return parts, flag, jnp.sum(terms[0] + terms[1], axis=0, keepdims=True)
 
 
 def attend_forward_body(lim, q_ref, k_ref, v_ref, o_ref, lse_ref, *, causal, rows):
@@ -570,7 +592,8 @@
     return hi, (a - hi.astype(f32)).astype(bf16)
 
 
-def shampoo_body(flag, mine_ref, other_ref, w_ref, ls_ref, rs_ref, lr_ref, rr_ref, og, ol, orr, ow, g_ref):
+def shampoo_body(flag, mine_ref, other_ref, w_ref, ls_ref, rs_ref, lr_ref, rr_ref, *refs):
+    og, ol, orr, ow, g_ref = refs[-5:]
     for k in range(mine_ref.shape[0]):
         for plane, src in ((flag[0], mine_ref), (1 - flag[0], other_ref)):
             row = pl.multiple_of(plane * 128 + chunk_of(k) * 16, 16)
@@ -587,21 +610,30 @@
     ow[0, 0] = w_ref[0, 0] - (D**-0.5) * d / jnp.sqrt(mean + 1e-06)
 
 
-def shampoo(flag, mine, other, weights, left_stat, right_stat, left_root, right_root):
-    n = mine.shape[1]
-    spec = pl.BlockSpec((1, 1, BS, BS), lambda i: (0, i, 0, 0))
-    g_spec = pl.BlockSpec((mine.shape[0], 1, mine.shape[2], BS), lambda i: (0, i, 0, 0))
-    return pl.pallas_call(
-        shampoo_body,
-        grid=(n,),
-        out_shape=(jax.ShapeDtypeStruct((1, n, BS, BS), f32),) * 4,
-        in_specs=[pl.BlockSpec(memory_space=pltpu.SMEM), g_spec, g_spec] + [spec] * 5,
-        out_specs=(spec,) * 4,
-        scratch_shapes=[pltpu.VMEM((BS, BS), bf16)],
-        compiler_params=params(),
-        cost_estimate=small(),
-        name="shampoo",
-    )(flag, mine, other, weights, left_stat, right_stat, left_root, right_root)
+def shampoo(flag, parts, *states):
+    total = states[0].shape[1]
+    out, first = (), 0
+    for mine, other, n in parts:
+        at = first // n
+        spec = pl.BlockSpec((1, 1, BS, BS), lambda i, at=at, n=n: (0, at * n + i, 0, 0))
+        g_spec = pl.BlockSpec((mine.shape[0], 1, mine.shape[2], BS), lambda i: (0, i, 0, 0))
+        anyspec = pl.BlockSpec(memory_space=pl.ANY)
+        out = pl.pallas_call(
+            shampoo_body,
+            grid=(n,),
+            out_shape=(jax.ShapeDtypeStruct((1, total, BS, BS), f32),) * 4,
+            in_specs=[pl.BlockSpec(memory_space=pltpu.SMEM), g_spec, g_spec]
+            + [spec] * 5
+            + [anyspec] * len(out),
+            out_specs=(spec,) * 4,
+            scratch_shapes=[pltpu.VMEM((BS, BS), bf16)],
+            input_output_aliases={8 + k: k for k in range(len(out))},
+            compiler_params=params(),
+            cost_estimate=small(),
+            name="shampoo",
+        )(flag, mine, other, *states, *out)
+        first += n
+    return out
 
 
 def norm_forward(z, gain, shift):
@@ -659,7 +691,7 @@
     data_index = lax.axis_index(("rep", "shard"))
     seq_index = data_index * inputs.shape[0] + core
     limit = lax.dynamic_slice_in_dim(lengths, seq_index, 1)
-    tables = [net.table(k, core, data_index) for k in range(len(GROUPS))]
+    tables = [net.table(k, core, data_index) for k in range(2 * len(GROUPS))]
     is_first = core == 0
 
     def pick(pair, which):
@@ -731,10 +763,11 @@
     v_c = (dot_nn(e, w_cv) + b_cv).astype(bf16)
     q_c, k_c, v_c = step((q_c, k_c, v_c), down)
     o_c, lse_c = attend_forward(limit, q_c, k_c, v_c, False)
+    cot_pieces, o_c, lse_c = step((cot_pieces, o_c, lse_c))
+    cot_home = route_home(cot_pieces, seq_slots)
     z_two = h_one + dot_nn(o_c, w_co) + b_co
     h_two, n_two, r_two = norm_forward(z_two, g_two, b_two)
-    cot_pieces, h_two, h_two_low = step((cot_pieces, h_two, h_two.astype(bf16)), up, down)
-    cot_home = route_home(cot_pieces, seq_slots)
+    h_two, h_two_low = step((h_two, h_two.astype(bf16)), up, down)
     (w_fi,) = placed(2)
     act, slope = gelu_forward(h_two_low, w_fi, b_fi)
     act_sib = net.swap_core(act)
@@ -749,10 +782,10 @@
     def gradient(k, *calls):
         held, first = None, 0
         for xs, *ys in calls:
-            held = weight_grad(net, k, tables[k], xs, ys, held, first, GROUPS[k][first][1])
+            held = weight_grad(net, k, tables[len(GROUPS) + k], xs, ys, held, first, GROUPS[k][first][1])
             first += len(ys)
         parts = tuple(h.reshape(h.shape[0], -1, net.rows, BS) for h in held)
-        return Flow(reduce_rounds(net, k, parts))
+        return Flow(reduce_rounds(net, len(GROUPS) + k, parts))
 
     cot, _ = whole(cot_home)
     grad_y = cot.astype(f32) * live
@@ -761,25 +794,24 @@
     d_hidden = (dot_nt(a_three, w_fo) * slope.astype(f32)).astype(bf16)
     d_hidden_sib = net.swap_core(d_hidden)
     down = gradient(3, ((act, act_sib), (a_three, net.swap_core(a_three))))
-    finished, d_hidden, d_hidden_sib = step((finished, d_hidden, d_hidden_sib), down)
+    d_hidden, d_hidden_sib = step((d_hidden, d_hidden_sib), down)
+    up = gradient(2, ((h_two_low, net.swap_core(h_two_low)), (d_hidden, d_hidden_sib)))
+    finished, d_hidden = step((finished, d_hidden), up)
     out_pieces = route_out(finished)
-    up = gradient(2, ((h_two_low, net.swap_core(h_two_low)), (d_hidden, d_hidden_sib)))
-    (d_hidden,) = step((d_hidden,), up)
     d_h_two = d_three + dot_nt(d_hidden, w_fi)
     d_two, dg_two, db_two = norm_backward(d_h_two, n_two, r_two, g_two)
     a_two = d_two.astype(bf16)
     d_oc = dot_nt(a_two, w_co).astype(bf16)
-    out_pieces, d_oc = step((out_pieces, d_oc), down)
-    outputs = route_home(out_pieces, source)
     dq_c, dk_c, dv_c = attend_backward(limit, q_c, k_c, v_c, o_c, d_oc, lse_c, False)
     dq_c_sib, dk_c_sib, dv_c_sib = [net.swap_core(v) for v in (dq_c, dk_c, dv_c)]
-    dq_c, dk_c, dv_c = step((dq_c, dk_c, dv_c), up)
+    dq_c, dk_c, dv_c = step((dq_c, dk_c, dv_c), up, down)
     d_h_one = d_two + dot_nt(dq_c, w_cq)
     d_one, dg_one, db_one = norm_backward(d_h_one, n_one, r_one, g_one)
     a_one = d_one.astype(bf16)
     a_one_sib = net.swap_core(a_one)
     d_os = dot_nt(a_one, w_so).astype(bf16)
-    a_one, a_one_sib, d_os = step((a_one, a_one_sib, d_os), down)
+    out_pieces, a_one, a_one_sib, d_os = step((out_pieces, a_one, a_one_sib, d_os), down)
+    outputs = route_home(out_pieces, source)
     cross = gradient(
         1,
         ((o_s, net.swap_core(o_s)), (a_one, a_one_sib)),
@@ -790,20 +822,17 @@
     (d_os,) = step((d_os,), cross, up, down)
     dq_s, dk_s, dv_s = attend_backward(limit, q_s, k_s, v_s, o_s, d_os, lse_s, True)
     sibs = [net.swap_core(v) for v in (dq_s, dk_s, dv_s)]
-    outputs, dq_s, dk_s, dv_s = step((outputs, dq_s, dk_s, dv_s), cross, up, down)
+    attn = gradient(0, ((x, x_sib), *zip((dq_s, dk_s, dv_s), sibs)))
+    dq_s, dk_s, dv_s = step((dq_s, dk_s, dv_s), attn, up, down)
+    d_hidden, dq_c, dk_c, dv_c, dq_s, dk_s, dv_s = step(
+        (d_hidden, dq_c, dk_c, dv_c, dq_s, dk_s, dv_s), cross
+    )
     state_back = dot_nt(dk_c, w_ck) + dot_nt(dv_c, w_cv)
-    attn = gradient(0, ((x, x_sib), *zip((dq_s, dk_s, dv_s), sibs)))
-    dq_s, dk_s, dv_s = step((dq_s, dk_s, dv_s), attn, cross, up)
     back = d_one + dot_nt(dq_s, w_sq) + dot_nt(dk_s, w_sk) + dot_nt(dv_s, w_sv)
-    (back,) = step((back,), attn)
+    outputs, back = step((outputs, back), attn, up)
     step((), cross)
     input_grad = halved(back.astype(bf16))
     encoded_grad = halved(state_back.astype(bf16))
-    step((), attn)
-    step((), attn, cross)
-    natural = [f.finish() for f in (attn, cross, up, down)]
-    mine, other, flag = last_pieces(net, jnp.concatenate(natural), block_slots)
-
     sums = (
         jnp.sum(dq_s.astype(f32), axis=0),
         jnp.sum(dv_s.astype(f32), axis=0),
@@ -822,14 +851,13 @@
     )
     vec_pair = jnp.concatenate([s.reshape(halves, -1) for s in sums], axis=1)
     vec_sum = pick(vec_pair, core) + net.swap_core(pick(vec_pair, 1 - core))
-    vec_parts = lax.all_to_all(
-        vec_sum.reshape(net.n_shard, -1), "shard", split_axis=0, concat_axis=0, tiled=True
-    )
-    vec_owned = jnp.sum(vec_parts, axis=0, keepdims=True)
-    vec_owned = vec_owned + net.swap_rep(vec_owned)
-
+    step((), attn)
+    vec_sum, input_grad, encoded_grad = step((vec_sum, input_grad, encoded_grad), attn, cross)
+    natural = [f.finish() for f in (attn, cross, up, down)]
+
+    parts, flag, vec_owned = last_pieces(net, jnp.concatenate(natural), block_slots, vec_sum)
     block_grad, left_new, right_new, weights_new = shampoo(
-        flag, mine, other, weights, left_stat, right_stat, left_root, right_root
+        flag, parts, weights, left_stat, right_stat, left_root, right_root
     )
     vec_stat_new = 0.5 * vec_stat + 0.5 * vec_owned * vec_owned
     vectors_new = vectors - 0.1 * vec_owned * lax.rsqrt(vec_stat_new)

time: 685 us -> 696 us (1.016)
  waiting for transfers between devices: 201 us -> 216 us
    ppermute x32, waiting for transfers between devices: 109 us -> 133 us  [swap_data(): return lax.ppermute(value, ('rep', 'shard', 'mp'), pairs)]
    all_to_all x2, waiting for transfers between devices: 16.3 us -> 6.69 us  [route_home(): lax.all_to_all(moved, ('rep', 'shard'), split_axis=0, concat_axis=1, tile...]
    all_to_all x2, waiting for transfers between devices: 20 us -> 27.4 us  [last_pieces(): mine = lax.all_to_all(cut, 'shard', split_axis=0, concat_axis=0, tiled=True)]
    ppermute x2, waiting for transfers between devices: 18.6 us -> 11.2 us  [swap_rep(): return lax.ppermute(value, 'rep', [(i, i ^ 1) for i in range(self.n_rep)])]
    unnamed x198 -> x201, local copies, waits for them, and re-layouts: 14.5 us -> 10.6 us
    pallas_call x1 -> x2, Pallas kernels: 20.3 us -> 21.9 us  [shampoo(): pl.pallas_call(shampoo_body, grid=(n,), out_shape=(jax.ShapeDtypeStruct((...]
  transfers between devices with their start and end apart: 72 -> 72, of which waited for: 30 -> 30; matrix products, arithmetic and copies ran while one was open for 24% -> 22% of each run, Pallas kernels for 24% -> 25%
where the time goes in v4:
time: 696 us; the launch traced here: 685 us
  waiting for transfers between devices  216 us (31%)
  Pallas kernels  184 us (26%)
  starting transfers between devices  104 us (15%)
  other arithmetic  76.1 us (11%)
  matrix products  63.4 us (9%)
  local copies, waits for them, and re-layouts  38.5 us (6%)
    ppermute x32, waiting for transfers between devices, swap_data(): return lax.ppermute(value, ('rep', 'shard', 'mp'), pairs)  133 us
    pallas_call x7, Pallas kernels, weight_grad(): pl.pallas_call(functools.partial(weight_grad_body, count=count, outs=outs...  49.7 us
    ppermute x32, starting transfers between devices, swap_data(): return lax.ppermute(value, ('rep', 'shard', 'mp'), pairs)  40.2 us
    pallas_call x4, Pallas kernels, place(): pl.pallas_call(functools.partial(place_body, dests=dests, many=many, two=...  37.9 us
    dot_general x10, matrix products, dot_nt(): return lax.dot_general(a, b, NT, preferred_element_type=f32)  34.4 us
    pallas_call x2, Pallas kernels, attend_forward(): pl.pallas_call(functools.partial(attend_forward_body, causal=causal, rows...  29.1 us
    dot_general x9, matrix products, dot_nn(): return jnp.dot(a, b, preferred_element_type=f32)  29 us
    all_to_all x2, waiting for transfers between devices, last_pieces(): mine = lax.all_to_all(cut, 'shard', split_axis=0, concat_axis=0, tiled=True)  27.4 us
  transfers between devices with their start and end apart: 72, of which 30 were waited for; matrix products, arithmetic and copies ran while one was open for 22% of the time, Pallas kernels for 25%

profile of v4, /device:TPU:0, one launch (start us, length us, event | category | flops | bytes accessed | tf_op | source)
XLA Modules:
  0.0 684.6 jit_solution(12486256127533038638)
XLA Ops:
  5.2 7.3 %all-to-all-start = ((bf16[136,16,256]{2,1,0:T(8,128)(2,1)}), bf16[136,16,256]{2,1,0:T(8,128)(2,1)S(1)}, u32[]{:S(2)}, u32[]{:S(2)}) async-start(bf16[136,16,256]{2,1,0:T(8,128)(2,1)} %bitcast.4), calls=%async_computation | async-start | bytes 2228224 | tf_op jit(solution)/shard_map/all_to_all | solution.py:271
  12.6 27.0 %all-to-all-done = bf16[136,16,256]{2,1,0:T(8,128)(2,1)S(1)} async-done(((bf16[136,16,256]{2,1,0:T(8,128)(2,1)}), bf16[136,16,256]{2,1,0:T(8,128)(2,1)S(1)}, u32[]{:S(2)}, u32[]{:S(2)}) %all-to-all-start) | async-done | bytes 1114144 | tf_op jit(solution)/shard_map/all_to_all | solution.py:271
  40.4 10.6 %collective-permute-done.2 = bf16[1,24,16,256]{3,2,1,0:T(8,128)(2,1)S(1)} collective-permute-done((bf16[1,24,16,256]{3,2,1,0:T(8,128)(2,1)S(1)}, bf16[1,24,16,256]{3,2,1,0:T(8,128)(2,1)S(1)}, u32[]{:S(2)}, u32[]{:S(2)}) %collective-permute-start.2) | collective-permute-done | bytes 196640 | tf_op jit(solution)/shard_map/ppermute | solution.py:105
  52.7 6.3 collective-permute-done.3
  62.2 14.0 %collective-permute-done.5 = bf16[1,40,16,256]{3,2,1,0:T(8,128)(2,1)S(1)} collective-permute-done((bf16[1,40,16,256]{3,2,1,0:T(8,128)(2,1)S(1)}, bf16[1,40,16,256]{3,2,1,0:T(8,128)(2,1)S(1)}, u32[]{:S(2)}, u32[]{:S(2)}) %collective-permute-start.5) | collective-permute-done | bytes 327712 | tf_op jit(solution)/shard_map/ppermute | solution.py:105
  93.2 9.8 %collective-permute-done.8 = bf16[2,40,16,256]{3,2,1,0:T(8,128)(2,1)} collective-permute-done((bf16[2,40,16,256]{3,2,1,0:T(8,128)(2,1)}, bf16[2,40,16,256]{3,2,1,0:T(8,128)(2,1)}, u32[]{:S(2)}, u32[]{:S(2)}) %collective-permute-start.8) | collective-permute-done | bytes 655392 | tf_op jit(solution)/shard_map/ppermute | solution.py:105
  109.1 8.6 %place.4 = (bf16[4,256,1024]{2,1,0:T(8,128)(2,1)}, bf16[4,256,1024]{2,1,0:T(8,128)(2,1)}, bf16[4,256,1024]{2,1,0:T(8,128)(2,1)}) custom-call(s32[41]{0:T(128)} %add_add_fusion.4.s, bf16[8,24,16,256]{3,2,1,0:T(8,128)(2,1)} %copy-done.14, bf16[8,24,16,256]{3,2,1,0:T(8,128)(2,1)} %collective-permute-done.6.refs_1_, ...), custom_call_target="tpu_custom_call" | custom-call | flops 1048576 | bytes 1048576 | tf_op jit(solution)/shard_map/place/pallas_call | solution.py:227
  119.3 4.0 add_convert_fusion.8.q_ref
  137.2 20.1 %attend_forward.2 = (bf16[512,1024]{1,0:T(8,128)(2,1)}, f32[512,128]{1,0:T(8,128)}) custom-call(s32[1]{0:T(128)} %dynamic_slice.97.lim, bf16[512,1024]{1,0:T(8,128)(2,1)} %add_convert_fusion.8.q_ref, bf16[512,1024]{1,0:T(8,128)(2,1)} %convolution_convert_fusion.2.k_ref, bf16[512,1024]{1,0:T(8,128)(2,1)} %add_convert_fusion.7.v_ref), custom_call_target="tpu_custom_call" | custom-call | flops 1048576 | bytes 1048576 | tf_op jit(solution)/shard_map/attend_forward/pallas_call | solution.py:376
  160.6 3.7 collective-permute-done.17
  166.6 3.0 pad_maximum_fusion.1.refs_0_
  172.2 5.2 all-to-all-start.1
  180.4 10.3 %place.5 = (bf16[4,256,1024]{2,1,0:T(8,128)(2,1)}, bf16[4,256,1024]{2,1,0:T(8,128)(2,1)}, bf16[4,256,1024]{2,1,0:T(8,128)(2,1)}, bf16[4,256,1024]{2,1,0:T(8,128)(2,1)}, bf16[4,256,1024]{2,1,0:T(8,128)(2,1)}) custom-call(s32[41]{0:T(128)} %add_add_fusion.5.s, bf16[8,40,16,256]{3,2,1,0:T(8,128)(2,1)} %copy-done.4, ...), custom_call_target="tpu_custom_call" | custom-call | flops 1048576 | bytes 1048576 | tf_op jit(solution)/shard_map/place/pallas_call | solution.py:227
  190.7 3.5 fusion.23
  197.0 3.7 add_convert_fusion.6.q_ref
  203.5 9.0 %attend_forward.3 = (bf16[512,1024]{1,0:T(8,128)(2,1)}, f32[512,128]{1,0:T(8,128)}) custom-call(s32[1]{0:T(128)} %dynamic_slice.97.lim, bf16[512,1024]{1,0:T(8,128)(2,1)} %add_convert_fusion.6.q_ref, bf16[128,1024]{1,0:T(8,128)(2,1)} %convolution_convert_fusion.3.k_ref, bf16[128,1024]{1,0:T(8,128)(2,1)} %fusion.4.v_ref), custom_call_target="tpu_custom_call" | custom-call | flops 1048576 | bytes 1048576 | tf_op jit(solution)/shard_map/attend_forward/pallas_call | solution.py:376
  218.7 2.8 fusion.26
  224.0 8.1 %collective-permute-done.22 = bf16[4,32,16,256]{3,2,1,0:T(8,128)(2,1)S(1)} collective-permute-done((bf16[4,32,16,256]{3,2,1,0:T(8,128)(2,1)S(1)}, bf16[4,32,16,256]{3,2,1,0:T(8,128)(2,1)S(1)}, u32[]{:S(2)}, u32[]{:S(2)}) %collective-permute-start.22) | collective-permute-done | bytes 1048608 | tf_op jit(solution)/shard_map/ppermute | solution.py:105
  232.1 2.7 pad_maximum_fusion.2.refs_0_
  238.0 5.9 all-to-all-start.2
  245.2 9.6 %place.6 = bf16[4,256,4096]{2,1,0:T(8,128)(2,1)} custom-call(s32[41]{0:T(128)} %add_add_fusion.6.s, bf16[8,32,16,256]{3,2,1,0:T(8,128)(2,1)} %pad_maximum_fusion.1.refs_0_, bf16[8,32,16,256]{3,2,1,0:T(8,128)(2,1)} %collective-permute-done.20.refs_1_, bf16[8,32,16,256]{3,2,1,0:T(8,128)(2,1)} %collective-permute-done.21.refs_2_, ...), custom_call_target="tpu_custom_call" | custom-call | flops 1048576 | bytes 1048576 | tf_op jit(solution)/shard_map/place/pallas_call | solution.py:227
  254.8 19.1 %gelu_forward.1 = (bf16[512,4096]{1,0:T(8,128)(2,1)}, bf16[512,4096]{1,0:T(8,128)(2,1)}) custom-call(bf16[512,1024]{1,0:T(8,128)(2,1)} %get-tuple-element.190.h_ref.x_own, bf16[1024,4096]{1,0:T(8,128)(2,1)} %bitcast.243, f32[1,4096]{1,0:T(1,128)} %bitcast.295), custom_call_target="tpu_custom_call" | custom-call | flops 1048576 | bytes 1048576 | tf_op jit(solution)/shard_map/gelu_forward/pallas_call | solution.py:509
  274.0 6.7 all-to-all-done.2
  283.8 9.6 %place.7 = bf16[16,256,1024]{2,1,0:T(8,128)(2,1)} custom-call(s32[41]{0:T(128)} %add_add_fusion.7.s, bf16[8,32,16,256]{3,2,1,0:T(8,128)(2,1)} %pad_maximum_fusion.2.refs_0_, bf16[8,32,16,256]{3,2,1,0:T(8,128)(2,1)} %collective-permute-done.24.refs_1_, bf16[8,32,16,256]{3,2,1,0:T(8,128)(2,1)} %collective-permute-done.25.refs_2_, ...), custom_call_target="tpu_custom_call" | custom-call | flops 1048576 | bytes 1048576 | tf_op jit(solution)/shard_map/place/pallas_call | solution.py:227
  293.3 8.3 %fusion.27 = f32[512,1024]{1,0:T(8,128)S(1)} fusion(bf16[512,4096]{1,0:T(8,128)(2,1)} %get-tuple-element.196.x_own, bf16[4096,1024]{1,0:T(8,128)(2,1)} %bitcast.246), kind=kOutput, calls=%fused_computation.239 | convolution fusion | flops 4294967296 | bytes 14680064 | tf_op jit(solution)/shard_map/dot_general | solution.py:43
  306.9 8.1 %multiply_convert_fusion.refs_0_ = bf16[512,4096]{1,0:T(8,128)(2,1)} fusion(bf16[512,4096]{1,0:T(8,128)(2,1)} %get-tuple-element.200, bf16[512,1024]{1,0:T(8,128)(2,1)S(1)} %convert_element_type.379.refs_0_, bf16[4096,1024]{1,0:T(8,128)(2,1)S(1)} %bitcast.249), kind=kOutput, calls=%fused_computation.6 | convolution fusion | flops 4301258752 | bytes 17825792 | tf_op jit(solution)/shard_map/dot_general | solution.py:47
  317.8 8.3 %collective-permute-done.27 = bf16[512,512]{1,0:T(8,128)(2,1)} collective-permute-done((bf16[512,512]{1,0:T(8,128)(2,1)}, bf16[512,512]{1,0:T(8,128)(2,1)}, u32[]{:S(2)}, u32[]{:S(2)}) %collective-permute-start.27) | collective-permute-done | bytes 524320 | tf_op jit(solution)/shard_map/ppermute | solution.py:94
  328.8 11.0 %weight_grad.7 = (bf16[8,1,32,16,256]{4,3,2,1,0:T(8,128)(2,1)}, bf16[8,1,32,16,256]{4,3,2,1,0:T(8,128)(2,1)}) custom-call(s32[41]{0:T(128)} %add_add_fusion.7.s, bf16[512,4096]{1,0:T(8,128)(2,1)} %get-tuple-element.196.x_own, bf16[512,4096]{1,0:T(8,128)(2,1)} %collective-permute-done.30.x_sib, bf16[512,1024]{1,0:T(8,128)(2,1)} %copy-done.24, ...), custom_call_target="tpu_custom_call" | custom-call | flops 1048576 | bytes 1048576 | tf_op jit(solution)/shard_map/weight_grad/pallas_call | solution.py:566
  339.8 9.8 %weight_grad.8 = (bf16[8,1,32,16,256]{4,3,2,1,0:T(8,128)(2,1)}, bf16[8,1,32,16,256]{4,3,2,1,0:T(8,128)(2,1)}) custom-call(s32[41]{0:T(128)} %add_add_fusion.6.s, bf16[512,1024]{1,0:T(8,128)(2,1)} %get-tuple-element.190.h_ref.x_own, bf16[512,1024]{1,0:T(8,128)(2,1)} %collective-permute-done.32.x_sib, bf16[512,4096]{1,0:T(8,128)(2,1)} %multiply_convert_fusion.refs_0_, ...), custom_call_target="tpu_custom_call" | custom-call | flops 1048576 | bytes 1048576 | tf_op jit(solution)/shard_map/weight_grad/pallas_call | solution.py:566
  350.7 4.8 all-to-all-start.3
  358.9 10.9 %multiply_reduce_fusion.1 = (f32[1024]{0:T(1024)S(1)}, f32[512]{0:T(512)S(1)}, f32[512]{0:T(512)S(1)}, f32[1024]{0:T(1024)S(1)}, f32[512,1024]{1,0:T(8,128)S(1)}) fusion(f32[512,1024]{1,0:T(8,128)} %copy-done.2, f32[512]{0:T(512)S(1)} %add_rsqrt_fusion.1, f32[512]{0:T(512)S(1)} %broadcast_multiply_fusion.7, f32[1024]{0:T(1024)S(1)} %bitcast.303, ...), kind=kOutput, calls=%fused_computation.13 | convolution fusion | flops 4300207104 | bytes 18894848 | tf_op jit(solution)/shard_map/dot_general | solution.py:47
  375.2 10.4 %attend_backward.2 = (bf16[512,1024]{1,0:T(8,128)(2,1)}, bf16[128,1024]{1,0:T(8,128)(2,1)}, bf16[128,1024]{1,0:T(8,128)(2,1)}) custom-call(s32[1]{0:T(128)} %dynamic_slice.97.lim, bf16[512,1024]{1,0:T(8,128)(2,1)} %add_convert_fusion.6.q_ref, bf16[128,1024]{1,0:T(8,128)(2,1)} %convolution_convert_fusion.3.k_ref, bf16[128,1024]{1,0:T(8,128)(2,1)} %fusion.4.v_ref, ...), custom_call_target="tpu_custom_call" | custom-call | flops 1048576 | bytes 1048576 | tf_op jit(solution)/shard_map/attend_backward/pallas_call | solution.py:459
  385.6 6.6 collective-permute-done.33
  392.2 6.3 collective-permute-done.34
  398.5 4.4 multiply_reduce_fusion.2
  405.4 16.1 %collective-permute-start.35 = (bf16[512,1024]{1,0:T(8,128)(2,1)S(1)}, bf16[512,1024]{1,0:T(8,128)(2,1)S(1)}, u32[]{:S(2)}, u32[]{:S(2)}) collective-permute-start(bf16[512,1024]{1,0:T(8,128)(2,1)S(1)} %convert_element_type.384.refs_0_), channel_id=1, source_target_pairs={{0,1},{1,0},{2,3},{3,2},{4,5},{5,4},{6,7},{7,6},{8,9},{9,8},{10,11... | collective-permute-start | bytes 3145736 | tf_op jit(solution)/shard_map/ppermute | solution.py:94
  421.4 3.2 add_convert_fusion.3
  427.5 3.5 add_convert_fusion.2
  431.6 7.8 %collective-permute-done.36 = bf16[4,32,16,256]{3,2,1,0:T(8,128)(2,1)S(1)} collective-permute-done((bf16[4,32,16,256]{3,2,1,0:T(8,128)(2,1)S(1)}, bf16[4,32,16,256]{3,2,1,0:T(8,128)(2,1)S(1)}, u32[]{:S(2)}, u32[]{:S(2)}) %collective-permute-start.36) | collective-permute-done | bytes 1048608 | tf_op jit(solution)/shard_map/ppermute | solution.py:105
  443.5 2.6 add_convert_fusion.14
  447.7 4.8 weight_grad.9
  452.5 5.5 weight_grad.10
  458.0 5.3 weight_grad.11
  463.3 4.8 weight_grad.12
  469.0 2.9 gather_fusion.2
  471.8 5.5 all-to-all-start.4
  477.4 16.3 %attend_backward.3 = (bf16[512,1024]{1,0:T(8,128)(2,1)}, bf16[512,1024]{1,0:T(8,128)(2,1)}, bf16[512,1024]{1,0:T(8,128)(2,1)}) custom-call(s32[1]{0:T(128)} %dynamic_slice.97.lim, bf16[512,1024]{1,0:T(8,128)(2,1)} %add_convert_fusion.8.q_ref, bf16[512,1024]{1,0:T(8,128)(2,1)} %convolution_convert_fusion.2.k_ref, bf16[512,1024]{1,0:T(8,128)(2,1)} %add_convert_fusion.7.v_ref, ...), custom_call_target="tpu_custom_call" | custom-call | flops 1048576 | bytes 1048576 | tf_op jit(solution)/shard_map/attend_backward/pallas_call | solution.py:459
  494.7 2.5 add_convert_fusion.13
  503.3 8.6 %weight_grad.13 = (bf16[8,3,8,16,256]{4,3,2,1,0:T(8,128)(2,1)}, bf16[8,3,8,16,256]{4,3,2,1,0:T(8,128)(2,1)}) custom-call(s32[41]{0:T(128)} %add_add_fusion.8.s, bf16[512,1024]{1,0:T(8,128)(2,1)} %get-tuple-element.149.x_own, bf16[512,1024]{1,0:T(8,128)(2,1)} %get-tuple-element.241.x_sib, bf16[512,1024]{1,0:T(8,128)(2,1)} %get-tuple-element.250.refs_0_, ...), custom_call_target="tpu_custom_call" | custom-call | flops 1048576 | bytes 1048576 | tf_op jit(solution)/shard_map/weight_grad/pallas_call | solution.py:566
  511.9 3.2 collective-permute-done.50
  532.8 4.9 collective-permute-done.52
  539.1 3.3 convert_reduce_fusion
  547.1 2.5 add_convert_fusion.1
  553.0 12.3 %collective-permute-done.57 = bf16[4,24,16,256]{3,2,1,0:T(8,128)(2,1)S(1)} collective-permute-done((bf16[4,24,16,256]{3,2,1,0:T(8,128)(2,1)S(1)}, bf16[4,24,16,256]{3,2,1,0:T(8,128)(2,1)S(1)}, u32[]{:S(2)}, u32[]{:S(2)}) %collective-permute-start.57) | collective-permute-done | bytes 786464 | tf_op jit(solution)/shard_map/ppermute | solution.py:105
  571.3 5.5 collective-permute-done.58
  576.8 6.3 collective-permute-done.60
  588.1 19.0 %collective-permute-done.61 = bf16[1,24,16,256]{3,2,1,0:T(8,128)(2,1)} collective-permute-done((bf16[1,24,16,256]{3,2,1,0:T(8,128)(2,1)}, bf16[1,24,16,256]{3,2,1,0:T(8,128)(2,1)}, u32[]{:S(2)}, u32[]{:S(2)}) %collective-permute-start.61) | collective-permute-done | bytes 196640 | tf_op jit(solution)/shard_map/ppermute | solution.py:105
  610.0 4.1 all-to-all-start.5
  615.4 14.2 %all-to-all-done.5 = bf16[72,16,256]{2,1,0:T(8,128)(2,1)S(1)} async-done(((bf16[72,16,256]{2,1,0:T(8,128)(2,1)}), bf16[72,16,256]{2,1,0:T(8,128)(2,1)S(1)}, u32[]{:S(2)}, u32[]{:S(2)}) %all-to-all-start.5) | async-done | bytes 589856 | tf_op jit(solution)/shard_map/all_to_all | solution.py:327
  629.6 3.6 all-to-all-start.6
  634.6 13.3 %all-to-all-done.6 = bf16[64,16,256]{2,1,0:T(8,128)(2,1)S(1)} async-done(((bf16[64,16,256]{2,1,0:T(8,128)(2,1)}), bf16[64,16,256]{2,1,0:T(8,128)(2,1)S(1)}, u32[]{:S(2)}, u32[]{:S(2)}) %all-to-all-start.6) | async-done | bytes 524320 | tf_op jit(solution)/shard_map/all_to_all | solution.py:327
  649.0 11.2 %collective-permute-done.64.other_ref = bf16[8,8,16,256]{3,2,1,0:T(8,128)(2,1)S(1)} collective-permute-done((bf16[8,8,16,256]{3,2,1,0:T(8,128)(2,1)S(1)}, bf16[8,8,16,256]{3,2,1,0:T(8,128)(2,1)S(1)}, u32[]{:S(2)}, u32[]{:S(2)}) %collective-permute-start.64) | collective-permute-done | bytes 524320 | tf_op jit(solution)/shard_map/ppermute | solution.py:97
  661.0 11.0 %shampoo.2 = (f32[1,16,256,256]{3,2,1,0:T(8,128)}, f32[1,16,256,256]{3,2,1,0:T(8,128)}, f32[1,16,256,256]{3,2,1,0:T(8,128)}, f32[1,16,256,256]{3,2,1,0:T(8,128)}) custom-call(s32[1]{0:T(128)} %bitcast.81.flag, bf16[8,8,16,256]{3,2,1,0:T(8,128)(2,1)} %bitcast.286, bf16[8,8,16,256]{3,2,1,0:T(8,128)(2,1)} %copy-done.57, f32[1,16,256,256]{3,2,1,0:T(8,128)} %w_ref.3, ...), custom_call_target="tpu_custom_call" | custom-call | flops 1048576 | bytes 1048576 | tf_op jit(solution)/shard_map/shampoo/pallas_call | solution.py:621
  673.4 10.9 %shampoo.3 = (f32[1,16,256,256]{3,2,1,0:T(8,128)}, f32[1,16,256,256]{3,2,1,0:T(8,128)}, f32[1,16,256,256]{3,2,1,0:T(8,128)}, f32[1,16,256,256]{3,2,1,0:T(8,128)}) custom-call(s32[1]{0:T(128)} %bitcast.81.flag, bf16[8,9,16,256]{3,2,1,0:T(8,128)(2,1)} %bitcast.278, ...), custom_call_target="tpu_custom_call", output_to_operand_aliasing={{0}: (8, {}), {1}: (9, {}), {2}: (10, {}), {3}: (11, {})} | custom-call | flops 1048576 | bytes 1048576 | tf_op jit(solution)/shard_map/shampoo/pallas_call | solution.py:621
  (482 shorter events, 168.5 us)
Async XLA Ops:
  5.2 34.5 %all-to-all-start = ((bf16[136,16,256]{2,1,0:T(8,128)(2,1)}), bf16[136,16,256]{2,1,0:T(8,128)(2,1)S(1)}, u32[]{:S(2)}, u32[]{:S(2)}) async-start(bf16[136,16,256]{2,1,0:T(8,128)(2,1)} %bitcast.4), calls=%async_computation | async-start | bytes 2228224 | tf_op jit(solution)/shard_map/all_to_all | solution.py:271
  40.3 10.7 %collective-permute-start.2 = (bf16[1,24,16,256]{3,2,1,0:T(8,128)(2,1)S(1)}, bf16[1,24,16,256]{3,2,1,0:T(8,128)(2,1)S(1)}, u32[]{:S(2)}, u32[]{:S(2)}) collective-permute-start(bf16[1,24,16,256]{3,2,1,0:T(8,128)(2,1)S(1)} %bitcast.272), channel_id=1, source_target_pairs={{0,8},{1,9},{2,10},{3,11},{4,12},{5,13},{6,14},{7,15},{8,0},{9,1},... | collective-permute-start | bytes 589832 | tf_op jit(solution)/shard_map/ppermute | solution.py:105
  59.9 19.3 %collective-permute-start.4 = (bf16[4,24,16,256]{3,2,1,0:T(8,128)(2,1)}, bf16[4,24,16,256]{3,2,1,0:T(8,128)(2,1)}, u32[]{:S(2)}, u32[]{:S(2)}) collective-permute-start(bf16[4,24,16,256]{3,2,1,0:T(8,128)(2,1)} %pad_maximum_fusion.14), channel_id=1, source_target_pairs={{0,4},{1,3},{2,6},{3,1},{4,0},{5,7},{6,2},{7,5},{8,12},{9,11},{10,... | collective-permute-start | bytes 2359304 | tf_op jit(solution)/shard_map/ppermute | solution.py:105
  59.9 16.3 %collective-permute-start.5 = (bf16[1,40,16,256]{3,2,1,0:T(8,128)(2,1)S(1)}, bf16[1,40,16,256]{3,2,1,0:T(8,128)(2,1)S(1)}, u32[]{:S(2)}, u32[]{:S(2)}) collective-permute-start(bf16[1,40,16,256]{3,2,1,0:T(8,128)(2,1)S(1)} %bitcast.254), channel_id=1, source_target_pairs={{0,8},{1,9},{2,10},{3,11},{4,12},{5,13},{6,14},{7,15},{8,0},{9,1},... | collective-permute-start | bytes 983048 | tf_op jit(solution)/shard_map/ppermute | solution.py:105
  61.7 23.9 %collective-permute-start = (bf16[2,512,512]{2,1,0:T(8,128)(2,1)}, bf16[2,512,512]{2,1,0:T(8,128)(2,1)}, u32[]{:S(2)}, u32[]{:S(2)}) collective-permute-start(bf16[2,512,512]{2,1,0:T(8,128)(2,1)} %param.21), channel_id=1, source_target_pairs={{0,1},{1,0},{2,3},{3,2},{4,5},{5,4},{6,7},{7,6},{8,9},{9,8},{10,11... | collective-permute-start | bytes 3145736 | tf_op jit(solution)/shard_map/ppermute | solution.py:94
  61.7 21.0 %collective-permute-start.1 = (bf16[2,128,512]{2,1,0:T(8,128)(2,1)}, bf16[2,128,512]{2,1,0:T(8,128)(2,1)}, u32[]{:S(2)}, u32[]{:S(2)}) collective-permute-start(bf16[2,128,512]{2,1,0:T(8,128)(2,1)} %param.22), channel_id=1, source_target_pairs={{0,1},{1,0},{2,3},{3,2},{4,5},{5,4},{6,7},{7,6},{8,9},{9,8},{10,11... | collective-permute-start | bytes 786440 | tf_op jit(solution)/shard_map/ppermute | solution.py:94
  80.7 22.3 %collective-permute-start.6 = (bf16[8,24,16,256]{3,2,1,0:T(8,128)(2,1)S(1)}, bf16[8,24,16,256]{3,2,1,0:T(8,128)(2,1)}, u32[]{:S(2)}, u32[]{:S(2)}) collective-permute-start(bf16[8,24,16,256]{3,2,1,0:T(8,128)(2,1)S(1)} %pad_maximum_fusion.3.refs_0_), channel_id=1, source_target_pairs={{0,2},{1,17},{2,0},{3,19},{4,6},{5,21},{6,4},{7,23},{8,10},{9,25},... | collective-permute-start | bytes 4718600 | tf_op jit(solution)/shard_map/ppermute | solution.py:105
  82.0 21.0 %collective-permute-start.7 = (bf16[8,24,16,256]{3,2,1,0:T(8,128)(2,1)S(1)}, bf16[8,24,16,256]{3,2,1,0:T(8,128)(2,1)}, u32[]{:S(2)}, u32[]{:S(2)}) collective-permute-start(bf16[8,24,16,256]{3,2,1,0:T(8,128)(2,1)S(1)} %pad_maximum_fusion.3.refs_0_), channel_id=1, source_target_pairs={{0,1},{1,0},{2,3},{3,2},{4,5},{5,4},{6,7},{7,6},{8,9},{9,8},{10,11... | collective-permute-start | bytes 4718600 | tf_op jit(solution)/shard_map/ppermute | solution.py:94
  85.5 17.5 %collective-permute-start.8 = (bf16[2,40,16,256]{3,2,1,0:T(8,128)(2,1)}, bf16[2,40,16,256]{3,2,1,0:T(8,128)(2,1)}, u32[]{:S(2)}, u32[]{:S(2)}) collective-permute-start(bf16[2,40,16,256]{3,2,1,0:T(8,128)(2,1)} %pad_maximum_fusion.15), channel_id=1, source_target_pairs={{0,4},{1,5},{2,6},{3,7},{4,0},{5,1},{6,2},{7,3},{8,12},{9,13},{10,... | collective-permute-start | bytes 1966088 | tf_op jit(solution)/shard_map/ppermute | solution.py:105
  103.5 14.5 %collective-permute-start.10 = (bf16[1,32,16,256]{3,2,1,0:T(8,128)(2,1)S(1)}, bf16[1,32,16,256]{3,2,1,0:T(8,128)(2,1)S(1)}, u32[]{:S(2)}, u32[]{:S(2)}) collective-permute-start(bf16[1,32,16,256]{3,2,1,0:T(8,128)(2,1)S(1)} %bitcast.268), channel_id=1, source_target_pairs={{0,8},{1,9},{2,10},{3,11},{4,12},{5,13},{6,14},{7,15},{8,0},{9,1},... | collective-permute-start | bytes 786440 | tf_op jit(solution)/shard_map/ppermute | solution.py:105
  106.3 21.5 %collective-permute-start.12 = (bf16[4,40,16,256]{3,2,1,0:T(8,128)(2,1)}, bf16[4,40,16,256]{3,2,1,0:T(8,128)(2,1)}, u32[]{:S(2)}, u32[]{:S(2)}) collective-permute-start(bf16[4,40,16,256]{3,2,1,0:T(8,128)(2,1)} %pad_maximum_fusion.4), channel_id=1, source_target_pairs={{0,16},{1,3},{2,18},{3,1},{4,20},{5,7},{6,22},{7,5},{8,24},{9,11},... | collective-permute-start | bytes 3932168 | tf_op jit(solution)/shard_map/ppermute | solution.py:105
  118.1 10.5 %collective-permute-start.13 = (bf16[2,32,16,256]{3,2,1,0:T(8,128)(2,1)S(1)}, bf16[2,32,16,256]{3,2,1,0:T(8,128)(2,1)S(1)}, u32[]{:S(2)}, u32[]{:S(2)}) collective-permute-start(bf16[2,32,16,256]{3,2,1,0:T(8,128)(2,1)S(1)} %pad_maximum_fusion.17), channel_id=1, source_target_pairs={{0,2},{1,17},{2,0},{3,19},{4,6},{5,21},{6,4},{7,23},{8,10},{9,25},... | collective-permute-start | bytes 1572872 | tf_op jit(solution)/shard_map/ppermute | solution.py:105
  130.5 34.8 %collective-permute-start.14 = (bf16[8,40,16,256]{3,2,1,0:T(8,128)(2,1)S(1)}, bf16[8,40,16,256]{3,2,1,0:T(8,128)(2,1)}, u32[]{:S(2)}, u32[]{:S(2)}) collective-permute-start(bf16[8,40,16,256]{3,2,1,0:T(8,128)(2,1)S(1)} %pad_maximum_fusion.refs_0_), channel_id=1, source_target_pairs={{0,2},{1,17},{2,0},{3,19},{4,6},{5,21},{6,4},{7,23},{8,10},{9,25},... | collective-permute-start | bytes 7864328 | tf_op jit(solution)/shard_map/ppermute | solution.py:105
  131.9 33.3 %collective-permute-start.15 = (bf16[8,40,16,256]{3,2,1,0:T(8,128)(2,1)S(1)}, bf16[8,40,16,256]{3,2,1,0:T(8,128)(2,1)}, u32[]{:S(2)}, u32[]{:S(2)}) collective-permute-start(bf16[8,40,16,256]{3,2,1,0:T(8,128)(2,1)S(1)} %pad_maximum_fusion.refs_0_), channel_id=1, source_target_pairs={{0,1},{1,0},{2,3},{3,2},{4,5},{5,4},{6,7},{7,6},{8,9},{9,8},{10,11... | collective-permute-start | bytes 7864328 | tf_op jit(solution)/shard_map/ppermute | solution.py:94
  133.9 31.4 %collective-permute-start.16 = (bf16[4,32,16,256]{3,2,1,0:T(8,128)(2,1)}, bf16[4,32,16,256]{3,2,1,0:T(8,128)(2,1)}, u32[]{:S(2)}, u32[]{:S(2)}) collective-permute-start(bf16[4,32,16,256]{3,2,1,0:T(8,128)(2,1)} %pad_maximum_fusion.8), channel_id=1, source_target_pairs={{0,4},{1,5},{2,6},{3,7},{4,0},{5,1},{6,2},{7,3},{8,12},{9,13},{10,... | collective-permute-start | bytes 3145736 | tf_op jit(solution)/shard_map/ppermute | solution.py:105
  136.0 28.4 %collective-permute-start.17 = (bf16[1,32,16,256]{3,2,1,0:T(8,128)(2,1)S(1)}, bf16[1,32,16,256]{3,2,1,0:T(8,128)(2,1)}, u32[]{:S(2)}, u32[]{:S(2)}) collective-permute-start(bf16[1,32,16,256]{3,2,1,0:T(8,128)(2,1)S(1)} %bitcast.264), channel_id=1, source_target_pairs={{0,8},{1,9},{2,10},{3,11},{4,12},{5,13},{6,14},{7,15},{8,0},{9,1},... | collective-permute-start | bytes 786440 | tf_op jit(solution)/shard_map/ppermute | solution.py:105
  165.2 15.2 %collective-permute-start.18 = (bf16[8,40,16,256]{3,2,1,0:T(8,128)(2,1)}, bf16[8,40,16,256]{3,2,1,0:T(8,128)(2,1)}, u32[]{:S(2)}, u32[]{:S(2)}) collective-permute-start(bf16[8,40,16,256]{3,2,1,0:T(8,128)(2,1)} %collective-permute-done.14.refs_1_), channel_id=1, source_target_pairs={{0,1},{1,0},{2,3},{3,2},{4,5},{5,4},{6,7},{7,6},{8,9},{9,8},{10,11... | collective-permute-start | bytes 7864328 | tf_op jit(solution)/shard_map/ppermute | solution.py:94
  169.7 54.3 %collective-permute-start.20 = (bf16[8,32,16,256]{3,2,1,0:T(8,128)(2,1)}, bf16[8,32,16,256]{3,2,1,0:T(8,128)(2,1)}, u32[]{:S(2)}, u32[]{:S(2)}) collective-permute-start(bf16[8,32,16,256]{3,2,1,0:T(8,128)(2,1)} %pad_maximum_fusion.1.refs_0_), channel_id=1, source_target_pairs={{0,16},{1,3},{2,18},{3,1},{4,20},{5,7},{6,22},{7,5},{8,24},{9,11},... | collective-permute-start | bytes 6291464 | tf_op jit(solution)/shard_map/ppermute | solution.py:105
  170.6 53.4 %collective-permute-start.21 = (bf16[8,32,16,256]{3,2,1,0:T(8,128)(2,1)}, bf16[8,32,16,256]{3,2,1,0:T(8,128)(2,1)}, u32[]{:S(2)}, u32[]{:S(2)}) collective-permute-start(bf16[8,32,16,256]{3,2,1,0:T(8,128)(2,1)} %pad_maximum_fusion.1.refs_0_), channel_id=1, source_target_pairs={{0,1},{1,0},{2,3},{3,2},{4,5},{5,4},{6,7},{7,6},{8,9},{9,8},{10,11... | collective-permute-start | bytes 6291464 | tf_op jit(solution)/shard_map/ppermute | solution.py:94
  172.2 43.7 %all-to-all-start.1 = ((bf16[2,16,32,512]{3,2,0,1:T(8,128)(2,1)}), bf16[2,16,32,512]{3,2,0,1:T(8,128)(2,1)S(1)}, u32[]{:S(2)}, u32[]{:S(2)}) async-start(bf16[2,16,32,512]{3,2,0,1:T(8,128)(2,1)} %copy.66), calls=%async_computation.1 | async-start | bytes 2097152 | tf_op jit(solution)/shard_map/all_to_all | solution.py:663
  178.4 25.1 %collective-permute-start.19 = (bf16[2,32,16,256]{3,2,1,0:T(8,128)(2,1)S(1)}, bf16[2,32,16,256]{3,2,1,0:T(8,128)(2,1)}, u32[]{:S(2)}, u32[]{:S(2)}) collective-permute-start(bf16[2,32,16,256]{3,2,1,0:T(8,128)(2,1)S(1)} %pad_maximum_fusion.18), channel_id=1, source_target_pairs={{0,2},{1,17},{2,0},{3,19},{4,6},{5,21},{6,4},{7,23},{8,10},{9,25},... | collective-permute-start | bytes 1572872 | tf_op jit(solution)/shard_map/ppermute | solution.py:105
  217.2 14.9 %collective-permute-start.22 = (bf16[4,32,16,256]{3,2,1,0:T(8,128)(2,1)S(1)}, bf16[4,32,16,256]{3,2,1,0:T(8,128)(2,1)S(1)}, u32[]{:S(2)}, u32[]{:S(2)}) collective-permute-start(bf16[4,32,16,256]{3,2,1,0:T(8,128)(2,1)S(1)} %pad_maximum_fusion.9), channel_id=1, source_target_pairs={{0,16},{1,5},{2,18},{3,7},{4,20},{5,1},{6,22},{7,3},{8,24},{9,13},... | collective-permute-start | bytes 3145736 | tf_op jit(solution)/shard_map/ppermute | solution.py:105
  232.1 13.1 %collective-permute-start.23 = (bf16[8,32,16,256]{3,2,1,0:T(8,128)(2,1)}, bf16[8,32,16,256]{3,2,1,0:T(8,128)(2,1)}, u32[]{:S(2)}, u32[]{:S(2)}) collective-permute-start(bf16[8,32,16,256]{3,2,1,0:T(8,128)(2,1)} %collective-permute-done.20.refs_1_), channel_id=1, source_target_pairs={{0,1},{1,0},{2,3},{3,2},{4,5},{5,4},{6,7},{7,6},{8,9},{9,8},{10,11... | collective-permute-start | bytes 6291464 | tf_op jit(solution)/shard_map/ppermute | solution.py:94
  234.8 39.1 %collective-permute-start.24 = (bf16[8,32,16,256]{3,2,1,0:T(8,128)(2,1)}, bf16[8,32,16,256]{3,2,1,0:T(8,128)(2,1)}, u32[]{:S(2)}, u32[]{:S(2)}) collective-permute-start(bf16[8,32,16,256]{3,2,1,0:T(8,128)(2,1)} %pad_maximum_fusion.2.refs_0_), channel_id=1, source_target_pairs={{0,4},{1,3},{2,6},{3,1},{4,0},{5,7},{6,2},{7,5},{8,12},{9,11},{10,... | collective-permute-start | bytes 6291464 | tf_op jit(solution)/shard_map/ppermute | solution.py:105
  236.3 37.6 %collective-permute-start.25 = (bf16[8,32,16,256]{3,2,1,0:T(8,128)(2,1)}, bf16[8,32,16,256]{3,2,1,0:T(8,128)(2,1)}, u32[]{:S(2)}, u32[]{:S(2)}) collective-permute-start(bf16[8,32,16,256]{3,2,1,0:T(8,128)(2,1)} %pad_maximum_fusion.2.refs_0_), channel_id=1, source_target_pairs={{0,1},{1,0},{2,3},{3,2},{4,5},{5,4},{6,7},{7,6},{8,9},{9,8},{10,11... | collective-permute-start | bytes 6291464 | tf_op jit(solution)/shard_map/ppermute | solution.py:94
  238.0 42.7 %all-to-all-start.2 = ((bf16[32,1,32,512]{3,2,1,0:T(8,128)(2,1)}), bf16[32,1,32,512]{3,2,1,0:T(8,128)(2,1)S(1)}, u32[]{:S(2)}, u32[]{:S(2)}) async-start(bf16[32,1,32,512]{3,2,1,0:T(8,128)(2,1)} %bitcast.260), calls=%async_computation.2 | async-start | bytes 2097152 | tf_op jit(solution)/shard_map/all_to_all | solution.py:668
  273.9 9.9 %collective-permute-start.26 = (bf16[8,32,16,256]{3,2,1,0:T(8,128)(2,1)}, bf16[8,32,16,256]{3,2,1,0:T(8,128)(2,1)}, u32[]{:S(2)}, u32[]{:S(2)}) collective-permute-start(bf16[8,32,16,256]{3,2,1,0:T(8,128)(2,1)} %collective-permute-done.24.refs_1_), channel_id=1, source_target_pairs={{0,1},{1,0},{2,3},{3,2},{4,5},{5,4},{6,7},{7,6},{8,9},{9,8},{10,11... | collective-permute-start | bytes 6291464 | tf_op jit(solution)/shard_map/ppermute | solution.py:94
  283.6 45.2 %collective-permute-start.30 = (bf16[512,4096]{1,0:T(8,128)(2,1)}, bf16[512,4096]{1,0:T(8,128)(2,1)}, u32[]{:S(2)}, u32[]{:S(2)}) collective-permute-start(bf16[512,4096]{1,0:T(8,128)(2,1)} %get-tuple-element.196.x_own), channel_id=1, source_target_pairs={{0,1},{1,0},{2,3},{3,2},{4,5},{5,4},{6,7},{7,6},{8,9},{9,8},{10,11... | collective-permute-start | bytes 12582920 | tf_op jit(solution)/shard_map/ppermute | solution.py:94
  314.9 24.9 %collective-permute-start.29 = (bf16[512,4096]{1,0:T(8,128)(2,1)}, bf16[512,4096]{1,0:T(8,128)(2,1)}, u32[]{:S(2)}, u32[]{:S(2)}) collective-permute-start(bf16[512,4096]{1,0:T(8,128)(2,1)} %multiply_convert_fusion.refs_0_), channel_id=1, source_target_pairs={{0,1},{1,0},{2,3},{3,2},{4,5},{5,4},{6,7},{7,6},{8,9},{9,8},{10,11... | collective-permute-start | bytes 12582920 | tf_op jit(solution)/shard_map/ppermute | solution.py:94
  314.9 24.9 %collective-permute-start.32 = (bf16[512,1024]{1,0:T(8,128)(2,1)S(1)}, bf16[512,1024]{1,0:T(8,128)(2,1)}, u32[]{:S(2)}, u32[]{:S(2)}) collective-permute-start(bf16[512,1024]{1,0:T(8,128)(2,1)S(1)} %copy-done.6), channel_id=1, source_target_pairs={{0,1},{1,0},{2,3},{3,2},{4,5},{5,4},{6,7},{7,6},{8,9},{9,8},{10,11... | collective-permute-start | bytes 3145736 | tf_op jit(solution)/shard_map/ppermute | solution.py:94
  315.4 13.4 %collective-permute-start.31 = (bf16[512,1024]{1,0:T(8,128)(2,1)}, bf16[512,1024]{1,0:T(8,128)(2,1)}, u32[]{:S(2)}, u32[]{:S(2)}) collective-permute-start(bf16[512,1024]{1,0:T(8,128)(2,1)} %copy-done.24), channel_id=1, source_target_pairs={{0,1},{1,0},{2,3},{3,2},{4,5},{5,4},{6,7},{7,6},{8,9},{9,8},{10,11... | collective-permute-start | bytes 3145736 | tf_op jit(solution)/shard_map/ppermute | solution.py:94
  317.4 8.8 %collective-permute-start.27 = (bf16[512,512]{1,0:T(8,128)(2,1)}, bf16[512,512]{1,0:T(8,128)(2,1)}, u32[]{:S(2)}, u32[]{:S(2)}) collective-permute-start(bf16[512,512]{1,0:T(8,128)(2,1)} %constant_dynamic-slice_fusion.3), channel_id=1, source_target_pairs={{0,1},{1,0},{2,3},{3,2},{4,5},{5,4},{6,7},{7,6},{8,9},{9,8},{10,11... | collective-permute-start | bytes 1572872 | tf_op jit(solution)/shard_map/ppermute | solution.py:94
  326.2 104.8 %collective-permute-start.43 = (bf16[512,1024]{1,0:T(8,128)(2,1)}, bf16[512,1024]{1,0:T(8,128)(2,1)}, u32[]{:S(2)}, u32[]{:S(2)}) collective-permute-start(bf16[512,1024]{1,0:T(8,128)(2,1)} %get-tuple-element.170.x_own.o_ref), channel_id=1, source_target_pairs={{0,1},{1,0},{2,3},{3,2},{4,5},{5,4},{6,7},{7,6},{8,9},{9,8},{10,11... | collective-permute-start | bytes 3145736 | tf_op jit(solution)/shard_map/ppermute | solution.py:94
  350.7 92.5 %all-to-all-start.3 = ((bf16[2,16,32,512]{3,2,0,1:T(8,128)(2,1)}), bf16[2,16,32,512]{3,2,0,1:T(8,128)(2,1)}, u32[]{:S(2)}, u32[]{:S(2)}) async-start(bf16[2,16,32,512]{3,2,0,1:T(8,128)(2,1)} %copy.70), calls=%async_computation.3 | async-start | bytes 2097152 | tf_op jit(solution)/shard_map/all_to_all | solution.py:663
  355.4 36.7 %collective-permute-start.33 = (bf16[8,32,16,256]{3,2,1,0:T(8,128)(2,1)}, bf16[8,32,16,256]{3,2,1,0:T(8,128)(2,1)}, u32[]{:S(2)}, u32[]{:S(2)}) collective-permute-start(bf16[8,32,16,256]{3,2,1,0:T(8,128)(2,1)} %bitcast.327), channel_id=1, source_target_pairs={{0,16},{1,3},{2,18},{3,1},{4,20},{5,7},{6,22},{7,5},{8,24},{9,11},... | collective-permute-start | bytes 6291464 | tf_op jit(solution)/shard_map/ppermute | solution.py:105
  357.5 41.1 %collective-permute-start.34 = (bf16[8,32,16,256]{3,2,1,0:T(8,128)(2,1)}, bf16[8,32,16,256]{3,2,1,0:T(8,128)(2,1)}, u32[]{:S(2)}, u32[]{:S(2)}) collective-permute-start(bf16[8,32,16,256]{3,2,1,0:T(8,128)(2,1)} %bitcast.326), channel_id=1, source_target_pairs={{0,4},{1,3},{2,6},{3,1},{4,0},{5,7},{6,2},{7,5},{8,12},{9,11},{10,... | collective-permute-start | bytes 6291464 | tf_op jit(solution)/shard_map/ppermute | solution.py:105
  405.4 26.2 %collective-permute-start.35 = (bf16[512,1024]{1,0:T(8,128)(2,1)S(1)}, bf16[512,1024]{1,0:T(8,128)(2,1)S(1)}, u32[]{:S(2)}, u32[]{:S(2)}) collective-permute-start(bf16[512,1024]{1,0:T(8,128)(2,1)S(1)} %convert_element_type.384.refs_0_), channel_id=1, source_target_pairs={{0,1},{1,0},{2,3},{3,2},{4,5},{5,4},{6,7},{7,6},{8,9},{9,8},{10,11... | collective-permute-start | bytes 3145736 | tf_op jit(solution)/shard_map/ppermute | solution.py:94
  424.6 14.8 %collective-permute-start.36 = (bf16[4,32,16,256]{3,2,1,0:T(8,128)(2,1)S(1)}, bf16[4,32,16,256]{3,2,1,0:T(8,128)(2,1)S(1)}, u32[]{:S(2)}, u32[]{:S(2)}) collective-permute-start(bf16[4,32,16,256]{3,2,1,0:T(8,128)(2,1)S(1)} %get-tuple-element.313), channel_id=1, source_target_pairs={{0,16},{1,5},{2,18},{3,7},{4,20},{5,1},{6,22},{7,3},{8,24},{9,13},... | collective-permute-start | bytes 3145736 | tf_op jit(solution)/shard_map/ppermute | solution.py:105
  426.1 17.0 %collective-permute-start.41 = (bf16[512,1024]{1,0:T(8,128)(2,1)}, bf16[512,1024]{1,0:T(8,128)(2,1)}, u32[]{:S(2)}, u32[]{:S(2)}) collective-permute-start(bf16[512,1024]{1,0:T(8,128)(2,1)} %fusion.3.x_own), channel_id=1, source_target_pairs={{0,1},{1,0},{2,3},{3,2},{4,5},{5,4},{6,7},{7,6},{8,9},{9,8},{10,11... | collective-permute-start | bytes 3145736 | tf_op jit(solution)/shard_map/ppermute | solution.py:94
  427.5 19.3 %collective-permute-start.42 = (bf16[512,1024]{1,0:T(8,128)(2,1)}, bf16[512,1024]{1,0:T(8,128)(2,1)}, u32[]{:S(2)}, u32[]{:S(2)}) collective-permute-start(bf16[512,1024]{1,0:T(8,128)(2,1)} %get-tuple-element.256.refs_0_), channel_id=1, source_target_pairs={{0,1},{1,0},{2,3},{3,2},{4,5},{5,4},{6,7},{7,6},{8,9},{9,8},{10,11... | collective-permute-start | bytes 3145736 | tf_op jit(solution)/shard_map/ppermute | solution.py:94
  431.0 32.3 %collective-permute-start.37 = (bf16[512,1024]{1,0:T(8,128)(2,1)}, bf16[512,1024]{1,0:T(8,128)(2,1)}, u32[]{:S(2)}, u32[]{:S(2)}) collective-permute-start(bf16[512,1024]{1,0:T(8,128)(2,1)} %get-tuple-element.185.o_ref.x_own), channel_id=1, source_target_pairs={{0,1},{1,0},{2,3},{3,2},{4,5},{5,4},{6,7},{7,6},{8,9},{9,8},{10,11... | collective-permute-start | bytes 3145736 | tf_op jit(solution)/shard_map/ppermute | solution.py:94
  431.5 31.8 %collective-permute-start.38 = (bf16[512,1024]{1,0:T(8,128)(2,1)S(1)}, bf16[512,1024]{1,0:T(8,128)(2,1)}, u32[]{:S(2)}, u32[]{:S(2)}) collective-permute-start(bf16[512,1024]{1,0:T(8,128)(2,1)S(1)} %convert_element_type.382.refs_0_), channel_id=1, source_target_pairs={{0,1},{1,0},{2,3},{3,2},{4,5},{5,4},{6,7},{7,6},{8,9},{9,8},{10,11... | collective-permute-start | bytes 3145736 | tf_op jit(solution)/shard_map/ppermute | solution.py:94
  439.4 28.7 %collective-permute-start.44 = (bf16[4,32,16,256]{3,2,1,0:T(8,128)(2,1)}, bf16[4,32,16,256]{3,2,1,0:T(8,128)(2,1)}, u32[]{:S(2)}, u32[]{:S(2)}) collective-permute-start(bf16[4,32,16,256]{3,2,1,0:T(8,128)(2,1)} %get-tuple-element.311), channel_id=1, source_target_pairs={{0,4},{1,5},{2,6},{3,7},{4,0},{5,1},{6,2},{7,3},{8,12},{9,13},{10,... | collective-permute-start | bytes 3145736 | tf_op jit(solution)/shard_map/ppermute | solution.py:105
  446.1 22.0 %collective-permute-start.45 = (bf16[2,32,16,256]{3,2,1,0:T(8,128)(2,1)S(1)}, bf16[2,32,16,256]{3,2,1,0:T(8,128)(2,1)}, u32[]{:S(2)}, u32[]{:S(2)}) collective-permute-start(bf16[2,32,16,256]{3,2,1,0:T(8,128)(2,1)S(1)} %get-tuple-element.322), channel_id=1, source_target_pairs={{0,2},{1,17},{2,0},{3,19},{4,6},{5,21},{6,4},{7,23},{8,10},{9,25},... | collective-permute-start | bytes 1572872 | tf_op jit(solution)/shard_map/ppermute | solution.py:105
  446.8 11.1 %collective-permute-start.40 = (bf16[128,1024]{1,0:T(8,128)(2,1)S(1)}, bf16[128,1024]{1,0:T(8,128)(2,1)}, u32[]{:S(2)}, u32[]{:S(2)}) collective-permute-start(bf16[128,1024]{1,0:T(8,128)(2,1)S(1)} %copy-done.35), channel_id=1, source_target_pairs={{0,1},{1,0},{2,3},{3,2},{4,5},{5,4},{6,7},{7,6},{8,9},{9,8},{10,11... | collective-permute-start | bytes 786440 | tf_op jit(solution)/shard_map/ppermute | solution.py:94
  468.1 56.4 %collective-permute-start.51 = (bf16[8,40,16,256]{3,2,1,0:T(8,128)(2,1)}, bf16[8,40,16,256]{3,2,1,0:T(8,128)(2,1)}, u32[]{:S(2)}, u32[]{:S(2)}) collective-permute-start(bf16[8,40,16,256]{3,2,1,0:T(8,128)(2,1)} %bitcast.245), channel_id=1, source_target_pairs={{0,2},{1,17},{2,0},{3,19},{4,6},{5,21},{6,4},{7,23},{8,10},{9,25},... | collective-permute-start | bytes 7864328 | tf_op jit(solution)/shard_map/ppermute | solution.py:105
  471.8 50.3 %all-to-all-start.4 = ((bf16[32,1,32,512]{3,2,1,0:T(8,128)(2,1)}), bf16[32,1,32,512]{3,2,1,0:T(8,128)(2,1)}, u32[]{:S(2)}, u32[]{:S(2)}) async-start(bf16[32,1,32,512]{3,2,1,0:T(8,128)(2,1)} %bitcast.67), calls=%async_computation.4 | async-start | bytes 2097152 | tf_op jit(solution)/shard_map/all_to_all | solution.py:668
  494.0 9.3 %collective-permute-start.47 = (bf16[512,1024]{1,0:T(8,128)(2,1)}, bf16[512,1024]{1,0:T(8,128)(2,1)}, u32[]{:S(2)}, u32[]{:S(2)}) collective-permute-start(bf16[512,1024]{1,0:T(8,128)(2,1)} %get-tuple-element.251.refs_1_), channel_id=1, source_target_pairs={{0,1},{1,0},{2,3},{3,2},{4,5},{5,4},{6,7},{7,6},{8,9},{9,8},{10,11... | collective-permute-start | bytes 3145736 | tf_op jit(solution)/shard_map/ppermute | solution.py:94
  494.6 8.8 %collective-permute-start.48 = (bf16[512,1024]{1,0:T(8,128)(2,1)}, bf16[512,1024]{1,0:T(8,128)(2,1)}, u32[]{:S(2)}, u32[]{:S(2)}) collective-permute-start(bf16[512,1024]{1,0:T(8,128)(2,1)} %get-tuple-element.252.refs_2_), channel_id=1, source_target_pairs={{0,1},{1,0},{2,3},{3,2},{4,5},{5,4},{6,7},{7,6},{8,9},{9,8},{10,11... | collective-permute-start | bytes 3145736 | tf_op jit(solution)/shard_map/ppermute | solution.py:94
  497.3 19.6 %collective-permute-start.49 = (bf16[2,32,16,256]{3,2,1,0:T(8,128)(2,1)}, bf16[2,32,16,256]{3,2,1,0:T(8,128)(2,1)S(1)}, u32[]{:S(2)}, u32[]{:S(2)}) collective-permute-start(bf16[2,32,16,256]{3,2,1,0:T(8,128)(2,1)} %get-tuple-element.320), channel_id=1, source_target_pairs={{0,2},{1,17},{2,0},{3,19},{4,6},{5,21},{6,4},{7,23},{8,10},{9,25},... | collective-permute-start | bytes 1572872 | tf_op jit(solution)/shard_map/ppermute | solution.py:105
  500.2 14.9 %collective-permute-start.50 = (bf16[1,32,16,256]{3,2,1,0:T(8,128)(2,1)S(1)}, bf16[1,32,16,256]{3,2,1,0:T(8,128)(2,1)S(1)}, u32[]{:S(2)}, u32[]{:S(2)}) collective-permute-start(bf16[1,32,16,256]{3,2,1,0:T(8,128)(2,1)S(1)} %add_convert_fusion.27), channel_id=1, source_target_pairs={{0,8},{1,9},{2,10},{3,11},{4,12},{5,13},{6,14},{7,15},{8,0},{9,1},... | collective-permute-start | bytes 786440 | tf_op jit(solution)/shard_map/ppermute | solution.py:105
  516.9 20.7 %collective-permute-start.52 = (bf16[8,24,16,256]{3,2,1,0:T(8,128)(2,1)}, bf16[8,24,16,256]{3,2,1,0:T(8,128)(2,1)}, u32[]{:S(2)}, u32[]{:S(2)}) collective-permute-start(bf16[8,24,16,256]{3,2,1,0:T(8,128)(2,1)} %bitcast.328), channel_id=1, source_target_pairs={{0,2},{1,17},{2,0},{3,19},{4,6},{5,21},{6,4},{7,23},{8,10},{9,25},... | collective-permute-start | bytes 4718600 | tf_op jit(solution)/shard_map/ppermute | solution.py:105
  518.5 14.3 %collective-permute-start.53 = (bf16[1,32,16,256]{3,2,1,0:T(8,128)(2,1)}, bf16[1,32,16,256]{3,2,1,0:T(8,128)(2,1)}, u32[]{:S(2)}, u32[]{:S(2)}) collective-permute-start(bf16[1,32,16,256]{3,2,1,0:T(8,128)(2,1)} %add_convert_fusion.26), channel_id=1, source_target_pairs={{0,8},{1,9},{2,10},{3,11},{4,12},{5,13},{6,14},{7,15},{8,0},{9,1},... | collective-permute-start | bytes 786440 | tf_op jit(solution)/shard_map/ppermute | solution.py:105
  543.3 8.9 %collective-permute-start.56 = (bf16[128,512]{1,0:T(8,128)(2,1)S(1)}, bf16[128,512]{1,0:T(8,128)(2,1)S(1)}, u32[]{:S(2)}, u32[]{:S(2)}) collective-permute-start(bf16[128,512]{1,0:T(8,128)(2,1)S(1)} %constant_dynamic-slice_fusion.2), channel_id=1, source_target_pairs={{0,1},{1,0},{2,3},{3,2},{4,5},{5,4},{6,7},{7,6},{8,9},{9,8},{10,11... | collective-permute-start | bytes 393224 | tf_op jit(solution)/shard_map/ppermute | solution.py:94
  546.0 19.3 %collective-permute-start.57 = (bf16[4,24,16,256]{3,2,1,0:T(8,128)(2,1)S(1)}, bf16[4,24,16,256]{3,2,1,0:T(8,128)(2,1)S(1)}, u32[]{:S(2)}, u32[]{:S(2)}) collective-permute-start(bf16[4,24,16,256]{3,2,1,0:T(8,128)(2,1)S(1)} %get-tuple-element.315), channel_id=1, source_target_pairs={{0,4},{1,5},{2,6},{3,7},{4,0},{5,1},{6,2},{7,3},{8,12},{9,13},{10,... | collective-permute-start | bytes 2359304 | tf_op jit(solution)/shard_map/ppermute | solution.py:105
  549.6 17.7 %collective-permute-start.59 = (bf16[4,40,16,256]{3,2,1,0:T(8,128)(2,1)S(1)}, bf16[4,40,16,256]{3,2,1,0:T(8,128)(2,1)S(1)}, u32[]{:S(2)}, u32[]{:S(2)}) collective-permute-start(bf16[4,40,16,256]{3,2,1,0:T(8,128)(2,1)S(1)} %get-tuple-element.309), channel_id=1, source_target_pairs={{0,16},{1,3},{2,18},{3,1},{4,20},{5,7},{6,22},{7,5},{8,24},{9,11},... | collective-permute-start | bytes 3932168 | tf_op jit(solution)/shard_map/ppermute | solution.py:105
  551.1 18.9 %collective-permute-start.55 = (bf16[512,512]{1,0:T(8,128)(2,1)S(1)}, bf16[512,512]{1,0:T(8,128)(2,1)S(1)}, u32[]{:S(2)}, u32[]{:S(2)}) collective-permute-start(bf16[512,512]{1,0:T(8,128)(2,1)S(1)} %constant_dynamic-slice_fusion), channel_id=1, source_target_pairs={{0,1},{1,0},{2,3},{3,2},{4,5},{5,4},{6,7},{7,6},{8,9},{9,8},{10,11... | collective-permute-start | bytes 1572872 | tf_op jit(solution)/shard_map/ppermute | solution.py:94
  567.7 15.4 %collective-permute-start.60 = (bf16[2,40,16,256]{3,2,1,0:T(8,128)(2,1)S(1)}, bf16[2,40,16,256]{3,2,1,0:T(8,128)(2,1)S(1)}, u32[]{:S(2)}, u32[]{:S(2)}) collective-permute-start(bf16[2,40,16,256]{3,2,1,0:T(8,128)(2,1)S(1)} %get-tuple-element.317), channel_id=1, source_target_pairs={{0,4},{1,5},{2,6},{3,7},{4,0},{5,1},{6,2},{7,3},{8,12},{9,13},{10,... | collective-permute-start | bytes 1966088 | tf_op jit(solution)/shard_map/ppermute | solution.py:105
  583.2 25.0 %collective-permute-start.62 = (bf16[1,40,16,256]{3,2,1,0:T(8,128)(2,1)S(1)}, bf16[1,40,16,256]{3,2,1,0:T(8,128)(2,1)S(1)}, u32[]{:S(2)}, u32[]{:S(2)}) collective-permute-start(bf16[1,40,16,256]{3,2,1,0:T(8,128)(2,1)S(1)} %add_convert_fusion.20), channel_id=1, source_target_pairs={{0,8},{1,9},{2,10},{3,11},{4,12},{5,13},{6,14},{7,15},{8,0},{9,1},... | collective-permute-start | bytes 983048 | tf_op jit(solution)/shard_map/ppermute | solution.py:105
  586.3 20.8 %collective-permute-start.61 = (bf16[1,24,16,256]{3,2,1,0:T(8,128)(2,1)}, bf16[1,24,16,256]{3,2,1,0:T(8,128)(2,1)}, u32[]{:S(2)}, u32[]{:S(2)}) collective-permute-start(bf16[1,24,16,256]{3,2,1,0:T(8,128)(2,1)} %add_convert_fusion.29), channel_id=1, source_target_pairs={{0,8},{1,9},{2,10},{3,11},{4,12},{5,13},{6,14},{7,15},{8,0},{9,1},... | collective-permute-start | bytes 589832 | tf_op jit(solution)/shard_map/ppermute | solution.py:105
  610.0 19.7 %all-to-all-start.5 = ((bf16[72,16,256]{2,1,0:T(8,128)(2,1)}), bf16[72,16,256]{2,1,0:T(8,128)(2,1)S(1)}, u32[]{:S(2)}, u32[]{:S(2)}) async-start(bf16[72,16,256]{2,1,0:T(8,128)(2,1)} %bitcast.88), calls=%async_computation.5 | async-start | bytes 1179648 | tf_op jit(solution)/shard_map/all_to_all | solution.py:327
  629.6 18.2 %all-to-all-start.6 = ((bf16[64,16,256]{2,1,0:T(8,128)(2,1)}), bf16[64,16,256]{2,1,0:T(8,128)(2,1)S(1)}, u32[]{:S(2)}, u32[]{:S(2)}) async-start(bf16[64,16,256]{2,1,0:T(8,128)(2,1)} %gather_fusion.4), calls=%async_computation.6 | async-start | bytes 1048576 | tf_op jit(solution)/shard_map/all_to_all | solution.py:327
  633.3 38.7 %collective-permute-start.63 = (bf16[8,9,16,256]{3,2,1,0:T(8,128)(2,1)S(1)}, bf16[8,9,16,256]{3,2,1,0:T(8,128)(2,1)S(1)}, u32[]{:S(2)}, u32[]{:S(2)}) collective-permute-start(bf16[8,9,16,256]{3,2,1,0:T(8,128)(2,1)S(1)} %bitcast.276), channel_id=1, source_target_pairs={{0,16},{16,0},{1,17},{17,1},{2,18},{18,2},{3,19},{19,3},{4,20},{20... | collective-permute-start | bytes 1769480 | tf_op jit(solution)/shard_map/ppermute | solution.py:97
  647.9 12.3 %collective-permute-start.64 = (bf16[8,8,16,256]{3,2,1,0:T(8,128)(2,1)S(1)}, bf16[8,8,16,256]{3,2,1,0:T(8,128)(2,1)S(1)}, u32[]{:S(2)}, u32[]{:S(2)}) collective-permute-start(bf16[8,8,16,256]{3,2,1,0:T(8,128)(2,1)S(1)} %bitcast.285), channel_id=1, source_target_pairs={{0,16},{16,0},{1,17},{17,1},{2,18},{18,2},{3,19},{19,3},{4,20},{20... | collective-permute-start | bytes 1572872 | tf_op jit(solution)/shard_map/ppermute | solution.py:97
  (92 other events, 1132.3 us)

commit v5 on v4

--- a/solution.py
+++ b/solution.py
@@ -317,16 +317,22 @@
     width = vec_cut.shape[1]
     vec_cut = jnp.pad(vec_cut.astype(bf16), ((0, 0), (0, room - width)))
     vec_cut = vec_cut.reshape(n, 1, net.rows, BS)
-    parts = []
+    cuts = []
     for k in range(2):
         index = slots[:, k * half : (k + 1) * half].reshape(-1)
-        cut = natural.at[index].get(mode="promise_in_bounds")
-        if k == 1:
-            cut = jnp.concatenate([cut.reshape(n, half, net.rows, BS), vec_cut], axis=1)
-            cut = cut.reshape(-1, net.rows, BS)
-        mine = lax.all_to_all(cut, "shard", split_axis=0, concat_axis=0, tiled=True)
-        mine = mine.reshape(n, -1, net.rows, BS)
-        parts.append((mine, net.swap_rep(mine), half))
+        cuts.append(natural.at[index].get(mode="promise_in_bounds").reshape(n, half, net.rows, BS))
+    cuts[1] = jnp.concatenate([cuts[1], vec_cut], axis=1)
+
+    def home(cut):
+        back = lax.all_to_all(
+            cut.reshape(-1, net.rows, BS), "shard", split_axis=0, concat_axis=0, tiled=True
+        )
+        return back.reshape(n, -1, net.rows, BS)
+
+    mine, cuts[1] = together(home(cuts[0]), cuts[1])
+    other = net.swap_rep(mine)
+    other, last = together(other, home(cuts[1]))
+    parts = [(mine, other, half), (last, net.swap_rep(last), half)]
     terms = [v[:, half].reshape(n, room)[:, :width].astype(f32) for v in parts[1][:2]]
     flag = lax.axis_index("rep").astype(jnp.int32).reshape(1)
     return parts, flag, jnp.sum(terms[0] + terms[1], axis=0, keepdims=True)
@@ -761,10 +767,9 @@
     q_c = (dot_nn(h_one_low, w_cq) + b_cq).astype(bf16)
     k_c = dot_nn(e, w_ck).astype(bf16)
     v_c = (dot_nn(e, w_cv) + b_cv).astype(bf16)
-    q_c, k_c, v_c = step((q_c, k_c, v_c), down)
+    cot_pieces, q_c, k_c, v_c = step((cot_pieces, q_c, k_c, v_c), down)
+    cot_home = route_home(cot_pieces, seq_slots)
     o_c, lse_c = attend_forward(limit, q_c, k_c, v_c, False)
-    cot_pieces, o_c, lse_c = step((cot_pieces, o_c, lse_c))
-    cot_home = route_home(cot_pieces, seq_slots)
     z_two = h_one + dot_nn(o_c, w_co) + b_co
     h_two, n_two, r_two = norm_forward(z_two, g_two, b_two)
     h_two, h_two_low = step((h_two, h_two.astype(bf16)), up, down)
@@ -795,22 +800,23 @@
     d_hidden_sib = net.swap_core(d_hidden)
     down = gradient(3, ((act, act_sib), (a_three, net.swap_core(a_three))))
     d_hidden, d_hidden_sib = step((d_hidden, d_hidden_sib), down)
-    up = gradient(2, ((h_two_low, net.swap_core(h_two_low)), (d_hidden, d_hidden_sib)))
-    finished, d_hidden = step((finished, d_hidden), up)
-    out_pieces = route_out(finished)
     d_h_two = d_three + dot_nt(d_hidden, w_fi)
     d_two, dg_two, db_two = norm_backward(d_h_two, n_two, r_two, g_two)
     a_two = d_two.astype(bf16)
     d_oc = dot_nt(a_two, w_co).astype(bf16)
+    finished, d_hidden, d_hidden_sib, d_oc = step((finished, d_hidden, d_hidden_sib, d_oc))
+    out_pieces = route_out(finished)
+    up = gradient(2, ((h_two_low, net.swap_core(h_two_low)), (d_hidden, d_hidden_sib)))
+    (d_oc,) = step((d_oc,), up, down)
     dq_c, dk_c, dv_c = attend_backward(limit, q_c, k_c, v_c, o_c, d_oc, lse_c, False)
     dq_c_sib, dk_c_sib, dv_c_sib = [net.swap_core(v) for v in (dq_c, dk_c, dv_c)]
-    dq_c, dk_c, dv_c = step((dq_c, dk_c, dv_c), up, down)
+    dq_c, dk_c, dv_c = step((dq_c, dk_c, dv_c), down)
     d_h_one = d_two + dot_nt(dq_c, w_cq)
     d_one, dg_one, db_one = norm_backward(d_h_one, n_one, r_one, g_one)
     a_one = d_one.astype(bf16)
     a_one_sib = net.swap_core(a_one)
     d_os = dot_nt(a_one, w_so).astype(bf16)
-    out_pieces, a_one, a_one_sib, d_os = step((out_pieces, a_one, a_one_sib, d_os), down)
+    out_pieces, a_one, a_one_sib, d_os = step((out_pieces, a_one, a_one_sib, d_os), up, down)
     outputs = route_home(out_pieces, source)
     cross = gradient(
         1,
@@ -822,15 +828,14 @@
     (d_os,) = step((d_os,), cross, up, down)
     dq_s, dk_s, dv_s = attend_backward(limit, q_s, k_s, v_s, o_s, d_os, lse_s, True)
     sibs = [net.swap_core(v) for v in (dq_s, dk_s, dv_s)]
+    dq_s, dk_s, dv_s = step((dq_s, dk_s, dv_s), cross, up)
     attn = gradient(0, ((x, x_sib), *zip((dq_s, dk_s, dv_s), sibs)))
-    dq_s, dk_s, dv_s = step((dq_s, dk_s, dv_s), attn, up, down)
     d_hidden, dq_c, dk_c, dv_c, dq_s, dk_s, dv_s = step(
-        (d_hidden, dq_c, dk_c, dv_c, dq_s, dk_s, dv_s), cross
+        (d_hidden, dq_c, dk_c, dv_c, dq_s, dk_s, dv_s), attn, cross, up
     )
     state_back = dot_nt(dk_c, w_ck) + dot_nt(dv_c, w_cv)
     back = d_one + dot_nt(dq_s, w_sq) + dot_nt(dk_s, w_sk) + dot_nt(dv_s, w_sv)
-    outputs, back = step((outputs, back), attn, up)
-    step((), cross)
+    outputs, back = step((outputs, back), attn, cross)
     input_grad = halved(back.astype(bf16))
     encoded_grad = halved(state_back.astype(bf16))
     sums = (

time: 696 us -> 676 us (0.971)
  starting transfers between devices: 104 us -> 87.6 us
  waiting for transfers between devices: 216 us -> 205 us
    all_to_all x2, waiting for transfers between devices: 27.4 us -> 15.5 us  [home(): lax.all_to_all(cut.reshape(-1, net.rows, BS), 'shard', split_axis=0, conc...]
    ppermute x31, starting transfers between devices: 24.5 us -> 14.6 us  [swap_core(): return lax.ppermute(value, 'mp', [(i, i ^ 1) for i in range(self.n_mp)])]
    all_to_all x2, waiting for transfers between devices: 0.01 us -> 9.42 us  [route_out(): return lax.all_to_all(cut, axes, split_axis=1, concat_axis=0, tiled=True)]
    ppermute x32, waiting for transfers between devices: 133 us -> 124 us  [swap_data(): return lax.ppermute(value, ('rep', 'shard', 'mp'), pairs)]
  transfers between devices with their start and end apart: 72 -> 72, of which waited for: 30 -> 30; matrix products, arithmetic and copies ran while one was open for 22% -> 24% of each run, Pallas kernels for 25% -> 26%
where the time goes in v5:
time: 676 us; the launch traced here: 665 us
  waiting for transfers between devices  205 us (30%)
  Pallas kernels  185 us (27%)
  starting transfers between devices  87.6 us (13%)
  other arithmetic  80.4 us (12%)
  matrix products  66.5 us (10%)
  local copies, waits for them, and re-layouts  37.9 us (6%)
    ppermute x32, waiting for transfers between devices, swap_data(): return lax.ppermute(value, ('rep', 'shard', 'mp'), pairs)  124 us
    pallas_call x7, Pallas kernels, weight_grad(): pl.pallas_call(functools.partial(weight_grad_body, count=count, outs=outs...  49.7 us
    dot_general x10, matrix products, dot_nt(): return lax.dot_general(a, b, NT, preferred_element_type=f32)  38.2 us
    pallas_call x4, Pallas kernels, place(): pl.pallas_call(functools.partial(place_body, dests=dests, many=many, two=...  38 us
    ppermute x32, starting transfers between devices, swap_data(): return lax.ppermute(value, ('rep', 'shard', 'mp'), pairs)  35.4 us
    pallas_call x2, Pallas kernels, attend_forward(): pl.pallas_call(functools.partial(attend_forward_body, causal=causal, rows...  29.1 us
    dot_general x9, matrix products, dot_nn(): return jnp.dot(a, b, preferred_element_type=f32)  28.2 us
    all_to_all x1, waiting for transfers between devices, first_pieces(): lax.all_to_all(cut.reshape(-1, net.rows, BS), 'shard', split_axis=0, conc...  27 us
  transfers between devices with their start and end apart: 72, of which 30 were waited for; matrix products, arithmetic and copies ran while one was open for 24% of the time, Pallas kernels for 26%

profile of v5, /device:TPU:0, one launch (start us, length us, event | category | flops | bytes accessed | tf_op | source)
XLA Modules:
  0.0 664.8 jit_solution(9538399578278424457)
XLA Ops:
  5.2 7.3 %all-to-all-start = ((bf16[136,16,256]{2,1,0:T(8,128)(2,1)}), bf16[136,16,256]{2,1,0:T(8,128)(2,1)S(1)}, u32[]{:S(2)}, u32[]{:S(2)}) async-start(bf16[136,16,256]{2,1,0:T(8,128)(2,1)} %bitcast.4), calls=%async_computation | async-start | bytes 2228224 | tf_op jit(solution)/shard_map/all_to_all | solution.py:271
  12.6 27.0 %all-to-all-done = bf16[136,16,256]{2,1,0:T(8,128)(2,1)S(1)} async-done(((bf16[136,16,256]{2,1,0:T(8,128)(2,1)}), bf16[136,16,256]{2,1,0:T(8,128)(2,1)S(1)}, u32[]{:S(2)}, u32[]{:S(2)}) %all-to-all-start) | async-done | bytes 1114144 | tf_op jit(solution)/shard_map/all_to_all | solution.py:271
  40.4 10.6 %collective-permute-done.2 = bf16[1,24,16,256]{3,2,1,0:T(8,128)(2,1)S(1)} collective-permute-done((bf16[1,24,16,256]{3,2,1,0:T(8,128)(2,1)S(1)}, bf16[1,24,16,256]{3,2,1,0:T(8,128)(2,1)S(1)}, u32[]{:S(2)}, u32[]{:S(2)}) %collective-permute-start.2) | collective-permute-done | bytes 196640 | tf_op jit(solution)/shard_map/ppermute | solution.py:105
  52.7 6.3 collective-permute-done.3
  62.2 14.0 %collective-permute-done.5 = bf16[1,40,16,256]{3,2,1,0:T(8,128)(2,1)S(1)} collective-permute-done((bf16[1,40,16,256]{3,2,1,0:T(8,128)(2,1)S(1)}, bf16[1,40,16,256]{3,2,1,0:T(8,128)(2,1)S(1)}, u32[]{:S(2)}, u32[]{:S(2)}) %collective-permute-start.5) | collective-permute-done | bytes 327712 | tf_op jit(solution)/shard_map/ppermute | solution.py:105
  93.2 9.8 %collective-permute-done.8 = bf16[2,40,16,256]{3,2,1,0:T(8,128)(2,1)} collective-permute-done((bf16[2,40,16,256]{3,2,1,0:T(8,128)(2,1)}, bf16[2,40,16,256]{3,2,1,0:T(8,128)(2,1)}, u32[]{:S(2)}, u32[]{:S(2)}) %collective-permute-start.8) | collective-permute-done | bytes 655392 | tf_op jit(solution)/shard_map/ppermute | solution.py:105
  109.1 8.5 %place.4 = (bf16[4,256,1024]{2,1,0:T(8,128)(2,1)}, bf16[4,256,1024]{2,1,0:T(8,128)(2,1)}, bf16[4,256,1024]{2,1,0:T(8,128)(2,1)}) custom-call(s32[41]{0:T(128)} %add_add_fusion.4.s, bf16[8,24,16,256]{3,2,1,0:T(8,128)(2,1)} %copy-done.16, bf16[8,24,16,256]{3,2,1,0:T(8,128)(2,1)} %collective-permute-done.6.refs_1_, ...), custom_call_target="tpu_custom_call" | custom-call | flops 1048576 | bytes 1048576 | tf_op jit(solution)/shard_map/place/pallas_call | solution.py:227
  119.2 4.0 add_convert_fusion.8.q_ref
  137.2 20.1 %attend_forward.2 = (bf16[512,1024]{1,0:T(8,128)(2,1)}, f32[512,128]{1,0:T(8,128)}) custom-call(s32[1]{0:T(128)} %dynamic_slice.97.lim, bf16[512,1024]{1,0:T(8,128)(2,1)} %add_convert_fusion.8.q_ref, bf16[512,1024]{1,0:T(8,128)(2,1)} %convolution_convert_fusion.2.k_ref, bf16[512,1024]{1,0:T(8,128)(2,1)} %add_convert_fusion.7.v_ref), custom_call_target="tpu_custom_call" | custom-call | flops 1048576 | bytes 1048576 | tf_op jit(solution)/shard_map/attend_forward/pallas_call | solution.py:382
  160.6 3.8 collective-permute-done.17
  166.1 3.0 pad_maximum_fusion.1.refs_0_
  171.6 5.2 all-to-all-start.1
  179.9 10.2 %place.5 = (bf16[4,256,1024]{2,1,0:T(8,128)(2,1)}, bf16[4,256,1024]{2,1,0:T(8,128)(2,1)}, bf16[4,256,1024]{2,1,0:T(8,128)(2,1)}, bf16[4,256,1024]{2,1,0:T(8,128)(2,1)}, bf16[4,256,1024]{2,1,0:T(8,128)(2,1)}) custom-call(s32[41]{0:T(128)} %add_add_fusion.5.s, bf16[8,40,16,256]{3,2,1,0:T(8,128)(2,1)} %copy-done.5, ...), custom_call_target="tpu_custom_call" | custom-call | flops 1048576 | bytes 1048576 | tf_op jit(solution)/shard_map/place/pallas_call | solution.py:227
  190.2 3.5 fusion.23
  202.8 9.4 %all-to-all-done.1 = bf16[2,16,32,512]{3,2,0,1:T(8,128)(2,1)S(1)} async-done(((bf16[2,16,32,512]{3,2,0,1:T(8,128)(2,1)}), bf16[2,16,32,512]{3,2,0,1:T(8,128)(2,1)S(1)}, u32[]{:S(2)}, u32[]{:S(2)}) %all-to-all-start.1) | async-done | bytes 1048608 | tf_op jit(solution)/shard_map/all_to_all | solution.py:669
  215.3 9.0 %attend_forward.3 = (bf16[512,1024]{1,0:T(8,128)(2,1)}, f32[512,128]{1,0:T(8,128)}) custom-call(s32[1]{0:T(128)} %dynamic_slice.97.lim, bf16[512,1024]{1,0:T(8,128)(2,1)} %add_convert_fusion.6.q_ref, bf16[128,1024]{1,0:T(8,128)(2,1)} %convolution_convert_fusion.3.k_ref, bf16[128,1024]{1,0:T(8,128)(2,1)} %fusion.4.v_ref), custom_call_target="tpu_custom_call" | custom-call | flops 1048576 | bytes 1048576 | tf_op jit(solution)/shard_map/attend_forward/pallas_call | solution.py:382
  224.3 3.4 fusion.26
  231.0 2.9 pad_maximum_fusion.2.refs_0_
  237.1 4.8 all-to-all-start.2
  243.3 9.6 %place.6 = bf16[4,256,4096]{2,1,0:T(8,128)(2,1)} custom-call(s32[41]{0:T(128)} %add_add_fusion.6.s, bf16[8,32,16,256]{3,2,1,0:T(8,128)(2,1)} %pad_maximum_fusion.1.refs_0_, bf16[8,32,16,256]{3,2,1,0:T(8,128)(2,1)} %collective-permute-done.20.refs_1_, bf16[8,32,16,256]{3,2,1,0:T(8,128)(2,1)} %collective-permute-done.21.refs_2_, ...), custom_call_target="tpu_custom_call" | custom-call | flops 1048576 | bytes 1048576 | tf_op jit(solution)/shard_map/place/pallas_call | solution.py:227
  252.9 19.1 %gelu_forward.1 = (bf16[512,4096]{1,0:T(8,128)(2,1)}, bf16[512,4096]{1,0:T(8,128)(2,1)}) custom-call(bf16[512,1024]{1,0:T(8,128)(2,1)} %get-tuple-element.195.h_ref.x_own, bf16[1024,4096]{1,0:T(8,128)(2,1)} %bitcast.243, f32[1,4096]{1,0:T(1,128)} %bitcast.295), custom_call_target="tpu_custom_call" | custom-call | flops 1048576 | bytes 1048576 | tf_op jit(solution)/shard_map/gelu_forward/pallas_call | solution.py:515
  272.3 6.7 %all-to-all-done.2 = bf16[32,1,32,512]{3,2,1,0:T(8,128)(2,1)S(1)} async-done(((bf16[32,1,32,512]{3,2,1,0:T(8,128)(2,1)}), bf16[32,1,32,512]{3,2,1,0:T(8,128)(2,1)S(1)}, u32[]{:S(2)}, u32[]{:S(2)}) %all-to-all-start.2) | async-done | bytes 1048608 | tf_op jit(solution)/shard_map/all_to_all | solution.py:674
  282.2 9.6 %place.7 = bf16[16,256,1024]{2,1,0:T(8,128)(2,1)} custom-call(s32[41]{0:T(128)} %add_add_fusion.7.s, bf16[8,32,16,256]{3,2,1,0:T(8,128)(2,1)} %pad_maximum_fusion.2.refs_0_, bf16[8,32,16,256]{3,2,1,0:T(8,128)(2,1)} %collective-permute-done.24.refs_1_, bf16[8,32,16,256]{3,2,1,0:T(8,128)(2,1)} %collective-permute-done.25.refs_2_, ...), custom_call_target="tpu_custom_call" | custom-call | flops 1048576 | bytes 1048576 | tf_op jit(solution)/shard_map/place/pallas_call | solution.py:227
  291.8 8.3 %fusion.27 = f32[512,1024]{1,0:T(8,128)S(1)} fusion(bf16[512,4096]{1,0:T(8,128)(2,1)} %get-tuple-element.201.x_own, bf16[4096,1024]{1,0:T(8,128)(2,1)} %bitcast.246), kind=kOutput, calls=%fused_computation.239 | convolution fusion | flops 4294967296 | bytes 14680064 | tf_op jit(solution)/shard_map/dot_general | solution.py:43
  305.3 8.1 %multiply_convert_fusion.refs_0_ = bf16[512,4096]{1,0:T(8,128)(2,1)} fusion(bf16[512,4096]{1,0:T(8,128)(2,1)} %get-tuple-element.205, bf16[512,1024]{1,0:T(8,128)(2,1)S(1)} %convert_element_type.379.refs_0_, bf16[4096,1024]{1,0:T(8,128)(2,1)S(1)} %bitcast.249), kind=kOutput, calls=%fused_computation.6 | convolution fusion | flops 4301258752 | bytes 17825792 | tf_op jit(solution)/shard_map/dot_general | solution.py:47
  316.3 6.8 %collective-permute-done.27 = bf16[512,512]{1,0:T(8,128)(2,1)} collective-permute-done((bf16[512,512]{1,0:T(8,128)(2,1)}, bf16[512,512]{1,0:T(8,128)(2,1)}, u32[]{:S(2)}, u32[]{:S(2)}) %collective-permute-start.27) | collective-permute-done | bytes 524320 | tf_op jit(solution)/shard_map/ppermute | solution.py:94
  325.7 11.3 %weight_grad.7 = (bf16[8,1,32,16,256]{4,3,2,1,0:T(8,128)(2,1)}, bf16[8,1,32,16,256]{4,3,2,1,0:T(8,128)(2,1)}) custom-call(s32[41]{0:T(128)} %add_add_fusion.7.s, bf16[512,4096]{1,0:T(8,128)(2,1)} %get-tuple-element.201.x_own, bf16[512,4096]{1,0:T(8,128)(2,1)} %collective-permute-done.30.x_sib, bf16[512,1024]{1,0:T(8,128)(2,1)} %copy-done.28, ...), custom_call_target="tpu_custom_call" | custom-call | flops 1048576 | bytes 1048576 | tf_op jit(solution)/shard_map/weight_grad/pallas_call | solution.py:572
  337.1 11.1 %multiply_reduce_fusion.1 = (f32[1024]{0:T(1024)S(1)}, f32[512]{0:T(512)S(1)}, f32[512]{0:T(512)S(1)}, f32[1024]{0:T(1024)S(1)}, f32[512,1024]{1,0:T(8,128)S(1)}) fusion(f32[512,1024]{1,0:T(8,128)} %copy-done.3, f32[512]{0:T(512)S(1)} %add_rsqrt_fusion.1, f32[512]{0:T(512)S(1)} %broadcast_multiply_fusion.7, f32[1024]{0:T(1024)S(1)} %bitcast.303, ...), kind=kOutput, calls=%fused_computation.13 | convolution fusion | flops 4300207104 | bytes 18894848 | tf_op jit(solution)/shard_map/dot_general | solution.py:47
  353.5 9.6 %weight_grad.8 = (bf16[8,1,32,16,256]{4,3,2,1,0:T(8,128)(2,1)}, bf16[8,1,32,16,256]{4,3,2,1,0:T(8,128)(2,1)}) custom-call(s32[41]{0:T(128)} %add_add_fusion.6.s, bf16[512,1024]{1,0:T(8,128)(2,1)} %get-tuple-element.195.h_ref.x_own, bf16[512,1024]{1,0:T(8,128)(2,1)} %collective-permute-done.32.x_sib, bf16[512,4096]{1,0:T(8,128)(2,1)} %multiply_convert_fusion.refs_0_, ...), custom_call_target="tpu_custom_call" | custom-call | flops 1048576 | bytes 1048576 | tf_op jit(solution)/shard_map/weight_grad/pallas_call | solution.py:572
  363.4 4.3 add_convert_fusion.4
  370.4 4.5 all-to-all-start.3
  377.0 10.3 %attend_backward.2 = (bf16[512,1024]{1,0:T(8,128)(2,1)}, bf16[128,1024]{1,0:T(8,128)(2,1)}, bf16[128,1024]{1,0:T(8,128)(2,1)}) custom-call(s32[1]{0:T(128)} %dynamic_slice.97.lim, bf16[512,1024]{1,0:T(8,128)(2,1)} %add_convert_fusion.6.q_ref, bf16[128,1024]{1,0:T(8,128)(2,1)} %convolution_convert_fusion.3.k_ref, bf16[128,1024]{1,0:T(8,128)(2,1)} %fusion.4.v_ref, ...), custom_call_target="tpu_custom_call" | custom-call | flops 1048576 | bytes 1048576 | tf_op jit(solution)/shard_map/attend_backward/pallas_call | solution.py:465
  387.8 4.4 multiply_reduce_fusion.2
  393.2 2.9 collective-permute-start.35
  399.7 3.1 collective-permute-start.42
  405.1 8.1 %collective-permute-done.37 = bf16[2,32,16,256]{3,2,1,0:T(8,128)(2,1)S(1)} collective-permute-done((bf16[2,32,16,256]{3,2,1,0:T(8,128)(2,1)S(1)}, bf16[2,32,16,256]{3,2,1,0:T(8,128)(2,1)S(1)}, u32[]{:S(2)}, u32[]{:S(2)}) %collective-permute-start.37) | collective-permute-done | bytes 524320 | tf_op jit(solution)/shard_map/ppermute | solution.py:105
  416.4 5.7 collective-permute-done.36
  422.2 4.0 add_convert_fusion.2
  430.7 4.8 weight_grad.9
  435.4 5.5 weight_grad.10
  441.6 5.3 weight_grad.11
  447.0 4.8 weight_grad.12
  451.8 4.9 collective-permute-done.46
  462.1 2.8 gather_fusion.2
  464.9 5.4 all-to-all-start.4
  470.6 16.4 %attend_backward.3 = (bf16[512,1024]{1,0:T(8,128)(2,1)}, bf16[512,1024]{1,0:T(8,128)(2,1)}, bf16[512,1024]{1,0:T(8,128)(2,1)}) custom-call(s32[1]{0:T(128)} %dynamic_slice.97.lim, bf16[512,1024]{1,0:T(8,128)(2,1)} %add_convert_fusion.8.q_ref, bf16[512,1024]{1,0:T(8,128)(2,1)} %convolution_convert_fusion.2.k_ref, bf16[512,1024]{1,0:T(8,128)(2,1)} %add_convert_fusion.7.v_ref, ...), custom_call_target="tpu_custom_call" | custom-call | flops 1048576 | bytes 1048576 | tf_op jit(solution)/shard_map/attend_backward/pallas_call | solution.py:465
  487.0 17.9 %collective-permute-done.48 = bf16[2,32,16,256]{3,2,1,0:T(8,128)(2,1)S(1)} collective-permute-done((bf16[2,32,16,256]{3,2,1,0:T(8,128)(2,1)S(1)}, bf16[2,32,16,256]{3,2,1,0:T(8,128)(2,1)S(1)}, u32[]{:S(2)}, u32[]{:S(2)}) %collective-permute-start.48) | collective-permute-done | bytes 524320 | tf_op jit(solution)/shard_map/ppermute | solution.py:105
  505.7 4.1 add_convert_fusion
  512.5 2.5 collective-permute-start.53
  520.0 8.5 %weight_grad.13 = (bf16[8,3,8,16,256]{4,3,2,1,0:T(8,128)(2,1)}, bf16[8,3,8,16,256]{4,3,2,1,0:T(8,128)(2,1)}) custom-call(s32[41]{0:T(128)} %add_add_fusion.8.s, bf16[512,1024]{1,0:T(8,128)(2,1)} %get-tuple-element.156.x_own, bf16[512,1024]{1,0:T(8,128)(2,1)} %get-tuple-element.255.x_sib, bf16[512,1024]{1,0:T(8,128)(2,1)} %get-tuple-element.261.refs_0_, ...), custom_call_target="tpu_custom_call" | custom-call | flops 1048576 | bytes 1048576 | tf_op jit(solution)/shard_map/weight_grad/pallas_call | solution.py:572
  532.1 2.8 add_convert_fusion.11
  538.7 3.3 convert_reduce_fusion
  545.2 2.7 fusion.28
  547.9 2.7 fusion.29
  559.3 21.9 %collective-permute-done.59 = bf16[4,24,16,256]{3,2,1,0:T(8,128)(2,1)S(1)} collective-permute-done((bf16[4,24,16,256]{3,2,1,0:T(8,128)(2,1)S(1)}, bf16[4,24,16,256]{3,2,1,0:T(8,128)(2,1)S(1)}, u32[]{:S(2)}, u32[]{:S(2)}) %collective-permute-start.59) | collective-permute-done | bytes 786464 | tf_op jit(solution)/shard_map/ppermute | solution.py:105
  583.5 5.8 collective-permute-done.60
  590.5 8.3 %collective-permute-done.62 = bf16[1,24,16,256]{3,2,1,0:T(8,128)(2,1)S(1)} collective-permute-done((bf16[1,24,16,256]{3,2,1,0:T(8,128)(2,1)S(1)}, bf16[1,24,16,256]{3,2,1,0:T(8,128)(2,1)S(1)}, u32[]{:S(2)}, u32[]{:S(2)}) %collective-permute-start.62) | collective-permute-done | bytes 196640 | tf_op jit(solution)/shard_map/ppermute | solution.py:105
  600.6 3.6 all-to-all-start.5
  605.8 13.0 %all-to-all-done.5 = bf16[64,16,256]{2,1,0:T(8,128)(2,1)S(1)} async-done(((bf16[64,16,256]{2,1,0:T(8,128)(2,1)}), bf16[64,16,256]{2,1,0:T(8,128)(2,1)S(1)}, u32[]{:S(2)}, u32[]{:S(2)}) %all-to-all-start.5) | async-done | bytes 524320 | tf_op jit(solution)/shard_map/all_to_all | solution.py:327
  618.7 3.6 all-to-all-start.6
  623.9 12.0 %collective-permute-done.63.other_ref = bf16[8,8,16,256]{3,2,1,0:T(8,128)(2,1)S(1)} collective-permute-done((bf16[8,8,16,256]{3,2,1,0:T(8,128)(2,1)S(1)}, bf16[8,8,16,256]{3,2,1,0:T(8,128)(2,1)S(1)}, u32[]{:S(2)}, u32[]{:S(2)}) %collective-permute-start.63) | collective-permute-done | bytes 524320 | tf_op jit(solution)/shard_map/ppermute | solution.py:97
  635.9 2.5 all-to-all-done.6
  640.1 11.0 %shampoo.2 = (f32[1,16,256,256]{3,2,1,0:T(8,128)}, f32[1,16,256,256]{3,2,1,0:T(8,128)}, f32[1,16,256,256]{3,2,1,0:T(8,128)}, f32[1,16,256,256]{3,2,1,0:T(8,128)}) custom-call(s32[1]{0:T(128)} %bitcast.81.flag, bf16[8,8,16,256]{3,2,1,0:T(8,128)(2,1)} %bitcast.286, bf16[8,8,16,256]{3,2,1,0:T(8,128)(2,1)} %copy-done.60, f32[1,16,256,256]{3,2,1,0:T(8,128)} %w_ref.3, ...), custom_call_target="tpu_custom_call" | custom-call | flops 1048576 | bytes 1048576 | tf_op jit(solution)/shard_map/shampoo/pallas_call | solution.py:627
  653.7 10.9 %shampoo.3 = (f32[1,16,256,256]{3,2,1,0:T(8,128)}, f32[1,16,256,256]{3,2,1,0:T(8,128)}, f32[1,16,256,256]{3,2,1,0:T(8,128)}, f32[1,16,256,256]{3,2,1,0:T(8,128)}) custom-call(s32[1]{0:T(128)} %bitcast.81.flag, bf16[8,9,16,256]{3,2,1,0:T(8,128)(2,1)} %bitcast.278, ...), custom_call_target="tpu_custom_call", output_to_operand_aliasing={{0}: (8, {}), {1}: (9, {}), {2}: (10, {}), {3}: (11, {})} | custom-call | flops 1048576 | bytes 1048576 | tf_op jit(solution)/shard_map/shampoo/pallas_call | solution.py:627
  (496 shorter events, 164.9 us)
Async XLA Ops:
  5.2 34.5 %all-to-all-start = ((bf16[136,16,256]{2,1,0:T(8,128)(2,1)}), bf16[136,16,256]{2,1,0:T(8,128)(2,1)S(1)}, u32[]{:S(2)}, u32[]{:S(2)}) async-start(bf16[136,16,256]{2,1,0:T(8,128)(2,1)} %bitcast.4), calls=%async_computation | async-start | bytes 2228224 | tf_op jit(solution)/shard_map/all_to_all | solution.py:271
  40.3 10.7 %collective-permute-start.2 = (bf16[1,24,16,256]{3,2,1,0:T(8,128)(2,1)S(1)}, bf16[1,24,16,256]{3,2,1,0:T(8,128)(2,1)S(1)}, u32[]{:S(2)}, u32[]{:S(2)}) collective-permute-start(bf16[1,24,16,256]{3,2,1,0:T(8,128)(2,1)S(1)} %bitcast.272), channel_id=1, source_target_pairs={{0,8},{1,9},{2,10},{3,11},{4,12},{5,13},{6,14},{7,15},{8,0},{9,1},... | collective-permute-start | bytes 589832 | tf_op jit(solution)/shard_map/ppermute | solution.py:105
  51.1 7.8 %collective-permute-start.3 = (bf16[2,24,16,256]{3,2,1,0:T(8,128)(2,1)S(1)}, bf16[2,24,16,256]{3,2,1,0:T(8,128)(2,1)S(1)}, u32[]{:S(2)}, u32[]{:S(2)}) collective-permute-start(bf16[2,24,16,256]{3,2,1,0:T(8,128)(2,1)S(1)} %pad_maximum_fusion.19), channel_id=1, source_target_pairs={{0,16},{1,5},{2,18},{3,7},{4,20},{5,1},{6,22},{7,3},{8,24},{9,13},... | collective-permute-start | bytes 1179656 | tf_op jit(solution)/shard_map/ppermute | solution.py:105
  59.9 19.3 %collective-permute-start.4 = (bf16[4,24,16,256]{3,2,1,0:T(8,128)(2,1)}, bf16[4,24,16,256]{3,2,1,0:T(8,128)(2,1)}, u32[]{:S(2)}, u32[]{:S(2)}) collective-permute-start(bf16[4,24,16,256]{3,2,1,0:T(8,128)(2,1)} %pad_maximum_fusion.14), channel_id=1, source_target_pairs={{0,4},{1,3},{2,6},{3,1},{4,0},{5,7},{6,2},{7,5},{8,12},{9,11},{10,... | collective-permute-start | bytes 2359304 | tf_op jit(solution)/shard_map/ppermute | solution.py:105
  59.9 16.3 %collective-permute-start.5 = (bf16[1,40,16,256]{3,2,1,0:T(8,128)(2,1)S(1)}, bf16[1,40,16,256]{3,2,1,0:T(8,128)(2,1)S(1)}, u32[]{:S(2)}, u32[]{:S(2)}) collective-permute-start(bf16[1,40,16,256]{3,2,1,0:T(8,128)(2,1)S(1)} %bitcast.254), channel_id=1, source_target_pairs={{0,8},{1,9},{2,10},{3,11},{4,12},{5,13},{6,14},{7,15},{8,0},{9,1},... | collective-permute-start | bytes 983048 | tf_op jit(solution)/shard_map/ppermute | solution.py:105
  61.7 23.8 %collective-permute-start = (bf16[2,512,512]{2,1,0:T(8,128)(2,1)}, bf16[2,512,512]{2,1,0:T(8,128)(2,1)}, u32[]{:S(2)}, u32[]{:S(2)}) collective-permute-start(bf16[2,512,512]{2,1,0:T(8,128)(2,1)} %param.21), channel_id=1, source_target_pairs={{0,1},{1,0},{2,3},{3,2},{4,5},{5,4},{6,7},{7,6},{8,9},{9,8},{10,11... | collective-permute-start | bytes 3145736 | tf_op jit(solution)/shard_map/ppermute | solution.py:94
  61.7 21.0 %collective-permute-start.1 = (bf16[2,128,512]{2,1,0:T(8,128)(2,1)}, bf16[2,128,512]{2,1,0:T(8,128)(2,1)}, u32[]{:S(2)}, u32[]{:S(2)}) collective-permute-start(bf16[2,128,512]{2,1,0:T(8,128)(2,1)} %param.22), channel_id=1, source_target_pairs={{0,1},{1,0},{2,3},{3,2},{4,5},{5,4},{6,7},{7,6},{8,9},{9,8},{10,11... | collective-permute-start | bytes 786440 | tf_op jit(solution)/shard_map/ppermute | solution.py:94
  80.7 22.3 %collective-permute-start.6 = (bf16[8,24,16,256]{3,2,1,0:T(8,128)(2,1)S(1)}, bf16[8,24,16,256]{3,2,1,0:T(8,128)(2,1)}, u32[]{:S(2)}, u32[]{:S(2)}) collective-permute-start(bf16[8,24,16,256]{3,2,1,0:T(8,128)(2,1)S(1)} %pad_maximum_fusion.3.refs_0_), channel_id=1, source_target_pairs={{0,2},{1,17},{2,0},{3,19},{4,6},{5,21},{6,4},{7,23},{8,10},{9,25},... | collective-permute-start | bytes 4718600 | tf_op jit(solution)/shard_map/ppermute | solution.py:105
  82.0 21.0 %collective-permute-start.7 = (bf16[8,24,16,256]{3,2,1,0:T(8,128)(2,1)S(1)}, bf16[8,24,16,256]{3,2,1,0:T(8,128)(2,1)}, u32[]{:S(2)}, u32[]{:S(2)}) collective-permute-start(bf16[8,24,16,256]{3,2,1,0:T(8,128)(2,1)S(1)} %pad_maximum_fusion.3.refs_0_), channel_id=1, source_target_pairs={{0,1},{1,0},{2,3},{3,2},{4,5},{5,4},{6,7},{7,6},{8,9},{9,8},{10,11... | collective-permute-start | bytes 4718600 | tf_op jit(solution)/shard_map/ppermute | solution.py:94
  85.5 17.5 %collective-permute-start.8 = (bf16[2,40,16,256]{3,2,1,0:T(8,128)(2,1)}, bf16[2,40,16,256]{3,2,1,0:T(8,128)(2,1)}, u32[]{:S(2)}, u32[]{:S(2)}) collective-permute-start(bf16[2,40,16,256]{3,2,1,0:T(8,128)(2,1)} %pad_maximum_fusion.15), channel_id=1, source_target_pairs={{0,4},{1,5},{2,6},{3,7},{4,0},{5,1},{6,2},{7,3},{8,12},{9,13},{10,... | collective-permute-start | bytes 1966088 | tf_op jit(solution)/shard_map/ppermute | solution.py:105
  103.5 14.5 %collective-permute-start.10 = (bf16[1,32,16,256]{3,2,1,0:T(8,128)(2,1)S(1)}, bf16[1,32,16,256]{3,2,1,0:T(8,128)(2,1)S(1)}, u32[]{:S(2)}, u32[]{:S(2)}) collective-permute-start(bf16[1,32,16,256]{3,2,1,0:T(8,128)(2,1)S(1)} %bitcast.268), channel_id=1, source_target_pairs={{0,8},{1,9},{2,10},{3,11},{4,12},{5,13},{6,14},{7,15},{8,0},{9,1},... | collective-permute-start | bytes 786440 | tf_op jit(solution)/shard_map/ppermute | solution.py:105
  106.3 21.4 %collective-permute-start.12 = (bf16[4,40,16,256]{3,2,1,0:T(8,128)(2,1)}, bf16[4,40,16,256]{3,2,1,0:T(8,128)(2,1)}, u32[]{:S(2)}, u32[]{:S(2)}) collective-permute-start(bf16[4,40,16,256]{3,2,1,0:T(8,128)(2,1)} %pad_maximum_fusion.4), channel_id=1, source_target_pairs={{0,16},{1,3},{2,18},{3,1},{4,20},{5,7},{6,22},{7,5},{8,24},{9,11},... | collective-permute-start | bytes 3932168 | tf_op jit(solution)/shard_map/ppermute | solution.py:105
  118.1 10.5 %collective-permute-start.13 = (bf16[2,32,16,256]{3,2,1,0:T(8,128)(2,1)S(1)}, bf16[2,32,16,256]{3,2,1,0:T(8,128)(2,1)S(1)}, u32[]{:S(2)}, u32[]{:S(2)}) collective-permute-start(bf16[2,32,16,256]{3,2,1,0:T(8,128)(2,1)S(1)} %pad_maximum_fusion.17), channel_id=1, source_target_pairs={{0,2},{1,17},{2,0},{3,19},{4,6},{5,21},{6,4},{7,23},{8,10},{9,25},... | collective-permute-start | bytes 1572872 | tf_op jit(solution)/shard_map/ppermute | solution.py:105
  130.4 34.8 %collective-permute-start.14 = (bf16[8,40,16,256]{3,2,1,0:T(8,128)(2,1)S(1)}, bf16[8,40,16,256]{3,2,1,0:T(8,128)(2,1)}, u32[]{:S(2)}, u32[]{:S(2)}) collective-permute-start(bf16[8,40,16,256]{3,2,1,0:T(8,128)(2,1)S(1)} %pad_maximum_fusion.refs_0_), channel_id=1, source_target_pairs={{0,2},{1,17},{2,0},{3,19},{4,6},{5,21},{6,4},{7,23},{8,10},{9,25},... | collective-permute-start | bytes 7864328 | tf_op jit(solution)/shard_map/ppermute | solution.py:105
  131.9 33.3 %collective-permute-start.15 = (bf16[8,40,16,256]{3,2,1,0:T(8,128)(2,1)S(1)}, bf16[8,40,16,256]{3,2,1,0:T(8,128)(2,1)}, u32[]{:S(2)}, u32[]{:S(2)}) collective-permute-start(bf16[8,40,16,256]{3,2,1,0:T(8,128)(2,1)S(1)} %pad_maximum_fusion.refs_0_), channel_id=1, source_target_pairs={{0,1},{1,0},{2,3},{3,2},{4,5},{5,4},{6,7},{7,6},{8,9},{9,8},{10,11... | collective-permute-start | bytes 7864328 | tf_op jit(solution)/shard_map/ppermute | solution.py:94
  133.8 31.4 %collective-permute-start.16 = (bf16[4,32,16,256]{3,2,1,0:T(8,128)(2,1)}, bf16[4,32,16,256]{3,2,1,0:T(8,128)(2,1)}, u32[]{:S(2)}, u32[]{:S(2)}) collective-permute-start(bf16[4,32,16,256]{3,2,1,0:T(8,128)(2,1)} %pad_maximum_fusion.8), channel_id=1, source_target_pairs={{0,4},{1,5},{2,6},{3,7},{4,0},{5,1},{6,2},{7,3},{8,12},{9,13},{10,... | collective-permute-start | bytes 3145736 | tf_op jit(solution)/shard_map/ppermute | solution.py:105
  135.9 28.4 %collective-permute-start.17 = (bf16[1,32,16,256]{3,2,1,0:T(8,128)(2,1)S(1)}, bf16[1,32,16,256]{3,2,1,0:T(8,128)(2,1)}, u32[]{:S(2)}, u32[]{:S(2)}) collective-permute-start(bf16[1,32,16,256]{3,2,1,0:T(8,128)(2,1)S(1)} %bitcast.264), channel_id=1, source_target_pairs={{0,8},{1,9},{2,10},{3,11},{4,12},{5,13},{6,14},{7,15},{8,0},{9,1},... | collective-permute-start | bytes 786440 | tf_op jit(solution)/shard_map/ppermute | solution.py:105
  165.2 14.7 %collective-permute-start.18 = (bf16[8,40,16,256]{3,2,1,0:T(8,128)(2,1)}, bf16[8,40,16,256]{3,2,1,0:T(8,128)(2,1)}, u32[]{:S(2)}, u32[]{:S(2)}) collective-permute-start(bf16[8,40,16,256]{3,2,1,0:T(8,128)(2,1)} %collective-permute-done.14.refs_1_), channel_id=1, source_target_pairs={{0,1},{1,0},{2,3},{3,2},{4,5},{5,4},{6,7},{7,6},{8,9},{9,8},{10,11... | collective-permute-start | bytes 7864328 | tf_op jit(solution)/shard_map/ppermute | solution.py:94
  169.1 61.1 %collective-permute-start.20 = (bf16[8,32,16,256]{3,2,1,0:T(8,128)(2,1)}, bf16[8,32,16,256]{3,2,1,0:T(8,128)(2,1)}, u32[]{:S(2)}, u32[]{:S(2)}) collective-permute-start(bf16[8,32,16,256]{3,2,1,0:T(8,128)(2,1)} %pad_maximum_fusion.1.refs_0_), channel_id=1, source_target_pairs={{0,16},{1,3},{2,18},{3,1},{4,20},{5,7},{6,22},{7,5},{8,24},{9,11},... | collective-permute-start | bytes 6291464 | tf_op jit(solution)/shard_map/ppermute | solution.py:105
  170.0 60.2 %collective-permute-start.21 = (bf16[8,32,16,256]{3,2,1,0:T(8,128)(2,1)}, bf16[8,32,16,256]{3,2,1,0:T(8,128)(2,1)}, u32[]{:S(2)}, u32[]{:S(2)}) collective-permute-start(bf16[8,32,16,256]{3,2,1,0:T(8,128)(2,1)} %pad_maximum_fusion.1.refs_0_), channel_id=1, source_target_pairs={{0,1},{1,0},{2,3},{3,2},{4,5},{5,4},{6,7},{7,6},{8,9},{9,8},{10,11... | collective-permute-start | bytes 6291464 | tf_op jit(solution)/shard_map/ppermute | solution.py:94
  171.6 40.6 %all-to-all-start.1 = ((bf16[2,16,32,512]{3,2,0,1:T(8,128)(2,1)}), bf16[2,16,32,512]{3,2,0,1:T(8,128)(2,1)S(1)}, u32[]{:S(2)}, u32[]{:S(2)}) async-start(bf16[2,16,32,512]{3,2,0,1:T(8,128)(2,1)} %copy.66), calls=%async_computation.1 | async-start | bytes 2097152 | tf_op jit(solution)/shard_map/all_to_all | solution.py:669
  177.8 24.9 %collective-permute-start.19 = (bf16[2,32,16,256]{3,2,1,0:T(8,128)(2,1)S(1)}, bf16[2,32,16,256]{3,2,1,0:T(8,128)(2,1)}, u32[]{:S(2)}, u32[]{:S(2)}) collective-permute-start(bf16[2,32,16,256]{3,2,1,0:T(8,128)(2,1)S(1)} %pad_maximum_fusion.18), channel_id=1, source_target_pairs={{0,2},{1,17},{2,0},{3,19},{4,6},{5,21},{6,4},{7,23},{8,10},{9,25},... | collective-permute-start | bytes 1572872 | tf_op jit(solution)/shard_map/ppermute | solution.py:105
  214.4 15.8 %collective-permute-start.22 = (bf16[4,32,16,256]{3,2,1,0:T(8,128)(2,1)}, bf16[4,32,16,256]{3,2,1,0:T(8,128)(2,1)}, u32[]{:S(2)}, u32[]{:S(2)}) collective-permute-start(bf16[4,32,16,256]{3,2,1,0:T(8,128)(2,1)} %pad_maximum_fusion.9), channel_id=1, source_target_pairs={{0,16},{1,5},{2,18},{3,7},{4,20},{5,1},{6,22},{7,3},{8,24},{9,13},... | collective-permute-start | bytes 3145736 | tf_op jit(solution)/shard_map/ppermute | solution.py:105
  230.3 13.0 %collective-permute-start.23 = (bf16[8,32,16,256]{3,2,1,0:T(8,128)(2,1)}, bf16[8,32,16,256]{3,2,1,0:T(8,128)(2,1)}, u32[]{:S(2)}, u32[]{:S(2)}) collective-permute-start(bf16[8,32,16,256]{3,2,1,0:T(8,128)(2,1)} %collective-permute-done.20.refs_1_), channel_id=1, source_target_pairs={{0,1},{1,0},{2,3},{3,2},{4,5},{5,4},{6,7},{7,6},{8,9},{9,8},{10,11... | collective-permute-start | bytes 6291464 | tf_op jit(solution)/shard_map/ppermute | solution.py:94
  233.9 38.1 %collective-permute-start.24 = (bf16[8,32,16,256]{3,2,1,0:T(8,128)(2,1)}, bf16[8,32,16,256]{3,2,1,0:T(8,128)(2,1)}, u32[]{:S(2)}, u32[]{:S(2)}) collective-permute-start(bf16[8,32,16,256]{3,2,1,0:T(8,128)(2,1)} %pad_maximum_fusion.2.refs_0_), channel_id=1, source_target_pairs={{0,4},{1,3},{2,6},{3,1},{4,0},{5,7},{6,2},{7,5},{8,12},{9,11},{10,... | collective-permute-start | bytes 6291464 | tf_op jit(solution)/shard_map/ppermute | solution.py:105
  235.5 36.5 %collective-permute-start.25 = (bf16[8,32,16,256]{3,2,1,0:T(8,128)(2,1)}, bf16[8,32,16,256]{3,2,1,0:T(8,128)(2,1)}, u32[]{:S(2)}, u32[]{:S(2)}) collective-permute-start(bf16[8,32,16,256]{3,2,1,0:T(8,128)(2,1)} %pad_maximum_fusion.2.refs_0_), channel_id=1, source_target_pairs={{0,1},{1,0},{2,3},{3,2},{4,5},{5,4},{6,7},{7,6},{8,9},{9,8},{10,11... | collective-permute-start | bytes 6291464 | tf_op jit(solution)/shard_map/ppermute | solution.py:94
  237.1 41.9 %all-to-all-start.2 = ((bf16[32,1,32,512]{3,2,1,0:T(8,128)(2,1)}), bf16[32,1,32,512]{3,2,1,0:T(8,128)(2,1)S(1)}, u32[]{:S(2)}, u32[]{:S(2)}) async-start(bf16[32,1,32,512]{3,2,1,0:T(8,128)(2,1)} %bitcast.260), calls=%async_computation.2 | async-start | bytes 2097152 | tf_op jit(solution)/shard_map/all_to_all | solution.py:674
  272.1 10.1 %collective-permute-start.26 = (bf16[8,32,16,256]{3,2,1,0:T(8,128)(2,1)}, bf16[8,32,16,256]{3,2,1,0:T(8,128)(2,1)}, u32[]{:S(2)}, u32[]{:S(2)}) collective-permute-start(bf16[8,32,16,256]{3,2,1,0:T(8,128)(2,1)} %collective-permute-done.24.refs_1_), channel_id=1, source_target_pairs={{0,1},{1,0},{2,3},{3,2},{4,5},{5,4},{6,7},{7,6},{8,9},{9,8},{10,11... | collective-permute-start | bytes 6291464 | tf_op jit(solution)/shard_map/ppermute | solution.py:94
  282.0 43.7 %collective-permute-start.30 = (bf16[512,4096]{1,0:T(8,128)(2,1)}, bf16[512,4096]{1,0:T(8,128)(2,1)}, u32[]{:S(2)}, u32[]{:S(2)}) collective-permute-start(bf16[512,4096]{1,0:T(8,128)(2,1)} %get-tuple-element.201.x_own), channel_id=1, source_target_pairs={{0,1},{1,0},{2,3},{3,2},{4,5},{5,4},{6,7},{7,6},{8,9},{9,8},{10,11... | collective-permute-start | bytes 12582920 | tf_op jit(solution)/shard_map/ppermute | solution.py:94
  313.4 23.5 %collective-permute-start.29 = (bf16[512,4096]{1,0:T(8,128)(2,1)}, bf16[512,4096]{1,0:T(8,128)(2,1)}, u32[]{:S(2)}, u32[]{:S(2)}) collective-permute-start(bf16[512,4096]{1,0:T(8,128)(2,1)} %multiply_convert_fusion.refs_0_), channel_id=1, source_target_pairs={{0,1},{1,0},{2,3},{3,2},{4,5},{5,4},{6,7},{7,6},{8,9},{9,8},{10,11... | collective-permute-start | bytes 12582920 | tf_op jit(solution)/shard_map/ppermute | solution.py:94
  313.4 12.2 %collective-permute-start.31 = (bf16[512,1024]{1,0:T(8,128)(2,1)}, bf16[512,1024]{1,0:T(8,128)(2,1)}, u32[]{:S(2)}, u32[]{:S(2)}) collective-permute-start(bf16[512,1024]{1,0:T(8,128)(2,1)} %copy-done.28), channel_id=1, source_target_pairs={{0,1},{1,0},{2,3},{3,2},{4,5},{5,4},{6,7},{7,6},{8,9},{9,8},{10,11... | collective-permute-start | bytes 3145736 | tf_op jit(solution)/shard_map/ppermute | solution.py:94
  315.8 37.6 %collective-permute-start.32 = (bf16[512,1024]{1,0:T(8,128)(2,1)S(1)}, bf16[512,1024]{1,0:T(8,128)(2,1)}, u32[]{:S(2)}, u32[]{:S(2)}) collective-permute-start(bf16[512,1024]{1,0:T(8,128)(2,1)S(1)} %copy-done.8), channel_id=1, source_target_pairs={{0,1},{1,0},{2,3},{3,2},{4,5},{5,4},{6,7},{7,6},{8,9},{9,8},{10,11... | collective-permute-start | bytes 3145736 | tf_op jit(solution)/shard_map/ppermute | solution.py:94
  337.0 26.4 %collective-permute-start.33 = (bf16[8,32,16,256]{3,2,1,0:T(8,128)(2,1)}, bf16[8,32,16,256]{3,2,1,0:T(8,128)(2,1)}, u32[]{:S(2)}, u32[]{:S(2)}) collective-permute-start(bf16[8,32,16,256]{3,2,1,0:T(8,128)(2,1)} %bitcast.327), channel_id=1, source_target_pairs={{0,4},{1,3},{2,6},{3,1},{4,0},{5,7},{6,2},{7,5},{8,12},{9,11},{10,... | collective-permute-start | bytes 6291464 | tf_op jit(solution)/shard_map/ppermute | solution.py:105
  367.7 20.1 %collective-permute-start.34 = (bf16[4,32,16,256]{3,2,1,0:T(8,128)(2,1)}, bf16[4,32,16,256]{3,2,1,0:T(8,128)(2,1)}, u32[]{:S(2)}, u32[]{:S(2)}) collective-permute-start(bf16[4,32,16,256]{3,2,1,0:T(8,128)(2,1)} %get-tuple-element.327), channel_id=1, source_target_pairs={{0,16},{1,5},{2,18},{3,7},{4,20},{5,1},{6,22},{7,3},{8,24},{9,13},... | collective-permute-start | bytes 3145736 | tf_op jit(solution)/shard_map/ppermute | solution.py:105
  370.4 51.7 %all-to-all-start.3 = ((bf16[2,16,32,512]{3,2,0,1:T(8,128)(2,1)}), bf16[2,16,32,512]{3,2,0,1:T(8,128)(2,1)}, u32[]{:S(2)}, u32[]{:S(2)}) async-start(bf16[2,16,32,512]{3,2,0,1:T(8,128)(2,1)} %copy.69), calls=%async_computation.3 | async-start | bytes 2097152 | tf_op jit(solution)/shard_map/all_to_all | solution.py:669
  374.9 47.2 %collective-permute-start.36 = (bf16[8,32,16,256]{3,2,1,0:T(8,128)(2,1)}, bf16[8,32,16,256]{3,2,1,0:T(8,128)(2,1)}, u32[]{:S(2)}, u32[]{:S(2)}) collective-permute-start(bf16[8,32,16,256]{3,2,1,0:T(8,128)(2,1)} %bitcast.326), channel_id=1, source_target_pairs={{0,16},{1,3},{2,18},{3,1},{4,20},{5,7},{6,22},{7,5},{8,24},{9,11},... | collective-permute-start | bytes 6291464 | tf_op jit(solution)/shard_map/ppermute | solution.py:105
  393.2 22.3 %collective-permute-start.35 = (bf16[512,1024]{1,0:T(8,128)(2,1)S(1)}, bf16[512,1024]{1,0:T(8,128)(2,1)S(1)}, u32[]{:S(2)}, u32[]{:S(2)}) collective-permute-start(bf16[512,1024]{1,0:T(8,128)(2,1)S(1)} %convert_element_type.387.refs_0_), channel_id=1, source_target_pairs={{0,1},{1,0},{2,3},{3,2},{4,5},{5,4},{6,7},{7,6},{8,9},{9,8},{10,11... | collective-permute-start | bytes 3145736 | tf_op jit(solution)/shard_map/ppermute | solution.py:94
  396.0 30.1 %collective-permute-start.44 = (bf16[512,1024]{1,0:T(8,128)(2,1)}, bf16[512,1024]{1,0:T(8,128)(2,1)}, u32[]{:S(2)}, u32[]{:S(2)}) collective-permute-start(bf16[512,1024]{1,0:T(8,128)(2,1)} %get-tuple-element.177.x_own.o_ref), channel_id=1, source_target_pairs={{0,1},{1,0},{2,3},{3,2},{4,5},{5,4},{6,7},{7,6},{8,9},{9,8},{10,11... | collective-permute-start | bytes 3145736 | tf_op jit(solution)/shard_map/ppermute | solution.py:94
  398.4 14.8 %collective-permute-start.37 = (bf16[2,32,16,256]{3,2,1,0:T(8,128)(2,1)S(1)}, bf16[2,32,16,256]{3,2,1,0:T(8,128)(2,1)S(1)}, u32[]{:S(2)}, u32[]{:S(2)}) collective-permute-start(bf16[2,32,16,256]{3,2,1,0:T(8,128)(2,1)S(1)} %get-tuple-element.336), channel_id=1, source_target_pairs={{0,2},{1,17},{2,0},{3,19},{4,6},{5,21},{6,4},{7,23},{8,10},{9,25},... | collective-permute-start | bytes 1572872 | tf_op jit(solution)/shard_map/ppermute | solution.py:105
  399.7 28.1 %collective-permute-start.42 = (bf16[512,1024]{1,0:T(8,128)(2,1)S(1)}, bf16[512,1024]{1,0:T(8,128)(2,1)}, u32[]{:S(2)}, u32[]{:S(2)}) collective-permute-start(bf16[512,1024]{1,0:T(8,128)(2,1)S(1)} %copy-done.22), channel_id=1, source_target_pairs={{0,1},{1,0},{2,3},{3,2},{4,5},{5,4},{6,7},{7,6},{8,9},{9,8},{10,11... | collective-permute-start | bytes 3145736 | tf_op jit(solution)/shard_map/ppermute | solution.py:94
  413.2 33.7 %collective-permute-start.38 = (bf16[512,1024]{1,0:T(8,128)(2,1)}, bf16[512,1024]{1,0:T(8,128)(2,1)}, u32[]{:S(2)}, u32[]{:S(2)}) collective-permute-start(bf16[512,1024]{1,0:T(8,128)(2,1)} %get-tuple-element.190.o_ref.x_own), channel_id=1, source_target_pairs={{0,1},{1,0},{2,3},{3,2},{4,5},{5,4},{6,7},{7,6},{8,9},{9,8},{10,11... | collective-permute-start | bytes 3145736 | tf_op jit(solution)/shard_map/ppermute | solution.py:94
  415.4 31.6 %collective-permute-start.39 = (bf16[512,1024]{1,0:T(8,128)(2,1)S(1)}, bf16[512,1024]{1,0:T(8,128)(2,1)}, u32[]{:S(2)}, u32[]{:S(2)}) collective-permute-start(bf16[512,1024]{1,0:T(8,128)(2,1)S(1)} %copy-done.19), channel_id=1, source_target_pairs={{0,1},{1,0},{2,3},{3,2},{4,5},{5,4},{6,7},{7,6},{8,9},{9,8},{10,11... | collective-permute-start | bytes 3145736 | tf_op jit(solution)/shard_map/ppermute | solution.py:94
  426.1 31.5 %collective-permute-start.45 = (bf16[4,32,16,256]{3,2,1,0:T(8,128)(2,1)}, bf16[4,32,16,256]{3,2,1,0:T(8,128)(2,1)}, u32[]{:S(2)}, u32[]{:S(2)}) collective-permute-start(bf16[4,32,16,256]{3,2,1,0:T(8,128)(2,1)} %get-tuple-element.325), channel_id=1, source_target_pairs={{0,4},{1,5},{2,6},{3,7},{4,0},{5,1},{6,2},{7,3},{8,12},{9,13},{10,... | collective-permute-start | bytes 3145736 | tf_op jit(solution)/shard_map/ppermute | solution.py:105
  429.3 11.6 %collective-permute-start.41 = (bf16[128,1024]{1,0:T(8,128)(2,1)S(1)}, bf16[128,1024]{1,0:T(8,128)(2,1)S(1)}, u32[]{:S(2)}, u32[]{:S(2)}) collective-permute-start(bf16[128,1024]{1,0:T(8,128)(2,1)S(1)} %copy-done.40), channel_id=1, source_target_pairs={{0,1},{1,0},{2,3},{3,2},{4,5},{5,4},{6,7},{7,6},{8,9},{9,8},{10,11... | collective-permute-start | bytes 786440 | tf_op jit(solution)/shard_map/ppermute | solution.py:94
  429.7 27.0 %collective-permute-start.46 = (bf16[1,32,16,256]{3,2,1,0:T(8,128)(2,1)S(1)}, bf16[1,32,16,256]{3,2,1,0:T(8,128)(2,1)S(1)}, u32[]{:S(2)}, u32[]{:S(2)}) collective-permute-start(bf16[1,32,16,256]{3,2,1,0:T(8,128)(2,1)S(1)} %add_convert_fusion.27), channel_id=1, source_target_pairs={{0,8},{1,9},{2,10},{3,11},{4,12},{5,13},{6,14},{7,15},{8,0},{9,1},... | collective-permute-start | bytes 786440 | tf_op jit(solution)/shard_map/ppermute | solution.py:105
  457.6 47.3 %collective-permute-start.47 = (bf16[8,40,16,256]{3,2,1,0:T(8,128)(2,1)}, bf16[8,40,16,256]{3,2,1,0:T(8,128)(2,1)}, u32[]{:S(2)}, u32[]{:S(2)}) collective-permute-start(bf16[8,40,16,256]{3,2,1,0:T(8,128)(2,1)} %bitcast.245), channel_id=1, source_target_pairs={{0,2},{1,17},{2,0},{3,19},{4,6},{5,21},{6,4},{7,23},{8,10},{9,25},... | collective-permute-start | bytes 7864328 | tf_op jit(solution)/shard_map/ppermute | solution.py:105
  461.0 43.9 %collective-permute-start.48 = (bf16[2,32,16,256]{3,2,1,0:T(8,128)(2,1)S(1)}, bf16[2,32,16,256]{3,2,1,0:T(8,128)(2,1)S(1)}, u32[]{:S(2)}, u32[]{:S(2)}) collective-permute-start(bf16[2,32,16,256]{3,2,1,0:T(8,128)(2,1)S(1)} %get-tuple-element.334), channel_id=1, source_target_pairs={{0,2},{1,17},{2,0},{3,19},{4,6},{5,21},{6,4},{7,23},{8,10},{9,25},... | collective-permute-start | bytes 1572872 | tf_op jit(solution)/shard_map/ppermute | solution.py:105
  464.9 52.7 %all-to-all-start.4 = ((bf16[32,1,32,512]{3,2,1,0:T(8,128)(2,1)}), bf16[32,1,32,512]{3,2,1,0:T(8,128)(2,1)}, u32[]{:S(2)}, u32[]{:S(2)}) async-start(bf16[32,1,32,512]{3,2,1,0:T(8,128)(2,1)} %bitcast.67), calls=%async_computation.4 | async-start | bytes 2097152 | tf_op jit(solution)/shard_map/all_to_all | solution.py:674
  509.8 18.7 %collective-permute-start.52 = (bf16[4,40,16,256]{3,2,1,0:T(8,128)(2,1)}, bf16[4,40,16,256]{3,2,1,0:T(8,128)(2,1)}, u32[]{:S(2)}, u32[]{:S(2)}) collective-permute-start(bf16[4,40,16,256]{3,2,1,0:T(8,128)(2,1)} %get-tuple-element.323), channel_id=1, source_target_pairs={{0,16},{1,3},{2,18},{3,1},{4,20},{5,7},{6,22},{7,5},{8,24},{9,11},... | collective-permute-start | bytes 3932168 | tf_op jit(solution)/shard_map/ppermute | solution.py:105
  511.9 8.1 %collective-permute-start.49 = (bf16[512,1024]{1,0:T(8,128)(2,1)}, bf16[512,1024]{1,0:T(8,128)(2,1)}, u32[]{:S(2)}, u32[]{:S(2)}) collective-permute-start(bf16[512,1024]{1,0:T(8,128)(2,1)} %get-tuple-element.261.refs_0_), channel_id=1, source_target_pairs={{0,1},{1,0},{2,3},{3,2},{4,5},{5,4},{6,7},{7,6},{8,9},{9,8},{10,11... | collective-permute-start | bytes 3145736 | tf_op jit(solution)/shard_map/ppermute | solution.py:94
  511.9 8.1 %collective-permute-start.50 = (bf16[512,1024]{1,0:T(8,128)(2,1)}, bf16[512,1024]{1,0:T(8,128)(2,1)}, u32[]{:S(2)}, u32[]{:S(2)}) collective-permute-start(bf16[512,1024]{1,0:T(8,128)(2,1)} %get-tuple-element.262.refs_1_), channel_id=1, source_target_pairs={{0,1},{1,0},{2,3},{3,2},{4,5},{5,4},{6,7},{7,6},{8,9},{9,8},{10,11... | collective-permute-start | bytes 3145736 | tf_op jit(solution)/shard_map/ppermute | solution.py:94
  512.5 16.0 %collective-permute-start.53 = (bf16[1,32,16,256]{3,2,1,0:T(8,128)(2,1)S(1)}, bf16[1,32,16,256]{3,2,1,0:T(8,128)(2,1)S(1)}, u32[]{:S(2)}, u32[]{:S(2)}) collective-permute-start(bf16[1,32,16,256]{3,2,1,0:T(8,128)(2,1)S(1)} %add_convert_fusion.26), channel_id=1, source_target_pairs={{0,8},{1,9},{2,10},{3,11},{4,12},{5,13},{6,14},{7,15},{8,0},{9,1},... | collective-permute-start | bytes 786440 | tf_op jit(solution)/shard_map/ppermute | solution.py:105
  530.3 22.2 %collective-permute-start.54 = (bf16[8,24,16,256]{3,2,1,0:T(8,128)(2,1)}, bf16[8,24,16,256]{3,2,1,0:T(8,128)(2,1)}, u32[]{:S(2)}, u32[]{:S(2)}) collective-permute-start(bf16[8,24,16,256]{3,2,1,0:T(8,128)(2,1)} %bitcast.76), channel_id=1, source_target_pairs={{0,2},{1,17},{2,0},{3,19},{4,6},{5,21},{6,4},{7,23},{8,10},{9,25},... | collective-permute-start | bytes 4718600 | tf_op jit(solution)/shard_map/ppermute | solution.py:105
  534.9 17.6 %collective-permute-start.55 = (bf16[2,40,16,256]{3,2,1,0:T(8,128)(2,1)}, bf16[2,40,16,256]{3,2,1,0:T(8,128)(2,1)}, u32[]{:S(2)}, u32[]{:S(2)}) collective-permute-start(bf16[2,40,16,256]{3,2,1,0:T(8,128)(2,1)} %get-tuple-element.331), channel_id=1, source_target_pairs={{0,4},{1,5},{2,6},{3,7},{4,0},{5,1},{6,2},{7,3},{8,12},{9,13},{10,... | collective-permute-start | bytes 1966088 | tf_op jit(solution)/shard_map/ppermute | solution.py:105
  543.2 13.4 %collective-permute-start.56 = (f32[8704]{0:T(1024)S(1)}, f32[8704]{0:T(1024)S(1)}, u32[]{:S(2)}, u32[]{:S(2)}) collective-permute-start(f32[8704]{0:T(1024)S(1)} %get-tuple-element.306), channel_id=1, source_target_pairs={{0,1},{1,0},{2,3},{3,2},{4,5},{5,4},{6,7},{7,6},{8,9},{9,8},{10,11... | collective-permute-start | bytes 104456 | tf_op jit(solution)/shard_map/ppermute | solution.py:94
  554.5 26.8 %collective-permute-start.59 = (bf16[4,24,16,256]{3,2,1,0:T(8,128)(2,1)S(1)}, bf16[4,24,16,256]{3,2,1,0:T(8,128)(2,1)S(1)}, u32[]{:S(2)}, u32[]{:S(2)}) collective-permute-start(bf16[4,24,16,256]{3,2,1,0:T(8,128)(2,1)S(1)} %get-tuple-element.329), channel_id=1, source_target_pairs={{0,4},{1,5},{2,6},{3,7},{4,0},{5,1},{6,2},{7,3},{8,12},{9,13},{10,... | collective-permute-start | bytes 2359304 | tf_op jit(solution)/shard_map/ppermute | solution.py:105
  556.8 25.4 %collective-permute-start.57 = (bf16[512,512]{1,0:T(8,128)(2,1)S(1)}, bf16[512,512]{1,0:T(8,128)(2,1)S(1)}, u32[]{:S(2)}, u32[]{:S(2)}) collective-permute-start(bf16[512,512]{1,0:T(8,128)(2,1)S(1)} %constant_dynamic-slice_fusion), channel_id=1, source_target_pairs={{0,1},{1,0},{2,3},{3,2},{4,5},{5,4},{6,7},{7,6},{8,9},{9,8},{10,11... | collective-permute-start | bytes 1572872 | tf_op jit(solution)/shard_map/ppermute | solution.py:94
  558.6 24.9 %collective-permute-start.61 = (bf16[1,40,16,256]{3,2,1,0:T(8,128)(2,1)S(1)}, bf16[1,40,16,256]{3,2,1,0:T(8,128)(2,1)S(1)}, u32[]{:S(2)}, u32[]{:S(2)}) collective-permute-start(bf16[1,40,16,256]{3,2,1,0:T(8,128)(2,1)S(1)} %add_convert_fusion.21), channel_id=1, source_target_pairs={{0,8},{1,9},{2,10},{3,11},{4,12},{5,13},{6,14},{7,15},{8,0},{9,1},... | collective-permute-start | bytes 983048 | tf_op jit(solution)/shard_map/ppermute | solution.py:105
  581.5 7.8 %collective-permute-start.60 = (bf16[2,24,16,256]{3,2,1,0:T(8,128)(2,1)S(1)}, bf16[2,24,16,256]{3,2,1,0:T(8,128)(2,1)S(1)}, u32[]{:S(2)}, u32[]{:S(2)}) collective-permute-start(bf16[2,24,16,256]{3,2,1,0:T(8,128)(2,1)S(1)} %get-tuple-element.344), channel_id=1, source_target_pairs={{0,16},{1,3},{2,18},{3,1},{4,20},{5,7},{6,22},{7,5},{8,24},{9,11},... | collective-permute-start | bytes 1179656 | tf_op jit(solution)/shard_map/ppermute | solution.py:105
  589.4 9.5 %collective-permute-start.62 = (bf16[1,24,16,256]{3,2,1,0:T(8,128)(2,1)S(1)}, bf16[1,24,16,256]{3,2,1,0:T(8,128)(2,1)S(1)}, u32[]{:S(2)}, u32[]{:S(2)}) collective-permute-start(bf16[1,24,16,256]{3,2,1,0:T(8,128)(2,1)S(1)} %add_convert_fusion.29), channel_id=1, source_target_pairs={{0,8},{1,9},{2,10},{3,11},{4,12},{5,13},{6,14},{7,15},{8,0},{9,1},... | collective-permute-start | bytes 589832 | tf_op jit(solution)/shard_map/ppermute | solution.py:105
  600.6 18.1 %all-to-all-start.5 = ((bf16[64,16,256]{2,1,0:T(8,128)(2,1)}), bf16[64,16,256]{2,1,0:T(8,128)(2,1)S(1)}, u32[]{:S(2)}, u32[]{:S(2)}) async-start(bf16[64,16,256]{2,1,0:T(8,128)(2,1)} %gather_fusion.3), calls=%async_computation.5 | async-start | bytes 1048576 | tf_op jit(solution)/shard_map/all_to_all | solution.py:327
  618.7 19.7 %all-to-all-start.6 = ((bf16[72,16,256]{2,1,0:T(8,128)(2,1)}), bf16[72,16,256]{2,1,0:T(8,128)(2,1)S(1)}, u32[]{:S(2)}, u32[]{:S(2)}) async-start(bf16[72,16,256]{2,1,0:T(8,128)(2,1)} %bitcast.90), calls=%async_computation.6 | async-start | bytes 1179648 | tf_op jit(solution)/shard_map/all_to_all | solution.py:327
  622.4 13.6 %collective-permute-start.63 = (bf16[8,8,16,256]{3,2,1,0:T(8,128)(2,1)S(1)}, bf16[8,8,16,256]{3,2,1,0:T(8,128)(2,1)S(1)}, u32[]{:S(2)}, u32[]{:S(2)}) collective-permute-start(bf16[8,8,16,256]{3,2,1,0:T(8,128)(2,1)S(1)} %bitcast.285), channel_id=1, source_target_pairs={{0,16},{16,0},{1,17},{17,1},{2,18},{18,2},{3,19},{19,3},{4,20},{20... | collective-permute-start | bytes 1572872 | tf_op jit(solution)/shard_map/ppermute | solution.py:97
  638.5 13.8 %collective-permute-start.64 = (bf16[8,9,16,256]{3,2,1,0:T(8,128)(2,1)S(1)}, bf16[8,9,16,256]{3,2,1,0:T(8,128)(2,1)S(1)}, u32[]{:S(2)}, u32[]{:S(2)}) collective-permute-start(bf16[8,9,16,256]{3,2,1,0:T(8,128)(2,1)S(1)} %bitcast.276), channel_id=1, source_target_pairs={{0,16},{16,0},{1,17},{17,1},{2,18},{18,2},{3,19},{19,3},{4,20},{20... | collective-permute-start | bytes 1769480 | tf_op jit(solution)/shard_map/ppermute | solution.py:97
  (99 other events, 868.8 us)

commit v6 on v5

--- a/solution.py
+++ b/solution.py
@@ -87,7 +87,7 @@
             ((z2, x, z1, y), (z2, y, z1, x)),
             ((z2, x, y, z1), (z2, y, z1, x)),
         )
-        reducing = (((z2, y, z1, x), (z2, x, z1, y)),) + gathering[1:]
+        reducing = (((z2, z1, y, x), (z2, z1, x, y)),) + gathering[1:]
         self.orders = gathering + reducing
 
     def swap_core(self, value):
@@ -767,22 +767,24 @@
     q_c = (dot_nn(h_one_low, w_cq) + b_cq).astype(bf16)
     k_c = dot_nn(e, w_ck).astype(bf16)
     v_c = (dot_nn(e, w_cv) + b_cv).astype(bf16)
-    cot_pieces, q_c, k_c, v_c = step((cot_pieces, q_c, k_c, v_c), down)
-    cot_home = route_home(cot_pieces, seq_slots)
+    q_c, k_c, v_c = step((q_c, k_c, v_c), down)
     o_c, lse_c = attend_forward(limit, q_c, k_c, v_c, False)
     z_two = h_one + dot_nn(o_c, w_co) + b_co
     h_two, n_two, r_two = norm_forward(z_two, g_two, b_two)
-    h_two, h_two_low = step((h_two, h_two.astype(bf16)), up, down)
+    cot_pieces, h_two, h_two_low = step((cot_pieces, h_two, h_two.astype(bf16)), up, down)
+    cot_home = route_home(cot_pieces, seq_slots)
     (w_fi,) = placed(2)
     act, slope = gelu_forward(h_two_low, w_fi, b_fi)
     act_sib = net.swap_core(act)
     act, slope = step((act, slope), down)
     (w_fo,) = placed(3)
     z_three = h_two + dot_nn(act, w_fo) + b_fo
+    cot_home, z_three = step((cot_home, z_three))
+    cot, _ = whole(cot_home)
     h_three, n_three, r_three = norm_forward(z_three, g_three, b_three)
     live = (jnp.arange(x.shape[0]) < limit).astype(f32)[:, None]
     source = inverse_of(seq_slots)
-    finished = halved((h_three * live).astype(bf16))
+    finished = (h_three * live).astype(bf16)
 
     def gradient(k, *calls):
         held, first = None, 0
@@ -792,14 +794,14 @@
         parts = tuple(h.reshape(h.shape[0], -1, net.rows, BS) for h in held)
         return Flow(reduce_rounds(net, len(GROUPS) + k, parts))
 
-    cot, _ = whole(cot_home)
     grad_y = cot.astype(f32) * live
     d_three, dg_three, db_three = norm_backward(grad_y, n_three, r_three, g_three)
     a_three = d_three.astype(bf16)
     d_hidden = (dot_nt(a_three, w_fo) * slope.astype(f32)).astype(bf16)
     d_hidden_sib = net.swap_core(d_hidden)
     down = gradient(3, ((act, act_sib), (a_three, net.swap_core(a_three))))
-    d_hidden, d_hidden_sib = step((d_hidden, d_hidden_sib), down)
+    finished, d_hidden, d_hidden_sib = step((finished, d_hidden, d_hidden_sib), down)
+    finished = halved(finished)
     d_h_two = d_three + dot_nt(d_hidden, w_fi)
     d_two, dg_two, db_two = norm_backward(d_h_two, n_two, r_two, g_two)
     a_two = d_two.astype(bf16)
@@ -816,7 +818,7 @@
     a_one = d_one.astype(bf16)
     a_one_sib = net.swap_core(a_one)
     d_os = dot_nt(a_one, w_so).astype(bf16)
-    out_pieces, a_one, a_one_sib, d_os = step((out_pieces, a_one, a_one_sib, d_os), up, down)
+    out_pieces, a_one, a_one_sib, d_os = step((out_pieces, a_one, a_one_sib, d_os))
     outputs = route_home(out_pieces, source)
     cross = gradient(
         1,
@@ -825,39 +827,38 @@
         ((e, e_sib), (dk_c, dk_c_sib), (dv_c, dv_c_sib)),
         ((o_c, net.swap_core(o_c)), (a_two, net.swap_core(a_two))),
     )
-    (d_os,) = step((d_os,), cross, up, down)
+    outputs, d_os = step((outputs, d_os), cross, up, down)
     dq_s, dk_s, dv_s = attend_backward(limit, q_s, k_s, v_s, o_s, d_os, lse_s, True)
     sibs = [net.swap_core(v) for v in (dq_s, dk_s, dv_s)]
     dq_s, dk_s, dv_s = step((dq_s, dk_s, dv_s), cross, up)
     attn = gradient(0, ((x, x_sib), *zip((dq_s, dk_s, dv_s), sibs)))
-    d_hidden, dq_c, dk_c, dv_c, dq_s, dk_s, dv_s = step(
-        (d_hidden, dq_c, dk_c, dv_c, dq_s, dk_s, dv_s), attn, cross, up
-    )
+    dk_c, dv_c, dq_s, dk_s, dv_s = step((dk_c, dv_c, dq_s, dk_s, dv_s), attn, cross, up, down)
     state_back = dot_nt(dk_c, w_ck) + dot_nt(dv_c, w_cv)
     back = d_one + dot_nt(dq_s, w_sq) + dot_nt(dk_s, w_sk) + dot_nt(dv_s, w_sv)
-    outputs, back = step((outputs, back), attn, cross)
+    back, d_hidden, dq_c, dv_c = step((back, d_hidden, dq_c, dv_c), attn, cross, up)
     input_grad = halved(back.astype(bf16))
     encoded_grad = halved(state_back.astype(bf16))
+    dq_s, dv_s = step((dq_s, dv_s), attn)
+    columns = [jnp.sum(v.astype(f32), axis=0) for v in (d_hidden, dq_c, dv_c, dq_s, dv_s)]
+    *columns, input_grad, encoded_grad = step((*columns, input_grad, encoded_grad), attn, cross)
     sums = (
-        jnp.sum(dq_s.astype(f32), axis=0),
-        jnp.sum(dv_s.astype(f32), axis=0),
+        columns[3],
+        columns[4],
         jnp.sum(d_one, axis=0),
         dg_one,
         db_one,
-        jnp.sum(dq_c.astype(f32), axis=0),
-        jnp.sum(dv_c.astype(f32), axis=0),
+        columns[1],
+        columns[2],
         jnp.sum(d_two, axis=0),
         dg_two,
         db_two,
         jnp.sum(d_three, axis=0),
         dg_three,
         db_three,
-        jnp.sum(d_hidden.astype(f32), axis=0),
+        columns[0],
     )
     vec_pair = jnp.concatenate([s.reshape(halves, -1) for s in sums], axis=1)
     vec_sum = pick(vec_pair, core) + net.swap_core(pick(vec_pair, 1 - core))
-    step((), attn)
-    vec_sum, input_grad, encoded_grad = step((vec_sum, input_grad, encoded_grad), attn, cross)
     natural = [f.finish() for f in (attn, cross, up, down)]
 
     parts, flag, vec_owned = last_pieces(net, jnp.concatenate(natural), block_slots, vec_sum)

time: 676 us -> 657 us (0.972)
  waiting for transfers between devices: 205 us -> 194 us
    ppermute x32, waiting for transfers between devices: 124 us -> 98.3 us  [swap_data(): return lax.ppermute(value, ('rep', 'shard', 'mp'), pairs)]
    all_to_all x2, waiting for transfers between devices: 6.73 us -> 25.5 us  [route_home(): lax.all_to_all(moved, ('rep', 'shard'), split_axis=0, concat_axis=1, tile...]
    ppermute x32, starting transfers between devices: 35.4 us -> 46.4 us  [swap_data(): return lax.ppermute(value, ('rep', 'shard', 'mp'), pairs)]
    all_to_all x2, waiting for transfers between devices: 9.42 us -> 0.01 us  [route_out(): return lax.all_to_all(cut, axes, split_axis=1, concat_axis=0, tiled=True)]
    ppermute x31, starting transfers between devices: 14.6 us -> 6.81 us  [swap_core(): return lax.ppermute(value, 'mp', [(i, i ^ 1) for i in range(self.n_mp)])]
    unnamed x215 -> x209, local copies, waits for them, and re-layouts: 12.6 us -> 16.7 us
  transfers between devices with their start and end apart: 72 -> 72, of which waited for: 30 -> 33; matrix products, arithmetic and copies ran while one was open for 24% -> 21% of each run, Pallas kernels for 26% -> 25%
where the time goes in v6:
time: 657 us; the launch traced here: 646 us
  waiting for transfers between devices  194 us (30%)
  Pallas kernels  184 us (28%)
  starting transfers between devices  87.4 us (13%)
  other arithmetic  74 us (11%)
  matrix products  62.9 us (10%)
  local copies, waits for them, and re-layouts  40.6 us (6%)
    ppermute x32, waiting for transfers between devices, swap_data(): return lax.ppermute(value, ('rep', 'shard', 'mp'), pairs)  98.3 us
    pallas_call x7, Pallas kernels, weight_grad(): pl.pallas_call(functools.partial(weight_grad_body, count=count, outs=outs...  49.7 us
    ppermute x32, starting transfers between devices, swap_data(): return lax.ppermute(value, ('rep', 'shard', 'mp'), pairs)  46.4 us
    pallas_call x4, Pallas kernels, place(): pl.pallas_call(functools.partial(place_body, dests=dests, many=many, two=...  37.8 us
    dot_general x10, matrix products, dot_nt(): return lax.dot_general(a, b, NT, preferred_element_type=f32)  34.7 us
    pallas_call x2, Pallas kernels, attend_forward(): pl.pallas_call(functools.partial(attend_forward_body, causal=causal, rows...  29.1 us
    dot_general x9, matrix products, dot_nn(): return jnp.dot(a, b, preferred_element_type=f32)  28.3 us
    all_to_all x1, waiting for transfers between devices, first_pieces(): lax.all_to_all(cut.reshape(-1, net.rows, BS), 'shard', split_axis=0, conc...  27 us
  transfers between devices with their start and end apart: 72, of which 33 were waited for; matrix products, arithmetic and copies ran while one was open for 21% of the time, Pallas kernels for 25%

profile of v6, /device:TPU:0, one launch (start us, length us, event | category | flops | bytes accessed | tf_op | source)
XLA Modules:
  0.0 645.8 jit_solution(12478036516896547165)
XLA Ops:
  1.4 2.4 convert_element_type.363
  5.2 7.3 %all-to-all-start = ((bf16[136,16,256]{2,1,0:T(8,128)(2,1)}), bf16[136,16,256]{2,1,0:T(8,128)(2,1)S(1)}, u32[]{:S(2)}, u32[]{:S(2)}) async-start(bf16[136,16,256]{2,1,0:T(8,128)(2,1)} %bitcast.4), calls=%async_computation | async-start | bytes 2228224 | tf_op jit(solution)/shard_map/all_to_all | solution.py:271
  12.6 27.0 %all-to-all-done = bf16[136,16,256]{2,1,0:T(8,128)(2,1)S(1)} async-done(((bf16[136,16,256]{2,1,0:T(8,128)(2,1)}), bf16[136,16,256]{2,1,0:T(8,128)(2,1)S(1)}, u32[]{:S(2)}, u32[]{:S(2)}) %all-to-all-start) | async-done | bytes 1114144 | tf_op jit(solution)/shard_map/all_to_all | solution.py:271
  40.4 10.6 %collective-permute-done.2 = bf16[1,24,16,256]{3,2,1,0:T(8,128)(2,1)S(1)} collective-permute-done((bf16[1,24,16,256]{3,2,1,0:T(8,128)(2,1)S(1)}, bf16[1,24,16,256]{3,2,1,0:T(8,128)(2,1)S(1)}, u32[]{:S(2)}, u32[]{:S(2)}) %collective-permute-start.2) | collective-permute-done | bytes 196640 | tf_op jit(solution)/shard_map/ppermute | solution.py:105
  52.7 6.3 collective-permute-done.3
  62.2 14.0 %collective-permute-done.5 = bf16[1,40,16,256]{3,2,1,0:T(8,128)(2,1)S(1)} collective-permute-done((bf16[1,40,16,256]{3,2,1,0:T(8,128)(2,1)S(1)}, bf16[1,40,16,256]{3,2,1,0:T(8,128)(2,1)S(1)}, u32[]{:S(2)}, u32[]{:S(2)}) %collective-permute-start.5) | collective-permute-done | bytes 327712 | tf_op jit(solution)/shard_map/ppermute | solution.py:105
  93.2 9.8 %collective-permute-done.8 = bf16[2,40,16,256]{3,2,1,0:T(8,128)(2,1)} collective-permute-done((bf16[2,40,16,256]{3,2,1,0:T(8,128)(2,1)}, bf16[2,40,16,256]{3,2,1,0:T(8,128)(2,1)}, u32[]{:S(2)}, u32[]{:S(2)}) %collective-permute-start.8) | collective-permute-done | bytes 655392 | tf_op jit(solution)/shard_map/ppermute | solution.py:105
  108.9 8.5 %place.4 = (bf16[4,256,1024]{2,1,0:T(8,128)(2,1)}, bf16[4,256,1024]{2,1,0:T(8,128)(2,1)}, bf16[4,256,1024]{2,1,0:T(8,128)(2,1)}) custom-call(s32[41]{0:T(128)} %add_add_fusion.4.s, bf16[8,24,16,256]{3,2,1,0:T(8,128)(2,1)} %copy-done.19, bf16[8,24,16,256]{3,2,1,0:T(8,128)(2,1)} %collective-permute-done.6.refs_1_, ...), custom_call_target="tpu_custom_call" | custom-call | flops 1048576 | bytes 1048576 | tf_op jit(solution)/shard_map/place/pallas_call | solution.py:227
  119.0 4.0 add_convert_fusion.8.q_ref
  136.9 20.1 %attend_forward.2 = (bf16[512,1024]{1,0:T(8,128)(2,1)}, f32[512,128]{1,0:T(8,128)}) custom-call(s32[1]{0:T(128)} %dynamic_slice.88.lim, bf16[512,1024]{1,0:T(8,128)(2,1)} %add_convert_fusion.8.q_ref, bf16[512,1024]{1,0:T(8,128)(2,1)} %convolution_convert_fusion.2.k_ref, bf16[512,1024]{1,0:T(8,128)(2,1)} %add_convert_fusion.7.v_ref), custom_call_target="tpu_custom_call" | custom-call | flops 1048576 | bytes 1048576 | tf_op jit(solution)/shard_map/attend_forward/pallas_call | solution.py:382
  160.4 3.4 collective-permute-done.17
  165.7 3.0 pad_maximum_fusion.1.refs_0_
  171.3 4.8 all-to-all-start.1
  179.9 10.2 %place.5 = (bf16[4,256,1024]{2,1,0:T(8,128)(2,1)}, bf16[4,256,1024]{2,1,0:T(8,128)(2,1)}, bf16[4,256,1024]{2,1,0:T(8,128)(2,1)}, bf16[4,256,1024]{2,1,0:T(8,128)(2,1)}, bf16[4,256,1024]{2,1,0:T(8,128)(2,1)}) custom-call(s32[41]{0:T(128)} %add_add_fusion.5.s, bf16[8,40,16,256]{3,2,1,0:T(8,128)(2,1)} %copy-done.7, ...), custom_call_target="tpu_custom_call" | custom-call | flops 1048576 | bytes 1048576 | tf_op jit(solution)/shard_map/place/pallas_call | solution.py:227
  190.2 3.5 fusion.22
  205.7 9.0 %attend_forward.3 = (bf16[512,1024]{1,0:T(8,128)(2,1)}, f32[512,128]{1,0:T(8,128)}) custom-call(s32[1]{0:T(128)} %dynamic_slice.88.lim, bf16[512,1024]{1,0:T(8,128)(2,1)} %add_convert_fusion.6.q_ref, bf16[128,1024]{1,0:T(8,128)(2,1)} %convolution_convert_fusion.3.k_ref, bf16[128,1024]{1,0:T(8,128)(2,1)} %fusion.4.v_ref), custom_call_target="tpu_custom_call" | custom-call | flops 1048576 | bytes 1048576 | tf_op jit(solution)/shard_map/attend_forward/pallas_call | solution.py:382
  214.7 3.4 fusion.25
  228.6 9.5 %place.6 = bf16[4,256,4096]{2,1,0:T(8,128)(2,1)} custom-call(s32[41]{0:T(128)} %add_add_fusion.6.s, bf16[8,32,16,256]{3,2,1,0:T(8,128)(2,1)} %pad_maximum_fusion.1.refs_0_, bf16[8,32,16,256]{3,2,1,0:T(8,128)(2,1)} %collective-permute-done.20.refs_1_, bf16[8,32,16,256]{3,2,1,0:T(8,128)(2,1)} %collective-permute-done.21.refs_2_, ...), custom_call_target="tpu_custom_call" | custom-call | flops 1048576 | bytes 1048576 | tf_op jit(solution)/shard_map/place/pallas_call | solution.py:227
  238.1 19.1 %gelu_forward.1 = (bf16[512,4096]{1,0:T(8,128)(2,1)}, bf16[512,4096]{1,0:T(8,128)(2,1)}) custom-call(bf16[512,1024]{1,0:T(8,128)(2,1)} %get-tuple-element.207.h_ref.x_own, bf16[1024,4096]{1,0:T(8,128)(2,1)} %bitcast.239, f32[1,4096]{1,0:T(1,128)} %bitcast.292), custom_call_target="tpu_custom_call" | custom-call | flops 1048576 | bytes 1048576 | tf_op jit(solution)/shard_map/gelu_forward/pallas_call | solution.py:515
  259.4 4.8 all-to-all-start.2
  264.9 25.5 %all-to-all-done.2 = bf16[32,1,32,512]{3,2,1,0:T(8,128)(2,1)S(1)} async-done(((bf16[32,1,32,512]{3,2,1,0:T(8,128)(2,1)}), bf16[32,1,32,512]{3,2,1,0:T(8,128)(2,1)S(1)}, u32[]{:S(2)}, u32[]{:S(2)}) %all-to-all-start.2) | async-done | bytes 1048608 | tf_op jit(solution)/shard_map/all_to_all | solution.py:674
  290.5 9.5 %place.7 = bf16[16,256,1024]{2,1,0:T(8,128)(2,1)} custom-call(s32[41]{0:T(128)} %add_add_fusion.7.s, bf16[8,32,16,256]{3,2,1,0:T(8,128)(2,1)} %copy-done.14, bf16[8,32,16,256]{3,2,1,0:T(8,128)(2,1)} %collective-permute-done.24.refs_1_, bf16[8,32,16,256]{3,2,1,0:T(8,128)(2,1)} %collective-permute-done.25.refs_2_, ...), custom_call_target="tpu_custom_call" | custom-call | flops 1048576 | bytes 1048576 | tf_op jit(solution)/shard_map/place/pallas_call | solution.py:227
  300.1 8.3 %fusion.26 = f32[512,1024]{1,0:T(8,128)S(1)} fusion(bf16[512,4096]{1,0:T(8,128)(2,1)} %get-tuple-element.213.x_own, bf16[4096,1024]{1,0:T(8,128)(2,1)} %bitcast.242), kind=kOutput, calls=%fused_computation.235 | convolution fusion | flops 4294967296 | bytes 14680064 | tf_op jit(solution)/shard_map/dot_general | solution.py:43
  318.2 8.0 %multiply_convert_fusion.refs_0_ = bf16[512,4096]{1,0:T(8,128)(2,1)} fusion(bf16[512,4096]{1,0:T(8,128)(2,1)} %get-tuple-element.218, bf16[512,1024]{1,0:T(8,128)(2,1)} %convert_element_type.379.refs_0_, bf16[4096,1024]{1,0:T(8,128)(2,1)S(1)} %bitcast.245), kind=kOutput, calls=%fused_computation.6 | convolution fusion | flops 4301258752 | bytes 17825792 | tf_op jit(solution)/shard_map/dot_general | solution.py:47
  326.9 8.3 %collective-permute-done.30.refs_1_ = bf16[512,1024]{1,0:T(8,128)(2,1)} collective-permute-done((bf16[512,1024]{1,0:T(8,128)(2,1)}, bf16[512,1024]{1,0:T(8,128)(2,1)}, u32[]{:S(2)}, u32[]{:S(2)}) %collective-permute-start.30) | collective-permute-done | bytes 1048608 | tf_op jit(solution)/shard_map/ppermute | solution.py:94
  335.2 11.1 %weight_grad.7 = (bf16[8,1,32,16,256]{4,3,2,1,0:T(8,128)(2,1)}, bf16[8,1,32,16,256]{4,3,2,1,0:T(8,128)(2,1)}) custom-call(s32[41]{0:T(128)} %add_add_fusion.7.s, bf16[512,4096]{1,0:T(8,128)(2,1)} %get-tuple-element.213.x_own, bf16[512,4096]{1,0:T(8,128)(2,1)} %collective-permute-done.29.x_sib, bf16[512,1024]{1,0:T(8,128)(2,1)} %convert_element_type.379.refs_0_, ...), custom_call_target="tpu_custom_call" | custom-call | flops 1048576 | bytes 1048576 | tf_op jit(solution)/shard_map/weight_grad/pallas_call | solution.py:572
  349.0 10.3 %multiply_reduce_fusion.1 = (f32[1024]{0:T(1024)S(1)}, f32[512]{0:T(512)S(1)}, f32[512]{0:T(512)S(1)}, f32[1024]{0:T(1024)S(1)}, f32[512,1024]{1,0:T(8,128)S(1)}) fusion(f32[512,1024]{1,0:T(8,128)S(1)} %copy-done.6, f32[512]{0:T(512)S(1)} %add_rsqrt_fusion.1, f32[512]{0:T(512)S(1)} %broadcast_multiply_fusion.7, f32[1024]{0:T(1024)S(1)} %bitcast.300, ...), kind=kOutput, calls=%fused_computation.13 | convolution fusion | flops 4300207104 | bytes 18894848 | tf_op jit(solution)/shard_map/dot_general | solution.py:47
  365.1 9.7 %weight_grad.8 = (bf16[8,1,32,16,256]{4,3,2,1,0:T(8,128)(2,1)}, bf16[8,1,32,16,256]{4,3,2,1,0:T(8,128)(2,1)}) custom-call(s32[41]{0:T(128)} %add_add_fusion.6.s, bf16[512,1024]{1,0:T(8,128)(2,1)} %get-tuple-element.207.h_ref.x_own, bf16[512,1024]{1,0:T(8,128)(2,1)} %collective-permute-done.32.x_sib, bf16[512,4096]{1,0:T(8,128)(2,1)} %multiply_convert_fusion.refs_0_, ...), custom_call_target="tpu_custom_call" | custom-call | flops 1048576 | bytes 1048576 | tf_op jit(solution)/shard_map/weight_grad/pallas_call | solution.py:572
  374.8 3.6 add_convert_fusion.4
  381.6 4.1 all-to-all-start.3
  385.7 10.4 %attend_backward.2 = (bf16[512,1024]{1,0:T(8,128)(2,1)}, bf16[128,1024]{1,0:T(8,128)(2,1)}, bf16[128,1024]{1,0:T(8,128)(2,1)}) custom-call(s32[1]{0:T(128)} %dynamic_slice.88.lim, bf16[512,1024]{1,0:T(8,128)(2,1)} %add_convert_fusion.6.q_ref, bf16[128,1024]{1,0:T(8,128)(2,1)} %convolution_convert_fusion.3.k_ref, bf16[128,1024]{1,0:T(8,128)(2,1)} %fusion.4.v_ref, ...), custom_call_target="tpu_custom_call" | custom-call | flops 1048576 | bytes 1048576 | tf_op jit(solution)/shard_map/attend_backward/pallas_call | solution.py:465
  396.2 2.7 collective-permute-done.34
  398.9 4.4 multiply_reduce_fusion.2
  412.5 3.0 gather_fusion.2
  415.4 4.8 all-to-all-start.4
  424.2 2.8 add_convert_fusion.14
  430.9 4.8 weight_grad.9
  435.6 5.5 weight_grad.10
  441.8 5.3 weight_grad.11
  447.2 4.8 weight_grad.12
  452.0 2.5 copy.72
  455.8 3.4 add_convert_fusion.2
  460.7 16.3 %attend_backward.3 = (bf16[512,1024]{1,0:T(8,128)(2,1)}, bf16[512,1024]{1,0:T(8,128)(2,1)}, bf16[512,1024]{1,0:T(8,128)(2,1)}) custom-call(s32[1]{0:T(128)} %dynamic_slice.88.lim, bf16[512,1024]{1,0:T(8,128)(2,1)} %add_convert_fusion.8.q_ref, bf16[512,1024]{1,0:T(8,128)(2,1)} %convolution_convert_fusion.2.k_ref, bf16[512,1024]{1,0:T(8,128)(2,1)} %add_convert_fusion.7.v_ref, ...), custom_call_target="tpu_custom_call" | custom-call | flops 1048576 | bytes 1048576 | tf_op jit(solution)/shard_map/attend_backward/pallas_call | solution.py:465
  477.1 7.7 %collective-permute-done.46 = bf16[4,32,16,256]{3,2,1,0:T(8,128)(2,1)S(1)} collective-permute-done((bf16[4,32,16,256]{3,2,1,0:T(8,128)(2,1)}, bf16[4,32,16,256]{3,2,1,0:T(8,128)(2,1)S(1)}, u32[]{:S(2)}, u32[]{:S(2)}) %collective-permute-start.46) | collective-permute-done | bytes 1048608 | tf_op jit(solution)/shard_map/ppermute | solution.py:105
  486.4 4.1 add_convert_fusion
  492.8 2.6 add_convert_fusion.13
  499.7 8.5 %weight_grad.13 = (bf16[8,3,8,16,256]{4,3,2,1,0:T(8,128)(2,1)}, bf16[8,3,8,16,256]{4,3,2,1,0:T(8,128)(2,1)}) custom-call(s32[41]{0:T(128)} %add_add_fusion.5.s, bf16[512,1024]{1,0:T(8,128)(2,1)} %get-tuple-element.167.x_own, bf16[512,1024]{1,0:T(8,128)(2,1)} %get-tuple-element.268.x_sib, bf16[512,1024]{1,0:T(8,128)(2,1)} %get-tuple-element.287.refs_0_, ...), custom_call_target="tpu_custom_call" | custom-call | flops 1048576 | bytes 1048576 | tf_op jit(solution)/shard_map/weight_grad/pallas_call | solution.py:572
  508.2 3.5 collective-permute-done.52
  514.1 3.0 fusion.28
  533.3 7.1 %collective-permute-done.55 = bf16[1,32,16,256]{3,2,1,0:T(8,128)(2,1)S(1)} collective-permute-done((bf16[1,32,16,256]{3,2,1,0:T(8,128)(2,1)S(1)}, bf16[1,32,16,256]{3,2,1,0:T(8,128)(2,1)S(1)}, u32[]{:S(2)}, u32[]{:S(2)}) %collective-permute-start.55) | collective-permute-done | bytes 262176 | tf_op jit(solution)/shard_map/ppermute | solution.py:105
  546.4 3.2 convert_reduce_fusion
  549.9 4.1 collective-permute-done.56
  558.0 4.0 collective-permute-done.60
  562.0 5.9 collective-permute-done.59
  568.0 2.6 collective-permute-start.61
  571.9 6.8 %collective-permute-done.61 = bf16[1,24,16,256]{3,2,1,0:T(8,128)(2,1)S(1)} collective-permute-done((bf16[1,24,16,256]{3,2,1,0:T(8,128)(2,1)S(1)}, bf16[1,24,16,256]{3,2,1,0:T(8,128)(2,1)S(1)}, u32[]{:S(2)}, u32[]{:S(2)}) %collective-permute-start.61) | collective-permute-done | bytes 196640 | tf_op jit(solution)/shard_map/ppermute | solution.py:105
  580.2 4.8 all-to-all-start.5
  588.2 11.6 %all-to-all-done.5 = bf16[64,16,256]{2,1,0:T(8,128)(2,1)S(1)} async-done(((bf16[64,16,256]{2,1,0:T(8,128)(2,1)}), bf16[64,16,256]{2,1,0:T(8,128)(2,1)S(1)}, u32[]{:S(2)}, u32[]{:S(2)}) %all-to-all-start.5) | async-done | bytes 524320 | tf_op jit(solution)/shard_map/all_to_all | solution.py:327
  599.7 3.6 all-to-all-start.6
  603.4 13.5 %collective-permute-done.63.other_ref = bf16[8,8,16,256]{3,2,1,0:T(8,128)(2,1)S(1)} collective-permute-done((bf16[8,8,16,256]{3,2,1,0:T(8,128)(2,1)S(1)}, bf16[8,8,16,256]{3,2,1,0:T(8,128)(2,1)S(1)}, u32[]{:S(2)}, u32[]{:S(2)}) %collective-permute-start.63) | collective-permute-done | bytes 524320 | tf_op jit(solution)/shard_map/ppermute | solution.py:97
  616.9 2.5 all-to-all-done.6
  619.5 11.1 %shampoo.2 = (f32[1,16,256,256]{3,2,1,0:T(8,128)}, f32[1,16,256,256]{3,2,1,0:T(8,128)}, f32[1,16,256,256]{3,2,1,0:T(8,128)}, f32[1,16,256,256]{3,2,1,0:T(8,128)}) custom-call(s32[1]{0:T(128)} %bitcast.79.flag, bf16[8,8,16,256]{3,2,1,0:T(8,128)(2,1)} %bitcast.283, bf16[8,8,16,256]{3,2,1,0:T(8,128)(2,1)} %copy-done.66, f32[1,16,256,256]{3,2,1,0:T(8,128)} %w_ref.3, ...), custom_call_target="tpu_custom_call" | custom-call | flops 1048576 | bytes 1048576 | tf_op jit(solution)/shard_map/shampoo/pallas_call | solution.py:627
  630.6 2.6 collective-permute-done.64.other_ref
  634.6 10.9 %shampoo.3 = (f32[1,16,256,256]{3,2,1,0:T(8,128)}, f32[1,16,256,256]{3,2,1,0:T(8,128)}, f32[1,16,256,256]{3,2,1,0:T(8,128)}, f32[1,16,256,256]{3,2,1,0:T(8,128)}) custom-call(s32[1]{0:T(128)} %bitcast.79.flag, bf16[8,9,16,256]{3,2,1,0:T(8,128)(2,1)} %bitcast.275, ...), custom_call_target="tpu_custom_call", output_to_operand_aliasing={{0}: (8, {}), {1}: (9, {}), {2}: (10, {}), {3}: (11, {})} | custom-call | flops 1048576 | bytes 1048576 | tf_op jit(solution)/shard_map/shampoo/pallas_call | solution.py:627
  (487 shorter events, 169.7 us)
Async XLA Ops:
  5.2 34.5 %all-to-all-start = ((bf16[136,16,256]{2,1,0:T(8,128)(2,1)}), bf16[136,16,256]{2,1,0:T(8,128)(2,1)S(1)}, u32[]{:S(2)}, u32[]{:S(2)}) async-start(bf16[136,16,256]{2,1,0:T(8,128)(2,1)} %bitcast.4), calls=%async_computation | async-start | bytes 2228224 | tf_op jit(solution)/shard_map/all_to_all | solution.py:271
  40.3 10.7 %collective-permute-start.2 = (bf16[1,24,16,256]{3,2,1,0:T(8,128)(2,1)S(1)}, bf16[1,24,16,256]{3,2,1,0:T(8,128)(2,1)S(1)}, u32[]{:S(2)}, u32[]{:S(2)}) collective-permute-start(bf16[1,24,16,256]{3,2,1,0:T(8,128)(2,1)S(1)} %bitcast.269), channel_id=1, source_target_pairs={{0,8},{1,9},{2,10},{3,11},{4,12},{5,13},{6,14},{7,15},{8,0},{9,1},... | collective-permute-start | bytes 589832 | tf_op jit(solution)/shard_map/ppermute | solution.py:105
  51.1 7.8 %collective-permute-start.3 = (bf16[2,24,16,256]{3,2,1,0:T(8,128)(2,1)S(1)}, bf16[2,24,16,256]{3,2,1,0:T(8,128)(2,1)S(1)}, u32[]{:S(2)}, u32[]{:S(2)}) collective-permute-start(bf16[2,24,16,256]{3,2,1,0:T(8,128)(2,1)S(1)} %pad_maximum_fusion.19), channel_id=1, source_target_pairs={{0,16},{1,5},{2,18},{3,7},{4,20},{5,1},{6,22},{7,3},{8,24},{9,13},... | collective-permute-start | bytes 1179656 | tf_op jit(solution)/shard_map/ppermute | solution.py:105
  59.9 19.3 %collective-permute-start.4 = (bf16[4,24,16,256]{3,2,1,0:T(8,128)(2,1)}, bf16[4,24,16,256]{3,2,1,0:T(8,128)(2,1)}, u32[]{:S(2)}, u32[]{:S(2)}) collective-permute-start(bf16[4,24,16,256]{3,2,1,0:T(8,128)(2,1)} %pad_maximum_fusion.14), channel_id=1, source_target_pairs={{0,4},{1,3},{2,6},{3,1},{4,0},{5,7},{6,2},{7,5},{8,12},{9,11},{10,... | collective-permute-start | bytes 2359304 | tf_op jit(solution)/shard_map/ppermute | solution.py:105
  59.9 16.3 %collective-permute-start.5 = (bf16[1,40,16,256]{3,2,1,0:T(8,128)(2,1)S(1)}, bf16[1,40,16,256]{3,2,1,0:T(8,128)(2,1)S(1)}, u32[]{:S(2)}, u32[]{:S(2)}) collective-permute-start(bf16[1,40,16,256]{3,2,1,0:T(8,128)(2,1)S(1)} %bitcast.250), channel_id=1, source_target_pairs={{0,8},{1,9},{2,10},{3,11},{4,12},{5,13},{6,14},{7,15},{8,0},{9,1},... | collective-permute-start | bytes 983048 | tf_op jit(solution)/shard_map/ppermute | solution.py:105
  61.7 23.9 %collective-permute-start = (bf16[2,512,512]{2,1,0:T(8,128)(2,1)}, bf16[2,512,512]{2,1,0:T(8,128)(2,1)}, u32[]{:S(2)}, u32[]{:S(2)}) collective-permute-start(bf16[2,512,512]{2,1,0:T(8,128)(2,1)} %param.21), channel_id=1, source_target_pairs={{0,1},{1,0},{2,3},{3,2},{4,5},{5,4},{6,7},{7,6},{8,9},{9,8},{10,11... | collective-permute-start | bytes 3145736 | tf_op jit(solution)/shard_map/ppermute | solution.py:94
  61.7 21.0 %collective-permute-start.1 = (bf16[2,128,512]{2,1,0:T(8,128)(2,1)}, bf16[2,128,512]{2,1,0:T(8,128)(2,1)}, u32[]{:S(2)}, u32[]{:S(2)}) collective-permute-start(bf16[2,128,512]{2,1,0:T(8,128)(2,1)} %param.22), channel_id=1, source_target_pairs={{0,1},{1,0},{2,3},{3,2},{4,5},{5,4},{6,7},{7,6},{8,9},{9,8},{10,11... | collective-permute-start | bytes 786440 | tf_op jit(solution)/shard_map/ppermute | solution.py:94
  80.7 22.3 %collective-permute-start.6 = (bf16[8,24,16,256]{3,2,1,0:T(8,128)(2,1)S(1)}, bf16[8,24,16,256]{3,2,1,0:T(8,128)(2,1)}, u32[]{:S(2)}, u32[]{:S(2)}) collective-permute-start(bf16[8,24,16,256]{3,2,1,0:T(8,128)(2,1)S(1)} %pad_maximum_fusion.3.refs_0_), channel_id=1, source_target_pairs={{0,2},{1,17},{2,0},{3,19},{4,6},{5,21},{6,4},{7,23},{8,10},{9,25},... | collective-permute-start | bytes 4718600 | tf_op jit(solution)/shard_map/ppermute | solution.py:105
  82.0 21.0 %collective-permute-start.7 = (bf16[8,24,16,256]{3,2,1,0:T(8,128)(2,1)S(1)}, bf16[8,24,16,256]{3,2,1,0:T(8,128)(2,1)}, u32[]{:S(2)}, u32[]{:S(2)}) collective-permute-start(bf16[8,24,16,256]{3,2,1,0:T(8,128)(2,1)S(1)} %pad_maximum_fusion.3.refs_0_), channel_id=1, source_target_pairs={{0,1},{1,0},{2,3},{3,2},{4,5},{5,4},{6,7},{7,6},{8,9},{9,8},{10,11... | collective-permute-start | bytes 4718600 | tf_op jit(solution)/shard_map/ppermute | solution.py:94
  85.6 17.5 %collective-permute-start.8 = (bf16[2,40,16,256]{3,2,1,0:T(8,128)(2,1)}, bf16[2,40,16,256]{3,2,1,0:T(8,128)(2,1)}, u32[]{:S(2)}, u32[]{:S(2)}) collective-permute-start(bf16[2,40,16,256]{3,2,1,0:T(8,128)(2,1)} %pad_maximum_fusion.15), channel_id=1, source_target_pairs={{0,4},{1,5},{2,6},{3,7},{4,0},{5,1},{6,2},{7,3},{8,12},{9,13},{10,... | collective-permute-start | bytes 1966088 | tf_op jit(solution)/shard_map/ppermute | solution.py:105
  103.0 15.0 %collective-permute-start.10 = (bf16[1,32,16,256]{3,2,1,0:T(8,128)(2,1)S(1)}, bf16[1,32,16,256]{3,2,1,0:T(8,128)(2,1)S(1)}, u32[]{:S(2)}, u32[]{:S(2)}) collective-permute-start(bf16[1,32,16,256]{3,2,1,0:T(8,128)(2,1)S(1)} %bitcast.265), channel_id=1, source_target_pairs={{0,8},{1,9},{2,10},{3,11},{4,12},{5,13},{6,14},{7,15},{8,0},{9,1},... | collective-permute-start | bytes 786440 | tf_op jit(solution)/shard_map/ppermute | solution.py:105
  106.1 21.5 %collective-permute-start.12 = (bf16[4,40,16,256]{3,2,1,0:T(8,128)(2,1)}, bf16[4,40,16,256]{3,2,1,0:T(8,128)(2,1)}, u32[]{:S(2)}, u32[]{:S(2)}) collective-permute-start(bf16[4,40,16,256]{3,2,1,0:T(8,128)(2,1)} %pad_maximum_fusion.4), channel_id=1, source_target_pairs={{0,16},{1,3},{2,18},{3,1},{4,20},{5,7},{6,22},{7,5},{8,24},{9,11},... | collective-permute-start | bytes 3932168 | tf_op jit(solution)/shard_map/ppermute | solution.py:105
  118.0 10.8 %collective-permute-start.13 = (bf16[2,32,16,256]{3,2,1,0:T(8,128)(2,1)S(1)}, bf16[2,32,16,256]{3,2,1,0:T(8,128)(2,1)S(1)}, u32[]{:S(2)}, u32[]{:S(2)}) collective-permute-start(bf16[2,32,16,256]{3,2,1,0:T(8,128)(2,1)S(1)} %pad_maximum_fusion.17), channel_id=1, source_target_pairs={{0,2},{1,17},{2,0},{3,19},{4,6},{5,21},{6,4},{7,23},{8,10},{9,25},... | collective-permute-start | bytes 1572872 | tf_op jit(solution)/shard_map/ppermute | solution.py:105
  130.8 34.1 %collective-permute-start.14 = (bf16[8,40,16,256]{3,2,1,0:T(8,128)(2,1)S(1)}, bf16[8,40,16,256]{3,2,1,0:T(8,128)(2,1)}, u32[]{:S(2)}, u32[]{:S(2)}) collective-permute-start(bf16[8,40,16,256]{3,2,1,0:T(8,128)(2,1)S(1)} %pad_maximum_fusion.refs_0_), channel_id=1, source_target_pairs={{0,2},{1,17},{2,0},{3,19},{4,6},{5,21},{6,4},{7,23},{8,10},{9,25},... | collective-permute-start | bytes 7864328 | tf_op jit(solution)/shard_map/ppermute | solution.py:105
  132.2 32.6 %collective-permute-start.15 = (bf16[8,40,16,256]{3,2,1,0:T(8,128)(2,1)S(1)}, bf16[8,40,16,256]{3,2,1,0:T(8,128)(2,1)}, u32[]{:S(2)}, u32[]{:S(2)}) collective-permute-start(bf16[8,40,16,256]{3,2,1,0:T(8,128)(2,1)S(1)} %pad_maximum_fusion.refs_0_), channel_id=1, source_target_pairs={{0,1},{1,0},{2,3},{3,2},{4,5},{5,4},{6,7},{7,6},{8,9},{9,8},{10,11... | collective-permute-start | bytes 7864328 | tf_op jit(solution)/shard_map/ppermute | solution.py:94
  133.6 31.3 %collective-permute-start.16 = (bf16[4,32,16,256]{3,2,1,0:T(8,128)(2,1)}, bf16[4,32,16,256]{3,2,1,0:T(8,128)(2,1)}, u32[]{:S(2)}, u32[]{:S(2)}) collective-permute-start(bf16[4,32,16,256]{3,2,1,0:T(8,128)(2,1)} %pad_maximum_fusion.8), channel_id=1, source_target_pairs={{0,4},{1,5},{2,6},{3,7},{4,0},{5,1},{6,2},{7,3},{8,12},{9,13},{10,... | collective-permute-start | bytes 3145736 | tf_op jit(solution)/shard_map/ppermute | solution.py:105
  135.3 28.4 %collective-permute-start.17 = (bf16[1,32,16,256]{3,2,1,0:T(8,128)(2,1)S(1)}, bf16[1,32,16,256]{3,2,1,0:T(8,128)(2,1)}, u32[]{:S(2)}, u32[]{:S(2)}) collective-permute-start(bf16[1,32,16,256]{3,2,1,0:T(8,128)(2,1)S(1)} %bitcast.261), channel_id=1, source_target_pairs={{0,8},{1,9},{2,10},{3,11},{4,12},{5,13},{6,14},{7,15},{8,0},{9,1},... | collective-permute-start | bytes 786440 | tf_op jit(solution)/shard_map/ppermute | solution.py:105
  164.8 15.1 %collective-permute-start.18 = (bf16[8,40,16,256]{3,2,1,0:T(8,128)(2,1)}, bf16[8,40,16,256]{3,2,1,0:T(8,128)(2,1)}, u32[]{:S(2)}, u32[]{:S(2)}) collective-permute-start(bf16[8,40,16,256]{3,2,1,0:T(8,128)(2,1)} %collective-permute-done.14.refs_1_), channel_id=1, source_target_pairs={{0,1},{1,0},{2,3},{3,2},{4,5},{5,4},{6,7},{7,6},{8,9},{9,8},{10,11... | collective-permute-start | bytes 7864328 | tf_op jit(solution)/shard_map/ppermute | solution.py:94
  168.7 52.8 %collective-permute-start.20 = (bf16[8,32,16,256]{3,2,1,0:T(8,128)(2,1)}, bf16[8,32,16,256]{3,2,1,0:T(8,128)(2,1)}, u32[]{:S(2)}, u32[]{:S(2)}) collective-permute-start(bf16[8,32,16,256]{3,2,1,0:T(8,128)(2,1)} %pad_maximum_fusion.1.refs_0_), channel_id=1, source_target_pairs={{0,16},{1,3},{2,18},{3,1},{4,20},{5,7},{6,22},{7,5},{8,24},{9,11},... | collective-permute-start | bytes 6291464 | tf_op jit(solution)/shard_map/ppermute | solution.py:105
  170.2 51.3 %collective-permute-start.21 = (bf16[8,32,16,256]{3,2,1,0:T(8,128)(2,1)}, bf16[8,32,16,256]{3,2,1,0:T(8,128)(2,1)}, u32[]{:S(2)}, u32[]{:S(2)}) collective-permute-start(bf16[8,32,16,256]{3,2,1,0:T(8,128)(2,1)} %pad_maximum_fusion.1.refs_0_), channel_id=1, source_target_pairs={{0,1},{1,0},{2,3},{3,2},{4,5},{5,4},{6,7},{7,6},{8,9},{9,8},{10,11... | collective-permute-start | bytes 6291464 | tf_op jit(solution)/shard_map/ppermute | solution.py:94
  171.3 50.2 %all-to-all-start.1 = ((bf16[2,16,32,512]{3,2,0,1:T(8,128)(2,1)}), bf16[2,16,32,512]{3,2,0,1:T(8,128)(2,1)S(1)}, u32[]{:S(2)}, u32[]{:S(2)}) async-start(bf16[2,16,32,512]{3,2,0,1:T(8,128)(2,1)} %copy.66), calls=%async_computation.1 | async-start | bytes 2097152 | tf_op jit(solution)/shard_map/all_to_all | solution.py:669
  177.9 24.1 %collective-permute-start.19 = (bf16[2,32,16,256]{3,2,1,0:T(8,128)(2,1)}, bf16[2,32,16,256]{3,2,1,0:T(8,128)(2,1)}, u32[]{:S(2)}, u32[]{:S(2)}) collective-permute-start(bf16[2,32,16,256]{3,2,1,0:T(8,128)(2,1)} %pad_maximum_fusion.18), channel_id=1, source_target_pairs={{0,2},{1,17},{2,0},{3,19},{4,6},{5,21},{6,4},{7,23},{8,10},{9,25},... | collective-permute-start | bytes 1572872 | tf_op jit(solution)/shard_map/ppermute | solution.py:105
  204.2 18.9 %collective-permute-start.22 = (bf16[4,32,16,256]{3,2,1,0:T(8,128)(2,1)}, bf16[4,32,16,256]{3,2,1,0:T(8,128)(2,1)}, u32[]{:S(2)}, u32[]{:S(2)}) collective-permute-start(bf16[4,32,16,256]{3,2,1,0:T(8,128)(2,1)} %pad_maximum_fusion.9), channel_id=1, source_target_pairs={{0,16},{1,5},{2,18},{3,7},{4,20},{5,1},{6,22},{7,3},{8,24},{9,13},... | collective-permute-start | bytes 3145736 | tf_op jit(solution)/shard_map/ppermute | solution.py:105
  224.8 32.4 %collective-permute-start.24 = (bf16[8,32,16,256]{3,2,1,0:T(8,128)(2,1)S(1)}, bf16[8,32,16,256]{3,2,1,0:T(8,128)(2,1)}, u32[]{:S(2)}, u32[]{:S(2)}) collective-permute-start(bf16[8,32,16,256]{3,2,1,0:T(8,128)(2,1)S(1)} %pad_maximum_fusion.2.refs_0_), channel_id=1, source_target_pairs={{0,4},{1,3},{2,6},{3,1},{4,0},{5,7},{6,2},{7,5},{8,12},{9,11},{10,... | collective-permute-start | bytes 6291464 | tf_op jit(solution)/shard_map/ppermute | solution.py:105
  227.2 30.1 %collective-permute-start.25 = (bf16[8,32,16,256]{3,2,1,0:T(8,128)(2,1)S(1)}, bf16[8,32,16,256]{3,2,1,0:T(8,128)(2,1)}, u32[]{:S(2)}, u32[]{:S(2)}) collective-permute-start(bf16[8,32,16,256]{3,2,1,0:T(8,128)(2,1)S(1)} %pad_maximum_fusion.2.refs_0_), channel_id=1, source_target_pairs={{0,1},{1,0},{2,3},{3,2},{4,5},{5,4},{6,7},{7,6},{8,9},{9,8},{10,11... | collective-permute-start | bytes 6291464 | tf_op jit(solution)/shard_map/ppermute | solution.py:94
  257.3 33.3 %collective-permute-start.26 = (bf16[8,32,16,256]{3,2,1,0:T(8,128)(2,1)}, bf16[8,32,16,256]{3,2,1,0:T(8,128)(2,1)}, u32[]{:S(2)}, u32[]{:S(2)}) collective-permute-start(bf16[8,32,16,256]{3,2,1,0:T(8,128)(2,1)} %collective-permute-done.24.refs_1_), channel_id=1, source_target_pairs={{0,1},{1,0},{2,3},{3,2},{4,5},{5,4},{6,7},{7,6},{8,9},{9,8},{10,11... | collective-permute-start | bytes 6291464 | tf_op jit(solution)/shard_map/ppermute | solution.py:94
  259.4 31.0 %all-to-all-start.2 = ((bf16[32,1,32,512]{3,2,1,0:T(8,128)(2,1)}), bf16[32,1,32,512]{3,2,1,0:T(8,128)(2,1)S(1)}, u32[]{:S(2)}, u32[]{:S(2)}) async-start(bf16[32,1,32,512]{3,2,1,0:T(8,128)(2,1)} %bitcast.39), calls=%async_computation.2 | async-start | bytes 2097152 | tf_op jit(solution)/shard_map/all_to_all | solution.py:674
  309.6 17.3 %collective-permute-start.29 = (bf16[512,4096]{1,0:T(8,128)(2,1)}, bf16[512,4096]{1,0:T(8,128)(2,1)}, u32[]{:S(2)}, u32[]{:S(2)}) collective-permute-start(bf16[512,4096]{1,0:T(8,128)(2,1)} %get-tuple-element.213.x_own), channel_id=1, source_target_pairs={{0,1},{1,0},{2,3},{3,2},{4,5},{5,4},{6,7},{7,6},{8,9},{9,8},{10,11... | collective-permute-start | bytes 12582920 | tf_op jit(solution)/shard_map/ppermute | solution.py:94
  326.2 20.1 %collective-permute-start.28 = (bf16[512,4096]{1,0:T(8,128)(2,1)}, bf16[512,4096]{1,0:T(8,128)(2,1)}, u32[]{:S(2)}, u32[]{:S(2)}) collective-permute-start(bf16[512,4096]{1,0:T(8,128)(2,1)} %multiply_convert_fusion.refs_0_), channel_id=1, source_target_pairs={{0,1},{1,0},{2,3},{3,2},{4,5},{5,4},{6,7},{7,6},{8,9},{9,8},{10,11... | collective-permute-start | bytes 12582920 | tf_op jit(solution)/shard_map/ppermute | solution.py:94
  326.4 8.9 %collective-permute-start.30 = (bf16[512,1024]{1,0:T(8,128)(2,1)}, bf16[512,1024]{1,0:T(8,128)(2,1)}, u32[]{:S(2)}, u32[]{:S(2)}) collective-permute-start(bf16[512,1024]{1,0:T(8,128)(2,1)} %convert_element_type.379.refs_0_), channel_id=1, source_target_pairs={{0,1},{1,0},{2,3},{3,2},{4,5},{5,4},{6,7},{7,6},{8,9},{9,8},{10,11... | collective-permute-start | bytes 3145736 | tf_op jit(solution)/shard_map/ppermute | solution.py:94
  326.8 38.3 %collective-permute-start.32 = (bf16[512,1024]{1,0:T(8,128)(2,1)S(1)}, bf16[512,1024]{1,0:T(8,128)(2,1)}, u32[]{:S(2)}, u32[]{:S(2)}) collective-permute-start(bf16[512,1024]{1,0:T(8,128)(2,1)S(1)} %copy-done.10), channel_id=1, source_target_pairs={{0,1},{1,0},{2,3},{3,2},{4,5},{5,4},{6,7},{7,6},{8,9},{9,8},{10,11... | collective-permute-start | bytes 3145736 | tf_op jit(solution)/shard_map/ppermute | solution.py:94
  347.5 17.2 %collective-permute-start.31 = (bf16[512,512]{1,0:T(8,128)(2,1)S(1)}, bf16[512,512]{1,0:T(8,128)(2,1)S(1)}, u32[]{:S(2)}, u32[]{:S(2)}) collective-permute-start(bf16[512,512]{1,0:T(8,128)(2,1)S(1)} %constant_dynamic-slice_fusion.2), channel_id=1, source_target_pairs={{0,1},{1,0},{2,3},{3,2},{4,5},{5,4},{6,7},{7,6},{8,9},{9,8},{10,11... | collective-permute-start | bytes 1572872 | tf_op jit(solution)/shard_map/ppermute | solution.py:94
  347.7 27.1 %collective-permute-start.33 = (bf16[8,32,16,256]{3,2,1,0:T(8,128)(2,1)}, bf16[8,32,16,256]{3,2,1,0:T(8,128)(2,1)}, u32[]{:S(2)}, u32[]{:S(2)}) collective-permute-start(bf16[8,32,16,256]{3,2,1,0:T(8,128)(2,1)} %bitcast.323), channel_id=1, source_target_pairs={{0,4},{1,3},{2,6},{3,1},{4,0},{5,7},{6,2},{7,5},{8,12},{9,11},{10,... | collective-permute-start | bytes 6291464 | tf_op jit(solution)/shard_map/ppermute | solution.py:105
  378.3 20.6 %collective-permute-start.34 = (bf16[4,32,16,256]{3,2,1,0:T(8,128)(2,1)}, bf16[4,32,16,256]{3,2,1,0:T(8,128)(2,1)}, u32[]{:S(2)}, u32[]{:S(2)}) collective-permute-start(bf16[4,32,16,256]{3,2,1,0:T(8,128)(2,1)} %get-tuple-element.347), channel_id=1, source_target_pairs={{0,16},{1,5},{2,18},{3,7},{4,20},{5,1},{6,22},{7,3},{8,24},{9,13},... | collective-permute-start | bytes 3145736 | tf_op jit(solution)/shard_map/ppermute | solution.py:105
  381.6 29.5 %all-to-all-start.3 = ((bf16[2,16,32,512]{3,2,0,1:T(8,128)(2,1)}), bf16[2,16,32,512]{3,2,0,1:T(8,128)(2,1)S(1)}, u32[]{:S(2)}, u32[]{:S(2)}) async-start(bf16[2,16,32,512]{3,2,0,1:T(8,128)(2,1)} %copy.69), calls=%async_computation.3 | async-start | bytes 2097152 | tf_op jit(solution)/shard_map/all_to_all | solution.py:669
  405.5 5.6 collective-permute-start.35
  407.1 14.0 %collective-permute-start.42 = (bf16[512,1024]{1,0:T(8,128)(2,1)}, bf16[512,1024]{1,0:T(8,128)(2,1)}, u32[]{:S(2)}, u32[]{:S(2)}) collective-permute-start(bf16[512,1024]{1,0:T(8,128)(2,1)} %get-tuple-element.189.x_own.o_ref), channel_id=1, source_target_pairs={{0,1},{1,0},{2,3},{3,2},{4,5},{5,4},{6,7},{7,6},{8,9},{9,8},{10,11... | collective-permute-start | bytes 3145736 | tf_op jit(solution)/shard_map/ppermute | solution.py:94
  407.2 47.2 %collective-permute-start.43 = (bf16[8,32,16,256]{3,2,1,0:T(8,128)(2,1)}, bf16[8,32,16,256]{3,2,1,0:T(8,128)(2,1)}, u32[]{:S(2)}, u32[]{:S(2)}) collective-permute-start(bf16[8,32,16,256]{3,2,1,0:T(8,128)(2,1)} %bitcast.61), channel_id=1, source_target_pairs={{0,16},{1,3},{2,18},{3,1},{4,20},{5,7},{6,22},{7,5},{8,24},{9,11},... | collective-permute-start | bytes 6291464 | tf_op jit(solution)/shard_map/ppermute | solution.py:105
  415.4 36.5 %all-to-all-start.4 = ((bf16[32,1,32,512]{3,2,1,0:T(8,128)(2,1)}), bf16[32,1,32,512]{3,2,1,0:T(8,128)(2,1)}, u32[]{:S(2)}, u32[]{:S(2)}) async-start(bf16[32,1,32,512]{3,2,1,0:T(8,128)(2,1)} %bitcast.256), calls=%async_computation.4 | async-start | bytes 2097152 | tf_op jit(solution)/shard_map/all_to_all | solution.py:674
  420.6 9.3 %collective-permute-start.41 = (bf16[512,1024]{1,0:T(8,128)(2,1)S(1)}, bf16[512,1024]{1,0:T(8,128)(2,1)S(1)}, u32[]{:S(2)}, u32[]{:S(2)}) collective-permute-start(bf16[512,1024]{1,0:T(8,128)(2,1)S(1)} %copy-done.26), channel_id=1, source_target_pairs={{0,1},{1,0},{2,3},{3,2},{4,5},{5,4},{6,7},{7,6},{8,9},{9,8},{10,11... | collective-permute-start | bytes 3145736 | tf_op jit(solution)/shard_map/ppermute | solution.py:94
  420.8 26.4 %collective-permute-start.36 = (bf16[512,1024]{1,0:T(8,128)(2,1)}, bf16[512,1024]{1,0:T(8,128)(2,1)}, u32[]{:S(2)}, u32[]{:S(2)}) collective-permute-start(bf16[512,1024]{1,0:T(8,128)(2,1)} %get-tuple-element.201.o_ref.x_own), channel_id=1, source_target_pairs={{0,1},{1,0},{2,3},{3,2},{4,5},{5,4},{6,7},{7,6},{8,9},{9,8},{10,11... | collective-permute-start | bytes 3145736 | tf_op jit(solution)/shard_map/ppermute | solution.py:94
  421.1 26.1 %collective-permute-start.37 = (bf16[512,1024]{1,0:T(8,128)(2,1)S(1)}, bf16[512,1024]{1,0:T(8,128)(2,1)}, u32[]{:S(2)}, u32[]{:S(2)}) collective-permute-start(bf16[512,1024]{1,0:T(8,128)(2,1)S(1)} %copy-done.22), channel_id=1, source_target_pairs={{0,1},{1,0},{2,3},{3,2},{4,5},{5,4},{6,7},{7,6},{8,9},{9,8},{10,11... | collective-permute-start | bytes 3145736 | tf_op jit(solution)/shard_map/ppermute | solution.py:94
  427.8 26.6 %collective-permute-start.44 = (bf16[2,32,16,256]{3,2,1,0:T(8,128)(2,1)}, bf16[2,32,16,256]{3,2,1,0:T(8,128)(2,1)}, u32[]{:S(2)}, u32[]{:S(2)}) collective-permute-start(bf16[2,32,16,256]{3,2,1,0:T(8,128)(2,1)} %get-tuple-element.356), channel_id=1, source_target_pairs={{0,2},{1,17},{2,0},{3,19},{4,6},{5,21},{6,4},{7,23},{8,10},{9,25},... | collective-permute-start | bytes 1572872 | tf_op jit(solution)/shard_map/ppermute | solution.py:105
  430.8 10.3 %collective-permute-start.39 = (bf16[128,1024]{1,0:T(8,128)(2,1)S(1)}, bf16[128,1024]{1,0:T(8,128)(2,1)S(1)}, u32[]{:S(2)}, u32[]{:S(2)}) collective-permute-start(bf16[128,1024]{1,0:T(8,128)(2,1)S(1)} %copy-done.44), channel_id=1, source_target_pairs={{0,1},{1,0},{2,3},{3,2},{4,5},{5,4},{6,7},{7,6},{8,9},{9,8},{10,11... | collective-permute-start | bytes 786440 | tf_op jit(solution)/shard_map/ppermute | solution.py:94
  454.4 32.0 %collective-permute-start.45 = (bf16[8,40,16,256]{3,2,1,0:T(8,128)(2,1)}, bf16[8,40,16,256]{3,2,1,0:T(8,128)(2,1)}, u32[]{:S(2)}, u32[]{:S(2)}) collective-permute-start(bf16[8,40,16,256]{3,2,1,0:T(8,128)(2,1)} %bitcast.241), channel_id=1, source_target_pairs={{0,2},{1,17},{2,0},{3,19},{4,6},{5,21},{6,4},{7,23},{8,10},{9,25},... | collective-permute-start | bytes 7864328 | tf_op jit(solution)/shard_map/ppermute | solution.py:105
  459.2 25.7 %collective-permute-start.46 = (bf16[4,32,16,256]{3,2,1,0:T(8,128)(2,1)}, bf16[4,32,16,256]{3,2,1,0:T(8,128)(2,1)S(1)}, u32[]{:S(2)}, u32[]{:S(2)}) collective-permute-start(bf16[4,32,16,256]{3,2,1,0:T(8,128)(2,1)} %get-tuple-element.345), channel_id=1, source_target_pairs={{0,4},{1,5},{2,6},{3,7},{4,0},{5,1},{6,2},{7,3},{8,12},{9,13},{10,... | collective-permute-start | bytes 3145736 | tf_op jit(solution)/shard_map/ppermute | solution.py:105
  477.0 20.1 %collective-permute-start.47 = (bf16[512,1024]{1,0:T(8,128)(2,1)}, bf16[512,1024]{1,0:T(8,128)(2,1)}, u32[]{:S(2)}, u32[]{:S(2)}) collective-permute-start(bf16[512,1024]{1,0:T(8,128)(2,1)} %get-tuple-element.287.refs_0_), channel_id=1, source_target_pairs={{0,1},{1,0},{2,3},{3,2},{4,5},{5,4},{6,7},{7,6},{8,9},{9,8},{10,11... | collective-permute-start | bytes 3145736 | tf_op jit(solution)/shard_map/ppermute | solution.py:94
  490.5 23.5 %collective-permute-start.50 = (bf16[4,40,16,256]{3,2,1,0:T(8,128)(2,1)}, bf16[4,40,16,256]{3,2,1,0:T(8,128)(2,1)}, u32[]{:S(2)}, u32[]{:S(2)}) collective-permute-start(bf16[4,40,16,256]{3,2,1,0:T(8,128)(2,1)} %get-tuple-element.343), channel_id=1, source_target_pairs={{0,16},{1,3},{2,18},{3,1},{4,20},{5,7},{6,22},{7,5},{8,24},{9,11},... | collective-permute-start | bytes 3932168 | tf_op jit(solution)/shard_map/ppermute | solution.py:105
  492.1 7.5 %collective-permute-start.48 = (bf16[512,1024]{1,0:T(8,128)(2,1)}, bf16[512,1024]{1,0:T(8,128)(2,1)}, u32[]{:S(2)}, u32[]{:S(2)}) collective-permute-start(bf16[512,1024]{1,0:T(8,128)(2,1)} %get-tuple-element.276.refs_1_), channel_id=1, source_target_pairs={{0,1},{1,0},{2,3},{3,2},{4,5},{5,4},{6,7},{7,6},{8,9},{9,8},{10,11... | collective-permute-start | bytes 3145736 | tf_op jit(solution)/shard_map/ppermute | solution.py:94
  492.1 7.5 %collective-permute-start.49 = (bf16[512,1024]{1,0:T(8,128)(2,1)S(1)}, bf16[512,1024]{1,0:T(8,128)(2,1)}, u32[]{:S(2)}, u32[]{:S(2)}) collective-permute-start(bf16[512,1024]{1,0:T(8,128)(2,1)S(1)} %copy-done.8), channel_id=1, source_target_pairs={{0,1},{1,0},{2,3},{3,2},{4,5},{5,4},{6,7},{7,6},{8,9},{9,8},{10,11... | collective-permute-start | bytes 3145736 | tf_op jit(solution)/shard_map/ppermute | solution.py:94
  495.5 16.2 %collective-permute-start.51 = (bf16[2,32,16,256]{3,2,1,0:T(8,128)(2,1)}, bf16[2,32,16,256]{3,2,1,0:T(8,128)(2,1)}, u32[]{:S(2)}, u32[]{:S(2)}) collective-permute-start(bf16[2,32,16,256]{3,2,1,0:T(8,128)(2,1)} %get-tuple-element.354), channel_id=1, source_target_pairs={{0,2},{1,17},{2,0},{3,19},{4,6},{5,21},{6,4},{7,23},{8,10},{9,25},... | collective-permute-start | bytes 1572872 | tf_op jit(solution)/shard_map/ppermute | solution.py:105
  497.1 14.6 %collective-permute-start.52 = (bf16[1,32,16,256]{3,2,1,0:T(8,128)(2,1)S(1)}, bf16[1,32,16,256]{3,2,1,0:T(8,128)(2,1)S(1)}, u32[]{:S(2)}, u32[]{:S(2)}) collective-permute-start(bf16[1,32,16,256]{3,2,1,0:T(8,128)(2,1)S(1)} %add_convert_fusion.27), channel_id=1, source_target_pairs={{0,8},{1,9},{2,10},{3,11},{4,12},{5,13},{6,14},{7,15},{8,0},{9,1},... | collective-permute-start | bytes 786440 | tf_op jit(solution)/shard_map/ppermute | solution.py:105
  517.1 24.3 %collective-permute-start.53 = (bf16[8,24,16,256]{3,2,1,0:T(8,128)(2,1)S(1)}, bf16[8,24,16,256]{3,2,1,0:T(8,128)(2,1)S(1)}, u32[]{:S(2)}, u32[]{:S(2)}) collective-permute-start(bf16[8,24,16,256]{3,2,1,0:T(8,128)(2,1)S(1)} %bitcast.324), channel_id=1, source_target_pairs={{0,2},{1,17},{2,0},{3,19},{4,6},{5,21},{6,4},{7,23},{8,10},{9,25},... | collective-permute-start | bytes 4718600 | tf_op jit(solution)/shard_map/ppermute | solution.py:105
  520.4 21.0 %collective-permute-start.54 = (bf16[2,40,16,256]{3,2,1,0:T(8,128)(2,1)S(1)}, bf16[2,40,16,256]{3,2,1,0:T(8,128)(2,1)S(1)}, u32[]{:S(2)}, u32[]{:S(2)}) collective-permute-start(bf16[2,40,16,256]{3,2,1,0:T(8,128)(2,1)S(1)} %get-tuple-element.351), channel_id=1, source_target_pairs={{0,4},{1,5},{2,6},{3,7},{4,0},{5,1},{6,2},{7,3},{8,12},{9,13},{10,... | collective-permute-start | bytes 1966088 | tf_op jit(solution)/shard_map/ppermute | solution.py:105
  522.9 17.4 %collective-permute-start.55 = (bf16[1,32,16,256]{3,2,1,0:T(8,128)(2,1)S(1)}, bf16[1,32,16,256]{3,2,1,0:T(8,128)(2,1)S(1)}, u32[]{:S(2)}, u32[]{:S(2)}) collective-permute-start(bf16[1,32,16,256]{3,2,1,0:T(8,128)(2,1)S(1)} %add_convert_fusion.26), channel_id=1, source_target_pairs={{0,8},{1,9},{2,10},{3,11},{4,12},{5,13},{6,14},{7,15},{8,0},{9,1},... | collective-permute-start | bytes 786440 | tf_op jit(solution)/shard_map/ppermute | solution.py:105
  541.9 12.1 %collective-permute-start.56 = (bf16[4,24,16,256]{3,2,1,0:T(8,128)(2,1)S(1)}, bf16[4,24,16,256]{3,2,1,0:T(8,128)(2,1)S(1)}, u32[]{:S(2)}, u32[]{:S(2)}) collective-permute-start(bf16[4,24,16,256]{3,2,1,0:T(8,128)(2,1)S(1)} %get-tuple-element.349), channel_id=1, source_target_pairs={{0,16},{1,3},{2,18},{3,1},{4,20},{5,7},{6,22},{7,5},{8,24},{9,11},... | collective-permute-start | bytes 2359304 | tf_op jit(solution)/shard_map/ppermute | solution.py:105
  542.5 7.1 %collective-permute-start.57 = (bf16[512,512]{1,0:T(8,128)(2,1)S(1)}, bf16[512,512]{1,0:T(8,128)(2,1)S(1)}, u32[]{:S(2)}, u32[]{:S(2)}) collective-permute-start(bf16[512,512]{1,0:T(8,128)(2,1)S(1)} %constant_dynamic-slice_fusion), channel_id=1, source_target_pairs={{0,1},{1,0},{2,3},{3,2},{4,5},{5,4},{6,7},{7,6},{8,9},{9,8},{10,11... | collective-permute-start | bytes 1572872 | tf_op jit(solution)/shard_map/ppermute | solution.py:94
  543.8 18.2 %collective-permute-start.60 = (bf16[1,40,16,256]{3,2,1,0:T(8,128)(2,1)S(1)}, bf16[1,40,16,256]{3,2,1,0:T(8,128)(2,1)S(1)}, u32[]{:S(2)}, u32[]{:S(2)}) collective-permute-start(bf16[1,40,16,256]{3,2,1,0:T(8,128)(2,1)S(1)} %add_convert_fusion.21), channel_id=1, source_target_pairs={{0,8},{1,9},{2,10},{3,11},{4,12},{5,13},{6,14},{7,15},{8,0},{9,1},... | collective-permute-start | bytes 983048 | tf_op jit(solution)/shard_map/ppermute | solution.py:105
  554.2 13.8 %collective-permute-start.59 = (bf16[2,24,16,256]{3,2,1,0:T(8,128)(2,1)S(1)}, bf16[2,24,16,256]{3,2,1,0:T(8,128)(2,1)S(1)}, u32[]{:S(2)}, u32[]{:S(2)}) collective-permute-start(bf16[2,24,16,256]{3,2,1,0:T(8,128)(2,1)S(1)} %get-tuple-element.364), channel_id=1, source_target_pairs={{0,4},{1,5},{2,6},{3,7},{4,0},{5,1},{6,2},{7,3},{8,12},{9,13},{10,... | collective-permute-start | bytes 1179656 | tf_op jit(solution)/shard_map/ppermute | solution.py:105
  568.0 10.6 %collective-permute-start.61 = (bf16[1,24,16,256]{3,2,1,0:T(8,128)(2,1)S(1)}, bf16[1,24,16,256]{3,2,1,0:T(8,128)(2,1)S(1)}, u32[]{:S(2)}, u32[]{:S(2)}) collective-permute-start(bf16[1,24,16,256]{3,2,1,0:T(8,128)(2,1)S(1)} %add_convert_fusion.29), channel_id=1, source_target_pairs={{0,8},{1,9},{2,10},{3,11},{4,12},{5,13},{6,14},{7,15},{8,0},{9,1},... | collective-permute-start | bytes 589832 | tf_op jit(solution)/shard_map/ppermute | solution.py:105
  580.2 19.5 %all-to-all-start.5 = ((bf16[64,16,256]{2,1,0:T(8,128)(2,1)}), bf16[64,16,256]{2,1,0:T(8,128)(2,1)S(1)}, u32[]{:S(2)}, u32[]{:S(2)}) async-start(bf16[64,16,256]{2,1,0:T(8,128)(2,1)} %gather_fusion.3), calls=%async_computation.5 | async-start | bytes 1048576 | tf_op jit(solution)/shard_map/all_to_all | solution.py:327
  599.7 19.7 %all-to-all-start.6 = ((bf16[72,16,256]{2,1,0:T(8,128)(2,1)}), bf16[72,16,256]{2,1,0:T(8,128)(2,1)S(1)}, u32[]{:S(2)}, u32[]{:S(2)}) async-start(bf16[72,16,256]{2,1,0:T(8,128)(2,1)} %bitcast.88), calls=%async_computation.6 | async-start | bytes 1179648 | tf_op jit(solution)/shard_map/all_to_all | solution.py:327
  603.4 13.6 %collective-permute-start.63 = (bf16[8,8,16,256]{3,2,1,0:T(8,128)(2,1)S(1)}, bf16[8,8,16,256]{3,2,1,0:T(8,128)(2,1)S(1)}, u32[]{:S(2)}, u32[]{:S(2)}) collective-permute-start(bf16[8,8,16,256]{3,2,1,0:T(8,128)(2,1)S(1)} %bitcast.282), channel_id=1, source_target_pairs={{0,16},{16,0},{1,17},{17,1},{2,18},{18,2},{3,19},{19,3},{4,20},{20... | collective-permute-start | bytes 1572872 | tf_op jit(solution)/shard_map/ppermute | solution.py:97
  619.4 13.8 %collective-permute-start.64 = (bf16[8,9,16,256]{3,2,1,0:T(8,128)(2,1)S(1)}, bf16[8,9,16,256]{3,2,1,0:T(8,128)(2,1)S(1)}, u32[]{:S(2)}, u32[]{:S(2)}) collective-permute-start(bf16[8,9,16,256]{3,2,1,0:T(8,128)(2,1)S(1)} %bitcast.273), channel_id=1, source_target_pairs={{0,16},{16,0},{1,17},{17,1},{2,18},{18,2},{3,19},{19,3},{4,20},{20... | collective-permute-start | bytes 1769480 | tf_op jit(solution)/shard_map/ppermute | solution.py:97
  (96 other events, 806.7 us)

commit v7 on v6

--- a/solution.py
+++ b/solution.py
@@ -779,7 +779,6 @@
     act, slope = step((act, slope), down)
     (w_fo,) = placed(3)
     z_three = h_two + dot_nn(act, w_fo) + b_fo
-    cot_home, z_three = step((cot_home, z_three))
     cot, _ = whole(cot_home)
     h_three, n_three, r_three = norm_forward(z_three, g_three, b_three)
     live = (jnp.arange(x.shape[0]) < limit).astype(f32)[:, None]
@@ -798,8 +797,9 @@
     d_three, dg_three, db_three = norm_backward(grad_y, n_three, r_three, g_three)
     a_three = d_three.astype(bf16)
     d_hidden = (dot_nt(a_three, w_fo) * slope.astype(f32)).astype(bf16)
+    a_three_sib, d_hidden = step((net.swap_core(a_three), d_hidden))
     d_hidden_sib = net.swap_core(d_hidden)
-    down = gradient(3, ((act, act_sib), (a_three, net.swap_core(a_three))))
+    down = gradient(3, ((act, act_sib), (a_three, a_three_sib)))
     finished, d_hidden, d_hidden_sib = step((finished, d_hidden, d_hidden_sib), down)
     finished = halved(finished)
     d_h_two = d_three + dot_nt(d_hidden, w_fi)
@@ -830,9 +830,10 @@
     outputs, d_os = step((outputs, d_os), cross, up, down)
     dq_s, dk_s, dv_s = attend_backward(limit, q_s, k_s, v_s, o_s, d_os, lse_s, True)
     sibs = [net.swap_core(v) for v in (dq_s, dk_s, dv_s)]
+    dq_s, dk_s, dv_s = step((dq_s, dk_s, dv_s), cross)
+    attn = gradient(0, ((x, x_sib), *zip((dq_s, dk_s, dv_s), sibs)))
+    dk_c, dv_c, dq_s, dk_s, dv_s = step((dk_c, dv_c, dq_s, dk_s, dv_s), attn)
     dq_s, dk_s, dv_s = step((dq_s, dk_s, dv_s), cross, up)
-    attn = gradient(0, ((x, x_sib), *zip((dq_s, dk_s, dv_s), sibs)))
-    dk_c, dv_c, dq_s, dk_s, dv_s = step((dk_c, dv_c, dq_s, dk_s, dv_s), attn, cross, up, down)
     state_back = dot_nt(dk_c, w_ck) + dot_nt(dv_c, w_cv)
     back = d_one + dot_nt(dq_s, w_sq) + dot_nt(dk_s, w_sk) + dot_nt(dv_s, w_sv)
     back, d_hidden, dq_c, dv_c = step((back, d_hidden, dq_c, dv_c), attn, cross, up)

time: 657 us -> 634 us (0.965)
  waiting for transfers between devices: 194 us -> 180 us
    all_to_all x2, waiting for transfers between devices: 25.5 us -> 7.31 us  [route_home(): lax.all_to_all(moved, ('rep', 'shard'), split_axis=0, concat_axis=1, tile...]
    ppermute x32, waiting for transfers between devices: 98.3 us -> 108 us  [swap_data(): return lax.ppermute(value, ('rep', 'shard', 'mp'), pairs)]
    ppermute x32, starting transfers between devices: 46.4 us -> 38.5 us  [swap_data(): return lax.ppermute(value, ('rep', 'shard', 'mp'), pairs)]
    ppermute x31, waiting for transfers between devices: 13 us -> 5.79 us  [swap_core(): return lax.ppermute(value, 'mp', [(i, i ^ 1) for i in range(self.n_mp)])]
    unnamed x209 -> x195, local copies, waits for them, and re-layouts: 16.7 us -> 11.7 us
  transfers between devices with their start and end apart: 72 -> 72, of which waited for: 33 -> 30; matrix products, arithmetic and copies ran while one was open for 21% -> 23% of each run, Pallas kernels for 25% -> 28%
where the time goes in v7:
time: 634 us; the launch traced here: 623 us
  Pallas kernels  184 us (29%)
  waiting for transfers between devices  180 us (28%)
  starting transfers between devices  85.3 us (13%)
  other arithmetic  73.3 us (12%)
  matrix products  63.7 us (10%)
  local copies, waits for them, and re-layouts  34.3 us (5%)
    ppermute x32, waiting for transfers between devices, swap_data(): return lax.ppermute(value, ('rep', 'shard', 'mp'), pairs)  108 us
    pallas_call x7, Pallas kernels, weight_grad(): pl.pallas_call(functools.partial(weight_grad_body, count=count, outs=outs...  49.5 us
    ppermute x32, starting transfers between devices, swap_data(): return lax.ppermute(value, ('rep', 'shard', 'mp'), pairs)  38.5 us
    pallas_call x4, Pallas kernels, place(): pl.pallas_call(functools.partial(place_body, dests=dests, many=many, two=...  37.9 us
    dot_general x10, matrix products, dot_nt(): return lax.dot_general(a, b, NT, preferred_element_type=f32)  35.5 us
    pallas_call x2, Pallas kernels, attend_forward(): pl.pallas_call(functools.partial(attend_forward_body, causal=causal, rows...  29 us
    dot_general x9, matrix products, dot_nn(): return jnp.dot(a, b, preferred_element_type=f32)  28.2 us
    all_to_all x1, waiting for transfers between devices, first_pieces(): lax.all_to_all(cut.reshape(-1, net.rows, BS), 'shard', split_axis=0, conc...  27 us
  transfers between devices with their start and end apart: 72, of which 30 were waited for; matrix products, arithmetic and copies ran while one was open for 23% of the time, Pallas kernels for 28%

profile of v7, /device:TPU:0, one launch (start us, length us, event | category | flops | bytes accessed | tf_op | source)
XLA Modules:
  0.0 623.3 jit_solution(11685000961121420516)
XLA Ops:
  0.6 2.4 convert_element_type.363
  5.0 7.3 %all-to-all-start = ((bf16[136,16,256]{2,1,0:T(8,128)(2,1)}), bf16[136,16,256]{2,1,0:T(8,128)(2,1)S(1)}, u32[]{:S(2)}, u32[]{:S(2)}) async-start(bf16[136,16,256]{2,1,0:T(8,128)(2,1)} %bitcast.4), calls=%async_computation | async-start | bytes 2228224 | tf_op jit(solution)/shard_map/all_to_all | solution.py:271
  12.4 27.0 %all-to-all-done = bf16[136,16,256]{2,1,0:T(8,128)(2,1)S(1)} async-done(((bf16[136,16,256]{2,1,0:T(8,128)(2,1)}), bf16[136,16,256]{2,1,0:T(8,128)(2,1)S(1)}, u32[]{:S(2)}, u32[]{:S(2)}) %all-to-all-start) | async-done | bytes 1114144 | tf_op jit(solution)/shard_map/all_to_all | solution.py:271
  40.2 10.6 %collective-permute-done.2 = bf16[1,24,16,256]{3,2,1,0:T(8,128)(2,1)S(1)} collective-permute-done((bf16[1,24,16,256]{3,2,1,0:T(8,128)(2,1)S(1)}, bf16[1,24,16,256]{3,2,1,0:T(8,128)(2,1)S(1)}, u32[]{:S(2)}, u32[]{:S(2)}) %collective-permute-start.2) | collective-permute-done | bytes 196640 | tf_op jit(solution)/shard_map/ppermute | solution.py:105
  52.5 6.3 %collective-permute-done.3 = bf16[2,24,16,256]{3,2,1,0:T(8,128)(2,1)S(1)} collective-permute-done((bf16[2,24,16,256]{3,2,1,0:T(8,128)(2,1)S(1)}, bf16[2,24,16,256]{3,2,1,0:T(8,128)(2,1)S(1)}, u32[]{:S(2)}, u32[]{:S(2)}) %collective-permute-start.3) | collective-permute-done | bytes 393248 | tf_op jit(solution)/shard_map/ppermute | solution.py:105
  62.0 14.0 %collective-permute-done.5 = bf16[1,40,16,256]{3,2,1,0:T(8,128)(2,1)S(1)} collective-permute-done((bf16[1,40,16,256]{3,2,1,0:T(8,128)(2,1)S(1)}, bf16[1,40,16,256]{3,2,1,0:T(8,128)(2,1)S(1)}, u32[]{:S(2)}, u32[]{:S(2)}) %collective-permute-start.5) | collective-permute-done | bytes 327712 | tf_op jit(solution)/shard_map/ppermute | solution.py:105
  93.0 9.8 %collective-permute-done.8 = bf16[2,40,16,256]{3,2,1,0:T(8,128)(2,1)} collective-permute-done((bf16[2,40,16,256]{3,2,1,0:T(8,128)(2,1)}, bf16[2,40,16,256]{3,2,1,0:T(8,128)(2,1)}, u32[]{:S(2)}, u32[]{:S(2)}) %collective-permute-start.8) | collective-permute-done | bytes 655392 | tf_op jit(solution)/shard_map/ppermute | solution.py:105
  103.5 2.4 pad_maximum_fusion.4
  108.7 8.5 %place.4 = (bf16[4,256,1024]{2,1,0:T(8,128)(2,1)}, bf16[4,256,1024]{2,1,0:T(8,128)(2,1)}, bf16[4,256,1024]{2,1,0:T(8,128)(2,1)}) custom-call(s32[41]{0:T(128)} %add_add_fusion.4.s, bf16[8,24,16,256]{3,2,1,0:T(8,128)(2,1)} %copy-done.13, bf16[8,24,16,256]{3,2,1,0:T(8,128)(2,1)} %collective-permute-done.6.refs_1_, ...), custom_call_target="tpu_custom_call" | custom-call | flops 1048576 | bytes 1048576 | tf_op jit(solution)/shard_map/place/pallas_call | solution.py:227
  118.7 4.0 add_convert_fusion.7.v_ref
  136.7 20.1 %attend_forward.2 = (bf16[512,1024]{1,0:T(8,128)(2,1)}, f32[512,128]{1,0:T(8,128)}) custom-call(s32[1]{0:T(128)} %dynamic_slice.88.lim, bf16[512,1024]{1,0:T(8,128)(2,1)} %add_convert_fusion.8.q_ref, bf16[512,1024]{1,0:T(8,128)(2,1)} %convolution_convert_fusion.2.k_ref, bf16[512,1024]{1,0:T(8,128)(2,1)} %add_convert_fusion.7.v_ref), custom_call_target="tpu_custom_call" | custom-call | flops 1048576 | bytes 1048576 | tf_op jit(solution)/shard_map/attend_forward/pallas_call | solution.py:382
  160.1 3.4 collective-permute-done.17
  165.5 3.0 pad_maximum_fusion.1.refs_0_
  173.7 5.4 all-to-all-start.1
  179.1 10.3 %place.5 = (bf16[4,256,1024]{2,1,0:T(8,128)(2,1)}, bf16[4,256,1024]{2,1,0:T(8,128)(2,1)}, bf16[4,256,1024]{2,1,0:T(8,128)(2,1)}, bf16[4,256,1024]{2,1,0:T(8,128)(2,1)}, bf16[4,256,1024]{2,1,0:T(8,128)(2,1)}) custom-call(s32[41]{0:T(128)} %add_add_fusion.5.s, bf16[8,40,16,256]{3,2,1,0:T(8,128)(2,1)} %copy-done.4, ...), custom_call_target="tpu_custom_call" | custom-call | flops 1048576 | bytes 1048576 | tf_op jit(solution)/shard_map/place/pallas_call | solution.py:227
  189.4 3.5 fusion.23
  204.9 9.0 %attend_forward.3 = (bf16[512,1024]{1,0:T(8,128)(2,1)}, f32[512,128]{1,0:T(8,128)}) custom-call(s32[1]{0:T(128)} %dynamic_slice.88.lim, bf16[512,1024]{1,0:T(8,128)(2,1)} %add_convert_fusion.6.q_ref, bf16[128,1024]{1,0:T(8,128)(2,1)} %convolution_convert_fusion.3.k_ref, bf16[128,1024]{1,0:T(8,128)(2,1)} %fusion.4.v_ref), custom_call_target="tpu_custom_call" | custom-call | flops 1048576 | bytes 1048576 | tf_op jit(solution)/shard_map/attend_forward/pallas_call | solution.py:382
  213.9 3.4 fusion.26
  222.9 3.0 pad_maximum_fusion.2.refs_0_
  225.9 2.3 collective-permute-start.24
  229.9 4.7 all-to-all-start.2
  236.0 9.6 %place.6 = bf16[4,256,4096]{2,1,0:T(8,128)(2,1)} custom-call(s32[41]{0:T(128)} %add_add_fusion.6.s, bf16[8,32,16,256]{3,2,1,0:T(8,128)(2,1)} %pad_maximum_fusion.1.refs_0_, bf16[8,32,16,256]{3,2,1,0:T(8,128)(2,1)} %collective-permute-done.20.refs_1_, bf16[8,32,16,256]{3,2,1,0:T(8,128)(2,1)} %collective-permute-done.21.refs_2_, ...), custom_call_target="tpu_custom_call" | custom-call | flops 1048576 | bytes 1048576 | tf_op jit(solution)/shard_map/place/pallas_call | solution.py:227
  245.6 19.1 %gelu_forward.1 = (bf16[512,4096]{1,0:T(8,128)(2,1)}, bf16[512,4096]{1,0:T(8,128)(2,1)}) custom-call(bf16[512,1024]{1,0:T(8,128)(2,1)} %get-tuple-element.207.h_ref.x_own, bf16[1024,4096]{1,0:T(8,128)(2,1)} %bitcast.239, f32[1,4096]{1,0:T(1,128)} %bitcast.292), custom_call_target="tpu_custom_call" | custom-call | flops 1048576 | bytes 1048576 | tf_op jit(solution)/shard_map/gelu_forward/pallas_call | solution.py:515
  265.0 6.3 %all-to-all-done.2 = bf16[32,1,32,512]{3,2,1,0:T(8,128)(2,1)S(1)} async-done(((bf16[32,1,32,512]{3,2,1,0:T(8,128)(2,1)}), bf16[32,1,32,512]{3,2,1,0:T(8,128)(2,1)S(1)}, u32[]{:S(2)}, u32[]{:S(2)}) %all-to-all-start.2) | async-done | bytes 1048608 | tf_op jit(solution)/shard_map/all_to_all | solution.py:674
  274.2 9.5 %place.7 = bf16[16,256,1024]{2,1,0:T(8,128)(2,1)} custom-call(s32[41]{0:T(128)} %add_add_fusion.7.s, bf16[8,32,16,256]{3,2,1,0:T(8,128)(2,1)} %pad_maximum_fusion.2.refs_0_, bf16[8,32,16,256]{3,2,1,0:T(8,128)(2,1)} %collective-permute-done.24.refs_1_, bf16[8,32,16,256]{3,2,1,0:T(8,128)(2,1)} %collective-permute-done.25.refs_2_, ...), custom_call_target="tpu_custom_call" | custom-call | flops 1048576 | bytes 1048576 | tf_op jit(solution)/shard_map/place/pallas_call | solution.py:227
  283.8 8.3 %fusion.27 = f32[512,1024]{1,0:T(8,128)S(1)} fusion(bf16[512,4096]{1,0:T(8,128)(2,1)} %get-tuple-element.213.x_own, bf16[4096,1024]{1,0:T(8,128)(2,1)} %bitcast.242), kind=kOutput, calls=%fused_computation.236 | convolution fusion | flops 4294967296 | bytes 14680064 | tf_op jit(solution)/shard_map/dot_general | solution.py:43
  297.4 8.1 %multiply_convert_fusion.refs_0_ = bf16[512,4096]{1,0:T(8,128)(2,1)} fusion(bf16[512,4096]{1,0:T(8,128)(2,1)} %get-tuple-element.217, bf16[512,1024]{1,0:T(8,128)(2,1)S(1)} %convert_element_type.379.refs_0_, bf16[4096,1024]{1,0:T(8,128)(2,1)S(1)} %bitcast.245), kind=kOutput, calls=%fused_computation.6 | convolution fusion | flops 4301258752 | bytes 17825792 | tf_op jit(solution)/shard_map/dot_general | solution.py:47
  306.0 11.1 %weight_grad.7 = (bf16[8,1,32,16,256]{4,3,2,1,0:T(8,128)(2,1)}, bf16[8,1,32,16,256]{4,3,2,1,0:T(8,128)(2,1)}) custom-call(s32[41]{0:T(128)} %add_add_fusion.7.s, bf16[512,4096]{1,0:T(8,128)(2,1)} %get-tuple-element.213.x_own, bf16[512,4096]{1,0:T(8,128)(2,1)} %collective-permute-done.30.x_sib, bf16[512,1024]{1,0:T(8,128)(2,1)} %copy-done.26, ...), custom_call_target="tpu_custom_call" | custom-call | flops 1048576 | bytes 1048576 | tf_op jit(solution)/shard_map/weight_grad/pallas_call | solution.py:572
  317.3 11.0 %multiply_reduce_fusion.1 = (f32[1024]{0:T(1024)S(1)}, f32[512]{0:T(512)S(1)}, f32[512]{0:T(512)S(1)}, f32[1024]{0:T(1024)S(1)}, f32[512,1024]{1,0:T(8,128)S(1)}) fusion(f32[512,1024]{1,0:T(8,128)} %copy-done.2, f32[512]{0:T(512)S(1)} %add_rsqrt_fusion.1, f32[512]{0:T(512)S(1)} %broadcast_multiply_fusion.7, f32[1024]{0:T(1024)S(1)} %bitcast.300, ...), kind=kOutput, calls=%fused_computation.13 | convolution fusion | flops 4300207104 | bytes 18894848 | tf_op jit(solution)/shard_map/dot_general | solution.py:47
  336.7 9.6 %weight_grad.8 = (bf16[8,1,32,16,256]{4,3,2,1,0:T(8,128)(2,1)}, bf16[8,1,32,16,256]{4,3,2,1,0:T(8,128)(2,1)}) custom-call(s32[41]{0:T(128)} %add_add_fusion.6.s, bf16[512,1024]{1,0:T(8,128)(2,1)} %get-tuple-element.207.h_ref.x_own, bf16[512,1024]{1,0:T(8,128)(2,1)} %collective-permute-done.32.x_sib, bf16[512,4096]{1,0:T(8,128)(2,1)} %multiply_convert_fusion.refs_0_, ...), custom_call_target="tpu_custom_call" | custom-call | flops 1048576 | bytes 1048576 | tf_op jit(solution)/shard_map/weight_grad/pallas_call | solution.py:572
  346.3 4.3 add_convert_fusion.4
  352.9 5.0 all-to-all-start.3
  357.9 10.3 %attend_backward.2 = (bf16[512,1024]{1,0:T(8,128)(2,1)}, bf16[128,1024]{1,0:T(8,128)(2,1)}, bf16[128,1024]{1,0:T(8,128)(2,1)}) custom-call(s32[1]{0:T(128)} %dynamic_slice.88.lim, bf16[512,1024]{1,0:T(8,128)(2,1)} %add_convert_fusion.6.q_ref, bf16[128,1024]{1,0:T(8,128)(2,1)} %convolution_convert_fusion.3.k_ref, bf16[128,1024]{1,0:T(8,128)(2,1)} %fusion.4.v_ref, ...), custom_call_target="tpu_custom_call" | custom-call | flops 1048576 | bytes 1048576 | tf_op jit(solution)/shard_map/attend_backward/pallas_call | solution.py:465
  370.4 4.4 multiply_reduce_fusion.2
  377.2 3.0 collective-permute-start.35
  384.2 2.9 gather_fusion.2
  387.1 4.6 all-to-all-start.4
  394.9 2.8 add_convert_fusion.13
  401.5 4.8 weight_grad.9
  406.3 5.5 weight_grad.10
  412.5 5.3 weight_grad.11
  417.9 4.8 weight_grad.12
  427.2 16.2 %attend_backward.3 = (bf16[512,1024]{1,0:T(8,128)(2,1)}, bf16[512,1024]{1,0:T(8,128)(2,1)}, bf16[512,1024]{1,0:T(8,128)(2,1)}) custom-call(s32[1]{0:T(128)} %dynamic_slice.88.lim, bf16[512,1024]{1,0:T(8,128)(2,1)} %add_convert_fusion.8.q_ref, bf16[512,1024]{1,0:T(8,128)(2,1)} %convolution_convert_fusion.2.k_ref, bf16[512,1024]{1,0:T(8,128)(2,1)} %add_convert_fusion.7.v_ref, ...), custom_call_target="tpu_custom_call" | custom-call | flops 1048576 | bytes 1048576 | tf_op jit(solution)/shard_map/attend_backward/pallas_call | solution.py:465
  444.2 4.3 add_convert_fusion.2
  451.4 6.5 %collective-permute-done.45 = bf16[8,40,16,256]{3,2,1,0:T(8,128)(2,1)} collective-permute-done((bf16[8,40,16,256]{3,2,1,0:T(8,128)(2,1)}, bf16[8,40,16,256]{3,2,1,0:T(8,128)(2,1)}, u32[]{:S(2)}, u32[]{:S(2)}) %collective-permute-start.45) | collective-permute-done | bytes 2621472 | tf_op jit(solution)/shard_map/ppermute | solution.py:105
  459.3 3.7 add_convert_fusion
  464.4 8.4 %weight_grad.13 = (bf16[8,3,8,16,256]{4,3,2,1,0:T(8,128)(2,1)}, bf16[8,3,8,16,256]{4,3,2,1,0:T(8,128)(2,1)}) custom-call(s32[41]{0:T(128)} %add_add_fusion.5.s, bf16[512,1024]{1,0:T(8,128)(2,1)} %get-tuple-element.168.x_own, bf16[512,1024]{1,0:T(8,128)(2,1)} %get-tuple-element.267.x_sib, bf16[512,1024]{1,0:T(8,128)(2,1)} %get-tuple-element.289.refs_0_, ...), custom_call_target="tpu_custom_call" | custom-call | flops 1048576 | bytes 1048576 | tf_op jit(solution)/shard_map/weight_grad/pallas_call | solution.py:572
  472.9 2.6 fusion.30
  486.3 3.5 collective-permute-start.52
  494.3 6.2 %collective-permute-done.51 = bf16[8,24,16,256]{3,2,1,0:T(8,128)(2,1)S(1)} collective-permute-done((bf16[8,24,16,256]{3,2,1,0:T(8,128)(2,1)S(1)}, bf16[8,24,16,256]{3,2,1,0:T(8,128)(2,1)S(1)}, u32[]{:S(2)}, u32[]{:S(2)}) %collective-permute-start.51) | collective-permute-done | bytes 1572896 | tf_op jit(solution)/shard_map/ppermute | solution.py:105
  500.6 5.6 collective-permute-done.53
  506.3 3.4 collective-permute-start.58
  511.6 3.2 convert_reduce_fusion
  514.8 19.5 %collective-permute-done.60 = bf16[1,32,16,256]{3,2,1,0:T(8,128)(2,1)S(1)} collective-permute-done((bf16[1,32,16,256]{3,2,1,0:T(8,128)(2,1)S(1)}, bf16[1,32,16,256]{3,2,1,0:T(8,128)(2,1)S(1)}, u32[]{:S(2)}, u32[]{:S(2)}) %collective-permute-start.60) | collective-permute-done | bytes 262176 | tf_op jit(solution)/shard_map/ppermute | solution.py:105
  536.4 7.5 %collective-permute-done.57 = bf16[2,24,16,256]{3,2,1,0:T(8,128)(2,1)S(1)} collective-permute-done((bf16[2,24,16,256]{3,2,1,0:T(8,128)(2,1)S(1)}, bf16[2,24,16,256]{3,2,1,0:T(8,128)(2,1)S(1)}, u32[]{:S(2)}, u32[]{:S(2)}) %collective-permute-start.57) | collective-permute-done | bytes 393248 | tf_op jit(solution)/shard_map/ppermute | solution.py:105
  546.5 7.3 %collective-permute-done.59 = bf16[1,24,16,256]{3,2,1,0:T(8,128)(2,1)S(1)} collective-permute-done((bf16[1,24,16,256]{3,2,1,0:T(8,128)(2,1)S(1)}, bf16[1,24,16,256]{3,2,1,0:T(8,128)(2,1)S(1)}, u32[]{:S(2)}, u32[]{:S(2)}) %collective-permute-start.59) | collective-permute-done | bytes 196640 | tf_op jit(solution)/shard_map/ppermute | solution.py:105
  555.5 7.1 %all-to-all-start.5 = ((bf16[64,16,256]{2,1,0:T(8,128)(2,1)}), bf16[64,16,256]{2,1,0:T(8,128)(2,1)S(1)}, u32[]{:S(2)}, u32[]{:S(2)}) async-start(bf16[64,16,256]{2,1,0:T(8,128)(2,1)} %gather_fusion.3), calls=%async_computation.5 | async-start | bytes 1048576 | tf_op jit(solution)/shard_map/all_to_all | solution.py:327
  565.7 11.6 %all-to-all-done.5 = bf16[64,16,256]{2,1,0:T(8,128)(2,1)S(1)} async-done(((bf16[64,16,256]{2,1,0:T(8,128)(2,1)}), bf16[64,16,256]{2,1,0:T(8,128)(2,1)S(1)}, u32[]{:S(2)}, u32[]{:S(2)}) %all-to-all-start.5) | async-done | bytes 524320 | tf_op jit(solution)/shard_map/all_to_all | solution.py:327
  577.3 3.6 all-to-all-start.6
  580.9 13.5 %collective-permute-done.63.other_ref = bf16[8,8,16,256]{3,2,1,0:T(8,128)(2,1)S(1)} collective-permute-done((bf16[8,8,16,256]{3,2,1,0:T(8,128)(2,1)S(1)}, bf16[8,8,16,256]{3,2,1,0:T(8,128)(2,1)S(1)}, u32[]{:S(2)}, u32[]{:S(2)}) %collective-permute-start.63) | collective-permute-done | bytes 524320 | tf_op jit(solution)/shard_map/ppermute | solution.py:97
  594.5 2.5 all-to-all-done.6
  597.1 11.1 %shampoo.2 = (f32[1,16,256,256]{3,2,1,0:T(8,128)}, f32[1,16,256,256]{3,2,1,0:T(8,128)}, f32[1,16,256,256]{3,2,1,0:T(8,128)}, f32[1,16,256,256]{3,2,1,0:T(8,128)}) custom-call(s32[1]{0:T(128)} %bitcast.79.flag, bf16[8,8,16,256]{3,2,1,0:T(8,128)(2,1)} %bitcast.283, bf16[8,8,16,256]{3,2,1,0:T(8,128)(2,1)} %copy-done.57, f32[1,16,256,256]{3,2,1,0:T(8,128)} %w_ref.3, ...), custom_call_target="tpu_custom_call" | custom-call | flops 1048576 | bytes 1048576 | tf_op jit(solution)/shard_map/shampoo/pallas_call | solution.py:627
  608.2 2.6 collective-permute-done.64.other_ref
  612.2 10.9 %shampoo.3 = (f32[1,16,256,256]{3,2,1,0:T(8,128)}, f32[1,16,256,256]{3,2,1,0:T(8,128)}, f32[1,16,256,256]{3,2,1,0:T(8,128)}, f32[1,16,256,256]{3,2,1,0:T(8,128)}) custom-call(s32[1]{0:T(128)} %bitcast.79.flag, bf16[8,9,16,256]{3,2,1,0:T(8,128)(2,1)} %bitcast.275, ...), custom_call_target="tpu_custom_call", output_to_operand_aliasing={{0}: (8, {}), {1}: (9, {}), {2}: (10, {}), {3}: (11, {})} | custom-call | flops 1048576 | bytes 1048576 | tf_op jit(solution)/shard_map/shampoo/pallas_call | solution.py:627
  (472 shorter events, 149.4 us)
Async XLA Ops:
  5.0 34.5 %all-to-all-start = ((bf16[136,16,256]{2,1,0:T(8,128)(2,1)}), bf16[136,16,256]{2,1,0:T(8,128)(2,1)S(1)}, u32[]{:S(2)}, u32[]{:S(2)}) async-start(bf16[136,16,256]{2,1,0:T(8,128)(2,1)} %bitcast.4), calls=%async_computation | async-start | bytes 2228224 | tf_op jit(solution)/shard_map/all_to_all | solution.py:271
  40.1 10.7 %collective-permute-start.2 = (bf16[1,24,16,256]{3,2,1,0:T(8,128)(2,1)S(1)}, bf16[1,24,16,256]{3,2,1,0:T(8,128)(2,1)S(1)}, u32[]{:S(2)}, u32[]{:S(2)}) collective-permute-start(bf16[1,24,16,256]{3,2,1,0:T(8,128)(2,1)S(1)} %bitcast.269), channel_id=1, source_target_pairs={{0,8},{1,9},{2,10},{3,11},{4,12},{5,13},{6,14},{7,15},{8,0},{9,1},... | collective-permute-start | bytes 589832 | tf_op jit(solution)/shard_map/ppermute | solution.py:105
  50.9 7.8 %collective-permute-start.3 = (bf16[2,24,16,256]{3,2,1,0:T(8,128)(2,1)S(1)}, bf16[2,24,16,256]{3,2,1,0:T(8,128)(2,1)S(1)}, u32[]{:S(2)}, u32[]{:S(2)}) collective-permute-start(bf16[2,24,16,256]{3,2,1,0:T(8,128)(2,1)S(1)} %pad_maximum_fusion.19), channel_id=1, source_target_pairs={{0,16},{1,5},{2,18},{3,7},{4,20},{5,1},{6,22},{7,3},{8,24},{9,13},... | collective-permute-start | bytes 1179656 | tf_op jit(solution)/shard_map/ppermute | solution.py:105
  59.7 19.3 %collective-permute-start.4 = (bf16[4,24,16,256]{3,2,1,0:T(8,128)(2,1)}, bf16[4,24,16,256]{3,2,1,0:T(8,128)(2,1)}, u32[]{:S(2)}, u32[]{:S(2)}) collective-permute-start(bf16[4,24,16,256]{3,2,1,0:T(8,128)(2,1)} %pad_maximum_fusion.14), channel_id=1, source_target_pairs={{0,4},{1,3},{2,6},{3,1},{4,0},{5,7},{6,2},{7,5},{8,12},{9,11},{10,... | collective-permute-start | bytes 2359304 | tf_op jit(solution)/shard_map/ppermute | solution.py:105
  59.7 16.3 %collective-permute-start.5 = (bf16[1,40,16,256]{3,2,1,0:T(8,128)(2,1)S(1)}, bf16[1,40,16,256]{3,2,1,0:T(8,128)(2,1)S(1)}, u32[]{:S(2)}, u32[]{:S(2)}) collective-permute-start(bf16[1,40,16,256]{3,2,1,0:T(8,128)(2,1)S(1)} %bitcast.250), channel_id=1, source_target_pairs={{0,8},{1,9},{2,10},{3,11},{4,12},{5,13},{6,14},{7,15},{8,0},{9,1},... | collective-permute-start | bytes 983048 | tf_op jit(solution)/shard_map/ppermute | solution.py:105
  61.5 23.8 %collective-permute-start = (bf16[2,512,512]{2,1,0:T(8,128)(2,1)}, bf16[2,512,512]{2,1,0:T(8,128)(2,1)}, u32[]{:S(2)}, u32[]{:S(2)}) collective-permute-start(bf16[2,512,512]{2,1,0:T(8,128)(2,1)} %param.21), channel_id=1, source_target_pairs={{0,1},{1,0},{2,3},{3,2},{4,5},{5,4},{6,7},{7,6},{8,9},{9,8},{10,11... | collective-permute-start | bytes 3145736 | tf_op jit(solution)/shard_map/ppermute | solution.py:94
  61.5 21.0 %collective-permute-start.1 = (bf16[2,128,512]{2,1,0:T(8,128)(2,1)}, bf16[2,128,512]{2,1,0:T(8,128)(2,1)}, u32[]{:S(2)}, u32[]{:S(2)}) collective-permute-start(bf16[2,128,512]{2,1,0:T(8,128)(2,1)} %param.22), channel_id=1, source_target_pairs={{0,1},{1,0},{2,3},{3,2},{4,5},{5,4},{6,7},{7,6},{8,9},{9,8},{10,11... | collective-permute-start | bytes 786440 | tf_op jit(solution)/shard_map/ppermute | solution.py:94
  80.5 22.3 %collective-permute-start.6 = (bf16[8,24,16,256]{3,2,1,0:T(8,128)(2,1)S(1)}, bf16[8,24,16,256]{3,2,1,0:T(8,128)(2,1)}, u32[]{:S(2)}, u32[]{:S(2)}) collective-permute-start(bf16[8,24,16,256]{3,2,1,0:T(8,128)(2,1)S(1)} %pad_maximum_fusion.3.refs_0_), channel_id=1, source_target_pairs={{0,2},{1,17},{2,0},{3,19},{4,6},{5,21},{6,4},{7,23},{8,10},{9,25},... | collective-permute-start | bytes 4718600 | tf_op jit(solution)/shard_map/ppermute | solution.py:105
  81.8 21.0 %collective-permute-start.7 = (bf16[8,24,16,256]{3,2,1,0:T(8,128)(2,1)S(1)}, bf16[8,24,16,256]{3,2,1,0:T(8,128)(2,1)}, u32[]{:S(2)}, u32[]{:S(2)}) collective-permute-start(bf16[8,24,16,256]{3,2,1,0:T(8,128)(2,1)S(1)} %pad_maximum_fusion.3.refs_0_), channel_id=1, source_target_pairs={{0,1},{1,0},{2,3},{3,2},{4,5},{5,4},{6,7},{7,6},{8,9},{9,8},{10,11... | collective-permute-start | bytes 4718600 | tf_op jit(solution)/shard_map/ppermute | solution.py:94
  85.3 17.5 %collective-permute-start.8 = (bf16[2,40,16,256]{3,2,1,0:T(8,128)(2,1)}, bf16[2,40,16,256]{3,2,1,0:T(8,128)(2,1)}, u32[]{:S(2)}, u32[]{:S(2)}) collective-permute-start(bf16[2,40,16,256]{3,2,1,0:T(8,128)(2,1)} %pad_maximum_fusion.15), channel_id=1, source_target_pairs={{0,4},{1,5},{2,6},{3,7},{4,0},{5,1},{6,2},{7,3},{8,12},{9,13},{10,... | collective-permute-start | bytes 1966088 | tf_op jit(solution)/shard_map/ppermute | solution.py:105
  102.8 15.0 %collective-permute-start.10 = (bf16[1,32,16,256]{3,2,1,0:T(8,128)(2,1)S(1)}, bf16[1,32,16,256]{3,2,1,0:T(8,128)(2,1)S(1)}, u32[]{:S(2)}, u32[]{:S(2)}) collective-permute-start(bf16[1,32,16,256]{3,2,1,0:T(8,128)(2,1)S(1)} %bitcast.265), channel_id=1, source_target_pairs={{0,8},{1,9},{2,10},{3,11},{4,12},{5,13},{6,14},{7,15},{8,0},{9,1},... | collective-permute-start | bytes 786440 | tf_op jit(solution)/shard_map/ppermute | solution.py:105
  105.8 21.4 %collective-permute-start.12 = (bf16[4,40,16,256]{3,2,1,0:T(8,128)(2,1)}, bf16[4,40,16,256]{3,2,1,0:T(8,128)(2,1)}, u32[]{:S(2)}, u32[]{:S(2)}) collective-permute-start(bf16[4,40,16,256]{3,2,1,0:T(8,128)(2,1)} %pad_maximum_fusion.4), channel_id=1, source_target_pairs={{0,16},{1,3},{2,18},{3,1},{4,20},{5,7},{6,22},{7,5},{8,24},{9,11},... | collective-permute-start | bytes 3932168 | tf_op jit(solution)/shard_map/ppermute | solution.py:105
  117.8 10.8 %collective-permute-start.13 = (bf16[2,32,16,256]{3,2,1,0:T(8,128)(2,1)S(1)}, bf16[2,32,16,256]{3,2,1,0:T(8,128)(2,1)S(1)}, u32[]{:S(2)}, u32[]{:S(2)}) collective-permute-start(bf16[2,32,16,256]{3,2,1,0:T(8,128)(2,1)S(1)} %pad_maximum_fusion.17), channel_id=1, source_target_pairs={{0,2},{1,17},{2,0},{3,19},{4,6},{5,21},{6,4},{7,23},{8,10},{9,25},... | collective-permute-start | bytes 1572872 | tf_op jit(solution)/shard_map/ppermute | solution.py:105
  130.5 34.1 %collective-permute-start.14 = (bf16[8,40,16,256]{3,2,1,0:T(8,128)(2,1)S(1)}, bf16[8,40,16,256]{3,2,1,0:T(8,128)(2,1)}, u32[]{:S(2)}, u32[]{:S(2)}) collective-permute-start(bf16[8,40,16,256]{3,2,1,0:T(8,128)(2,1)S(1)} %pad_maximum_fusion.refs_0_), channel_id=1, source_target_pairs={{0,2},{1,17},{2,0},{3,19},{4,6},{5,21},{6,4},{7,23},{8,10},{9,25},... | collective-permute-start | bytes 7864328 | tf_op jit(solution)/shard_map/ppermute | solution.py:105
  132.0 32.6 %collective-permute-start.15 = (bf16[8,40,16,256]{3,2,1,0:T(8,128)(2,1)S(1)}, bf16[8,40,16,256]{3,2,1,0:T(8,128)(2,1)}, u32[]{:S(2)}, u32[]{:S(2)}) collective-permute-start(bf16[8,40,16,256]{3,2,1,0:T(8,128)(2,1)S(1)} %pad_maximum_fusion.refs_0_), channel_id=1, source_target_pairs={{0,1},{1,0},{2,3},{3,2},{4,5},{5,4},{6,7},{7,6},{8,9},{9,8},{10,11... | collective-permute-start | bytes 7864328 | tf_op jit(solution)/shard_map/ppermute | solution.py:94
  133.4 31.2 %collective-permute-start.16 = (bf16[4,32,16,256]{3,2,1,0:T(8,128)(2,1)}, bf16[4,32,16,256]{3,2,1,0:T(8,128)(2,1)}, u32[]{:S(2)}, u32[]{:S(2)}) collective-permute-start(bf16[4,32,16,256]{3,2,1,0:T(8,128)(2,1)} %pad_maximum_fusion.8), channel_id=1, source_target_pairs={{0,4},{1,5},{2,6},{3,7},{4,0},{5,1},{6,2},{7,3},{8,12},{9,13},{10,... | collective-permute-start | bytes 3145736 | tf_op jit(solution)/shard_map/ppermute | solution.py:105
  135.1 28.4 %collective-permute-start.17 = (bf16[1,32,16,256]{3,2,1,0:T(8,128)(2,1)S(1)}, bf16[1,32,16,256]{3,2,1,0:T(8,128)(2,1)}, u32[]{:S(2)}, u32[]{:S(2)}) collective-permute-start(bf16[1,32,16,256]{3,2,1,0:T(8,128)(2,1)S(1)} %bitcast.261), channel_id=1, source_target_pairs={{0,8},{1,9},{2,10},{3,11},{4,12},{5,13},{6,14},{7,15},{8,0},{9,1},... | collective-permute-start | bytes 786440 | tf_op jit(solution)/shard_map/ppermute | solution.py:105
  164.6 14.5 %collective-permute-start.18 = (bf16[8,40,16,256]{3,2,1,0:T(8,128)(2,1)}, bf16[8,40,16,256]{3,2,1,0:T(8,128)(2,1)}, u32[]{:S(2)}, u32[]{:S(2)}) collective-permute-start(bf16[8,40,16,256]{3,2,1,0:T(8,128)(2,1)} %collective-permute-done.14.refs_1_), channel_id=1, source_target_pairs={{0,1},{1,0},{2,3},{3,2},{4,5},{5,4},{6,7},{7,6},{8,9},{9,8},{10,11... | collective-permute-start | bytes 7864328 | tf_op jit(solution)/shard_map/ppermute | solution.py:94
  168.5 52.2 %collective-permute-start.20 = (bf16[8,32,16,256]{3,2,1,0:T(8,128)(2,1)}, bf16[8,32,16,256]{3,2,1,0:T(8,128)(2,1)}, u32[]{:S(2)}, u32[]{:S(2)}) collective-permute-start(bf16[8,32,16,256]{3,2,1,0:T(8,128)(2,1)} %pad_maximum_fusion.1.refs_0_), channel_id=1, source_target_pairs={{0,16},{1,3},{2,18},{3,1},{4,20},{5,7},{6,22},{7,5},{8,24},{9,11},... | collective-permute-start | bytes 6291464 | tf_op jit(solution)/shard_map/ppermute | solution.py:105
  170.0 50.7 %collective-permute-start.21 = (bf16[8,32,16,256]{3,2,1,0:T(8,128)(2,1)}, bf16[8,32,16,256]{3,2,1,0:T(8,128)(2,1)}, u32[]{:S(2)}, u32[]{:S(2)}) collective-permute-start(bf16[8,32,16,256]{3,2,1,0:T(8,128)(2,1)} %pad_maximum_fusion.1.refs_0_), channel_id=1, source_target_pairs={{0,1},{1,0},{2,3},{3,2},{4,5},{5,4},{6,7},{7,6},{8,9},{9,8},{10,11... | collective-permute-start | bytes 6291464 | tf_op jit(solution)/shard_map/ppermute | solution.py:94
  171.8 28.9 %collective-permute-start.19 = (bf16[2,32,16,256]{3,2,1,0:T(8,128)(2,1)}, bf16[2,32,16,256]{3,2,1,0:T(8,128)(2,1)}, u32[]{:S(2)}, u32[]{:S(2)}) collective-permute-start(bf16[2,32,16,256]{3,2,1,0:T(8,128)(2,1)} %pad_maximum_fusion.18), channel_id=1, source_target_pairs={{0,2},{1,17},{2,0},{3,19},{4,6},{5,21},{6,4},{7,23},{8,10},{9,25},... | collective-permute-start | bytes 1572872 | tf_op jit(solution)/shard_map/ppermute | solution.py:105
  173.7 47.0 %all-to-all-start.1 = ((bf16[2,16,32,512]{3,2,0,1:T(8,128)(2,1)}), bf16[2,16,32,512]{3,2,0,1:T(8,128)(2,1)S(1)}, u32[]{:S(2)}, u32[]{:S(2)}) async-start(bf16[2,16,32,512]{3,2,0,1:T(8,128)(2,1)} %copy.66), calls=%async_computation.1 | async-start | bytes 2097152 | tf_op jit(solution)/shard_map/all_to_all | solution.py:669
  202.9 20.0 %collective-permute-start.22 = (bf16[4,32,16,256]{3,2,1,0:T(8,128)(2,1)}, bf16[4,32,16,256]{3,2,1,0:T(8,128)(2,1)}, u32[]{:S(2)}, u32[]{:S(2)}) collective-permute-start(bf16[4,32,16,256]{3,2,1,0:T(8,128)(2,1)} %pad_maximum_fusion.9), channel_id=1, source_target_pairs={{0,16},{1,5},{2,18},{3,7},{4,20},{5,1},{6,22},{7,3},{8,24},{9,13},... | collective-permute-start | bytes 3145736 | tf_op jit(solution)/shard_map/ppermute | solution.py:105
  222.9 13.1 %collective-permute-start.23 = (bf16[8,32,16,256]{3,2,1,0:T(8,128)(2,1)}, bf16[8,32,16,256]{3,2,1,0:T(8,128)(2,1)}, u32[]{:S(2)}, u32[]{:S(2)}) collective-permute-start(bf16[8,32,16,256]{3,2,1,0:T(8,128)(2,1)} %collective-permute-done.20.refs_1_), channel_id=1, source_target_pairs={{0,1},{1,0},{2,3},{3,2},{4,5},{5,4},{6,7},{7,6},{8,9},{9,8},{10,11... | collective-permute-start | bytes 6291464 | tf_op jit(solution)/shard_map/ppermute | solution.py:94
  225.9 38.8 %collective-permute-start.24 = (bf16[8,32,16,256]{3,2,1,0:T(8,128)(2,1)}, bf16[8,32,16,256]{3,2,1,0:T(8,128)(2,1)}, u32[]{:S(2)}, u32[]{:S(2)}) collective-permute-start(bf16[8,32,16,256]{3,2,1,0:T(8,128)(2,1)} %pad_maximum_fusion.2.refs_0_), channel_id=1, source_target_pairs={{0,4},{1,3},{2,6},{3,1},{4,0},{5,7},{6,2},{7,5},{8,12},{9,11},{10,... | collective-permute-start | bytes 6291464 | tf_op jit(solution)/shard_map/ppermute | solution.py:105
  228.3 36.5 %collective-permute-start.25 = (bf16[8,32,16,256]{3,2,1,0:T(8,128)(2,1)}, bf16[8,32,16,256]{3,2,1,0:T(8,128)(2,1)}, u32[]{:S(2)}, u32[]{:S(2)}) collective-permute-start(bf16[8,32,16,256]{3,2,1,0:T(8,128)(2,1)} %pad_maximum_fusion.2.refs_0_), channel_id=1, source_target_pairs={{0,1},{1,0},{2,3},{3,2},{4,5},{5,4},{6,7},{7,6},{8,9},{9,8},{10,11... | collective-permute-start | bytes 6291464 | tf_op jit(solution)/shard_map/ppermute | solution.py:94
  229.9 41.4 %all-to-all-start.2 = ((bf16[32,1,32,512]{3,2,1,0:T(8,128)(2,1)}), bf16[32,1,32,512]{3,2,1,0:T(8,128)(2,1)S(1)}, u32[]{:S(2)}, u32[]{:S(2)}) async-start(bf16[32,1,32,512]{3,2,1,0:T(8,128)(2,1)} %bitcast.257), calls=%async_computation.2 | async-start | bytes 2097152 | tf_op jit(solution)/shard_map/all_to_all | solution.py:674
  264.7 9.5 %collective-permute-start.26 = (bf16[8,32,16,256]{3,2,1,0:T(8,128)(2,1)}, bf16[8,32,16,256]{3,2,1,0:T(8,128)(2,1)}, u32[]{:S(2)}, u32[]{:S(2)}) collective-permute-start(bf16[8,32,16,256]{3,2,1,0:T(8,128)(2,1)} %collective-permute-done.24.refs_1_), channel_id=1, source_target_pairs={{0,1},{1,0},{2,3},{3,2},{4,5},{5,4},{6,7},{7,6},{8,9},{9,8},{10,11... | collective-permute-start | bytes 6291464 | tf_op jit(solution)/shard_map/ppermute | solution.py:94
  272.9 33.2 %collective-permute-start.30 = (bf16[512,4096]{1,0:T(8,128)(2,1)}, bf16[512,4096]{1,0:T(8,128)(2,1)}, u32[]{:S(2)}, u32[]{:S(2)}) collective-permute-start(bf16[512,4096]{1,0:T(8,128)(2,1)} %get-tuple-element.213.x_own), channel_id=1, source_target_pairs={{0,1},{1,0},{2,3},{3,2},{4,5},{5,4},{6,7},{7,6},{8,9},{9,8},{10,11... | collective-permute-start | bytes 12582920 | tf_op jit(solution)/shard_map/ppermute | solution.py:94
  297.3 8.2 %collective-permute-start.28 = (bf16[512,1024]{1,0:T(8,128)(2,1)S(1)}, bf16[512,1024]{1,0:T(8,128)(2,1)}, u32[]{:S(2)}, u32[]{:S(2)}) collective-permute-start(bf16[512,1024]{1,0:T(8,128)(2,1)S(1)} %convert_element_type.379.refs_0_), channel_id=1, source_target_pairs={{0,1},{1,0},{2,3},{3,2},{4,5},{5,4},{6,7},{7,6},{8,9},{9,8},{10,11... | collective-permute-start | bytes 3145736 | tf_op jit(solution)/shard_map/ppermute | solution.py:94
  305.5 11.7 %collective-permute-start.29 = (bf16[512,4096]{1,0:T(8,128)(2,1)}, bf16[512,4096]{1,0:T(8,128)(2,1)}, u32[]{:S(2)}, u32[]{:S(2)}) collective-permute-start(bf16[512,4096]{1,0:T(8,128)(2,1)} %multiply_convert_fusion.refs_0_), channel_id=1, source_target_pairs={{0,1},{1,0},{2,3},{3,2},{4,5},{5,4},{6,7},{7,6},{8,9},{9,8},{10,11... | collective-permute-start | bytes 12582920 | tf_op jit(solution)/shard_map/ppermute | solution.py:94
  305.5 31.1 %collective-permute-start.32 = (bf16[512,1024]{1,0:T(8,128)(2,1)S(1)}, bf16[512,1024]{1,0:T(8,128)(2,1)}, u32[]{:S(2)}, u32[]{:S(2)}) collective-permute-start(bf16[512,1024]{1,0:T(8,128)(2,1)S(1)} %copy-done.6), channel_id=1, source_target_pairs={{0,1},{1,0},{2,3},{3,2},{4,5},{5,4},{6,7},{7,6},{8,9},{9,8},{10,11... | collective-permute-start | bytes 3145736 | tf_op jit(solution)/shard_map/ppermute | solution.py:94
  317.2 29.1 %collective-permute-start.33 = (bf16[8,32,16,256]{3,2,1,0:T(8,128)(2,1)}, bf16[8,32,16,256]{3,2,1,0:T(8,128)(2,1)}, u32[]{:S(2)}, u32[]{:S(2)}) collective-permute-start(bf16[8,32,16,256]{3,2,1,0:T(8,128)(2,1)} %bitcast.323), channel_id=1, source_target_pairs={{0,4},{1,3},{2,6},{3,1},{4,0},{5,7},{6,2},{7,5},{8,12},{9,11},{10,... | collective-permute-start | bytes 6291464 | tf_op jit(solution)/shard_map/ppermute | solution.py:105
  350.6 19.8 %collective-permute-start.34 = (bf16[4,32,16,256]{3,2,1,0:T(8,128)(2,1)}, bf16[4,32,16,256]{3,2,1,0:T(8,128)(2,1)}, u32[]{:S(2)}, u32[]{:S(2)}) collective-permute-start(bf16[4,32,16,256]{3,2,1,0:T(8,128)(2,1)} %get-tuple-element.351), channel_id=1, source_target_pairs={{0,16},{1,5},{2,18},{3,7},{4,20},{5,1},{6,22},{7,3},{8,24},{9,13},... | collective-permute-start | bytes 3145736 | tf_op jit(solution)/shard_map/ppermute | solution.py:105
  352.9 31.2 %all-to-all-start.3 = ((bf16[2,16,32,512]{3,2,0,1:T(8,128)(2,1)}), bf16[2,16,32,512]{3,2,0,1:T(8,128)(2,1)}, u32[]{:S(2)}, u32[]{:S(2)}) async-start(bf16[2,16,32,512]{3,2,0,1:T(8,128)(2,1)} %copy.69), calls=%async_computation.3 | async-start | bytes 2097152 | tf_op jit(solution)/shard_map/all_to_all | solution.py:669
  377.2 7.0 %collective-permute-start.35 = (bf16[512,1024]{1,0:T(8,128)(2,1)S(1)}, bf16[512,1024]{1,0:T(8,128)(2,1)}, u32[]{:S(2)}, u32[]{:S(2)}) collective-permute-start(bf16[512,1024]{1,0:T(8,128)(2,1)S(1)} %convert_element_type.387.refs_0_), channel_id=1, source_target_pairs={{0,1},{1,0},{2,3},{3,2},{4,5},{5,4},{6,7},{7,6},{8,9},{9,8},{10,11... | collective-permute-start | bytes 3145736 | tf_op jit(solution)/shard_map/ppermute | solution.py:94
  380.3 12.0 %collective-permute-start.42 = (bf16[512,1024]{1,0:T(8,128)(2,1)}, bf16[512,1024]{1,0:T(8,128)(2,1)}, u32[]{:S(2)}, u32[]{:S(2)}) collective-permute-start(bf16[512,1024]{1,0:T(8,128)(2,1)} %get-tuple-element.190.x_own.o_ref), channel_id=1, source_target_pairs={{0,1},{1,0},{2,3},{3,2},{4,5},{5,4},{6,7},{7,6},{8,9},{9,8},{10,11... | collective-permute-start | bytes 3145736 | tf_op jit(solution)/shard_map/ppermute | solution.py:94
  380.4 45.6 %collective-permute-start.43 = (bf16[8,32,16,256]{3,2,1,0:T(8,128)(2,1)}, bf16[8,32,16,256]{3,2,1,0:T(8,128)(2,1)}, u32[]{:S(2)}, u32[]{:S(2)}) collective-permute-start(bf16[8,32,16,256]{3,2,1,0:T(8,128)(2,1)} %bitcast.61), channel_id=1, source_target_pairs={{0,16},{1,3},{2,18},{3,1},{4,20},{5,7},{6,22},{7,5},{8,24},{9,11},... | collective-permute-start | bytes 6291464 | tf_op jit(solution)/shard_map/ppermute | solution.py:105
  387.1 36.6 %all-to-all-start.4 = ((bf16[32,1,32,512]{3,2,1,0:T(8,128)(2,1)}), bf16[32,1,32,512]{3,2,1,0:T(8,128)(2,1)}, u32[]{:S(2)}, u32[]{:S(2)}) async-start(bf16[32,1,32,512]{3,2,1,0:T(8,128)(2,1)} %bitcast.256), calls=%async_computation.4 | async-start | bytes 2097152 | tf_op jit(solution)/shard_map/all_to_all | solution.py:674
  391.8 9.7 %collective-permute-start.41 = (bf16[512,1024]{1,0:T(8,128)(2,1)}, bf16[512,1024]{1,0:T(8,128)(2,1)}, u32[]{:S(2)}, u32[]{:S(2)}) collective-permute-start(bf16[512,1024]{1,0:T(8,128)(2,1)} %get-tuple-element.285.refs_0_), channel_id=1, source_target_pairs={{0,1},{1,0},{2,3},{3,2},{4,5},{5,4},{6,7},{7,6},{8,9},{9,8},{10,11... | collective-permute-start | bytes 3145736 | tf_op jit(solution)/shard_map/ppermute | solution.py:94
  392.3 25.6 %collective-permute-start.36 = (bf16[512,1024]{1,0:T(8,128)(2,1)}, bf16[512,1024]{1,0:T(8,128)(2,1)}, u32[]{:S(2)}, u32[]{:S(2)}) collective-permute-start(bf16[512,1024]{1,0:T(8,128)(2,1)} %get-tuple-element.202.o_ref.x_own), channel_id=1, source_target_pairs={{0,1},{1,0},{2,3},{3,2},{4,5},{5,4},{6,7},{7,6},{8,9},{9,8},{10,11... | collective-permute-start | bytes 3145736 | tf_op jit(solution)/shard_map/ppermute | solution.py:94
  392.4 25.5 %collective-permute-start.37 = (bf16[512,1024]{1,0:T(8,128)(2,1)S(1)}, bf16[512,1024]{1,0:T(8,128)(2,1)}, u32[]{:S(2)}, u32[]{:S(2)}) collective-permute-start(bf16[512,1024]{1,0:T(8,128)(2,1)S(1)} %copy-done.15), channel_id=1, source_target_pairs={{0,1},{1,0},{2,3},{3,2},{4,5},{5,4},{6,7},{7,6},{8,9},{9,8},{10,11... | collective-permute-start | bytes 3145736 | tf_op jit(solution)/shard_map/ppermute | solution.py:94
  399.5 26.5 %collective-permute-start.44 = (bf16[2,32,16,256]{3,2,1,0:T(8,128)(2,1)}, bf16[2,32,16,256]{3,2,1,0:T(8,128)(2,1)}, u32[]{:S(2)}, u32[]{:S(2)}) collective-permute-start(bf16[2,32,16,256]{3,2,1,0:T(8,128)(2,1)} %get-tuple-element.360), channel_id=1, source_target_pairs={{0,2},{1,17},{2,0},{3,19},{4,6},{5,21},{6,4},{7,23},{8,10},{9,25},... | collective-permute-start | bytes 1572872 | tf_op jit(solution)/shard_map/ppermute | solution.py:105
  401.5 10.3 %collective-permute-start.39 = (bf16[128,1024]{1,0:T(8,128)(2,1)S(1)}, bf16[128,1024]{1,0:T(8,128)(2,1)S(1)}, u32[]{:S(2)}, u32[]{:S(2)}) collective-permute-start(bf16[128,1024]{1,0:T(8,128)(2,1)S(1)} %copy-done.39), channel_id=1, source_target_pairs={{0,1},{1,0},{2,3},{3,2},{4,5},{5,4},{6,7},{7,6},{8,9},{9,8},{10,11... | collective-permute-start | bytes 786440 | tf_op jit(solution)/shard_map/ppermute | solution.py:94
  426.0 32.0 %collective-permute-start.45 = (bf16[8,40,16,256]{3,2,1,0:T(8,128)(2,1)}, bf16[8,40,16,256]{3,2,1,0:T(8,128)(2,1)}, u32[]{:S(2)}, u32[]{:S(2)}) collective-permute-start(bf16[8,40,16,256]{3,2,1,0:T(8,128)(2,1)} %bitcast.241), channel_id=1, source_target_pairs={{0,2},{1,17},{2,0},{3,19},{4,6},{5,21},{6,4},{7,23},{8,10},{9,25},... | collective-permute-start | bytes 7864328 | tf_op jit(solution)/shard_map/ppermute | solution.py:105
  443.4 19.6 %collective-permute-start.46 = (bf16[512,1024]{1,0:T(8,128)(2,1)}, bf16[512,1024]{1,0:T(8,128)(2,1)}, u32[]{:S(2)}, u32[]{:S(2)}) collective-permute-start(bf16[512,1024]{1,0:T(8,128)(2,1)} %get-tuple-element.289.refs_0_), channel_id=1, source_target_pairs={{0,1},{1,0},{2,3},{3,2},{4,5},{5,4},{6,7},{7,6},{8,9},{9,8},{10,11... | collective-permute-start | bytes 3145736 | tf_op jit(solution)/shard_map/ppermute | solution.py:94
  443.5 21.0 %collective-permute-start.47 = (bf16[512,1024]{1,0:T(8,128)(2,1)}, bf16[512,1024]{1,0:T(8,128)(2,1)}, u32[]{:S(2)}, u32[]{:S(2)}) collective-permute-start(bf16[512,1024]{1,0:T(8,128)(2,1)} %get-tuple-element.278.refs_1_), channel_id=1, source_target_pairs={{0,1},{1,0},{2,3},{3,2},{4,5},{5,4},{6,7},{7,6},{8,9},{9,8},{10,11... | collective-permute-start | bytes 3145736 | tf_op jit(solution)/shard_map/ppermute | solution.py:94
  444.0 20.5 %collective-permute-start.48 = (bf16[512,1024]{1,0:T(8,128)(2,1)}, bf16[512,1024]{1,0:T(8,128)(2,1)}, u32[]{:S(2)}, u32[]{:S(2)}) collective-permute-start(bf16[512,1024]{1,0:T(8,128)(2,1)} %get-tuple-element.290.refs_2_), channel_id=1, source_target_pairs={{0,1},{1,0},{2,3},{3,2},{4,5},{5,4},{6,7},{7,6},{8,9},{9,8},{10,11... | collective-permute-start | bytes 3145736 | tf_op jit(solution)/shard_map/ppermute | solution.py:94
  448.5 33.2 %collective-permute-start.50 = (bf16[4,32,16,256]{3,2,1,0:T(8,128)(2,1)}, bf16[4,32,16,256]{3,2,1,0:T(8,128)(2,1)}, u32[]{:S(2)}, u32[]{:S(2)}) collective-permute-start(bf16[4,32,16,256]{3,2,1,0:T(8,128)(2,1)} %get-tuple-element.349), channel_id=1, source_target_pairs={{0,4},{1,5},{2,6},{3,7},{4,0},{5,1},{6,2},{7,3},{8,12},{9,13},{10,... | collective-permute-start | bytes 3145736 | tf_op jit(solution)/shard_map/ppermute | solution.py:105
  458.0 20.4 %collective-permute-start.61 = (bf16[1,32,16,256]{3,2,1,0:T(8,128)(2,1)}, bf16[1,32,16,256]{3,2,1,0:T(8,128)(2,1)}, u32[]{:S(2)}, u32[]{:S(2)}) collective-permute-start(bf16[1,32,16,256]{3,2,1,0:T(8,128)(2,1)} %add_convert_fusion.23), channel_id=1, source_target_pairs={{0,8},{1,9},{2,10},{3,11},{4,12},{5,13},{6,14},{7,15},{8,0},{9,1},... | collective-permute-start | bytes 786440 | tf_op jit(solution)/shard_map/ppermute | solution.py:105
  463.0 18.7 %collective-permute-start.49 = (bf16[4,40,16,256]{3,2,1,0:T(8,128)(2,1)}, bf16[4,40,16,256]{3,2,1,0:T(8,128)(2,1)}, u32[]{:S(2)}, u32[]{:S(2)}) collective-permute-start(bf16[4,40,16,256]{3,2,1,0:T(8,128)(2,1)} %get-tuple-element.347), channel_id=1, source_target_pairs={{0,16},{1,3},{2,18},{3,1},{4,20},{5,7},{6,22},{7,5},{8,24},{9,11},... | collective-permute-start | bytes 3932168 | tf_op jit(solution)/shard_map/ppermute | solution.py:105
  480.2 20.4 %collective-permute-start.51 = (bf16[8,24,16,256]{3,2,1,0:T(8,128)(2,1)S(1)}, bf16[8,24,16,256]{3,2,1,0:T(8,128)(2,1)S(1)}, u32[]{:S(2)}, u32[]{:S(2)}) collective-permute-start(bf16[8,24,16,256]{3,2,1,0:T(8,128)(2,1)S(1)} %bitcast.324), channel_id=1, source_target_pairs={{0,2},{1,17},{2,0},{3,19},{4,6},{5,21},{6,4},{7,23},{8,10},{9,25},... | collective-permute-start | bytes 4718600 | tf_op jit(solution)/shard_map/ppermute | solution.py:105
  483.2 23.0 %collective-permute-start.53 = (bf16[2,32,16,256]{3,2,1,0:T(8,128)(2,1)S(1)}, bf16[2,32,16,256]{3,2,1,0:T(8,128)(2,1)S(1)}, u32[]{:S(2)}, u32[]{:S(2)}) collective-permute-start(bf16[2,32,16,256]{3,2,1,0:T(8,128)(2,1)S(1)} %get-tuple-element.358), channel_id=1, source_target_pairs={{0,2},{1,17},{2,0},{3,19},{4,6},{5,21},{6,4},{7,23},{8,10},{9,25},... | collective-permute-start | bytes 1572872 | tf_op jit(solution)/shard_map/ppermute | solution.py:105
  486.3 19.9 %collective-permute-start.52 = (bf16[2,40,16,256]{3,2,1,0:T(8,128)(2,1)S(1)}, bf16[2,40,16,256]{3,2,1,0:T(8,128)(2,1)S(1)}, u32[]{:S(2)}, u32[]{:S(2)}) collective-permute-start(bf16[2,40,16,256]{3,2,1,0:T(8,128)(2,1)S(1)} %get-tuple-element.355), channel_id=1, source_target_pairs={{0,4},{1,5},{2,6},{3,7},{4,0},{5,1},{6,2},{7,3},{8,12},{9,13},{10,... | collective-permute-start | bytes 1966088 | tf_op jit(solution)/shard_map/ppermute | solution.py:105
  506.3 30.1 %collective-permute-start.58 = (bf16[1,40,16,256]{3,2,1,0:T(8,128)(2,1)S(1)}, bf16[1,40,16,256]{3,2,1,0:T(8,128)(2,1)S(1)}, u32[]{:S(2)}, u32[]{:S(2)}) collective-permute-start(bf16[1,40,16,256]{3,2,1,0:T(8,128)(2,1)S(1)} %add_convert_fusion.21), channel_id=1, source_target_pairs={{0,8},{1,9},{2,10},{3,11},{4,12},{5,13},{6,14},{7,15},{8,0},{9,1},... | collective-permute-start | bytes 983048 | tf_op jit(solution)/shard_map/ppermute | solution.py:105
  510.2 24.4 %collective-permute-start.54 = (bf16[4,24,16,256]{3,2,1,0:T(8,128)(2,1)S(1)}, bf16[4,24,16,256]{3,2,1,0:T(8,128)(2,1)S(1)}, u32[]{:S(2)}, u32[]{:S(2)}) collective-permute-start(bf16[4,24,16,256]{3,2,1,0:T(8,128)(2,1)S(1)} %get-tuple-element.353), channel_id=1, source_target_pairs={{0,16},{1,3},{2,18},{3,1},{4,20},{5,7},{6,22},{7,5},{8,24},{9,11},... | collective-permute-start | bytes 2359304 | tf_op jit(solution)/shard_map/ppermute | solution.py:105
  511.1 23.3 %collective-permute-start.55 = (bf16[512,512]{1,0:T(8,128)(2,1)S(1)}, bf16[512,512]{1,0:T(8,128)(2,1)S(1)}, u32[]{:S(2)}, u32[]{:S(2)}) collective-permute-start(bf16[512,512]{1,0:T(8,128)(2,1)S(1)} %constant_dynamic-slice_fusion), channel_id=1, source_target_pairs={{0,1},{1,0},{2,3},{3,2},{4,5},{5,4},{6,7},{7,6},{8,9},{9,8},{10,11... | collective-permute-start | bytes 1572872 | tf_op jit(solution)/shard_map/ppermute | solution.py:94
  511.5 22.8 %collective-permute-start.60 = (bf16[1,32,16,256]{3,2,1,0:T(8,128)(2,1)S(1)}, bf16[1,32,16,256]{3,2,1,0:T(8,128)(2,1)S(1)}, u32[]{:S(2)}, u32[]{:S(2)}) collective-permute-start(bf16[1,32,16,256]{3,2,1,0:T(8,128)(2,1)S(1)} %add_convert_fusion.26), channel_id=1, source_target_pairs={{0,8},{1,9},{2,10},{3,11},{4,12},{5,13},{6,14},{7,15},{8,0},{9,1},... | collective-permute-start | bytes 786440 | tf_op jit(solution)/shard_map/ppermute | solution.py:105
  534.9 9.0 %collective-permute-start.57 = (bf16[2,24,16,256]{3,2,1,0:T(8,128)(2,1)S(1)}, bf16[2,24,16,256]{3,2,1,0:T(8,128)(2,1)S(1)}, u32[]{:S(2)}, u32[]{:S(2)}) collective-permute-start(bf16[2,24,16,256]{3,2,1,0:T(8,128)(2,1)S(1)} %get-tuple-element.368), channel_id=1, source_target_pairs={{0,4},{1,5},{2,6},{3,7},{4,0},{5,1},{6,2},{7,3},{8,12},{9,13},{10,... | collective-permute-start | bytes 1179656 | tf_op jit(solution)/shard_map/ppermute | solution.py:105
  544.0 9.9 %collective-permute-start.59 = (bf16[1,24,16,256]{3,2,1,0:T(8,128)(2,1)S(1)}, bf16[1,24,16,256]{3,2,1,0:T(8,128)(2,1)S(1)}, u32[]{:S(2)}, u32[]{:S(2)}) collective-permute-start(bf16[1,24,16,256]{3,2,1,0:T(8,128)(2,1)S(1)} %add_convert_fusion.29), channel_id=1, source_target_pairs={{0,8},{1,9},{2,10},{3,11},{4,12},{5,13},{6,14},{7,15},{8,0},{9,1},... | collective-permute-start | bytes 589832 | tf_op jit(solution)/shard_map/ppermute | solution.py:105
  555.5 21.8 %all-to-all-start.5 = ((bf16[64,16,256]{2,1,0:T(8,128)(2,1)}), bf16[64,16,256]{2,1,0:T(8,128)(2,1)S(1)}, u32[]{:S(2)}, u32[]{:S(2)}) async-start(bf16[64,16,256]{2,1,0:T(8,128)(2,1)} %gather_fusion.3), calls=%async_computation.5 | async-start | bytes 1048576 | tf_op jit(solution)/shard_map/all_to_all | solution.py:327
  577.3 19.7 %all-to-all-start.6 = ((bf16[72,16,256]{2,1,0:T(8,128)(2,1)}), bf16[72,16,256]{2,1,0:T(8,128)(2,1)S(1)}, u32[]{:S(2)}, u32[]{:S(2)}) async-start(bf16[72,16,256]{2,1,0:T(8,128)(2,1)} %bitcast.88), calls=%async_computation.6 | async-start | bytes 1179648 | tf_op jit(solution)/shard_map/all_to_all | solution.py:327
  580.9 13.6 %collective-permute-start.63 = (bf16[8,8,16,256]{3,2,1,0:T(8,128)(2,1)S(1)}, bf16[8,8,16,256]{3,2,1,0:T(8,128)(2,1)S(1)}, u32[]{:S(2)}, u32[]{:S(2)}) collective-permute-start(bf16[8,8,16,256]{3,2,1,0:T(8,128)(2,1)S(1)} %bitcast.282), channel_id=1, source_target_pairs={{0,16},{16,0},{1,17},{17,1},{2,18},{18,2},{3,19},{19,3},{4,20},{20... | collective-permute-start | bytes 1572872 | tf_op jit(solution)/shard_map/ppermute | solution.py:97
  597.0 13.8 %collective-permute-start.64 = (bf16[8,9,16,256]{3,2,1,0:T(8,128)(2,1)S(1)}, bf16[8,9,16,256]{3,2,1,0:T(8,128)(2,1)S(1)}, u32[]{:S(2)}, u32[]{:S(2)}) collective-permute-start(bf16[8,9,16,256]{3,2,1,0:T(8,128)(2,1)S(1)} %bitcast.273), channel_id=1, source_target_pairs={{0,16},{16,0},{1,17},{17,1},{2,18},{18,2},{3,19},{19,3},{4,20},{20... | collective-permute-start | bytes 1769480 | tf_op jit(solution)/shard_map/ppermute | solution.py:97
  (89 other events, 933.6 us)

commit v8 on v7

--- a/solution.py
+++ b/solution.py
@@ -529,7 +529,7 @@
     )(h, w, b)
 
 
-def weight_grad_body(s, x_own, x_sib, *refs, count, outs, many, rows):
+def weight_grad_body(s, x_own, x_sib, *refs, count, outs, many, rows, nb):
     y_own, y_sib = refs[:count], refs[count : 2 * count]
     targets = refs[-3 - outs : -3]
     t_own, t_sib, buf = refs[-3:]
@@ -540,10 +540,11 @@
         acc = dot_nn(t_own[...], y_own[k][...]) + dot_nn(t_sib[...], y_sib[k][...])
         buf[k] = acc.astype(bf16)
     for q in range(many):
-        here = pl.ds(pl.multiple_of(s[q] * rows, rows), rows)
-        for k in range(count):
-            for c in range(targets[0].shape[2]):
-                targets[q // per][q % per, k, c] = buf[k, here, c * BS : (c + 1) * BS]
+        for r in range(x_own.shape[1] // BS):
+            here = pl.ds(pl.multiple_of(s[q] * rows + r * BS, rows), rows)
+            for k in range(count):
+                for c in range(nb):
+                    targets[q // per][q % per, k, r * nb + c] = buf[k, here, c * BS : (c + 1) * BS]
 
 
 def weight_grad(net, group, table, xs, ys, held, first, wide):
@@ -553,36 +554,42 @@
     count = len(ys)
     width = ys[0][0].shape[1]
     if wide:
-        steps = xs[0].shape[1] // BS
+        tall = xs[0].shape[1] // BS
+        deep = 2 if tall >= 4 else 1
+        steps = tall // deep
         y_width = width // halves
-        x_spec = pl.BlockSpec((seq, BS), lambda i, s: (0, i))
+        x_spec = pl.BlockSpec((seq, deep * BS), lambda i, s: (0, i))
         y_spec = pl.BlockSpec((seq, y_width), lambda i, s: (0, s[at_core]))
     else:
-        steps = xs[0].shape[1] // halves // BS
+        tall = xs[0].shape[1] // halves // BS
+        deep = 2 if tall >= 4 else 1
+        steps = tall // deep
         y_width = width
-        x_spec = pl.BlockSpec((seq, BS), lambda i, s: (0, s[at_core] * steps + i))
+        x_spec = pl.BlockSpec((seq, deep * BS), lambda i, s: (0, s[at_core] * steps + i))
         y_spec = pl.BlockSpec((seq, y_width), lambda i, s: (0, 0))
     nb = y_width // BS
     at = first // count
     outs = 2 if many > 1 else 1
-    shape = (many // outs, len(GROUPS[group]), steps * nb, rows, BS)
+    shape = (many // outs, len(GROUPS[group]), tall * nb, rows, BS)
     anyspec = pl.BlockSpec(memory_space=pl.ANY)
     held = held or ()
     before = 3 + 2 * count
     return pl.pallas_call(
-        functools.partial(weight_grad_body, count=count, outs=outs, many=many, rows=rows),
+        functools.partial(
+            weight_grad_body, count=count, outs=outs, many=many, rows=rows, nb=nb
+        ),
         grid_spec=pltpu.PrefetchScalarGridSpec(
             num_scalar_prefetch=1,
             grid=(steps,),
             in_specs=[x_spec] * 2 + [y_spec] * (2 * count) + [anyspec] * len(held),
             out_specs=(
-                pl.BlockSpec((many // outs, count, nb, rows, BS), lambda i, s: (0, at, i, 0, 0)),
+                pl.BlockSpec((many // outs, count, deep * nb, rows, BS), lambda i, s: (0, at, i, 0, 0)),
             )
             * outs,
             scratch_shapes=[
-                pltpu.VMEM((BS, seq), bf16),
-                pltpu.VMEM((BS, seq), bf16),
-                pltpu.VMEM((count, BS, y_width), bf16),
+                pltpu.VMEM((deep * BS, seq), bf16),
+                pltpu.VMEM((deep * BS, seq), bf16),
+                pltpu.VMEM((count, deep * BS, y_width), bf16),
             ],
         ),
         out_shape=(jax.ShapeDtypeStruct(shape, bf16),) * outs,
@@ -832,8 +839,8 @@
     sibs = [net.swap_core(v) for v in (dq_s, dk_s, dv_s)]
     dq_s, dk_s, dv_s = step((dq_s, dk_s, dv_s), cross)
     attn = gradient(0, ((x, x_sib), *zip((dq_s, dk_s, dv_s), sibs)))
-    dk_c, dv_c, dq_s, dk_s, dv_s = step((dk_c, dv_c, dq_s, dk_s, dv_s), attn)
-    dq_s, dk_s, dv_s = step((dq_s, dk_s, dv_s), cross, up)
+    dq_s, dk_s, dv_s = step((dq_s, dk_s, dv_s), attn)
+    dk_c, dv_c, dq_s, dk_s, dv_s = step((dk_c, dv_c, dq_s, dk_s, dv_s), cross, up)
     state_back = dot_nt(dk_c, w_ck) + dot_nt(dv_c, w_cv)
     back = d_one + dot_nt(dq_s, w_sq) + dot_nt(dk_s, w_sk) + dot_nt(dv_s, w_sv)
     back, d_hidden, dq_c, dv_c = step((back, d_hidden, dq_c, dv_c), attn, cross, up)
@@ -841,7 +848,7 @@
     encoded_grad = halved(state_back.astype(bf16))
     dq_s, dv_s = step((dq_s, dv_s), attn)
     columns = [jnp.sum(v.astype(f32), axis=0) for v in (d_hidden, dq_c, dv_c, dq_s, dv_s)]
-    *columns, input_grad, encoded_grad = step((*columns, input_grad, encoded_grad), attn, cross)
+    *columns, input_grad, encoded_grad = step((*columns, input_grad, encoded_grad), attn, cross, up)
     sums = (
         columns[3],
         columns[4],

time: 634 us -> 635 us (level)
  local copies, waits for them, and re-layouts: 34.3 us -> 43.2 us
    unnamed x195 -> x219, local copies, waits for them, and re-layouts: 11.7 us -> 19.8 us
  transfers between devices with their start and end apart: 72 -> 72, of which waited for: 30 -> 31; matrix products, arithmetic and copies ran while one was open for 23% -> 23% of each run, Pallas kernels for 28% -> 27%
where the time goes in v8:
time: 635 us; the launch traced here: 625 us
  waiting for transfers between devices  183 us (29%)
  Pallas kernels  181 us (29%)
  starting transfers between devices  82.1 us (13%)
  other arithmetic  70 us (11%)
  matrix products  62.1 us (10%)
  local copies, waits for them, and re-layouts  43.2 us (7%)
    ppermute x32, waiting for transfers between devices, swap_data(): return lax.ppermute(value, ('rep', 'shard', 'mp'), pairs)  114 us
    pallas_call x7, Pallas kernels, weight_grad(): pl.pallas_call(functools.partial(weight_grad_body, count=count, outs=outs...  46.2 us
    pallas_call x4, Pallas kernels, place(): pl.pallas_call(functools.partial(place_body, dests=dests, many=many, two=...  38 us
    ppermute x32, starting transfers between devices, swap_data(): return lax.ppermute(value, ('rep', 'shard', 'mp'), pairs)  36.8 us
    dot_general x10, matrix products, dot_nt(): return lax.dot_general(a, b, NT, preferred_element_type=f32)  33.8 us
    pallas_call x2, Pallas kernels, attend_forward(): pl.pallas_call(functools.partial(attend_forward_body, causal=causal, rows...  29 us
    dot_general x9, matrix products, dot_nn(): return jnp.dot(a, b, preferred_element_type=f32)  28.3 us
    all_to_all x1, waiting for transfers between devices, first_pieces(): lax.all_to_all(cut.reshape(-1, net.rows, BS), 'shard', split_axis=0, conc...  27 us
  transfers between devices with their start and end apart: 72, of which 31 were waited for; matrix products, arithmetic and copies ran while one was open for 23% of the time, Pallas kernels for 27%

profile of v8, /device:TPU:0, one launch (start us, length us, event | category | flops | bytes accessed | tf_op | source)
XLA Modules:
  0.0 624.7 jit_solution(13449231050772475150)
XLA Ops:
  0.6 2.4 convert_element_type.363
  5.0 7.3 %all-to-all-start = ((bf16[136,16,256]{2,1,0:T(8,128)(2,1)}), bf16[136,16,256]{2,1,0:T(8,128)(2,1)S(1)}, u32[]{:S(2)}, u32[]{:S(2)}) async-start(bf16[136,16,256]{2,1,0:T(8,128)(2,1)} %bitcast.4), calls=%async_computation | async-start | bytes 2228224 | tf_op jit(solution)/shard_map/all_to_all | solution.py:271
  12.4 27.0 %all-to-all-done = bf16[136,16,256]{2,1,0:T(8,128)(2,1)S(1)} async-done(((bf16[136,16,256]{2,1,0:T(8,128)(2,1)}), bf16[136,16,256]{2,1,0:T(8,128)(2,1)S(1)}, u32[]{:S(2)}, u32[]{:S(2)}) %all-to-all-start) | async-done | bytes 1114144 | tf_op jit(solution)/shard_map/all_to_all | solution.py:271
  40.2 10.6 %collective-permute-done.2 = bf16[1,24,16,256]{3,2,1,0:T(8,128)(2,1)S(1)} collective-permute-done((bf16[1,24,16,256]{3,2,1,0:T(8,128)(2,1)S(1)}, bf16[1,24,16,256]{3,2,1,0:T(8,128)(2,1)S(1)}, u32[]{:S(2)}, u32[]{:S(2)}) %collective-permute-start.2) | collective-permute-done | bytes 196640 | tf_op jit(solution)/shard_map/ppermute | solution.py:105
  52.5 6.3 %collective-permute-done.3 = bf16[2,24,16,256]{3,2,1,0:T(8,128)(2,1)S(1)} collective-permute-done((bf16[2,24,16,256]{3,2,1,0:T(8,128)(2,1)S(1)}, bf16[2,24,16,256]{3,2,1,0:T(8,128)(2,1)S(1)}, u32[]{:S(2)}, u32[]{:S(2)}) %collective-permute-start.3) | collective-permute-done | bytes 393248 | tf_op jit(solution)/shard_map/ppermute | solution.py:105
  62.0 14.0 %collective-permute-done.5 = bf16[1,40,16,256]{3,2,1,0:T(8,128)(2,1)S(1)} collective-permute-done((bf16[1,40,16,256]{3,2,1,0:T(8,128)(2,1)S(1)}, bf16[1,40,16,256]{3,2,1,0:T(8,128)(2,1)S(1)}, u32[]{:S(2)}, u32[]{:S(2)}) %collective-permute-start.5) | collective-permute-done | bytes 327712 | tf_op jit(solution)/shard_map/ppermute | solution.py:105
  93.0 9.8 %collective-permute-done.8 = bf16[2,40,16,256]{3,2,1,0:T(8,128)(2,1)} collective-permute-done((bf16[2,40,16,256]{3,2,1,0:T(8,128)(2,1)}, bf16[2,40,16,256]{3,2,1,0:T(8,128)(2,1)}, u32[]{:S(2)}, u32[]{:S(2)}) %collective-permute-start.8) | collective-permute-done | bytes 655392 | tf_op jit(solution)/shard_map/ppermute | solution.py:105
  108.7 8.5 %place.4 = (bf16[4,256,1024]{2,1,0:T(8,128)(2,1)}, bf16[4,256,1024]{2,1,0:T(8,128)(2,1)}, bf16[4,256,1024]{2,1,0:T(8,128)(2,1)}) custom-call(s32[41]{0:T(128)} %add_add_fusion.4.s, bf16[8,24,16,256]{3,2,1,0:T(8,128)(2,1)} %copy-done.15, bf16[8,24,16,256]{3,2,1,0:T(8,128)(2,1)} %collective-permute-done.6.refs_1_, ...), custom_call_target="tpu_custom_call" | custom-call | flops 1048576 | bytes 1048576 | tf_op jit(solution)/shard_map/place/pallas_call | solution.py:227
  118.8 4.0 add_convert_fusion.7.v_ref
  136.7 20.1 %attend_forward.2 = (bf16[512,1024]{1,0:T(8,128)(2,1)}, f32[512,128]{1,0:T(8,128)}) custom-call(s32[1]{0:T(128)} %dynamic_slice.88.lim, bf16[512,1024]{1,0:T(8,128)(2,1)} %add_convert_fusion.8.q_ref, bf16[512,1024]{1,0:T(8,128)(2,1)} %convolution_convert_fusion.2.k_ref, bf16[512,1024]{1,0:T(8,128)(2,1)} %add_convert_fusion.7.v_ref), custom_call_target="tpu_custom_call" | custom-call | flops 1048576 | bytes 1048576 | tf_op jit(solution)/shard_map/attend_forward/pallas_call | solution.py:382
  160.1 3.4 collective-permute-done.17
  165.5 3.0 pad_maximum_fusion.1.refs_0_
  173.7 5.4 all-to-all-start.1
  179.1 10.3 %place.5 = (bf16[4,256,1024]{2,1,0:T(8,128)(2,1)}, bf16[4,256,1024]{2,1,0:T(8,128)(2,1)}, bf16[4,256,1024]{2,1,0:T(8,128)(2,1)}, bf16[4,256,1024]{2,1,0:T(8,128)(2,1)}, bf16[4,256,1024]{2,1,0:T(8,128)(2,1)}) custom-call(s32[41]{0:T(128)} %add_add_fusion.5.s, bf16[8,40,16,256]{3,2,1,0:T(8,128)(2,1)} %copy-done.5, ...), custom_call_target="tpu_custom_call" | custom-call | flops 1048576 | bytes 1048576 | tf_op jit(solution)/shard_map/place/pallas_call | solution.py:227
  189.4 3.5 fusion.23
  204.5 9.0 %attend_forward.3 = (bf16[512,1024]{1,0:T(8,128)(2,1)}, f32[512,128]{1,0:T(8,128)}) custom-call(s32[1]{0:T(128)} %dynamic_slice.88.lim, bf16[512,1024]{1,0:T(8,128)(2,1)} %add_convert_fusion.6.q_ref, bf16[128,1024]{1,0:T(8,128)(2,1)} %convolution_convert_fusion.3.k_ref, bf16[128,1024]{1,0:T(8,128)(2,1)} %fusion.4.v_ref), custom_call_target="tpu_custom_call" | custom-call | flops 1048576 | bytes 1048576 | tf_op jit(solution)/shard_map/attend_forward/pallas_call | solution.py:382
  213.5 3.4 fusion.26
  220.4 2.5 collective-permute-done.22
  222.9 2.9 pad_maximum_fusion.2.refs_0_
  229.9 4.7 all-to-all-start.2
  236.0 9.6 %place.6 = bf16[4,256,4096]{2,1,0:T(8,128)(2,1)} custom-call(s32[41]{0:T(128)} %add_add_fusion.6.s, bf16[8,32,16,256]{3,2,1,0:T(8,128)(2,1)} %pad_maximum_fusion.1.refs_0_, bf16[8,32,16,256]{3,2,1,0:T(8,128)(2,1)} %collective-permute-done.20.refs_1_, bf16[8,32,16,256]{3,2,1,0:T(8,128)(2,1)} %collective-permute-done.21.refs_2_, ...), custom_call_target="tpu_custom_call" | custom-call | flops 1048576 | bytes 1048576 | tf_op jit(solution)/shard_map/place/pallas_call | solution.py:227
  245.6 19.1 %gelu_forward.1 = (bf16[512,4096]{1,0:T(8,128)(2,1)}, bf16[512,4096]{1,0:T(8,128)(2,1)}) custom-call(bf16[512,1024]{1,0:T(8,128)(2,1)} %get-tuple-element.208.h_ref.x_own, bf16[1024,4096]{1,0:T(8,128)(2,1)} %bitcast.239, f32[1,4096]{1,0:T(1,128)} %bitcast.293), custom_call_target="tpu_custom_call" | custom-call | flops 1048576 | bytes 1048576 | tf_op jit(solution)/shard_map/gelu_forward/pallas_call | solution.py:515
  265.1 6.2 all-to-all-done.2
  274.2 9.6 %place.7 = bf16[16,256,1024]{2,1,0:T(8,128)(2,1)} custom-call(s32[41]{0:T(128)} %add_add_fusion.7.s, bf16[8,32,16,256]{3,2,1,0:T(8,128)(2,1)} %pad_maximum_fusion.2.refs_0_, bf16[8,32,16,256]{3,2,1,0:T(8,128)(2,1)} %collective-permute-done.24.refs_1_, bf16[8,32,16,256]{3,2,1,0:T(8,128)(2,1)} %collective-permute-done.25.refs_2_, ...), custom_call_target="tpu_custom_call" | custom-call | flops 1048576 | bytes 1048576 | tf_op jit(solution)/shard_map/place/pallas_call | solution.py:227
  283.8 8.3 %fusion.27 = f32[512,1024]{1,0:T(8,128)S(1)} fusion(bf16[512,4096]{1,0:T(8,128)(2,1)} %get-tuple-element.214.x_own, bf16[4096,1024]{1,0:T(8,128)(2,1)} %bitcast.242), kind=kOutput, calls=%fused_computation.236 | convolution fusion | flops 4294967296 | bytes 14680064 | tf_op jit(solution)/shard_map/dot_general | solution.py:43
  297.4 8.1 %multiply_convert_fusion.refs_0_ = bf16[512,4096]{1,0:T(8,128)(2,1)} fusion(bf16[512,4096]{1,0:T(8,128)(2,1)} %get-tuple-element.218, bf16[512,1024]{1,0:T(8,128)(2,1)S(1)} %convert_element_type.379.refs_0_, bf16[4096,1024]{1,0:T(8,128)(2,1)S(1)} %bitcast.245), kind=kOutput, calls=%fused_computation.6 | convolution fusion | flops 4301258752 | bytes 17825792 | tf_op jit(solution)/shard_map/dot_general | solution.py:47
  306.1 9.7 %weight_grad.7 = (bf16[8,1,32,16,256]{4,3,2,1,0:T(8,128)(2,1)}, bf16[8,1,32,16,256]{4,3,2,1,0:T(8,128)(2,1)}) custom-call(s32[41]{0:T(128)} %add_add_fusion.7.s, bf16[512,4096]{1,0:T(8,128)(2,1)} %get-tuple-element.214.x_own, bf16[512,4096]{1,0:T(8,128)(2,1)} %collective-permute-done.30.x_sib, bf16[512,1024]{1,0:T(8,128)(2,1)} %copy-done.30, ...), custom_call_target="tpu_custom_call" | custom-call | flops 1048576 | bytes 1048576 | tf_op jit(solution)/shard_map/weight_grad/pallas_call | solution.py:577
  315.9 11.1 %multiply_reduce_fusion.1 = (f32[1024]{0:T(1024)S(1)}, f32[512]{0:T(512)S(1)}, f32[512]{0:T(512)S(1)}, f32[1024]{0:T(1024)S(1)}, f32[512,1024]{1,0:T(8,128)S(1)}) fusion(f32[512,1024]{1,0:T(8,128)} %copy-done.3, f32[512]{0:T(512)S(1)} %add_rsqrt_fusion.1, f32[512]{0:T(512)S(1)} %broadcast_multiply_fusion.7, f32[1024]{0:T(1024)S(1)} %bitcast.301, ...), kind=kOutput, calls=%fused_computation.13 | convolution fusion | flops 4300207104 | bytes 18894848 | tf_op jit(solution)/shard_map/dot_general | solution.py:47
  335.2 9.6 %weight_grad.8 = (bf16[8,1,32,16,256]{4,3,2,1,0:T(8,128)(2,1)}, bf16[8,1,32,16,256]{4,3,2,1,0:T(8,128)(2,1)}) custom-call(s32[41]{0:T(128)} %add_add_fusion.6.s, bf16[512,1024]{1,0:T(8,128)(2,1)} %get-tuple-element.208.h_ref.x_own, bf16[512,1024]{1,0:T(8,128)(2,1)} %collective-permute-done.32.x_sib, bf16[512,4096]{1,0:T(8,128)(2,1)} %multiply_convert_fusion.refs_0_, ...), custom_call_target="tpu_custom_call" | custom-call | flops 1048576 | bytes 1048576 | tf_op jit(solution)/shard_map/weight_grad/pallas_call | solution.py:577
  344.9 4.3 add_convert_fusion.4
  351.4 4.7 all-to-all-start.3
  356.1 10.3 %attend_backward.2 = (bf16[512,1024]{1,0:T(8,128)(2,1)}, bf16[128,1024]{1,0:T(8,128)(2,1)}, bf16[128,1024]{1,0:T(8,128)(2,1)}) custom-call(s32[1]{0:T(128)} %dynamic_slice.88.lim, bf16[512,1024]{1,0:T(8,128)(2,1)} %add_convert_fusion.6.q_ref, bf16[128,1024]{1,0:T(8,128)(2,1)} %convolution_convert_fusion.3.k_ref, bf16[128,1024]{1,0:T(8,128)(2,1)} %fusion.4.v_ref, ...), custom_call_target="tpu_custom_call" | custom-call | flops 1048576 | bytes 1048576 | tf_op jit(solution)/shard_map/attend_backward/pallas_call | solution.py:465
  366.4 3.2 collective-permute-done.34
  369.6 4.4 multiply_reduce_fusion.2
  376.3 2.6 collective-permute-start.35
  383.5 3.0 gather_fusion.2
  386.5 5.2 all-to-all-start.4
  395.6 2.6 add_convert_fusion.13
  402.2 4.8 weight_grad.9
  407.0 4.6 weight_grad.10
  412.3 4.6 weight_grad.11
  416.9 4.8 weight_grad.12
  426.1 16.6 %attend_backward.3 = (bf16[512,1024]{1,0:T(8,128)(2,1)}, bf16[512,1024]{1,0:T(8,128)(2,1)}, bf16[512,1024]{1,0:T(8,128)(2,1)}) custom-call(s32[1]{0:T(128)} %dynamic_slice.88.lim, bf16[512,1024]{1,0:T(8,128)(2,1)} %add_convert_fusion.8.q_ref, bf16[512,1024]{1,0:T(8,128)(2,1)} %convolution_convert_fusion.2.k_ref, bf16[512,1024]{1,0:T(8,128)(2,1)} %add_convert_fusion.7.v_ref, ...), custom_call_target="tpu_custom_call" | custom-call | flops 1048576 | bytes 1048576 | tf_op jit(solution)/shard_map/attend_backward/pallas_call | solution.py:465
  443.5 2.4 collective-permute-start.61
  445.8 11.6 %collective-permute-done.45 = bf16[8,40,16,256]{3,2,1,0:T(8,128)(2,1)} collective-permute-done((bf16[8,40,16,256]{3,2,1,0:T(8,128)(2,1)}, bf16[8,40,16,256]{3,2,1,0:T(8,128)(2,1)}, u32[]{:S(2)}, u32[]{:S(2)}) %collective-permute-start.45) | collective-permute-done | bytes 2621472 | tf_op jit(solution)/shard_map/ppermute | solution.py:105
  457.4 3.6 add_convert_fusion
  461.8 3.2 add_convert_fusion.2
  470.0 8.1 %weight_grad.13 = (bf16[8,3,8,16,256]{4,3,2,1,0:T(8,128)(2,1)}, bf16[8,3,8,16,256]{4,3,2,1,0:T(8,128)(2,1)}) custom-call(s32[41]{0:T(128)} %add_add_fusion.5.s, bf16[512,1024]{1,0:T(8,128)(2,1)} %get-tuple-element.169.x_own, bf16[512,1024]{1,0:T(8,128)(2,1)} %get-tuple-element.268.x_sib, bf16[512,1024]{1,0:T(8,128)(2,1)} %get-tuple-element.290.refs_0_, ...), custom_call_target="tpu_custom_call" | custom-call | flops 1048576 | bytes 1048576 | tf_op jit(solution)/shard_map/weight_grad/pallas_call | solution.py:577
  478.7 11.1 %collective-permute-done.50 = bf16[4,32,16,256]{3,2,1,0:T(8,128)(2,1)} collective-permute-done((bf16[4,32,16,256]{3,2,1,0:T(8,128)(2,1)}, bf16[4,32,16,256]{3,2,1,0:T(8,128)(2,1)}, u32[]{:S(2)}, u32[]{:S(2)}) %collective-permute-start.50) | collective-permute-done | bytes 1048608 | tf_op jit(solution)/shard_map/ppermute | solution.py:105
  504.7 4.3 collective-permute-done.52
  509.1 2.7 collective-permute-start.59
  514.3 3.2 convert_reduce_fusion
  517.7 7.1 %collective-permute-done.54 = bf16[4,24,16,256]{3,2,1,0:T(8,128)(2,1)S(1)} collective-permute-done((bf16[4,24,16,256]{3,2,1,0:T(8,128)(2,1)S(1)}, bf16[4,24,16,256]{3,2,1,0:T(8,128)(2,1)S(1)}, u32[]{:S(2)}, u32[]{:S(2)}) %collective-permute-start.54) | collective-permute-done | bytes 786464 | tf_op jit(solution)/shard_map/ppermute | solution.py:105
  529.6 5.9 collective-permute-done.58
  535.5 8.2 %collective-permute-done.57 = bf16[2,24,16,256]{3,2,1,0:T(8,128)(2,1)S(1)} collective-permute-done((bf16[2,24,16,256]{3,2,1,0:T(8,128)(2,1)S(1)}, bf16[2,24,16,256]{3,2,1,0:T(8,128)(2,1)S(1)}, u32[]{:S(2)}, u32[]{:S(2)}) %collective-permute-start.57) | collective-permute-done | bytes 393248 | tf_op jit(solution)/shard_map/ppermute | solution.py:105
  547.4 9.1 %collective-permute-done.60 = bf16[1,24,16,256]{3,2,1,0:T(8,128)(2,1)S(1)} collective-permute-done((bf16[1,24,16,256]{3,2,1,0:T(8,128)(2,1)S(1)}, bf16[1,24,16,256]{3,2,1,0:T(8,128)(2,1)S(1)}, u32[]{:S(2)}, u32[]{:S(2)}) %collective-permute-start.60) | collective-permute-done | bytes 196640 | tf_op jit(solution)/shard_map/ppermute | solution.py:105
  558.2 5.6 all-to-all-start.5
  566.9 11.6 %all-to-all-done.5 = bf16[64,16,256]{2,1,0:T(8,128)(2,1)S(1)} async-done(((bf16[64,16,256]{2,1,0:T(8,128)(2,1)}), bf16[64,16,256]{2,1,0:T(8,128)(2,1)S(1)}, u32[]{:S(2)}, u32[]{:S(2)}) %all-to-all-start.5) | async-done | bytes 524320 | tf_op jit(solution)/shard_map/all_to_all | solution.py:327
  578.5 3.6 all-to-all-start.6
  582.2 13.5 %collective-permute-done.63.other_ref = bf16[8,8,16,256]{3,2,1,0:T(8,128)(2,1)S(1)} collective-permute-done((bf16[8,8,16,256]{3,2,1,0:T(8,128)(2,1)S(1)}, bf16[8,8,16,256]{3,2,1,0:T(8,128)(2,1)S(1)}, u32[]{:S(2)}, u32[]{:S(2)}) %collective-permute-start.63) | collective-permute-done | bytes 524320 | tf_op jit(solution)/shard_map/ppermute | solution.py:97
  595.7 2.5 all-to-all-done.6
  598.3 11.1 %shampoo.2 = (f32[1,16,256,256]{3,2,1,0:T(8,128)}, f32[1,16,256,256]{3,2,1,0:T(8,128)}, f32[1,16,256,256]{3,2,1,0:T(8,128)}, f32[1,16,256,256]{3,2,1,0:T(8,128)}) custom-call(s32[1]{0:T(128)} %bitcast.79.flag, bf16[8,8,16,256]{3,2,1,0:T(8,128)(2,1)} %bitcast.284, bf16[8,8,16,256]{3,2,1,0:T(8,128)(2,1)} %copy-done.62, f32[1,16,256,256]{3,2,1,0:T(8,128)} %w_ref.3, ...), custom_call_target="tpu_custom_call" | custom-call | flops 1048576 | bytes 1048576 | tf_op jit(solution)/shard_map/shampoo/pallas_call | solution.py:634
  609.4 2.6 collective-permute-done.64.other_ref
  613.4 10.9 %shampoo.3 = (f32[1,16,256,256]{3,2,1,0:T(8,128)}, f32[1,16,256,256]{3,2,1,0:T(8,128)}, f32[1,16,256,256]{3,2,1,0:T(8,128)}, f32[1,16,256,256]{3,2,1,0:T(8,128)}) custom-call(s32[1]{0:T(128)} %bitcast.79.flag, bf16[8,9,16,256]{3,2,1,0:T(8,128)(2,1)} %bitcast.276, ...), custom_call_target="tpu_custom_call", output_to_operand_aliasing={{0}: (8, {}), {1}: (9, {}), {2}: (10, {}), {3}: (11, {})} | custom-call | flops 1048576 | bytes 1048576 | tf_op jit(solution)/shard_map/shampoo/pallas_call | solution.py:634
  (496 shorter events, 154.9 us)
Async XLA Ops:
  5.0 34.5 %all-to-all-start = ((bf16[136,16,256]{2,1,0:T(8,128)(2,1)}), bf16[136,16,256]{2,1,0:T(8,128)(2,1)S(1)}, u32[]{:S(2)}, u32[]{:S(2)}) async-start(bf16[136,16,256]{2,1,0:T(8,128)(2,1)} %bitcast.4), calls=%async_computation | async-start | bytes 2228224 | tf_op jit(solution)/shard_map/all_to_all | solution.py:271
  40.1 10.7 %collective-permute-start.2 = (bf16[1,24,16,256]{3,2,1,0:T(8,128)(2,1)S(1)}, bf16[1,24,16,256]{3,2,1,0:T(8,128)(2,1)S(1)}, u32[]{:S(2)}, u32[]{:S(2)}) collective-permute-start(bf16[1,24,16,256]{3,2,1,0:T(8,128)(2,1)S(1)} %bitcast.270), channel_id=1, source_target_pairs={{0,8},{1,9},{2,10},{3,11},{4,12},{5,13},{6,14},{7,15},{8,0},{9,1},... | collective-permute-start | bytes 589832 | tf_op jit(solution)/shard_map/ppermute | solution.py:105
  50.9 7.8 %collective-permute-start.3 = (bf16[2,24,16,256]{3,2,1,0:T(8,128)(2,1)S(1)}, bf16[2,24,16,256]{3,2,1,0:T(8,128)(2,1)S(1)}, u32[]{:S(2)}, u32[]{:S(2)}) collective-permute-start(bf16[2,24,16,256]{3,2,1,0:T(8,128)(2,1)S(1)} %pad_maximum_fusion.19), channel_id=1, source_target_pairs={{0,16},{1,5},{2,18},{3,7},{4,20},{5,1},{6,22},{7,3},{8,24},{9,13},... | collective-permute-start | bytes 1179656 | tf_op jit(solution)/shard_map/ppermute | solution.py:105
  59.7 19.3 %collective-permute-start.4 = (bf16[4,24,16,256]{3,2,1,0:T(8,128)(2,1)}, bf16[4,24,16,256]{3,2,1,0:T(8,128)(2,1)}, u32[]{:S(2)}, u32[]{:S(2)}) collective-permute-start(bf16[4,24,16,256]{3,2,1,0:T(8,128)(2,1)} %pad_maximum_fusion.14), channel_id=1, source_target_pairs={{0,4},{1,3},{2,6},{3,1},{4,0},{5,7},{6,2},{7,5},{8,12},{9,11},{10,... | collective-permute-start | bytes 2359304 | tf_op jit(solution)/shard_map/ppermute | solution.py:105
  59.7 16.3 %collective-permute-start.5 = (bf16[1,40,16,256]{3,2,1,0:T(8,128)(2,1)S(1)}, bf16[1,40,16,256]{3,2,1,0:T(8,128)(2,1)S(1)}, u32[]{:S(2)}, u32[]{:S(2)}) collective-permute-start(bf16[1,40,16,256]{3,2,1,0:T(8,128)(2,1)S(1)} %bitcast.250), channel_id=1, source_target_pairs={{0,8},{1,9},{2,10},{3,11},{4,12},{5,13},{6,14},{7,15},{8,0},{9,1},... | collective-permute-start | bytes 983048 | tf_op jit(solution)/shard_map/ppermute | solution.py:105
  61.5 23.8 %collective-permute-start = (bf16[2,512,512]{2,1,0:T(8,128)(2,1)}, bf16[2,512,512]{2,1,0:T(8,128)(2,1)}, u32[]{:S(2)}, u32[]{:S(2)}) collective-permute-start(bf16[2,512,512]{2,1,0:T(8,128)(2,1)} %param.21), channel_id=1, source_target_pairs={{0,1},{1,0},{2,3},{3,2},{4,5},{5,4},{6,7},{7,6},{8,9},{9,8},{10,11... | collective-permute-start | bytes 3145736 | tf_op jit(solution)/shard_map/ppermute | solution.py:94
  61.5 21.0 %collective-permute-start.1 = (bf16[2,128,512]{2,1,0:T(8,128)(2,1)}, bf16[2,128,512]{2,1,0:T(8,128)(2,1)}, u32[]{:S(2)}, u32[]{:S(2)}) collective-permute-start(bf16[2,128,512]{2,1,0:T(8,128)(2,1)} %param.22), channel_id=1, source_target_pairs={{0,1},{1,0},{2,3},{3,2},{4,5},{5,4},{6,7},{7,6},{8,9},{9,8},{10,11... | collective-permute-start | bytes 786440 | tf_op jit(solution)/shard_map/ppermute | solution.py:94
  80.5 22.3 %collective-permute-start.6 = (bf16[8,24,16,256]{3,2,1,0:T(8,128)(2,1)S(1)}, bf16[8,24,16,256]{3,2,1,0:T(8,128)(2,1)}, u32[]{:S(2)}, u32[]{:S(2)}) collective-permute-start(bf16[8,24,16,256]{3,2,1,0:T(8,128)(2,1)S(1)} %pad_maximum_fusion.3.refs_0_), channel_id=1, source_target_pairs={{0,2},{1,17},{2,0},{3,19},{4,6},{5,21},{6,4},{7,23},{8,10},{9,25},... | collective-permute-start | bytes 4718600 | tf_op jit(solution)/shard_map/ppermute | solution.py:105
  81.8 21.0 %collective-permute-start.7 = (bf16[8,24,16,256]{3,2,1,0:T(8,128)(2,1)S(1)}, bf16[8,24,16,256]{3,2,1,0:T(8,128)(2,1)}, u32[]{:S(2)}, u32[]{:S(2)}) collective-permute-start(bf16[8,24,16,256]{3,2,1,0:T(8,128)(2,1)S(1)} %pad_maximum_fusion.3.refs_0_), channel_id=1, source_target_pairs={{0,1},{1,0},{2,3},{3,2},{4,5},{5,4},{6,7},{7,6},{8,9},{9,8},{10,11... | collective-permute-start | bytes 4718600 | tf_op jit(solution)/shard_map/ppermute | solution.py:94
  85.3 17.5 %collective-permute-start.8 = (bf16[2,40,16,256]{3,2,1,0:T(8,128)(2,1)}, bf16[2,40,16,256]{3,2,1,0:T(8,128)(2,1)}, u32[]{:S(2)}, u32[]{:S(2)}) collective-permute-start(bf16[2,40,16,256]{3,2,1,0:T(8,128)(2,1)} %pad_maximum_fusion.15), channel_id=1, source_target_pairs={{0,4},{1,5},{2,6},{3,7},{4,0},{5,1},{6,2},{7,3},{8,12},{9,13},{10,... | collective-permute-start | bytes 1966088 | tf_op jit(solution)/shard_map/ppermute | solution.py:105
  102.8 15.0 %collective-permute-start.10 = (bf16[1,32,16,256]{3,2,1,0:T(8,128)(2,1)S(1)}, bf16[1,32,16,256]{3,2,1,0:T(8,128)(2,1)S(1)}, u32[]{:S(2)}, u32[]{:S(2)}) collective-permute-start(bf16[1,32,16,256]{3,2,1,0:T(8,128)(2,1)S(1)} %bitcast.266), channel_id=1, source_target_pairs={{0,8},{1,9},{2,10},{3,11},{4,12},{5,13},{6,14},{7,15},{8,0},{9,1},... | collective-permute-start | bytes 786440 | tf_op jit(solution)/shard_map/ppermute | solution.py:105
  105.8 21.5 %collective-permute-start.12 = (bf16[4,40,16,256]{3,2,1,0:T(8,128)(2,1)}, bf16[4,40,16,256]{3,2,1,0:T(8,128)(2,1)}, u32[]{:S(2)}, u32[]{:S(2)}) collective-permute-start(bf16[4,40,16,256]{3,2,1,0:T(8,128)(2,1)} %pad_maximum_fusion.4), channel_id=1, source_target_pairs={{0,16},{1,3},{2,18},{3,1},{4,20},{5,7},{6,22},{7,5},{8,24},{9,11},... | collective-permute-start | bytes 3932168 | tf_op jit(solution)/shard_map/ppermute | solution.py:105
  117.8 10.8 %collective-permute-start.13 = (bf16[2,32,16,256]{3,2,1,0:T(8,128)(2,1)S(1)}, bf16[2,32,16,256]{3,2,1,0:T(8,128)(2,1)S(1)}, u32[]{:S(2)}, u32[]{:S(2)}) collective-permute-start(bf16[2,32,16,256]{3,2,1,0:T(8,128)(2,1)S(1)} %pad_maximum_fusion.17), channel_id=1, source_target_pairs={{0,2},{1,17},{2,0},{3,19},{4,6},{5,21},{6,4},{7,23},{8,10},{9,25},... | collective-permute-start | bytes 1572872 | tf_op jit(solution)/shard_map/ppermute | solution.py:105
  130.5 34.1 %collective-permute-start.14 = (bf16[8,40,16,256]{3,2,1,0:T(8,128)(2,1)S(1)}, bf16[8,40,16,256]{3,2,1,0:T(8,128)(2,1)}, u32[]{:S(2)}, u32[]{:S(2)}) collective-permute-start(bf16[8,40,16,256]{3,2,1,0:T(8,128)(2,1)S(1)} %pad_maximum_fusion.refs_0_), channel_id=1, source_target_pairs={{0,2},{1,17},{2,0},{3,19},{4,6},{5,21},{6,4},{7,23},{8,10},{9,25},... | collective-permute-start | bytes 7864328 | tf_op jit(solution)/shard_map/ppermute | solution.py:105
  132.0 32.6 %collective-permute-start.15 = (bf16[8,40,16,256]{3,2,1,0:T(8,128)(2,1)S(1)}, bf16[8,40,16,256]{3,2,1,0:T(8,128)(2,1)}, u32[]{:S(2)}, u32[]{:S(2)}) collective-permute-start(bf16[8,40,16,256]{3,2,1,0:T(8,128)(2,1)S(1)} %pad_maximum_fusion.refs_0_), channel_id=1, source_target_pairs={{0,1},{1,0},{2,3},{3,2},{4,5},{5,4},{6,7},{7,6},{8,9},{9,8},{10,11... | collective-permute-start | bytes 7864328 | tf_op jit(solution)/shard_map/ppermute | solution.py:94
  133.4 31.2 %collective-permute-start.16 = (bf16[4,32,16,256]{3,2,1,0:T(8,128)(2,1)}, bf16[4,32,16,256]{3,2,1,0:T(8,128)(2,1)}, u32[]{:S(2)}, u32[]{:S(2)}) collective-permute-start(bf16[4,32,16,256]{3,2,1,0:T(8,128)(2,1)} %pad_maximum_fusion.8), channel_id=1, source_target_pairs={{0,4},{1,5},{2,6},{3,7},{4,0},{5,1},{6,2},{7,3},{8,12},{9,13},{10,... | collective-permute-start | bytes 3145736 | tf_op jit(solution)/shard_map/ppermute | solution.py:105
  135.1 28.4 %collective-permute-start.17 = (bf16[1,32,16,256]{3,2,1,0:T(8,128)(2,1)S(1)}, bf16[1,32,16,256]{3,2,1,0:T(8,128)(2,1)}, u32[]{:S(2)}, u32[]{:S(2)}) collective-permute-start(bf16[1,32,16,256]{3,2,1,0:T(8,128)(2,1)S(1)} %bitcast.262), channel_id=1, source_target_pairs={{0,8},{1,9},{2,10},{3,11},{4,12},{5,13},{6,14},{7,15},{8,0},{9,1},... | collective-permute-start | bytes 786440 | tf_op jit(solution)/shard_map/ppermute | solution.py:105
  164.6 14.5 %collective-permute-start.18 = (bf16[8,40,16,256]{3,2,1,0:T(8,128)(2,1)}, bf16[8,40,16,256]{3,2,1,0:T(8,128)(2,1)}, u32[]{:S(2)}, u32[]{:S(2)}) collective-permute-start(bf16[8,40,16,256]{3,2,1,0:T(8,128)(2,1)} %collective-permute-done.14.refs_1_), channel_id=1, source_target_pairs={{0,1},{1,0},{2,3},{3,2},{4,5},{5,4},{6,7},{7,6},{8,9},{9,8},{10,11... | collective-permute-start | bytes 7864328 | tf_op jit(solution)/shard_map/ppermute | solution.py:94
  168.5 51.9 %collective-permute-start.20 = (bf16[8,32,16,256]{3,2,1,0:T(8,128)(2,1)}, bf16[8,32,16,256]{3,2,1,0:T(8,128)(2,1)}, u32[]{:S(2)}, u32[]{:S(2)}) collective-permute-start(bf16[8,32,16,256]{3,2,1,0:T(8,128)(2,1)} %pad_maximum_fusion.1.refs_0_), channel_id=1, source_target_pairs={{0,16},{1,3},{2,18},{3,1},{4,20},{5,7},{6,22},{7,5},{8,24},{9,11},... | collective-permute-start | bytes 6291464 | tf_op jit(solution)/shard_map/ppermute | solution.py:105
  170.0 50.4 %collective-permute-start.21 = (bf16[8,32,16,256]{3,2,1,0:T(8,128)(2,1)}, bf16[8,32,16,256]{3,2,1,0:T(8,128)(2,1)}, u32[]{:S(2)}, u32[]{:S(2)}) collective-permute-start(bf16[8,32,16,256]{3,2,1,0:T(8,128)(2,1)} %pad_maximum_fusion.1.refs_0_), channel_id=1, source_target_pairs={{0,1},{1,0},{2,3},{3,2},{4,5},{5,4},{6,7},{7,6},{8,9},{9,8},{10,11... | collective-permute-start | bytes 6291464 | tf_op jit(solution)/shard_map/ppermute | solution.py:94
  171.8 28.5 %collective-permute-start.19 = (bf16[2,32,16,256]{3,2,1,0:T(8,128)(2,1)}, bf16[2,32,16,256]{3,2,1,0:T(8,128)(2,1)}, u32[]{:S(2)}, u32[]{:S(2)}) collective-permute-start(bf16[2,32,16,256]{3,2,1,0:T(8,128)(2,1)} %pad_maximum_fusion.18), channel_id=1, source_target_pairs={{0,2},{1,17},{2,0},{3,19},{4,6},{5,21},{6,4},{7,23},{8,10},{9,25},... | collective-permute-start | bytes 1572872 | tf_op jit(solution)/shard_map/ppermute | solution.py:105
  173.7 46.7 %all-to-all-start.1 = ((bf16[2,16,32,512]{3,2,0,1:T(8,128)(2,1)}), bf16[2,16,32,512]{3,2,0,1:T(8,128)(2,1)S(1)}, u32[]{:S(2)}, u32[]{:S(2)}) async-start(bf16[2,16,32,512]{3,2,0,1:T(8,128)(2,1)} %copy.66), calls=%async_computation.1 | async-start | bytes 2097152 | tf_op jit(solution)/shard_map/all_to_all | solution.py:676
  202.5 20.4 %collective-permute-start.22 = (bf16[4,32,16,256]{3,2,1,0:T(8,128)(2,1)}, bf16[4,32,16,256]{3,2,1,0:T(8,128)(2,1)}, u32[]{:S(2)}, u32[]{:S(2)}) collective-permute-start(bf16[4,32,16,256]{3,2,1,0:T(8,128)(2,1)} %pad_maximum_fusion.9), channel_id=1, source_target_pairs={{0,16},{1,5},{2,18},{3,7},{4,20},{5,1},{6,22},{7,3},{8,24},{9,13},... | collective-permute-start | bytes 3145736 | tf_op jit(solution)/shard_map/ppermute | solution.py:105
  222.9 13.1 %collective-permute-start.23 = (bf16[8,32,16,256]{3,2,1,0:T(8,128)(2,1)}, bf16[8,32,16,256]{3,2,1,0:T(8,128)(2,1)}, u32[]{:S(2)}, u32[]{:S(2)}) collective-permute-start(bf16[8,32,16,256]{3,2,1,0:T(8,128)(2,1)} %collective-permute-done.20.refs_1_), channel_id=1, source_target_pairs={{0,1},{1,0},{2,3},{3,2},{4,5},{5,4},{6,7},{7,6},{8,9},{9,8},{10,11... | collective-permute-start | bytes 6291464 | tf_op jit(solution)/shard_map/ppermute | solution.py:94
  225.9 38.9 %collective-permute-start.24 = (bf16[8,32,16,256]{3,2,1,0:T(8,128)(2,1)}, bf16[8,32,16,256]{3,2,1,0:T(8,128)(2,1)}, u32[]{:S(2)}, u32[]{:S(2)}) collective-permute-start(bf16[8,32,16,256]{3,2,1,0:T(8,128)(2,1)} %pad_maximum_fusion.2.refs_0_), channel_id=1, source_target_pairs={{0,4},{1,3},{2,6},{3,1},{4,0},{5,7},{6,2},{7,5},{8,12},{9,11},{10,... | collective-permute-start | bytes 6291464 | tf_op jit(solution)/shard_map/ppermute | solution.py:105
  228.2 36.6 %collective-permute-start.25 = (bf16[8,32,16,256]{3,2,1,0:T(8,128)(2,1)}, bf16[8,32,16,256]{3,2,1,0:T(8,128)(2,1)}, u32[]{:S(2)}, u32[]{:S(2)}) collective-permute-start(bf16[8,32,16,256]{3,2,1,0:T(8,128)(2,1)} %pad_maximum_fusion.2.refs_0_), channel_id=1, source_target_pairs={{0,1},{1,0},{2,3},{3,2},{4,5},{5,4},{6,7},{7,6},{8,9},{9,8},{10,11... | collective-permute-start | bytes 6291464 | tf_op jit(solution)/shard_map/ppermute | solution.py:94
  229.9 41.4 %all-to-all-start.2 = ((bf16[32,1,32,512]{3,2,1,0:T(8,128)(2,1)}), bf16[32,1,32,512]{3,2,1,0:T(8,128)(2,1)S(1)}, u32[]{:S(2)}, u32[]{:S(2)}) async-start(bf16[32,1,32,512]{3,2,1,0:T(8,128)(2,1)} %bitcast.258), calls=%async_computation.2 | async-start | bytes 2097152 | tf_op jit(solution)/shard_map/all_to_all | solution.py:681
  264.8 9.4 %collective-permute-start.26 = (bf16[8,32,16,256]{3,2,1,0:T(8,128)(2,1)}, bf16[8,32,16,256]{3,2,1,0:T(8,128)(2,1)}, u32[]{:S(2)}, u32[]{:S(2)}) collective-permute-start(bf16[8,32,16,256]{3,2,1,0:T(8,128)(2,1)} %collective-permute-done.24.refs_1_), channel_id=1, source_target_pairs={{0,1},{1,0},{2,3},{3,2},{4,5},{5,4},{6,7},{7,6},{8,9},{9,8},{10,11... | collective-permute-start | bytes 6291464 | tf_op jit(solution)/shard_map/ppermute | solution.py:94
  272.8 33.2 %collective-permute-start.30 = (bf16[512,4096]{1,0:T(8,128)(2,1)}, bf16[512,4096]{1,0:T(8,128)(2,1)}, u32[]{:S(2)}, u32[]{:S(2)}) collective-permute-start(bf16[512,4096]{1,0:T(8,128)(2,1)} %get-tuple-element.214.x_own), channel_id=1, source_target_pairs={{0,1},{1,0},{2,3},{3,2},{4,5},{5,4},{6,7},{7,6},{8,9},{9,8},{10,11... | collective-permute-start | bytes 12582920 | tf_op jit(solution)/shard_map/ppermute | solution.py:94
  297.3 8.2 %collective-permute-start.28 = (bf16[512,1024]{1,0:T(8,128)(2,1)S(1)}, bf16[512,1024]{1,0:T(8,128)(2,1)}, u32[]{:S(2)}, u32[]{:S(2)}) collective-permute-start(bf16[512,1024]{1,0:T(8,128)(2,1)S(1)} %convert_element_type.379.refs_0_), channel_id=1, source_target_pairs={{0,1},{1,0},{2,3},{3,2},{4,5},{5,4},{6,7},{7,6},{8,9},{9,8},{10,11... | collective-permute-start | bytes 3145736 | tf_op jit(solution)/shard_map/ppermute | solution.py:94
  305.5 10.2 %collective-permute-start.29 = (bf16[512,4096]{1,0:T(8,128)(2,1)}, bf16[512,4096]{1,0:T(8,128)(2,1)}, u32[]{:S(2)}, u32[]{:S(2)}) collective-permute-start(bf16[512,4096]{1,0:T(8,128)(2,1)} %multiply_convert_fusion.refs_0_), channel_id=1, source_target_pairs={{0,1},{1,0},{2,3},{3,2},{4,5},{5,4},{6,7},{7,6},{8,9},{9,8},{10,11... | collective-permute-start | bytes 12582920 | tf_op jit(solution)/shard_map/ppermute | solution.py:94
  305.6 29.6 %collective-permute-start.32 = (bf16[512,1024]{1,0:T(8,128)(2,1)S(1)}, bf16[512,1024]{1,0:T(8,128)(2,1)}, u32[]{:S(2)}, u32[]{:S(2)}) collective-permute-start(bf16[512,1024]{1,0:T(8,128)(2,1)S(1)} %copy-done.7), channel_id=1, source_target_pairs={{0,1},{1,0},{2,3},{3,2},{4,5},{5,4},{6,7},{7,6},{8,9},{9,8},{10,11... | collective-permute-start | bytes 3145736 | tf_op jit(solution)/shard_map/ppermute | solution.py:94
  315.8 29.0 %collective-permute-start.33 = (bf16[8,32,16,256]{3,2,1,0:T(8,128)(2,1)}, bf16[8,32,16,256]{3,2,1,0:T(8,128)(2,1)}, u32[]{:S(2)}, u32[]{:S(2)}) collective-permute-start(bf16[8,32,16,256]{3,2,1,0:T(8,128)(2,1)} %bitcast.324), channel_id=1, source_target_pairs={{0,4},{1,3},{2,6},{3,1},{4,0},{5,7},{6,2},{7,5},{8,12},{9,11},{10,... | collective-permute-start | bytes 6291464 | tf_op jit(solution)/shard_map/ppermute | solution.py:105
  327.0 6.8 %collective-permute-start.31 = (bf16[512,512]{1,0:T(8,128)(2,1)S(1)}, bf16[512,512]{1,0:T(8,128)(2,1)S(1)}, u32[]{:S(2)}, u32[]{:S(2)}) collective-permute-start(bf16[512,512]{1,0:T(8,128)(2,1)S(1)} %constant_dynamic-slice_fusion.2), channel_id=1, source_target_pairs={{0,1},{1,0},{2,3},{3,2},{4,5},{5,4},{6,7},{7,6},{8,9},{9,8},{10,11... | collective-permute-start | bytes 1572872 | tf_op jit(solution)/shard_map/ppermute | solution.py:94
  349.1 20.5 %collective-permute-start.34 = (bf16[4,32,16,256]{3,2,1,0:T(8,128)(2,1)}, bf16[4,32,16,256]{3,2,1,0:T(8,128)(2,1)}, u32[]{:S(2)}, u32[]{:S(2)}) collective-permute-start(bf16[4,32,16,256]{3,2,1,0:T(8,128)(2,1)} %get-tuple-element.353), channel_id=1, source_target_pairs={{0,16},{1,5},{2,18},{3,7},{4,20},{5,1},{6,22},{7,3},{8,24},{9,13},... | collective-permute-start | bytes 3145736 | tf_op jit(solution)/shard_map/ppermute | solution.py:105
  351.4 30.8 %all-to-all-start.3 = ((bf16[2,16,32,512]{3,2,0,1:T(8,128)(2,1)}), bf16[2,16,32,512]{3,2,0,1:T(8,128)(2,1)S(1)}, u32[]{:S(2)}, u32[]{:S(2)}) async-start(bf16[2,16,32,512]{3,2,0,1:T(8,128)(2,1)} %copy.69), calls=%async_computation.3 | async-start | bytes 2097152 | tf_op jit(solution)/shard_map/all_to_all | solution.py:676
  379.0 13.4 %collective-permute-start.42 = (bf16[512,1024]{1,0:T(8,128)(2,1)}, bf16[512,1024]{1,0:T(8,128)(2,1)}, u32[]{:S(2)}, u32[]{:S(2)}) collective-permute-start(bf16[512,1024]{1,0:T(8,128)(2,1)} %get-tuple-element.191.x_own.o_ref), channel_id=1, source_target_pairs={{0,1},{1,0},{2,3},{3,2},{4,5},{5,4},{6,7},{7,6},{8,9},{9,8},{10,11... | collective-permute-start | bytes 3145736 | tf_op jit(solution)/shard_map/ppermute | solution.py:94
  379.1 45.6 %collective-permute-start.43 = (bf16[8,32,16,256]{3,2,1,0:T(8,128)(2,1)}, bf16[8,32,16,256]{3,2,1,0:T(8,128)(2,1)}, u32[]{:S(2)}, u32[]{:S(2)}) collective-permute-start(bf16[8,32,16,256]{3,2,1,0:T(8,128)(2,1)} %bitcast.61), channel_id=1, source_target_pairs={{0,16},{1,3},{2,18},{3,1},{4,20},{5,7},{6,22},{7,5},{8,24},{9,11},... | collective-permute-start | bytes 6291464 | tf_op jit(solution)/shard_map/ppermute | solution.py:105
  386.5 35.8 %all-to-all-start.4 = ((bf16[32,1,32,512]{3,2,1,0:T(8,128)(2,1)}), bf16[32,1,32,512]{3,2,1,0:T(8,128)(2,1)}, u32[]{:S(2)}, u32[]{:S(2)}) async-start(bf16[32,1,32,512]{3,2,1,0:T(8,128)(2,1)} %bitcast.256), calls=%async_computation.4 | async-start | bytes 2097152 | tf_op jit(solution)/shard_map/all_to_all | solution.py:681
  391.9 9.4 %collective-permute-start.41 = (bf16[512,1024]{1,0:T(8,128)(2,1)S(1)}, bf16[512,1024]{1,0:T(8,128)(2,1)S(1)}, u32[]{:S(2)}, u32[]{:S(2)}) collective-permute-start(bf16[512,1024]{1,0:T(8,128)(2,1)S(1)} %copy-done.21), channel_id=1, source_target_pairs={{0,1},{1,0},{2,3},{3,2},{4,5},{5,4},{6,7},{7,6},{8,9},{9,8},{10,11... | collective-permute-start | bytes 3145736 | tf_op jit(solution)/shard_map/ppermute | solution.py:94
  392.4 24.5 %collective-permute-start.36 = (bf16[512,1024]{1,0:T(8,128)(2,1)}, bf16[512,1024]{1,0:T(8,128)(2,1)}, u32[]{:S(2)}, u32[]{:S(2)}) collective-permute-start(bf16[512,1024]{1,0:T(8,128)(2,1)} %get-tuple-element.203.o_ref.x_own), channel_id=1, source_target_pairs={{0,1},{1,0},{2,3},{3,2},{4,5},{5,4},{6,7},{7,6},{8,9},{9,8},{10,11... | collective-permute-start | bytes 3145736 | tf_op jit(solution)/shard_map/ppermute | solution.py:94
  392.4 24.4 %collective-permute-start.37 = (bf16[512,1024]{1,0:T(8,128)(2,1)S(1)}, bf16[512,1024]{1,0:T(8,128)(2,1)}, u32[]{:S(2)}, u32[]{:S(2)}) collective-permute-start(bf16[512,1024]{1,0:T(8,128)(2,1)S(1)} %copy-done.17), channel_id=1, source_target_pairs={{0,1},{1,0},{2,3},{3,2},{4,5},{5,4},{6,7},{7,6},{8,9},{9,8},{10,11... | collective-permute-start | bytes 3145736 | tf_op jit(solution)/shard_map/ppermute | solution.py:94
  399.4 25.3 %collective-permute-start.44 = (bf16[2,32,16,256]{3,2,1,0:T(8,128)(2,1)S(1)}, bf16[2,32,16,256]{3,2,1,0:T(8,128)(2,1)S(1)}, u32[]{:S(2)}, u32[]{:S(2)}) collective-permute-start(bf16[2,32,16,256]{3,2,1,0:T(8,128)(2,1)S(1)} %get-tuple-element.360), channel_id=1, source_target_pairs={{0,2},{1,17},{2,0},{3,19},{4,6},{5,21},{6,4},{7,23},{8,10},{9,25},... | collective-permute-start | bytes 1572872 | tf_op jit(solution)/shard_map/ppermute | solution.py:105
  402.2 9.4 %collective-permute-start.39 = (bf16[128,1024]{1,0:T(8,128)(2,1)S(1)}, bf16[128,1024]{1,0:T(8,128)(2,1)S(1)}, u32[]{:S(2)}, u32[]{:S(2)}) collective-permute-start(bf16[128,1024]{1,0:T(8,128)(2,1)S(1)} %copy-done.41), channel_id=1, source_target_pairs={{0,1},{1,0},{2,3},{3,2},{4,5},{5,4},{6,7},{7,6},{8,9},{9,8},{10,11... | collective-permute-start | bytes 786440 | tf_op jit(solution)/shard_map/ppermute | solution.py:94
  425.5 32.0 %collective-permute-start.45 = (bf16[8,40,16,256]{3,2,1,0:T(8,128)(2,1)}, bf16[8,40,16,256]{3,2,1,0:T(8,128)(2,1)}, u32[]{:S(2)}, u32[]{:S(2)}) collective-permute-start(bf16[8,40,16,256]{3,2,1,0:T(8,128)(2,1)} %bitcast.241), channel_id=1, source_target_pairs={{0,2},{1,17},{2,0},{3,19},{4,6},{5,21},{6,4},{7,23},{8,10},{9,25},... | collective-permute-start | bytes 7864328 | tf_op jit(solution)/shard_map/ppermute | solution.py:105
  442.7 27.2 %collective-permute-start.46 = (bf16[512,1024]{1,0:T(8,128)(2,1)}, bf16[512,1024]{1,0:T(8,128)(2,1)}, u32[]{:S(2)}, u32[]{:S(2)}) collective-permute-start(bf16[512,1024]{1,0:T(8,128)(2,1)} %get-tuple-element.290.refs_0_), channel_id=1, source_target_pairs={{0,1},{1,0},{2,3},{3,2},{4,5},{5,4},{6,7},{7,6},{8,9},{9,8},{10,11... | collective-permute-start | bytes 3145736 | tf_op jit(solution)/shard_map/ppermute | solution.py:94
  442.8 27.1 %collective-permute-start.47 = (bf16[512,1024]{1,0:T(8,128)(2,1)}, bf16[512,1024]{1,0:T(8,128)(2,1)}, u32[]{:S(2)}, u32[]{:S(2)}) collective-permute-start(bf16[512,1024]{1,0:T(8,128)(2,1)} %get-tuple-element.279.refs_1_), channel_id=1, source_target_pairs={{0,1},{1,0},{2,3},{3,2},{4,5},{5,4},{6,7},{7,6},{8,9},{9,8},{10,11... | collective-permute-start | bytes 3145736 | tf_op jit(solution)/shard_map/ppermute | solution.py:94
  443.3 26.7 %collective-permute-start.48 = (bf16[512,1024]{1,0:T(8,128)(2,1)}, bf16[512,1024]{1,0:T(8,128)(2,1)}, u32[]{:S(2)}, u32[]{:S(2)}) collective-permute-start(bf16[512,1024]{1,0:T(8,128)(2,1)} %get-tuple-element.291.refs_2_), channel_id=1, source_target_pairs={{0,1},{1,0},{2,3},{3,2},{4,5},{5,4},{6,7},{7,6},{8,9},{9,8},{10,11... | collective-permute-start | bytes 3145736 | tf_op jit(solution)/shard_map/ppermute | solution.py:94
  443.5 21.6 %collective-permute-start.61 = (bf16[1,32,16,256]{3,2,1,0:T(8,128)(2,1)S(1)}, bf16[1,32,16,256]{3,2,1,0:T(8,128)(2,1)S(1)}, u32[]{:S(2)}, u32[]{:S(2)}) collective-permute-start(bf16[1,32,16,256]{3,2,1,0:T(8,128)(2,1)S(1)} %add_convert_fusion.23), channel_id=1, source_target_pairs={{0,8},{1,9},{2,10},{3,11},{4,12},{5,13},{6,14},{7,15},{8,0},{9,1},... | collective-permute-start | bytes 786440 | tf_op jit(solution)/shard_map/ppermute | solution.py:105
  461.0 28.8 %collective-permute-start.49 = (bf16[4,40,16,256]{3,2,1,0:T(8,128)(2,1)}, bf16[4,40,16,256]{3,2,1,0:T(8,128)(2,1)}, u32[]{:S(2)}, u32[]{:S(2)}) collective-permute-start(bf16[4,40,16,256]{3,2,1,0:T(8,128)(2,1)} %get-tuple-element.349), channel_id=1, source_target_pairs={{0,16},{1,3},{2,18},{3,1},{4,20},{5,7},{6,22},{7,5},{8,24},{9,11},... | collective-permute-start | bytes 3932168 | tf_op jit(solution)/shard_map/ppermute | solution.py:105
  465.7 24.1 %collective-permute-start.50 = (bf16[4,32,16,256]{3,2,1,0:T(8,128)(2,1)}, bf16[4,32,16,256]{3,2,1,0:T(8,128)(2,1)}, u32[]{:S(2)}, u32[]{:S(2)}) collective-permute-start(bf16[4,32,16,256]{3,2,1,0:T(8,128)(2,1)} %get-tuple-element.351), channel_id=1, source_target_pairs={{0,4},{1,5},{2,6},{3,7},{4,0},{5,1},{6,2},{7,3},{8,12},{9,13},{10,... | collective-permute-start | bytes 3145736 | tf_op jit(solution)/shard_map/ppermute | solution.py:105
  478.1 26.6 %collective-permute-start.51 = (bf16[8,24,16,256]{3,2,1,0:T(8,128)(2,1)}, bf16[8,24,16,256]{3,2,1,0:T(8,128)(2,1)S(1)}, u32[]{:S(2)}, u32[]{:S(2)}) collective-permute-start(bf16[8,24,16,256]{3,2,1,0:T(8,128)(2,1)} %bitcast.325), channel_id=1, source_target_pairs={{0,2},{1,17},{2,0},{3,19},{4,6},{5,21},{6,4},{7,23},{8,10},{9,25},... | collective-permute-start | bytes 4718600 | tf_op jit(solution)/shard_map/ppermute | solution.py:105
  491.4 13.3 %collective-permute-start.53 = (bf16[2,32,16,256]{3,2,1,0:T(8,128)(2,1)S(1)}, bf16[2,32,16,256]{3,2,1,0:T(8,128)(2,1)S(1)}, u32[]{:S(2)}, u32[]{:S(2)}) collective-permute-start(bf16[2,32,16,256]{3,2,1,0:T(8,128)(2,1)S(1)} %get-tuple-element.362), channel_id=1, source_target_pairs={{0,2},{1,17},{2,0},{3,19},{4,6},{5,21},{6,4},{7,23},{8,10},{9,25},... | collective-permute-start | bytes 1572872 | tf_op jit(solution)/shard_map/ppermute | solution.py:105
  494.3 14.7 %collective-permute-start.52 = (bf16[2,40,16,256]{3,2,1,0:T(8,128)(2,1)S(1)}, bf16[2,40,16,256]{3,2,1,0:T(8,128)(2,1)S(1)}, u32[]{:S(2)}, u32[]{:S(2)}) collective-permute-start(bf16[2,40,16,256]{3,2,1,0:T(8,128)(2,1)S(1)} %get-tuple-element.357), channel_id=1, source_target_pairs={{0,4},{1,5},{2,6},{3,7},{4,0},{5,1},{6,2},{7,3},{8,12},{9,13},{10,... | collective-permute-start | bytes 1966088 | tf_op jit(solution)/shard_map/ppermute | solution.py:105
  497.7 6.2 collective-permute-start.56
  509.1 20.6 %collective-permute-start.59 = (bf16[1,32,16,256]{3,2,1,0:T(8,128)(2,1)S(1)}, bf16[1,32,16,256]{3,2,1,0:T(8,128)(2,1)S(1)}, u32[]{:S(2)}, u32[]{:S(2)}) collective-permute-start(bf16[1,32,16,256]{3,2,1,0:T(8,128)(2,1)S(1)} %add_convert_fusion.27), channel_id=1, source_target_pairs={{0,8},{1,9},{2,10},{3,11},{4,12},{5,13},{6,14},{7,15},{8,0},{9,1},... | collective-permute-start | bytes 786440 | tf_op jit(solution)/shard_map/ppermute | solution.py:105
  511.9 23.6 %collective-permute-start.58 = (bf16[1,40,16,256]{3,2,1,0:T(8,128)(2,1)S(1)}, bf16[1,40,16,256]{3,2,1,0:T(8,128)(2,1)}, u32[]{:S(2)}, u32[]{:S(2)}) collective-permute-start(bf16[1,40,16,256]{3,2,1,0:T(8,128)(2,1)S(1)} %add_convert_fusion.21), channel_id=1, source_target_pairs={{0,8},{1,9},{2,10},{3,11},{4,12},{5,13},{6,14},{7,15},{8,0},{9,1},... | collective-permute-start | bytes 983048 | tf_op jit(solution)/shard_map/ppermute | solution.py:105
  512.7 12.1 %collective-permute-start.54 = (bf16[4,24,16,256]{3,2,1,0:T(8,128)(2,1)S(1)}, bf16[4,24,16,256]{3,2,1,0:T(8,128)(2,1)S(1)}, u32[]{:S(2)}, u32[]{:S(2)}) collective-permute-start(bf16[4,24,16,256]{3,2,1,0:T(8,128)(2,1)S(1)} %get-tuple-element.355), channel_id=1, source_target_pairs={{0,16},{1,3},{2,18},{3,1},{4,20},{5,7},{6,22},{7,5},{8,24},{9,11},... | collective-permute-start | bytes 2359304 | tf_op jit(solution)/shard_map/ppermute | solution.py:105
  525.0 18.7 %collective-permute-start.57 = (bf16[2,24,16,256]{3,2,1,0:T(8,128)(2,1)S(1)}, bf16[2,24,16,256]{3,2,1,0:T(8,128)(2,1)S(1)}, u32[]{:S(2)}, u32[]{:S(2)}) collective-permute-start(bf16[2,24,16,256]{3,2,1,0:T(8,128)(2,1)S(1)} %get-tuple-element.370), channel_id=1, source_target_pairs={{0,4},{1,5},{2,6},{3,7},{4,0},{5,1},{6,2},{7,3},{8,12},{9,13},{10,... | collective-permute-start | bytes 1179656 | tf_op jit(solution)/shard_map/ppermute | solution.py:105
  544.5 12.0 %collective-permute-start.60 = (bf16[1,24,16,256]{3,2,1,0:T(8,128)(2,1)S(1)}, bf16[1,24,16,256]{3,2,1,0:T(8,128)(2,1)S(1)}, u32[]{:S(2)}, u32[]{:S(2)}) collective-permute-start(bf16[1,24,16,256]{3,2,1,0:T(8,128)(2,1)S(1)} %add_convert_fusion.29), channel_id=1, source_target_pairs={{0,8},{1,9},{2,10},{3,11},{4,12},{5,13},{6,14},{7,15},{8,0},{9,1},... | collective-permute-start | bytes 589832 | tf_op jit(solution)/shard_map/ppermute | solution.py:105
  558.2 20.3 %all-to-all-start.5 = ((bf16[64,16,256]{2,1,0:T(8,128)(2,1)}), bf16[64,16,256]{2,1,0:T(8,128)(2,1)S(1)}, u32[]{:S(2)}, u32[]{:S(2)}) async-start(bf16[64,16,256]{2,1,0:T(8,128)(2,1)} %gather_fusion.3), calls=%async_computation.5 | async-start | bytes 1048576 | tf_op jit(solution)/shard_map/all_to_all | solution.py:327
  578.5 19.7 %all-to-all-start.6 = ((bf16[72,16,256]{2,1,0:T(8,128)(2,1)}), bf16[72,16,256]{2,1,0:T(8,128)(2,1)S(1)}, u32[]{:S(2)}, u32[]{:S(2)}) async-start(bf16[72,16,256]{2,1,0:T(8,128)(2,1)} %bitcast.88), calls=%async_computation.6 | async-start | bytes 1179648 | tf_op jit(solution)/shard_map/all_to_all | solution.py:327
  582.1 13.6 %collective-permute-start.63 = (bf16[8,8,16,256]{3,2,1,0:T(8,128)(2,1)S(1)}, bf16[8,8,16,256]{3,2,1,0:T(8,128)(2,1)S(1)}, u32[]{:S(2)}, u32[]{:S(2)}) collective-permute-start(bf16[8,8,16,256]{3,2,1,0:T(8,128)(2,1)S(1)} %bitcast.283), channel_id=1, source_target_pairs={{0,16},{16,0},{1,17},{17,1},{2,18},{18,2},{3,19},{19,3},{4,20},{20... | collective-permute-start | bytes 1572872 | tf_op jit(solution)/shard_map/ppermute | solution.py:97
  598.2 13.8 %collective-permute-start.64 = (bf16[8,9,16,256]{3,2,1,0:T(8,128)(2,1)S(1)}, bf16[8,9,16,256]{3,2,1,0:T(8,128)(2,1)S(1)}, u32[]{:S(2)}, u32[]{:S(2)}) collective-permute-start(bf16[8,9,16,256]{3,2,1,0:T(8,128)(2,1)S(1)} %bitcast.274), channel_id=1, source_target_pairs={{0,16},{16,0},{1,17},{17,1},{2,18},{18,2},{3,19},{19,3},{4,20},{20... | collective-permute-start | bytes 1769480 | tf_op jit(solution)/shard_map/ppermute | solution.py:97
  (101 other events, 814.3 us)

commit v9 on v8

--- a/solution.py
+++ b/solution.py
@@ -837,7 +837,7 @@
     outputs, d_os = step((outputs, d_os), cross, up, down)
     dq_s, dk_s, dv_s = attend_backward(limit, q_s, k_s, v_s, o_s, d_os, lse_s, True)
     sibs = [net.swap_core(v) for v in (dq_s, dk_s, dv_s)]
-    dq_s, dk_s, dv_s = step((dq_s, dk_s, dv_s), cross)
+    dq_s, dk_s, dv_s = step((dq_s, dk_s, dv_s), cross, up)
     attn = gradient(0, ((x, x_sib), *zip((dq_s, dk_s, dv_s), sibs)))
     dq_s, dk_s, dv_s = step((dq_s, dk_s, dv_s), attn)
     dk_c, dv_c, dq_s, dk_s, dv_s = step((dk_c, dv_c, dq_s, dk_s, dv_s), cross, up)

time: 635 us -> 630 us (level)
  waiting for transfers between devices: 183 us -> 175 us
    unnamed x219 -> x215, local copies, waits for them, and re-layouts: 19.8 us -> 19.9 us
  transfers between devices with their start and end apart: 72 -> 72, of which waited for: 31 -> 31; matrix products, arithmetic and copies ran while one was open for 23% -> 22% of each run, Pallas kernels for 27% -> 27%
where the time goes in v9:
time: 630 us; the launch traced here: 619 us
  Pallas kernels  181 us (29%)
  waiting for transfers between devices  175 us (28%)
  starting transfers between devices  82.6 us (13%)
  other arithmetic  73.1 us (12%)
  matrix products  62 us (10%)
  local copies, waits for them, and re-layouts  42.7 us (7%)
    ppermute x32, waiting for transfers between devices, swap_data(): return lax.ppermute(value, ('rep', 'shard', 'mp'), pairs)  108 us
    pallas_call x7, Pallas kernels, weight_grad(): pl.pallas_call(functools.partial(weight_grad_body, count=count, outs=outs...  46.3 us
    pallas_call x4, Pallas kernels, place(): pl.pallas_call(functools.partial(place_body, dests=dests, many=many, two=...  38 us
    ppermute x32, starting transfers between devices, swap_data(): return lax.ppermute(value, ('rep', 'shard', 'mp'), pairs)  37.1 us
    dot_general x10, matrix products, dot_nt(): return lax.dot_general(a, b, NT, preferred_element_type=f32)  33.8 us
    pallas_call x2, Pallas kernels, attend_forward(): pl.pallas_call(functools.partial(attend_forward_body, causal=causal, rows...  29 us
    dot_general x9, matrix products, dot_nn(): return jnp.dot(a, b, preferred_element_type=f32)  28.3 us
    all_to_all x1, waiting for transfers between devices, first_pieces(): lax.all_to_all(cut.reshape(-1, net.rows, BS), 'shard', split_axis=0, conc...  27 us
  transfers between devices with their start and end apart: 72, of which 31 were waited for; matrix products, arithmetic and copies ran while one was open for 22% of the time, Pallas kernels for 27%

profile of v9, /device:TPU:0, one launch (start us, length us, event | category | flops | bytes accessed | tf_op | source)
XLA Modules:
  0.0 618.8 jit_solution(4897618729925264243)
XLA Ops:
  0.6 2.4 convert_element_type.363
  5.0 7.3 %all-to-all-start = ((bf16[136,16,256]{2,1,0:T(8,128)(2,1)}), bf16[136,16,256]{2,1,0:T(8,128)(2,1)S(1)}, u32[]{:S(2)}, u32[]{:S(2)}) async-start(bf16[136,16,256]{2,1,0:T(8,128)(2,1)} %bitcast.4), calls=%async_computation | async-start | bytes 2228224 | tf_op jit(solution)/shard_map/all_to_all | solution.py:271
  12.4 27.0 %all-to-all-done = bf16[136,16,256]{2,1,0:T(8,128)(2,1)S(1)} async-done(((bf16[136,16,256]{2,1,0:T(8,128)(2,1)}), bf16[136,16,256]{2,1,0:T(8,128)(2,1)S(1)}, u32[]{:S(2)}, u32[]{:S(2)}) %all-to-all-start) | async-done | bytes 1114144 | tf_op jit(solution)/shard_map/all_to_all | solution.py:271
  40.2 10.6 %collective-permute-done.2 = bf16[1,24,16,256]{3,2,1,0:T(8,128)(2,1)S(1)} collective-permute-done((bf16[1,24,16,256]{3,2,1,0:T(8,128)(2,1)S(1)}, bf16[1,24,16,256]{3,2,1,0:T(8,128)(2,1)S(1)}, u32[]{:S(2)}, u32[]{:S(2)}) %collective-permute-start.2) | collective-permute-done | bytes 196640 | tf_op jit(solution)/shard_map/ppermute | solution.py:105
  52.5 6.3 %collective-permute-done.3 = bf16[2,24,16,256]{3,2,1,0:T(8,128)(2,1)S(1)} collective-permute-done((bf16[2,24,16,256]{3,2,1,0:T(8,128)(2,1)S(1)}, bf16[2,24,16,256]{3,2,1,0:T(8,128)(2,1)S(1)}, u32[]{:S(2)}, u32[]{:S(2)}) %collective-permute-start.3) | collective-permute-done | bytes 393248 | tf_op jit(solution)/shard_map/ppermute | solution.py:105
  62.0 14.0 %collective-permute-done.5 = bf16[1,40,16,256]{3,2,1,0:T(8,128)(2,1)S(1)} collective-permute-done((bf16[1,40,16,256]{3,2,1,0:T(8,128)(2,1)S(1)}, bf16[1,40,16,256]{3,2,1,0:T(8,128)(2,1)S(1)}, u32[]{:S(2)}, u32[]{:S(2)}) %collective-permute-start.5) | collective-permute-done | bytes 327712 | tf_op jit(solution)/shard_map/ppermute | solution.py:105
  93.0 9.8 %collective-permute-done.8 = bf16[2,40,16,256]{3,2,1,0:T(8,128)(2,1)} collective-permute-done((bf16[2,40,16,256]{3,2,1,0:T(8,128)(2,1)}, bf16[2,40,16,256]{3,2,1,0:T(8,128)(2,1)}, u32[]{:S(2)}, u32[]{:S(2)}) %collective-permute-start.8) | collective-permute-done | bytes 655392 | tf_op jit(solution)/shard_map/ppermute | solution.py:105
  108.7 8.5 %place.4 = (bf16[4,256,1024]{2,1,0:T(8,128)(2,1)}, bf16[4,256,1024]{2,1,0:T(8,128)(2,1)}, bf16[4,256,1024]{2,1,0:T(8,128)(2,1)}) custom-call(s32[41]{0:T(128)} %add_add_fusion.4.s, bf16[8,24,16,256]{3,2,1,0:T(8,128)(2,1)} %copy-done.16, bf16[8,24,16,256]{3,2,1,0:T(8,128)(2,1)} %collective-permute-done.6.refs_1_, ...), custom_call_target="tpu_custom_call" | custom-call | flops 1048576 | bytes 1048576 | tf_op jit(solution)/shard_map/place/pallas_call | solution.py:227
  118.8 4.0 add_convert_fusion.7.v_ref
  136.7 20.1 %attend_forward.2 = (bf16[512,1024]{1,0:T(8,128)(2,1)}, f32[512,128]{1,0:T(8,128)}) custom-call(s32[1]{0:T(128)} %dynamic_slice.88.lim, bf16[512,1024]{1,0:T(8,128)(2,1)} %add_convert_fusion.8.q_ref, bf16[512,1024]{1,0:T(8,128)(2,1)} %convolution_convert_fusion.2.k_ref, bf16[512,1024]{1,0:T(8,128)(2,1)} %add_convert_fusion.7.v_ref), custom_call_target="tpu_custom_call" | custom-call | flops 1048576 | bytes 1048576 | tf_op jit(solution)/shard_map/attend_forward/pallas_call | solution.py:382
  160.1 3.4 collective-permute-done.17
  165.5 3.0 pad_maximum_fusion.1.refs_0_
  173.7 5.4 all-to-all-start.1
  179.1 10.3 %place.5 = (bf16[4,256,1024]{2,1,0:T(8,128)(2,1)}, bf16[4,256,1024]{2,1,0:T(8,128)(2,1)}, bf16[4,256,1024]{2,1,0:T(8,128)(2,1)}, bf16[4,256,1024]{2,1,0:T(8,128)(2,1)}, bf16[4,256,1024]{2,1,0:T(8,128)(2,1)}) custom-call(s32[41]{0:T(128)} %add_add_fusion.5.s, bf16[8,40,16,256]{3,2,1,0:T(8,128)(2,1)} %copy-done.5, ...), custom_call_target="tpu_custom_call" | custom-call | flops 1048576 | bytes 1048576 | tf_op jit(solution)/shard_map/place/pallas_call | solution.py:227
  189.4 3.5 fusion.23
  204.5 9.0 %attend_forward.3 = (bf16[512,1024]{1,0:T(8,128)(2,1)}, f32[512,128]{1,0:T(8,128)}) custom-call(s32[1]{0:T(128)} %dynamic_slice.88.lim, bf16[512,1024]{1,0:T(8,128)(2,1)} %add_convert_fusion.6.q_ref, bf16[128,1024]{1,0:T(8,128)(2,1)} %convolution_convert_fusion.3.k_ref, bf16[128,1024]{1,0:T(8,128)(2,1)} %fusion.4.v_ref), custom_call_target="tpu_custom_call" | custom-call | flops 1048576 | bytes 1048576 | tf_op jit(solution)/shard_map/attend_forward/pallas_call | solution.py:382
  213.5 3.4 fusion.26
  220.4 2.5 collective-permute-done.22
  222.9 2.9 pad_maximum_fusion.2.refs_0_
  229.8 4.7 all-to-all-start.2
  236.0 9.6 %place.6 = bf16[4,256,4096]{2,1,0:T(8,128)(2,1)} custom-call(s32[41]{0:T(128)} %add_add_fusion.6.s, bf16[8,32,16,256]{3,2,1,0:T(8,128)(2,1)} %pad_maximum_fusion.1.refs_0_, bf16[8,32,16,256]{3,2,1,0:T(8,128)(2,1)} %collective-permute-done.20.refs_1_, bf16[8,32,16,256]{3,2,1,0:T(8,128)(2,1)} %collective-permute-done.21.refs_2_, ...), custom_call_target="tpu_custom_call" | custom-call | flops 1048576 | bytes 1048576 | tf_op jit(solution)/shard_map/place/pallas_call | solution.py:227
  245.6 19.1 %gelu_forward.1 = (bf16[512,4096]{1,0:T(8,128)(2,1)}, bf16[512,4096]{1,0:T(8,128)(2,1)}) custom-call(bf16[512,1024]{1,0:T(8,128)(2,1)} %get-tuple-element.208.h_ref.x_own, bf16[1024,4096]{1,0:T(8,128)(2,1)} %bitcast.239, f32[1,4096]{1,0:T(1,128)} %bitcast.293), custom_call_target="tpu_custom_call" | custom-call | flops 1048576 | bytes 1048576 | tf_op jit(solution)/shard_map/gelu_forward/pallas_call | solution.py:515
  265.0 6.3 %all-to-all-done.2 = bf16[32,1,32,512]{3,2,1,0:T(8,128)(2,1)S(1)} async-done(((bf16[32,1,32,512]{3,2,1,0:T(8,128)(2,1)}), bf16[32,1,32,512]{3,2,1,0:T(8,128)(2,1)S(1)}, u32[]{:S(2)}, u32[]{:S(2)}) %all-to-all-start.2) | async-done | bytes 1048608 | tf_op jit(solution)/shard_map/all_to_all | solution.py:681
  274.2 9.6 %place.7 = bf16[16,256,1024]{2,1,0:T(8,128)(2,1)} custom-call(s32[41]{0:T(128)} %add_add_fusion.7.s, bf16[8,32,16,256]{3,2,1,0:T(8,128)(2,1)} %pad_maximum_fusion.2.refs_0_, bf16[8,32,16,256]{3,2,1,0:T(8,128)(2,1)} %collective-permute-done.24.refs_1_, bf16[8,32,16,256]{3,2,1,0:T(8,128)(2,1)} %collective-permute-done.25.refs_2_, ...), custom_call_target="tpu_custom_call" | custom-call | flops 1048576 | bytes 1048576 | tf_op jit(solution)/shard_map/place/pallas_call | solution.py:227
  283.8 8.3 %fusion.27 = f32[512,1024]{1,0:T(8,128)S(1)} fusion(bf16[512,4096]{1,0:T(8,128)(2,1)} %get-tuple-element.214.x_own, bf16[4096,1024]{1,0:T(8,128)(2,1)} %bitcast.242), kind=kOutput, calls=%fused_computation.236 | convolution fusion | flops 4294967296 | bytes 14680064 | tf_op jit(solution)/shard_map/dot_general | solution.py:43
  297.4 8.1 %multiply_convert_fusion.refs_0_ = bf16[512,4096]{1,0:T(8,128)(2,1)} fusion(bf16[512,4096]{1,0:T(8,128)(2,1)} %get-tuple-element.218, bf16[512,1024]{1,0:T(8,128)(2,1)S(1)} %convert_element_type.379.refs_0_, bf16[4096,1024]{1,0:T(8,128)(2,1)S(1)} %bitcast.245), kind=kOutput, calls=%fused_computation.6 | convolution fusion | flops 4301258752 | bytes 17825792 | tf_op jit(solution)/shard_map/dot_general | solution.py:47
  306.0 9.7 %weight_grad.7 = (bf16[8,1,32,16,256]{4,3,2,1,0:T(8,128)(2,1)}, bf16[8,1,32,16,256]{4,3,2,1,0:T(8,128)(2,1)}) custom-call(s32[41]{0:T(128)} %add_add_fusion.7.s, bf16[512,4096]{1,0:T(8,128)(2,1)} %get-tuple-element.214.x_own, bf16[512,4096]{1,0:T(8,128)(2,1)} %collective-permute-done.30.x_sib, bf16[512,1024]{1,0:T(8,128)(2,1)} %copy-done.32, ...), custom_call_target="tpu_custom_call" | custom-call | flops 1048576 | bytes 1048576 | tf_op jit(solution)/shard_map/weight_grad/pallas_call | solution.py:577
  315.9 11.1 %multiply_reduce_fusion.1 = (f32[1024]{0:T(1024)S(1)}, f32[512]{0:T(512)S(1)}, f32[512]{0:T(512)S(1)}, f32[1024]{0:T(1024)S(1)}, f32[512,1024]{1,0:T(8,128)S(1)}) fusion(f32[512,1024]{1,0:T(8,128)} %copy-done.3, f32[512]{0:T(512)S(1)} %add_rsqrt_fusion.1, f32[512]{0:T(512)S(1)} %broadcast_multiply_fusion.7, f32[1024]{0:T(1024)S(1)} %bitcast.301, ...), kind=kOutput, calls=%fused_computation.13 | convolution fusion | flops 4300207104 | bytes 18894848 | tf_op jit(solution)/shard_map/dot_general | solution.py:47
  335.2 9.6 %weight_grad.8 = (bf16[8,1,32,16,256]{4,3,2,1,0:T(8,128)(2,1)}, bf16[8,1,32,16,256]{4,3,2,1,0:T(8,128)(2,1)}) custom-call(s32[41]{0:T(128)} %add_add_fusion.6.s, bf16[512,1024]{1,0:T(8,128)(2,1)} %get-tuple-element.208.h_ref.x_own, bf16[512,1024]{1,0:T(8,128)(2,1)} %collective-permute-done.32.x_sib, bf16[512,4096]{1,0:T(8,128)(2,1)} %multiply_convert_fusion.refs_0_, ...), custom_call_target="tpu_custom_call" | custom-call | flops 1048576 | bytes 1048576 | tf_op jit(solution)/shard_map/weight_grad/pallas_call | solution.py:577
  344.9 4.3 add_convert_fusion.4
  351.5 4.7 all-to-all-start.3
  356.2 10.3 %attend_backward.2 = (bf16[512,1024]{1,0:T(8,128)(2,1)}, bf16[128,1024]{1,0:T(8,128)(2,1)}, bf16[128,1024]{1,0:T(8,128)(2,1)}) custom-call(s32[1]{0:T(128)} %dynamic_slice.88.lim, bf16[512,1024]{1,0:T(8,128)(2,1)} %add_convert_fusion.6.q_ref, bf16[128,1024]{1,0:T(8,128)(2,1)} %convolution_convert_fusion.3.k_ref, bf16[128,1024]{1,0:T(8,128)(2,1)} %fusion.4.v_ref, ...), custom_call_target="tpu_custom_call" | custom-call | flops 1048576 | bytes 1048576 | tf_op jit(solution)/shard_map/attend_backward/pallas_call | solution.py:465
  366.5 3.1 collective-permute-done.34
  369.6 4.4 multiply_reduce_fusion.2
  376.3 2.5 collective-permute-start.35
  383.6 3.0 gather_fusion.2
  386.6 5.1 all-to-all-start.4
  395.6 2.8 add_convert_fusion.13
  402.2 4.8 weight_grad.9
  407.0 4.6 weight_grad.10
  412.3 4.6 weight_grad.11
  416.9 4.8 weight_grad.12
  425.4 3.5 add_convert_fusion.2
  430.4 16.3 %attend_backward.3 = (bf16[512,1024]{1,0:T(8,128)(2,1)}, bf16[512,1024]{1,0:T(8,128)(2,1)}, bf16[512,1024]{1,0:T(8,128)(2,1)}) custom-call(s32[1]{0:T(128)} %dynamic_slice.88.lim, bf16[512,1024]{1,0:T(8,128)(2,1)} %add_convert_fusion.8.q_ref, bf16[512,1024]{1,0:T(8,128)(2,1)} %convolution_convert_fusion.2.k_ref, bf16[512,1024]{1,0:T(8,128)(2,1)} %add_convert_fusion.7.v_ref, ...), custom_call_target="tpu_custom_call" | custom-call | flops 1048576 | bytes 1048576 | tf_op jit(solution)/shard_map/attend_backward/pallas_call | solution.py:465
  446.8 7.8 %collective-permute-done.46 = bf16[4,32,16,256]{3,2,1,0:T(8,128)(2,1)S(1)} collective-permute-done((bf16[4,32,16,256]{3,2,1,0:T(8,128)(2,1)}, bf16[4,32,16,256]{3,2,1,0:T(8,128)(2,1)S(1)}, u32[]{:S(2)}, u32[]{:S(2)}) %collective-permute-start.46) | collective-permute-done | bytes 1048608 | tf_op jit(solution)/shard_map/ppermute | solution.py:105
  456.6 4.1 add_convert_fusion
  466.1 2.6 add_convert_fusion.14
  468.7 10.2 %collective-permute-done.61 = bf16[1,32,16,256]{3,2,1,0:T(8,128)(2,1)S(1)} collective-permute-done((bf16[1,32,16,256]{3,2,1,0:T(8,128)(2,1)S(1)}, bf16[1,32,16,256]{3,2,1,0:T(8,128)(2,1)S(1)}, u32[]{:S(2)}, u32[]{:S(2)}) %collective-permute-start.61) | collective-permute-done | bytes 262176 | tf_op jit(solution)/shard_map/ppermute | solution.py:105
  481.4 8.2 %weight_grad.13 = (bf16[8,3,8,16,256]{4,3,2,1,0:T(8,128)(2,1)}, bf16[8,3,8,16,256]{4,3,2,1,0:T(8,128)(2,1)}) custom-call(s32[41]{0:T(128)} %add_add_fusion.5.s, bf16[512,1024]{1,0:T(8,128)(2,1)} %get-tuple-element.169.x_own, bf16[512,1024]{1,0:T(8,128)(2,1)} %get-tuple-element.270.x_sib, bf16[512,1024]{1,0:T(8,128)(2,1)} %get-tuple-element.291.refs_0_, ...), custom_call_target="tpu_custom_call" | custom-call | flops 1048576 | bytes 1048576 | tf_op jit(solution)/shard_map/weight_grad/pallas_call | solution.py:577
  493.8 3.2 collective-permute-start.53
  505.8 4.6 collective-permute-done.52
  510.4 5.1 collective-permute-done.53
  519.6 3.2 convert_reduce_fusion
  523.1 7.2 %collective-permute-done.55 = bf16[4,24,16,256]{3,2,1,0:T(8,128)(2,1)S(1)} collective-permute-done((bf16[4,24,16,256]{3,2,1,0:T(8,128)(2,1)S(1)}, bf16[4,24,16,256]{3,2,1,0:T(8,128)(2,1)S(1)}, u32[]{:S(2)}, u32[]{:S(2)}) %collective-permute-start.55) | collective-permute-done | bytes 786464 | tf_op jit(solution)/shard_map/ppermute | solution.py:105
  530.5 2.5 collective-permute-start.58
  534.5 6.6 %collective-permute-done.58 = bf16[2,24,16,256]{3,2,1,0:T(8,128)(2,1)} collective-permute-done((bf16[2,24,16,256]{3,2,1,0:T(8,128)(2,1)S(1)}, bf16[2,24,16,256]{3,2,1,0:T(8,128)(2,1)}, u32[]{:S(2)}, u32[]{:S(2)}) %collective-permute-start.58) | collective-permute-done | bytes 393248 | tf_op jit(solution)/shard_map/ppermute | solution.py:105
  542.7 9.4 %collective-permute-done.60 = bf16[1,24,16,256]{3,2,1,0:T(8,128)(2,1)S(1)} collective-permute-done((bf16[1,24,16,256]{3,2,1,0:T(8,128)(2,1)S(1)}, bf16[1,24,16,256]{3,2,1,0:T(8,128)(2,1)S(1)}, u32[]{:S(2)}, u32[]{:S(2)}) %collective-permute-start.60) | collective-permute-done | bytes 196640 | tf_op jit(solution)/shard_map/ppermute | solution.py:105
  554.6 3.5 all-to-all-start.5
  561.2 11.4 %all-to-all-done.5 = bf16[64,16,256]{2,1,0:T(8,128)(2,1)S(1)} async-done(((bf16[64,16,256]{2,1,0:T(8,128)(2,1)}), bf16[64,16,256]{2,1,0:T(8,128)(2,1)S(1)}, u32[]{:S(2)}, u32[]{:S(2)}) %all-to-all-start.5) | async-done | bytes 524320 | tf_op jit(solution)/shard_map/all_to_all | solution.py:327
  572.6 3.6 all-to-all-start.6
  577.6 12.2 %collective-permute-done.63.other_ref = bf16[8,8,16,256]{3,2,1,0:T(8,128)(2,1)S(1)} collective-permute-done((bf16[8,8,16,256]{3,2,1,0:T(8,128)(2,1)S(1)}, bf16[8,8,16,256]{3,2,1,0:T(8,128)(2,1)S(1)}, u32[]{:S(2)}, u32[]{:S(2)}) %collective-permute-start.63) | collective-permute-done | bytes 524320 | tf_op jit(solution)/shard_map/ppermute | solution.py:97
  589.8 2.5 all-to-all-done.6
  593.7 11.0 %shampoo.2 = (f32[1,16,256,256]{3,2,1,0:T(8,128)}, f32[1,16,256,256]{3,2,1,0:T(8,128)}, f32[1,16,256,256]{3,2,1,0:T(8,128)}, f32[1,16,256,256]{3,2,1,0:T(8,128)}) custom-call(s32[1]{0:T(128)} %bitcast.79.flag, bf16[8,8,16,256]{3,2,1,0:T(8,128)(2,1)} %bitcast.284, bf16[8,8,16,256]{3,2,1,0:T(8,128)(2,1)} %copy-done.65, f32[1,16,256,256]{3,2,1,0:T(8,128)} %w_ref.3, ...), custom_call_target="tpu_custom_call" | custom-call | flops 1048576 | bytes 1048576 | tf_op jit(solution)/shard_map/shampoo/pallas_call | solution.py:634
  607.5 10.9 %shampoo.3 = (f32[1,16,256,256]{3,2,1,0:T(8,128)}, f32[1,16,256,256]{3,2,1,0:T(8,128)}, f32[1,16,256,256]{3,2,1,0:T(8,128)}, f32[1,16,256,256]{3,2,1,0:T(8,128)}) custom-call(s32[1]{0:T(128)} %bitcast.79.flag, bf16[8,9,16,256]{3,2,1,0:T(8,128)(2,1)} %bitcast.276, ...), custom_call_target="tpu_custom_call", output_to_operand_aliasing={{0}: (8, {}), {1}: (9, {}), {2}: (10, {}), {3}: (11, {})} | custom-call | flops 1048576 | bytes 1048576 | tf_op jit(solution)/shard_map/shampoo/pallas_call | solution.py:634
  (492 shorter events, 158.0 us)
Async XLA Ops:
  5.0 34.5 %all-to-all-start = ((bf16[136,16,256]{2,1,0:T(8,128)(2,1)}), bf16[136,16,256]{2,1,0:T(8,128)(2,1)S(1)}, u32[]{:S(2)}, u32[]{:S(2)}) async-start(bf16[136,16,256]{2,1,0:T(8,128)(2,1)} %bitcast.4), calls=%async_computation | async-start | bytes 2228224 | tf_op jit(solution)/shard_map/all_to_all | solution.py:271
  40.1 10.7 %collective-permute-start.2 = (bf16[1,24,16,256]{3,2,1,0:T(8,128)(2,1)S(1)}, bf16[1,24,16,256]{3,2,1,0:T(8,128)(2,1)S(1)}, u32[]{:S(2)}, u32[]{:S(2)}) collective-permute-start(bf16[1,24,16,256]{3,2,1,0:T(8,128)(2,1)S(1)} %bitcast.270), channel_id=1, source_target_pairs={{0,8},{1,9},{2,10},{3,11},{4,12},{5,13},{6,14},{7,15},{8,0},{9,1},... | collective-permute-start | bytes 589832 | tf_op jit(solution)/shard_map/ppermute | solution.py:105
  50.9 7.8 %collective-permute-start.3 = (bf16[2,24,16,256]{3,2,1,0:T(8,128)(2,1)S(1)}, bf16[2,24,16,256]{3,2,1,0:T(8,128)(2,1)S(1)}, u32[]{:S(2)}, u32[]{:S(2)}) collective-permute-start(bf16[2,24,16,256]{3,2,1,0:T(8,128)(2,1)S(1)} %pad_maximum_fusion.19), channel_id=1, source_target_pairs={{0,16},{1,5},{2,18},{3,7},{4,20},{5,1},{6,22},{7,3},{8,24},{9,13},... | collective-permute-start | bytes 1179656 | tf_op jit(solution)/shard_map/ppermute | solution.py:105
  59.7 19.3 %collective-permute-start.4 = (bf16[4,24,16,256]{3,2,1,0:T(8,128)(2,1)}, bf16[4,24,16,256]{3,2,1,0:T(8,128)(2,1)}, u32[]{:S(2)}, u32[]{:S(2)}) collective-permute-start(bf16[4,24,16,256]{3,2,1,0:T(8,128)(2,1)} %pad_maximum_fusion.14), channel_id=1, source_target_pairs={{0,4},{1,3},{2,6},{3,1},{4,0},{5,7},{6,2},{7,5},{8,12},{9,11},{10,... | collective-permute-start | bytes 2359304 | tf_op jit(solution)/shard_map/ppermute | solution.py:105
  59.7 16.3 %collective-permute-start.5 = (bf16[1,40,16,256]{3,2,1,0:T(8,128)(2,1)S(1)}, bf16[1,40,16,256]{3,2,1,0:T(8,128)(2,1)S(1)}, u32[]{:S(2)}, u32[]{:S(2)}) collective-permute-start(bf16[1,40,16,256]{3,2,1,0:T(8,128)(2,1)S(1)} %bitcast.250), channel_id=1, source_target_pairs={{0,8},{1,9},{2,10},{3,11},{4,12},{5,13},{6,14},{7,15},{8,0},{9,1},... | collective-permute-start | bytes 983048 | tf_op jit(solution)/shard_map/ppermute | solution.py:105
  61.5 23.8 %collective-permute-start = (bf16[2,512,512]{2,1,0:T(8,128)(2,1)}, bf16[2,512,512]{2,1,0:T(8,128)(2,1)}, u32[]{:S(2)}, u32[]{:S(2)}) collective-permute-start(bf16[2,512,512]{2,1,0:T(8,128)(2,1)} %param.21), channel_id=1, source_target_pairs={{0,1},{1,0},{2,3},{3,2},{4,5},{5,4},{6,7},{7,6},{8,9},{9,8},{10,11... | collective-permute-start | bytes 3145736 | tf_op jit(solution)/shard_map/ppermute | solution.py:94
  61.5 21.0 %collective-permute-start.1 = (bf16[2,128,512]{2,1,0:T(8,128)(2,1)}, bf16[2,128,512]{2,1,0:T(8,128)(2,1)}, u32[]{:S(2)}, u32[]{:S(2)}) collective-permute-start(bf16[2,128,512]{2,1,0:T(8,128)(2,1)} %param.22), channel_id=1, source_target_pairs={{0,1},{1,0},{2,3},{3,2},{4,5},{5,4},{6,7},{7,6},{8,9},{9,8},{10,11... | collective-permute-start | bytes 786440 | tf_op jit(solution)/shard_map/ppermute | solution.py:94
  80.5 22.3 %collective-permute-start.6 = (bf16[8,24,16,256]{3,2,1,0:T(8,128)(2,1)S(1)}, bf16[8,24,16,256]{3,2,1,0:T(8,128)(2,1)}, u32[]{:S(2)}, u32[]{:S(2)}) collective-permute-start(bf16[8,24,16,256]{3,2,1,0:T(8,128)(2,1)S(1)} %pad_maximum_fusion.3.refs_0_), channel_id=1, source_target_pairs={{0,2},{1,17},{2,0},{3,19},{4,6},{5,21},{6,4},{7,23},{8,10},{9,25},... | collective-permute-start | bytes 4718600 | tf_op jit(solution)/shard_map/ppermute | solution.py:105
  81.8 21.0 %collective-permute-start.7 = (bf16[8,24,16,256]{3,2,1,0:T(8,128)(2,1)S(1)}, bf16[8,24,16,256]{3,2,1,0:T(8,128)(2,1)}, u32[]{:S(2)}, u32[]{:S(2)}) collective-permute-start(bf16[8,24,16,256]{3,2,1,0:T(8,128)(2,1)S(1)} %pad_maximum_fusion.3.refs_0_), channel_id=1, source_target_pairs={{0,1},{1,0},{2,3},{3,2},{4,5},{5,4},{6,7},{7,6},{8,9},{9,8},{10,11... | collective-permute-start | bytes 4718600 | tf_op jit(solution)/shard_map/ppermute | solution.py:94
  85.3 17.5 %collective-permute-start.8 = (bf16[2,40,16,256]{3,2,1,0:T(8,128)(2,1)}, bf16[2,40,16,256]{3,2,1,0:T(8,128)(2,1)}, u32[]{:S(2)}, u32[]{:S(2)}) collective-permute-start(bf16[2,40,16,256]{3,2,1,0:T(8,128)(2,1)} %pad_maximum_fusion.15), channel_id=1, source_target_pairs={{0,4},{1,5},{2,6},{3,7},{4,0},{5,1},{6,2},{7,3},{8,12},{9,13},{10,... | collective-permute-start | bytes 1966088 | tf_op jit(solution)/shard_map/ppermute | solution.py:105
  102.8 15.0 %collective-permute-start.10 = (bf16[1,32,16,256]{3,2,1,0:T(8,128)(2,1)S(1)}, bf16[1,32,16,256]{3,2,1,0:T(8,128)(2,1)S(1)}, u32[]{:S(2)}, u32[]{:S(2)}) collective-permute-start(bf16[1,32,16,256]{3,2,1,0:T(8,128)(2,1)S(1)} %bitcast.266), channel_id=1, source_target_pairs={{0,8},{1,9},{2,10},{3,11},{4,12},{5,13},{6,14},{7,15},{8,0},{9,1},... | collective-permute-start | bytes 786440 | tf_op jit(solution)/shard_map/ppermute | solution.py:105
  105.8 21.5 %collective-permute-start.12 = (bf16[4,40,16,256]{3,2,1,0:T(8,128)(2,1)}, bf16[4,40,16,256]{3,2,1,0:T(8,128)(2,1)}, u32[]{:S(2)}, u32[]{:S(2)}) collective-permute-start(bf16[4,40,16,256]{3,2,1,0:T(8,128)(2,1)} %pad_maximum_fusion.4), channel_id=1, source_target_pairs={{0,16},{1,3},{2,18},{3,1},{4,20},{5,7},{6,22},{7,5},{8,24},{9,11},... | collective-permute-start | bytes 3932168 | tf_op jit(solution)/shard_map/ppermute | solution.py:105
  117.8 10.8 %collective-permute-start.13 = (bf16[2,32,16,256]{3,2,1,0:T(8,128)(2,1)S(1)}, bf16[2,32,16,256]{3,2,1,0:T(8,128)(2,1)S(1)}, u32[]{:S(2)}, u32[]{:S(2)}) collective-permute-start(bf16[2,32,16,256]{3,2,1,0:T(8,128)(2,1)S(1)} %pad_maximum_fusion.17), channel_id=1, source_target_pairs={{0,2},{1,17},{2,0},{3,19},{4,6},{5,21},{6,4},{7,23},{8,10},{9,25},... | collective-permute-start | bytes 1572872 | tf_op jit(solution)/shard_map/ppermute | solution.py:105
  130.5 34.1 %collective-permute-start.14 = (bf16[8,40,16,256]{3,2,1,0:T(8,128)(2,1)S(1)}, bf16[8,40,16,256]{3,2,1,0:T(8,128)(2,1)}, u32[]{:S(2)}, u32[]{:S(2)}) collective-permute-start(bf16[8,40,16,256]{3,2,1,0:T(8,128)(2,1)S(1)} %pad_maximum_fusion.refs_0_), channel_id=1, source_target_pairs={{0,2},{1,17},{2,0},{3,19},{4,6},{5,21},{6,4},{7,23},{8,10},{9,25},... | collective-permute-start | bytes 7864328 | tf_op jit(solution)/shard_map/ppermute | solution.py:105
  132.0 32.6 %collective-permute-start.15 = (bf16[8,40,16,256]{3,2,1,0:T(8,128)(2,1)S(1)}, bf16[8,40,16,256]{3,2,1,0:T(8,128)(2,1)}, u32[]{:S(2)}, u32[]{:S(2)}) collective-permute-start(bf16[8,40,16,256]{3,2,1,0:T(8,128)(2,1)S(1)} %pad_maximum_fusion.refs_0_), channel_id=1, source_target_pairs={{0,1},{1,0},{2,3},{3,2},{4,5},{5,4},{6,7},{7,6},{8,9},{9,8},{10,11... | collective-permute-start | bytes 7864328 | tf_op jit(solution)/shard_map/ppermute | solution.py:94
  133.4 31.2 %collective-permute-start.16 = (bf16[4,32,16,256]{3,2,1,0:T(8,128)(2,1)}, bf16[4,32,16,256]{3,2,1,0:T(8,128)(2,1)}, u32[]{:S(2)}, u32[]{:S(2)}) collective-permute-start(bf16[4,32,16,256]{3,2,1,0:T(8,128)(2,1)} %pad_maximum_fusion.8), channel_id=1, source_target_pairs={{0,4},{1,5},{2,6},{3,7},{4,0},{5,1},{6,2},{7,3},{8,12},{9,13},{10,... | collective-permute-start | bytes 3145736 | tf_op jit(solution)/shard_map/ppermute | solution.py:105
  135.1 28.4 %collective-permute-start.17 = (bf16[1,32,16,256]{3,2,1,0:T(8,128)(2,1)S(1)}, bf16[1,32,16,256]{3,2,1,0:T(8,128)(2,1)}, u32[]{:S(2)}, u32[]{:S(2)}) collective-permute-start(bf16[1,32,16,256]{3,2,1,0:T(8,128)(2,1)S(1)} %bitcast.262), channel_id=1, source_target_pairs={{0,8},{1,9},{2,10},{3,11},{4,12},{5,13},{6,14},{7,15},{8,0},{9,1},... | collective-permute-start | bytes 786440 | tf_op jit(solution)/shard_map/ppermute | solution.py:105
  164.6 14.5 %collective-permute-start.18 = (bf16[8,40,16,256]{3,2,1,0:T(8,128)(2,1)}, bf16[8,40,16,256]{3,2,1,0:T(8,128)(2,1)}, u32[]{:S(2)}, u32[]{:S(2)}) collective-permute-start(bf16[8,40,16,256]{3,2,1,0:T(8,128)(2,1)} %collective-permute-done.14.refs_1_), channel_id=1, source_target_pairs={{0,1},{1,0},{2,3},{3,2},{4,5},{5,4},{6,7},{7,6},{8,9},{9,8},{10,11... | collective-permute-start | bytes 7864328 | tf_op jit(solution)/shard_map/ppermute | solution.py:94
  168.5 51.9 %collective-permute-start.20 = (bf16[8,32,16,256]{3,2,1,0:T(8,128)(2,1)}, bf16[8,32,16,256]{3,2,1,0:T(8,128)(2,1)}, u32[]{:S(2)}, u32[]{:S(2)}) collective-permute-start(bf16[8,32,16,256]{3,2,1,0:T(8,128)(2,1)} %pad_maximum_fusion.1.refs_0_), channel_id=1, source_target_pairs={{0,16},{1,3},{2,18},{3,1},{4,20},{5,7},{6,22},{7,5},{8,24},{9,11},... | collective-permute-start | bytes 6291464 | tf_op jit(solution)/shard_map/ppermute | solution.py:105
  170.0 50.4 %collective-permute-start.21 = (bf16[8,32,16,256]{3,2,1,0:T(8,128)(2,1)}, bf16[8,32,16,256]{3,2,1,0:T(8,128)(2,1)}, u32[]{:S(2)}, u32[]{:S(2)}) collective-permute-start(bf16[8,32,16,256]{3,2,1,0:T(8,128)(2,1)} %pad_maximum_fusion.1.refs_0_), channel_id=1, source_target_pairs={{0,1},{1,0},{2,3},{3,2},{4,5},{5,4},{6,7},{7,6},{8,9},{9,8},{10,11... | collective-permute-start | bytes 6291464 | tf_op jit(solution)/shard_map/ppermute | solution.py:94
  171.8 28.5 %collective-permute-start.19 = (bf16[2,32,16,256]{3,2,1,0:T(8,128)(2,1)}, bf16[2,32,16,256]{3,2,1,0:T(8,128)(2,1)}, u32[]{:S(2)}, u32[]{:S(2)}) collective-permute-start(bf16[2,32,16,256]{3,2,1,0:T(8,128)(2,1)} %pad_maximum_fusion.18), channel_id=1, source_target_pairs={{0,2},{1,17},{2,0},{3,19},{4,6},{5,21},{6,4},{7,23},{8,10},{9,25},... | collective-permute-start | bytes 1572872 | tf_op jit(solution)/shard_map/ppermute | solution.py:105
  173.7 46.7 %all-to-all-start.1 = ((bf16[2,16,32,512]{3,2,0,1:T(8,128)(2,1)}), bf16[2,16,32,512]{3,2,0,1:T(8,128)(2,1)S(1)}, u32[]{:S(2)}, u32[]{:S(2)}) async-start(bf16[2,16,32,512]{3,2,0,1:T(8,128)(2,1)} %copy.66), calls=%async_computation.1 | async-start | bytes 2097152 | tf_op jit(solution)/shard_map/all_to_all | solution.py:676
  202.5 20.4 %collective-permute-start.22 = (bf16[4,32,16,256]{3,2,1,0:T(8,128)(2,1)}, bf16[4,32,16,256]{3,2,1,0:T(8,128)(2,1)}, u32[]{:S(2)}, u32[]{:S(2)}) collective-permute-start(bf16[4,32,16,256]{3,2,1,0:T(8,128)(2,1)} %pad_maximum_fusion.9), channel_id=1, source_target_pairs={{0,16},{1,5},{2,18},{3,7},{4,20},{5,1},{6,22},{7,3},{8,24},{9,13},... | collective-permute-start | bytes 3145736 | tf_op jit(solution)/shard_map/ppermute | solution.py:105
  222.9 13.0 %collective-permute-start.23 = (bf16[8,32,16,256]{3,2,1,0:T(8,128)(2,1)}, bf16[8,32,16,256]{3,2,1,0:T(8,128)(2,1)}, u32[]{:S(2)}, u32[]{:S(2)}) collective-permute-start(bf16[8,32,16,256]{3,2,1,0:T(8,128)(2,1)} %collective-permute-done.20.refs_1_), channel_id=1, source_target_pairs={{0,1},{1,0},{2,3},{3,2},{4,5},{5,4},{6,7},{7,6},{8,9},{9,8},{10,11... | collective-permute-start | bytes 6291464 | tf_op jit(solution)/shard_map/ppermute | solution.py:94
  225.9 38.8 %collective-permute-start.24 = (bf16[8,32,16,256]{3,2,1,0:T(8,128)(2,1)}, bf16[8,32,16,256]{3,2,1,0:T(8,128)(2,1)}, u32[]{:S(2)}, u32[]{:S(2)}) collective-permute-start(bf16[8,32,16,256]{3,2,1,0:T(8,128)(2,1)} %pad_maximum_fusion.2.refs_0_), channel_id=1, source_target_pairs={{0,4},{1,3},{2,6},{3,1},{4,0},{5,7},{6,2},{7,5},{8,12},{9,11},{10,... | collective-permute-start | bytes 6291464 | tf_op jit(solution)/shard_map/ppermute | solution.py:105
  228.2 36.5 %collective-permute-start.25 = (bf16[8,32,16,256]{3,2,1,0:T(8,128)(2,1)}, bf16[8,32,16,256]{3,2,1,0:T(8,128)(2,1)}, u32[]{:S(2)}, u32[]{:S(2)}) collective-permute-start(bf16[8,32,16,256]{3,2,1,0:T(8,128)(2,1)} %pad_maximum_fusion.2.refs_0_), channel_id=1, source_target_pairs={{0,1},{1,0},{2,3},{3,2},{4,5},{5,4},{6,7},{7,6},{8,9},{9,8},{10,11... | collective-permute-start | bytes 6291464 | tf_op jit(solution)/shard_map/ppermute | solution.py:94
  229.8 41.4 %all-to-all-start.2 = ((bf16[32,1,32,512]{3,2,1,0:T(8,128)(2,1)}), bf16[32,1,32,512]{3,2,1,0:T(8,128)(2,1)S(1)}, u32[]{:S(2)}, u32[]{:S(2)}) async-start(bf16[32,1,32,512]{3,2,1,0:T(8,128)(2,1)} %bitcast.258), calls=%async_computation.2 | async-start | bytes 2097152 | tf_op jit(solution)/shard_map/all_to_all | solution.py:681
  264.7 9.4 %collective-permute-start.26 = (bf16[8,32,16,256]{3,2,1,0:T(8,128)(2,1)}, bf16[8,32,16,256]{3,2,1,0:T(8,128)(2,1)}, u32[]{:S(2)}, u32[]{:S(2)}) collective-permute-start(bf16[8,32,16,256]{3,2,1,0:T(8,128)(2,1)} %collective-permute-done.24.refs_1_), channel_id=1, source_target_pairs={{0,1},{1,0},{2,3},{3,2},{4,5},{5,4},{6,7},{7,6},{8,9},{9,8},{10,11... | collective-permute-start | bytes 6291464 | tf_op jit(solution)/shard_map/ppermute | solution.py:94
  272.9 33.2 %collective-permute-start.30 = (bf16[512,4096]{1,0:T(8,128)(2,1)}, bf16[512,4096]{1,0:T(8,128)(2,1)}, u32[]{:S(2)}, u32[]{:S(2)}) collective-permute-start(bf16[512,4096]{1,0:T(8,128)(2,1)} %get-tuple-element.214.x_own), channel_id=1, source_target_pairs={{0,1},{1,0},{2,3},{3,2},{4,5},{5,4},{6,7},{7,6},{8,9},{9,8},{10,11... | collective-permute-start | bytes 12582920 | tf_op jit(solution)/shard_map/ppermute | solution.py:94
  297.3 8.2 %collective-permute-start.28 = (bf16[512,1024]{1,0:T(8,128)(2,1)S(1)}, bf16[512,1024]{1,0:T(8,128)(2,1)}, u32[]{:S(2)}, u32[]{:S(2)}) collective-permute-start(bf16[512,1024]{1,0:T(8,128)(2,1)S(1)} %convert_element_type.379.refs_0_), channel_id=1, source_target_pairs={{0,1},{1,0},{2,3},{3,2},{4,5},{5,4},{6,7},{7,6},{8,9},{9,8},{10,11... | collective-permute-start | bytes 3145736 | tf_op jit(solution)/shard_map/ppermute | solution.py:94
  305.5 10.3 %collective-permute-start.29 = (bf16[512,4096]{1,0:T(8,128)(2,1)}, bf16[512,4096]{1,0:T(8,128)(2,1)}, u32[]{:S(2)}, u32[]{:S(2)}) collective-permute-start(bf16[512,4096]{1,0:T(8,128)(2,1)} %multiply_convert_fusion.refs_0_), channel_id=1, source_target_pairs={{0,1},{1,0},{2,3},{3,2},{4,5},{5,4},{6,7},{7,6},{8,9},{9,8},{10,11... | collective-permute-start | bytes 12582920 | tf_op jit(solution)/shard_map/ppermute | solution.py:94
  305.6 29.7 %collective-permute-start.32 = (bf16[512,1024]{1,0:T(8,128)(2,1)S(1)}, bf16[512,1024]{1,0:T(8,128)(2,1)}, u32[]{:S(2)}, u32[]{:S(2)}) collective-permute-start(bf16[512,1024]{1,0:T(8,128)(2,1)S(1)} %copy-done.8), channel_id=1, source_target_pairs={{0,1},{1,0},{2,3},{3,2},{4,5},{5,4},{6,7},{7,6},{8,9},{9,8},{10,11... | collective-permute-start | bytes 3145736 | tf_op jit(solution)/shard_map/ppermute | solution.py:94
  315.8 29.1 %collective-permute-start.33 = (bf16[8,32,16,256]{3,2,1,0:T(8,128)(2,1)}, bf16[8,32,16,256]{3,2,1,0:T(8,128)(2,1)}, u32[]{:S(2)}, u32[]{:S(2)}) collective-permute-start(bf16[8,32,16,256]{3,2,1,0:T(8,128)(2,1)} %bitcast.324), channel_id=1, source_target_pairs={{0,4},{1,3},{2,6},{3,1},{4,0},{5,7},{6,2},{7,5},{8,12},{9,11},{10,... | collective-permute-start | bytes 6291464 | tf_op jit(solution)/shard_map/ppermute | solution.py:105
  327.0 6.8 %collective-permute-start.31 = (bf16[512,512]{1,0:T(8,128)(2,1)S(1)}, bf16[512,512]{1,0:T(8,128)(2,1)S(1)}, u32[]{:S(2)}, u32[]{:S(2)}) collective-permute-start(bf16[512,512]{1,0:T(8,128)(2,1)S(1)} %constant_dynamic-slice_fusion.2), channel_id=1, source_target_pairs={{0,1},{1,0},{2,3},{3,2},{4,5},{5,4},{6,7},{7,6},{8,9},{9,8},{10,11... | collective-permute-start | bytes 1572872 | tf_op jit(solution)/shard_map/ppermute | solution.py:94
  349.2 20.5 %collective-permute-start.34 = (bf16[4,32,16,256]{3,2,1,0:T(8,128)(2,1)}, bf16[4,32,16,256]{3,2,1,0:T(8,128)(2,1)}, u32[]{:S(2)}, u32[]{:S(2)}) collective-permute-start(bf16[4,32,16,256]{3,2,1,0:T(8,128)(2,1)} %get-tuple-element.353), channel_id=1, source_target_pairs={{0,16},{1,5},{2,18},{3,7},{4,20},{5,1},{6,22},{7,3},{8,24},{9,13},... | collective-permute-start | bytes 3145736 | tf_op jit(solution)/shard_map/ppermute | solution.py:105
  351.5 30.8 %all-to-all-start.3 = ((bf16[2,16,32,512]{3,2,0,1:T(8,128)(2,1)}), bf16[2,16,32,512]{3,2,0,1:T(8,128)(2,1)S(1)}, u32[]{:S(2)}, u32[]{:S(2)}) async-start(bf16[2,16,32,512]{3,2,0,1:T(8,128)(2,1)} %copy.69), calls=%async_computation.3 | async-start | bytes 2097152 | tf_op jit(solution)/shard_map/all_to_all | solution.py:676
  378.9 13.5 %collective-permute-start.42 = (bf16[512,1024]{1,0:T(8,128)(2,1)}, bf16[512,1024]{1,0:T(8,128)(2,1)}, u32[]{:S(2)}, u32[]{:S(2)}) collective-permute-start(bf16[512,1024]{1,0:T(8,128)(2,1)} %get-tuple-element.191.x_own.o_ref), channel_id=1, source_target_pairs={{0,1},{1,0},{2,3},{3,2},{4,5},{5,4},{6,7},{7,6},{8,9},{9,8},{10,11... | collective-permute-start | bytes 3145736 | tf_op jit(solution)/shard_map/ppermute | solution.py:94
  379.0 45.6 %collective-permute-start.43 = (bf16[8,32,16,256]{3,2,1,0:T(8,128)(2,1)}, bf16[8,32,16,256]{3,2,1,0:T(8,128)(2,1)}, u32[]{:S(2)}, u32[]{:S(2)}) collective-permute-start(bf16[8,32,16,256]{3,2,1,0:T(8,128)(2,1)} %bitcast.61), channel_id=1, source_target_pairs={{0,16},{1,3},{2,18},{3,1},{4,20},{5,7},{6,22},{7,5},{8,24},{9,11},... | collective-permute-start | bytes 6291464 | tf_op jit(solution)/shard_map/ppermute | solution.py:105
  386.6 35.7 %all-to-all-start.4 = ((bf16[32,1,32,512]{3,2,1,0:T(8,128)(2,1)}), bf16[32,1,32,512]{3,2,1,0:T(8,128)(2,1)}, u32[]{:S(2)}, u32[]{:S(2)}) async-start(bf16[32,1,32,512]{3,2,1,0:T(8,128)(2,1)} %bitcast.256), calls=%async_computation.4 | async-start | bytes 2097152 | tf_op jit(solution)/shard_map/all_to_all | solution.py:681
  391.8 9.4 %collective-permute-start.41 = (bf16[512,1024]{1,0:T(8,128)(2,1)S(1)}, bf16[512,1024]{1,0:T(8,128)(2,1)S(1)}, u32[]{:S(2)}, u32[]{:S(2)}) collective-permute-start(bf16[512,1024]{1,0:T(8,128)(2,1)S(1)} %copy-done.23), channel_id=1, source_target_pairs={{0,1},{1,0},{2,3},{3,2},{4,5},{5,4},{6,7},{7,6},{8,9},{9,8},{10,11... | collective-permute-start | bytes 3145736 | tf_op jit(solution)/shard_map/ppermute | solution.py:94
  392.3 24.5 %collective-permute-start.36 = (bf16[512,1024]{1,0:T(8,128)(2,1)}, bf16[512,1024]{1,0:T(8,128)(2,1)}, u32[]{:S(2)}, u32[]{:S(2)}) collective-permute-start(bf16[512,1024]{1,0:T(8,128)(2,1)} %get-tuple-element.203.o_ref.x_own), channel_id=1, source_target_pairs={{0,1},{1,0},{2,3},{3,2},{4,5},{5,4},{6,7},{7,6},{8,9},{9,8},{10,11... | collective-permute-start | bytes 3145736 | tf_op jit(solution)/shard_map/ppermute | solution.py:94
  392.4 24.5 %collective-permute-start.37 = (bf16[512,1024]{1,0:T(8,128)(2,1)S(1)}, bf16[512,1024]{1,0:T(8,128)(2,1)}, u32[]{:S(2)}, u32[]{:S(2)}) collective-permute-start(bf16[512,1024]{1,0:T(8,128)(2,1)S(1)} %copy-done.19), channel_id=1, source_target_pairs={{0,1},{1,0},{2,3},{3,2},{4,5},{5,4},{6,7},{7,6},{8,9},{9,8},{10,11... | collective-permute-start | bytes 3145736 | tf_op jit(solution)/shard_map/ppermute | solution.py:94
  399.3 25.3 %collective-permute-start.44 = (bf16[2,32,16,256]{3,2,1,0:T(8,128)(2,1)}, bf16[2,32,16,256]{3,2,1,0:T(8,128)(2,1)}, u32[]{:S(2)}, u32[]{:S(2)}) collective-permute-start(bf16[2,32,16,256]{3,2,1,0:T(8,128)(2,1)} %get-tuple-element.360), channel_id=1, source_target_pairs={{0,2},{1,17},{2,0},{3,19},{4,6},{5,21},{6,4},{7,23},{8,10},{9,25},... | collective-permute-start | bytes 1572872 | tf_op jit(solution)/shard_map/ppermute | solution.py:105
  402.2 9.4 %collective-permute-start.39 = (bf16[128,1024]{1,0:T(8,128)(2,1)S(1)}, bf16[128,1024]{1,0:T(8,128)(2,1)S(1)}, u32[]{:S(2)}, u32[]{:S(2)}) collective-permute-start(bf16[128,1024]{1,0:T(8,128)(2,1)S(1)} %copy-done.43), channel_id=1, source_target_pairs={{0,1},{1,0},{2,3},{3,2},{4,5},{5,4},{6,7},{7,6},{8,9},{9,8},{10,11... | collective-permute-start | bytes 786440 | tf_op jit(solution)/shard_map/ppermute | solution.py:94
  424.6 32.0 %collective-permute-start.45 = (bf16[8,40,16,256]{3,2,1,0:T(8,128)(2,1)}, bf16[8,40,16,256]{3,2,1,0:T(8,128)(2,1)}, u32[]{:S(2)}, u32[]{:S(2)}) collective-permute-start(bf16[8,40,16,256]{3,2,1,0:T(8,128)(2,1)} %bitcast.241), channel_id=1, source_target_pairs={{0,2},{1,17},{2,0},{3,19},{4,6},{5,21},{6,4},{7,23},{8,10},{9,25},... | collective-permute-start | bytes 7864328 | tf_op jit(solution)/shard_map/ppermute | solution.py:105
  428.9 25.6 %collective-permute-start.46 = (bf16[4,32,16,256]{3,2,1,0:T(8,128)(2,1)}, bf16[4,32,16,256]{3,2,1,0:T(8,128)(2,1)S(1)}, u32[]{:S(2)}, u32[]{:S(2)}) collective-permute-start(bf16[4,32,16,256]{3,2,1,0:T(8,128)(2,1)} %get-tuple-element.351), channel_id=1, source_target_pairs={{0,4},{1,5},{2,6},{3,7},{4,0},{5,1},{6,2},{7,3},{8,12},{9,13},{10,... | collective-permute-start | bytes 3145736 | tf_op jit(solution)/shard_map/ppermute | solution.py:105
  460.7 30.5 %collective-permute-start.50 = (bf16[4,40,16,256]{3,2,1,0:T(8,128)(2,1)}, bf16[4,40,16,256]{3,2,1,0:T(8,128)(2,1)}, u32[]{:S(2)}, u32[]{:S(2)}) collective-permute-start(bf16[4,40,16,256]{3,2,1,0:T(8,128)(2,1)} %get-tuple-element.349), channel_id=1, source_target_pairs={{0,16},{1,3},{2,18},{3,1},{4,20},{5,7},{6,22},{7,5},{8,24},{9,11},... | collective-permute-start | bytes 3932168 | tf_op jit(solution)/shard_map/ppermute | solution.py:105
  461.9 19.5 %collective-permute-start.47 = (bf16[512,1024]{1,0:T(8,128)(2,1)}, bf16[512,1024]{1,0:T(8,128)(2,1)}, u32[]{:S(2)}, u32[]{:S(2)}) collective-permute-start(bf16[512,1024]{1,0:T(8,128)(2,1)} %get-tuple-element.291.refs_0_), channel_id=1, source_target_pairs={{0,1},{1,0},{2,3},{3,2},{4,5},{5,4},{6,7},{7,6},{8,9},{9,8},{10,11... | collective-permute-start | bytes 3145736 | tf_op jit(solution)/shard_map/ppermute | solution.py:94
  462.0 19.5 %collective-permute-start.48 = (bf16[512,1024]{1,0:T(8,128)(2,1)}, bf16[512,1024]{1,0:T(8,128)(2,1)}, u32[]{:S(2)}, u32[]{:S(2)}) collective-permute-start(bf16[512,1024]{1,0:T(8,128)(2,1)} %get-tuple-element.280.refs_1_), channel_id=1, source_target_pairs={{0,1},{1,0},{2,3},{3,2},{4,5},{5,4},{6,7},{7,6},{8,9},{9,8},{10,11... | collective-permute-start | bytes 3145736 | tf_op jit(solution)/shard_map/ppermute | solution.py:94
  462.5 19.0 %collective-permute-start.49 = (bf16[512,1024]{1,0:T(8,128)(2,1)S(1)}, bf16[512,1024]{1,0:T(8,128)(2,1)}, u32[]{:S(2)}, u32[]{:S(2)}) collective-permute-start(bf16[512,1024]{1,0:T(8,128)(2,1)S(1)} %copy-done.6), channel_id=1, source_target_pairs={{0,1},{1,0},{2,3},{3,2},{4,5},{5,4},{6,7},{7,6},{8,9},{9,8},{10,11... | collective-permute-start | bytes 3145736 | tf_op jit(solution)/shard_map/ppermute | solution.py:94
  463.6 15.2 %collective-permute-start.61 = (bf16[1,32,16,256]{3,2,1,0:T(8,128)(2,1)S(1)}, bf16[1,32,16,256]{3,2,1,0:T(8,128)(2,1)S(1)}, u32[]{:S(2)}, u32[]{:S(2)}) collective-permute-start(bf16[1,32,16,256]{3,2,1,0:T(8,128)(2,1)S(1)} %add_convert_fusion.23), channel_id=1, source_target_pairs={{0,8},{1,9},{2,10},{3,11},{4,12},{5,13},{6,14},{7,15},{8,0},{9,1},... | collective-permute-start | bytes 786440 | tf_op jit(solution)/shard_map/ppermute | solution.py:105
  479.6 11.7 %collective-permute-start.51 = (bf16[2,32,16,256]{3,2,1,0:T(8,128)(2,1)}, bf16[2,32,16,256]{3,2,1,0:T(8,128)(2,1)S(1)}, u32[]{:S(2)}, u32[]{:S(2)}) collective-permute-start(bf16[2,32,16,256]{3,2,1,0:T(8,128)(2,1)} %get-tuple-element.362), channel_id=1, source_target_pairs={{0,2},{1,17},{2,0},{3,19},{4,6},{5,21},{6,4},{7,23},{8,10},{9,25},... | collective-permute-start | bytes 1572872 | tf_op jit(solution)/shard_map/ppermute | solution.py:105
  489.7 20.7 %collective-permute-start.52 = (bf16[8,24,16,256]{3,2,1,0:T(8,128)(2,1)}, bf16[8,24,16,256]{3,2,1,0:T(8,128)(2,1)S(1)}, u32[]{:S(2)}, u32[]{:S(2)}) collective-permute-start(bf16[8,24,16,256]{3,2,1,0:T(8,128)(2,1)} %bitcast.325), channel_id=1, source_target_pairs={{0,2},{1,17},{2,0},{3,19},{4,6},{5,21},{6,4},{7,23},{8,10},{9,25},... | collective-permute-start | bytes 4718600 | tf_op jit(solution)/shard_map/ppermute | solution.py:105
  491.3 14.5 %collective-permute-start.54 = (bf16[1,32,16,256]{3,2,1,0:T(8,128)(2,1)S(1)}, bf16[1,32,16,256]{3,2,1,0:T(8,128)(2,1)S(1)}, u32[]{:S(2)}, u32[]{:S(2)}) collective-permute-start(bf16[1,32,16,256]{3,2,1,0:T(8,128)(2,1)S(1)} %add_convert_fusion.27), channel_id=1, source_target_pairs={{0,8},{1,9},{2,10},{3,11},{4,12},{5,13},{6,14},{7,15},{8,0},{9,1},... | collective-permute-start | bytes 786440 | tf_op jit(solution)/shard_map/ppermute | solution.py:105
  493.8 21.7 %collective-permute-start.53 = (bf16[2,40,16,256]{3,2,1,0:T(8,128)(2,1)S(1)}, bf16[2,40,16,256]{3,2,1,0:T(8,128)(2,1)S(1)}, u32[]{:S(2)}, u32[]{:S(2)}) collective-permute-start(bf16[2,40,16,256]{3,2,1,0:T(8,128)(2,1)S(1)} %get-tuple-element.357), channel_id=1, source_target_pairs={{0,4},{1,5},{2,6},{3,7},{4,0},{5,1},{6,2},{7,3},{8,12},{9,13},{10,... | collective-permute-start | bytes 1966088 | tf_op jit(solution)/shard_map/ppermute | solution.py:105
  498.8 6.2 collective-permute-start.57
  516.4 18.2 %collective-permute-start.59 = (bf16[1,40,16,256]{3,2,1,0:T(8,128)(2,1)S(1)}, bf16[1,40,16,256]{3,2,1,0:T(8,128)(2,1)S(1)}, u32[]{:S(2)}, u32[]{:S(2)}) collective-permute-start(bf16[1,40,16,256]{3,2,1,0:T(8,128)(2,1)S(1)} %add_convert_fusion.21), channel_id=1, source_target_pairs={{0,8},{1,9},{2,10},{3,11},{4,12},{5,13},{6,14},{7,15},{8,0},{9,1},... | collective-permute-start | bytes 983048 | tf_op jit(solution)/shard_map/ppermute | solution.py:105
  518.2 12.1 %collective-permute-start.55 = (bf16[4,24,16,256]{3,2,1,0:T(8,128)(2,1)S(1)}, bf16[4,24,16,256]{3,2,1,0:T(8,128)(2,1)S(1)}, u32[]{:S(2)}, u32[]{:S(2)}) collective-permute-start(bf16[4,24,16,256]{3,2,1,0:T(8,128)(2,1)S(1)} %get-tuple-element.355), channel_id=1, source_target_pairs={{0,16},{1,3},{2,18},{3,1},{4,20},{5,7},{6,22},{7,5},{8,24},{9,11},... | collective-permute-start | bytes 2359304 | tf_op jit(solution)/shard_map/ppermute | solution.py:105
  530.5 10.5 %collective-permute-start.58 = (bf16[2,24,16,256]{3,2,1,0:T(8,128)(2,1)S(1)}, bf16[2,24,16,256]{3,2,1,0:T(8,128)(2,1)}, u32[]{:S(2)}, u32[]{:S(2)}) collective-permute-start(bf16[2,24,16,256]{3,2,1,0:T(8,128)(2,1)S(1)} %get-tuple-element.370), channel_id=1, source_target_pairs={{0,4},{1,5},{2,6},{3,7},{4,0},{5,1},{6,2},{7,3},{8,12},{9,13},{10,... | collective-permute-start | bytes 1179656 | tf_op jit(solution)/shard_map/ppermute | solution.py:105
  542.1 10.0 %collective-permute-start.60 = (bf16[1,24,16,256]{3,2,1,0:T(8,128)(2,1)S(1)}, bf16[1,24,16,256]{3,2,1,0:T(8,128)(2,1)S(1)}, u32[]{:S(2)}, u32[]{:S(2)}) collective-permute-start(bf16[1,24,16,256]{3,2,1,0:T(8,128)(2,1)S(1)} %add_convert_fusion.29), channel_id=1, source_target_pairs={{0,8},{1,9},{2,10},{3,11},{4,12},{5,13},{6,14},{7,15},{8,0},{9,1},... | collective-permute-start | bytes 589832 | tf_op jit(solution)/shard_map/ppermute | solution.py:105
  554.6 18.0 %all-to-all-start.5 = ((bf16[64,16,256]{2,1,0:T(8,128)(2,1)}), bf16[64,16,256]{2,1,0:T(8,128)(2,1)S(1)}, u32[]{:S(2)}, u32[]{:S(2)}) async-start(bf16[64,16,256]{2,1,0:T(8,128)(2,1)} %gather_fusion.3), calls=%async_computation.5 | async-start | bytes 1048576 | tf_op jit(solution)/shard_map/all_to_all | solution.py:327
  572.6 19.7 %all-to-all-start.6 = ((bf16[72,16,256]{2,1,0:T(8,128)(2,1)}), bf16[72,16,256]{2,1,0:T(8,128)(2,1)S(1)}, u32[]{:S(2)}, u32[]{:S(2)}) async-start(bf16[72,16,256]{2,1,0:T(8,128)(2,1)} %bitcast.88), calls=%async_computation.6 | async-start | bytes 1179648 | tf_op jit(solution)/shard_map/all_to_all | solution.py:327
  576.3 13.6 %collective-permute-start.63 = (bf16[8,8,16,256]{3,2,1,0:T(8,128)(2,1)S(1)}, bf16[8,8,16,256]{3,2,1,0:T(8,128)(2,1)S(1)}, u32[]{:S(2)}, u32[]{:S(2)}) collective-permute-start(bf16[8,8,16,256]{3,2,1,0:T(8,128)(2,1)S(1)} %bitcast.283), channel_id=1, source_target_pairs={{0,16},{16,0},{1,17},{17,1},{2,18},{18,2},{3,19},{19,3},{4,20},{20... | collective-permute-start | bytes 1572872 | tf_op jit(solution)/shard_map/ppermute | solution.py:97
  592.3 13.8 %collective-permute-start.64 = (bf16[8,9,16,256]{3,2,1,0:T(8,128)(2,1)S(1)}, bf16[8,9,16,256]{3,2,1,0:T(8,128)(2,1)S(1)}, u32[]{:S(2)}, u32[]{:S(2)}) collective-permute-start(bf16[8,9,16,256]{3,2,1,0:T(8,128)(2,1)S(1)} %bitcast.274), channel_id=1, source_target_pairs={{0,16},{16,0},{1,17},{17,1},{2,18},{18,2},{3,19},{19,3},{4,20},{20... | collective-permute-start | bytes 1769480 | tf_op jit(solution)/shard_map/ppermute | solution.py:97
  (99 other events, 755.8 us)

commit v10 on v9

--- a/solution.py
+++ b/solution.py
@@ -840,7 +840,7 @@
     dq_s, dk_s, dv_s = step((dq_s, dk_s, dv_s), cross, up)
     attn = gradient(0, ((x, x_sib), *zip((dq_s, dk_s, dv_s), sibs)))
     dq_s, dk_s, dv_s = step((dq_s, dk_s, dv_s), attn)
-    dk_c, dv_c, dq_s, dk_s, dv_s = step((dk_c, dv_c, dq_s, dk_s, dv_s), cross, up)
+    dk_c, dv_c, dq_s, dk_s, dv_s = step((dk_c, dv_c, dq_s, dk_s, dv_s), cross, up, down)
     state_back = dot_nt(dk_c, w_ck) + dot_nt(dv_c, w_cv)
     back = d_one + dot_nt(dq_s, w_sq) + dot_nt(dk_s, w_sk) + dot_nt(dv_s, w_sv)
     back, d_hidden, dq_c, dv_c = step((back, d_hidden, dq_c, dv_c), attn, cross, up)

time: 630 us -> 621 us (0.986)
  waiting for transfers between devices: 175 us -> 163 us
    ppermute x32, waiting for transfers between devices: 108 us -> 98.7 us  [swap_data(): return lax.ppermute(value, ('rep', 'shard', 'mp'), pairs)]
    unnamed x215 -> x209, local copies, waits for them, and re-layouts: 19.9 us -> 17.5 us
  transfers between devices with their start and end apart: 72 -> 72, of which waited for: 31 -> 31; matrix products, arithmetic and copies ran while one was open for 22% -> 24% of each run, Pallas kernels for 27% -> 28%
where the time goes in v10:
time: 621 us; the launch traced here: 610 us
  Pallas kernels  181 us (29%)
  waiting for transfers between devices  163 us (26%)
  starting transfers between devices  88.4 us (14%)
  other arithmetic  73 us (12%)
  matrix products  61.9 us (10%)
  local copies, waits for them, and re-layouts  40.2 us (6%)
    ppermute x32, waiting for transfers between devices, swap_data(): return lax.ppermute(value, ('rep', 'shard', 'mp'), pairs)  98.7 us
    pallas_call x7, Pallas kernels, weight_grad(): pl.pallas_call(functools.partial(weight_grad_body, count=count, outs=outs...  46.4 us
    ppermute x32, starting transfers between devices, swap_data(): return lax.ppermute(value, ('rep', 'shard', 'mp'), pairs)  39.3 us
    pallas_call x4, Pallas kernels, place(): pl.pallas_call(functools.partial(place_body, dests=dests, many=many, two=...  38 us
    dot_general x10, matrix products, dot_nt(): return lax.dot_general(a, b, NT, preferred_element_type=f32)  33.7 us
    pallas_call x2, Pallas kernels, attend_forward(): pl.pallas_call(functools.partial(attend_forward_body, causal=causal, rows...  29 us
    dot_general x9, matrix products, dot_nn(): return jnp.dot(a, b, preferred_element_type=f32)  28.3 us
    all_to_all x1, waiting for transfers between devices, first_pieces(): lax.all_to_all(cut.reshape(-1, net.rows, BS), 'shard', split_axis=0, conc...  27 us
  transfers between devices with their start and end apart: 72, of which 31 were waited for; matrix products, arithmetic and copies ran while one was open for 24% of the time, Pallas kernels for 28%

profile of v10, /device:TPU:0, one launch (start us, length us, event | category | flops | bytes accessed | tf_op | source)
XLA Modules:
  0.0 610.2 jit_solution(9575817135093284052)
XLA Ops:
  5.0 7.3 %all-to-all-start = ((bf16[136,16,256]{2,1,0:T(8,128)(2,1)}), bf16[136,16,256]{2,1,0:T(8,128)(2,1)S(1)}, u32[]{:S(2)}, u32[]{:S(2)}) async-start(bf16[136,16,256]{2,1,0:T(8,128)(2,1)} %bitcast.4), calls=%async_computation | async-start | bytes 2228224 | tf_op jit(solution)/shard_map/all_to_all | solution.py:271
  12.4 27.0 %all-to-all-done = bf16[136,16,256]{2,1,0:T(8,128)(2,1)S(1)} async-done(((bf16[136,16,256]{2,1,0:T(8,128)(2,1)}), bf16[136,16,256]{2,1,0:T(8,128)(2,1)S(1)}, u32[]{:S(2)}, u32[]{:S(2)}) %all-to-all-start) | async-done | bytes 1114144 | tf_op jit(solution)/shard_map/all_to_all | solution.py:271
  40.2 10.6 %collective-permute-done.2 = bf16[1,24,16,256]{3,2,1,0:T(8,128)(2,1)S(1)} collective-permute-done((bf16[1,24,16,256]{3,2,1,0:T(8,128)(2,1)S(1)}, bf16[1,24,16,256]{3,2,1,0:T(8,128)(2,1)S(1)}, u32[]{:S(2)}, u32[]{:S(2)}) %collective-permute-start.2) | collective-permute-done | bytes 196640 | tf_op jit(solution)/shard_map/ppermute | solution.py:105
  52.5 6.3 %collective-permute-done.3 = bf16[2,24,16,256]{3,2,1,0:T(8,128)(2,1)S(1)} collective-permute-done((bf16[2,24,16,256]{3,2,1,0:T(8,128)(2,1)S(1)}, bf16[2,24,16,256]{3,2,1,0:T(8,128)(2,1)S(1)}, u32[]{:S(2)}, u32[]{:S(2)}) %collective-permute-start.3) | collective-permute-done | bytes 393248 | tf_op jit(solution)/shard_map/ppermute | solution.py:105
  62.0 14.0 %collective-permute-done.5 = bf16[1,40,16,256]{3,2,1,0:T(8,128)(2,1)S(1)} collective-permute-done((bf16[1,40,16,256]{3,2,1,0:T(8,128)(2,1)S(1)}, bf16[1,40,16,256]{3,2,1,0:T(8,128)(2,1)S(1)}, u32[]{:S(2)}, u32[]{:S(2)}) %collective-permute-start.5) | collective-permute-done | bytes 327712 | tf_op jit(solution)/shard_map/ppermute | solution.py:105
  93.0 9.8 %collective-permute-done.8 = bf16[2,40,16,256]{3,2,1,0:T(8,128)(2,1)} collective-permute-done((bf16[2,40,16,256]{3,2,1,0:T(8,128)(2,1)}, bf16[2,40,16,256]{3,2,1,0:T(8,128)(2,1)}, u32[]{:S(2)}, u32[]{:S(2)}) %collective-permute-start.8) | collective-permute-done | bytes 655392 | tf_op jit(solution)/shard_map/ppermute | solution.py:105
  108.7 8.6 %place.4 = (bf16[4,256,1024]{2,1,0:T(8,128)(2,1)}, bf16[4,256,1024]{2,1,0:T(8,128)(2,1)}, bf16[4,256,1024]{2,1,0:T(8,128)(2,1)}) custom-call(s32[41]{0:T(128)} %add_add_fusion.4.s, bf16[8,24,16,256]{3,2,1,0:T(8,128)(2,1)} %copy-done.16, bf16[8,24,16,256]{3,2,1,0:T(8,128)(2,1)} %collective-permute-done.6.refs_1_, ...), custom_call_target="tpu_custom_call" | custom-call | flops 1048576 | bytes 1048576 | tf_op jit(solution)/shard_map/place/pallas_call | solution.py:227
  118.8 4.0 add_convert_fusion.7.v_ref
  136.7 20.1 %attend_forward.2 = (bf16[512,1024]{1,0:T(8,128)(2,1)}, f32[512,128]{1,0:T(8,128)}) custom-call(s32[1]{0:T(128)} %dynamic_slice.88.lim, bf16[512,1024]{1,0:T(8,128)(2,1)} %add_convert_fusion.8.q_ref, bf16[512,1024]{1,0:T(8,128)(2,1)} %convolution_convert_fusion.2.k_ref, bf16[512,1024]{1,0:T(8,128)(2,1)} %add_convert_fusion.7.v_ref), custom_call_target="tpu_custom_call" | custom-call | flops 1048576 | bytes 1048576 | tf_op jit(solution)/shard_map/attend_forward/pallas_call | solution.py:382
  160.1 3.4 collective-permute-done.17
  165.4 3.0 pad_maximum_fusion.1.refs_0_
  173.7 5.4 all-to-all-start.1
  179.1 10.3 %place.5 = (bf16[4,256,1024]{2,1,0:T(8,128)(2,1)}, bf16[4,256,1024]{2,1,0:T(8,128)(2,1)}, bf16[4,256,1024]{2,1,0:T(8,128)(2,1)}, bf16[4,256,1024]{2,1,0:T(8,128)(2,1)}, bf16[4,256,1024]{2,1,0:T(8,128)(2,1)}) custom-call(s32[41]{0:T(128)} %add_add_fusion.5.s, bf16[8,40,16,256]{3,2,1,0:T(8,128)(2,1)} %copy-done.5, ...), custom_call_target="tpu_custom_call" | custom-call | flops 1048576 | bytes 1048576 | tf_op jit(solution)/shard_map/place/pallas_call | solution.py:227
  189.4 3.5 fusion.23
  204.5 9.0 %attend_forward.3 = (bf16[512,1024]{1,0:T(8,128)(2,1)}, f32[512,128]{1,0:T(8,128)}) custom-call(s32[1]{0:T(128)} %dynamic_slice.88.lim, bf16[512,1024]{1,0:T(8,128)(2,1)} %add_convert_fusion.6.q_ref, bf16[128,1024]{1,0:T(8,128)(2,1)} %convolution_convert_fusion.3.k_ref, bf16[128,1024]{1,0:T(8,128)(2,1)} %fusion.4.v_ref), custom_call_target="tpu_custom_call" | custom-call | flops 1048576 | bytes 1048576 | tf_op jit(solution)/shard_map/attend_forward/pallas_call | solution.py:382
  213.5 3.4 fusion.26
  220.4 2.5 collective-permute-done.22
  222.9 2.9 pad_maximum_fusion.2.refs_0_
  229.8 4.7 all-to-all-start.2
  235.9 9.5 %place.6 = bf16[4,256,4096]{2,1,0:T(8,128)(2,1)} custom-call(s32[41]{0:T(128)} %add_add_fusion.6.s, bf16[8,32,16,256]{3,2,1,0:T(8,128)(2,1)} %pad_maximum_fusion.1.refs_0_, bf16[8,32,16,256]{3,2,1,0:T(8,128)(2,1)} %collective-permute-done.20.refs_1_, bf16[8,32,16,256]{3,2,1,0:T(8,128)(2,1)} %collective-permute-done.21.refs_2_, ...), custom_call_target="tpu_custom_call" | custom-call | flops 1048576 | bytes 1048576 | tf_op jit(solution)/shard_map/place/pallas_call | solution.py:227
  245.4 19.1 %gelu_forward.1 = (bf16[512,4096]{1,0:T(8,128)(2,1)}, bf16[512,4096]{1,0:T(8,128)(2,1)}) custom-call(bf16[512,1024]{1,0:T(8,128)(2,1)} %get-tuple-element.209.h_ref.x_own, bf16[1024,4096]{1,0:T(8,128)(2,1)} %bitcast.239, f32[1,4096]{1,0:T(1,128)} %bitcast.293), custom_call_target="tpu_custom_call" | custom-call | flops 1048576 | bytes 1048576 | tf_op jit(solution)/shard_map/gelu_forward/pallas_call | solution.py:515
  264.8 6.4 %all-to-all-done.2 = bf16[32,1,32,512]{3,2,1,0:T(8,128)(2,1)S(1)} async-done(((bf16[32,1,32,512]{3,2,1,0:T(8,128)(2,1)}), bf16[32,1,32,512]{3,2,1,0:T(8,128)(2,1)S(1)}, u32[]{:S(2)}, u32[]{:S(2)}) %all-to-all-start.2) | async-done | bytes 1048608 | tf_op jit(solution)/shard_map/all_to_all | solution.py:681
  274.2 9.6 %place.7 = bf16[16,256,1024]{2,1,0:T(8,128)(2,1)} custom-call(s32[41]{0:T(128)} %add_add_fusion.7.s, bf16[8,32,16,256]{3,2,1,0:T(8,128)(2,1)} %pad_maximum_fusion.2.refs_0_, bf16[8,32,16,256]{3,2,1,0:T(8,128)(2,1)} %collective-permute-done.24.refs_1_, bf16[8,32,16,256]{3,2,1,0:T(8,128)(2,1)} %collective-permute-done.25.refs_2_, ...), custom_call_target="tpu_custom_call" | custom-call | flops 1048576 | bytes 1048576 | tf_op jit(solution)/shard_map/place/pallas_call | solution.py:227
  283.8 8.3 %fusion.27 = f32[512,1024]{1,0:T(8,128)S(1)} fusion(bf16[512,4096]{1,0:T(8,128)(2,1)} %get-tuple-element.215.x_own, bf16[4096,1024]{1,0:T(8,128)(2,1)} %bitcast.242), kind=kOutput, calls=%fused_computation.236 | convolution fusion | flops 4294967296 | bytes 14680064 | tf_op jit(solution)/shard_map/dot_general | solution.py:43
  297.4 8.1 %multiply_convert_fusion.refs_0_ = bf16[512,4096]{1,0:T(8,128)(2,1)} fusion(bf16[512,4096]{1,0:T(8,128)(2,1)} %get-tuple-element.219, bf16[512,1024]{1,0:T(8,128)(2,1)S(1)} %convert_element_type.379.refs_0_, bf16[4096,1024]{1,0:T(8,128)(2,1)S(1)} %bitcast.245), kind=kOutput, calls=%fused_computation.6 | convolution fusion | flops 4301258752 | bytes 17825792 | tf_op jit(solution)/shard_map/dot_general | solution.py:47
  306.0 9.7 %weight_grad.7 = (bf16[8,1,32,16,256]{4,3,2,1,0:T(8,128)(2,1)}, bf16[8,1,32,16,256]{4,3,2,1,0:T(8,128)(2,1)}) custom-call(s32[41]{0:T(128)} %add_add_fusion.7.s, bf16[512,4096]{1,0:T(8,128)(2,1)} %get-tuple-element.215.x_own, bf16[512,4096]{1,0:T(8,128)(2,1)} %collective-permute-done.30.x_sib, bf16[512,1024]{1,0:T(8,128)(2,1)} %copy-done.32, ...), custom_call_target="tpu_custom_call" | custom-call | flops 1048576 | bytes 1048576 | tf_op jit(solution)/shard_map/weight_grad/pallas_call | solution.py:577
  315.9 11.0 %multiply_reduce_fusion.1 = (f32[1024]{0:T(1024)S(1)}, f32[512]{0:T(512)S(1)}, f32[512]{0:T(512)S(1)}, f32[1024]{0:T(1024)S(1)}, f32[512,1024]{1,0:T(8,128)S(1)}) fusion(f32[512,1024]{1,0:T(8,128)} %copy-done.3, f32[512]{0:T(512)S(1)} %add_rsqrt_fusion.1, f32[512]{0:T(512)S(1)} %broadcast_multiply_fusion.7, f32[1024]{0:T(1024)S(1)} %bitcast.301, ...), kind=kOutput, calls=%fused_computation.13 | convolution fusion | flops 4300207104 | bytes 18894848 | tf_op jit(solution)/shard_map/dot_general | solution.py:47
  335.2 9.7 %weight_grad.8 = (bf16[8,1,32,16,256]{4,3,2,1,0:T(8,128)(2,1)}, bf16[8,1,32,16,256]{4,3,2,1,0:T(8,128)(2,1)}) custom-call(s32[41]{0:T(128)} %add_add_fusion.6.s, bf16[512,1024]{1,0:T(8,128)(2,1)} %get-tuple-element.209.h_ref.x_own, bf16[512,1024]{1,0:T(8,128)(2,1)} %collective-permute-done.32.x_sib, bf16[512,4096]{1,0:T(8,128)(2,1)} %multiply_convert_fusion.refs_0_, ...), custom_call_target="tpu_custom_call" | custom-call | flops 1048576 | bytes 1048576 | tf_op jit(solution)/shard_map/weight_grad/pallas_call | solution.py:577
  344.9 4.3 add_convert_fusion.4
  351.6 4.7 all-to-all-start.3
  356.3 10.3 %attend_backward.2 = (bf16[512,1024]{1,0:T(8,128)(2,1)}, bf16[128,1024]{1,0:T(8,128)(2,1)}, bf16[128,1024]{1,0:T(8,128)(2,1)}) custom-call(s32[1]{0:T(128)} %dynamic_slice.88.lim, bf16[512,1024]{1,0:T(8,128)(2,1)} %add_convert_fusion.6.q_ref, bf16[128,1024]{1,0:T(8,128)(2,1)} %convolution_convert_fusion.3.k_ref, bf16[128,1024]{1,0:T(8,128)(2,1)} %fusion.4.v_ref, ...), custom_call_target="tpu_custom_call" | custom-call | flops 1048576 | bytes 1048576 | tf_op jit(solution)/shard_map/attend_backward/pallas_call | solution.py:465
  366.6 2.8 collective-permute-done.34
  369.4 4.4 multiply_reduce_fusion.2
  376.1 2.8 collective-permute-start.35
  383.8 3.0 gather_fusion.2
  386.8 4.9 all-to-all-start.4
  395.5 2.8 add_convert_fusion.14
  402.1 4.8 weight_grad.9
  406.9 4.6 weight_grad.10
  412.2 4.6 weight_grad.11
  416.8 4.8 weight_grad.12
  425.4 3.5 add_convert_fusion.2
  430.3 16.2 %attend_backward.3 = (bf16[512,1024]{1,0:T(8,128)(2,1)}, bf16[512,1024]{1,0:T(8,128)(2,1)}, bf16[512,1024]{1,0:T(8,128)(2,1)}) custom-call(s32[1]{0:T(128)} %dynamic_slice.88.lim, bf16[512,1024]{1,0:T(8,128)(2,1)} %add_convert_fusion.8.q_ref, bf16[512,1024]{1,0:T(8,128)(2,1)} %convolution_convert_fusion.2.k_ref, bf16[512,1024]{1,0:T(8,128)(2,1)} %add_convert_fusion.7.v_ref, ...), custom_call_target="tpu_custom_call" | custom-call | flops 1048576 | bytes 1048576 | tf_op jit(solution)/shard_map/attend_backward/pallas_call | solution.py:465
  446.7 7.8 %collective-permute-done.46 = bf16[4,32,16,256]{3,2,1,0:T(8,128)(2,1)S(1)} collective-permute-done((bf16[4,32,16,256]{3,2,1,0:T(8,128)(2,1)}, bf16[4,32,16,256]{3,2,1,0:T(8,128)(2,1)S(1)}, u32[]{:S(2)}, u32[]{:S(2)}) %collective-permute-start.46) | collective-permute-done | bytes 1048608 | tf_op jit(solution)/shard_map/ppermute | solution.py:105
  456.6 4.1 add_convert_fusion
  462.5 2.6 add_convert_fusion.13
  469.3 8.2 %weight_grad.13 = (bf16[8,3,8,16,256]{4,3,2,1,0:T(8,128)(2,1)}, bf16[8,3,8,16,256]{4,3,2,1,0:T(8,128)(2,1)}) custom-call(s32[41]{0:T(128)} %add_add_fusion.5.s, bf16[512,1024]{1,0:T(8,128)(2,1)} %get-tuple-element.170.x_own, bf16[512,1024]{1,0:T(8,128)(2,1)} %get-tuple-element.271.x_sib, bf16[512,1024]{1,0:T(8,128)(2,1)} %get-tuple-element.293.refs_0_, ...), custom_call_target="tpu_custom_call" | custom-call | flops 1048576 | bytes 1048576 | tf_op jit(solution)/shard_map/weight_grad/pallas_call | solution.py:577
  479.0 2.9 collective-permute-done.52
  481.9 6.5 %collective-permute-done.50 = bf16[4,40,16,256]{3,2,1,0:T(8,128)(2,1)} collective-permute-done((bf16[4,40,16,256]{3,2,1,0:T(8,128)(2,1)}, bf16[4,40,16,256]{3,2,1,0:T(8,128)(2,1)}, u32[]{:S(2)}, u32[]{:S(2)}) %collective-permute-start.50) | collective-permute-done | bytes 1310752 | tf_op jit(solution)/shard_map/ppermute | solution.py:105
  493.3 2.5 collective-permute-start.54
  505.8 5.2 collective-permute-done.54
  515.5 3.2 convert_reduce_fusion
  518.9 5.1 collective-permute-done.56
  524.3 2.5 collective-permute-start.59
  528.1 6.2 %collective-permute-done.59 = bf16[2,24,16,256]{3,2,1,0:T(8,128)(2,1)S(1)} collective-permute-done((bf16[2,24,16,256]{3,2,1,0:T(8,128)(2,1)S(1)}, bf16[2,24,16,256]{3,2,1,0:T(8,128)(2,1)S(1)}, u32[]{:S(2)}, u32[]{:S(2)}) %collective-permute-start.59) | collective-permute-done | bytes 393248 | tf_op jit(solution)/shard_map/ppermute | solution.py:105
  535.5 8.4 %collective-permute-done.61 = bf16[1,24,16,256]{3,2,1,0:T(8,128)(2,1)S(1)} collective-permute-done((bf16[1,24,16,256]{3,2,1,0:T(8,128)(2,1)S(1)}, bf16[1,24,16,256]{3,2,1,0:T(8,128)(2,1)S(1)}, u32[]{:S(2)}, u32[]{:S(2)}) %collective-permute-start.61) | collective-permute-done | bytes 196640 | tf_op jit(solution)/shard_map/ppermute | solution.py:105
  545.5 3.5 all-to-all-start.5
  552.1 10.8 %all-to-all-done.5 = bf16[64,16,256]{2,1,0:T(8,128)(2,1)S(1)} async-done(((bf16[64,16,256]{2,1,0:T(8,128)(2,1)}), bf16[64,16,256]{2,1,0:T(8,128)(2,1)S(1)}, u32[]{:S(2)}, u32[]{:S(2)}) %all-to-all-start.5) | async-done | bytes 524320 | tf_op jit(solution)/shard_map/all_to_all | solution.py:327
  562.9 3.6 all-to-all-start.6
  566.5 2.9 collective-permute-start.63
  569.4 11.8 %collective-permute-done.63.other_ref = bf16[8,8,16,256]{3,2,1,0:T(8,128)(2,1)S(1)} collective-permute-done((bf16[8,8,16,256]{3,2,1,0:T(8,128)(2,1)S(1)}, bf16[8,8,16,256]{3,2,1,0:T(8,128)(2,1)S(1)}, u32[]{:S(2)}, u32[]{:S(2)}) %collective-permute-start.63) | collective-permute-done | bytes 524320 | tf_op jit(solution)/shard_map/ppermute | solution.py:97
  582.1 3.3 collective-permute-start.64
  585.5 10.9 %shampoo.2 = (f32[1,16,256,256]{3,2,1,0:T(8,128)}, f32[1,16,256,256]{3,2,1,0:T(8,128)}, f32[1,16,256,256]{3,2,1,0:T(8,128)}, f32[1,16,256,256]{3,2,1,0:T(8,128)}) custom-call(s32[1]{0:T(128)} %bitcast.79.flag, bf16[8,8,16,256]{3,2,1,0:T(8,128)(2,1)} %bitcast.284, bf16[8,8,16,256]{3,2,1,0:T(8,128)(2,1)} %copy-done.65, f32[1,16,256,256]{3,2,1,0:T(8,128)} %w_ref.3, ...), custom_call_target="tpu_custom_call" | custom-call | flops 1048576 | bytes 1048576 | tf_op jit(solution)/shard_map/shampoo/pallas_call | solution.py:634
  598.9 10.9 %shampoo.3 = (f32[1,16,256,256]{3,2,1,0:T(8,128)}, f32[1,16,256,256]{3,2,1,0:T(8,128)}, f32[1,16,256,256]{3,2,1,0:T(8,128)}, f32[1,16,256,256]{3,2,1,0:T(8,128)}) custom-call(s32[1]{0:T(128)} %bitcast.79.flag, bf16[8,9,16,256]{3,2,1,0:T(8,128)(2,1)} %bitcast.276, ...), custom_call_target="tpu_custom_call", output_to_operand_aliasing={{0}: (8, {}), {1}: (9, {}), {2}: (10, {}), {3}: (11, {})} | custom-call | flops 1048576 | bytes 1048576 | tf_op jit(solution)/shard_map/shampoo/pallas_call | solution.py:634
  (486 shorter events, 159.2 us)
Async XLA Ops:
  5.0 34.5 %all-to-all-start = ((bf16[136,16,256]{2,1,0:T(8,128)(2,1)}), bf16[136,16,256]{2,1,0:T(8,128)(2,1)S(1)}, u32[]{:S(2)}, u32[]{:S(2)}) async-start(bf16[136,16,256]{2,1,0:T(8,128)(2,1)} %bitcast.4), calls=%async_computation | async-start | bytes 2228224 | tf_op jit(solution)/shard_map/all_to_all | solution.py:271
  40.1 10.7 %collective-permute-start.2 = (bf16[1,24,16,256]{3,2,1,0:T(8,128)(2,1)S(1)}, bf16[1,24,16,256]{3,2,1,0:T(8,128)(2,1)S(1)}, u32[]{:S(2)}, u32[]{:S(2)}) collective-permute-start(bf16[1,24,16,256]{3,2,1,0:T(8,128)(2,1)S(1)} %bitcast.270), channel_id=1, source_target_pairs={{0,8},{1,9},{2,10},{3,11},{4,12},{5,13},{6,14},{7,15},{8,0},{9,1},... | collective-permute-start | bytes 589832 | tf_op jit(solution)/shard_map/ppermute | solution.py:105
  50.9 7.8 %collective-permute-start.3 = (bf16[2,24,16,256]{3,2,1,0:T(8,128)(2,1)S(1)}, bf16[2,24,16,256]{3,2,1,0:T(8,128)(2,1)S(1)}, u32[]{:S(2)}, u32[]{:S(2)}) collective-permute-start(bf16[2,24,16,256]{3,2,1,0:T(8,128)(2,1)S(1)} %pad_maximum_fusion.19), channel_id=1, source_target_pairs={{0,16},{1,5},{2,18},{3,7},{4,20},{5,1},{6,22},{7,3},{8,24},{9,13},... | collective-permute-start | bytes 1179656 | tf_op jit(solution)/shard_map/ppermute | solution.py:105
  59.7 19.3 %collective-permute-start.4 = (bf16[4,24,16,256]{3,2,1,0:T(8,128)(2,1)}, bf16[4,24,16,256]{3,2,1,0:T(8,128)(2,1)}, u32[]{:S(2)}, u32[]{:S(2)}) collective-permute-start(bf16[4,24,16,256]{3,2,1,0:T(8,128)(2,1)} %pad_maximum_fusion.14), channel_id=1, source_target_pairs={{0,4},{1,3},{2,6},{3,1},{4,0},{5,7},{6,2},{7,5},{8,12},{9,11},{10,... | collective-permute-start | bytes 2359304 | tf_op jit(solution)/shard_map/ppermute | solution.py:105
  59.7 16.3 %collective-permute-start.5 = (bf16[1,40,16,256]{3,2,1,0:T(8,128)(2,1)S(1)}, bf16[1,40,16,256]{3,2,1,0:T(8,128)(2,1)S(1)}, u32[]{:S(2)}, u32[]{:S(2)}) collective-permute-start(bf16[1,40,16,256]{3,2,1,0:T(8,128)(2,1)S(1)} %bitcast.250), channel_id=1, source_target_pairs={{0,8},{1,9},{2,10},{3,11},{4,12},{5,13},{6,14},{7,15},{8,0},{9,1},... | collective-permute-start | bytes 983048 | tf_op jit(solution)/shard_map/ppermute | solution.py:105
  61.5 23.8 %collective-permute-start = (bf16[2,512,512]{2,1,0:T(8,128)(2,1)}, bf16[2,512,512]{2,1,0:T(8,128)(2,1)}, u32[]{:S(2)}, u32[]{:S(2)}) collective-permute-start(bf16[2,512,512]{2,1,0:T(8,128)(2,1)} %param.21), channel_id=1, source_target_pairs={{0,1},{1,0},{2,3},{3,2},{4,5},{5,4},{6,7},{7,6},{8,9},{9,8},{10,11... | collective-permute-start | bytes 3145736 | tf_op jit(solution)/shard_map/ppermute | solution.py:94
  61.5 21.0 %collective-permute-start.1 = (bf16[2,128,512]{2,1,0:T(8,128)(2,1)}, bf16[2,128,512]{2,1,0:T(8,128)(2,1)}, u32[]{:S(2)}, u32[]{:S(2)}) collective-permute-start(bf16[2,128,512]{2,1,0:T(8,128)(2,1)} %param.22), channel_id=1, source_target_pairs={{0,1},{1,0},{2,3},{3,2},{4,5},{5,4},{6,7},{7,6},{8,9},{9,8},{10,11... | collective-permute-start | bytes 786440 | tf_op jit(solution)/shard_map/ppermute | solution.py:94
  80.5 22.3 %collective-permute-start.6 = (bf16[8,24,16,256]{3,2,1,0:T(8,128)(2,1)S(1)}, bf16[8,24,16,256]{3,2,1,0:T(8,128)(2,1)}, u32[]{:S(2)}, u32[]{:S(2)}) collective-permute-start(bf16[8,24,16,256]{3,2,1,0:T(8,128)(2,1)S(1)} %pad_maximum_fusion.3.refs_0_), channel_id=1, source_target_pairs={{0,2},{1,17},{2,0},{3,19},{4,6},{5,21},{6,4},{7,23},{8,10},{9,25},... | collective-permute-start | bytes 4718600 | tf_op jit(solution)/shard_map/ppermute | solution.py:105
  81.8 21.0 %collective-permute-start.7 = (bf16[8,24,16,256]{3,2,1,0:T(8,128)(2,1)S(1)}, bf16[8,24,16,256]{3,2,1,0:T(8,128)(2,1)}, u32[]{:S(2)}, u32[]{:S(2)}) collective-permute-start(bf16[8,24,16,256]{3,2,1,0:T(8,128)(2,1)S(1)} %pad_maximum_fusion.3.refs_0_), channel_id=1, source_target_pairs={{0,1},{1,0},{2,3},{3,2},{4,5},{5,4},{6,7},{7,6},{8,9},{9,8},{10,11... | collective-permute-start | bytes 4718600 | tf_op jit(solution)/shard_map/ppermute | solution.py:94
  85.3 17.5 %collective-permute-start.8 = (bf16[2,40,16,256]{3,2,1,0:T(8,128)(2,1)}, bf16[2,40,16,256]{3,2,1,0:T(8,128)(2,1)}, u32[]{:S(2)}, u32[]{:S(2)}) collective-permute-start(bf16[2,40,16,256]{3,2,1,0:T(8,128)(2,1)} %pad_maximum_fusion.15), channel_id=1, source_target_pairs={{0,4},{1,5},{2,6},{3,7},{4,0},{5,1},{6,2},{7,3},{8,12},{9,13},{10,... | collective-permute-start | bytes 1966088 | tf_op jit(solution)/shard_map/ppermute | solution.py:105
  102.8 15.0 %collective-permute-start.10 = (bf16[1,32,16,256]{3,2,1,0:T(8,128)(2,1)S(1)}, bf16[1,32,16,256]{3,2,1,0:T(8,128)(2,1)S(1)}, u32[]{:S(2)}, u32[]{:S(2)}) collective-permute-start(bf16[1,32,16,256]{3,2,1,0:T(8,128)(2,1)S(1)} %bitcast.266), channel_id=1, source_target_pairs={{0,8},{1,9},{2,10},{3,11},{4,12},{5,13},{6,14},{7,15},{8,0},{9,1},... | collective-permute-start | bytes 786440 | tf_op jit(solution)/shard_map/ppermute | solution.py:105
  105.8 21.5 %collective-permute-start.12 = (bf16[4,40,16,256]{3,2,1,0:T(8,128)(2,1)}, bf16[4,40,16,256]{3,2,1,0:T(8,128)(2,1)}, u32[]{:S(2)}, u32[]{:S(2)}) collective-permute-start(bf16[4,40,16,256]{3,2,1,0:T(8,128)(2,1)} %pad_maximum_fusion.4), channel_id=1, source_target_pairs={{0,16},{1,3},{2,18},{3,1},{4,20},{5,7},{6,22},{7,5},{8,24},{9,11},... | collective-permute-start | bytes 3932168 | tf_op jit(solution)/shard_map/ppermute | solution.py:105
  117.8 10.8 %collective-permute-start.13 = (bf16[2,32,16,256]{3,2,1,0:T(8,128)(2,1)S(1)}, bf16[2,32,16,256]{3,2,1,0:T(8,128)(2,1)S(1)}, u32[]{:S(2)}, u32[]{:S(2)}) collective-permute-start(bf16[2,32,16,256]{3,2,1,0:T(8,128)(2,1)S(1)} %pad_maximum_fusion.17), channel_id=1, source_target_pairs={{0,2},{1,17},{2,0},{3,19},{4,6},{5,21},{6,4},{7,23},{8,10},{9,25},... | collective-permute-start | bytes 1572872 | tf_op jit(solution)/shard_map/ppermute | solution.py:105
  130.5 34.1 %collective-permute-start.14 = (bf16[8,40,16,256]{3,2,1,0:T(8,128)(2,1)S(1)}, bf16[8,40,16,256]{3,2,1,0:T(8,128)(2,1)}, u32[]{:S(2)}, u32[]{:S(2)}) collective-permute-start(bf16[8,40,16,256]{3,2,1,0:T(8,128)(2,1)S(1)} %pad_maximum_fusion.refs_0_), channel_id=1, source_target_pairs={{0,2},{1,17},{2,0},{3,19},{4,6},{5,21},{6,4},{7,23},{8,10},{9,25},... | collective-permute-start | bytes 7864328 | tf_op jit(solution)/shard_map/ppermute | solution.py:105
  132.0 32.6 %collective-permute-start.15 = (bf16[8,40,16,256]{3,2,1,0:T(8,128)(2,1)S(1)}, bf16[8,40,16,256]{3,2,1,0:T(8,128)(2,1)}, u32[]{:S(2)}, u32[]{:S(2)}) collective-permute-start(bf16[8,40,16,256]{3,2,1,0:T(8,128)(2,1)S(1)} %pad_maximum_fusion.refs_0_), channel_id=1, source_target_pairs={{0,1},{1,0},{2,3},{3,2},{4,5},{5,4},{6,7},{7,6},{8,9},{9,8},{10,11... | collective-permute-start | bytes 7864328 | tf_op jit(solution)/shard_map/ppermute | solution.py:94
  133.4 31.2 %collective-permute-start.16 = (bf16[4,32,16,256]{3,2,1,0:T(8,128)(2,1)}, bf16[4,32,16,256]{3,2,1,0:T(8,128)(2,1)}, u32[]{:S(2)}, u32[]{:S(2)}) collective-permute-start(bf16[4,32,16,256]{3,2,1,0:T(8,128)(2,1)} %pad_maximum_fusion.8), channel_id=1, source_target_pairs={{0,4},{1,5},{2,6},{3,7},{4,0},{5,1},{6,2},{7,3},{8,12},{9,13},{10,... | collective-permute-start | bytes 3145736 | tf_op jit(solution)/shard_map/ppermute | solution.py:105
  135.1 28.4 %collective-permute-start.17 = (bf16[1,32,16,256]{3,2,1,0:T(8,128)(2,1)S(1)}, bf16[1,32,16,256]{3,2,1,0:T(8,128)(2,1)}, u32[]{:S(2)}, u32[]{:S(2)}) collective-permute-start(bf16[1,32,16,256]{3,2,1,0:T(8,128)(2,1)S(1)} %bitcast.262), channel_id=1, source_target_pairs={{0,8},{1,9},{2,10},{3,11},{4,12},{5,13},{6,14},{7,15},{8,0},{9,1},... | collective-permute-start | bytes 786440 | tf_op jit(solution)/shard_map/ppermute | solution.py:105
  164.6 14.5 %collective-permute-start.18 = (bf16[8,40,16,256]{3,2,1,0:T(8,128)(2,1)}, bf16[8,40,16,256]{3,2,1,0:T(8,128)(2,1)}, u32[]{:S(2)}, u32[]{:S(2)}) collective-permute-start(bf16[8,40,16,256]{3,2,1,0:T(8,128)(2,1)} %collective-permute-done.14.refs_1_), channel_id=1, source_target_pairs={{0,1},{1,0},{2,3},{3,2},{4,5},{5,4},{6,7},{7,6},{8,9},{9,8},{10,11... | collective-permute-start | bytes 7864328 | tf_op jit(solution)/shard_map/ppermute | solution.py:94
  168.5 51.9 %collective-permute-start.20 = (bf16[8,32,16,256]{3,2,1,0:T(8,128)(2,1)}, bf16[8,32,16,256]{3,2,1,0:T(8,128)(2,1)}, u32[]{:S(2)}, u32[]{:S(2)}) collective-permute-start(bf16[8,32,16,256]{3,2,1,0:T(8,128)(2,1)} %pad_maximum_fusion.1.refs_0_), channel_id=1, source_target_pairs={{0,16},{1,3},{2,18},{3,1},{4,20},{5,7},{6,22},{7,5},{8,24},{9,11},... | collective-permute-start | bytes 6291464 | tf_op jit(solution)/shard_map/ppermute | solution.py:105
  170.0 50.4 %collective-permute-start.21 = (bf16[8,32,16,256]{3,2,1,0:T(8,128)(2,1)}, bf16[8,32,16,256]{3,2,1,0:T(8,128)(2,1)}, u32[]{:S(2)}, u32[]{:S(2)}) collective-permute-start(bf16[8,32,16,256]{3,2,1,0:T(8,128)(2,1)} %pad_maximum_fusion.1.refs_0_), channel_id=1, source_target_pairs={{0,1},{1,0},{2,3},{3,2},{4,5},{5,4},{6,7},{7,6},{8,9},{9,8},{10,11... | collective-permute-start | bytes 6291464 | tf_op jit(solution)/shard_map/ppermute | solution.py:94
  171.8 28.5 %collective-permute-start.19 = (bf16[2,32,16,256]{3,2,1,0:T(8,128)(2,1)}, bf16[2,32,16,256]{3,2,1,0:T(8,128)(2,1)}, u32[]{:S(2)}, u32[]{:S(2)}) collective-permute-start(bf16[2,32,16,256]{3,2,1,0:T(8,128)(2,1)} %pad_maximum_fusion.18), channel_id=1, source_target_pairs={{0,2},{1,17},{2,0},{3,19},{4,6},{5,21},{6,4},{7,23},{8,10},{9,25},... | collective-permute-start | bytes 1572872 | tf_op jit(solution)/shard_map/ppermute | solution.py:105
  173.7 46.7 %all-to-all-start.1 = ((bf16[2,16,32,512]{3,2,0,1:T(8,128)(2,1)}), bf16[2,16,32,512]{3,2,0,1:T(8,128)(2,1)S(1)}, u32[]{:S(2)}, u32[]{:S(2)}) async-start(bf16[2,16,32,512]{3,2,0,1:T(8,128)(2,1)} %copy.66), calls=%async_computation.1 | async-start | bytes 2097152 | tf_op jit(solution)/shard_map/all_to_all | solution.py:676
  202.5 20.4 %collective-permute-start.22 = (bf16[4,32,16,256]{3,2,1,0:T(8,128)(2,1)}, bf16[4,32,16,256]{3,2,1,0:T(8,128)(2,1)}, u32[]{:S(2)}, u32[]{:S(2)}) collective-permute-start(bf16[4,32,16,256]{3,2,1,0:T(8,128)(2,1)} %pad_maximum_fusion.9), channel_id=1, source_target_pairs={{0,16},{1,5},{2,18},{3,7},{4,20},{5,1},{6,22},{7,3},{8,24},{9,13},... | collective-permute-start | bytes 3145736 | tf_op jit(solution)/shard_map/ppermute | solution.py:105
  222.9 12.9 %collective-permute-start.23 = (bf16[8,32,16,256]{3,2,1,0:T(8,128)(2,1)}, bf16[8,32,16,256]{3,2,1,0:T(8,128)(2,1)}, u32[]{:S(2)}, u32[]{:S(2)}) collective-permute-start(bf16[8,32,16,256]{3,2,1,0:T(8,128)(2,1)} %collective-permute-done.20.refs_1_), channel_id=1, source_target_pairs={{0,1},{1,0},{2,3},{3,2},{4,5},{5,4},{6,7},{7,6},{8,9},{9,8},{10,11... | collective-permute-start | bytes 6291464 | tf_op jit(solution)/shard_map/ppermute | solution.py:94
  225.9 38.6 %collective-permute-start.24 = (bf16[8,32,16,256]{3,2,1,0:T(8,128)(2,1)}, bf16[8,32,16,256]{3,2,1,0:T(8,128)(2,1)}, u32[]{:S(2)}, u32[]{:S(2)}) collective-permute-start(bf16[8,32,16,256]{3,2,1,0:T(8,128)(2,1)} %pad_maximum_fusion.2.refs_0_), channel_id=1, source_target_pairs={{0,4},{1,3},{2,6},{3,1},{4,0},{5,7},{6,2},{7,5},{8,12},{9,11},{10,... | collective-permute-start | bytes 6291464 | tf_op jit(solution)/shard_map/ppermute | solution.py:105
  228.2 36.3 %collective-permute-start.25 = (bf16[8,32,16,256]{3,2,1,0:T(8,128)(2,1)}, bf16[8,32,16,256]{3,2,1,0:T(8,128)(2,1)}, u32[]{:S(2)}, u32[]{:S(2)}) collective-permute-start(bf16[8,32,16,256]{3,2,1,0:T(8,128)(2,1)} %pad_maximum_fusion.2.refs_0_), channel_id=1, source_target_pairs={{0,1},{1,0},{2,3},{3,2},{4,5},{5,4},{6,7},{7,6},{8,9},{9,8},{10,11... | collective-permute-start | bytes 6291464 | tf_op jit(solution)/shard_map/ppermute | solution.py:94
  229.8 41.4 %all-to-all-start.2 = ((bf16[32,1,32,512]{3,2,1,0:T(8,128)(2,1)}), bf16[32,1,32,512]{3,2,1,0:T(8,128)(2,1)S(1)}, u32[]{:S(2)}, u32[]{:S(2)}) async-start(bf16[32,1,32,512]{3,2,1,0:T(8,128)(2,1)} %bitcast.258), calls=%async_computation.2 | async-start | bytes 2097152 | tf_op jit(solution)/shard_map/all_to_all | solution.py:681
  264.5 9.6 %collective-permute-start.26 = (bf16[8,32,16,256]{3,2,1,0:T(8,128)(2,1)}, bf16[8,32,16,256]{3,2,1,0:T(8,128)(2,1)}, u32[]{:S(2)}, u32[]{:S(2)}) collective-permute-start(bf16[8,32,16,256]{3,2,1,0:T(8,128)(2,1)} %collective-permute-done.24.refs_1_), channel_id=1, source_target_pairs={{0,1},{1,0},{2,3},{3,2},{4,5},{5,4},{6,7},{7,6},{8,9},{9,8},{10,11... | collective-permute-start | bytes 6291464 | tf_op jit(solution)/shard_map/ppermute | solution.py:94
  272.8 33.2 %collective-permute-start.30 = (bf16[512,4096]{1,0:T(8,128)(2,1)}, bf16[512,4096]{1,0:T(8,128)(2,1)}, u32[]{:S(2)}, u32[]{:S(2)}) collective-permute-start(bf16[512,4096]{1,0:T(8,128)(2,1)} %get-tuple-element.215.x_own), channel_id=1, source_target_pairs={{0,1},{1,0},{2,3},{3,2},{4,5},{5,4},{6,7},{7,6},{8,9},{9,8},{10,11... | collective-permute-start | bytes 12582920 | tf_op jit(solution)/shard_map/ppermute | solution.py:94
  297.3 8.2 %collective-permute-start.28 = (bf16[512,1024]{1,0:T(8,128)(2,1)S(1)}, bf16[512,1024]{1,0:T(8,128)(2,1)}, u32[]{:S(2)}, u32[]{:S(2)}) collective-permute-start(bf16[512,1024]{1,0:T(8,128)(2,1)S(1)} %convert_element_type.379.refs_0_), channel_id=1, source_target_pairs={{0,1},{1,0},{2,3},{3,2},{4,5},{5,4},{6,7},{7,6},{8,9},{9,8},{10,11... | collective-permute-start | bytes 3145736 | tf_op jit(solution)/shard_map/ppermute | solution.py:94
  305.5 10.3 %collective-permute-start.29 = (bf16[512,4096]{1,0:T(8,128)(2,1)}, bf16[512,4096]{1,0:T(8,128)(2,1)}, u32[]{:S(2)}, u32[]{:S(2)}) collective-permute-start(bf16[512,4096]{1,0:T(8,128)(2,1)} %multiply_convert_fusion.refs_0_), channel_id=1, source_target_pairs={{0,1},{1,0},{2,3},{3,2},{4,5},{5,4},{6,7},{7,6},{8,9},{9,8},{10,11... | collective-permute-start | bytes 12582920 | tf_op jit(solution)/shard_map/ppermute | solution.py:94
  305.5 29.7 %collective-permute-start.32 = (bf16[512,1024]{1,0:T(8,128)(2,1)S(1)}, bf16[512,1024]{1,0:T(8,128)(2,1)}, u32[]{:S(2)}, u32[]{:S(2)}) collective-permute-start(bf16[512,1024]{1,0:T(8,128)(2,1)S(1)} %copy-done.8), channel_id=1, source_target_pairs={{0,1},{1,0},{2,3},{3,2},{4,5},{5,4},{6,7},{7,6},{8,9},{9,8},{10,11... | collective-permute-start | bytes 3145736 | tf_op jit(solution)/shard_map/ppermute | solution.py:94
  315.8 29.1 %collective-permute-start.33 = (bf16[8,32,16,256]{3,2,1,0:T(8,128)(2,1)}, bf16[8,32,16,256]{3,2,1,0:T(8,128)(2,1)}, u32[]{:S(2)}, u32[]{:S(2)}) collective-permute-start(bf16[8,32,16,256]{3,2,1,0:T(8,128)(2,1)} %bitcast.324), channel_id=1, source_target_pairs={{0,4},{1,3},{2,6},{3,1},{4,0},{5,7},{6,2},{7,5},{8,12},{9,11},{10,... | collective-permute-start | bytes 6291464 | tf_op jit(solution)/shard_map/ppermute | solution.py:105
  327.0 6.8 %collective-permute-start.31 = (bf16[512,512]{1,0:T(8,128)(2,1)S(1)}, bf16[512,512]{1,0:T(8,128)(2,1)S(1)}, u32[]{:S(2)}, u32[]{:S(2)}) collective-permute-start(bf16[512,512]{1,0:T(8,128)(2,1)S(1)} %constant_dynamic-slice_fusion.2), channel_id=1, source_target_pairs={{0,1},{1,0},{2,3},{3,2},{4,5},{5,4},{6,7},{7,6},{8,9},{9,8},{10,11... | collective-permute-start | bytes 1572872 | tf_op jit(solution)/shard_map/ppermute | solution.py:94
  349.2 20.2 %collective-permute-start.34 = (bf16[4,32,16,256]{3,2,1,0:T(8,128)(2,1)}, bf16[4,32,16,256]{3,2,1,0:T(8,128)(2,1)}, u32[]{:S(2)}, u32[]{:S(2)}) collective-permute-start(bf16[4,32,16,256]{3,2,1,0:T(8,128)(2,1)} %get-tuple-element.355), channel_id=1, source_target_pairs={{0,16},{1,5},{2,18},{3,7},{4,20},{5,1},{6,22},{7,3},{8,24},{9,13},... | collective-permute-start | bytes 3145736 | tf_op jit(solution)/shard_map/ppermute | solution.py:105
  351.6 30.9 %all-to-all-start.3 = ((bf16[2,16,32,512]{3,2,0,1:T(8,128)(2,1)}), bf16[2,16,32,512]{3,2,0,1:T(8,128)(2,1)S(1)}, u32[]{:S(2)}, u32[]{:S(2)}) async-start(bf16[2,16,32,512]{3,2,0,1:T(8,128)(2,1)} %copy.69), calls=%async_computation.3 | async-start | bytes 2097152 | tf_op jit(solution)/shard_map/all_to_all | solution.py:676
  376.1 6.5 %collective-permute-start.35 = (bf16[512,1024]{1,0:T(8,128)(2,1)S(1)}, bf16[512,1024]{1,0:T(8,128)(2,1)S(1)}, u32[]{:S(2)}, u32[]{:S(2)}) collective-permute-start(bf16[512,1024]{1,0:T(8,128)(2,1)S(1)} %convert_element_type.387.refs_0_), channel_id=1, source_target_pairs={{0,1},{1,0},{2,3},{3,2},{4,5},{5,4},{6,7},{7,6},{8,9},{9,8},{10,11... | collective-permute-start | bytes 3145736 | tf_op jit(solution)/shard_map/ppermute | solution.py:94
  378.9 13.4 %collective-permute-start.42 = (bf16[512,1024]{1,0:T(8,128)(2,1)}, bf16[512,1024]{1,0:T(8,128)(2,1)}, u32[]{:S(2)}, u32[]{:S(2)}) collective-permute-start(bf16[512,1024]{1,0:T(8,128)(2,1)} %get-tuple-element.192.x_own.o_ref), channel_id=1, source_target_pairs={{0,1},{1,0},{2,3},{3,2},{4,5},{5,4},{6,7},{7,6},{8,9},{9,8},{10,11... | collective-permute-start | bytes 3145736 | tf_op jit(solution)/shard_map/ppermute | solution.py:94
  379.0 45.6 %collective-permute-start.43 = (bf16[8,32,16,256]{3,2,1,0:T(8,128)(2,1)}, bf16[8,32,16,256]{3,2,1,0:T(8,128)(2,1)}, u32[]{:S(2)}, u32[]{:S(2)}) collective-permute-start(bf16[8,32,16,256]{3,2,1,0:T(8,128)(2,1)} %bitcast.61), channel_id=1, source_target_pairs={{0,16},{1,3},{2,18},{3,1},{4,20},{5,7},{6,22},{7,5},{8,24},{9,11},... | collective-permute-start | bytes 6291464 | tf_op jit(solution)/shard_map/ppermute | solution.py:105
  386.8 35.5 %all-to-all-start.4 = ((bf16[32,1,32,512]{3,2,1,0:T(8,128)(2,1)}), bf16[32,1,32,512]{3,2,1,0:T(8,128)(2,1)}, u32[]{:S(2)}, u32[]{:S(2)}) async-start(bf16[32,1,32,512]{3,2,1,0:T(8,128)(2,1)} %bitcast.256), calls=%async_computation.4 | async-start | bytes 2097152 | tf_op jit(solution)/shard_map/all_to_all | solution.py:681
  391.8 9.4 %collective-permute-start.41 = (bf16[512,1024]{1,0:T(8,128)(2,1)S(1)}, bf16[512,1024]{1,0:T(8,128)(2,1)S(1)}, u32[]{:S(2)}, u32[]{:S(2)}) collective-permute-start(bf16[512,1024]{1,0:T(8,128)(2,1)S(1)} %copy-done.23), channel_id=1, source_target_pairs={{0,1},{1,0},{2,3},{3,2},{4,5},{5,4},{6,7},{7,6},{8,9},{9,8},{10,11... | collective-permute-start | bytes 3145736 | tf_op jit(solution)/shard_map/ppermute | solution.py:94
  392.3 24.5 %collective-permute-start.36 = (bf16[512,1024]{1,0:T(8,128)(2,1)}, bf16[512,1024]{1,0:T(8,128)(2,1)}, u32[]{:S(2)}, u32[]{:S(2)}) collective-permute-start(bf16[512,1024]{1,0:T(8,128)(2,1)} %get-tuple-element.204.o_ref.x_own), channel_id=1, source_target_pairs={{0,1},{1,0},{2,3},{3,2},{4,5},{5,4},{6,7},{7,6},{8,9},{9,8},{10,11... | collective-permute-start | bytes 3145736 | tf_op jit(solution)/shard_map/ppermute | solution.py:94
  392.4 24.4 %collective-permute-start.37 = (bf16[512,1024]{1,0:T(8,128)(2,1)S(1)}, bf16[512,1024]{1,0:T(8,128)(2,1)}, u32[]{:S(2)}, u32[]{:S(2)}) collective-permute-start(bf16[512,1024]{1,0:T(8,128)(2,1)S(1)} %copy-done.19), channel_id=1, source_target_pairs={{0,1},{1,0},{2,3},{3,2},{4,5},{5,4},{6,7},{7,6},{8,9},{9,8},{10,11... | collective-permute-start | bytes 3145736 | tf_op jit(solution)/shard_map/ppermute | solution.py:94
  399.3 25.3 %collective-permute-start.44 = (bf16[2,32,16,256]{3,2,1,0:T(8,128)(2,1)}, bf16[2,32,16,256]{3,2,1,0:T(8,128)(2,1)}, u32[]{:S(2)}, u32[]{:S(2)}) collective-permute-start(bf16[2,32,16,256]{3,2,1,0:T(8,128)(2,1)} %get-tuple-element.364), channel_id=1, source_target_pairs={{0,2},{1,17},{2,0},{3,19},{4,6},{5,21},{6,4},{7,23},{8,10},{9,25},... | collective-permute-start | bytes 1572872 | tf_op jit(solution)/shard_map/ppermute | solution.py:105
  402.1 9.4 %collective-permute-start.39 = (bf16[128,1024]{1,0:T(8,128)(2,1)S(1)}, bf16[128,1024]{1,0:T(8,128)(2,1)S(1)}, u32[]{:S(2)}, u32[]{:S(2)}) collective-permute-start(bf16[128,1024]{1,0:T(8,128)(2,1)S(1)} %copy-done.43), channel_id=1, source_target_pairs={{0,1},{1,0},{2,3},{3,2},{4,5},{5,4},{6,7},{7,6},{8,9},{9,8},{10,11... | collective-permute-start | bytes 786440 | tf_op jit(solution)/shard_map/ppermute | solution.py:94
  424.6 32.0 %collective-permute-start.45 = (bf16[8,40,16,256]{3,2,1,0:T(8,128)(2,1)}, bf16[8,40,16,256]{3,2,1,0:T(8,128)(2,1)}, u32[]{:S(2)}, u32[]{:S(2)}) collective-permute-start(bf16[8,40,16,256]{3,2,1,0:T(8,128)(2,1)} %bitcast.241), channel_id=1, source_target_pairs={{0,2},{1,17},{2,0},{3,19},{4,6},{5,21},{6,4},{7,23},{8,10},{9,25},... | collective-permute-start | bytes 7864328 | tf_op jit(solution)/shard_map/ppermute | solution.py:105
  428.8 25.6 %collective-permute-start.46 = (bf16[4,32,16,256]{3,2,1,0:T(8,128)(2,1)}, bf16[4,32,16,256]{3,2,1,0:T(8,128)(2,1)S(1)}, u32[]{:S(2)}, u32[]{:S(2)}) collective-permute-start(bf16[4,32,16,256]{3,2,1,0:T(8,128)(2,1)} %get-tuple-element.353), channel_id=1, source_target_pairs={{0,4},{1,5},{2,6},{3,7},{4,0},{5,1},{6,2},{7,3},{8,12},{9,13},{10,... | collective-permute-start | bytes 3145736 | tf_op jit(solution)/shard_map/ppermute | solution.py:105
  446.5 20.2 %collective-permute-start.47 = (bf16[512,1024]{1,0:T(8,128)(2,1)}, bf16[512,1024]{1,0:T(8,128)(2,1)}, u32[]{:S(2)}, u32[]{:S(2)}) collective-permute-start(bf16[512,1024]{1,0:T(8,128)(2,1)} %get-tuple-element.293.refs_0_), channel_id=1, source_target_pairs={{0,1},{1,0},{2,3},{3,2},{4,5},{5,4},{6,7},{7,6},{8,9},{9,8},{10,11... | collective-permute-start | bytes 3145736 | tf_op jit(solution)/shard_map/ppermute | solution.py:94
  460.7 27.8 %collective-permute-start.50 = (bf16[4,40,16,256]{3,2,1,0:T(8,128)(2,1)}, bf16[4,40,16,256]{3,2,1,0:T(8,128)(2,1)}, u32[]{:S(2)}, u32[]{:S(2)}) collective-permute-start(bf16[4,40,16,256]{3,2,1,0:T(8,128)(2,1)} %get-tuple-element.351), channel_id=1, source_target_pairs={{0,16},{1,3},{2,18},{3,1},{4,20},{5,7},{6,22},{7,5},{8,24},{9,11},... | collective-permute-start | bytes 3932168 | tf_op jit(solution)/shard_map/ppermute | solution.py:105
  461.7 7.5 %collective-permute-start.48 = (bf16[512,1024]{1,0:T(8,128)(2,1)}, bf16[512,1024]{1,0:T(8,128)(2,1)}, u32[]{:S(2)}, u32[]{:S(2)}) collective-permute-start(bf16[512,1024]{1,0:T(8,128)(2,1)} %get-tuple-element.282.refs_1_), channel_id=1, source_target_pairs={{0,1},{1,0},{2,3},{3,2},{4,5},{5,4},{6,7},{7,6},{8,9},{9,8},{10,11... | collective-permute-start | bytes 3145736 | tf_op jit(solution)/shard_map/ppermute | solution.py:94
  461.7 7.5 %collective-permute-start.49 = (bf16[512,1024]{1,0:T(8,128)(2,1)S(1)}, bf16[512,1024]{1,0:T(8,128)(2,1)}, u32[]{:S(2)}, u32[]{:S(2)}) collective-permute-start(bf16[512,1024]{1,0:T(8,128)(2,1)S(1)} %copy-done.6), channel_id=1, source_target_pairs={{0,1},{1,0},{2,3},{3,2},{4,5},{5,4},{6,7},{7,6},{8,9},{9,8},{10,11... | collective-permute-start | bytes 3145736 | tf_op jit(solution)/shard_map/ppermute | solution.py:94
  465.1 16.8 %collective-permute-start.51 = (bf16[2,32,16,256]{3,2,1,0:T(8,128)(2,1)}, bf16[2,32,16,256]{3,2,1,0:T(8,128)(2,1)}, u32[]{:S(2)}, u32[]{:S(2)}) collective-permute-start(bf16[2,32,16,256]{3,2,1,0:T(8,128)(2,1)} %get-tuple-element.362), channel_id=1, source_target_pairs={{0,2},{1,17},{2,0},{3,19},{4,6},{5,21},{6,4},{7,23},{8,10},{9,25},... | collective-permute-start | bytes 1572872 | tf_op jit(solution)/shard_map/ppermute | solution.py:105
  466.7 15.2 %collective-permute-start.52 = (bf16[1,32,16,256]{3,2,1,0:T(8,128)(2,1)S(1)}, bf16[1,32,16,256]{3,2,1,0:T(8,128)(2,1)}, u32[]{:S(2)}, u32[]{:S(2)}) collective-permute-start(bf16[1,32,16,256]{3,2,1,0:T(8,128)(2,1)S(1)} %add_convert_fusion.27), channel_id=1, source_target_pairs={{0,8},{1,9},{2,10},{3,11},{4,12},{5,13},{6,14},{7,15},{8,0},{9,1},... | collective-permute-start | bytes 786440 | tf_op jit(solution)/shard_map/ppermute | solution.py:105
  477.5 28.2 %collective-permute-start.53 = (bf16[8,24,16,256]{3,2,1,0:T(8,128)(2,1)}, bf16[8,24,16,256]{3,2,1,0:T(8,128)(2,1)S(1)}, u32[]{:S(2)}, u32[]{:S(2)}) collective-permute-start(bf16[8,24,16,256]{3,2,1,0:T(8,128)(2,1)} %bitcast.325), channel_id=1, source_target_pairs={{0,2},{1,17},{2,0},{3,19},{4,6},{5,21},{6,4},{7,23},{8,10},{9,25},... | collective-permute-start | bytes 4718600 | tf_op jit(solution)/shard_map/ppermute | solution.py:105
  489.5 16.3 %collective-permute-start.55 = (bf16[1,32,16,256]{3,2,1,0:T(8,128)(2,1)S(1)}, bf16[1,32,16,256]{3,2,1,0:T(8,128)(2,1)S(1)}, u32[]{:S(2)}, u32[]{:S(2)}) collective-permute-start(bf16[1,32,16,256]{3,2,1,0:T(8,128)(2,1)S(1)} %add_convert_fusion.26), channel_id=1, source_target_pairs={{0,8},{1,9},{2,10},{3,11},{4,12},{5,13},{6,14},{7,15},{8,0},{9,1},... | collective-permute-start | bytes 786440 | tf_op jit(solution)/shard_map/ppermute | solution.py:105
  493.3 17.6 %collective-permute-start.54 = (bf16[2,40,16,256]{3,2,1,0:T(8,128)(2,1)S(1)}, bf16[2,40,16,256]{3,2,1,0:T(8,128)(2,1)S(1)}, u32[]{:S(2)}, u32[]{:S(2)}) collective-permute-start(bf16[2,40,16,256]{3,2,1,0:T(8,128)(2,1)S(1)} %get-tuple-element.359), channel_id=1, source_target_pairs={{0,4},{1,5},{2,6},{3,7},{4,0},{5,1},{6,2},{7,3},{8,12},{9,13},{10,... | collective-permute-start | bytes 1966088 | tf_op jit(solution)/shard_map/ppermute | solution.py:105
  511.0 17.1 %collective-permute-start.60 = (bf16[1,40,16,256]{3,2,1,0:T(8,128)(2,1)S(1)}, bf16[1,40,16,256]{3,2,1,0:T(8,128)(2,1)S(1)}, u32[]{:S(2)}, u32[]{:S(2)}) collective-permute-start(bf16[1,40,16,256]{3,2,1,0:T(8,128)(2,1)S(1)} %add_convert_fusion.21), channel_id=1, source_target_pairs={{0,8},{1,9},{2,10},{3,11},{4,12},{5,13},{6,14},{7,15},{8,0},{9,1},... | collective-permute-start | bytes 983048 | tf_op jit(solution)/shard_map/ppermute | solution.py:105
  511.9 12.1 %collective-permute-start.56 = (bf16[4,24,16,256]{3,2,1,0:T(8,128)(2,1)S(1)}, bf16[4,24,16,256]{3,2,1,0:T(8,128)(2,1)S(1)}, u32[]{:S(2)}, u32[]{:S(2)}) collective-permute-start(bf16[4,24,16,256]{3,2,1,0:T(8,128)(2,1)S(1)} %get-tuple-element.357), channel_id=1, source_target_pairs={{0,16},{1,3},{2,18},{3,1},{4,20},{5,7},{6,22},{7,5},{8,24},{9,11},... | collective-permute-start | bytes 2359304 | tf_op jit(solution)/shard_map/ppermute | solution.py:105
  524.3 10.1 %collective-permute-start.59 = (bf16[2,24,16,256]{3,2,1,0:T(8,128)(2,1)S(1)}, bf16[2,24,16,256]{3,2,1,0:T(8,128)(2,1)S(1)}, u32[]{:S(2)}, u32[]{:S(2)}) collective-permute-start(bf16[2,24,16,256]{3,2,1,0:T(8,128)(2,1)S(1)} %get-tuple-element.372), channel_id=1, source_target_pairs={{0,4},{1,5},{2,6},{3,7},{4,0},{5,1},{6,2},{7,3},{8,12},{9,13},{10,... | collective-permute-start | bytes 1179656 | tf_op jit(solution)/shard_map/ppermute | solution.py:105
  534.5 9.4 %collective-permute-start.61 = (bf16[1,24,16,256]{3,2,1,0:T(8,128)(2,1)S(1)}, bf16[1,24,16,256]{3,2,1,0:T(8,128)(2,1)S(1)}, u32[]{:S(2)}, u32[]{:S(2)}) collective-permute-start(bf16[1,24,16,256]{3,2,1,0:T(8,128)(2,1)S(1)} %add_convert_fusion.29), channel_id=1, source_target_pairs={{0,8},{1,9},{2,10},{3,11},{4,12},{5,13},{6,14},{7,15},{8,0},{9,1},... | collective-permute-start | bytes 589832 | tf_op jit(solution)/shard_map/ppermute | solution.py:105
  545.5 17.4 %all-to-all-start.5 = ((bf16[64,16,256]{2,1,0:T(8,128)(2,1)}), bf16[64,16,256]{2,1,0:T(8,128)(2,1)S(1)}, u32[]{:S(2)}, u32[]{:S(2)}) async-start(bf16[64,16,256]{2,1,0:T(8,128)(2,1)} %gather_fusion.3), calls=%async_computation.5 | async-start | bytes 1048576 | tf_op jit(solution)/shard_map/all_to_all | solution.py:327
  562.9 19.3 %all-to-all-start.6 = ((bf16[72,16,256]{2,1,0:T(8,128)(2,1)}), bf16[72,16,256]{2,1,0:T(8,128)(2,1)S(1)}, u32[]{:S(2)}, u32[]{:S(2)}) async-start(bf16[72,16,256]{2,1,0:T(8,128)(2,1)} %bitcast.88), calls=%async_computation.6 | async-start | bytes 1179648 | tf_op jit(solution)/shard_map/all_to_all | solution.py:327
  566.5 14.7 %collective-permute-start.63 = (bf16[8,8,16,256]{3,2,1,0:T(8,128)(2,1)S(1)}, bf16[8,8,16,256]{3,2,1,0:T(8,128)(2,1)S(1)}, u32[]{:S(2)}, u32[]{:S(2)}) collective-permute-start(bf16[8,8,16,256]{3,2,1,0:T(8,128)(2,1)S(1)} %bitcast.283), channel_id=1, source_target_pairs={{0,16},{16,0},{1,17},{17,1},{2,18},{18,2},{3,19},{19,3},{4,20},{20... | collective-permute-start | bytes 1572872 | tf_op jit(solution)/shard_map/ppermute | solution.py:97
  582.1 15.4 %collective-permute-start.64 = (bf16[8,9,16,256]{3,2,1,0:T(8,128)(2,1)S(1)}, bf16[8,9,16,256]{3,2,1,0:T(8,128)(2,1)S(1)}, u32[]{:S(2)}, u32[]{:S(2)}) collective-permute-start(bf16[8,9,16,256]{3,2,1,0:T(8,128)(2,1)S(1)} %bitcast.274), channel_id=1, source_target_pairs={{0,16},{16,0},{1,17},{17,1},{2,18},{18,2},{3,19},{19,3},{4,20},{20... | collective-permute-start | bytes 1769480 | tf_op jit(solution)/shard_map/ppermute | solution.py:97
  (96 other events, 766.4 us)

commit v11 on v10

--- a/solution.py
+++ b/solution.py
@@ -607,39 +607,42 @@
 
 def shampoo_body(flag, mine_ref, other_ref, w_ref, ls_ref, rs_ref, lr_ref, rr_ref, *refs):
     og, ol, orr, ow, g_ref = refs[-5:]
-    for k in range(mine_ref.shape[0]):
-        for plane, src in ((flag[0], mine_ref), (1 - flag[0], other_ref)):
-            row = pl.multiple_of(plane * 128 + chunk_of(k) * 16, 16)
-            g_ref[pl.ds(row, 16), :] = src[k, 0]
-    g = g_ref[...]
-    og[0, 0] = g.astype(f32)
-    ol[0, 0] = 0.5 * ls_ref[0, 0] + 0.5 * dot_nt(g, g)
-    orr[0, 0] = 0.5 * rs_ref[0, 0] + 0.5 * dot_tn(g, g)
-    r_hi, r_lo = split_low(rr_ref[0, 0])
-    i_hi, i_lo = split_low(dot_nn(g, r_hi) + dot_nn(g, r_lo))
-    l_hi, l_lo = split_low(lr_ref[0, 0])
-    d = dot_nn(l_hi, i_hi) + (dot_nn(l_hi, i_lo) + dot_nn(l_lo, i_hi))
-    mean = jnp.mean(jnp.mean(d * d, axis=1, keepdims=True), axis=0, keepdims=True)
-    ow[0, 0] = w_ref[0, 0] - (D**-0.5) * d / jnp.sqrt(mean + 1e-06)
+    for j in range(mine_ref.shape[1]):
+        for k in range(mine_ref.shape[0]):
+            for plane, src in ((flag[0], mine_ref), (1 - flag[0], other_ref)):
+                row = pl.multiple_of(plane * 128 + chunk_of(k) * 16, 16)
+                g_ref[j, pl.ds(row, 16), :] = src[k, j]
+    for j in range(mine_ref.shape[1]):
+        g = g_ref[j]
+        og[0, j] = g.astype(f32)
+        ol[0, j] = 0.5 * ls_ref[0, j] + 0.5 * dot_nt(g, g)
+        orr[0, j] = 0.5 * rs_ref[0, j] + 0.5 * dot_tn(g, g)
+        r_hi, r_lo = split_low(rr_ref[0, j])
+        i_hi, i_lo = split_low(dot_nn(g, r_hi) + dot_nn(g, r_lo))
+        l_hi, l_lo = split_low(lr_ref[0, j])
+        d = dot_nn(l_hi, i_hi) + (dot_nn(l_hi, i_lo) + dot_nn(l_lo, i_hi))
+        mean = jnp.mean(jnp.mean(d * d, axis=1, keepdims=True), axis=0, keepdims=True)
+        ow[0, j] = w_ref[0, j] - (D**-0.5) * d / jnp.sqrt(mean + 1e-06)
 
 
 def shampoo(flag, parts, *states):
     total = states[0].shape[1]
     out, first = (), 0
     for mine, other, n in parts:
-        at = first // n
-        spec = pl.BlockSpec((1, 1, BS, BS), lambda i, at=at, n=n: (0, at * n + i, 0, 0))
-        g_spec = pl.BlockSpec((mine.shape[0], 1, mine.shape[2], BS), lambda i: (0, i, 0, 0))
+        per = 2 if n % 2 == 0 else 1
+        at = first // per
+        spec = pl.BlockSpec((1, per, BS, BS), lambda i, at=at: (0, at + i, 0, 0))
+        g_spec = pl.BlockSpec((mine.shape[0], per, mine.shape[2], BS), lambda i: (0, i, 0, 0))
         anyspec = pl.BlockSpec(memory_space=pl.ANY)
         out = pl.pallas_call(
             shampoo_body,
-            grid=(n,),
+            grid=(n // per,),
             out_shape=(jax.ShapeDtypeStruct((1, total, BS, BS), f32),) * 4,
             in_specs=[pl.BlockSpec(memory_space=pltpu.SMEM), g_spec, g_spec]
             + [spec] * 5
             + [anyspec] * len(out),
             out_specs=(spec,) * 4,
-            scratch_shapes=[pltpu.VMEM((BS, BS), bf16)],
+            scratch_shapes=[pltpu.VMEM((per, BS, BS), bf16)],
             input_output_aliases={8 + k: k for k in range(len(out))},
             compiler_params=params(),
             cost_estimate=small(),

time: 621 us -> 619 us (level)
  no operation moved by 1% of the time
where the time goes in v11:
time: 619 us; the launch traced here: 609 us
  Pallas kernels  178 us (29%)
  waiting for transfers between devices  165 us (27%)
  starting transfers between devices  88.7 us (14%)
  other arithmetic  73 us (12%)
  matrix products  61.9 us (10%)
  local copies, waits for them, and re-layouts  40.2 us (6%)
    ppermute x32, waiting for transfers between devices, swap_data(): return lax.ppermute(value, ('rep', 'shard', 'mp'), pairs)  98.7 us
    pallas_call x7, Pallas kernels, weight_grad(): pl.pallas_call(functools.partial(weight_grad_body, count=count, outs=outs...  46.4 us
    ppermute x32, starting transfers between devices, swap_data(): return lax.ppermute(value, ('rep', 'shard', 'mp'), pairs)  39.3 us
    pallas_call x4, Pallas kernels, place(): pl.pallas_call(functools.partial(place_body, dests=dests, many=many, two=...  38 us
    dot_general x10, matrix products, dot_nt(): return lax.dot_general(a, b, NT, preferred_element_type=f32)  33.7 us
    pallas_call x2, Pallas kernels, attend_forward(): pl.pallas_call(functools.partial(attend_forward_body, causal=causal, rows...  29 us
    dot_general x9, matrix products, dot_nn(): return jnp.dot(a, b, preferred_element_type=f32)  28.3 us
    all_to_all x1, waiting for transfers between devices, first_pieces(): lax.all_to_all(cut.reshape(-1, net.rows, BS), 'shard', split_axis=0, conc...  27 us
  transfers between devices with their start and end apart: 72, of which 31 were waited for; matrix products, arithmetic and copies ran while one was open for 24% of the time, Pallas kernels for 28%

profile of v11, /device:TPU:0, one launch (start us, length us, event | category | flops | bytes accessed | tf_op | source)
XLA Modules:
  0.0 608.9 jit_solution(10693423687482762075)
XLA Ops:
  5.0 7.3 %all-to-all-start = ((bf16[136,16,256]{2,1,0:T(8,128)(2,1)}), bf16[136,16,256]{2,1,0:T(8,128)(2,1)S(1)}, u32[]{:S(2)}, u32[]{:S(2)}) async-start(bf16[136,16,256]{2,1,0:T(8,128)(2,1)} %bitcast.4), calls=%async_computation | async-start | bytes 2228224 | tf_op jit(solution)/shard_map/all_to_all | solution.py:271
  12.4 27.0 %all-to-all-done = bf16[136,16,256]{2,1,0:T(8,128)(2,1)S(1)} async-done(((bf16[136,16,256]{2,1,0:T(8,128)(2,1)}), bf16[136,16,256]{2,1,0:T(8,128)(2,1)S(1)}, u32[]{:S(2)}, u32[]{:S(2)}) %all-to-all-start) | async-done | bytes 1114144 | tf_op jit(solution)/shard_map/all_to_all | solution.py:271
  40.2 10.6 %collective-permute-done.2 = bf16[1,24,16,256]{3,2,1,0:T(8,128)(2,1)S(1)} collective-permute-done((bf16[1,24,16,256]{3,2,1,0:T(8,128)(2,1)S(1)}, bf16[1,24,16,256]{3,2,1,0:T(8,128)(2,1)S(1)}, u32[]{:S(2)}, u32[]{:S(2)}) %collective-permute-start.2) | collective-permute-done | bytes 196640 | tf_op jit(solution)/shard_map/ppermute | solution.py:105
  52.5 6.3 %collective-permute-done.3 = bf16[2,24,16,256]{3,2,1,0:T(8,128)(2,1)S(1)} collective-permute-done((bf16[2,24,16,256]{3,2,1,0:T(8,128)(2,1)S(1)}, bf16[2,24,16,256]{3,2,1,0:T(8,128)(2,1)S(1)}, u32[]{:S(2)}, u32[]{:S(2)}) %collective-permute-start.3) | collective-permute-done | bytes 393248 | tf_op jit(solution)/shard_map/ppermute | solution.py:105
  62.0 14.0 %collective-permute-done.5 = bf16[1,40,16,256]{3,2,1,0:T(8,128)(2,1)S(1)} collective-permute-done((bf16[1,40,16,256]{3,2,1,0:T(8,128)(2,1)S(1)}, bf16[1,40,16,256]{3,2,1,0:T(8,128)(2,1)S(1)}, u32[]{:S(2)}, u32[]{:S(2)}) %collective-permute-start.5) | collective-permute-done | bytes 327712 | tf_op jit(solution)/shard_map/ppermute | solution.py:105
  93.0 9.8 %collective-permute-done.8 = bf16[2,40,16,256]{3,2,1,0:T(8,128)(2,1)} collective-permute-done((bf16[2,40,16,256]{3,2,1,0:T(8,128)(2,1)}, bf16[2,40,16,256]{3,2,1,0:T(8,128)(2,1)}, u32[]{:S(2)}, u32[]{:S(2)}) %collective-permute-start.8) | collective-permute-done | bytes 655392 | tf_op jit(solution)/shard_map/ppermute | solution.py:105
  108.7 8.6 %place.4 = (bf16[4,256,1024]{2,1,0:T(8,128)(2,1)}, bf16[4,256,1024]{2,1,0:T(8,128)(2,1)}, bf16[4,256,1024]{2,1,0:T(8,128)(2,1)}) custom-call(s32[41]{0:T(128)} %add_add_fusion.4.s, bf16[8,24,16,256]{3,2,1,0:T(8,128)(2,1)} %copy-done.16, bf16[8,24,16,256]{3,2,1,0:T(8,128)(2,1)} %collective-permute-done.6.refs_1_, ...), custom_call_target="tpu_custom_call" | custom-call | flops 1048576 | bytes 1048576 | tf_op jit(solution)/shard_map/place/pallas_call | solution.py:227
  118.8 4.0 add_convert_fusion.7.v_ref
  136.7 20.1 %attend_forward.2 = (bf16[512,1024]{1,0:T(8,128)(2,1)}, f32[512,128]{1,0:T(8,128)}) custom-call(s32[1]{0:T(128)} %dynamic_slice.88.lim, bf16[512,1024]{1,0:T(8,128)(2,1)} %add_convert_fusion.8.q_ref, bf16[512,1024]{1,0:T(8,128)(2,1)} %convolution_convert_fusion.2.k_ref, bf16[512,1024]{1,0:T(8,128)(2,1)} %add_convert_fusion.7.v_ref), custom_call_target="tpu_custom_call" | custom-call | flops 1048576 | bytes 1048576 | tf_op jit(solution)/shard_map/attend_forward/pallas_call | solution.py:382
  160.1 3.4 collective-permute-done.17
  165.4 3.0 pad_maximum_fusion.1.refs_0_
  173.7 5.4 all-to-all-start.1
  179.1 10.3 %place.5 = (bf16[4,256,1024]{2,1,0:T(8,128)(2,1)}, bf16[4,256,1024]{2,1,0:T(8,128)(2,1)}, bf16[4,256,1024]{2,1,0:T(8,128)(2,1)}, bf16[4,256,1024]{2,1,0:T(8,128)(2,1)}, bf16[4,256,1024]{2,1,0:T(8,128)(2,1)}) custom-call(s32[41]{0:T(128)} %add_add_fusion.5.s, bf16[8,40,16,256]{3,2,1,0:T(8,128)(2,1)} %copy-done.5, ...), custom_call_target="tpu_custom_call" | custom-call | flops 1048576 | bytes 1048576 | tf_op jit(solution)/shard_map/place/pallas_call | solution.py:227
  189.4 3.5 fusion.23
  204.5 9.0 %attend_forward.3 = (bf16[512,1024]{1,0:T(8,128)(2,1)}, f32[512,128]{1,0:T(8,128)}) custom-call(s32[1]{0:T(128)} %dynamic_slice.88.lim, bf16[512,1024]{1,0:T(8,128)(2,1)} %add_convert_fusion.6.q_ref, bf16[128,1024]{1,0:T(8,128)(2,1)} %convolution_convert_fusion.3.k_ref, bf16[128,1024]{1,0:T(8,128)(2,1)} %fusion.4.v_ref), custom_call_target="tpu_custom_call" | custom-call | flops 1048576 | bytes 1048576 | tf_op jit(solution)/shard_map/attend_forward/pallas_call | solution.py:382
  213.5 3.4 fusion.26
  220.4 2.5 collective-permute-done.22
  222.9 2.9 pad_maximum_fusion.2.refs_0_
  229.8 4.7 all-to-all-start.2
  235.9 9.5 %place.6 = bf16[4,256,4096]{2,1,0:T(8,128)(2,1)} custom-call(s32[41]{0:T(128)} %add_add_fusion.6.s, bf16[8,32,16,256]{3,2,1,0:T(8,128)(2,1)} %pad_maximum_fusion.1.refs_0_, bf16[8,32,16,256]{3,2,1,0:T(8,128)(2,1)} %collective-permute-done.20.refs_1_, bf16[8,32,16,256]{3,2,1,0:T(8,128)(2,1)} %collective-permute-done.21.refs_2_, ...), custom_call_target="tpu_custom_call" | custom-call | flops 1048576 | bytes 1048576 | tf_op jit(solution)/shard_map/place/pallas_call | solution.py:227
  245.4 19.1 %gelu_forward.1 = (bf16[512,4096]{1,0:T(8,128)(2,1)}, bf16[512,4096]{1,0:T(8,128)(2,1)}) custom-call(bf16[512,1024]{1,0:T(8,128)(2,1)} %get-tuple-element.209.h_ref.x_own, bf16[1024,4096]{1,0:T(8,128)(2,1)} %bitcast.239, f32[1,4096]{1,0:T(1,128)} %bitcast.293), custom_call_target="tpu_custom_call" | custom-call | flops 1048576 | bytes 1048576 | tf_op jit(solution)/shard_map/gelu_forward/pallas_call | solution.py:515
  264.8 6.4 %all-to-all-done.2 = bf16[32,1,32,512]{3,2,1,0:T(8,128)(2,1)S(1)} async-done(((bf16[32,1,32,512]{3,2,1,0:T(8,128)(2,1)}), bf16[32,1,32,512]{3,2,1,0:T(8,128)(2,1)S(1)}, u32[]{:S(2)}, u32[]{:S(2)}) %all-to-all-start.2) | async-done | bytes 1048608 | tf_op jit(solution)/shard_map/all_to_all | solution.py:684
  274.2 9.6 %place.7 = bf16[16,256,1024]{2,1,0:T(8,128)(2,1)} custom-call(s32[41]{0:T(128)} %add_add_fusion.7.s, bf16[8,32,16,256]{3,2,1,0:T(8,128)(2,1)} %pad_maximum_fusion.2.refs_0_, bf16[8,32,16,256]{3,2,1,0:T(8,128)(2,1)} %collective-permute-done.24.refs_1_, bf16[8,32,16,256]{3,2,1,0:T(8,128)(2,1)} %collective-permute-done.25.refs_2_, ...), custom_call_target="tpu_custom_call" | custom-call | flops 1048576 | bytes 1048576 | tf_op jit(solution)/shard_map/place/pallas_call | solution.py:227
  283.8 8.3 %fusion.27 = f32[512,1024]{1,0:T(8,128)S(1)} fusion(bf16[512,4096]{1,0:T(8,128)(2,1)} %get-tuple-element.215.x_own, bf16[4096,1024]{1,0:T(8,128)(2,1)} %bitcast.242), kind=kOutput, calls=%fused_computation.236 | convolution fusion | flops 4294967296 | bytes 14680064 | tf_op jit(solution)/shard_map/dot_general | solution.py:43
  297.4 8.1 %multiply_convert_fusion.refs_0_ = bf16[512,4096]{1,0:T(8,128)(2,1)} fusion(bf16[512,4096]{1,0:T(8,128)(2,1)} %get-tuple-element.219, bf16[512,1024]{1,0:T(8,128)(2,1)S(1)} %convert_element_type.379.refs_0_, bf16[4096,1024]{1,0:T(8,128)(2,1)S(1)} %bitcast.245), kind=kOutput, calls=%fused_computation.6 | convolution fusion | flops 4301258752 | bytes 17825792 | tf_op jit(solution)/shard_map/dot_general | solution.py:47
  306.0 9.7 %weight_grad.7 = (bf16[8,1,32,16,256]{4,3,2,1,0:T(8,128)(2,1)}, bf16[8,1,32,16,256]{4,3,2,1,0:T(8,128)(2,1)}) custom-call(s32[41]{0:T(128)} %add_add_fusion.7.s, bf16[512,4096]{1,0:T(8,128)(2,1)} %get-tuple-element.215.x_own, bf16[512,4096]{1,0:T(8,128)(2,1)} %collective-permute-done.30.x_sib, bf16[512,1024]{1,0:T(8,128)(2,1)} %copy-done.32, ...), custom_call_target="tpu_custom_call" | custom-call | flops 1048576 | bytes 1048576 | tf_op jit(solution)/shard_map/weight_grad/pallas_call | solution.py:577
  315.9 11.0 %multiply_reduce_fusion.1 = (f32[1024]{0:T(1024)S(1)}, f32[512]{0:T(512)S(1)}, f32[512]{0:T(512)S(1)}, f32[1024]{0:T(1024)S(1)}, f32[512,1024]{1,0:T(8,128)S(1)}) fusion(f32[512,1024]{1,0:T(8,128)} %copy-done.3, f32[512]{0:T(512)S(1)} %add_rsqrt_fusion.1, f32[512]{0:T(512)S(1)} %broadcast_multiply_fusion.7, f32[1024]{0:T(1024)S(1)} %bitcast.301, ...), kind=kOutput, calls=%fused_computation.13 | convolution fusion | flops 4300207104 | bytes 18894848 | tf_op jit(solution)/shard_map/dot_general | solution.py:47
  335.2 9.7 %weight_grad.8 = (bf16[8,1,32,16,256]{4,3,2,1,0:T(8,128)(2,1)}, bf16[8,1,32,16,256]{4,3,2,1,0:T(8,128)(2,1)}) custom-call(s32[41]{0:T(128)} %add_add_fusion.6.s, bf16[512,1024]{1,0:T(8,128)(2,1)} %get-tuple-element.209.h_ref.x_own, bf16[512,1024]{1,0:T(8,128)(2,1)} %collective-permute-done.32.x_sib, bf16[512,4096]{1,0:T(8,128)(2,1)} %multiply_convert_fusion.refs_0_, ...), custom_call_target="tpu_custom_call" | custom-call | flops 1048576 | bytes 1048576 | tf_op jit(solution)/shard_map/weight_grad/pallas_call | solution.py:577
  344.9 4.3 add_convert_fusion.4
  351.6 4.7 all-to-all-start.3
  356.3 10.3 %attend_backward.2 = (bf16[512,1024]{1,0:T(8,128)(2,1)}, bf16[128,1024]{1,0:T(8,128)(2,1)}, bf16[128,1024]{1,0:T(8,128)(2,1)}) custom-call(s32[1]{0:T(128)} %dynamic_slice.88.lim, bf16[512,1024]{1,0:T(8,128)(2,1)} %add_convert_fusion.6.q_ref, bf16[128,1024]{1,0:T(8,128)(2,1)} %convolution_convert_fusion.3.k_ref, bf16[128,1024]{1,0:T(8,128)(2,1)} %fusion.4.v_ref, ...), custom_call_target="tpu_custom_call" | custom-call | flops 1048576 | bytes 1048576 | tf_op jit(solution)/shard_map/attend_backward/pallas_call | solution.py:465
  366.6 2.8 collective-permute-done.34
  369.4 4.4 multiply_reduce_fusion.2
  376.1 2.8 collective-permute-start.35
  383.8 3.0 gather_fusion.2
  386.8 4.9 all-to-all-start.4
  395.5 2.8 add_convert_fusion.14
  402.1 4.8 weight_grad.9
  406.9 4.6 weight_grad.10
  412.2 4.6 weight_grad.11
  416.8 4.8 weight_grad.12
  425.4 3.5 add_convert_fusion.2
  430.3 16.2 %attend_backward.3 = (bf16[512,1024]{1,0:T(8,128)(2,1)}, bf16[512,1024]{1,0:T(8,128)(2,1)}, bf16[512,1024]{1,0:T(8,128)(2,1)}) custom-call(s32[1]{0:T(128)} %dynamic_slice.88.lim, bf16[512,1024]{1,0:T(8,128)(2,1)} %add_convert_fusion.8.q_ref, bf16[512,1024]{1,0:T(8,128)(2,1)} %convolution_convert_fusion.2.k_ref, bf16[512,1024]{1,0:T(8,128)(2,1)} %add_convert_fusion.7.v_ref, ...), custom_call_target="tpu_custom_call" | custom-call | flops 1048576 | bytes 1048576 | tf_op jit(solution)/shard_map/attend_backward/pallas_call | solution.py:465
  446.7 7.8 %collective-permute-done.46 = bf16[4,32,16,256]{3,2,1,0:T(8,128)(2,1)S(1)} collective-permute-done((bf16[4,32,16,256]{3,2,1,0:T(8,128)(2,1)}, bf16[4,32,16,256]{3,2,1,0:T(8,128)(2,1)S(1)}, u32[]{:S(2)}, u32[]{:S(2)}) %collective-permute-start.46) | collective-permute-done | bytes 1048608 | tf_op jit(solution)/shard_map/ppermute | solution.py:105
  456.6 4.1 add_convert_fusion
  462.5 2.6 add_convert_fusion.13
  469.3 8.2 %weight_grad.13 = (bf16[8,3,8,16,256]{4,3,2,1,0:T(8,128)(2,1)}, bf16[8,3,8,16,256]{4,3,2,1,0:T(8,128)(2,1)}) custom-call(s32[41]{0:T(128)} %add_add_fusion.5.s, bf16[512,1024]{1,0:T(8,128)(2,1)} %get-tuple-element.170.x_own, bf16[512,1024]{1,0:T(8,128)(2,1)} %get-tuple-element.271.x_sib, bf16[512,1024]{1,0:T(8,128)(2,1)} %get-tuple-element.293.refs_0_, ...), custom_call_target="tpu_custom_call" | custom-call | flops 1048576 | bytes 1048576 | tf_op jit(solution)/shard_map/weight_grad/pallas_call | solution.py:577
  479.0 2.9 collective-permute-done.52
  481.9 6.5 %collective-permute-done.50 = bf16[4,40,16,256]{3,2,1,0:T(8,128)(2,1)} collective-permute-done((bf16[4,40,16,256]{3,2,1,0:T(8,128)(2,1)}, bf16[4,40,16,256]{3,2,1,0:T(8,128)(2,1)}, u32[]{:S(2)}, u32[]{:S(2)}) %collective-permute-start.50) | collective-permute-done | bytes 1310752 | tf_op jit(solution)/shard_map/ppermute | solution.py:105
  493.3 2.5 collective-permute-start.54
  505.8 5.2 collective-permute-done.54
  515.5 3.2 convert_reduce_fusion
  518.9 5.1 collective-permute-done.56
  528.1 6.2 %collective-permute-done.59 = bf16[2,24,16,256]{3,2,1,0:T(8,128)(2,1)S(1)} collective-permute-done((bf16[2,24,16,256]{3,2,1,0:T(8,128)(2,1)S(1)}, bf16[2,24,16,256]{3,2,1,0:T(8,128)(2,1)S(1)}, u32[]{:S(2)}, u32[]{:S(2)}) %collective-permute-start.59) | collective-permute-done | bytes 393248 | tf_op jit(solution)/shard_map/ppermute | solution.py:105
  535.5 8.4 %collective-permute-done.61 = bf16[1,24,16,256]{3,2,1,0:T(8,128)(2,1)S(1)} collective-permute-done((bf16[1,24,16,256]{3,2,1,0:T(8,128)(2,1)S(1)}, bf16[1,24,16,256]{3,2,1,0:T(8,128)(2,1)S(1)}, u32[]{:S(2)}, u32[]{:S(2)}) %collective-permute-start.61) | collective-permute-done | bytes 196640 | tf_op jit(solution)/shard_map/ppermute | solution.py:105
  545.5 3.5 all-to-all-start.5
  552.1 10.8 %all-to-all-done.5 = bf16[64,16,256]{2,1,0:T(8,128)(2,1)S(1)} async-done(((bf16[64,16,256]{2,1,0:T(8,128)(2,1)}), bf16[64,16,256]{2,1,0:T(8,128)(2,1)S(1)}, u32[]{:S(2)}, u32[]{:S(2)}) %all-to-all-start.5) | async-done | bytes 524320 | tf_op jit(solution)/shard_map/all_to_all | solution.py:327
  562.9 3.9 all-to-all-start.6
  566.8 2.9 collective-permute-start.63
  569.7 11.8 %collective-permute-done.63.other_ref = bf16[8,8,16,256]{3,2,1,0:T(8,128)(2,1)S(1)} collective-permute-done((bf16[8,8,16,256]{3,2,1,0:T(8,128)(2,1)S(1)}, bf16[8,8,16,256]{3,2,1,0:T(8,128)(2,1)S(1)}, u32[]{:S(2)}, u32[]{:S(2)}) %collective-permute-start.63) | collective-permute-done | bytes 524320 | tf_op jit(solution)/shard_map/ppermute | solution.py:97
  582.3 3.3 collective-permute-start.64
  585.7 9.3 %shampoo.2 = (f32[1,16,256,256]{3,2,1,0:T(8,128)}, f32[1,16,256,256]{3,2,1,0:T(8,128)}, f32[1,16,256,256]{3,2,1,0:T(8,128)}, f32[1,16,256,256]{3,2,1,0:T(8,128)}) custom-call(s32[1]{0:T(128)} %bitcast.79.flag, bf16[8,8,16,256]{3,2,1,0:T(8,128)(2,1)} %bitcast.284, bf16[8,8,16,256]{3,2,1,0:T(8,128)(2,1)} %copy-done.65, f32[1,16,256,256]{3,2,1,0:T(8,128)} %w_ref.3, ...), custom_call_target="tpu_custom_call" | custom-call | flops 1048576 | bytes 1048576 | tf_op jit(solution)/shard_map/shampoo/pallas_call | solution.py:637
  595.1 2.6 collective-permute-done.64.other_ref
  599.1 9.4 %shampoo.3 = (f32[1,16,256,256]{3,2,1,0:T(8,128)}, f32[1,16,256,256]{3,2,1,0:T(8,128)}, f32[1,16,256,256]{3,2,1,0:T(8,128)}, f32[1,16,256,256]{3,2,1,0:T(8,128)}) custom-call(s32[1]{0:T(128)} %bitcast.79.flag, bf16[8,9,16,256]{3,2,1,0:T(8,128)(2,1)} %bitcast.276, ...), custom_call_target="tpu_custom_call", output_to_operand_aliasing={{0}: (8, {}), {1}: (9, {}), {2}: (10, {}), {3}: (11, {})} | custom-call | flops 1048576 | bytes 1048576 | tf_op jit(solution)/shard_map/shampoo/pallas_call | solution.py:637
  (486 shorter events, 160.4 us)
Async XLA Ops:
  5.0 34.5 %all-to-all-start = ((bf16[136,16,256]{2,1,0:T(8,128)(2,1)}), bf16[136,16,256]{2,1,0:T(8,128)(2,1)S(1)}, u32[]{:S(2)}, u32[]{:S(2)}) async-start(bf16[136,16,256]{2,1,0:T(8,128)(2,1)} %bitcast.4), calls=%async_computation | async-start | bytes 2228224 | tf_op jit(solution)/shard_map/all_to_all | solution.py:271
  40.1 10.7 %collective-permute-start.2 = (bf16[1,24,16,256]{3,2,1,0:T(8,128)(2,1)S(1)}, bf16[1,24,16,256]{3,2,1,0:T(8,128)(2,1)S(1)}, u32[]{:S(2)}, u32[]{:S(2)}) collective-permute-start(bf16[1,24,16,256]{3,2,1,0:T(8,128)(2,1)S(1)} %bitcast.270), channel_id=1, source_target_pairs={{0,8},{1,9},{2,10},{3,11},{4,12},{5,13},{6,14},{7,15},{8,0},{9,1},... | collective-permute-start | bytes 589832 | tf_op jit(solution)/shard_map/ppermute | solution.py:105
  50.9 7.8 %collective-permute-start.3 = (bf16[2,24,16,256]{3,2,1,0:T(8,128)(2,1)S(1)}, bf16[2,24,16,256]{3,2,1,0:T(8,128)(2,1)S(1)}, u32[]{:S(2)}, u32[]{:S(2)}) collective-permute-start(bf16[2,24,16,256]{3,2,1,0:T(8,128)(2,1)S(1)} %pad_maximum_fusion.19), channel_id=1, source_target_pairs={{0,16},{1,5},{2,18},{3,7},{4,20},{5,1},{6,22},{7,3},{8,24},{9,13},... | collective-permute-start | bytes 1179656 | tf_op jit(solution)/shard_map/ppermute | solution.py:105
  59.7 19.3 %collective-permute-start.4 = (bf16[4,24,16,256]{3,2,1,0:T(8,128)(2,1)}, bf16[4,24,16,256]{3,2,1,0:T(8,128)(2,1)}, u32[]{:S(2)}, u32[]{:S(2)}) collective-permute-start(bf16[4,24,16,256]{3,2,1,0:T(8,128)(2,1)} %pad_maximum_fusion.14), channel_id=1, source_target_pairs={{0,4},{1,3},{2,6},{3,1},{4,0},{5,7},{6,2},{7,5},{8,12},{9,11},{10,... | collective-permute-start | bytes 2359304 | tf_op jit(solution)/shard_map/ppermute | solution.py:105
  59.7 16.3 %collective-permute-start.5 = (bf16[1,40,16,256]{3,2,1,0:T(8,128)(2,1)S(1)}, bf16[1,40,16,256]{3,2,1,0:T(8,128)(2,1)S(1)}, u32[]{:S(2)}, u32[]{:S(2)}) collective-permute-start(bf16[1,40,16,256]{3,2,1,0:T(8,128)(2,1)S(1)} %bitcast.250), channel_id=1, source_target_pairs={{0,8},{1,9},{2,10},{3,11},{4,12},{5,13},{6,14},{7,15},{8,0},{9,1},... | collective-permute-start | bytes 983048 | tf_op jit(solution)/shard_map/ppermute | solution.py:105
  61.5 23.8 %collective-permute-start = (bf16[2,512,512]{2,1,0:T(8,128)(2,1)}, bf16[2,512,512]{2,1,0:T(8,128)(2,1)}, u32[]{:S(2)}, u32[]{:S(2)}) collective-permute-start(bf16[2,512,512]{2,1,0:T(8,128)(2,1)} %param.21), channel_id=1, source_target_pairs={{0,1},{1,0},{2,3},{3,2},{4,5},{5,4},{6,7},{7,6},{8,9},{9,8},{10,11... | collective-permute-start | bytes 3145736 | tf_op jit(solution)/shard_map/ppermute | solution.py:94
  61.5 21.0 %collective-permute-start.1 = (bf16[2,128,512]{2,1,0:T(8,128)(2,1)}, bf16[2,128,512]{2,1,0:T(8,128)(2,1)}, u32[]{:S(2)}, u32[]{:S(2)}) collective-permute-start(bf16[2,128,512]{2,1,0:T(8,128)(2,1)} %param.22), channel_id=1, source_target_pairs={{0,1},{1,0},{2,3},{3,2},{4,5},{5,4},{6,7},{7,6},{8,9},{9,8},{10,11... | collective-permute-start | bytes 786440 | tf_op jit(solution)/shard_map/ppermute | solution.py:94
  80.5 22.3 %collective-permute-start.6 = (bf16[8,24,16,256]{3,2,1,0:T(8,128)(2,1)S(1)}, bf16[8,24,16,256]{3,2,1,0:T(8,128)(2,1)}, u32[]{:S(2)}, u32[]{:S(2)}) collective-permute-start(bf16[8,24,16,256]{3,2,1,0:T(8,128)(2,1)S(1)} %pad_maximum_fusion.3.refs_0_), channel_id=1, source_target_pairs={{0,2},{1,17},{2,0},{3,19},{4,6},{5,21},{6,4},{7,23},{8,10},{9,25},... | collective-permute-start | bytes 4718600 | tf_op jit(solution)/shard_map/ppermute | solution.py:105
  81.8 21.0 %collective-permute-start.7 = (bf16[8,24,16,256]{3,2,1,0:T(8,128)(2,1)S(1)}, bf16[8,24,16,256]{3,2,1,0:T(8,128)(2,1)}, u32[]{:S(2)}, u32[]{:S(2)}) collective-permute-start(bf16[8,24,16,256]{3,2,1,0:T(8,128)(2,1)S(1)} %pad_maximum_fusion.3.refs_0_), channel_id=1, source_target_pairs={{0,1},{1,0},{2,3},{3,2},{4,5},{5,4},{6,7},{7,6},{8,9},{9,8},{10,11... | collective-permute-start | bytes 4718600 | tf_op jit(solution)/shard_map/ppermute | solution.py:94
  85.3 17.5 %collective-permute-start.8 = (bf16[2,40,16,256]{3,2,1,0:T(8,128)(2,1)}, bf16[2,40,16,256]{3,2,1,0:T(8,128)(2,1)}, u32[]{:S(2)}, u32[]{:S(2)}) collective-permute-start(bf16[2,40,16,256]{3,2,1,0:T(8,128)(2,1)} %pad_maximum_fusion.15), channel_id=1, source_target_pairs={{0,4},{1,5},{2,6},{3,7},{4,0},{5,1},{6,2},{7,3},{8,12},{9,13},{10,... | collective-permute-start | bytes 1966088 | tf_op jit(solution)/shard_map/ppermute | solution.py:105
  102.8 15.0 %collective-permute-start.10 = (bf16[1,32,16,256]{3,2,1,0:T(8,128)(2,1)S(1)}, bf16[1,32,16,256]{3,2,1,0:T(8,128)(2,1)S(1)}, u32[]{:S(2)}, u32[]{:S(2)}) collective-permute-start(bf16[1,32,16,256]{3,2,1,0:T(8,128)(2,1)S(1)} %bitcast.266), channel_id=1, source_target_pairs={{0,8},{1,9},{2,10},{3,11},{4,12},{5,13},{6,14},{7,15},{8,0},{9,1},... | collective-permute-start | bytes 786440 | tf_op jit(solution)/shard_map/ppermute | solution.py:105
  105.8 21.5 %collective-permute-start.12 = (bf16[4,40,16,256]{3,2,1,0:T(8,128)(2,1)}, bf16[4,40,16,256]{3,2,1,0:T(8,128)(2,1)}, u32[]{:S(2)}, u32[]{:S(2)}) collective-permute-start(bf16[4,40,16,256]{3,2,1,0:T(8,128)(2,1)} %pad_maximum_fusion.4), channel_id=1, source_target_pairs={{0,16},{1,3},{2,18},{3,1},{4,20},{5,7},{6,22},{7,5},{8,24},{9,11},... | collective-permute-start | bytes 3932168 | tf_op jit(solution)/shard_map/ppermute | solution.py:105
  117.8 10.8 %collective-permute-start.13 = (bf16[2,32,16,256]{3,2,1,0:T(8,128)(2,1)S(1)}, bf16[2,32,16,256]{3,2,1,0:T(8,128)(2,1)S(1)}, u32[]{:S(2)}, u32[]{:S(2)}) collective-permute-start(bf16[2,32,16,256]{3,2,1,0:T(8,128)(2,1)S(1)} %pad_maximum_fusion.17), channel_id=1, source_target_pairs={{0,2},{1,17},{2,0},{3,19},{4,6},{5,21},{6,4},{7,23},{8,10},{9,25},... | collective-permute-start | bytes 1572872 | tf_op jit(solution)/shard_map/ppermute | solution.py:105
  130.5 34.1 %collective-permute-start.14 = (bf16[8,40,16,256]{3,2,1,0:T(8,128)(2,1)S(1)}, bf16[8,40,16,256]{3,2,1,0:T(8,128)(2,1)}, u32[]{:S(2)}, u32[]{:S(2)}) collective-permute-start(bf16[8,40,16,256]{3,2,1,0:T(8,128)(2,1)S(1)} %pad_maximum_fusion.refs_0_), channel_id=1, source_target_pairs={{0,2},{1,17},{2,0},{3,19},{4,6},{5,21},{6,4},{7,23},{8,10},{9,25},... | collective-permute-start | bytes 7864328 | tf_op jit(solution)/shard_map/ppermute | solution.py:105
  132.0 32.6 %collective-permute-start.15 = (bf16[8,40,16,256]{3,2,1,0:T(8,128)(2,1)S(1)}, bf16[8,40,16,256]{3,2,1,0:T(8,128)(2,1)}, u32[]{:S(2)}, u32[]{:S(2)}) collective-permute-start(bf16[8,40,16,256]{3,2,1,0:T(8,128)(2,1)S(1)} %pad_maximum_fusion.refs_0_), channel_id=1, source_target_pairs={{0,1},{1,0},{2,3},{3,2},{4,5},{5,4},{6,7},{7,6},{8,9},{9,8},{10,11... | collective-permute-start | bytes 7864328 | tf_op jit(solution)/shard_map/ppermute | solution.py:94
  133.4 31.2 %collective-permute-start.16 = (bf16[4,32,16,256]{3,2,1,0:T(8,128)(2,1)}, bf16[4,32,16,256]{3,2,1,0:T(8,128)(2,1)}, u32[]{:S(2)}, u32[]{:S(2)}) collective-permute-start(bf16[4,32,16,256]{3,2,1,0:T(8,128)(2,1)} %pad_maximum_fusion.8), channel_id=1, source_target_pairs={{0,4},{1,5},{2,6},{3,7},{4,0},{5,1},{6,2},{7,3},{8,12},{9,13},{10,... | collective-permute-start | bytes 3145736 | tf_op jit(solution)/shard_map/ppermute | solution.py:105
  135.1 28.4 %collective-permute-start.17 = (bf16[1,32,16,256]{3,2,1,0:T(8,128)(2,1)S(1)}, bf16[1,32,16,256]{3,2,1,0:T(8,128)(2,1)}, u32[]{:S(2)}, u32[]{:S(2)}) collective-permute-start(bf16[1,32,16,256]{3,2,1,0:T(8,128)(2,1)S(1)} %bitcast.262), channel_id=1, source_target_pairs={{0,8},{1,9},{2,10},{3,11},{4,12},{5,13},{6,14},{7,15},{8,0},{9,1},... | collective-permute-start | bytes 786440 | tf_op jit(solution)/shard_map/ppermute | solution.py:105
  164.6 14.5 %collective-permute-start.18 = (bf16[8,40,16,256]{3,2,1,0:T(8,128)(2,1)}, bf16[8,40,16,256]{3,2,1,0:T(8,128)(2,1)}, u32[]{:S(2)}, u32[]{:S(2)}) collective-permute-start(bf16[8,40,16,256]{3,2,1,0:T(8,128)(2,1)} %collective-permute-done.14.refs_1_), channel_id=1, source_target_pairs={{0,1},{1,0},{2,3},{3,2},{4,5},{5,4},{6,7},{7,6},{8,9},{9,8},{10,11... | collective-permute-start | bytes 7864328 | tf_op jit(solution)/shard_map/ppermute | solution.py:94
  168.5 51.9 %collective-permute-start.20 = (bf16[8,32,16,256]{3,2,1,0:T(8,128)(2,1)}, bf16[8,32,16,256]{3,2,1,0:T(8,128)(2,1)}, u32[]{:S(2)}, u32[]{:S(2)}) collective-permute-start(bf16[8,32,16,256]{3,2,1,0:T(8,128)(2,1)} %pad_maximum_fusion.1.refs_0_), channel_id=1, source_target_pairs={{0,16},{1,3},{2,18},{3,1},{4,20},{5,7},{6,22},{7,5},{8,24},{9,11},... | collective-permute-start | bytes 6291464 | tf_op jit(solution)/shard_map/ppermute | solution.py:105
  170.0 50.4 %collective-permute-start.21 = (bf16[8,32,16,256]{3,2,1,0:T(8,128)(2,1)}, bf16[8,32,16,256]{3,2,1,0:T(8,128)(2,1)}, u32[]{:S(2)}, u32[]{:S(2)}) collective-permute-start(bf16[8,32,16,256]{3,2,1,0:T(8,128)(2,1)} %pad_maximum_fusion.1.refs_0_), channel_id=1, source_target_pairs={{0,1},{1,0},{2,3},{3,2},{4,5},{5,4},{6,7},{7,6},{8,9},{9,8},{10,11... | collective-permute-start | bytes 6291464 | tf_op jit(solution)/shard_map/ppermute | solution.py:94
  171.8 28.5 %collective-permute-start.19 = (bf16[2,32,16,256]{3,2,1,0:T(8,128)(2,1)}, bf16[2,32,16,256]{3,2,1,0:T(8,128)(2,1)}, u32[]{:S(2)}, u32[]{:S(2)}) collective-permute-start(bf16[2,32,16,256]{3,2,1,0:T(8,128)(2,1)} %pad_maximum_fusion.18), channel_id=1, source_target_pairs={{0,2},{1,17},{2,0},{3,19},{4,6},{5,21},{6,4},{7,23},{8,10},{9,25},... | collective-permute-start | bytes 1572872 | tf_op jit(solution)/shard_map/ppermute | solution.py:105
  173.7 46.7 %all-to-all-start.1 = ((bf16[2,16,32,512]{3,2,0,1:T(8,128)(2,1)}), bf16[2,16,32,512]{3,2,0,1:T(8,128)(2,1)S(1)}, u32[]{:S(2)}, u32[]{:S(2)}) async-start(bf16[2,16,32,512]{3,2,0,1:T(8,128)(2,1)} %copy.66), calls=%async_computation.1 | async-start | bytes 2097152 | tf_op jit(solution)/shard_map/all_to_all | solution.py:679
  202.5 20.4 %collective-permute-start.22 = (bf16[4,32,16,256]{3,2,1,0:T(8,128)(2,1)}, bf16[4,32,16,256]{3,2,1,0:T(8,128)(2,1)}, u32[]{:S(2)}, u32[]{:S(2)}) collective-permute-start(bf16[4,32,16,256]{3,2,1,0:T(8,128)(2,1)} %pad_maximum_fusion.9), channel_id=1, source_target_pairs={{0,16},{1,5},{2,18},{3,7},{4,20},{5,1},{6,22},{7,3},{8,24},{9,13},... | collective-permute-start | bytes 3145736 | tf_op jit(solution)/shard_map/ppermute | solution.py:105
  222.9 12.9 %collective-permute-start.23 = (bf16[8,32,16,256]{3,2,1,0:T(8,128)(2,1)}, bf16[8,32,16,256]{3,2,1,0:T(8,128)(2,1)}, u32[]{:S(2)}, u32[]{:S(2)}) collective-permute-start(bf16[8,32,16,256]{3,2,1,0:T(8,128)(2,1)} %collective-permute-done.20.refs_1_), channel_id=1, source_target_pairs={{0,1},{1,0},{2,3},{3,2},{4,5},{5,4},{6,7},{7,6},{8,9},{9,8},{10,11... | collective-permute-start | bytes 6291464 | tf_op jit(solution)/shard_map/ppermute | solution.py:94
  225.9 38.6 %collective-permute-start.24 = (bf16[8,32,16,256]{3,2,1,0:T(8,128)(2,1)}, bf16[8,32,16,256]{3,2,1,0:T(8,128)(2,1)}, u32[]{:S(2)}, u32[]{:S(2)}) collective-permute-start(bf16[8,32,16,256]{3,2,1,0:T(8,128)(2,1)} %pad_maximum_fusion.2.refs_0_), channel_id=1, source_target_pairs={{0,4},{1,3},{2,6},{3,1},{4,0},{5,7},{6,2},{7,5},{8,12},{9,11},{10,... | collective-permute-start | bytes 6291464 | tf_op jit(solution)/shard_map/ppermute | solution.py:105
  228.2 36.3 %collective-permute-start.25 = (bf16[8,32,16,256]{3,2,1,0:T(8,128)(2,1)}, bf16[8,32,16,256]{3,2,1,0:T(8,128)(2,1)}, u32[]{:S(2)}, u32[]{:S(2)}) collective-permute-start(bf16[8,32,16,256]{3,2,1,0:T(8,128)(2,1)} %pad_maximum_fusion.2.refs_0_), channel_id=1, source_target_pairs={{0,1},{1,0},{2,3},{3,2},{4,5},{5,4},{6,7},{7,6},{8,9},{9,8},{10,11... | collective-permute-start | bytes 6291464 | tf_op jit(solution)/shard_map/ppermute | solution.py:94
  229.8 41.4 %all-to-all-start.2 = ((bf16[32,1,32,512]{3,2,1,0:T(8,128)(2,1)}), bf16[32,1,32,512]{3,2,1,0:T(8,128)(2,1)S(1)}, u32[]{:S(2)}, u32[]{:S(2)}) async-start(bf16[32,1,32,512]{3,2,1,0:T(8,128)(2,1)} %bitcast.258), calls=%async_computation.2 | async-start | bytes 2097152 | tf_op jit(solution)/shard_map/all_to_all | solution.py:684
  264.5 9.6 %collective-permute-start.26 = (bf16[8,32,16,256]{3,2,1,0:T(8,128)(2,1)}, bf16[8,32,16,256]{3,2,1,0:T(8,128)(2,1)}, u32[]{:S(2)}, u32[]{:S(2)}) collective-permute-start(bf16[8,32,16,256]{3,2,1,0:T(8,128)(2,1)} %collective-permute-done.24.refs_1_), channel_id=1, source_target_pairs={{0,1},{1,0},{2,3},{3,2},{4,5},{5,4},{6,7},{7,6},{8,9},{9,8},{10,11... | collective-permute-start | bytes 6291464 | tf_op jit(solution)/shard_map/ppermute | solution.py:94
  272.8 33.2 %collective-permute-start.30 = (bf16[512,4096]{1,0:T(8,128)(2,1)}, bf16[512,4096]{1,0:T(8,128)(2,1)}, u32[]{:S(2)}, u32[]{:S(2)}) collective-permute-start(bf16[512,4096]{1,0:T(8,128)(2,1)} %get-tuple-element.215.x_own), channel_id=1, source_target_pairs={{0,1},{1,0},{2,3},{3,2},{4,5},{5,4},{6,7},{7,6},{8,9},{9,8},{10,11... | collective-permute-start | bytes 12582920 | tf_op jit(solution)/shard_map/ppermute | solution.py:94
  297.3 8.2 %collective-permute-start.28 = (bf16[512,1024]{1,0:T(8,128)(2,1)S(1)}, bf16[512,1024]{1,0:T(8,128)(2,1)}, u32[]{:S(2)}, u32[]{:S(2)}) collective-permute-start(bf16[512,1024]{1,0:T(8,128)(2,1)S(1)} %convert_element_type.379.refs_0_), channel_id=1, source_target_pairs={{0,1},{1,0},{2,3},{3,2},{4,5},{5,4},{6,7},{7,6},{8,9},{9,8},{10,11... | collective-permute-start | bytes 3145736 | tf_op jit(solution)/shard_map/ppermute | solution.py:94
  305.5 10.3 %collective-permute-start.29 = (bf16[512,4096]{1,0:T(8,128)(2,1)}, bf16[512,4096]{1,0:T(8,128)(2,1)}, u32[]{:S(2)}, u32[]{:S(2)}) collective-permute-start(bf16[512,4096]{1,0:T(8,128)(2,1)} %multiply_convert_fusion.refs_0_), channel_id=1, source_target_pairs={{0,1},{1,0},{2,3},{3,2},{4,5},{5,4},{6,7},{7,6},{8,9},{9,8},{10,11... | collective-permute-start | bytes 12582920 | tf_op jit(solution)/shard_map/ppermute | solution.py:94
  305.5 29.7 %collective-permute-start.32 = (bf16[512,1024]{1,0:T(8,128)(2,1)S(1)}, bf16[512,1024]{1,0:T(8,128)(2,1)}, u32[]{:S(2)}, u32[]{:S(2)}) collective-permute-start(bf16[512,1024]{1,0:T(8,128)(2,1)S(1)} %copy-done.8), channel_id=1, source_target_pairs={{0,1},{1,0},{2,3},{3,2},{4,5},{5,4},{6,7},{7,6},{8,9},{9,8},{10,11... | collective-permute-start | bytes 3145736 | tf_op jit(solution)/shard_map/ppermute | solution.py:94
  315.8 29.1 %collective-permute-start.33 = (bf16[8,32,16,256]{3,2,1,0:T(8,128)(2,1)}, bf16[8,32,16,256]{3,2,1,0:T(8,128)(2,1)}, u32[]{:S(2)}, u32[]{:S(2)}) collective-permute-start(bf16[8,32,16,256]{3,2,1,0:T(8,128)(2,1)} %bitcast.324), channel_id=1, source_target_pairs={{0,4},{1,3},{2,6},{3,1},{4,0},{5,7},{6,2},{7,5},{8,12},{9,11},{10,... | collective-permute-start | bytes 6291464 | tf_op jit(solution)/shard_map/ppermute | solution.py:105
  327.0 6.8 %collective-permute-start.31 = (bf16[512,512]{1,0:T(8,128)(2,1)S(1)}, bf16[512,512]{1,0:T(8,128)(2,1)S(1)}, u32[]{:S(2)}, u32[]{:S(2)}) collective-permute-start(bf16[512,512]{1,0:T(8,128)(2,1)S(1)} %constant_dynamic-slice_fusion.2), channel_id=1, source_target_pairs={{0,1},{1,0},{2,3},{3,2},{4,5},{5,4},{6,7},{7,6},{8,9},{9,8},{10,11... | collective-permute-start | bytes 1572872 | tf_op jit(solution)/shard_map/ppermute | solution.py:94
  349.2 20.2 %collective-permute-start.34 = (bf16[4,32,16,256]{3,2,1,0:T(8,128)(2,1)}, bf16[4,32,16,256]{3,2,1,0:T(8,128)(2,1)}, u32[]{:S(2)}, u32[]{:S(2)}) collective-permute-start(bf16[4,32,16,256]{3,2,1,0:T(8,128)(2,1)} %get-tuple-element.355), channel_id=1, source_target_pairs={{0,16},{1,5},{2,18},{3,7},{4,20},{5,1},{6,22},{7,3},{8,24},{9,13},... | collective-permute-start | bytes 3145736 | tf_op jit(solution)/shard_map/ppermute | solution.py:105
  351.6 30.9 %all-to-all-start.3 = ((bf16[2,16,32,512]{3,2,0,1:T(8,128)(2,1)}), bf16[2,16,32,512]{3,2,0,1:T(8,128)(2,1)S(1)}, u32[]{:S(2)}, u32[]{:S(2)}) async-start(bf16[2,16,32,512]{3,2,0,1:T(8,128)(2,1)} %copy.69), calls=%async_computation.3 | async-start | bytes 2097152 | tf_op jit(solution)/shard_map/all_to_all | solution.py:679
  376.1 6.5 %collective-permute-start.35 = (bf16[512,1024]{1,0:T(8,128)(2,1)S(1)}, bf16[512,1024]{1,0:T(8,128)(2,1)S(1)}, u32[]{:S(2)}, u32[]{:S(2)}) collective-permute-start(bf16[512,1024]{1,0:T(8,128)(2,1)S(1)} %convert_element_type.387.refs_0_), channel_id=1, source_target_pairs={{0,1},{1,0},{2,3},{3,2},{4,5},{5,4},{6,7},{7,6},{8,9},{9,8},{10,11... | collective-permute-start | bytes 3145736 | tf_op jit(solution)/shard_map/ppermute | solution.py:94
  378.9 13.4 %collective-permute-start.42 = (bf16[512,1024]{1,0:T(8,128)(2,1)}, bf16[512,1024]{1,0:T(8,128)(2,1)}, u32[]{:S(2)}, u32[]{:S(2)}) collective-permute-start(bf16[512,1024]{1,0:T(8,128)(2,1)} %get-tuple-element.192.x_own.o_ref), channel_id=1, source_target_pairs={{0,1},{1,0},{2,3},{3,2},{4,5},{5,4},{6,7},{7,6},{8,9},{9,8},{10,11... | collective-permute-start | bytes 3145736 | tf_op jit(solution)/shard_map/ppermute | solution.py:94
  379.0 45.6 %collective-permute-start.43 = (bf16[8,32,16,256]{3,2,1,0:T(8,128)(2,1)}, bf16[8,32,16,256]{3,2,1,0:T(8,128)(2,1)}, u32[]{:S(2)}, u32[]{:S(2)}) collective-permute-start(bf16[8,32,16,256]{3,2,1,0:T(8,128)(2,1)} %bitcast.61), channel_id=1, source_target_pairs={{0,16},{1,3},{2,18},{3,1},{4,20},{5,7},{6,22},{7,5},{8,24},{9,11},... | collective-permute-start | bytes 6291464 | tf_op jit(solution)/shard_map/ppermute | solution.py:105
  386.8 35.5 %all-to-all-start.4 = ((bf16[32,1,32,512]{3,2,1,0:T(8,128)(2,1)}), bf16[32,1,32,512]{3,2,1,0:T(8,128)(2,1)}, u32[]{:S(2)}, u32[]{:S(2)}) async-start(bf16[32,1,32,512]{3,2,1,0:T(8,128)(2,1)} %bitcast.256), calls=%async_computation.4 | async-start | bytes 2097152 | tf_op jit(solution)/shard_map/all_to_all | solution.py:684
  391.8 9.4 %collective-permute-start.41 = (bf16[512,1024]{1,0:T(8,128)(2,1)S(1)}, bf16[512,1024]{1,0:T(8,128)(2,1)S(1)}, u32[]{:S(2)}, u32[]{:S(2)}) collective-permute-start(bf16[512,1024]{1,0:T(8,128)(2,1)S(1)} %copy-done.23), channel_id=1, source_target_pairs={{0,1},{1,0},{2,3},{3,2},{4,5},{5,4},{6,7},{7,6},{8,9},{9,8},{10,11... | collective-permute-start | bytes 3145736 | tf_op jit(solution)/shard_map/ppermute | solution.py:94
  392.3 24.5 %collective-permute-start.36 = (bf16[512,1024]{1,0:T(8,128)(2,1)}, bf16[512,1024]{1,0:T(8,128)(2,1)}, u32[]{:S(2)}, u32[]{:S(2)}) collective-permute-start(bf16[512,1024]{1,0:T(8,128)(2,1)} %get-tuple-element.204.o_ref.x_own), channel_id=1, source_target_pairs={{0,1},{1,0},{2,3},{3,2},{4,5},{5,4},{6,7},{7,6},{8,9},{9,8},{10,11... | collective-permute-start | bytes 3145736 | tf_op jit(solution)/shard_map/ppermute | solution.py:94
  392.4 24.4 %collective-permute-start.37 = (bf16[512,1024]{1,0:T(8,128)(2,1)S(1)}, bf16[512,1024]{1,0:T(8,128)(2,1)}, u32[]{:S(2)}, u32[]{:S(2)}) collective-permute-start(bf16[512,1024]{1,0:T(8,128)(2,1)S(1)} %copy-done.19), channel_id=1, source_target_pairs={{0,1},{1,0},{2,3},{3,2},{4,5},{5,4},{6,7},{7,6},{8,9},{9,8},{10,11... | collective-permute-start | bytes 3145736 | tf_op jit(solution)/shard_map/ppermute | solution.py:94
  399.3 25.3 %collective-permute-start.44 = (bf16[2,32,16,256]{3,2,1,0:T(8,128)(2,1)}, bf16[2,32,16,256]{3,2,1,0:T(8,128)(2,1)}, u32[]{:S(2)}, u32[]{:S(2)}) collective-permute-start(bf16[2,32,16,256]{3,2,1,0:T(8,128)(2,1)} %get-tuple-element.364), channel_id=1, source_target_pairs={{0,2},{1,17},{2,0},{3,19},{4,6},{5,21},{6,4},{7,23},{8,10},{9,25},... | collective-permute-start | bytes 1572872 | tf_op jit(solution)/shard_map/ppermute | solution.py:105
  402.1 9.4 %collective-permute-start.39 = (bf16[128,1024]{1,0:T(8,128)(2,1)S(1)}, bf16[128,1024]{1,0:T(8,128)(2,1)S(1)}, u32[]{:S(2)}, u32[]{:S(2)}) collective-permute-start(bf16[128,1024]{1,0:T(8,128)(2,1)S(1)} %copy-done.43), channel_id=1, source_target_pairs={{0,1},{1,0},{2,3},{3,2},{4,5},{5,4},{6,7},{7,6},{8,9},{9,8},{10,11... | collective-permute-start | bytes 786440 | tf_op jit(solution)/shard_map/ppermute | solution.py:94
  424.6 32.0 %collective-permute-start.45 = (bf16[8,40,16,256]{3,2,1,0:T(8,128)(2,1)}, bf16[8,40,16,256]{3,2,1,0:T(8,128)(2,1)}, u32[]{:S(2)}, u32[]{:S(2)}) collective-permute-start(bf16[8,40,16,256]{3,2,1,0:T(8,128)(2,1)} %bitcast.241), channel_id=1, source_target_pairs={{0,2},{1,17},{2,0},{3,19},{4,6},{5,21},{6,4},{7,23},{8,10},{9,25},... | collective-permute-start | bytes 7864328 | tf_op jit(solution)/shard_map/ppermute | solution.py:105
  428.8 25.6 %collective-permute-start.46 = (bf16[4,32,16,256]{3,2,1,0:T(8,128)(2,1)}, bf16[4,32,16,256]{3,2,1,0:T(8,128)(2,1)S(1)}, u32[]{:S(2)}, u32[]{:S(2)}) collective-permute-start(bf16[4,32,16,256]{3,2,1,0:T(8,128)(2,1)} %get-tuple-element.353), channel_id=1, source_target_pairs={{0,4},{1,5},{2,6},{3,7},{4,0},{5,1},{6,2},{7,3},{8,12},{9,13},{10,... | collective-permute-start | bytes 3145736 | tf_op jit(solution)/shard_map/ppermute | solution.py:105
  446.5 20.2 %collective-permute-start.47 = (bf16[512,1024]{1,0:T(8,128)(2,1)}, bf16[512,1024]{1,0:T(8,128)(2,1)}, u32[]{:S(2)}, u32[]{:S(2)}) collective-permute-start(bf16[512,1024]{1,0:T(8,128)(2,1)} %get-tuple-element.293.refs_0_), channel_id=1, source_target_pairs={{0,1},{1,0},{2,3},{3,2},{4,5},{5,4},{6,7},{7,6},{8,9},{9,8},{10,11... | collective-permute-start | bytes 3145736 | tf_op jit(solution)/shard_map/ppermute | solution.py:94
  460.7 27.8 %collective-permute-start.50 = (bf16[4,40,16,256]{3,2,1,0:T(8,128)(2,1)}, bf16[4,40,16,256]{3,2,1,0:T(8,128)(2,1)}, u32[]{:S(2)}, u32[]{:S(2)}) collective-permute-start(bf16[4,40,16,256]{3,2,1,0:T(8,128)(2,1)} %get-tuple-element.351), channel_id=1, source_target_pairs={{0,16},{1,3},{2,18},{3,1},{4,20},{5,7},{6,22},{7,5},{8,24},{9,11},... | collective-permute-start | bytes 3932168 | tf_op jit(solution)/shard_map/ppermute | solution.py:105
  461.7 7.5 %collective-permute-start.48 = (bf16[512,1024]{1,0:T(8,128)(2,1)}, bf16[512,1024]{1,0:T(8,128)(2,1)}, u32[]{:S(2)}, u32[]{:S(2)}) collective-permute-start(bf16[512,1024]{1,0:T(8,128)(2,1)} %get-tuple-element.282.refs_1_), channel_id=1, source_target_pairs={{0,1},{1,0},{2,3},{3,2},{4,5},{5,4},{6,7},{7,6},{8,9},{9,8},{10,11... | collective-permute-start | bytes 3145736 | tf_op jit(solution)/shard_map/ppermute | solution.py:94
  461.7 7.5 %collective-permute-start.49 = (bf16[512,1024]{1,0:T(8,128)(2,1)S(1)}, bf16[512,1024]{1,0:T(8,128)(2,1)}, u32[]{:S(2)}, u32[]{:S(2)}) collective-permute-start(bf16[512,1024]{1,0:T(8,128)(2,1)S(1)} %copy-done.6), channel_id=1, source_target_pairs={{0,1},{1,0},{2,3},{3,2},{4,5},{5,4},{6,7},{7,6},{8,9},{9,8},{10,11... | collective-permute-start | bytes 3145736 | tf_op jit(solution)/shard_map/ppermute | solution.py:94
  465.1 16.8 %collective-permute-start.51 = (bf16[2,32,16,256]{3,2,1,0:T(8,128)(2,1)}, bf16[2,32,16,256]{3,2,1,0:T(8,128)(2,1)}, u32[]{:S(2)}, u32[]{:S(2)}) collective-permute-start(bf16[2,32,16,256]{3,2,1,0:T(8,128)(2,1)} %get-tuple-element.362), channel_id=1, source_target_pairs={{0,2},{1,17},{2,0},{3,19},{4,6},{5,21},{6,4},{7,23},{8,10},{9,25},... | collective-permute-start | bytes 1572872 | tf_op jit(solution)/shard_map/ppermute | solution.py:105
  466.7 15.2 %collective-permute-start.52 = (bf16[1,32,16,256]{3,2,1,0:T(8,128)(2,1)S(1)}, bf16[1,32,16,256]{3,2,1,0:T(8,128)(2,1)}, u32[]{:S(2)}, u32[]{:S(2)}) collective-permute-start(bf16[1,32,16,256]{3,2,1,0:T(8,128)(2,1)S(1)} %add_convert_fusion.27), channel_id=1, source_target_pairs={{0,8},{1,9},{2,10},{3,11},{4,12},{5,13},{6,14},{7,15},{8,0},{9,1},... | collective-permute-start | bytes 786440 | tf_op jit(solution)/shard_map/ppermute | solution.py:105
  477.5 28.2 %collective-permute-start.53 = (bf16[8,24,16,256]{3,2,1,0:T(8,128)(2,1)}, bf16[8,24,16,256]{3,2,1,0:T(8,128)(2,1)S(1)}, u32[]{:S(2)}, u32[]{:S(2)}) collective-permute-start(bf16[8,24,16,256]{3,2,1,0:T(8,128)(2,1)} %bitcast.325), channel_id=1, source_target_pairs={{0,2},{1,17},{2,0},{3,19},{4,6},{5,21},{6,4},{7,23},{8,10},{9,25},... | collective-permute-start | bytes 4718600 | tf_op jit(solution)/shard_map/ppermute | solution.py:105
  489.5 16.3 %collective-permute-start.55 = (bf16[1,32,16,256]{3,2,1,0:T(8,128)(2,1)S(1)}, bf16[1,32,16,256]{3,2,1,0:T(8,128)(2,1)S(1)}, u32[]{:S(2)}, u32[]{:S(2)}) collective-permute-start(bf16[1,32,16,256]{3,2,1,0:T(8,128)(2,1)S(1)} %add_convert_fusion.26), channel_id=1, source_target_pairs={{0,8},{1,9},{2,10},{3,11},{4,12},{5,13},{6,14},{7,15},{8,0},{9,1},... | collective-permute-start | bytes 786440 | tf_op jit(solution)/shard_map/ppermute | solution.py:105
  493.3 17.6 %collective-permute-start.54 = (bf16[2,40,16,256]{3,2,1,0:T(8,128)(2,1)S(1)}, bf16[2,40,16,256]{3,2,1,0:T(8,128)(2,1)S(1)}, u32[]{:S(2)}, u32[]{:S(2)}) collective-permute-start(bf16[2,40,16,256]{3,2,1,0:T(8,128)(2,1)S(1)} %get-tuple-element.359), channel_id=1, source_target_pairs={{0,4},{1,5},{2,6},{3,7},{4,0},{5,1},{6,2},{7,3},{8,12},{9,13},{10,... | collective-permute-start | bytes 1966088 | tf_op jit(solution)/shard_map/ppermute | solution.py:105
  511.0 17.1 %collective-permute-start.60 = (bf16[1,40,16,256]{3,2,1,0:T(8,128)(2,1)S(1)}, bf16[1,40,16,256]{3,2,1,0:T(8,128)(2,1)S(1)}, u32[]{:S(2)}, u32[]{:S(2)}) collective-permute-start(bf16[1,40,16,256]{3,2,1,0:T(8,128)(2,1)S(1)} %add_convert_fusion.21), channel_id=1, source_target_pairs={{0,8},{1,9},{2,10},{3,11},{4,12},{5,13},{6,14},{7,15},{8,0},{9,1},... | collective-permute-start | bytes 983048 | tf_op jit(solution)/shard_map/ppermute | solution.py:105
  511.9 12.1 %collective-permute-start.56 = (bf16[4,24,16,256]{3,2,1,0:T(8,128)(2,1)S(1)}, bf16[4,24,16,256]{3,2,1,0:T(8,128)(2,1)S(1)}, u32[]{:S(2)}, u32[]{:S(2)}) collective-permute-start(bf16[4,24,16,256]{3,2,1,0:T(8,128)(2,1)S(1)} %get-tuple-element.357), channel_id=1, source_target_pairs={{0,16},{1,3},{2,18},{3,1},{4,20},{5,7},{6,22},{7,5},{8,24},{9,11},... | collective-permute-start | bytes 2359304 | tf_op jit(solution)/shard_map/ppermute | solution.py:105
  524.3 10.1 %collective-permute-start.59 = (bf16[2,24,16,256]{3,2,1,0:T(8,128)(2,1)S(1)}, bf16[2,24,16,256]{3,2,1,0:T(8,128)(2,1)S(1)}, u32[]{:S(2)}, u32[]{:S(2)}) collective-permute-start(bf16[2,24,16,256]{3,2,1,0:T(8,128)(2,1)S(1)} %get-tuple-element.372), channel_id=1, source_target_pairs={{0,4},{1,5},{2,6},{3,7},{4,0},{5,1},{6,2},{7,3},{8,12},{9,13},{10,... | collective-permute-start | bytes 1179656 | tf_op jit(solution)/shard_map/ppermute | solution.py:105
  534.5 9.4 %collective-permute-start.61 = (bf16[1,24,16,256]{3,2,1,0:T(8,128)(2,1)S(1)}, bf16[1,24,16,256]{3,2,1,0:T(8,128)(2,1)S(1)}, u32[]{:S(2)}, u32[]{:S(2)}) collective-permute-start(bf16[1,24,16,256]{3,2,1,0:T(8,128)(2,1)S(1)} %add_convert_fusion.29), channel_id=1, source_target_pairs={{0,8},{1,9},{2,10},{3,11},{4,12},{5,13},{6,14},{7,15},{8,0},{9,1},... | collective-permute-start | bytes 589832 | tf_op jit(solution)/shard_map/ppermute | solution.py:105
  545.5 17.4 %all-to-all-start.5 = ((bf16[64,16,256]{2,1,0:T(8,128)(2,1)}), bf16[64,16,256]{2,1,0:T(8,128)(2,1)S(1)}, u32[]{:S(2)}, u32[]{:S(2)}) async-start(bf16[64,16,256]{2,1,0:T(8,128)(2,1)} %gather_fusion.3), calls=%async_computation.5 | async-start | bytes 1048576 | tf_op jit(solution)/shard_map/all_to_all | solution.py:327
  562.9 19.5 %all-to-all-start.6 = ((bf16[72,16,256]{2,1,0:T(8,128)(2,1)}), bf16[72,16,256]{2,1,0:T(8,128)(2,1)S(1)}, u32[]{:S(2)}, u32[]{:S(2)}) async-start(bf16[72,16,256]{2,1,0:T(8,128)(2,1)} %bitcast.88), calls=%async_computation.6 | async-start | bytes 1179648 | tf_op jit(solution)/shard_map/all_to_all | solution.py:327
  566.8 14.8 %collective-permute-start.63 = (bf16[8,8,16,256]{3,2,1,0:T(8,128)(2,1)S(1)}, bf16[8,8,16,256]{3,2,1,0:T(8,128)(2,1)S(1)}, u32[]{:S(2)}, u32[]{:S(2)}) collective-permute-start(bf16[8,8,16,256]{3,2,1,0:T(8,128)(2,1)S(1)} %bitcast.283), channel_id=1, source_target_pairs={{0,16},{16,0},{1,17},{17,1},{2,18},{18,2},{3,19},{19,3},{4,20},{20... | collective-permute-start | bytes 1572872 | tf_op jit(solution)/shard_map/ppermute | solution.py:97
  582.3 15.4 %collective-permute-start.64 = (bf16[8,9,16,256]{3,2,1,0:T(8,128)(2,1)S(1)}, bf16[8,9,16,256]{3,2,1,0:T(8,128)(2,1)S(1)}, u32[]{:S(2)}, u32[]{:S(2)}) collective-permute-start(bf16[8,9,16,256]{3,2,1,0:T(8,128)(2,1)S(1)} %bitcast.274), channel_id=1, source_target_pairs={{0,16},{16,0},{1,17},{17,1},{2,18},{18,2},{3,19},{19,3},{4,20},{20... | collective-permute-start | bytes 1769480 | tf_op jit(solution)/shard_map/ppermute | solution.py:97
  (96 other events, 765.0 us)
